TPU v7x, 32 devices: a whole 2x2x4 slice. The times are simulated.
32 devices in a mesh: dp: 8 (over y, x, core), mp: 4 (over z).
Axes of the slice: x: 2, y: 2, z: 4, core: 2. Of those that a mesh axis runs over, the one named last changes fastest.
Arguments:
- tokens: bfloat16 [8, 1024, 2048], P('dp', 'mp'), may hold values from -6 to 6
- mixed_grad: bfloat16 [8, 1024, 2048], P('dp', 'mp'), may hold values from -6 to 6
- doc_ids: int32 [8, 1024], P('dp'), may hold values from 0 to 7, never falling along the last dimension, each value on 1 to 512 neighbouring positions
- head_count: int32 [8, 1024], P('dp'), may hold values from 1 to 16
- width_bucket: int32 [8, 1024], P('dp'), may hold values from 0 to 3
- first_gain: float32 [2048], replicated, may hold values from 0.5 to 1.5
- first_shift: float32 [2048], replicated, may hold values from -3 to 3
- query_weight: bfloat16 [2048, 2048], P(None, 'mp'), may hold values from -0.125 to 0.125
- key_weight: bfloat16 [2048, 2048], P(None, 'mp'), may hold values from -0.125 to 0.125
- value_weight: bfloat16 [2048, 2048], P(None, 'mp'), may hold values from -0.125 to 0.125
- output_weight: bfloat16 [2048, 2048], P(None, 'mp'), may hold values from -0.375 to 0.375
- second_gain: float32 [2048], replicated, may hold values from 0.5 to 1.5
- second_shift: float32 [2048], replicated, may hold values from -3 to 3
- up_weight: bfloat16 [2048, 8192], P(None, 'mp'), may hold values from -0.125 to 0.125
- down_weight: bfloat16 [2048, 8192], P(None, 'mp'), may hold values from -0.0625 to 0.0625
Outputs:
- mixed: bfloat16 [8, 1024, 2048], P('dp', 'mp')
- input_grad: bfloat16 [8, 1024, 2048], P('dp', 'mp')
- first_gain_grad: float32 [2048], replicated
- first_shift_grad: float32 [2048], replicated
- query_grad: float32 [2048, 2048], P('dp', 'mp')
- key_grad: float32 [2048, 2048], P('dp', 'mp')
- value_grad: float32 [2048, 2048], P('dp', 'mp')
- output_grad: float32 [2048, 2048], P('dp', 'mp')
- second_gain_grad: float32 [2048], replicated
- second_shift_grad: float32 [2048], replicated
- up_grad: float32 [2048, 8192], P('dp', 'mp')
- down_grad: float32 [2048, 8192], P('dp', 'mp')
- bucket_tally: int32 [4], replicated
- head_tally: int32 [16], replicated
Inputs may be any that keep to these rules, and one draw needn't show every extreme that they name: `doc_ids`: within each sequence, document numbers never fall; a document has 1 to 512 tokens.
All inputs are finite; a program needn't handle non-finite values.
Results may differ from a plain program's by a relative error of at most 0.023.
Values may be sent and summed in bfloat16 or wider, within the bound.
No kernel may reach another device: no remote copies, remote signals or barrier semaphores. Data moves between devices by JAX's collectives and lax.ppermute only.
A program may use at most 192 MiB of HBM per device.

v0:
```python
import jax
import jax.numpy as jnp
from jax import lax
from jax.sharding import PartitionSpec as P

HEADS = 16
E = 128
FF = 8192


EPS = 1e-05
BLOCK = 512


def norm_forward(values, gain, shift):
    mean = jnp.mean(values, axis=-1, keepdims=True)
    cent = values - mean
    inverse = lax.rsqrt(jnp.mean(cent * cent, axis=-1, keepdims=True) + EPS)
    normed = cent * inverse
    return (normed * gain + shift, normed, inverse)


def norm_backward(grad_out, normed, inverse, gain):
    scaled = grad_out * gain
    grad_in = inverse * (
        scaled
        - jnp.mean(scaled, axis=-1, keepdims=True)
        - normed * jnp.mean(scaled * normed, axis=-1, keepdims=True)
    )
    return (grad_in, jnp.sum(grad_out * normed, axis=0), jnp.sum(grad_out, axis=0))


def rotary_tables(length, size):
    half = size // 2
    freq = 10000.0 ** (-(jnp.arange(half, dtype=jnp.float32) * 2.0 / size))
    angle = jnp.arange(length, dtype=jnp.float32)[:, None] * freq[None, :]
    return (jnp.cos(angle)[:, None, :], jnp.sin(angle)[:, None, :])


def rotate(values, cosine, sine):
    half = values.shape[-1] // 2
    first = values[..., :half]
    second = values[..., half:]
    return jnp.concatenate(
        [first * cosine - second * sine, second * cosine + first * sine], axis=-1
    )


def unrotate(grads, cosine, sine):
    half = grads.shape[-1] // 2
    first = grads[..., :half]
    second = grads[..., half:]
    return jnp.concatenate(
        [first * cosine + second * sine, second * cosine - first * sine], axis=-1
    )


def outer(left, right):
    return lax.dot_general(
        left, right, (((0,), (0,)), ((), ())), preferred_element_type=jnp.float32
    )


def per_device(
    tokens,
    mixed_grad,
    doc_ids,
    head_count,
    width_bucket,
    first_gain,
    first_shift,
    query_weight,
    key_weight,
    value_weight,
    output_weight,
    second_gain,
    second_shift,
    up_weight,
    down_weight,
):
    rank = lax.axis_index("mp")
    rows = tokens.shape[1]
    local = query_weight.shape[1]
    local_heads = local // E
    hidden = up_weight.shape[1]
    scale = E ** (-0.5)
    x_rows = tokens[0].astype(jnp.float32)
    docs = doc_ids[0]
    heads = head_count[0]
    bucket = width_bucket[0]
    normed_out, normed_one, inverse_one = norm_forward(x_rows, first_gain, first_shift)
    first_all = lax.all_gather(normed_out.astype(jnp.bfloat16), "mp", axis=0, tiled=True)
    length = first_all.shape[0]
    span = min(BLOCK, length)
    blocks = length // span
    cosine, sine = rotary_tables(length, E)
    positions = jnp.arange(length, dtype=jnp.int32)
    q_lin = jnp.dot(first_all, query_weight, preferred_element_type=jnp.float32).reshape(
        length, local_heads, E
    )
    k_lin = jnp.dot(first_all, key_weight, preferred_element_type=jnp.float32).reshape(
        length, local_heads, E
    )
    vals = (
        jnp.dot(first_all, value_weight, preferred_element_type=jnp.float32)
        .astype(jnp.bfloat16)
        .reshape(length, local_heads, E)
    )
    query = rotate(q_lin, cosine, sine).astype(jnp.bfloat16)
    keys = rotate(k_lin, cosine, sine).astype(jnp.bfloat16)

    def block_scores(start):
        q_blk = lax.dynamic_slice_in_dim(query, start, span, 0)
        q_pos = start + jnp.arange(span, dtype=jnp.int32)
        q_doc = lax.dynamic_slice_in_dim(docs, start, span, 0)
        scores = jnp.einsum("qhe,khe->hqk", q_blk, keys, preferred_element_type=jnp.float32) * scale
        allowed = (positions[None, :] <= q_pos[:, None]) & (docs[None, :] == q_doc[:, None])
        return (jnp.where(allowed[None], scores, -1e30), q_blk)

    def forward_block(start):
        scores, q_blk = block_scores(start)
        top = jnp.max(scores, axis=-1, keepdims=True)
        expo = jnp.exp(scores - top)
        total = jnp.sum(expo, axis=-1, keepdims=True)
        prob = (expo / total).astype(jnp.bfloat16)
        out = jnp.einsum("hqk,khe->qhe", prob, vals, preferred_element_type=jnp.float32)
        return (out, (top + jnp.log(total))[..., 0])

    starts = jnp.arange(blocks, dtype=jnp.int32) * span
    attended, log_totals = lax.map(forward_block, starts)
    attended = attended.reshape(length, local_heads, E)
    head_ids = rank * local_heads + jnp.arange(local_heads, dtype=jnp.int32)
    head_mask = (head_ids[None, :] < heads[:, None]).astype(jnp.float32)
    masked = (attended * head_mask[:, :, None]).astype(jnp.bfloat16).reshape(length, local)
    piece = masked
    state = x_rows + lax.psum_scatter(
        jnp.dot(piece, output_weight.T, preferred_element_type=jnp.float32).astype(jnp.bfloat16),
        "mp",
        scatter_dimension=0,
        tiled=True,
    ).astype(jnp.float32)
    second_out, normed_two, inverse_two = norm_forward(state, second_gain, second_shift)
    second_all = lax.all_gather(second_out.astype(jnp.bfloat16), "mp", axis=0, tiled=True)
    upper = jnp.dot(second_all, up_weight, preferred_element_type=jnp.float32)
    columns = rank * hidden + jnp.arange(hidden, dtype=jnp.int32)
    width_mask = (columns[None, :] < (bucket[:, None] + 1) * (FF // 4)).astype(jnp.float32)
    lifted = jnp.maximum(upper, 0.0)
    active = (lifted * lifted * width_mask).astype(jnp.bfloat16)
    piece = active
    mixed = (
        state
        + lax.psum_scatter(
            jnp.dot(piece, down_weight.T, preferred_element_type=jnp.float32).astype(jnp.bfloat16),
            "mp",
            scatter_dimension=0,
            tiled=True,
        ).astype(jnp.float32)
    ).astype(jnp.bfloat16)
    grad_all = lax.all_gather(mixed_grad[0], "mp", axis=0, tiled=True)
    grad_active = jnp.dot(grad_all, down_weight, preferred_element_type=jnp.float32).astype(
        jnp.bfloat16
    )
    grad_upper = (grad_active.astype(jnp.float32) * 2.0 * lifted * width_mask).astype(jnp.bfloat16)
    down_term = outer(grad_all, active)
    up_term = outer(second_all, grad_upper)
    piece = grad_upper
    grad_second = lax.psum_scatter(
        jnp.dot(piece, up_weight.T, preferred_element_type=jnp.float32).astype(jnp.bfloat16),
        "mp",
        scatter_dimension=0,
        tiled=True,
    ).astype(jnp.float32)
    back_two, second_gain_part, second_shift_part = norm_backward(
        grad_second, normed_two, inverse_two, second_gain
    )
    grad_state = mixed_grad[0].astype(jnp.float32) + back_two
    state_all = lax.all_gather(grad_state.astype(jnp.bfloat16), "mp", axis=0, tiled=True)
    out_term = outer(state_all, masked)
    grad_masked = jnp.dot(state_all, output_weight, preferred_element_type=jnp.float32).astype(
        jnp.bfloat16
    )
    grad_heads = (
        grad_masked.astype(jnp.float32).reshape(length, local_heads, E) * head_mask[:, :, None]
    ).astype(jnp.bfloat16)
    grad_blocks = grad_heads.reshape(blocks, span, local_heads, E)

    def backward_block(carry, item):
        key_acc, val_acc = carry
        start, log_total, grad_blk = item
        scores, q_blk = block_scores(start)
        prob = jnp.exp(scores - log_total[..., None])
        grad_prob = jnp.einsum("qhe,khe->hqk", grad_blk, vals, preferred_element_type=jnp.float32)
        delta = jnp.sum(prob * grad_prob, axis=-1, keepdims=True)
        grad_scores = (prob * (grad_prob - delta)).astype(jnp.bfloat16)
        grad_query = (
            jnp.einsum("hqk,khe->qhe", grad_scores, keys, preferred_element_type=jnp.float32)
            * scale
        )
        key_acc = (
            key_acc
            + jnp.einsum("hqk,qhe->khe", grad_scores, q_blk, preferred_element_type=jnp.float32)
            * scale
        )
        val_acc = val_acc + jnp.einsum(
            "hqk,qhe->khe", prob.astype(jnp.bfloat16), grad_blk, preferred_element_type=jnp.float32
        )
        return ((key_acc, val_acc), grad_query)

    zeros_kv = jnp.zeros((length, local_heads, E), jnp.float32)
    (grad_keys, grad_vals), grad_queries = lax.scan(
        backward_block, (zeros_kv, zeros_kv), (starts, log_totals, grad_blocks)
    )
    grad_queries = grad_queries.reshape(length, local_heads, E)
    dq_low = unrotate(grad_queries, cosine, sine).astype(jnp.bfloat16).reshape(length, local)
    dk_low = unrotate(grad_keys, cosine, sine).astype(jnp.bfloat16).reshape(length, local)
    dv_low = grad_vals.astype(jnp.bfloat16).reshape(length, local)
    query_term = outer(first_all, dq_low)
    key_term = outer(first_all, dk_low)
    value_term = outer(first_all, dv_low)
    total = jnp.dot(dq_low, query_weight.T, preferred_element_type=jnp.float32)
    total = total + jnp.dot(dk_low, key_weight.T, preferred_element_type=jnp.float32)
    grad_first = lax.psum_scatter(
        (total + jnp.dot(dv_low, value_weight.T, preferred_element_type=jnp.float32)).astype(
            jnp.bfloat16
        ),
        "mp",
        scatter_dimension=0,
        tiled=True,
    ).astype(jnp.float32)
    back_one, first_gain_part, first_shift_part = norm_backward(
        grad_first, normed_one, inverse_one, first_gain
    )
    input_grad = (grad_state + back_one).astype(jnp.bfloat16)
    own_bucket = lax.dynamic_slice_in_dim(bucket, rank * rows, rows, 0)
    own_heads = lax.dynamic_slice_in_dim(heads, rank * rows, rows, 0)
    bucket_part = jnp.sum(
        (own_bucket[:, None] == jnp.arange(4, dtype=jnp.int32)[None, :]).astype(jnp.float32), axis=0
    )
    head_part = jnp.sum(
        (own_heads[:, None] == jnp.arange(1, HEADS + 1, dtype=jnp.int32)[None, :]).astype(
            jnp.float32
        ),
        axis=0,
    )
    first_gain_grad, first_shift_grad, second_gain_grad, second_shift_grad, bucket_sum, head_sum = (
        lax.psum(
            (
                first_gain_part,
                first_shift_part,
                second_gain_part,
                second_shift_part,
                bucket_part,
                head_part,
            ),
            ("dp", "mp"),
        )
    )
    query_grad, key_grad, value_grad, output_grad, up_grad, down_grad = (
        lax.psum_scatter(
            query_term.astype(jnp.bfloat16), "dp", scatter_dimension=0, tiled=True
        ).astype(jnp.float32),
        lax.psum_scatter(
            key_term.astype(jnp.bfloat16), "dp", scatter_dimension=0, tiled=True
        ).astype(jnp.float32),
        lax.psum_scatter(
            value_term.astype(jnp.bfloat16), "dp", scatter_dimension=0, tiled=True
        ).astype(jnp.float32),
        lax.psum_scatter(
            out_term.astype(jnp.bfloat16), "dp", scatter_dimension=0, tiled=True
        ).astype(jnp.float32),
        lax.psum_scatter(
            up_term.astype(jnp.bfloat16), "dp", scatter_dimension=0, tiled=True
        ).astype(jnp.float32),
        lax.psum_scatter(
            down_term.astype(jnp.bfloat16), "dp", scatter_dimension=0, tiled=True
        ).astype(jnp.float32),
    )
    return (
        mixed[None],
        input_grad[None],
        first_gain_grad,
        first_shift_grad,
        query_grad,
        key_grad,
        value_grad,
        output_grad,
        second_gain_grad,
        second_shift_grad,
        up_grad,
        down_grad,
        bucket_sum.astype(jnp.int32),
        head_sum.astype(jnp.int32),
    )


def solution(mesh):
    placed = (
        P("dp", "mp", None),
        P("dp", "mp", None),
        P("dp", None),
        P("dp", None),
        P("dp", None),
        P(),
        P(),
        P(None, "mp"),
        P(None, "mp"),
        P(None, "mp"),
        P(None, "mp"),
        P(),
        P(),
        P(None, "mp"),
        P(None, "mp"),
    )
    return jax.shard_map(
        per_device,
        mesh=mesh,
        in_specs=placed,
        out_specs=(
            P("dp", "mp", None),
            P("dp", "mp", None),
            P(),
            P(),
            P("dp", "mp"),
            P("dp", "mp"),
            P("dp", "mp"),
            P("dp", "mp"),
            P(),
            P(),
            P("dp", "mp"),
            P("dp", "mp"),
            P(),
            P(),
        ),
        check_vma=False,
    )
```

profile of v0, /device:TPU:0, one launch (start us, length us, event | category | flops | bytes accessed | tf_op | source)
XLA Modules:
  0.0 1108.8 jit_solution(1855700280244004894)
XLA Ops:
  15.3 80.4 %all-gather.6.cloned.1.call-done = bf16[1024,2048]{1,0:T(8,128)(2,1)} async-done(((bf16[256,2048]{1,0:T(8,128)(2,1)}), bf16[1024,2048]{1,0:T(8,128)(2,1)}) %all-gather.6.cloned.1.call-update) | async-done | bytes 4194320 | tf_op jit(solution)/shard_map/all_gather | solution.py:92
  95.7 6.2 convolution_convert_fusion.9
  104.4 5.2 fusion.87
  111.2 3.2 copy.111
  114.4 3.2 copy.110
  117.6 5.2 fusion.86
  124.4 3.2 copy.109
  127.6 3.2 copy.108
  130.8 4.6 subtract_convert_fusion.2
  137.5 29.4 %while.28 = (s32[]{:T(128)}, f32[2,512,4,128]{3,2,1,0:T(4,128)}, f32[2,4,512]{2,1,0:T(4,128)S(1)}, s32[2]{0:T(128)S(1)}, s32[1,1024]{1,0:T(1,128)S(1)}, /*index=...) while((s32[]{:T(128)}, f32[2,512,4,128]{3,2,1,0:T(4,128)}, ...), condition=%wide.region_5.6_spmd.clone, body=%wide.region_2.5_spmd.clone.sunk | while | flops 1100478976 | bytes 54081812 | solution.py:130
  141.8 2.9 fusion.151
  147.1 3.2 fusion.153
  161.6 3.2 fusion.153
  170.8 4.4 convolution_convert_fusion.3
  175.3 75.4 %reduce-scatter.11.cloned.1.call-done = bf16[256,2048]{1,0:T(8,128)(2,1)} async-done(((bf16[1024,2048]{1,0:T(8,128)(2,1)}), bf16[256,2048]{1,0:T(8,128)(2,1)}) %reduce-scatter.11.cloned.1.call-update) | async-done | bytes 1048592 | tf_op jit(solution)/shard_map/reduce_scatter | solution.py:136
  255.6 80.7 %all-gather.8.cloned.1.call-done = bf16[1024,2048]{1,0:T(8,128)(2,1)} async-done(((bf16[256,2048]{1,0:T(8,128)(2,1)}), bf16[1024,2048]{1,0:T(8,128)(2,1)}) %all-gather.8.cloned.1.call-update) | async-done | bytes 4194320 | tf_op jit(solution)/shard_map/all_gather | solution.py:143
  336.4 14.7 %fusion.88 = f32[1024,2048]{1,0:T(8,128)} fusion(bf16[1024,2048]{1,0:T(8,128)(2,1)} %all-gather.8.cloned.1.call-done, bf16[2048,2048]{1,0:T(8,128)(2,1)} %param.32), kind=kOutput, calls=%fused_computation.157 | convolution fusion | flops 8589934592 | bytes 20971520 | tf_op jit(solution)/shard_map/dot_general | solution.py:144
  351.1 66.1 %all-gather.12.cloned.1.call-done = bf16[1,1024,2048]{2,1,0:T(8,128)(2,1)} async-done(((bf16[1,256,2048]{2,1,0:T(8,128)(2,1)}), bf16[1,1024,2048]{2,1,0:T(8,128)(2,1)}) %all-gather.12.cloned.1.call-update) | async-done | bytes 4194320 | tf_op jit(solution)/shard_map/all_gather | solution.py:159
  417.2 14.2 %fusion.41 = bf16[1024,2048]{1,0:T(8,128)(2,1)S(1)} fusion(f32[1024,2048]{1,0:T(8,128)} %fusion.88, s32[2048]{0:T(1024)S(1)} %iota_add_fusion.2, s32[1024]{0:T(1024)S(1)} %bitcast.224, bf16[2048,2048]{1,0:T(8,128)(2,1)} %param.33, bf16[1,1024,2048]{2,1,0:T(8,128)(2,1)} %all-gather.12.cloned.1.call-done), kind=kOutput, calls=%fused_computation.54 | convolution fusion | flops 8606711808 | bytes 25178112 | tf_op jit(solution)/shard_map/dot_general | solution.py:160
  433.4 12.7 %convolution_convert_fusion.1 = bf16[1024,2048]{1,0:T(8,128)(2,1)} fusion(bf16[1024,2048]{1,0:T(8,128)(2,1)S(1)} %fusion.41, bf16[2048,2048]{1,0:T(8,128)(2,1)} %param.32), kind=kOutput, calls=%fused_computation.61 | convolution fusion | flops 8592031744 | bytes 16777216 | tf_op jit(solution)/shard_map/dot_general | solution.py:168
  446.6 75.0 %reduce-scatter.15.cloned.1.call-done = bf16[256,2048]{1,0:T(8,128)(2,1)} async-done(((bf16[1024,2048]{1,0:T(8,128)(2,1)}), bf16[256,2048]{1,0:T(8,128)(2,1)}) %reduce-scatter.15.cloned.1.call-update) | async-done | bytes 1048592 | tf_op jit(solution)/shard_map/reduce_scatter | solution.py:167
  521.6 3.7 fusion.71
  525.4 3.4 fusion.81
  528.8 15.0 %convert_bitcast_fusion = bf16[2048,2048]{0,1:T(8,128)(2,1)} fusion(bf16[1,1024,2048]{2,1,0:T(8,128)(2,1)} %all-gather.12.cloned.1.call-done, f32[1024,2048]{1,0:T(8,128)} %fusion.88, s32[2048]{0:T(1024)S(1)} %iota_add_fusion.2, s32[1024]{0:T(1024)S(1)} %bitcast.225), kind=kOutput, calls=%fused_computation.55 | convolution fusion | flops 8604614656 | bytes 20983808 | tf_op jit(solution)/shard_map/dot_general | solution.py:59
  543.9 14.1 %convolution_convert_fusion = bf16[2048,2048]{1,0:T(8,128)(2,1)} fusion(bf16[1024,2048]{1,0:T(8,128)(2,1)} %all-gather.8.cloned.1.call-done, bf16[1024,2048]{1,0:T(8,128)(2,1)} %copy-done.64), kind=kOutput, calls=%fused_computation.57 | convolution fusion | flops 8594128896 | bytes 16777216 | tf_op jit(solution)/shard_map/dot_general | solution.py:59
  559.6 50.6 %all-gather.10.cloned.1.call-done = bf16[1024,2048]{1,0:T(8,128)(2,1)} async-done(((bf16[256,2048]{1,0:T(8,128)(2,1)}), bf16[1024,2048]{1,0:T(8,128)(2,1)}) %all-gather.10.cloned.1.call-update) | async-done | bytes 4194320 | tf_op jit(solution)/shard_map/all_gather | solution.py:177
  610.2 5.8 fusion.76
  619.4 6.8 convolution_convert_fusion.4
  628.1 38.4 %while.29 = (s32[]{:T(128)}, f32[1024,4,128]{0,2,1:T(8,128)S(1)}, f32[1024,4,128]{0,2,1:T(8,128)}, f32[2,512,4,128]{3,1,0,2:T(8,128)}, s32[2]{0:T(128)S(1)}, /*i...) while((s32[]{:T(128)}, f32[1024,4,128]{0,2,1:T(8,128)S(1)}, ...), condition=%wide.region_15.16_spmd.clone, body=%wide.region_13.15_spmd.clone.sunk | while | flops 2720266752 | bytes 125901240 | solution.py:210
  637.2 3.4 multiply_reduce_fusion.3
  656.5 3.4 multiply_reduce_fusion.3
  668.3 6.4 convolution_convert_fusion.5
  676.9 5.9 add_convert_fusion.1
  684.9 5.9 convolution_convert_fusion.7
  693.2 6.2 convolution_convert_fusion.6
  699.9 4.5 fusion.90
  704.4 5.6 fusion.89
  710.1 8.8 add_convert_fusion
  719.6 15.5 %convolution_convert_fusion.2 = bf16[1024,2048]{1,0:T(8,128)(2,1)} fusion(bf16[2048,2048]{1,0:T(8,128)(2,1)} %param.33, f32[1024,2048]{1,0:T(8,128)} %fusion.88, s32[2048]{0:T(1024)S(1)} %copy-done.57, s32[1024]{0:T(1024)S(1)} %bitcast.226), kind=kOutput, calls=%fused_computation.62 | convolution fusion | flops 8602517504 | bytes 20983808 | tf_op jit(solution)/shard_map/dot_general | solution.py:153
  739.4 19.2 %reduce-scatter.27.cloned.1.call-done = bf16[256,2048]{1,0:T(8,128)(2,1)} async-done(((bf16[2048,2048]{1,0:T(8,128)(2,1)}), bf16[256,2048]{1,0:T(8,128)(2,1)}) %reduce-scatter.27.cloned.1.call-update) | async-done | bytes 1048592 | tf_op jit(solution)/shard_map/reduce_scatter | solution.py:271
  761.4 41.7 %reduce-scatter.25.cloned.1.call-done = bf16[256,512]{1,0:T(8,128)(2,1)} async-done(((bf16[2048,512]{1,0:T(8,128)(2,1)}), bf16[256,512]{1,0:T(8,128)(2,1)}) %reduce-scatter.25.cloned.1.call-update) | async-done | bytes 262160 | tf_op jit(solution)/shard_map/reduce_scatter | solution.py:268
  804.9 42.9 %reduce-scatter.23.cloned.1.call-done = bf16[256,512]{1,0:T(8,128)(2,1)} async-done(((bf16[2048,512]{1,0:T(8,128)(2,1)}), bf16[256,512]{1,0:T(8,128)(2,1)}) %reduce-scatter.23.cloned.1.call-update) | async-done | bytes 262160 | tf_op jit(solution)/shard_map/reduce_scatter | solution.py:265
  849.6 42.7 %reduce-scatter.19.cloned.1.call-done = bf16[256,512]{1,0:T(8,128)(2,1)} async-done(((bf16[2048,512]{1,0:T(8,128)(2,1)}), bf16[256,512]{1,0:T(8,128)(2,1)}) %reduce-scatter.19.cloned.1.call-update) | async-done | bytes 262160 | tf_op jit(solution)/shard_map/reduce_scatter | solution.py:259
  894.2 42.9 %reduce-scatter.21.cloned.1.call-done = bf16[256,512]{1,0:T(8,128)(2,1)} async-done(((bf16[2048,512]{1,0:T(8,128)(2,1)}), bf16[256,512]{1,0:T(8,128)(2,1)}) %reduce-scatter.21.cloned.1.call-update) | async-done | bytes 262160 | tf_op jit(solution)/shard_map/reduce_scatter | solution.py:262
  938.9 77.3 %reduce-scatter.17.cloned.1.call-done = bf16[256,2048]{1,0:T(8,128)(2,1)} async-done(((bf16[1024,2048]{1,0:T(8,128)(2,1)}), bf16[256,2048]{1,0:T(8,128)(2,1)}) %reduce-scatter.17.cloned.1.call-update) | async-done | bytes 1048592 | tf_op jit(solution)/shard_map/reduce_scatter | solution.py:222
  1018.5 46.8 %all-reduce = (f32[2048]{0:T(1024)}, f32[2048]{0:T(1024)}, f32[2048]{0:T(1024)}, f32[2048]{0:T(1024)}, f32[4]{0:T(128)S(1)}, /*index=5*/f32[16]{0:T(128)S(1)}) all-reduce(f32[2048]{0:T(1024)S(1)} %get-tuple-element.379, f32[2048]{0:T(1024)S(1)} %get-tuple-element.384, ...), channel_id=1, replica_groups=mesh['dp'=8,'mp'=4] {'dp','mp'}, use_global_device_ids=true, to_apply=%region_20.21 | all-reduce | flops 8212 | bytes 65696 | tf_op jit(solution)/shard_map/psum | solution.py:246
  1066.4 30.4 %reduce-scatter.13.cloned.1.call-done = bf16[256,2048]{1,0:T(8,128)(2,1)} async-done(((bf16[1024,2048]{1,0:T(8,128)(2,1)}), bf16[256,2048]{1,0:T(8,128)(2,1)}) %reduce-scatter.13.cloned.1.call-update) | async-done | bytes 1048592 | tf_op jit(solution)/shard_map/reduce_scatter | solution.py:152
  1096.8 5.2 fusion.78
  (273 shorter events, 103.9 us)
Async XLA Ops:
  7.2 163.7 %copy-start = (bf16[2048,512]{1,0:T(8,128)(2,1)S(1)}, bf16[2048,512]{1,0:T(8,128)(2,1)}, u32[]{:S(2)}) copy-start(bf16[2048,512]{1,0:T(8,128)(2,1)} %param.29) | copy-start | bytes 6291460
  7.2 3.4 copy-start.3
  7.2 88.5 %all-gather.6.cloned.1.call-start = ((), (), s32[]{:S(2)}) async-start(), calls=%async_computation.10 | async-start | bytes 5242880 | tf_op jit(solution)/shard_map/all_gather | solution.py:92
  12.1 238.6 %reduce-scatter.11.cloned.1.call-start = ((), (), s32[]{:S(2)}) async-start(), calls=%async_computation.11 | async-start | bytes 5242880 | tf_op jit(solution)/shard_map/reduce_scatter | solution.py:136
  12.2 89.7 %copy-start.61 = (s32[4]{0:T(128)}, s32[4]{0:T(128)S(1)}, u32[]{:S(2)}) copy-start(s32[4]{0:T(128)S(1)} %iota_add_fusion.4) | copy-start | bytes 52
  15.2 115.5 %copy-start.16 = (f32[1024,64]{1,0:T(8,128)}, f32[1024,64]{1,0:T(8,128)S(1)}, u32[]{:S(2)}) copy-start(f32[1024,64]{1,0:T(8,128)S(1)} %get-tuple-element.455) | copy-start | bytes 786436
  15.3 115.5 %copy-start.18 = (f32[1024,64]{1,0:T(8,128)}, f32[1024,64]{1,0:T(8,128)S(1)}, u32[]{:S(2)}) copy-start(f32[1024,64]{1,0:T(8,128)S(1)} %get-tuple-element.456) | copy-start | bytes 786436
  175.2 78.2 %copy-start.34 = (f32[2048]{0:T(1024)S(1)}, f32[2048]{0:T(1024)}, u32[]{:S(2)}) copy-start(f32[2048]{0:T(1024)} %param.30) | copy-start | bytes 24580
  175.2 78.2 %copy-start.55 = (f32[2048]{0:T(1024)S(1)}, f32[2048]{0:T(1024)}, u32[]{:S(2)}) copy-start(f32[2048]{0:T(1024)} %param.31) | copy-start | bytes 24580
  175.2 161.2 %all-gather.8.cloned.1.call-start = ((), (), s32[]{:S(2)}) async-start(), calls=%async_computation.12 | async-start | bytes 5242880 | tf_op jit(solution)/shard_map/all_gather | solution.py:143
  252.8 272.5 %copy-start.38 = (f32[256]{0:T(256)}, f32[256]{0:T(256)S(1)}, u32[]{:S(2)}) copy-start(f32[256]{0:T(256)S(1)} %broadcast_multiply_fusion.4) | copy-start | bytes 3076
  253.4 271.9 %copy-start.44 = (f32[256]{0:T(256)}, f32[256]{0:T(256)S(1)}, u32[]{:S(2)}) copy-start(f32[256]{0:T(256)S(1)} %add_rsqrt_fusion) | copy-start | bytes 3076
  254.9 162.3 %all-gather.12.cloned.1.call-start = ((), (), s32[]{:S(2)}) async-start(), calls=%async_computation.23 | async-start | bytes 5242880 | tf_op jit(solution)/shard_map/all_gather | solution.py:159
  255.5 266.0 %reduce-scatter.15.cloned.1.call-start = ((), (), s32[]{:S(2)}) async-start(), calls=%async_computation.14 | async-start | bytes 5242880 | tf_op jit(solution)/shard_map/reduce_scatter | solution.py:167
  255.6 273.2 %copy-start.56 = (s32[2048]{0:T(1024)}, s32[2048]{0:T(1024)S(1)}, u32[]{:S(2)}) copy-start(s32[2048]{0:T(1024)S(1)} %iota_add_fusion.2) | copy-start | bytes 24580
  255.6 273.2 %copy-start.59 = (s32[1,1024]{1,0:T(1,128)}, s32[1,1024]{1,0:T(1,128)S(1)}, u32[]{:S(2)}) copy-start(s32[1,1024]{1,0:T(1,128)S(1)} %add_multiply_fusion) | copy-start | bytes 12292
  446.1 164.1 %all-gather.10.cloned.1.call-start = ((), (), s32[]{:S(2)}) async-start(), calls=%async_computation.15 | async-start | bytes 5242880 | tf_op jit(solution)/shard_map/all_gather | solution.py:177
  521.6 3.8 copy-start.5
  521.6 3.8 copy-start.11
  521.6 3.8 copy-start.13
  525.3 3.4 copy-start.50
  528.7 208.1 %reduce-scatter.29.cloned.1.call-start = ((), (), s32[]{:S(2)}) async-start(), calls=%async_computation.22 | async-start | bytes 9437184 | tf_op jit(solution)/shard_map/reduce_scatter | solution.py:274
  543.8 214.7 %reduce-scatter.27.cloned.1.call-start = ((), (), s32[]{:S(2)}) async-start(), calls=%async_computation.21 | async-start | bytes 9437184 | tf_op jit(solution)/shard_map/reduce_scatter | solution.py:271
  558.0 245.1 %reduce-scatter.25.cloned.1.call-start = ((), (), s32[]{:S(2)}) async-start(), calls=%async_computation.20 | async-start | bytes 2359296 | tf_op jit(solution)/shard_map/reduce_scatter | solution.py:268
  626.3 221.6 %reduce-scatter.23.cloned.1.call-start = ((), (), s32[]{:S(2)}) async-start(), calls=%async_computation.19 | async-start | bytes 2359296 | tf_op jit(solution)/shard_map/reduce_scatter | solution.py:265
  637.1 3.4 copy-start.25
  656.5 3.4 copy-start.25
  668.3 6.4 copy-start.20
  674.8 217.6 %reduce-scatter.19.cloned.1.call-start = ((), (), s32[]{:S(2)}) async-start(), calls=%async_computation.17 | async-start | bytes 2359296 | tf_op jit(solution)/shard_map/reduce_scatter | solution.py:259
  690.9 246.2 %reduce-scatter.21.cloned.1.call-start = ((), (), s32[]{:S(2)}) async-start(), calls=%async_computation.18 | async-start | bytes 2359296 | tf_op jit(solution)/shard_map/reduce_scatter | solution.py:262
  699.5 316.7 %reduce-scatter.17.cloned.1.call-start = ((), (), s32[]{:S(2)}) async-start(), calls=%async_computation.16 | async-start | bytes 5242880 | tf_op jit(solution)/shard_map/reduce_scatter | solution.py:222
  699.9 4.5 copy-start.32
  699.9 4.5 copy-start.63
  704.4 5.6 copy-start.21
  704.4 5.6 copy-start.23
  718.9 377.9 %reduce-scatter.13.cloned.1.call-start = ((), (), s32[]{:S(2)}) async-start(), calls=%async_computation.13 | async-start | bytes 5242880 | tf_op jit(solution)/shard_map/reduce_scatter | solution.py:152
  761.3 254.8 %copy-start.6 = (bf16[1,256,2048]{2,1,0:T(8,128)(2,1)S(1)}, bf16[1,256,2048]{2,1,0:T(8,128)(2,1)}, u32[]{:S(2)}) copy-start(bf16[1,256,2048]{2,1,0:T(8,128)(2,1)} %param.19) | copy-start | bytes 3145732
  761.3 254.8 %copy-start.37 = (f32[2048]{0:T(1024)S(1)}, f32[2048]{0:T(1024)}, u32[]{:S(2)}) copy-start(f32[2048]{0:T(1024)} %param.24) | copy-start | bytes 24580
  761.4 254.9 %copy-start.43 = (f32[256]{0:T(256)S(1)}, f32[256]{0:T(256)}, u32[]{:S(2)}) copy-start(f32[256]{0:T(256)} %copy-done.42) | copy-start | bytes 3076
  761.4 254.9 %copy-start.49 = (f32[256]{0:T(256)S(1)}, f32[256]{0:T(256)}, u32[]{:S(2)}) copy-start(f32[256]{0:T(256)} %copy-done.48) | copy-start | bytes 3076
  804.9 213.6 %copy-start.40 = (f32[2048]{0:T(1024)S(1)}, f32[2048]{0:T(1024)}, u32[]{:S(2)}) copy-start(f32[2048]{0:T(1024)} %get-tuple-element.377) | copy-start | bytes 24580
  804.9 213.6 %copy-start.41 = (f32[2048]{0:T(1024)S(1)}, f32[2048]{0:T(1024)}, u32[]{:S(2)}) copy-start(f32[2048]{0:T(1024)} %get-tuple-element.383) | copy-start | bytes 24580
  804.9 291.9 %copy-start.35 = (f32[2048]{0:T(1024)S(1)}, f32[2048]{0:T(1024)}, u32[]{:S(2)}) copy-start(f32[2048]{0:T(1024)} %param.30) | copy-start | bytes 24580
  804.9 291.9 %copy-start.39 = (f32[256]{0:T(256)S(1)}, f32[256]{0:T(256)}, u32[]{:S(2)}) copy-start(f32[256]{0:T(256)} %copy-done.38) | copy-start | bytes 3076
  804.9 291.9 %copy-start.45 = (f32[256]{0:T(256)S(1)}, f32[256]{0:T(256)}, u32[]{:S(2)}) copy-start(f32[256]{0:T(256)} %copy-done.44) | copy-start | bytes 3076
  804.9 291.9 %copy-start.51 = (f32[256]{0:T(256)S(1)}, f32[256]{0:T(256)}, u32[]{:S(2)}) copy-start(f32[256]{0:T(256)} %copy-done.50) | copy-start | bytes 3076
  804.9 291.9 %copy-start.53 = (f32[256]{0:T(256)S(1)}, f32[256]{0:T(256)}, u32[]{:S(2)}) copy-start(f32[256]{0:T(256)} %copy-done.52) | copy-start | bytes 3076
  1096.8 5.2 copy-start.1
  (41 other events, 83.9 us)
Sparse Core Ops, SparseCore 0:
  12.2 83.4 all-gather.5
  175.3 75.2 reduce-scatter.10
  255.1 81.2 all-gather.7
  337.9 79.2 all-gather.11
  446.2 75.2 reduce-scatter.14
  528.9 81.2 all-gather.9
  613.6 69.7 reduce-scatter.28
  687.3 71.2 reduce-scatter.26
  761.8 41.1 reduce-scatter.24
  806.6 41.2 reduce-scatter.22
  851.1 41.1 reduce-scatter.18
  895.8 41.2 reduce-scatter.20
  939.4 76.7 reduce-scatter.16
  1018.4 78.3 reduce-scatter.12
where the time goes:
time: 1110 us
  waiting for transfers between devices  726 us (65%)
  matrix products  192 us (17%)
  other arithmetic  69.3 us (6%)
  local copies, waits for them, and re-layouts  48.8 us (4%)
  blocking collectives  46.8 us (4%)
  between operations  14.8 us (1%)
    all_gather x1, waiting for transfers between devices, per_device(): lax.all_gather(second_out.astype(jnp.bfloat16), 'mp', axis=0, tiled=True)  80.7 us
    all_gather x1, waiting for transfers between devices, per_device(): lax.all_gather(normed_out.astype(jnp.bfloat16), 'mp', axis=0, tiled=True)  80.4 us
    reduce_scatter x1, waiting for transfers between devices, per_device(): lax.psum_scatter((total + jnp.dot(dv_low, value_weight.T, preferred_eleme...  77.3 us
    reduce_scatter x1, waiting for transfers between devices, per_device(): lax.psum_scatter(jnp.dot(piece, output_weight.T, preferred_element_type=j...  75.4 us
    reduce_scatter x1, waiting for transfers between devices, per_device(): lax.psum_scatter(jnp.dot(piece, up_weight.T, preferred_element_type=jnp.f...  75 us
    all_gather x1, waiting for transfers between devices, per_device(): grad_all = lax.all_gather(mixed_grad[0], 'mp', axis=0, tiled=True)  66.1 us
    dot_general x6, matrix products, outer(): lax.dot_general(left, right, (((0,), (0,)), ((), ())), preferred_element_...  54.5 us
    all_gather x1, waiting for transfers between devices, per_device(): lax.all_gather(grad_state.astype(jnp.bfloat16), 'mp', axis=0, tiled=True)  50.6 us
  transfers between devices with their start and end apart: 14, of which 13 were waited for; matrix products, arithmetic and copies ran while one was open for 16% of the time, Pallas kernels for 0%

commit v1 on v0

v1 whole, which is shorter than its diff:
```python
import functools
import jax
import jax.numpy as jnp
from jax import lax
from jax.experimental import pallas as pl
from jax.experimental.pallas import tpu as pltpu
from jax.sharding import PartitionSpec as P

HEADS = 16
E = 128
FF = 8192
EPS = 1e-05
DOC_MAX = 512
LOG2E = 1.4426950408889634
F32 = jnp.float32
BF16 = jnp.bfloat16
VMEM_LIMIT = 56 * 1024 * 1024


def params(**kw):
    return pltpu.CompilerParams(vmem_limit_bytes=VMEM_LIMIT, **kw)


def cost(flops, nbytes, trans=0):
    return pl.CostEstimate(flops=int(flops), bytes_accessed=int(nbytes), transcendentals=int(trans))


def norm_forward(values, gain, shift):
    mean = jnp.mean(values, axis=-1, keepdims=True)
    cent = values - mean
    inverse = lax.rsqrt(jnp.mean(cent * cent, axis=-1, keepdims=True) + EPS)
    normed = cent * inverse
    return (normed * gain + shift, normed, inverse)


def norm_backward(grad_out, normed, inverse, gain):
    scaled = grad_out * gain
    return inverse * (
        scaled
        - jnp.mean(scaled, axis=-1, keepdims=True)
        - normed * jnp.mean(scaled * normed, axis=-1, keepdims=True)
    )


def rotary_tables(length):
    half = E // 2
    freq = 10000.0 ** (-(jnp.arange(half, dtype=F32) * 2.0 / E))
    angle = jnp.arange(length, dtype=F32)[:, None] * freq[None, :]
    cos, sin = jnp.cos(angle), jnp.sin(angle)
    return jnp.concatenate([cos, cos], axis=1), jnp.concatenate([-sin, sin], axis=1)


def dot_t(left, right):
    return lax.dot_general(left, right, (((1,), (1,)), ((), ())), preferred_element_type=F32)


def dot_n(left, right):
    return lax.dot_general(left, right, (((1,), (0,)), ((), ())), preferred_element_type=F32)


def outer(left, right):
    return lax.dot_general(left, right, (((0,), (0,)), ((), ())), preferred_element_type=F32)


def qkv_body(rank_ref, x_ref, gain_ref, shift_ref, wq_ref, wk_ref, wv_ref, cos_ref, sin_ref, *rest):
    a_ref, q_ref, k_ref, v_ref = rest[-4:]

    @pl.when(pl.program_id(0) == 0)
    def _():
        out, _, _ = norm_forward(x_ref[...].astype(F32), gain_ref[...], shift_ref[...])
        a_ref[0] = out.astype(BF16)

    act = a_ref[0]
    cos, sin = cos_ref[0], sin_ref[0]
    v_ref[0] = dot_n(act, wv_ref[...]).astype(BF16)
    for w_ref, o_ref in ((wq_ref, q_ref), (wk_ref, k_ref)):
        lin = dot_n(act, w_ref[...])
        for j in range(lin.shape[1] // E):
            part = lin[:, j * E : (j + 1) * E]
            turned = part * cos + pltpu.roll(part, E // 2, 1) * sin
            o_ref[0, :, j * E : (j + 1) * E] = turned.astype(BF16)


def qkv_slot(slot, n, rank, x, gain, shift, wq, wk, wv, cos, sin, held):
    rows, d = x.shape
    local = wq.shape[1]
    cb = min(256, local)
    whole = lambda j, r: (0, 0)
    wspec = pl.BlockSpec((d, cb), lambda j, r: (0, j))
    tspec = pl.BlockSpec((1, rows, E), lambda j, r: (lax.rem(r[0] + slot, n), 0, 0))
    in_specs = [
        pl.BlockSpec((rows, d), whole),
        pl.BlockSpec((1, d), whole),
        pl.BlockSpec((1, d), whole),
        wspec,
        wspec,
        wspec,
        tspec,
        tspec,
    ]
    extra = [] if held is None else list(held)
    aliases = {} if held is None else {9 + i: i for i in range(4)}
    ospec = pl.BlockSpec((1, rows, cb), lambda j, r: (slot, 0, j))
    return pl.pallas_call(
        qkv_body,
        grid_spec=pltpu.PrefetchScalarGridSpec(
            num_scalar_prefetch=1,
            grid=(local // cb,),
            in_specs=in_specs + [pl.BlockSpec(memory_space=pl.ANY)] * len(extra),
            out_specs=[pl.BlockSpec((1, rows, d), lambda j, r: (slot, 0, 0)), ospec, ospec, ospec],
        ),
        out_shape=[jax.ShapeDtypeStruct((n, rows, d), BF16)]
        + [jax.ShapeDtypeStruct((n, rows, local), BF16)] * 3,
        input_output_aliases=aliases,
        compiler_params=params(),
        cost_estimate=cost(6 * rows * d * local, 6 * d * local + 4 * rows * d),
        name="qkv_slot",
    )(rank, x, gain, shift, wq, wk, wv, cos, sin, *extra)


def first_key(block, rows):
    return max(0, block - (DOC_MAX - 1 + rows - 1) // rows)


def attend_body(rank_ref, q_ref, k_ref, v_ref, dcol_ref, drow_ref, hc_ref, o_ref):
    n, rows, _ = q_ref.shape
    rank = rank_ref[0]
    head = rank_ref[1] + pl.program_id(0)
    slot = lambda b: lax.rem(b + n - rank, n)
    factor = E ** (-0.5) * LOG2E
    low = lax.broadcasted_iota(jnp.int32, (rows, rows), 0) >= lax.broadcasted_iota(
        jnp.int32, (rows, rows), 1
    )
    for b in range(n):
        q = q_ref[slot(b)]
        doc = dcol_ref[b]
        keys = range(first_key(b, rows), b + 1)
        scores = []
        for c in keys:
            s = dot_t(q, k_ref[slot(c)])
            ok = doc == drow_ref[c]
            if c == b:
                ok = ok & low
            scores.append(jnp.where(ok, s, -1e30))
        top = scores[0]
        for s in scores[1:]:
            top = jnp.maximum(top, s)
        top = jnp.max(top, axis=1, keepdims=True)
        total = None
        out = None
        for c, s in zip(keys, scores):
            p = jnp.exp2((s - top) * factor)
            total = p if total is None else total + p
            o = dot_n(p.astype(BF16), v_ref[slot(c)])
            out = o if out is None else out + o
        total = jnp.sum(total, axis=1, keepdims=True)
        gate = jnp.where(hc_ref[b] > head, 1.0, 0.0)
        o_ref[slot(b)] = (out * (gate / total)).astype(BF16)


def attend(rank, q, k, v, docs_col, docs_row, heads_col):
    n, rows, local = q.shape
    spec = pl.BlockSpec((n, rows, E), lambda h, r: (0, 0, h))
    col = pl.BlockSpec((n, rows, 1), lambda h, r: (0, 0, 0))
    row = pl.BlockSpec((n, 1, rows), lambda h, r: (0, 0, 0))
    t = n * rows
    return pl.pallas_call(
        attend_body,
        grid_spec=pltpu.PrefetchScalarGridSpec(
            num_scalar_prefetch=1,
            grid=(local // E,),
            in_specs=[spec, spec, spec, col, row, col],
            out_specs=spec,
        ),
        out_shape=jax.ShapeDtypeStruct((n, rows, local), BF16),
        compiler_params=params(),
        cost_estimate=cost(4 * t * t * local, 8 * t * local, t * t * local // E),
        name="attend",
    )(rank, q, k, v, docs_col, docs_row, heads_col)


def attend_back_body(
    rank_ref, q_ref, k_ref, v_ref, do_ref, dcol_ref, drow_ref, hc_ref, cos_ref, sin_ref, out_ref, dk_ref, dv_ref
):
    n, rows, _ = q_ref.shape
    rank = rank_ref[0]
    head = rank_ref[1] + pl.program_id(0)
    slot = lambda b: lax.rem(b + n - rank, n)
    scale = E ** (-0.5)
    factor = scale * LOG2E
    low = lax.broadcasted_iota(jnp.int32, (rows, rows), 0) <= lax.broadcasted_iota(
        jnp.int32, (rows, rows), 1
    )
    dk_ref[...] = jnp.zeros_like(dk_ref)
    dv_ref[...] = jnp.zeros_like(dv_ref)

    def unrotate(w, b):
        w = w * scale
        return (w * cos_ref[b] - pltpu.roll(w, E // 2, 1) * sin_ref[b]).astype(BF16)

    for b in range(n):
        q = q_ref[slot(b)]
        grad = jnp.where(hc_ref[b] > head, do_ref[slot(b)].astype(F32), 0.0).astype(BF16)
        keys = range(first_key(b, rows), b + 1)
        scores = []
        for c in keys:
            s = dot_t(k_ref[slot(c)], q)
            ok = dcol_ref[c] == drow_ref[b]
            if c == b:
                ok = ok & low
            scores.append(jnp.where(ok, s, -1e30))
        top = scores[0]
        for s in scores[1:]:
            top = jnp.maximum(top, s)
        top = jnp.max(top, axis=0, keepdims=True)
        probs = [jnp.exp2((s - top) * factor) for s in scores]
        total = probs[0]
        for p in probs[1:]:
            total = total + p
        inv = 1.0 / jnp.sum(total, axis=0, keepdims=True)
        probs = [p * inv for p in probs]
        dprobs = [dot_t(v_ref[slot(c)], grad) for c in keys]
        delta = None
        for p, g in zip(probs, dprobs):
            delta = p * g if delta is None else delta + p * g
        delta = jnp.sum(delta, axis=0, keepdims=True)
        dq = None
        for c, p, g in zip(keys, probs, dprobs):
            ds = (p * (g - delta)).astype(BF16)
            dk_ref[c] += dot_n(ds, q)
            dv_ref[c] += dot_n(p.astype(BF16), grad)
            part = outer(ds, k_ref[slot(c)])
            dq = part if dq is None else dq + part
        out_ref[slot(b), :, :E] = unrotate(dq, b)
    for b in range(n):
        out_ref[slot(b), :, E : 2 * E] = unrotate(dk_ref[b], b)
        out_ref[slot(b), :, 2 * E :] = dv_ref[b].astype(BF16)


def attend_back(rank, q, k, v, do, docs_col, docs_row, heads_col, cos, sin):
    n, rows, local = q.shape
    spec = pl.BlockSpec((n, rows, E), lambda h, r: (0, 0, h))
    col = pl.BlockSpec((n, rows, 1), lambda h, r: (0, 0, 0))
    row = pl.BlockSpec((n, 1, rows), lambda h, r: (0, 0, 0))
    table = pl.BlockSpec((n, rows, E), lambda h, r: (0, 0, 0))
    t = n * rows
    return pl.pallas_call(
        attend_back_body,
        grid_spec=pltpu.PrefetchScalarGridSpec(
            num_scalar_prefetch=1,
            grid=(local // E,),
            in_specs=[spec, spec, spec, spec, col, row, col, table, table],
            out_specs=pl.BlockSpec((n, rows, 3 * E), lambda h, r: (0, 0, h)),
            scratch_shapes=[pltpu.VMEM((n, rows, E), F32), pltpu.VMEM((n, rows, E), F32)],
        ),
        out_shape=jax.ShapeDtypeStruct((n, rows, 3 * local), BF16),
        compiler_params=params(),
        cost_estimate=cost(8 * t * t * local, 14 * t * local, t * t * local // E),
        name="attend_back",
    )(rank, q, k, v, do, docs_col, docs_row, heads_col, cos, sin)


def mlp_body(rank_ref, a_ref, g_ref, up_ref, down_ref, bucket_ref, *rest):
    r_ref, du_ref, aa_ref, ga_ref = rest[-4:]
    rows, cb = a_ref.shape[0], up_ref.shape[1]

    @pl.when(pl.program_id(0) == 0)
    def _():
        aa_ref[0] = a_ref[...]
        ga_ref[0] = g_ref[...]

    u = dot_n(a_ref[...], up_ref[...])
    dr = dot_n(g_ref[...], down_ref[...]).astype(BF16).astype(F32)
    column = rank_ref[2] + pl.program_id(0) * cb + lax.broadcasted_iota(jnp.int32, (rows, cb), 1)
    lifted = jnp.where(column < (bucket_ref[0] + 1) * (FF // 4), jnp.maximum(u, 0.0), 0.0)
    r_ref[0] = (lifted * lifted).astype(BF16)
    du_ref[0] = (dr * (2.0 * lifted)).astype(BF16)


def mlp_slot(slot, n, rank, act, grad, up, down, bucket_col, held):
    rows, d = act.shape
    hidden = up.shape[1]
    cb = min(512, hidden)
    whole = lambda j, r: (0, 0)
    wspec = pl.BlockSpec((d, cb), lambda j, r: (0, j))
    extra = [] if held is None else list(held)
    aliases = {} if held is None else {6 + i: i for i in range(4)}
    ospec = pl.BlockSpec((1, rows, cb), lambda j, r: (slot, 0, j))
    aspec = pl.BlockSpec((1, rows, d), lambda j, r: (slot, 0, 0))
    return pl.pallas_call(
        mlp_body,
        grid_spec=pltpu.PrefetchScalarGridSpec(
            num_scalar_prefetch=1,
            grid=(hidden // cb,),
            in_specs=[
                pl.BlockSpec((rows, d), whole),
                pl.BlockSpec((rows, d), whole),
                wspec,
                wspec,
                pl.BlockSpec((1, rows, 1), lambda j, r: (lax.rem(r[0] + slot, n), 0, 0)),
            ]
            + [pl.BlockSpec(memory_space=pl.ANY)] * len(extra),
            out_specs=[ospec, ospec, aspec, aspec],
        ),
        out_shape=[jax.ShapeDtypeStruct((n, rows, hidden), BF16)] * 2
        + [jax.ShapeDtypeStruct((n, rows, d), BF16)] * 2,
        input_output_aliases=aliases,
        compiler_params=params(),
        cost_estimate=cost(4 * rows * d * hidden, 4 * d * hidden + 4 * rows * (d + hidden)),
        name="mlp_slot",
    )(rank, act, grad, up, down, bucket_col, *extra)


def xor_sum(vec, axis, size):
    step = 1
    while step < size:
        vec = vec + lax.ppermute(vec, axis, [(i, i ^ step) for i in range(size)])
        step *= 2
    return vec


def per_device(
    n,
    n_dp,
    tokens,
    mixed_grad,
    doc_ids,
    head_count,
    width_bucket,
    first_gain,
    first_shift,
    query_weight,
    key_weight,
    value_weight,
    output_weight,
    second_gain,
    second_shift,
    up_weight,
    down_weight,
):
    rank = lax.axis_index("mp")
    rows, d = tokens.shape[1:]
    local = query_weight.shape[1]
    local_heads = local // E
    hidden = up_weight.shape[1]
    length = n * rows
    own = tokens[0]
    ring = [(i, (i - 1) % n) for i in range(n)]
    hop = lambda v: lax.ppermute(v, "mp", ring)
    where = jnp.stack([rank, rank * local_heads, rank * hidden]).astype(jnp.int32)
    docs_col = doc_ids.reshape(n, rows, 1)
    docs_row = doc_ids.reshape(n, 1, rows)
    heads_col = head_count.reshape(n, rows, 1)
    bucket_col = width_bucket.reshape(n, rows, 1)
    cos, sin = (t.reshape(n, rows, E) for t in rotary_tables(length))
    gain1, shift1 = first_gain[None], first_shift[None]
    gain2, shift2 = second_gain[None], second_shift[None]

    held, block = None, own
    for s in range(n):
        after = hop(block) if s < n - 1 else None
        held = qkv_slot(
            s, n, where, block, gain1, shift1, query_weight, key_weight, value_weight, cos, sin, held
        )
        block = after
    first_all, query, keys, vals = held
    masked = attend(where, query, keys, vals, docs_col, docs_row, heads_col)

    grads = [mixed_grad[0]]
    for s in range(n - 1):
        grads.append(hop(grads[-1]))

    def scatter_ring(term):
        moved = None
        for s in range(1, n):
            t = term(s)
            moved = hop((t if moved is None else t + moved.astype(F32)).astype(BF16))
        return term(0).astype(BF16).astype(F32) + moved.astype(F32)

    attn = scatter_ring(lambda s: dot_t(masked[s], output_weight))
    x_rows = own.astype(F32)
    state = x_rows + attn
    second_out, normed_two, inverse_two = norm_forward(state, gain2, shift2)

    held, block = None, second_out.astype(BF16)
    for s in range(n):
        after = hop(block) if s < n - 1 else None
        held = mlp_slot(s, n, where, block, grads[s], up_weight, down_weight, bucket_col, held)
        block = after
    active, grad_upper, second_all, grad_all = held
    grad_second = scatter_ring(lambda s: dot_t(grad_upper[s], up_weight))
    back_two = norm_backward(grad_second, normed_two, inverse_two, gain2)
    second_gain_part = jnp.sum(grad_second * normed_two, axis=0)
    second_shift_part = jnp.sum(grad_second, axis=0)
    grad_state = mixed_grad[0].astype(F32) + back_two

    flat = lambda v: v.reshape(length, v.shape[-1])
    scatter = lambda v: lax.psum_scatter(v.astype(BF16), "dp", scatter_dimension=0, tiled=True)
    down_grad = scatter(outer(flat(grad_all), flat(active)))
    up_grad = scatter(outer(flat(second_all), flat(grad_upper)))

    states = [grad_state.astype(BF16)]
    for s in range(n - 1):
        states.append(hop(states[-1]))
    grad_masked = jnp.stack([dot_n(v, output_weight).astype(BF16) for v in states])
    state_all = jnp.concatenate(states)
    output_grad = scatter(outer(state_all, flat(masked)))
    mixed = (state + scatter_ring(lambda s: dot_t(active[s], down_weight))).astype(BF16)

    dqkv = attend_back(
        where, query, keys, vals, grad_masked, docs_col, docs_row, heads_col, cos, sin
    )
    weights = jnp.stack(
        [w.reshape(d, local_heads, E) for w in (query_weight, key_weight, value_weight)], axis=2
    ).reshape(d, 3 * local)
    term = outer(flat(first_all), flat(dqkv)).astype(BF16)
    qkv_grad = scatter(term)
    grad_first = scatter_ring(lambda s: dot_t(dqkv[s], weights))
    n1_out, normed_one, inverse_one = norm_forward(x_rows, gain1, shift1)
    back_one = norm_backward(grad_first, normed_one, inverse_one, gain1)
    input_grad = (grad_state + back_one).astype(BF16)

    wide = weights.astype(F32)
    total_d = jnp.sum(flat(dqkv).astype(F32), axis=0)
    first_shift_part = jnp.sum(wide * total_d[None], axis=1)
    product = jnp.sum(wide * term.astype(F32), axis=1)
    first_gain_part = (product - first_shift * first_shift_part) / first_gain

    lead = (rank == 0).astype(F32)
    bucket_part = lead * jnp.sum(
        (width_bucket[0][:, None] == jnp.arange(4, dtype=jnp.int32)[None, :]).astype(F32), axis=0
    )
    head_part = lead * jnp.sum(
        (head_count[0][:, None] == jnp.arange(1, HEADS + 1, dtype=jnp.int32)[None, :]).astype(F32),
        axis=0,
    )
    small = jnp.concatenate(
        [
            first_gain_part,
            first_shift_part,
            second_gain_part,
            second_shift_part,
            bucket_part,
            head_part,
            jnp.zeros((128 - 4 - HEADS,), F32),
        ]
    )
    small = xor_sum(xor_sum(small, "dp", n_dp), "mp", n)
    qkv_grad = qkv_grad.reshape(-1, local_heads, 3, E).astype(F32)
    pick = lambda i: qkv_grad[:, :, i].reshape(-1, local)
    return (
        mixed[None],
        input_grad[None],
        small[:d],
        small[d : 2 * d],
        pick(0),
        pick(1),
        pick(2),
        output_grad.astype(F32),
        small[2 * d : 3 * d],
        small[3 * d : 4 * d],
        up_grad.astype(F32),
        down_grad.astype(F32),
        small[4 * d : 4 * d + 4].astype(jnp.int32),
        small[4 * d + 4 : 4 * d + 4 + HEADS].astype(jnp.int32),
    )


def solution(mesh):
    token, seq, copy, col = P("dp", "mp", None), P("dp", None), P(), P(None, "mp")
    grad = P("dp", "mp")
    return jax.shard_map(
        functools.partial(per_device, mesh.shape["mp"], mesh.shape["dp"]),
        mesh=mesh,
        in_specs=(token, token, seq, seq, seq, copy, copy, col, col, col, col, copy, copy, col, col),
        out_specs=(token, token, copy, copy, grad, grad, grad, grad, copy, copy, grad, grad, copy, copy),
        check_vma=False,
    )
```

time: 1110 us -> 762 us (0.69)
  waiting for transfers between devices: 726 us -> 378 us
  Pallas kernels: 0 us -> 99.3 us
  starting transfers between devices: 1.94 us -> 92.3 us
  matrix products: 192 us -> 109 us
  blocking collectives: 46.8 us -> 0 us
  other arithmetic: 69.3 us -> 30.4 us
  local copies, waits for them, and re-layouts: 48.8 us -> 27.9 us
    reduce_scatter x10 -> x4, waiting for transfers between devices: 448 us -> 19.4 us  [per_device(): lax.psum_scatter(v.astype(BF16), 'dp', scatter_dimension=0, tiled=True)]
    ppermute x0 -> x29, waiting for transfers between devices: none -> 358 us  [the longest x24 335 us: per_device(): hop = lambda v: lax.ppermute(v, 'mp', ring)]
    all_gather x4 -> x0, waiting for transfers between devices: 278 us -> none  [the longest x1 80.7 us: per_device(): lax.all_gather(second_out.astype(jnp.bfloat16), 'mp', axis=0, tiled=True)]
    pallas_call x0 -> x10, Pallas kernels: none -> 99.3 us  [the longest x4 44.4 us: mlp_slot(): pl.pallas_call(mlp_body, grid_spec=pltpu.PrefetchScalarGridSpec(num_scala...]
    ppermute x0 -> x29, starting transfers between devices: none -> 91.8 us  [the longest x24 87.4 us: per_device(): hop = lambda v: lax.ppermute(v, 'mp', ring)]
    dot_general x26 -> x20, matrix products: 138 us -> 68.2 us  [the longest x16 64.1 us: dot_t(): lax.dot_general(left, right, (((1,), (1,)), ((), ())), preferred_element_...]
    psum x1 -> x0, blocking collectives: 46.8 us -> none  [per_device(): lax.psum((first_gain_part, first_shift_part, second_gain_part, second_shi...]
    unnamed x117 -> x81, local copies, waits for them, and re-layouts: 26 us -> 5.71 us
  transfers between devices with their start and end apart: 14 -> 33, of which waited for: 13 -> 24; matrix products, arithmetic and copies ran while one was open for 16% -> 17% of each run, Pallas kernels for 0% -> 9%
where the time goes in v1:
time: 762 us; the launch traced here: 752 us
  waiting for transfers between devices  378 us (50%)
  matrix products  109 us (14%)
  Pallas kernels  99.3 us (13%)
  starting transfers between devices  92.3 us (12%)
  other arithmetic  30.4 us (4%)
  local copies, waits for them, and re-layouts  27.9 us (4%)
  between operations  14.6 us (2%)
    ppermute x24, waiting for transfers between devices, per_device(): hop = lambda v: lax.ppermute(v, 'mp', ring)  335 us
    ppermute x24, starting transfers between devices, per_device(): hop = lambda v: lax.ppermute(v, 'mp', ring)  87.4 us
    dot_general x16, matrix products, dot_t(): lax.dot_general(left, right, (((1,), (1,)), ((), ())), preferred_element_...  64.1 us
    pallas_call x4, Pallas kernels, mlp_slot(): pl.pallas_call(mlp_body, grid_spec=pltpu.PrefetchScalarGridSpec(num_scala...  44.4 us
    dot_general x4, matrix products, outer(): lax.dot_general(left, right, (((0,), (0,)), ((), ())), preferred_element_...  41.2 us
    pallas_call x4, Pallas kernels, qkv_slot(): pl.pallas_call(qkv_body, grid_spec=pltpu.PrefetchScalarGridSpec(num_scala...  28.2 us
    ppermute x5, waiting for transfers between devices, xor_sum(): vec = vec + lax.ppermute(vec, axis, [(i, i ^ step) for i in range(size)])  23 us
    reduce_scatter x4, waiting for transfers between devices, per_device(): lax.psum_scatter(v.astype(BF16), 'dp', scatter_dimension=0, tiled=True)  19.4 us
  transfers between devices with their start and end apart: 33, of which 24 were waited for; matrix products, arithmetic and copies ran while one was open for 17% of the time, Pallas kernels for 9%

profile of v1, /device:TPU:0, one launch (start us, length us, event | category | flops | bytes accessed | tf_op | source)
XLA Modules:
  0.0 751.8 jit_solution(17653122278493206884)
XLA Ops:
  7.2 5.1 collective-permute-start
  12.3 22.7 %collective-permute-done.x_ref = bf16[256,2048]{1,0:T(8,128)(2,1)} collective-permute-done((bf16[256,2048]{1,0:T(8,128)(2,1)}, bf16[256,2048]{1,0:T(8,128)(2,1)}, u32[]{:S(2)}, u32[]{:S(2)}) %collective-permute-start) | collective-permute-done | bytes 1048608 | tf_op jit(solution)/shard_map/ppermute | solution.py:349
  44.8 16.4 %collective-permute-done.1.x_ref = bf16[256,2048]{1,0:T(8,128)(2,1)S(1)} collective-permute-done((bf16[256,2048]{1,0:T(8,128)(2,1)}, bf16[256,2048]{1,0:T(8,128)(2,1)S(1)}, u32[]{:S(2)}, u32[]{:S(2)}) %collective-permute-start.1) | collective-permute-done | bytes 1048608 | tf_op jit(solution)/shard_map/ppermute | solution.py:349
  69.2 7.0 qkv_slot.4
  76.3 7.1 qkv_slot.5
  83.3 7.0 qkv_slot.6
  91.3 7.0 qkv_slot.7
  98.4 10.2 %attend.1 = bf16[4,256,512]{2,1,0:T(8,128)(2,1)} custom-call(s32[3]{0:T(128)} %pad_add_fusion.rank_ref, bf16[4,256,512]{2,1,0:T(8,128)(2,1)} %get-tuple-element.58.q_ref, bf16[4,256,512]{2,1,0:T(8,128)(2,1)} %get-tuple-element.59.k_ref, bf16[4,256,512]{2,1,0:T(8,128)(2,1)} %get-tuple-element.60.v_ref, s32[4,256,1]{2,1,0:T(8,128)} %reshape.171.dcol_ref, ...), custom_call_target="tpu_custom_call" | custom-call | flops 2147483648 | bytes 4194304 | tf_op jit(solution)/shard_map/attend/pallas_call | solution.py:167
  110.6 22.7 %collective-permute-done.3 = bf16[256,2048]{1,0:T(8,128)(2,1)S(1)} collective-permute-done((bf16[256,2048]{1,0:T(8,128)(2,1)S(1)}, bf16[256,2048]{1,0:T(8,128)(2,1)S(1)}, u32[]{:S(2)}, u32[]{:S(2)}) %collective-permute-start.3) | collective-permute-done | bytes 1048608 | tf_op jit(solution)/shard_map/ppermute | solution.py:349
  136.6 20.1 %collective-permute-done.4 = bf16[256,2048]{1,0:T(8,128)(2,1)S(1)} collective-permute-done((bf16[256,2048]{1,0:T(8,128)(2,1)S(1)}, bf16[256,2048]{1,0:T(8,128)(2,1)S(1)}, u32[]{:S(2)}, u32[]{:S(2)}) %collective-permute-start.4) | collective-permute-done | bytes 1048608 | tf_op jit(solution)/shard_map/ppermute | solution.py:349
  161.5 23.5 %collective-permute-done.5 = bf16[256,2048]{1,0:T(8,128)(2,1)S(1)} collective-permute-done((bf16[256,2048]{1,0:T(8,128)(2,1)S(1)}, bf16[256,2048]{1,0:T(8,128)(2,1)S(1)}, u32[]{:S(2)}, u32[]{:S(2)}) %collective-permute-start.5) | collective-permute-done | bytes 1048608 | tf_op jit(solution)/shard_map/ppermute | solution.py:349
  191.6 16.0 %collective-permute-done.9.g_ref = bf16[256,2048]{1,0:T(8,128)(2,1)} collective-permute-done((bf16[256,2048]{1,0:T(8,128)(2,1)S(1)}, bf16[256,2048]{1,0:T(8,128)(2,1)}, u32[]{:S(2)}, u32[]{:S(2)}) %collective-permute-start.9) | collective-permute-done | bytes 1048608 | tf_op jit(solution)/shard_map/ppermute | solution.py:349
  207.5 4.4 collective-permute-start.10
  211.9 18.1 %collective-permute-done.6.a_ref = bf16[256,2048]{1,0:T(8,128)(2,1)} collective-permute-done((bf16[256,2048]{1,0:T(8,128)(2,1)S(1)}, bf16[256,2048]{1,0:T(8,128)(2,1)}, u32[]{:S(2)}, u32[]{:S(2)}) %collective-permute-start.6) | collective-permute-done | bytes 1048608 | tf_op jit(solution)/shard_map/ppermute | solution.py:349
  230.0 4.4 collective-permute-start.7
  236.2 16.4 %collective-permute-done.10.g_ref = bf16[256,2048]{1,0:T(8,128)(2,1)} collective-permute-done((bf16[256,2048]{1,0:T(8,128)(2,1)}, bf16[256,2048]{1,0:T(8,128)(2,1)}, u32[]{:S(2)}, u32[]{:S(2)}) %collective-permute-start.10) | collective-permute-done | bytes 1048608 | tf_op jit(solution)/shard_map/ppermute | solution.py:349
  256.8 18.2 %collective-permute-done.7.a_ref = bf16[256,2048]{1,0:T(8,128)(2,1)} collective-permute-done((bf16[256,2048]{1,0:T(8,128)(2,1)}, bf16[256,2048]{1,0:T(8,128)(2,1)}, u32[]{:S(2)}, u32[]{:S(2)}) %collective-permute-start.7) | collective-permute-done | bytes 1048608 | tf_op jit(solution)/shard_map/ppermute | solution.py:349
  279.3 10.9 %mlp_slot.4 = (bf16[4,256,2048]{2,1,0:T(8,128)(2,1)}, bf16[4,256,2048]{2,1,0:T(8,128)(2,1)}, bf16[4,256,2048]{2,1,0:T(8,128)(2,1)}, bf16[4,256,2048]{2,1,0:T(8,128)(2,1)}) custom-call(s32[3]{0:T(128)} %pad_add_fusion.rank_ref, bf16[256,2048]{1,0:T(8,128)(2,1)} %copy-done.13, bf16[256,2048]{1,0:T(8,128)(2,1)} %bitcast.158, bf16[2048,2048]{1,0:T(8,128)(2,1)} %up_ref.7, ...), custom_call_target="tpu_custom_call" | custom-call | flops 4294967296 | bytes 20971520 | tf_op jit(solution)/shard_map/mlp_slot/pallas_call | solution.py:290
  290.2 11.2 %mlp_slot.5 = (bf16[4,256,2048]{2,1,0:T(8,128)(2,1)}, bf16[4,256,2048]{2,1,0:T(8,128)(2,1)}, bf16[4,256,2048]{2,1,0:T(8,128)(2,1)}, bf16[4,256,2048]{2,1,0:T(8,128)(2,1)}) custom-call(s32[3]{0:T(128)} %pad_add_fusion.rank_ref, ...), custom_call_target="tpu_custom_call", output_to_operand_aliasing={{0}: (6, {}), {1}: (7, {}), {2}: (8, {}), {3}: (9, {})} | custom-call | flops 4294967296 | bytes 20971520 | tf_op jit(solution)/shard_map/mlp_slot/pallas_call | solution.py:290
  301.4 11.1 %mlp_slot.6 = (bf16[4,256,2048]{2,1,0:T(8,128)(2,1)}, bf16[4,256,2048]{2,1,0:T(8,128)(2,1)}, bf16[4,256,2048]{2,1,0:T(8,128)(2,1)}, bf16[4,256,2048]{2,1,0:T(8,128)(2,1)}) custom-call(s32[3]{0:T(128)} %pad_add_fusion.rank_ref, ...), custom_call_target="tpu_custom_call", output_to_operand_aliasing={{0}: (6, {}), {1}: (7, {}), {2}: (8, {}), {3}: (9, {})} | custom-call | flops 4294967296 | bytes 20971520 | tf_op jit(solution)/shard_map/mlp_slot/pallas_call | solution.py:290
  316.1 11.2 %mlp_slot.7 = (bf16[4,256,2048]{2,1,0:T(8,128)(2,1)}, bf16[4,256,2048]{2,1,0:T(8,128)(2,1)}, bf16[4,256,2048]{2,1,0:T(8,128)(2,1)}, bf16[4,256,2048]{2,1,0:T(8,128)(2,1)}) custom-call(s32[3]{0:T(128)} %pad_add_fusion.rank_ref, bf16[256,2048]{1,0:T(8,128)(2,1)} %copy-done.17, ...), custom_call_target="tpu_custom_call", output_to_operand_aliasing={{0}: (6, {}), {1}: (7, {}), {2}: (8, {}), {3}: (9, {})} | custom-call | flops 4294967296 | bytes 20971520 | tf_op jit(solution)/shard_map/mlp_slot/pallas_call | solution.py:290
  327.3 6.2 convolution_convert_fusion.4
  337.7 17.9 %collective-permute-done.15 = bf16[256,2048]{1,0:T(8,128)(2,1)S(1)} collective-permute-done((bf16[256,2048]{1,0:T(8,128)(2,1)S(1)}, bf16[256,2048]{1,0:T(8,128)(2,1)S(1)}, u32[]{:S(2)}, u32[]{:S(2)}) %collective-permute-start.15) | collective-permute-done | bytes 1048608 | tf_op jit(solution)/shard_map/ppermute | solution.py:349
  355.6 5.7 fusion.14
  361.4 4.5 collective-permute-start.16
  365.9 16.9 %collective-permute-done.16 = bf16[256,2048]{1,0:T(8,128)(2,1)S(1)} collective-permute-done((bf16[256,2048]{1,0:T(8,128)(2,1)S(1)}, bf16[256,2048]{1,0:T(8,128)(2,1)S(1)}, u32[]{:S(2)}, u32[]{:S(2)}) %collective-permute-start.16) | collective-permute-done | bytes 1048608 | tf_op jit(solution)/shard_map/ppermute | solution.py:349
  389.6 16.0 %collective-permute-done.17 = bf16[256,2048]{1,0:T(8,128)(2,1)S(1)} collective-permute-done((bf16[256,2048]{1,0:T(8,128)(2,1)S(1)}, bf16[256,2048]{1,0:T(8,128)(2,1)S(1)}, u32[]{:S(2)}, u32[]{:S(2)}) %collective-permute-start.17) | collective-permute-done | bytes 1048608 | tf_op jit(solution)/shard_map/ppermute | solution.py:349
  415.4 19.0 %collective-permute-done.18 = bf16[256,2048]{1,0:T(8,128)(2,1)S(1)} collective-permute-done((bf16[256,2048]{1,0:T(8,128)(2,1)S(1)}, bf16[256,2048]{1,0:T(8,128)(2,1)S(1)}, u32[]{:S(2)}, u32[]{:S(2)}) %collective-permute-start.18) | collective-permute-done | bytes 1048608 | tf_op jit(solution)/shard_map/ppermute | solution.py:349
  438.7 19.0 %collective-permute-done.19 = bf16[256,2048]{1,0:T(8,128)(2,1)S(1)} collective-permute-done((bf16[256,2048]{1,0:T(8,128)(2,1)S(1)}, bf16[256,2048]{1,0:T(8,128)(2,1)S(1)}, u32[]{:S(2)}, u32[]{:S(2)}) %collective-permute-start.19) | collective-permute-done | bytes 1048608 | tf_op jit(solution)/shard_map/ppermute | solution.py:349
  462.0 13.4 %collective-permute-done.20 = bf16[256,2048]{1,0:T(8,128)(2,1)S(1)} collective-permute-done((bf16[256,2048]{1,0:T(8,128)(2,1)S(1)}, bf16[256,2048]{1,0:T(8,128)(2,1)S(1)}, u32[]{:S(2)}, u32[]{:S(2)}) %collective-permute-start.20) | collective-permute-done | bytes 1048608 | tf_op jit(solution)/shard_map/ppermute | solution.py:349
  480.0 14.1 %bitcast_convert_fusion = bf16[2048,2048]{1,0:T(8,128)(2,1)} fusion(bf16[4,256,2048]{2,1,0:T(8,128)(2,1)} %get-tuple-element.77, bf16[4,256,2048]{2,1,0:T(8,128)(2,1)} %get-tuple-element.73), kind=kOutput, calls=%fused_computation | convolution fusion | flops 8594128896 | bytes 16777216 | tf_op jit(solution)/shard_map/dot_general | solution.py:62
  494.7 14.1 %bitcast_convert_fusion.1 = bf16[2048,2048]{1,0:T(8,128)(2,1)} fusion(bf16[4,256,2048]{2,1,0:T(8,128)(2,1)} %get-tuple-element.76, bf16[4,256,2048]{2,1,0:T(8,128)(2,1)} %get-tuple-element.74), kind=kOutput, calls=%fused_computation.1 | convolution fusion | flops 8594128896 | bytes 16777216 | tf_op jit(solution)/shard_map/dot_general | solution.py:62
  527.1 16.4 %attend_back.1 = bf16[4,256,1536]{2,1,0:T(8,128)(2,1)} custom-call(s32[3]{0:T(128)} %pad_add_fusion.rank_ref, bf16[4,256,512]{2,1,0:T(8,128)(2,1)} %get-tuple-element.58.q_ref, bf16[4,256,512]{2,1,0:T(8,128)(2,1)} %get-tuple-element.59.k_ref, bf16[4,256,512]{2,1,0:T(8,128)(2,1)} %get-tuple-element.60.v_ref, bf16[4,256,512]{2,1,0:T(8,128)(2,1)} %pad_maximum_fusion.1.do_ref, ...), custom_call_target="tpu_custom_call" | custom-call | flops 4294967296 | bytes 7340032 | tf_op jit(solution)/shard_map/attend_back/pallas_call | solution.py:247
  546.1 5.3 multiply_reduce_fusion
  551.4 9.4 %multiply_reduce_fusion.1 = (f32[2048]{0:T(1024)S(1)}, bf16[2048,1536]{0,1:T(8,128)(2,1)}) fusion(bf16[2048,4,3,128]{0,3,2,1:T(8,128)(2,1)S(1)} %get-tuple-element.85, bf16[4,256,2048]{2,1,0:T(8,128)(2,1)S(1)} %copy-done.3, bf16[4,256,1536]{2,1,0:T(8,128)(2,1)S(1)} %copy-done.14), kind=kOutput, calls=%fused_computation.4 | convolution fusion | flops 6458177536 | bytes 19931136 | tf_op jit(solution)/shard_map/dot_general | solution.py:62
  561.7 6.5 convolution_convert_fusion.6
  576.8 19.1 %collective-permute-done.12 = bf16[256,2048]{1,0:T(8,128)(2,1)S(1)} collective-permute-done((bf16[256,2048]{1,0:T(8,128)(2,1)S(1)}, bf16[256,2048]{1,0:T(8,128)(2,1)S(1)}, u32[]{:S(2)}, u32[]{:S(2)}) %collective-permute-start.12) | collective-permute-done | bytes 1048608 | tf_op jit(solution)/shard_map/ppermute | solution.py:349
  596.0 4.6 fusion.12
  604.9 13.6 %collective-permute-done.21 = bf16[256,2048]{1,0:T(8,128)(2,1)} collective-permute-done((bf16[256,2048]{1,0:T(8,128)(2,1)}, bf16[256,2048]{1,0:T(8,128)(2,1)}, u32[]{:S(2)}, u32[]{:S(2)}) %collective-permute-start.21) | collective-permute-done | bytes 1048608 | tf_op jit(solution)/shard_map/ppermute | solution.py:349
  618.5 5.1 add_convert_fusion.1
  627.9 13.1 %collective-permute-done.13 = bf16[256,2048]{1,0:T(8,128)(2,1)} collective-permute-done((bf16[256,2048]{1,0:T(8,128)(2,1)}, bf16[256,2048]{1,0:T(8,128)(2,1)}, u32[]{:S(2)}, u32[]{:S(2)}) %collective-permute-start.13) | collective-permute-done | bytes 1048608 | tf_op jit(solution)/shard_map/ppermute | solution.py:349
  641.0 6.2 fusion.11
  647.2 4.5 collective-permute-start.14
  659.8 18.4 %collective-permute-done.27 = f32[8320]{0:T(1024)S(1)} collective-permute-done((f32[8320]{0:T(1024)S(1)}, f32[8320]{0:T(1024)S(1)}, u32[]{:S(2)}, u32[]{:S(2)}) %collective-permute-start.27) | collective-permute-done | bytes 33312 | tf_op jit(solution)/shard_map/ppermute | solution.py:317
  679.6 6.9 add_convert_fusion
  695.9 10.7 %collective-permute-done.23 = bf16[256,2048]{1,0:T(8,128)(2,1)} collective-permute-done((bf16[256,2048]{1,0:T(8,128)(2,1)}, bf16[256,2048]{1,0:T(8,128)(2,1)}, u32[]{:S(2)}, u32[]{:S(2)}) %collective-permute-start.23) | collective-permute-done | bytes 1048608 | tf_op jit(solution)/shard_map/ppermute | solution.py:349
  706.6 5.5 fusion.61
  719.5 19.4 %reduce-scatter.5.cloned.1.call-done = bf16[256,1536]{0,1:T(8,128)(2,1)} async-done(((bf16[2048,1536]{0,1:T(8,128)(2,1)}), bf16[256,1536]{0,1:T(8,128)(2,1)}) %reduce-scatter.5.cloned.1.call-update) | async-done | bytes 786448 | tf_op jit(solution)/shard_map/reduce_scatter | solution.py:398
  (195 shorter events, 154.6 us)
Async XLA Ops:
  7.2 101.4 %copy-start = (bf16[2048,512]{1,0:T(8,128)(2,1)S(1)}, bf16[2048,512]{1,0:T(8,128)(2,1)}, u32[]{:S(2)}) copy-start(bf16[2048,512]{1,0:T(8,128)(2,1)} %param.25) | copy-start | bytes 6291460
  7.2 686.9 %reduce-scatter.7.cloned.1.call-start = ((), (), s32[]{:S(2)}) async-start(), calls=%async_computation.5 | async-start | bytes 2359296 | tf_op jit(solution)/shard_map/reduce_scatter | solution.py:398
  7.2 27.8 %collective-permute-start = (bf16[256,2048]{1,0:T(8,128)(2,1)}, bf16[256,2048]{1,0:T(8,128)(2,1)}, u32[]{:S(2)}, u32[]{:S(2)}) collective-permute-start(bf16[256,2048]{1,0:T(8,128)(2,1)} %bitcast.149), channel_id=1, source_target_pairs={{0,3},{1,0},{2,1},{3,2},{4,7},{5,4},{6,5},{7,6},{8,11},{9,8},{10,9... | collective-permute-start | bytes 3145736 | tf_op jit(solution)/shard_map/ppermute | solution.py:349
  35.1 26.1 %collective-permute-start.1 = (bf16[256,2048]{1,0:T(8,128)(2,1)}, bf16[256,2048]{1,0:T(8,128)(2,1)S(1)}, u32[]{:S(2)}, u32[]{:S(2)}) collective-permute-start(bf16[256,2048]{1,0:T(8,128)(2,1)} %collective-permute-done.x_ref), channel_id=1, source_target_pairs={{0,3},{1,0},{2,1},{3,2},{4,7},{5,4},{6,5},{7,6},{8,11},{9,8},{10,9... | collective-permute-start | bytes 3145736 | tf_op jit(solution)/shard_map/ppermute | solution.py:349
  61.2 29.1 %collective-permute-start.2 = (bf16[256,2048]{1,0:T(8,128)(2,1)S(1)}, bf16[256,2048]{1,0:T(8,128)(2,1)S(1)}, u32[]{:S(2)}, u32[]{:S(2)}) collective-permute-start(bf16[256,2048]{1,0:T(8,128)(2,1)S(1)} %collective-permute-done.1.x_ref), channel_id=1, source_target_pairs={{0,3},{1,0},{2,1},{3,2},{4,7},{5,4},{6,5},{7,6},{8,11},{9,8},{10,9... | collective-permute-start | bytes 3145736 | tf_op jit(solution)/shard_map/ppermute | solution.py:349
  110.4 22.9 %collective-permute-start.3 = (bf16[256,2048]{1,0:T(8,128)(2,1)S(1)}, bf16[256,2048]{1,0:T(8,128)(2,1)S(1)}, u32[]{:S(2)}, u32[]{:S(2)}) collective-permute-start(bf16[256,2048]{1,0:T(8,128)(2,1)S(1)} %convolution_convert_fusion), channel_id=1, source_target_pairs={{0,3},{1,0},{2,1},{3,2},{4,7},{5,4},{6,5},{7,6},{8,11},{9,8},{10,9... | collective-permute-start | bytes 3145736 | tf_op jit(solution)/shard_map/ppermute | solution.py:349
  134.0 27.4 %copy-start.11 = (bf16[1,256,2048]{2,1,0:T(8,128)(2,1)S(1)}, bf16[1,256,2048]{2,1,0:T(8,128)(2,1)}, u32[]{:S(2)}) copy-start(bf16[1,256,2048]{2,1,0:T(8,128)(2,1)} %param.16) | copy-start | bytes 3145732
  134.1 51.0 %copy-start.7 = (bf16[1,256,2048]{2,1,0:T(8,128)(2,1)S(1)}, bf16[1,256,2048]{2,1,0:T(8,128)(2,1)}, u32[]{:S(2)}) copy-start(bf16[1,256,2048]{2,1,0:T(8,128)(2,1)} %param.15) | copy-start | bytes 3145732
  134.1 22.7 %collective-permute-start.4 = (bf16[256,2048]{1,0:T(8,128)(2,1)S(1)}, bf16[256,2048]{1,0:T(8,128)(2,1)S(1)}, u32[]{:S(2)}, u32[]{:S(2)}) collective-permute-start(bf16[256,2048]{1,0:T(8,128)(2,1)S(1)} %add_convert_fusion.4), channel_id=1, source_target_pairs={{0,3},{1,0},{2,1},{3,2},{4,7},{5,4},{6,5},{7,6},{8,11},{9,8},{10,9... | collective-permute-start | bytes 3145736 | tf_op jit(solution)/shard_map/ppermute | solution.py:349
  157.5 27.5 %collective-permute-start.5 = (bf16[256,2048]{1,0:T(8,128)(2,1)S(1)}, bf16[256,2048]{1,0:T(8,128)(2,1)S(1)}, u32[]{:S(2)}, u32[]{:S(2)}) collective-permute-start(bf16[256,2048]{1,0:T(8,128)(2,1)S(1)} %add_convert_fusion.3), channel_id=1, source_target_pairs={{0,3},{1,0},{2,1},{3,2},{4,7},{5,4},{6,5},{7,6},{8,11},{9,8},{10,9... | collective-permute-start | bytes 3145736 | tf_op jit(solution)/shard_map/ppermute | solution.py:349
  161.4 46.1 %collective-permute-start.9 = (bf16[256,2048]{1,0:T(8,128)(2,1)S(1)}, bf16[256,2048]{1,0:T(8,128)(2,1)}, u32[]{:S(2)}, u32[]{:S(2)}) collective-permute-start(bf16[256,2048]{1,0:T(8,128)(2,1)S(1)} %bitcast.159), channel_id=1, source_target_pairs={{0,3},{1,0},{2,1},{3,2},{4,7},{5,4},{6,5},{7,6},{8,11},{9,8},{10,9... | collective-permute-start | bytes 3145736 | tf_op jit(solution)/shard_map/ppermute | solution.py:349
  186.3 48.0 %copy-start.26 = (s32[1,1024]{1,0:T(1,128)S(1)}, s32[1,1024]{1,0:T(1,128)}, u32[]{:S(2)}) copy-start(s32[1,1024]{1,0:T(1,128)} %param.19) | copy-start | bytes 12292
  187.3 42.7 %collective-permute-start.6 = (bf16[256,2048]{1,0:T(8,128)(2,1)S(1)}, bf16[256,2048]{1,0:T(8,128)(2,1)}, u32[]{:S(2)}, u32[]{:S(2)}) collective-permute-start(bf16[256,2048]{1,0:T(8,128)(2,1)S(1)} %add_convert_fusion.2.a_ref), channel_id=1, source_target_pairs={{0,3},{1,0},{2,1},{3,2},{4,7},{5,4},{6,5},{7,6},{8,11},{9,8},{10,9... | collective-permute-start | bytes 3145736 | tf_op jit(solution)/shard_map/ppermute | solution.py:349
  207.5 45.0 %collective-permute-start.10 = (bf16[256,2048]{1,0:T(8,128)(2,1)}, bf16[256,2048]{1,0:T(8,128)(2,1)}, u32[]{:S(2)}, u32[]{:S(2)}) collective-permute-start(bf16[256,2048]{1,0:T(8,128)(2,1)} %collective-permute-done.9.g_ref), channel_id=1, source_target_pairs={{0,3},{1,0},{2,1},{3,2},{4,7},{5,4},{6,5},{7,6},{8,11},{9,8},{10,9... | collective-permute-start | bytes 3145736 | tf_op jit(solution)/shard_map/ppermute | solution.py:349
  230.0 45.0 %collective-permute-start.7 = (bf16[256,2048]{1,0:T(8,128)(2,1)}, bf16[256,2048]{1,0:T(8,128)(2,1)}, u32[]{:S(2)}, u32[]{:S(2)}) collective-permute-start(bf16[256,2048]{1,0:T(8,128)(2,1)} %collective-permute-done.6.a_ref), channel_id=1, source_target_pairs={{0,3},{1,0},{2,1},{3,2},{4,7},{5,4},{6,5},{7,6},{8,11},{9,8},{10,9... | collective-permute-start | bytes 3145736 | tf_op jit(solution)/shard_map/ppermute | solution.py:349
  252.6 60.0 %collective-permute-start.11 = (bf16[256,2048]{1,0:T(8,128)(2,1)}, bf16[256,2048]{1,0:T(8,128)(2,1)S(1)}, u32[]{:S(2)}, u32[]{:S(2)}) collective-permute-start(bf16[256,2048]{1,0:T(8,128)(2,1)} %collective-permute-done.10.g_ref), channel_id=1, source_target_pairs={{0,3},{1,0},{2,1},{3,2},{4,7},{5,4},{6,5},{7,6},{8,11},{9,8},{10,9... | collective-permute-start | bytes 3145736 | tf_op jit(solution)/shard_map/ppermute | solution.py:349
  275.0 40.1 %collective-permute-start.8 = (bf16[256,2048]{1,0:T(8,128)(2,1)}, bf16[256,2048]{1,0:T(8,128)(2,1)S(1)}, u32[]{:S(2)}, u32[]{:S(2)}) collective-permute-start(bf16[256,2048]{1,0:T(8,128)(2,1)} %collective-permute-done.7.a_ref), channel_id=1, source_target_pairs={{0,3},{1,0},{2,1},{3,2},{4,7},{5,4},{6,5},{7,6},{8,11},{9,8},{10,9... | collective-permute-start | bytes 3145736 | tf_op jit(solution)/shard_map/ppermute | solution.py:349
  327.3 28.3 %copy-start.2 = (bf16[4,256,2048]{2,1,0:T(8,128)(2,1)S(1)}, bf16[4,256,2048]{2,1,0:T(8,128)(2,1)}, u32[]{:S(2)}) copy-start(bf16[4,256,2048]{2,1,0:T(8,128)(2,1)} %get-tuple-element.74) | copy-start | bytes 12582916
  327.3 55.5 %slice-start = ((s8[8388608]{0:T(1024)(128)(4,1)}), s8[4194304]{0:T(1024)(128)(4,1)S(1)}, s32[]{:S(2)}) async-start(s8[8388608]{0:T(1024)(128)(4,1)} %bitcast.143), calls=%async_computation.8 | async-start | bytes 8388608
  333.5 49.3 %slice-start.1 = ((s8[8388608]{0:T(1024)(128)(4,1)}), s8[4194304]{0:T(1024)(128)(4,1)S(1)}, s32[]{:S(2)}) async-start(s8[8388608]{0:T(1024)(128)(4,1)} %bitcast.143), calls=%async_computation.9 | async-start | bytes 8388608
  333.5 22.1 %collective-permute-start.15 = (bf16[256,2048]{1,0:T(8,128)(2,1)S(1)}, bf16[256,2048]{1,0:T(8,128)(2,1)S(1)}, u32[]{:S(2)}, u32[]{:S(2)}) collective-permute-start(bf16[256,2048]{1,0:T(8,128)(2,1)S(1)} %convolution_convert_fusion.4), channel_id=1, source_target_pairs={{0,3},{1,0},{2,1},{3,2},{4,7},{5,4},{6,5},{7,6},{8,11},{9,8},{10,9... | collective-permute-start | bytes 3145736 | tf_op jit(solution)/shard_map/ppermute | solution.py:349
  361.3 44.3 %copy-start.5 = (f32[256,2048]{1,0:T(8,128)S(1)}, f32[256,2048]{1,0:T(8,128)}, u32[]{:S(2)}) copy-start(f32[256,2048]{1,0:T(8,128)} %copy-done.4) | copy-start | bytes 6291460
  361.4 21.4 %collective-permute-start.16 = (bf16[256,2048]{1,0:T(8,128)(2,1)S(1)}, bf16[256,2048]{1,0:T(8,128)(2,1)S(1)}, u32[]{:S(2)}, u32[]{:S(2)}) collective-permute-start(bf16[256,2048]{1,0:T(8,128)(2,1)S(1)} %fusion.14), channel_id=1, source_target_pairs={{0,3},{1,0},{2,1},{3,2},{4,7},{5,4},{6,5},{7,6},{8,11},{9,8},{10,9... | collective-permute-start | bytes 3145736 | tf_op jit(solution)/shard_map/ppermute | solution.py:349
  385.2 20.4 %collective-permute-start.17 = (bf16[256,2048]{1,0:T(8,128)(2,1)S(1)}, bf16[256,2048]{1,0:T(8,128)(2,1)S(1)}, u32[]{:S(2)}, u32[]{:S(2)}) collective-permute-start(bf16[256,2048]{1,0:T(8,128)(2,1)S(1)} %fusion.13), channel_id=1, source_target_pairs={{0,3},{1,0},{2,1},{3,2},{4,7},{5,4},{6,5},{7,6},{8,11},{9,8},{10,9... | collective-permute-start | bytes 3145736 | tf_op jit(solution)/shard_map/ppermute | solution.py:349
  408.8 67.6 %copy-start.19 = (bf16[4,256,512]{2,1,0:T(8,128)(2,1)S(1)}, bf16[4,256,512]{2,1,0:T(8,128)(2,1)}, u32[]{:S(2)}) copy-start(bf16[4,256,512]{2,1,0:T(8,128)(2,1)} %attend.1) | copy-start | bytes 3145732
  411.1 64.3 %copy-start.15 = (bf16[256,2048]{1,0:T(8,128)(2,1)}, bf16[256,2048]{1,0:T(8,128)(2,1)S(1)}, u32[]{:S(2)}) copy-start(bf16[256,2048]{1,0:T(8,128)(2,1)S(1)} %get-tuple-element.86) | copy-start | bytes 3145732
  411.1 23.3 %collective-permute-start.18 = (bf16[256,2048]{1,0:T(8,128)(2,1)S(1)}, bf16[256,2048]{1,0:T(8,128)(2,1)S(1)}, u32[]{:S(2)}, u32[]{:S(2)}) collective-permute-start(bf16[256,2048]{1,0:T(8,128)(2,1)S(1)} %get-tuple-element.86), channel_id=1, source_target_pairs={{0,3},{1,0},{2,1},{3,2},{4,7},{5,4},{6,5},{7,6},{8,11},{9,8},{10,9... | collective-permute-start | bytes 3145736 | tf_op jit(solution)/shard_map/ppermute | solution.py:349
  434.4 41.0 %copy-start.28 = (bf16[256,2048]{1,0:T(8,128)(2,1)}, bf16[256,2048]{1,0:T(8,128)(2,1)S(1)}, u32[]{:S(2)}) copy-start(bf16[256,2048]{1,0:T(8,128)(2,1)S(1)} %collective-permute-done.18) | copy-start | bytes 3145732
  434.4 23.3 %collective-permute-start.19 = (bf16[256,2048]{1,0:T(8,128)(2,1)S(1)}, bf16[256,2048]{1,0:T(8,128)(2,1)S(1)}, u32[]{:S(2)}, u32[]{:S(2)}) collective-permute-start(bf16[256,2048]{1,0:T(8,128)(2,1)S(1)} %collective-permute-done.18), channel_id=1, source_target_pairs={{0,3},{1,0},{2,1},{3,2},{4,7},{5,4},{6,5},{7,6},{8,11},{9,8},{10,9... | collective-permute-start | bytes 3145736 | tf_op jit(solution)/shard_map/ppermute | solution.py:349
  457.7 17.7 %collective-permute-start.20 = (bf16[256,2048]{1,0:T(8,128)(2,1)S(1)}, bf16[256,2048]{1,0:T(8,128)(2,1)S(1)}, u32[]{:S(2)}, u32[]{:S(2)}) collective-permute-start(bf16[256,2048]{1,0:T(8,128)(2,1)S(1)} %collective-permute-done.19), channel_id=1, source_target_pairs={{0,3},{1,0},{2,1},{3,2},{4,7},{5,4},{6,5},{7,6},{8,11},{9,8},{10,9... | collective-permute-start | bytes 3145736 | tf_op jit(solution)/shard_map/ppermute | solution.py:349
  480.0 233.9 %reduce-scatter.11.cloned.1.call-start = ((), (), s32[]{:S(2)}) async-start(), calls=%async_computation.7 | async-start | bytes 9437184 | tf_op jit(solution)/shard_map/reduce_scatter | solution.py:398
  494.2 222.5 %reduce-scatter.9.cloned.1.call-start = ((), (), s32[]{:S(2)}) async-start(), calls=%async_computation.6 | async-start | bytes 9437184 | tf_op jit(solution)/shard_map/reduce_scatter | solution.py:398
  508.7 230.2 %reduce-scatter.5.cloned.1.call-start = ((), (), s32[]{:S(2)}) async-start(), calls=%async_computation.4 | async-start | bytes 7077888 | tf_op jit(solution)/shard_map/reduce_scatter | solution.py:398
  561.7 34.3 %slice-start.2 = ((s8[8388608]{0:T(1024)(128)(4,1)}), s8[4194304]{0:T(1024)(128)(4,1)S(1)}, s32[]{:S(2)}) async-start(s8[8388608]{0:T(1024)(128)(4,1)} %bitcast.145), calls=%async_computation.10 | async-start | bytes 8388608
  568.2 27.8 %collective-permute-start.12 = (bf16[256,2048]{1,0:T(8,128)(2,1)S(1)}, bf16[256,2048]{1,0:T(8,128)(2,1)S(1)}, u32[]{:S(2)}, u32[]{:S(2)}) collective-permute-start(bf16[256,2048]{1,0:T(8,128)(2,1)S(1)} %convolution_convert_fusion.6), channel_id=1, source_target_pairs={{0,3},{1,0},{2,1},{3,2},{4,7},{5,4},{6,5},{7,6},{8,11},{9,8},{10,9... | collective-permute-start | bytes 3145736 | tf_op jit(solution)/shard_map/ppermute | solution.py:349
  576.8 28.0 %copy-start.22 = (f32[2048]{0:T(1024)S(1)}, f32[2048]{0:T(1024)}, u32[]{:S(2)}) copy-start(f32[2048]{0:T(1024)} %param.21) | copy-start | bytes 24580
  576.8 28.0 %copy-start.23 = (f32[2048]{0:T(1024)S(1)}, f32[2048]{0:T(1024)}, u32[]{:S(2)}) copy-start(f32[2048]{0:T(1024)} %param.20) | copy-start | bytes 24580
  576.8 41.8 %collective-permute-start.21 = (bf16[256,2048]{1,0:T(8,128)(2,1)}, bf16[256,2048]{1,0:T(8,128)(2,1)}, u32[]{:S(2)}, u32[]{:S(2)}) collective-permute-start(bf16[256,2048]{1,0:T(8,128)(2,1)} %convolution_convert_fusion.2), channel_id=1, source_target_pairs={{0,3},{1,0},{2,1},{3,2},{4,7},{5,4},{6,5},{7,6},{8,11},{9,8},{10,9... | collective-permute-start | bytes 3145736 | tf_op jit(solution)/shard_map/ppermute | solution.py:349
  600.5 40.5 %collective-permute-start.13 = (bf16[256,2048]{1,0:T(8,128)(2,1)}, bf16[256,2048]{1,0:T(8,128)(2,1)}, u32[]{:S(2)}, u32[]{:S(2)}) collective-permute-start(bf16[256,2048]{1,0:T(8,128)(2,1)} %fusion.12), channel_id=1, source_target_pairs={{0,3},{1,0},{2,1},{3,2},{4,7},{5,4},{6,5},{7,6},{8,11},{9,8},{10,9... | collective-permute-start | bytes 3145736 | tf_op jit(solution)/shard_map/ppermute | solution.py:349
  604.9 36.1 %copy-start.1 = (bf16[4,256,2048]{2,1,0:T(8,128)(2,1)S(1)}, bf16[4,256,2048]{2,1,0:T(8,128)(2,1)}, u32[]{:S(2)}) copy-start(bf16[4,256,2048]{2,1,0:T(8,128)(2,1)} %get-tuple-element.73) | copy-start | bytes 12582916
  604.9 46.8 %collective-permute-start.24 = (f32[8320]{0:T(1024)S(1)}, f32[8320]{0:T(1024)S(1)}, u32[]{:S(2)}, u32[]{:S(2)}) collective-permute-start(f32[8320]{0:T(1024)S(1)} %concatenate.16), channel_id=1, source_target_pairs={{0,4},{4,0},{8,12},{12,8},{16,20},{20,16},{24,28},{28,24},{1,5},{5... | collective-permute-start | bytes 99848 | tf_op jit(solution)/shard_map/ppermute | solution.py:317
  623.7 55.9 %collective-permute-start.22 = (bf16[256,2048]{1,0:T(8,128)(2,1)S(1)}, bf16[256,2048]{1,0:T(8,128)(2,1)S(1)}, u32[]{:S(2)}, u32[]{:S(2)}) collective-permute-start(bf16[256,2048]{1,0:T(8,128)(2,1)S(1)} %add_convert_fusion.1), channel_id=1, source_target_pairs={{0,3},{1,0},{2,1},{3,2},{4,7},{5,4},{6,5},{7,6},{8,11},{9,8},{10,9... | collective-permute-start | bytes 3145736 | tf_op jit(solution)/shard_map/ppermute | solution.py:349
  647.2 41.7 %collective-permute-start.14 = (bf16[256,2048]{1,0:T(8,128)(2,1)S(1)}, bf16[256,2048]{1,0:T(8,128)(2,1)S(1)}, u32[]{:S(2)}, u32[]{:S(2)}) collective-permute-start(bf16[256,2048]{1,0:T(8,128)(2,1)S(1)} %fusion.11), channel_id=1, source_target_pairs={{0,3},{1,0},{2,1},{3,2},{4,7},{5,4},{6,5},{7,6},{8,11},{9,8},{10,9... | collective-permute-start | bytes 3145736 | tf_op jit(solution)/shard_map/ppermute | solution.py:349
  651.8 4.0 collective-permute-start.25
  655.8 4.0 collective-permute-start.26
  659.8 18.4 %collective-permute-start.27 = (f32[8320]{0:T(1024)S(1)}, f32[8320]{0:T(1024)S(1)}, u32[]{:S(2)}, u32[]{:S(2)}) collective-permute-start(f32[8320]{0:T(1024)S(1)} %add.132), channel_id=1, source_target_pairs={{0,1},{1,0},{2,3},{3,2},{4,5},{5,4},{6,7},{7,6},{8,9},{9,8},{10,11... | collective-permute-start | bytes 99848 | tf_op jit(solution)/shard_map/ppermute | solution.py:317
  678.2 14.2 %collective-permute-start.28 = (f32[8320]{0:T(1024)S(1)}, f32[8320]{0:T(1024)S(1)}, u32[]{:S(2)}, u32[]{:S(2)}) collective-permute-start(f32[8320]{0:T(1024)S(1)} %add.133), channel_id=1, source_target_pairs={{0,2},{1,3},{2,0},{3,1},{4,6},{5,7},{6,4},{7,5},{8,10},{9,11},{10,... | collective-permute-start | bytes 99848 | tf_op jit(solution)/shard_map/ppermute | solution.py:317
  686.5 20.1 %collective-permute-start.23 = (bf16[256,2048]{1,0:T(8,128)(2,1)}, bf16[256,2048]{1,0:T(8,128)(2,1)}, u32[]{:S(2)}, u32[]{:S(2)}) collective-permute-start(bf16[256,2048]{1,0:T(8,128)(2,1)} %add_convert_fusion), channel_id=1, source_target_pairs={{0,3},{1,0},{2,1},{3,2},{4,7},{5,4},{6,5},{7,6},{8,11},{9,8},{10,9... | collective-permute-start | bytes 3145736 | tf_op jit(solution)/shard_map/ppermute | solution.py:349
  (25 other events, 210.6 us)
Sparse Core Ops, SparseCore 0:
  480.1 43.0 reduce-scatter.6
  527.1 71.2 reduce-scatter.10
  601.9 71.6 reduce-scatter.8
  677.2 61.7 reduce-scatter.4

commit v2 on v1

--- a/solution.py
+++ b/solution.py
@@ -62,12 +62,13 @@
     return lax.dot_general(left, right, (((0,), (0,)), ((), ())), preferred_element_type=F32)
 
 
-def qkv_body(rank_ref, x_ref, gain_ref, shift_ref, wq_ref, wk_ref, wv_ref, cos_ref, sin_ref, *rest):
+def qkv_body(rank_ref, xa_ref, xb_ref, gain_ref, shift_ref, wq_ref, wk_ref, wv_ref, cos_ref, sin_ref, *rest):
     a_ref, q_ref, k_ref, v_ref = rest[-4:]
 
     @pl.when(pl.program_id(0) == 0)
     def _():
-        out, _, _ = norm_forward(x_ref[...].astype(F32), gain_ref[...], shift_ref[...])
+        x = jnp.concatenate([xa_ref[...], xb_ref[...]], axis=1).astype(F32)
+        out, _, _ = norm_forward(x, gain_ref[...], shift_ref[...])
         a_ref[0] = out.astype(BF16)
 
     act = a_ref[0]
@@ -81,15 +82,17 @@
             o_ref[0, :, j * E : (j + 1) * E] = turned.astype(BF16)
 
 
-def qkv_slot(slot, n, rank, x, gain, shift, wq, wk, wv, cos, sin, held):
-    rows, d = x.shape
+def qkv_slot(slot, n, rank, xa, xb, gain, shift, wq, wk, wv, cos, sin, held):
+    rows, half = xa.shape
+    d = 2 * half
     local = wq.shape[1]
-    cb = min(256, local)
+    cb = min(512, local)
     whole = lambda j, r: (0, 0)
     wspec = pl.BlockSpec((d, cb), lambda j, r: (0, j))
     tspec = pl.BlockSpec((1, rows, E), lambda j, r: (lax.rem(r[0] + slot, n), 0, 0))
     in_specs = [
-        pl.BlockSpec((rows, d), whole),
+        pl.BlockSpec((rows, half), whole),
+        pl.BlockSpec((rows, half), whole),
         pl.BlockSpec((1, d), whole),
         pl.BlockSpec((1, d), whole),
         wspec,
@@ -99,7 +102,7 @@
         tspec,
     ]
     extra = [] if held is None else list(held)
-    aliases = {} if held is None else {9 + i: i for i in range(4)}
+    aliases = {} if held is None else {10 + i: i for i in range(4)}
     ospec = pl.BlockSpec((1, rows, cb), lambda j, r: (slot, 0, j))
     return pl.pallas_call(
         qkv_body,
@@ -115,7 +118,7 @@
         compiler_params=params(),
         cost_estimate=cost(6 * rows * d * local, 6 * d * local + 4 * rows * d),
         name="qkv_slot",
-    )(rank, x, gain, shift, wq, wk, wv, cos, sin, *extra)
+    )(rank, xa, xb, gain, shift, wq, wk, wv, cos, sin, *extra)
 
 
 def first_key(block, rows):
@@ -191,6 +194,8 @@
     low = lax.broadcasted_iota(jnp.int32, (rows, rows), 0) <= lax.broadcasted_iota(
         jnp.int32, (rows, rows), 1
     )
+    local = out_ref.shape[2] // 3
+    lanes = lambda i: pl.ds(pl.multiple_of(i * local + pl.program_id(0) * E, E), E)
     dk_ref[...] = jnp.zeros_like(dk_ref)
     dv_ref[...] = jnp.zeros_like(dv_ref)
 
@@ -231,10 +236,10 @@
             dv_ref[c] += dot_n(p.astype(BF16), grad)
             part = outer(ds, k_ref[slot(c)])
             dq = part if dq is None else dq + part
-        out_ref[slot(b), :, :E] = unrotate(dq, b)
+        out_ref[slot(b), :, lanes(0)] = unrotate(dq, b)
     for b in range(n):
-        out_ref[slot(b), :, E : 2 * E] = unrotate(dk_ref[b], b)
-        out_ref[slot(b), :, 2 * E :] = dv_ref[b].astype(BF16)
+        out_ref[slot(b), :, lanes(1)] = unrotate(dk_ref[b], b)
+        out_ref[slot(b), :, lanes(2)] = dv_ref[b].astype(BF16)
 
 
 def attend_back(rank, q, k, v, do, docs_col, docs_row, heads_col, cos, sin):
@@ -250,51 +255,62 @@
             num_scalar_prefetch=1,
             grid=(local // E,),
             in_specs=[spec, spec, spec, spec, col, row, col, table, table],
-            out_specs=pl.BlockSpec((n, rows, 3 * E), lambda h, r: (0, 0, h)),
+            out_specs=pl.BlockSpec((n, rows, 3 * local), lambda h, r: (0, 0, 0)),
             scratch_shapes=[pltpu.VMEM((n, rows, E), F32), pltpu.VMEM((n, rows, E), F32)],
         ),
         out_shape=jax.ShapeDtypeStruct((n, rows, 3 * local), BF16),
         compiler_params=params(),
-        cost_estimate=cost(8 * t * t * local, 14 * t * local, t * t * local // E),
+        cost_estimate=cost(200e9, 14 * t * local),
         name="attend_back",
     )(rank, q, k, v, do, docs_col, docs_row, heads_col, cos, sin)
 
 
-def mlp_body(rank_ref, a_ref, g_ref, up_ref, down_ref, bucket_ref, *rest):
+def mlp_body(slot, n, rank_ref, a_ref, gl_ref, gr_ref, up_ref, down_ref, bucket_ref, *rest):
     r_ref, du_ref, aa_ref, ga_ref = rest[-4:]
     rows, cb = a_ref.shape[0], up_ref.shape[1]
 
     @pl.when(pl.program_id(0) == 0)
     def _():
         aa_ref[0] = a_ref[...]
-        ga_ref[0] = g_ref[...]
+        ahead = rank_ref[0] + slot < n
+
+
+        @pl.when(ahead)
+        def _():
+            ga_ref[0] = gl_ref[...]
+
+        @pl.when(jnp.logical_not(ahead))
+        def _():
+            ga_ref[0] = gr_ref[...]
 
     u = dot_n(a_ref[...], up_ref[...])
-    dr = dot_n(g_ref[...], down_ref[...]).astype(BF16).astype(F32)
+    dr = dot_n(ga_ref[0], down_ref[...]).astype(BF16).astype(F32)
     column = rank_ref[2] + pl.program_id(0) * cb + lax.broadcasted_iota(jnp.int32, (rows, cb), 1)
     lifted = jnp.where(column < (bucket_ref[0] + 1) * (FF // 4), jnp.maximum(u, 0.0), 0.0)
     r_ref[0] = (lifted * lifted).astype(BF16)
     du_ref[0] = (dr * (2.0 * lifted)).astype(BF16)
 
 
-def mlp_slot(slot, n, rank, act, grad, up, down, bucket_col, held):
+def mlp_slot(slot, n, rank, act, grads, up, down, bucket_col, held):
     rows, d = act.shape
     hidden = up.shape[1]
     cb = min(512, hidden)
     whole = lambda j, r: (0, 0)
     wspec = pl.BlockSpec((d, cb), lambda j, r: (0, j))
     extra = [] if held is None else list(held)
-    aliases = {} if held is None else {6 + i: i for i in range(4)}
+    aliases = {} if held is None else {7 + i: i for i in range(4)}
     ospec = pl.BlockSpec((1, rows, cb), lambda j, r: (slot, 0, j))
     aspec = pl.BlockSpec((1, rows, d), lambda j, r: (slot, 0, 0))
     return pl.pallas_call(
-        mlp_body,
+        functools.partial(mlp_body, slot, n),
         grid_spec=pltpu.PrefetchScalarGridSpec(
             num_scalar_prefetch=1,
             grid=(hidden // cb,),
             in_specs=[
                 pl.BlockSpec((rows, d), whole),
-                pl.BlockSpec((rows, d), whole),
+            ]
+            + [pl.BlockSpec((rows, d), whole)] * 2
+            + [
                 wspec,
                 wspec,
                 pl.BlockSpec((1, rows, 1), lambda j, r: (lax.rem(r[0] + slot, n), 0, 0)),
@@ -308,15 +324,174 @@
         compiler_params=params(),
         cost_estimate=cost(4 * rows * d * hidden, 4 * d * hidden + 4 * rows * (d + hidden)),
         name="mlp_slot",
-    )(rank, act, grad, up, down, bucket_col, *extra)
-
-
-def xor_sum(vec, axis, size):
-    step = 1
-    while step < size:
-        vec = vec + lax.ppermute(vec, axis, [(i, i ^ step) for i in range(size)])
-        step *= 2
-    return vec
+    )(rank, act, *grads, up, down, bucket_col, *extra)
+
+
+def dom_body(n, slots, rank_ref, slot_ref, *refs):
+    dom_ref, all_ref = refs[-2:]
+    count = sum(2 if s == 0 else 4 for s in slots)
+    flows, w_ref = list(refs[:count]), refs[count]
+    half = flows[0].shape[1]
+
+    def fill(pair):
+        all_ref[0, :, :half] = pair[0][...]
+        all_ref[0, :, half:] = pair[1][...]
+
+    for i, s in enumerate(slots):
+        here = pl.program_id(0) == i
+        if s == 0:
+            pl.when(here)(functools.partial(fill, flows[:2]))
+            flows = flows[2:]
+        else:
+            ahead = rank_ref[0] + s < n
+            pl.when(here & ahead)(functools.partial(fill, flows[:2]))
+            pl.when(here & jnp.logical_not(ahead))(functools.partial(fill, flows[2:4]))
+            flows = flows[4:]
+    dom_ref[0] = dot_n(all_ref[0], w_ref[...]).astype(BF16)
+
+
+def dom_part(n, slots, rank, flows, weight, held):
+    rows, half = flows[0].shape
+    d, local = weight.shape
+    whole = lambda i, r, s: (0, 0)
+    extra = [] if held is None else list(held)
+    at = 2 + len(flows) + 1
+    return pl.pallas_call(
+        functools.partial(dom_body, n, slots),
+        grid_spec=pltpu.PrefetchScalarGridSpec(
+            num_scalar_prefetch=2,
+            grid=(len(slots),),
+            in_specs=[pl.BlockSpec((rows, half), whole)] * len(flows)
+            + [pl.BlockSpec((d, local), whole)]
+            + [pl.BlockSpec(memory_space=pl.ANY)] * len(extra),
+            out_specs=[
+                pl.BlockSpec((1, rows, local), lambda i, r, s: (s[i], 0, 0)),
+                pl.BlockSpec((1, rows, d), lambda i, r, s: (s[i], 0, 0)),
+            ],
+        ),
+        out_shape=[
+            jax.ShapeDtypeStruct((n, rows, local), BF16),
+            jax.ShapeDtypeStruct((n, rows, d), BF16),
+        ],
+        input_output_aliases={at + i: i for i in range(len(extra))},
+        compiler_params=params(),
+        cost_estimate=cost(
+            2 * len(slots) * rows * d * local, 2 * d * local + 6 * len(slots) * rows * d
+        ),
+        name="dom_part",
+    )(rank, jnp.asarray(slots, jnp.int32), *flows, weight, *extra)
+
+
+def grad_body(lhs_ref, rhs_ref, *rest):
+    rest[-1][0] = outer(lhs_ref[...], rhs_ref[...]).astype(BF16)
+
+
+def grad_part(which, lhs, rhs, held):
+    t, d = lhs.shape
+    width = rhs.shape[1]
+    tile = min(512, d)
+    extra = [] if held is None else [held]
+    return pl.pallas_call(
+        grad_body,
+        grid=(d // tile,),
+        in_specs=[
+            pl.BlockSpec((t, tile), lambda j: (0, j)),
+            pl.BlockSpec((t, width), lambda j: (0, 0)),
+        ]
+        + [pl.BlockSpec(memory_space=pl.ANY)] * len(extra),
+        out_specs=pl.BlockSpec((1, tile, width), lambda j: (which, j, 0)),
+        out_shape=jax.ShapeDtypeStruct((2, d, width), BF16),
+        input_output_aliases={2: 0} if extra else {},
+        compiler_params=params(),
+        cost_estimate=cost(2 * t * d * width, 2 * t * (d + width) + 2 * d * width),
+        name="grad_part",
+    )(lhs, rhs, *extra)
+
+
+def attn_grad_body(a_ref, s_ref, dqkv_ref, om_ref, wq_ref, wk_ref, wv_ref, out_ref, sum_ref, dot_ref, tot_ref):
+    local = om_ref.shape[1]
+
+    @pl.when(pl.program_id(0) == 0)
+    def _():
+        tot_ref[...] = jnp.sum(dqkv_ref[...].astype(F32), axis=0, keepdims=True)
+
+    act = a_ref[...]
+    plain = None
+    for i, w_ref in enumerate((wq_ref, wk_ref, wv_ref)):
+        cols = slice(i * local, (i + 1) * local)
+        part = outer(act, dqkv_ref[:, cols])
+        out_ref[:, cols] = part.astype(BF16)
+        w = w_ref[...].astype(F32)
+        one, two = w * tot_ref[:, cols], w * part
+        plain = one if plain is None else plain + one
+        mixed = two if i == 0 else mixed + two
+    sum_ref[...] = jnp.sum(plain, axis=1, keepdims=True)
+    dot_ref[...] = jnp.sum(mixed, axis=1, keepdims=True)
+    out_ref[:, 3 * local :] = outer(s_ref[...], om_ref[...]).astype(BF16)
+
+
+def attn_grads(act, states, dqkv, om, wq, wk, wv):
+    t, d = act.shape
+    local = om.shape[1]
+    tile = min(512, d)
+    col = pl.BlockSpec((t, tile), lambda j: (0, j))
+    wspec = pl.BlockSpec((tile, local), lambda j: (j, 0))
+    vec = pl.BlockSpec((tile, 1), lambda j: (j, 0))
+    return pl.pallas_call(
+        attn_grad_body,
+        grid=(d // tile,),
+        in_specs=[
+            col,
+            col,
+            pl.BlockSpec((t, 3 * local), lambda j: (0, 0)),
+            pl.BlockSpec((t, local), lambda j: (0, 0)),
+            wspec,
+            wspec,
+            wspec,
+        ],
+        out_specs=[pl.BlockSpec((tile, 4 * local), lambda j: (j, 0)), vec, vec],
+        out_shape=[
+            jax.ShapeDtypeStruct((d, 4 * local), BF16),
+            jax.ShapeDtypeStruct((d, 1), F32),
+            jax.ShapeDtypeStruct((d, 1), F32),
+        ],
+        scratch_shapes=[pltpu.VMEM((1, 3 * local), F32)],
+        compiler_params=params(),
+        cost_estimate=cost(8 * t * d * local, 2 * t * (2 * d + 4 * local) + 14 * d * local),
+        name="attn_grads",
+    )(act, states, dqkv, om, wq, wk, wv)
+
+
+def last_body(x_ref, gain_ref, term_ref, moved_ref, state_ref, out_ref):
+    gain = gain_ref[...]
+    _, normed, inverse = norm_forward(x_ref[...].astype(F32), gain, gain)
+    back = norm_backward(term_ref[...].astype(F32) + moved_ref[...].astype(F32), normed, inverse, gain)
+    out_ref[...] = (state_ref[...] + back).astype(BF16)
+
+
+def last_step(x, gain, term, moved, state):
+    rows, d = x.shape
+    tile = min(64, rows)
+    row = lambda w: pl.BlockSpec((tile, w), lambda i: (i, 0))
+    return pl.pallas_call(
+        last_body,
+        grid=(rows // tile,),
+        in_specs=[row(d), pl.BlockSpec((1, d), lambda i: (0, 0)), row(d), row(d), row(d)],
+        out_specs=row(d),
+        out_shape=jax.ShapeDtypeStruct((rows, d), BF16),
+        compiler_params=params(),
+        cost_estimate=cost(73e9, 12 * rows * d),
+        name="last_step",
+    )(x, gain, term, moved, state)
+
+
+def tie(values, *others):
+    values = tuple(values)
+    return lax.optimization_barrier(values + others)[: len(values)]
+
+
+def sum_over(vec, axis, moves):
+    return sum((lax.ppermute(vec, axis, pairs) for pairs in moves), vec)
 
 
 def per_device(
@@ -340,13 +515,36 @@
 ):
     rank = lax.axis_index("mp")
     rows, d = tokens.shape[1:]
+    half = d // 2
     local = query_weight.shape[1]
     local_heads = local // E
     hidden = up_weight.shape[1]
     length = n * rows
     own = tokens[0]
+    send = lambda v, pairs: lax.ppermute(v, "mp", pairs)
     ring = [(i, (i - 1) % n) for i in range(n)]
-    hop = lambda v: lax.ppermute(v, "mp", ring)
+    hop = lambda v: send(v, ring)
+    right_line = [(i, i + 1) for i in range(n - 1)]
+    left_line = [(i + 1, i) for i in range(n - 1)]
+
+    def tick(k, right, left, terms):
+        width = d // len(right)
+        for p in range(len(right)):
+            cols = slice(p * width, (p + 1) * width)
+            r, l = right[p], left[p]
+            if k:
+                r = low(r.astype(F32) + (rank < k).astype(F32) * terms[n - k][:, cols].astype(F32))
+                l = low(l.astype(F32) + (rank >= n - k).astype(F32) * terms[k][:, cols].astype(F32))
+            right[p], left[p] = send(r, right_line), send(l, left_line)
+
+    def owned(terms, right, left):
+        moved = [r.astype(F32) + l.astype(F32) for r, l in zip(right, left)]
+        return terms[0].astype(F32) + (jnp.concatenate(moved, axis=1) if len(moved) > 1 else moved[0])
+
+    low = lambda v: v.astype(BF16)
+    flat = lambda v: v.reshape(length, v.shape[-1])
+    add = lambda t, moved: (t.astype(F32) + moved.astype(F32)).astype(BF16)
+
     where = jnp.stack([rank, rank * local_heads, rank * hidden]).astype(jnp.int32)
     docs_col = doc_ids.reshape(n, rows, 1)
     docs_row = doc_ids.reshape(n, 1, rows)
@@ -356,75 +554,105 @@
     gain1, shift1 = first_gain[None], first_shift[None]
     gain2, shift2 = second_gain[None], second_shift[None]
 
-    held, block = None, own
+    held, block = None, [own[:, :half], own[:, half:]]
     for s in range(n):
-        after = hop(block) if s < n - 1 else None
+        after = [None, None]
+        for p in range(2):
+            if s >= 1:
+                block[p], *held = tie([block[p]] + list(held))
+            if s < n - 1:
+                after[p] = hop(block[p])
         held = qkv_slot(
-            s, n, where, block, gain1, shift1, query_weight, key_weight, value_weight, cos, sin, held
+            s, n, where, *block, gain1, shift1, query_weight, key_weight, value_weight, cos, sin, held
         )
-        block = after
+        if s < n - 1:
+            block = after
     first_all, query, keys, vals = held
+
+    grad_own = mixed_grad[0]
+    right = list(tie([grad_own], *block))
+    left = list(right)
+    grads_r, grads_l = [list(right)], [list(left)]
+    tick(0, right, left, None)
     masked = attend(where, query, keys, vals, docs_col, docs_row, heads_col)
-
-    grads = [mixed_grad[0]]
-    for s in range(n - 1):
-        grads.append(hop(grads[-1]))
-
-    def scatter_ring(term):
-        moved = None
-        for s in range(1, n):
-            t = term(s)
-            moved = hop((t if moved is None else t + moved.astype(F32)).astype(BF16))
-        return term(0).astype(BF16).astype(F32) + moved.astype(F32)
-
-    attn = scatter_ring(lambda s: dot_t(masked[s], output_weight))
+    terms = low(dot_t(flat(masked), output_weight)).reshape(n, rows, d)
+    for k in range(1, n):
+        grads_r.append(list(right))
+        grads_l.append(list(left))
+        tick(k, right, left, terms)
+    attn = owned(terms, right, left)
     x_rows = own.astype(F32)
     state = x_rows + attn
     second_out, normed_two, inverse_two = norm_forward(state, gain2, shift2)
 
-    held, block = None, second_out.astype(BF16)
+    weights = jnp.concatenate([query_weight, key_weight, value_weight], axis=1)
+    held, moved = None, None
+    (block,) = tie([low(second_out)], weights)
     for s in range(n):
+        if s >= 1:
+            block, *held = tie([block] + list(held) + ([term0] if s == n - 1 else []))
+            if s == n - 1:
+                term0, held = held[-1], held[:-1]
         after = hop(block) if s < n - 1 else None
-        held = mlp_slot(s, n, where, block, grads[s], up_weight, down_weight, bucket_col, held)
+        held = mlp_slot(
+            s, n, where, block, grads_l[s] + grads_r[n - s if s else 0], up_weight, down_weight, bucket_col, held
+        )
+        if s >= 1:
+            term = dot_t(held[1][s], up_weight)
+            if s > 1:
+                (term,) = tie([term])
+            sent = low(term) if moved is None else add(term, moved)
+            moved = hop(sent)
+        else:
+            term0 = dot_t(held[1][0], up_weight)
         block = after
     active, grad_upper, second_all, grad_all = held
-    grad_second = scatter_ring(lambda s: dot_t(grad_upper[s], up_weight))
+    grad_all, active, second_all, grad_upper = tie([grad_all, active, second_all, grad_upper], sent)
+    pair = grad_part(0, flat(grad_all), flat(active), None)
+    pair = grad_part(1, flat(second_all), flat(grad_upper), pair)
+    (moved,) = tie([moved], pair)
+    grad_second = term0 + moved.astype(F32)
     back_two = norm_backward(grad_second, normed_two, inverse_two, gain2)
     second_gain_part = jnp.sum(grad_second * normed_two, axis=0)
     second_shift_part = jnp.sum(grad_second, axis=0)
-    grad_state = mixed_grad[0].astype(F32) + back_two
-
-    flat = lambda v: v.reshape(length, v.shape[-1])
-    scatter = lambda v: lax.psum_scatter(v.astype(BF16), "dp", scatter_dimension=0, tiled=True)
-    down_grad = scatter(outer(flat(grad_all), flat(active)))
-    up_grad = scatter(outer(flat(second_all), flat(grad_upper)))
-
-    states = [grad_state.astype(BF16)]
-    for s in range(n - 1):
-        states.append(hop(states[-1]))
-    grad_masked = jnp.stack([dot_n(v, output_weight).astype(BF16) for v in states])
-    state_all = jnp.concatenate(states)
-    output_grad = scatter(outer(state_all, flat(masked)))
-    mixed = (state + scatter_ring(lambda s: dot_t(active[s], down_weight))).astype(BF16)
-
+    grad_state = grad_own.astype(F32) + back_two
+
+    wide_grad = lax.psum_scatter(pair, "dp", scatter_dimension=1, tiled=True)
+
+    start = low(grad_state)
+    active, start = tie([active, start])
+    ffn = low(dot_t(flat(active), down_weight)).reshape(n, rows, d)
+    right = [start[:, :half], start[:, half:]]
+    left = list(right)
+    rights, lefts = [list(right)], [list(left)]
+    tick(0, right, left, None)
+    for k in range(1, n):
+        rights.append(list(right))
+        lefts.append(list(left))
+        tick(k, right, left, ffn)
+    late = sorted({1, n - 1})
+    early = [s for s in range(n) if s not in late]
+    pick = lambda slots: sum((rights[0] if s == 0 else lefts[s] + rights[n - s] for s in slots), [])
+    held = dom_part(n, early, where, pick(early), output_weight, None)
+    grad_masked, state_all = dom_part(n, late, where, pick(late), output_weight, held)
     dqkv = attend_back(
         where, query, keys, vals, grad_masked, docs_col, docs_row, heads_col, cos, sin
     )
-    weights = jnp.stack(
-        [w.reshape(d, local_heads, E) for w in (query_weight, key_weight, value_weight)], axis=2
-    ).reshape(d, 3 * local)
-    term = outer(flat(first_all), flat(dqkv)).astype(BF16)
-    qkv_grad = scatter(term)
-    grad_first = scatter_ring(lambda s: dot_t(dqkv[s], weights))
-    n1_out, normed_one, inverse_one = norm_forward(x_rows, gain1, shift1)
-    back_one = norm_backward(grad_first, normed_one, inverse_one, gain1)
-    input_grad = (grad_state + back_one).astype(BF16)
-
-    wide = weights.astype(F32)
-    total_d = jnp.sum(flat(dqkv).astype(F32), axis=0)
-    first_shift_part = jnp.sum(wide * total_d[None], axis=1)
-    product = jnp.sum(wide * term.astype(F32), axis=1)
-    first_gain_part = (product - first_shift * first_shift_part) / first_gain
+    mixed = low(state + owned(ffn, right, left))
+
+    (dqkv,) = tie([dqkv], *right, *left)
+    terms = low(dot_t(flat(dqkv), weights)).reshape(n, rows, d)
+    sent = terms[1]
+    (dqkv,) = tie([dqkv], sent)
+    moved = hop(sent)
+    attn_term, sum_d, sum_da = attn_grads(
+        flat(first_all), flat(state_all), flat(dqkv), flat(masked), query_weight, key_weight, value_weight
+    )
+    (late,) = tie([attn_term], wide_grad)
+    attn_grad = lax.psum_scatter(late, "dp", scatter_dimension=0, tiled=True)
+    (moved,) = tie([moved], attn_term)
+    first_shift_part = sum_d[:, 0]
+    first_gain_part = (sum_da[:, 0] - first_shift * first_shift_part) / first_gain
 
     lead = (rank == 0).astype(F32)
     bucket_part = lead * jnp.sum(
@@ -445,22 +673,37 @@
             jnp.zeros((128 - 4 - HEADS,), F32),
         ]
     )
-    small = xor_sum(xor_sum(small, "dp", n_dp), "mp", n)
-    qkv_grad = qkv_grad.reshape(-1, local_heads, 3, E).astype(F32)
-    pick = lambda i: qkv_grad[:, :, i].reshape(-1, local)
+    small = sum_over(small, "dp", [[(i, i ^ 1) for i in range(n_dp)]])
+    for s in range(2, n):
+        sent = add(terms[s], moved)
+        if s == 2:
+            first_sent = sent
+        moved = hop(sent)
+    if n == 2:
+        first_sent = sent
+
+    planes = tie([send(small, [(i, (i + m) % n) for i in range(n)]) for m in range(1, n)], first_sent)
+    small = small + sum(planes)
+    others = [
+        lax.ppermute(small, "dp", [(i, (i + 2 * m) % n_dp) for i in range(n_dp)])
+        for m in range(1, n_dp // 2)
+    ]
+    small = small + sum(tie(others, moved))
+    input_grad = last_step(own, gain1, terms[0], moved, grad_state)
+    wide_grad, attn_grad = wide_grad.astype(F32), attn_grad.astype(F32)
     return (
         mixed[None],
         input_grad[None],
         small[:d],
         small[d : 2 * d],
-        pick(0),
-        pick(1),
-        pick(2),
-        output_grad.astype(F32),
+        attn_grad[:, :local],
+        attn_grad[:, local : 2 * local],
+        attn_grad[:, 2 * local : 3 * local],
+        attn_grad[:, 3 * local :],
         small[2 * d : 3 * d],
         small[3 * d : 4 * d],
-        up_grad.astype(F32),
-        down_grad.astype(F32),
+        wide_grad[1],
+        wide_grad[0],
         small[4 * d : 4 * d + 4].astype(jnp.int32),
         small[4 * d + 4 : 4 * d + 4 + HEADS].astype(jnp.int32),
     )

time: 762 us -> 595 us (0.78)
  waiting for transfers between devices: 378 us -> 179 us
  Pallas kernels: 99.3 us -> 163 us
  matrix products: 109 us -> 46.6 us
  starting transfers between devices: 92.3 us -> 116 us
  other arithmetic: 30.4 us -> 46.6 us
  local copies, waits for them, and re-layouts: 27.9 us -> 19.3 us
    ppermute x29 -> x46, waiting for transfers between devices: 358 us -> 163 us  [the longest x42 162 us: per_device(): send = lambda v, pairs: lax.ppermute(v, 'mp', pairs)]
    pallas_call x4 -> x10, Pallas kernels: 44.4 us -> 107 us  [the longest x4 46.4 us: mlp_slot(): pl.pallas_call(functools.partial(mlp_body, slot, n), grid_spec=pltpu.Pref...]
    dot_general x8 -> x0, matrix products: 45.3 us -> none  [the longest x4 41.2 us: outer(): lax.dot_general(left, right, (((0,), (0,)), ((), ())), preferred_element_...]
    ppermute x29 -> x46, starting transfers between devices: 91.8 us -> 116 us  [the longest x42 111 us: per_device(): send = lambda v, pairs: lax.ppermute(v, 'mp', pairs)]
    dot_general x16 -> x7, matrix products: 64.1 us -> 46.6 us  [dot_t(): lax.dot_general(left, right, (((1,), (1,)), ((), ())), preferred_element_...]
    another operation x6 -> x0, local copies, waits for them, and re-layouts: 16 us -> none  [the longest x3 12 us: per_device(): jnp.stack([w.reshape(d, local_heads, E) for w in (query_weight, key_weigh...]
    convert_element_type x5 -> x14, other arithmetic: 10.1 us -> 24.7 us  [the longest x9 19.4 us: per_device(): low = lambda v: v.astype(BF16)]
    reduce_scatter x4 -> x2, waiting for transfers between devices: 19.4 us -> 15.9 us  [the longest x1 15.9 us: per_device(): attn_grad = lax.psum_scatter(late, 'dp', scatter_dimension=0, tiled=True)]
  transfers between devices with their start and end apart: 33 -> 48, of which waited for: 24 -> 26; matrix products, arithmetic and copies ran while one was open for 17% -> 15% of each run, Pallas kernels for 9% -> 28%
where the time goes in v2:
time: 595 us; the launch traced here: 586 us
  waiting for transfers between devices  179 us (30%)
  Pallas kernels  163 us (27%)
  starting transfers between devices  116 us (19%)
  other arithmetic  46.6 us (8%)
  matrix products  46.6 us (8%)
  local copies, waits for them, and re-layouts  19.3 us (3%)
  between operations  15.6 us (3%)
    ppermute x42, waiting for transfers between devices, per_device(): send = lambda v, pairs: lax.ppermute(v, 'mp', pairs)  162 us
    ppermute x42, starting transfers between devices, per_device(): send = lambda v, pairs: lax.ppermute(v, 'mp', pairs)  111 us
    dot_general x7, matrix products, dot_t(): lax.dot_general(left, right, (((1,), (1,)), ((), ())), preferred_element_...  46.6 us
    pallas_call x4, Pallas kernels, mlp_slot(): pl.pallas_call(functools.partial(mlp_body, slot, n), grid_spec=pltpu.Pref...  46.4 us
    pallas_call x4, Pallas kernels, qkv_slot(): pl.pallas_call(qkv_body, grid_spec=pltpu.PrefetchScalarGridSpec(num_scala...  28.5 us
    pallas_call x2, Pallas kernels, grad_part(): pl.pallas_call(grad_body, grid=(d // tile,), in_specs=[pl.BlockSpec((t, t...  26.8 us
    convert_element_type x9, other arithmetic, per_device(): low = lambda v: v.astype(BF16)  19.4 us
    pallas_call x1, Pallas kernels, attend_back(): pl.pallas_call(attend_back_body, grid_spec=pltpu.PrefetchScalarGridSpec(n...  17.6 us
  transfers between devices with their start and end apart: 48, of which 26 were waited for; matrix products, arithmetic and copies ran while one was open for 15% of the time, Pallas kernels for 28%

profile of v2, /device:TPU:0, one launch (start us, length us, event | category | flops | bytes accessed | tf_op | source)
XLA Modules:
  0.0 586.2 jit_solution(4541933422370961630)
XLA Ops:
  8.5 5.1 collective-permute-start
  17.9 7.1 %qkv_slot.4 = (bf16[4,256,2048]{2,1,0:T(8,128)(2,1)}, bf16[4,256,512]{2,1,0:T(8,128)(2,1)}, bf16[4,256,512]{2,1,0:T(8,128)(2,1)}, bf16[4,256,512]{2,1,0:T(8,128)(2,1)}) custom-call(s32[3]{0:T(128)} %pad_add_fusion.rank_ref, bf16[256,1024]{1,0:T(8,128)(2,1)} %copy-done.27, bf16[256,1024]{1,0:T(8,128)(2,1)} %copy-done.26, f32[1,2048]{1,0:T(1,128)} %bitcast.72, ...), custom_call_target="tpu_custom_call" | custom-call | flops 1610612736 | bytes 8388608 | tf_op jit(solution)/shard_map/qkv_slot/pallas_call | solution.py:107
  26.0 4.3 collective-permute-start.1
  30.2 7.0 %collective-permute-done.2.xb_ref = bf16[256,1024]{1,0:T(8,128)(2,1)S(1)} collective-permute-done((bf16[256,1024]{1,0:T(8,128)(2,1)S(1)}, bf16[256,1024]{1,0:T(8,128)(2,1)S(1)}, u32[]{:S(2)}, u32[]{:S(2)}) %collective-permute-start.2) | collective-permute-done | bytes 524320 | tf_op jit(solution)/shard_map/ppermute | solution.py:524
  37.2 4.3 collective-permute-start.4
  41.5 7.1 %qkv_slot.5 = (bf16[4,256,2048]{2,1,0:T(8,128)(2,1)}, bf16[4,256,512]{2,1,0:T(8,128)(2,1)}, bf16[4,256,512]{2,1,0:T(8,128)(2,1)}, bf16[4,256,512]{2,1,0:T(8,128)(2,1)}) custom-call(s32[3]{0:T(128)} %pad_add_fusion.rank_ref, bf16[256,1024]{1,0:T(8,128)(2,1)} %copy-done.44, ...), custom_call_target="tpu_custom_call", output_to_operand_aliasing={{0}: (10, {}), {1}: (11, {}), {2}: (12, {}), {3}: (13, {})} | custom-call | flops 1610612736 | bytes 8388608 | tf_op jit(solution)/shard_map/qkv_slot/pallas_call | solution.py:107
  52.8 6.9 %collective-permute-done.4.xb_ref = bf16[256,1024]{1,0:T(8,128)(2,1)S(1)} collective-permute-done((bf16[256,1024]{1,0:T(8,128)(2,1)S(1)}, bf16[256,1024]{1,0:T(8,128)(2,1)S(1)}, u32[]{:S(2)}, u32[]{:S(2)}) %collective-permute-start.4) | collective-permute-done | bytes 524320 | tf_op jit(solution)/shard_map/ppermute | solution.py:524
  63.9 7.1 %qkv_slot.6 = (bf16[4,256,2048]{2,1,0:T(8,128)(2,1)}, bf16[4,256,512]{2,1,0:T(8,128)(2,1)}, bf16[4,256,512]{2,1,0:T(8,128)(2,1)}, bf16[4,256,512]{2,1,0:T(8,128)(2,1)}) custom-call(s32[3]{0:T(128)} %pad_add_fusion.rank_ref, bf16[256,1024]{1,0:T(8,128)(2,1)} %copy-done.47, ...), custom_call_target="tpu_custom_call", output_to_operand_aliasing={{0}: (10, {}), {1}: (11, {}), {2}: (12, {}), {3}: (13, {})} | custom-call | flops 1610612736 | bytes 8388608 | tf_op jit(solution)/shard_map/qkv_slot/pallas_call | solution.py:107
  71.1 9.9 %collective-permute-done.5.xb_ref = bf16[256,1024]{1,0:T(8,128)(2,1)S(1)} collective-permute-done((bf16[256,1024]{1,0:T(8,128)(2,1)S(1)}, bf16[256,1024]{1,0:T(8,128)(2,1)S(1)}, u32[]{:S(2)}, u32[]{:S(2)}) %collective-permute-start.5) | collective-permute-done | bytes 524320 | tf_op jit(solution)/shard_map/ppermute | solution.py:524
  89.1 7.1 %qkv_slot.7 = (bf16[4,256,2048]{2,1,0:T(8,128)(2,1)}, bf16[4,256,512]{2,1,0:T(8,128)(2,1)}, bf16[4,256,512]{2,1,0:T(8,128)(2,1)}, bf16[4,256,512]{2,1,0:T(8,128)(2,1)}) custom-call(s32[3]{0:T(128)} %pad_add_fusion.rank_ref, bf16[256,1024]{1,0:T(8,128)(2,1)} %copy-done.45, ...), custom_call_target="tpu_custom_call", output_to_operand_aliasing={{0}: (10, {}), {1}: (11, {}), {2}: (12, {}), {3}: (13, {})} | custom-call | flops 1610612736 | bytes 8388608 | tf_op jit(solution)/shard_map/qkv_slot/pallas_call | solution.py:107
  96.2 10.4 %attend.1 = bf16[4,256,512]{2,1,0:T(8,128)(2,1)} custom-call(s32[3]{0:T(128)} %pad_add_fusion.rank_ref, bf16[4,256,512]{2,1,0:T(8,128)(2,1)} %get-tuple-element.160.q_ref, bf16[4,256,512]{2,1,0:T(8,128)(2,1)} %get-tuple-element.161.k_ref, bf16[4,256,512]{2,1,0:T(8,128)(2,1)} %get-tuple-element.162.v_ref, s32[4,256,1]{2,1,0:T(8,128)} %reshape.190.dcol_ref, ...), custom_call_target="tpu_custom_call" | custom-call | flops 2147483648 | bytes 4194304 | tf_op jit(solution)/shard_map/attend/pallas_call | solution.py:170
  113.5 4.6 collective-permute-start.7
  119.4 19.9 %collective-permute-done.7.gr_ref = bf16[256,2048]{1,0:T(8,128)(2,1)S(1)} collective-permute-done((bf16[256,2048]{1,0:T(8,128)(2,1)}, bf16[256,2048]{1,0:T(8,128)(2,1)S(1)}, u32[]{:S(2)}, u32[]{:S(2)}) %collective-permute-start.7) | collective-permute-done | bytes 1048608 | tf_op jit(solution)/shard_map/ppermute | solution.py:524
  139.3 5.4 collective-permute-done.11.gl_ref
  148.3 4.8 collective-permute-start.8
  154.4 18.0 %collective-permute-done.8.gr_ref = bf16[256,2048]{1,0:T(8,128)(2,1)} collective-permute-done((bf16[256,2048]{1,0:T(8,128)(2,1)}, bf16[256,2048]{1,0:T(8,128)(2,1)}, u32[]{:S(2)}, u32[]{:S(2)}) %collective-permute-start.8) | collective-permute-done | bytes 1048608 | tf_op jit(solution)/shard_map/ppermute | solution.py:524
  172.4 5.1 collective-permute-done.12.gl_ref
  177.5 4.4 fusion.9
  183.2 5.6 collective-permute-start.9
  193.9 11.4 %collective-permute-done.13 = bf16[256,2048]{1,0:T(8,128)(2,1)S(1)} collective-permute-done((bf16[256,2048]{1,0:T(8,128)(2,1)}, bf16[256,2048]{1,0:T(8,128)(2,1)S(1)}, u32[]{:S(2)}, u32[]{:S(2)}) %collective-permute-start.13) | collective-permute-done | bytes 1048608 | tf_op jit(solution)/shard_map/ppermute | solution.py:524
  212.7 12.4 %mlp_slot.4 = (bf16[4,256,2048]{2,1,0:T(8,128)(2,1)}, bf16[4,256,2048]{2,1,0:T(8,128)(2,1)}, bf16[4,256,2048]{2,1,0:T(8,128)(2,1)}, bf16[4,256,2048]{2,1,0:T(8,128)(2,1)}) custom-call(s32[3]{0:T(128)} %pad_add_fusion.rank_ref, bf16[256,2048]{1,0:T(8,128)(2,1)} %copy-done.18, bf16[256,2048]{1,0:T(8,128)(2,1)} %bitcast.61, bf16[256,2048]{1,0:T(8,128)(2,1)} %bitcast.62, ...), custom_call_target="tpu_custom_call" | custom-call | flops 4294967296 | bytes 20971520 | tf_op jit(solution)/shard_map/mlp_slot/pallas_call | solution.py:304
  225.1 7.4 %fusion.44 = f32[256,2048]{1,0:T(8,128)} fusion(bf16[2048,2048]{1,0:T(8,128)(2,1)} %up_ref.7, bf16[4,256,2048]{2,1,0:T(8,128)(2,1)} %get-tuple-element.171.rest_1_), kind=kOutput, calls=%fused_computation.82 | convolution fusion | flops 2147483648 | bytes 11534336 | tf_op jit(solution)/shard_map/dot_general | solution.py:54
  236.1 11.4 %mlp_slot.5 = (bf16[4,256,2048]{2,1,0:T(8,128)(2,1)}, bf16[4,256,2048]{2,1,0:T(8,128)(2,1)}, bf16[4,256,2048]{2,1,0:T(8,128)(2,1)}, bf16[4,256,2048]{2,1,0:T(8,128)(2,1)}) custom-call(s32[3]{0:T(128)} %pad_add_fusion.rank_ref, bf16[256,2048]{1,0:T(8,128)(2,1)} %copy-done.39, ...), custom_call_target="tpu_custom_call", output_to_operand_aliasing={{0}: (7, {}), {1}: (8, {}), {2}: (9, {}), {3}: (10, {})} | custom-call | flops 4294967296 | bytes 20971520 | tf_op jit(solution)/shard_map/mlp_slot/pallas_call | solution.py:304
  247.4 6.1 %convolution_convert_fusion.3 = bf16[256,2048]{1,0:T(8,128)(2,1)S(1)} fusion(bf16[2048,2048]{1,0:T(8,128)(2,1)} %up_ref.7, bf16[4,256,2048]{2,1,0:T(8,128)(2,1)} %get-tuple-element.180.rest_1_), kind=kOutput, calls=%fused_computation.9 | convolution fusion | flops 2148007936 | bytes 10485760 | tf_op jit(solution)/shard_map/dot_general | solution.py:54
  254.5 4.4 collective-permute-done.15.a_ref
  262.3 11.3 %mlp_slot.6 = (bf16[4,256,2048]{2,1,0:T(8,128)(2,1)}, bf16[4,256,2048]{2,1,0:T(8,128)(2,1)}, bf16[4,256,2048]{2,1,0:T(8,128)(2,1)}, bf16[4,256,2048]{2,1,0:T(8,128)(2,1)}) custom-call(s32[3]{0:T(128)} %pad_add_fusion.rank_ref, bf16[256,2048]{1,0:T(8,128)(2,1)} %copy-done.37, ...), custom_call_target="tpu_custom_call", output_to_operand_aliasing={{0}: (7, {}), {1}: (8, {}), {2}: (9, {}), {3}: (10, {})} | custom-call | flops 4294967296 | bytes 20971520 | tf_op jit(solution)/shard_map/mlp_slot/pallas_call | solution.py:304
  273.6 6.1 %fusion.40 = f32[256,2048]{1,0:T(8,128)S(1)} fusion(bf16[2048,2048]{1,0:T(8,128)(2,1)} %up_ref.7, bf16[4,256,2048]{2,1,0:T(8,128)(2,1)} %get-tuple-element.189.rest_1_), kind=kOutput, calls=%fused_computation.78 | convolution fusion | flops 2147483648 | bytes 11534336 | tf_op jit(solution)/shard_map/dot_general | solution.py:54
  285.3 18.5 %collective-permute-done.16.a_ref = bf16[256,2048]{1,0:T(8,128)(2,1)S(1)} collective-permute-done((bf16[256,2048]{1,0:T(8,128)(2,1)S(1)}, bf16[256,2048]{1,0:T(8,128)(2,1)S(1)}, u32[]{:S(2)}, u32[]{:S(2)}) %collective-permute-start.16) | collective-permute-done | bytes 1048608 | tf_op jit(solution)/shard_map/ppermute | solution.py:524
  304.8 11.4 %mlp_slot.7 = (bf16[4,256,2048]{2,1,0:T(8,128)(2,1)}, bf16[4,256,2048]{2,1,0:T(8,128)(2,1)}, bf16[4,256,2048]{2,1,0:T(8,128)(2,1)}, bf16[4,256,2048]{2,1,0:T(8,128)(2,1)}) custom-call(s32[3]{0:T(128)} %pad_add_fusion.rank_ref, bf16[256,2048]{1,0:T(8,128)(2,1)} %copy-done.38, ...), custom_call_target="tpu_custom_call", output_to_operand_aliasing={{0}: (7, {}), {1}: (8, {}), {2}: (9, {}), {3}: (10, {})} | custom-call | flops 4294967296 | bytes 20971520 | tf_op jit(solution)/shard_map/mlp_slot/pallas_call | solution.py:304
  316.1 6.1 %fusion.42 = f32[256,2048]{1,0:T(8,128)S(1)} fusion(bf16[2048,2048]{1,0:T(8,128)(2,1)} %up_ref.7, bf16[4,256,2048]{2,1,0:T(8,128)(2,1)} %get-tuple-element.199), kind=kOutput, calls=%fused_computation.80 | convolution fusion | flops 2147483648 | bytes 11534336 | tf_op jit(solution)/shard_map/dot_general | solution.py:54
  326.9 13.4 %grad_part.2.rest_0_ = bf16[2,2048,2048]{2,1,0:T(8,128)(2,1)} custom-call(bf16[1024,2048]{1,0:T(8,128)(2,1)} %bitcast.59, bf16[1024,2048]{1,0:T(8,128)(2,1)} %bitcast.57), custom_call_target="tpu_custom_call" | custom-call | flops 8589934592 | bytes 16777216 | tf_op jit(solution)/shard_map/grad_part/pallas_call | solution.py:394
  340.3 13.4 %grad_part.3 = bf16[2,2048,2048]{2,1,0:T(8,128)(2,1)} custom-call(bf16[1024,2048]{1,0:T(8,128)(2,1)} %bitcast.56, bf16[1024,2048]{1,0:T(8,128)(2,1)} %bitcast.55, bf16[2,2048,2048]{2,1,0:T(8,128)(2,1)} %grad_part.2.rest_0_), custom_call_target="tpu_custom_call", output_to_operand_aliasing={{}: (2, {})} | custom-call | flops 8589934592 | bytes 16777216 | tf_op jit(solution)/shard_map/grad_part/pallas_call | solution.py:394
  365.5 5.4 collective-permute-start.28
  370.9 9.1 %convolution_convert_fusion.1 = bf16[1024,2048]{1,0:T(8,128)(2,1)S(1)} fusion(bf16[1024,2048]{1,0:T(8,128)(2,1)S(1)} %bitcast.58, bf16[2048,2048]{1,0:T(8,128)(2,1)S(1)} %bitcast.54), kind=kOutput, calls=%fused_computation.1 | convolution fusion | flops 8592031744 | bytes 16777216 | tf_op jit(solution)/shard_map/dot_general | solution.py:54
  392.7 7.5 %collective-permute-done.25.refs_2_ = bf16[256,1024]{1,0:T(8,128)(2,1)S(1)} collective-permute-done((bf16[256,1024]{1,0:T(8,128)(2,1)S(1)}, bf16[256,1024]{1,0:T(8,128)(2,1)S(1)}, u32[]{:S(2)}, u32[]{:S(2)}) %collective-permute-start.25) | collective-permute-done | bytes 524320 | tf_op jit(solution)/shard_map/ppermute | solution.py:524
  400.2 6.0 %collective-permute-done.33.refs_3_ = bf16[256,1024]{1,0:T(8,128)(2,1)S(1)} collective-permute-done((bf16[256,1024]{1,0:T(8,128)(2,1)S(1)}, bf16[256,1024]{1,0:T(8,128)(2,1)S(1)}, u32[]{:S(2)}, u32[]{:S(2)}) %collective-permute-start.33) | collective-permute-done | bytes 524320 | tf_op jit(solution)/shard_map/ppermute | solution.py:524
  412.9 5.2 collective-permute-start.29
  422.6 5.6 collective-permute-done.34.refs_5_
  436.6 6.0 %collective-permute-start.23 = (bf16[256,1024]{1,0:T(8,128)(2,1)}, bf16[256,1024]{1,0:T(8,128)(2,1)}, u32[]{:S(2)}, u32[]{:S(2)}) collective-permute-start(bf16[256,1024]{1,0:T(8,128)(2,1)} %get-tuple-element.234), channel_id=1, source_target_pairs={{0,1},{1,2},{2,3},{4,5},{5,6},{6,7},{8,9},{9,10},{10,11},{12,13},{... | collective-permute-start | bytes 1572872 | tf_op jit(solution)/shard_map/ppermute | solution.py:524
  442.6 5.6 dom_part.2
  453.4 6.2 %dom_part.3 = (bf16[4,256,512]{2,1,0:T(8,128)(2,1)}, bf16[4,256,2048]{2,1,0:T(8,128)(2,1)}) custom-call(s32[3]{0:T(128)} %pad_add_fusion.rank_ref, s32[2]{0:T(128)} %constant.46.clone.slot_ref, bf16[256,1024]{1,0:T(8,128)(2,1)} %copy-done.22, bf16[256,1024]{1,0:T(8,128)(2,1)} %copy-done.23, ...), custom_call_target="tpu_custom_call", output_to_operand_aliasing={{0}: (11, {}), {1}: (12, {})} | custom-call | flops 1073741824 | bytes 8388608 | tf_op jit(solution)/shard_map/dom_part/pallas_call | solution.py:359
  459.5 17.6 %attend_back.1 = bf16[4,256,1536]{2,1,0:T(8,128)(2,1)} custom-call(s32[3]{0:T(128)} %pad_add_fusion.rank_ref, bf16[4,256,512]{2,1,0:T(8,128)(2,1)} %get-tuple-element.160.q_ref, bf16[4,256,512]{2,1,0:T(8,128)(2,1)} %get-tuple-element.161.k_ref, bf16[4,256,512]{2,1,0:T(8,128)(2,1)} %get-tuple-element.162.v_ref, ...), custom_call_target="tpu_custom_call" | custom-call | flops 199999995904 | bytes 7340032 | tf_op jit(solution)/shard_map/attend_back/pallas_call | solution.py:252
  477.2 8.3 %convolution_convert_fusion = bf16[1024,2048]{1,0:T(8,128)(2,1)S(1)} fusion(bf16[1024,1536]{1,0:T(8,128)(2,1)} %bitcast.81, bf16[2048,1536]{1,0:T(8,128)(2,1)S(1)} %copy-done.42), kind=kOutput, calls=%fused_computation | convolution fusion | flops 6444548096 | bytes 13631488 | tf_op jit(solution)/shard_map/dot_general | solution.py:54
  487.9 16.5 %attn_grads.1 = (bf16[2048,2048]{1,0:T(8,128)(2,1)}, f32[2048,1]{1,0:T(8,128)}, f32[2048,1]{1,0:T(8,128)}) custom-call(bf16[1024,2048]{1,0:T(8,128)(2,1)} %bitcast.60, bf16[1024,2048]{1,0:T(8,128)(2,1)} %bitcast.65, bf16[1024,1536]{1,0:T(8,128)(2,1)} %bitcast.82, bf16[1024,512]{1,0:T(8,128)(2,1)} %bitcast.84, bf16[2048,512]{1,0:T(8,128)(2,1)} %wq_ref.9, ...), custom_call_target="tpu_custom_call" | custom-call | flops 8589934592 | bytes 27262976 | tf_op jit(solution)/shard_map/attn_grads/pallas_call | solution.py:440
  518.5 12.7 %collective-permute-done.37 = bf16[256,2048]{1,0:T(8,128)(2,1)S(1)} collective-permute-done((bf16[256,2048]{1,0:T(8,128)(2,1)S(1)}, bf16[256,2048]{1,0:T(8,128)(2,1)S(1)}, u32[]{:S(2)}, u32[]{:S(2)}) %collective-permute-start.37) | collective-permute-done | bytes 1048608 | tf_op jit(solution)/shard_map/ppermute | solution.py:524
  544.1 6.6 %collective-permute-done.38.moved_ref = bf16[256,2048]{1,0:T(8,128)(2,1)S(1)} collective-permute-done((bf16[256,2048]{1,0:T(8,128)(2,1)S(1)}, bf16[256,2048]{1,0:T(8,128)(2,1)S(1)}, u32[]{:S(2)}, u32[]{:S(2)}) %collective-permute-start.38) | collective-permute-done | bytes 1048608 | tf_op jit(solution)/shard_map/ppermute | solution.py:524
  552.5 5.1 last_step.1
  560.4 15.9 %reduce-scatter.5.cloned.1.call-done = bf16[256,2048]{1,0:T(8,128)(2,1)} async-done(((bf16[2048,2048]{1,0:T(8,128)(2,1)}), bf16[256,2048]{1,0:T(8,128)(2,1)}) %reduce-scatter.5.cloned.1.call-update) | async-done | bytes 1048592 | tf_op jit(solution)/shard_map/reduce_scatter | solution.py:652
  (261 shorter events, 154.0 us)
Async XLA Ops:
  7.2 497.2 %reduce-scatter.3.cloned.1.call-start = ((), (), s32[]{:S(2)}) async-start(), calls=%async_computation.2 | async-start | bytes 18874368 | tf_op jit(solution)/shard_map/reduce_scatter | solution.py:620
  8.5 17.4 %collective-permute-start = (bf16[256,1024]{1,0:T(8,128)(2,1)S(1)}, bf16[256,1024]{1,0:T(8,128)(2,1)S(1)}, u32[]{:S(2)}, u32[]{:S(2)}) collective-permute-start(bf16[256,1024]{1,0:T(8,128)(2,1)S(1)} %get-tuple-element.258.xa_ref), channel_id=1, source_target_pairs={{0,3},{1,0},{2,1},{3,2},{4,7},{5,4},{6,5},{7,6},{8,11},{9,8},{10,9... | collective-permute-start | bytes 1572872 | tf_op jit(solution)/shard_map/ppermute | solution.py:524
  13.6 23.6 %collective-permute-start.2 = (bf16[256,1024]{1,0:T(8,128)(2,1)S(1)}, bf16[256,1024]{1,0:T(8,128)(2,1)S(1)}, u32[]{:S(2)}, u32[]{:S(2)}) collective-permute-start(bf16[256,1024]{1,0:T(8,128)(2,1)S(1)} %get-tuple-element.257.xb_ref), channel_id=1, source_target_pairs={{0,3},{1,0},{2,1},{3,2},{4,7},{5,4},{6,5},{7,6},{8,11},{9,8},{10,9... | collective-permute-start | bytes 1572872 | tf_op jit(solution)/shard_map/ppermute | solution.py:524
  26.0 22.7 %collective-permute-start.1 = (bf16[256,1024]{1,0:T(8,128)(2,1)S(1)}, bf16[256,1024]{1,0:T(8,128)(2,1)S(1)}, u32[]{:S(2)}, u32[]{:S(2)}) collective-permute-start(bf16[256,1024]{1,0:T(8,128)(2,1)S(1)} %collective-permute-done.xa_ref), channel_id=1, source_target_pairs={{0,3},{1,0},{2,1},{3,2},{4,7},{5,4},{6,5},{7,6},{8,11},{9,8},{10,9... | collective-permute-start | bytes 1572872 | tf_op jit(solution)/shard_map/ppermute | solution.py:524
  37.2 22.5 %collective-permute-start.4 = (bf16[256,1024]{1,0:T(8,128)(2,1)S(1)}, bf16[256,1024]{1,0:T(8,128)(2,1)S(1)}, u32[]{:S(2)}, u32[]{:S(2)}) collective-permute-start(bf16[256,1024]{1,0:T(8,128)(2,1)S(1)} %collective-permute-done.2.xb_ref), channel_id=1, source_target_pairs={{0,3},{1,0},{2,1},{3,2},{4,7},{5,4},{6,5},{7,6},{8,11},{9,8},{10,9... | collective-permute-start | bytes 1572872 | tf_op jit(solution)/shard_map/ppermute | solution.py:524
  48.7 22.4 %collective-permute-start.3 = (bf16[256,1024]{1,0:T(8,128)(2,1)S(1)}, bf16[256,1024]{1,0:T(8,128)(2,1)S(1)}, u32[]{:S(2)}, u32[]{:S(2)}) collective-permute-start(bf16[256,1024]{1,0:T(8,128)(2,1)S(1)} %collective-permute-done.1.xa_ref), channel_id=1, source_target_pairs={{0,3},{1,0},{2,1},{3,2},{4,7},{5,4},{6,5},{7,6},{8,11},{9,8},{10,9... | collective-permute-start | bytes 1572872 | tf_op jit(solution)/shard_map/ppermute | solution.py:524
  59.7 21.3 %collective-permute-start.5 = (bf16[256,1024]{1,0:T(8,128)(2,1)S(1)}, bf16[256,1024]{1,0:T(8,128)(2,1)S(1)}, u32[]{:S(2)}, u32[]{:S(2)}) collective-permute-start(bf16[256,1024]{1,0:T(8,128)(2,1)S(1)} %collective-permute-done.4.xb_ref), channel_id=1, source_target_pairs={{0,3},{1,0},{2,1},{3,2},{4,7},{5,4},{6,5},{7,6},{8,11},{9,8},{10,9... | collective-permute-start | bytes 1572872 | tf_op jit(solution)/shard_map/ppermute | solution.py:524
  81.0 29.2 %collective-permute-start.6 = (bf16[256,2048]{1,0:T(8,128)(2,1)S(1)}, bf16[256,2048]{1,0:T(8,128)(2,1)S(1)}, u32[]{:S(2)}, u32[]{:S(2)}) collective-permute-start(bf16[256,2048]{1,0:T(8,128)(2,1)S(1)} %bitcast.63), channel_id=1, source_target_pairs={{0,1},{1,2},{2,3},{4,5},{5,6},{6,7},{8,9},{9,10},{10,11},{12,13},{... | collective-permute-start | bytes 3145736 | tf_op jit(solution)/shard_map/ppermute | solution.py:524
  83.4 26.8 %collective-permute-start.10 = (bf16[256,2048]{1,0:T(8,128)(2,1)S(1)}, bf16[256,2048]{1,0:T(8,128)(2,1)S(1)}, u32[]{:S(2)}, u32[]{:S(2)}) collective-permute-start(bf16[256,2048]{1,0:T(8,128)(2,1)S(1)} %bitcast.64), channel_id=1, source_target_pairs={{1,0},{2,1},{3,2},{5,4},{6,5},{7,6},{9,8},{10,9},{11,10},{13,12},{... | collective-permute-start | bytes 3145736 | tf_op jit(solution)/shard_map/ppermute | solution.py:524
  113.5 25.8 %collective-permute-start.7 = (bf16[256,2048]{1,0:T(8,128)(2,1)}, bf16[256,2048]{1,0:T(8,128)(2,1)S(1)}, u32[]{:S(2)}, u32[]{:S(2)}) collective-permute-start(bf16[256,2048]{1,0:T(8,128)(2,1)} %get-tuple-element.249), channel_id=1, source_target_pairs={{0,1},{1,2},{2,3},{4,5},{5,6},{6,7},{8,9},{9,10},{10,11},{12,13},{... | collective-permute-start | bytes 3145736 | tf_op jit(solution)/shard_map/ppermute | solution.py:524
  118.1 26.6 %collective-permute-start.11 = (bf16[256,2048]{1,0:T(8,128)(2,1)}, bf16[256,2048]{1,0:T(8,128)(2,1)S(1)}, u32[]{:S(2)}, u32[]{:S(2)}) collective-permute-start(bf16[256,2048]{1,0:T(8,128)(2,1)} %get-tuple-element.250), channel_id=1, source_target_pairs={{1,0},{2,1},{3,2},{5,4},{6,5},{7,6},{9,8},{10,9},{11,10},{13,12},{... | collective-permute-start | bytes 3145736 | tf_op jit(solution)/shard_map/ppermute | solution.py:524
  148.3 24.1 %collective-permute-start.8 = (bf16[256,2048]{1,0:T(8,128)(2,1)}, bf16[256,2048]{1,0:T(8,128)(2,1)}, u32[]{:S(2)}, u32[]{:S(2)}) collective-permute-start(bf16[256,2048]{1,0:T(8,128)(2,1)} %get-tuple-element.247), channel_id=1, source_target_pairs={{0,1},{1,2},{2,3},{4,5},{5,6},{6,7},{8,9},{9,10},{10,11},{12,13},{... | collective-permute-start | bytes 3145736 | tf_op jit(solution)/shard_map/ppermute | solution.py:524
  153.1 24.4 %collective-permute-start.12 = (bf16[256,2048]{1,0:T(8,128)(2,1)}, bf16[256,2048]{1,0:T(8,128)(2,1)S(1)}, u32[]{:S(2)}, u32[]{:S(2)}) collective-permute-start(bf16[256,2048]{1,0:T(8,128)(2,1)} %get-tuple-element.248), channel_id=1, source_target_pairs={{1,0},{2,1},{3,2},{5,4},{6,5},{7,6},{9,8},{10,9},{11,10},{13,12},{... | collective-permute-start | bytes 3145736 | tf_op jit(solution)/shard_map/ppermute | solution.py:524
  181.9 23.4 %collective-permute-start.13 = (bf16[256,2048]{1,0:T(8,128)(2,1)}, bf16[256,2048]{1,0:T(8,128)(2,1)S(1)}, u32[]{:S(2)}, u32[]{:S(2)}) collective-permute-start(bf16[256,2048]{1,0:T(8,128)(2,1)} %get-tuple-element.246), channel_id=1, source_target_pairs={{1,0},{2,1},{3,2},{5,4},{6,5},{7,6},{9,8},{10,9},{11,10},{13,12},{... | collective-permute-start | bytes 3145736 | tf_op jit(solution)/shard_map/ppermute | solution.py:524
  183.2 23.4 %collective-permute-start.9 = (bf16[256,2048]{1,0:T(8,128)(2,1)}, bf16[256,2048]{1,0:T(8,128)(2,1)}, u32[]{:S(2)}, u32[]{:S(2)}) collective-permute-start(bf16[256,2048]{1,0:T(8,128)(2,1)} %get-tuple-element.245), channel_id=1, source_target_pairs={{0,1},{1,2},{2,3},{4,5},{5,6},{6,7},{8,9},{9,10},{10,11},{12,13},{... | collective-permute-start | bytes 3145736 | tf_op jit(solution)/shard_map/ppermute | solution.py:524
  210.1 22.7 %collective-permute-start.14 = (bf16[256,2048]{1,0:T(8,128)(2,1)S(1)}, bf16[256,2048]{1,0:T(8,128)(2,1)S(1)}, u32[]{:S(2)}, u32[]{:S(2)}) collective-permute-start(bf16[256,2048]{1,0:T(8,128)(2,1)S(1)} %add_convert_fusion.4.a_ref), channel_id=1, source_target_pairs={{0,3},{1,0},{2,1},{3,2},{4,7},{5,4},{6,5},{7,6},{8,11},{9,8},{10,9... | collective-permute-start | bytes 3145736 | tf_op jit(solution)/shard_map/ppermute | solution.py:524
  232.8 26.1 %collective-permute-start.15 = (bf16[256,2048]{1,0:T(8,128)(2,1)S(1)}, bf16[256,2048]{1,0:T(8,128)(2,1)S(1)}, u32[]{:S(2)}, u32[]{:S(2)}) collective-permute-start(bf16[256,2048]{1,0:T(8,128)(2,1)S(1)} %collective-permute-done.14.a_ref), channel_id=1, source_target_pairs={{0,3},{1,0},{2,1},{3,2},{4,7},{5,4},{6,5},{7,6},{8,11},{9,8},{10,9... | collective-permute-start | bytes 3145736 | tf_op jit(solution)/shard_map/ppermute | solution.py:524
  253.5 27.8 %collective-permute-start.17 = (bf16[256,2048]{1,0:T(8,128)(2,1)S(1)}, bf16[256,2048]{1,0:T(8,128)(2,1)S(1)}, u32[]{:S(2)}, u32[]{:S(2)}) collective-permute-start(bf16[256,2048]{1,0:T(8,128)(2,1)S(1)} %convolution_convert_fusion.3), channel_id=1, source_target_pairs={{0,3},{1,0},{2,1},{3,2},{4,7},{5,4},{6,5},{7,6},{8,11},{9,8},{10,9... | collective-permute-start | bytes 3145736 | tf_op jit(solution)/shard_map/ppermute | solution.py:524
  258.9 44.9 %collective-permute-start.16 = (bf16[256,2048]{1,0:T(8,128)(2,1)S(1)}, bf16[256,2048]{1,0:T(8,128)(2,1)S(1)}, u32[]{:S(2)}, u32[]{:S(2)}) collective-permute-start(bf16[256,2048]{1,0:T(8,128)(2,1)S(1)} %collective-permute-done.15.a_ref), channel_id=1, source_target_pairs={{0,3},{1,0},{2,1},{3,2},{4,7},{5,4},{6,5},{7,6},{8,11},{9,8},{10,9... | collective-permute-start | bytes 3145736 | tf_op jit(solution)/shard_map/ppermute | solution.py:524
  281.6 40.6 %collective-permute-start.18 = (bf16[256,2048]{1,0:T(8,128)(2,1)S(1)}, bf16[256,2048]{1,0:T(8,128)(2,1)S(1)}, u32[]{:S(2)}, u32[]{:S(2)}) collective-permute-start(bf16[256,2048]{1,0:T(8,128)(2,1)S(1)} %add_convert_fusion.3), channel_id=1, source_target_pairs={{0,3},{1,0},{2,1},{3,2},{4,7},{5,4},{6,5},{7,6},{8,11},{9,8},{10,9... | collective-permute-start | bytes 3145736 | tf_op jit(solution)/shard_map/ppermute | solution.py:524
  323.5 30.3 %collective-permute-start.19 = (bf16[256,2048]{1,0:T(8,128)(2,1)}, bf16[256,2048]{1,0:T(8,128)(2,1)}, u32[]{:S(2)}, u32[]{:S(2)}) collective-permute-start(bf16[256,2048]{1,0:T(8,128)(2,1)} %add_convert_fusion.2), channel_id=1, source_target_pairs={{0,3},{1,0},{2,1},{3,2},{4,7},{5,4},{6,5},{7,6},{8,11},{9,8},{10,9... | collective-permute-start | bytes 3145736 | tf_op jit(solution)/shard_map/ppermute | solution.py:524
  353.7 222.6 %reduce-scatter.5.cloned.1.call-start = ((), (), s32[]{:S(2)}) async-start(), calls=%async_computation.3 | async-start | bytes 9437184 | tf_op jit(solution)/shard_map/reduce_scatter | solution.py:652
  361.3 18.8 %collective-permute-start.20 = (bf16[256,1024]{1,0:T(8,128)(2,1)S(1)}, bf16[256,1024]{1,0:T(8,128)(2,1)S(1)}, u32[]{:S(2)}, u32[]{:S(2)}) collective-permute-start(bf16[256,1024]{1,0:T(8,128)(2,1)S(1)} %get-tuple-element.255.refs_0_), channel_id=1, source_target_pairs={{0,1},{1,2},{2,3},{4,5},{5,6},{6,7},{8,9},{9,10},{10,11},{12,13},{... | collective-permute-start | bytes 1572872 | tf_op jit(solution)/shard_map/ppermute | solution.py:524
  362.9 17.2 %collective-permute-start.24 = (bf16[256,1024]{1,0:T(8,128)(2,1)S(1)}, bf16[256,1024]{1,0:T(8,128)(2,1)S(1)}, u32[]{:S(2)}, u32[]{:S(2)}) collective-permute-start(bf16[256,1024]{1,0:T(8,128)(2,1)S(1)} %get-tuple-element.255.refs_0_), channel_id=1, source_target_pairs={{1,0},{2,1},{3,2},{5,4},{6,5},{7,6},{9,8},{10,9},{11,10},{13,12},{... | collective-permute-start | bytes 1572872 | tf_op jit(solution)/shard_map/ppermute | solution.py:524
  364.2 19.7 %collective-permute-start.32 = (bf16[256,1024]{1,0:T(8,128)(2,1)S(1)}, bf16[256,1024]{1,0:T(8,128)(2,1)S(1)}, u32[]{:S(2)}, u32[]{:S(2)}) collective-permute-start(bf16[256,1024]{1,0:T(8,128)(2,1)S(1)} %get-tuple-element.256.refs_1_), channel_id=1, source_target_pairs={{1,0},{2,1},{3,2},{5,4},{6,5},{7,6},{9,8},{10,9},{11,10},{13,12},{... | collective-permute-start | bytes 1572872 | tf_op jit(solution)/shard_map/ppermute | solution.py:524
  365.5 23.2 %collective-permute-start.28 = (bf16[256,1024]{1,0:T(8,128)(2,1)S(1)}, bf16[256,1024]{1,0:T(8,128)(2,1)S(1)}, u32[]{:S(2)}, u32[]{:S(2)}) collective-permute-start(bf16[256,1024]{1,0:T(8,128)(2,1)S(1)} %get-tuple-element.256.refs_1_), channel_id=1, source_target_pairs={{0,1},{1,2},{2,3},{4,5},{5,6},{6,7},{8,9},{9,10},{10,11},{12,13},{... | collective-permute-start | bytes 1572872 | tf_op jit(solution)/shard_map/ppermute | solution.py:524
  384.6 8.1 %collective-permute-start.21 = (bf16[256,1024]{1,0:T(8,128)(2,1)S(1)}, bf16[256,1024]{1,0:T(8,128)(2,1)S(1)}, u32[]{:S(2)}, u32[]{:S(2)}) collective-permute-start(bf16[256,1024]{1,0:T(8,128)(2,1)S(1)} %get-tuple-element.242), channel_id=1, source_target_pairs={{0,1},{1,2},{2,3},{4,5},{5,6},{6,7},{8,9},{9,10},{10,11},{12,13},{... | collective-permute-start | bytes 1572872 | tf_op jit(solution)/shard_map/ppermute | solution.py:524
  386.1 14.1 %collective-permute-start.25 = (bf16[256,1024]{1,0:T(8,128)(2,1)S(1)}, bf16[256,1024]{1,0:T(8,128)(2,1)S(1)}, u32[]{:S(2)}, u32[]{:S(2)}) collective-permute-start(bf16[256,1024]{1,0:T(8,128)(2,1)S(1)} %get-tuple-element.243), channel_id=1, source_target_pairs={{1,0},{2,1},{3,2},{5,4},{6,5},{7,6},{9,8},{10,9},{11,10},{13,12},{... | collective-permute-start | bytes 1572872 | tf_op jit(solution)/shard_map/ppermute | solution.py:524
  387.4 18.9 %collective-permute-start.33 = (bf16[256,1024]{1,0:T(8,128)(2,1)S(1)}, bf16[256,1024]{1,0:T(8,128)(2,1)S(1)}, u32[]{:S(2)}, u32[]{:S(2)}) collective-permute-start(bf16[256,1024]{1,0:T(8,128)(2,1)S(1)} %get-tuple-element.244), channel_id=1, source_target_pairs={{1,0},{2,1},{3,2},{5,4},{6,5},{7,6},{9,8},{10,9},{11,10},{13,12},{... | collective-permute-start | bytes 1572872 | tf_op jit(solution)/shard_map/ppermute | solution.py:524
  407.1 12.5 %collective-permute-start.22 = (bf16[256,1024]{1,0:T(8,128)(2,1)S(1)}, bf16[256,1024]{1,0:T(8,128)(2,1)S(1)}, u32[]{:S(2)}, u32[]{:S(2)}) collective-permute-start(bf16[256,1024]{1,0:T(8,128)(2,1)S(1)} %get-tuple-element.238), channel_id=1, source_target_pairs={{0,1},{1,2},{2,3},{4,5},{5,6},{6,7},{8,9},{9,10},{10,11},{12,13},{... | collective-permute-start | bytes 1572872 | tf_op jit(solution)/shard_map/ppermute | solution.py:524
  410.3 12.4 %collective-permute-start.26 = (bf16[256,1024]{1,0:T(8,128)(2,1)S(1)}, bf16[256,1024]{1,0:T(8,128)(2,1)S(1)}, u32[]{:S(2)}, u32[]{:S(2)}) collective-permute-start(bf16[256,1024]{1,0:T(8,128)(2,1)S(1)} %get-tuple-element.239), channel_id=1, source_target_pairs={{1,0},{2,1},{3,2},{5,4},{6,5},{7,6},{9,8},{10,9},{11,10},{13,12},{... | collective-permute-start | bytes 1572872 | tf_op jit(solution)/shard_map/ppermute | solution.py:524
  411.6 16.7 %collective-permute-start.34 = (bf16[256,1024]{1,0:T(8,128)(2,1)S(1)}, bf16[256,1024]{1,0:T(8,128)(2,1)S(1)}, u32[]{:S(2)}, u32[]{:S(2)}) collective-permute-start(bf16[256,1024]{1,0:T(8,128)(2,1)S(1)} %get-tuple-element.240), channel_id=1, source_target_pairs={{1,0},{2,1},{3,2},{5,4},{6,5},{7,6},{9,8},{10,9},{11,10},{13,12},{... | collective-permute-start | bytes 1572872 | tf_op jit(solution)/shard_map/ppermute | solution.py:524
  412.9 15.4 %collective-permute-start.29 = (bf16[256,1024]{1,0:T(8,128)(2,1)S(1)}, bf16[256,1024]{1,0:T(8,128)(2,1)S(1)}, u32[]{:S(2)}, u32[]{:S(2)}) collective-permute-start(bf16[256,1024]{1,0:T(8,128)(2,1)S(1)} %get-tuple-element.241), channel_id=1, source_target_pairs={{0,1},{1,2},{2,3},{4,5},{5,6},{6,7},{8,9},{9,10},{10,11},{12,13},{... | collective-permute-start | bytes 1572872 | tf_op jit(solution)/shard_map/ppermute | solution.py:524
  430.4 17.8 %collective-permute-start.30 = (bf16[256,1024]{1,0:T(8,128)(2,1)}, bf16[256,1024]{1,0:T(8,128)(2,1)S(1)}, u32[]{:S(2)}, u32[]{:S(2)}) collective-permute-start(bf16[256,1024]{1,0:T(8,128)(2,1)} %get-tuple-element.237), channel_id=1, source_target_pairs={{0,1},{1,2},{2,3},{4,5},{5,6},{6,7},{8,9},{9,10},{10,11},{12,13},{... | collective-permute-start | bytes 1572872 | tf_op jit(solution)/shard_map/ppermute | solution.py:524
  434.0 43.2 %collective-permute-start.35 = (bf16[256,1024]{1,0:T(8,128)(2,1)}, bf16[256,1024]{1,0:T(8,128)(2,1)}, u32[]{:S(2)}, u32[]{:S(2)}) collective-permute-start(bf16[256,1024]{1,0:T(8,128)(2,1)} %get-tuple-element.236), channel_id=1, source_target_pairs={{1,0},{2,1},{3,2},{5,4},{6,5},{7,6},{9,8},{10,9},{11,10},{13,12},{... | collective-permute-start | bytes 1572872 | tf_op jit(solution)/shard_map/ppermute | solution.py:524
  435.3 41.9 %collective-permute-start.27 = (bf16[256,1024]{1,0:T(8,128)(2,1)}, bf16[256,1024]{1,0:T(8,128)(2,1)}, u32[]{:S(2)}, u32[]{:S(2)}) collective-permute-start(bf16[256,1024]{1,0:T(8,128)(2,1)} %get-tuple-element.235), channel_id=1, source_target_pairs={{1,0},{2,1},{3,2},{5,4},{6,5},{7,6},{9,8},{10,9},{11,10},{13,12},{... | collective-permute-start | bytes 1572872 | tf_op jit(solution)/shard_map/ppermute | solution.py:524
  436.6 40.6 %collective-permute-start.23 = (bf16[256,1024]{1,0:T(8,128)(2,1)}, bf16[256,1024]{1,0:T(8,128)(2,1)}, u32[]{:S(2)}, u32[]{:S(2)}) collective-permute-start(bf16[256,1024]{1,0:T(8,128)(2,1)} %get-tuple-element.234), channel_id=1, source_target_pairs={{0,1},{1,2},{2,3},{4,5},{5,6},{6,7},{8,9},{9,10},{10,11},{12,13},{... | collective-permute-start | bytes 1572872 | tf_op jit(solution)/shard_map/ppermute | solution.py:524
  449.2 28.0 %collective-permute-start.31 = (bf16[256,1024]{1,0:T(8,128)(2,1)}, bf16[256,1024]{1,0:T(8,128)(2,1)}, u32[]{:S(2)}, u32[]{:S(2)}) collective-permute-start(bf16[256,1024]{1,0:T(8,128)(2,1)} %fusion.35), channel_id=1, source_target_pairs={{0,1},{1,2},{2,3},{4,5},{5,6},{6,7},{8,9},{9,10},{10,11},{12,13},{... | collective-permute-start | bytes 1572872 | tf_op jit(solution)/shard_map/ppermute | solution.py:524
  487.9 18.4 %collective-permute-start.36 = (bf16[256,2048]{1,0:T(8,128)(2,1)S(1)}, bf16[256,2048]{1,0:T(8,128)(2,1)S(1)}, u32[]{:S(2)}, u32[]{:S(2)}) collective-permute-start(bf16[256,2048]{1,0:T(8,128)(2,1)S(1)} %get-tuple-element.232), channel_id=1, source_target_pairs={{0,3},{1,0},{2,1},{3,2},{4,7},{5,4},{6,5},{7,6},{8,11},{9,8},{10,9... | collective-permute-start | bytes 3145736 | tf_op jit(solution)/shard_map/ppermute | solution.py:524
  507.9 23.4 %collective-permute-start.37 = (bf16[256,2048]{1,0:T(8,128)(2,1)S(1)}, bf16[256,2048]{1,0:T(8,128)(2,1)S(1)}, u32[]{:S(2)}, u32[]{:S(2)}) collective-permute-start(bf16[256,2048]{1,0:T(8,128)(2,1)S(1)} %add_convert_fusion.1), channel_id=1, source_target_pairs={{0,3},{1,0},{2,1},{3,2},{4,7},{5,4},{6,5},{7,6},{8,11},{9,8},{10,9... | collective-permute-start | bytes 3145736 | tf_op jit(solution)/shard_map/ppermute | solution.py:524
  511.4 1.7 collective-permute-start.39
  513.1 23.0 %collective-permute-start.40 = (f32[8320]{0:T(1024)S(1)}, f32[8320]{0:T(1024)S(1)}, u32[]{:S(2)}, u32[]{:S(2)}) collective-permute-start(f32[8320]{0:T(1024)S(1)} %add.187), channel_id=1, source_target_pairs={{0,1},{1,2},{2,3},{3,0},{4,5},{5,6},{6,7},{7,4},{8,9},{9,10},{10,1... | collective-permute-start | bytes 99848 | tf_op jit(solution)/shard_map/ppermute | solution.py:524
  513.7 22.4 %collective-permute-start.41 = (f32[8320]{0:T(1024)S(1)}, f32[8320]{0:T(1024)S(1)}, u32[]{:S(2)}, u32[]{:S(2)}) collective-permute-start(f32[8320]{0:T(1024)S(1)} %add.187), channel_id=1, source_target_pairs={{0,2},{1,3},{2,0},{3,1},{4,6},{5,7},{6,4},{7,5},{8,10},{9,11},{10,... | collective-permute-start | bytes 99848 | tf_op jit(solution)/shard_map/ppermute | solution.py:524
  515.7 20.5 %collective-permute-start.42 = (f32[8320]{0:T(1024)S(1)}, f32[8320]{0:T(1024)S(1)}, u32[]{:S(2)}, u32[]{:S(2)}) collective-permute-start(f32[8320]{0:T(1024)S(1)} %add.187), channel_id=1, source_target_pairs={{0,3},{1,0},{2,1},{3,2},{4,7},{5,4},{6,5},{7,6},{8,11},{9,8},{10,9... | collective-permute-start | bytes 99848 | tf_op jit(solution)/shard_map/ppermute | solution.py:524
  532.9 17.8 %collective-permute-start.38 = (bf16[256,2048]{1,0:T(8,128)(2,1)S(1)}, bf16[256,2048]{1,0:T(8,128)(2,1)S(1)}, u32[]{:S(2)}, u32[]{:S(2)}) collective-permute-start(bf16[256,2048]{1,0:T(8,128)(2,1)S(1)} %add_convert_fusion), channel_id=1, source_target_pairs={{0,3},{1,0},{2,1},{3,2},{4,7},{5,4},{6,5},{7,6},{8,11},{9,8},{10,9... | collective-permute-start | bytes 3145736 | tf_op jit(solution)/shard_map/ppermute | solution.py:524
  536.2 7.3 %collective-permute-start.43 = (f32[8320]{0:T(1024)S(1)}, f32[8320]{0:T(1024)S(1)}, u32[]{:S(2)}, u32[]{:S(2)}) collective-permute-start(f32[8320]{0:T(1024)S(1)} %add_add_fusion.2), channel_id=1, source_target_pairs={{0,8},{4,12},{8,16},{12,20},{16,24},{20,28},{24,0},{28,4},{1,9},{5... | collective-permute-start | bytes 99848 | tf_op jit(solution)/shard_map/ppermute | solution.py:688
  537.8 5.7 collective-permute-start.44
  539.4 4.7 collective-permute-start.45
  (63 other events, 893.3 us)
Sparse Core Ops, SparseCore 0:
  353.8 114.1 reduce-scatter.2
  504.5 71.7 reduce-scatter.4

commit v3 on v2

--- a/solution.py
+++ b/solution.py
@@ -260,7 +260,7 @@
         ),
         out_shape=jax.ShapeDtypeStruct((n, rows, 3 * local), BF16),
         compiler_params=params(),
-        cost_estimate=cost(200e9, 14 * t * local),
+        cost_estimate=cost(230e9, 14 * t * local),
         name="attend_back",
     )(rank, q, k, v, do, docs_col, docs_row, heads_col, cos, sin)
 
@@ -329,30 +329,28 @@
 
 def dom_body(n, slots, rank_ref, slot_ref, *refs):
     dom_ref, all_ref = refs[-2:]
-    count = sum(2 if s == 0 else 4 for s in slots)
+    count = sum(1 if s == 0 else 2 for s in slots)
     flows, w_ref = list(refs[:count]), refs[count]
-    half = flows[0].shape[1]
-
-    def fill(pair):
-        all_ref[0, :, :half] = pair[0][...]
-        all_ref[0, :, half:] = pair[1][...]
+
+    def fill(ref):
+        all_ref[0] = ref[...]
 
     for i, s in enumerate(slots):
         here = pl.program_id(0) == i
         if s == 0:
-            pl.when(here)(functools.partial(fill, flows[:2]))
-            flows = flows[2:]
+            pl.when(here)(functools.partial(fill, flows[0]))
+            flows = flows[1:]
         else:
             ahead = rank_ref[0] + s < n
-            pl.when(here & ahead)(functools.partial(fill, flows[:2]))
-            pl.when(here & jnp.logical_not(ahead))(functools.partial(fill, flows[2:4]))
-            flows = flows[4:]
+            pl.when(here & ahead)(functools.partial(fill, flows[0]))
+            pl.when(here & jnp.logical_not(ahead))(functools.partial(fill, flows[1]))
+            flows = flows[2:]
     dom_ref[0] = dot_n(all_ref[0], w_ref[...]).astype(BF16)
 
 
 def dom_part(n, slots, rank, flows, weight, held):
-    rows, half = flows[0].shape
-    d, local = weight.shape
+    rows, d = flows[0].shape
+    local = weight.shape[1]
     whole = lambda i, r, s: (0, 0)
     extra = [] if held is None else list(held)
     at = 2 + len(flows) + 1
@@ -361,7 +359,7 @@
         grid_spec=pltpu.PrefetchScalarGridSpec(
             num_scalar_prefetch=2,
             grid=(len(slots),),
-            in_specs=[pl.BlockSpec((rows, half), whole)] * len(flows)
+            in_specs=[pl.BlockSpec((rows, d), whole)] * len(flows)
             + [pl.BlockSpec((d, local), whole)]
             + [pl.BlockSpec(memory_space=pl.ANY)] * len(extra),
             out_specs=[
@@ -408,35 +406,17 @@
     )(lhs, rhs, *extra)
 
 
-def attn_grad_body(a_ref, s_ref, dqkv_ref, om_ref, wq_ref, wk_ref, wv_ref, out_ref, sum_ref, dot_ref, tot_ref):
-    local = om_ref.shape[1]
-
-    @pl.when(pl.program_id(0) == 0)
-    def _():
-        tot_ref[...] = jnp.sum(dqkv_ref[...].astype(F32), axis=0, keepdims=True)
-
-    act = a_ref[...]
-    plain = None
-    for i, w_ref in enumerate((wq_ref, wk_ref, wv_ref)):
-        cols = slice(i * local, (i + 1) * local)
-        part = outer(act, dqkv_ref[:, cols])
-        out_ref[:, cols] = part.astype(BF16)
-        w = w_ref[...].astype(F32)
-        one, two = w * tot_ref[:, cols], w * part
-        plain = one if plain is None else plain + one
-        mixed = two if i == 0 else mixed + two
-    sum_ref[...] = jnp.sum(plain, axis=1, keepdims=True)
-    dot_ref[...] = jnp.sum(mixed, axis=1, keepdims=True)
-    out_ref[:, 3 * local :] = outer(s_ref[...], om_ref[...]).astype(BF16)
-
-
-def attn_grads(act, states, dqkv, om, wq, wk, wv):
+def attn_grad_body(a_ref, s_ref, dqkv_ref, om_ref, out_ref):
+    wide = dqkv_ref.shape[1]
+    out_ref[:, :wide] = outer(a_ref[...], dqkv_ref[...]).astype(BF16)
+    out_ref[:, wide:] = outer(s_ref[...], om_ref[...]).astype(BF16)
+
+
+def attn_grads(act, states, dqkv, om):
     t, d = act.shape
     local = om.shape[1]
     tile = min(512, d)
     col = pl.BlockSpec((t, tile), lambda j: (0, j))
-    wspec = pl.BlockSpec((tile, local), lambda j: (j, 0))
-    vec = pl.BlockSpec((tile, 1), lambda j: (j, 0))
     return pl.pallas_call(
         attn_grad_body,
         grid=(d // tile,),
@@ -445,21 +425,44 @@
             col,
             pl.BlockSpec((t, 3 * local), lambda j: (0, 0)),
             pl.BlockSpec((t, local), lambda j: (0, 0)),
-            wspec,
-            wspec,
-            wspec,
         ],
-        out_specs=[pl.BlockSpec((tile, 4 * local), lambda j: (j, 0)), vec, vec],
-        out_shape=[
-            jax.ShapeDtypeStruct((d, 4 * local), BF16),
-            jax.ShapeDtypeStruct((d, 1), F32),
-            jax.ShapeDtypeStruct((d, 1), F32),
-        ],
-        scratch_shapes=[pltpu.VMEM((1, 3 * local), F32)],
-        compiler_params=params(),
-        cost_estimate=cost(8 * t * d * local, 2 * t * (2 * d + 4 * local) + 14 * d * local),
+        out_specs=pl.BlockSpec((tile, 4 * local), lambda j: (j, 0)),
+        out_shape=jax.ShapeDtypeStruct((d, 4 * local), BF16),
+        compiler_params=params(),
+        cost_estimate=cost(8 * t * d * local, 2 * t * (2 * d + 4 * local) + 8 * d * local),
         name="attn_grads",
-    )(act, states, dqkv, om, wq, wk, wv)
+    )(act, states, dqkv, om)
+
+
+def join_body(slot, first, rank_ref, moved_ref, term_ref, out_ref):
+    adds = rank_ref[0] < first if slot >= 0 else rank_ref[0] >= first
+
+    @pl.when(adds)
+    def _():
+        out_ref[...] = (moved_ref[...].astype(F32) + term_ref[0].astype(F32)).astype(BF16)
+
+    @pl.when(jnp.logical_not(adds))
+    def _():
+        out_ref[...] = moved_ref[...]
+
+
+def join(rank, moved, terms, slot, first, right):
+    rows, d = moved.shape
+    tile = min(64, rows)
+    row = pl.BlockSpec((tile, d), lambda i, r: (i, 0))
+    return pl.pallas_call(
+        functools.partial(join_body, 0 if right else -1, first),
+        grid_spec=pltpu.PrefetchScalarGridSpec(
+            num_scalar_prefetch=1,
+            grid=(rows // tile,),
+            in_specs=[row, pl.BlockSpec((1, tile, d), lambda i, r: (slot, i, 0))],
+            out_specs=row,
+        ),
+        out_shape=jax.ShapeDtypeStruct((rows, d), BF16),
+        compiler_params=params(),
+        cost_estimate=cost(rows * d, 6 * rows * d),
+        name="join",
+    )(rank, moved, terms)
 
 
 def last_body(x_ref, gain_ref, term_ref, moved_ref, state_ref, out_ref):
@@ -528,18 +531,13 @@
     left_line = [(i + 1, i) for i in range(n - 1)]
 
     def tick(k, right, left, terms):
-        width = d // len(right)
-        for p in range(len(right)):
-            cols = slice(p * width, (p + 1) * width)
-            r, l = right[p], left[p]
-            if k:
-                r = low(r.astype(F32) + (rank < k).astype(F32) * terms[n - k][:, cols].astype(F32))
-                l = low(l.astype(F32) + (rank >= n - k).astype(F32) * terms[k][:, cols].astype(F32))
-            right[p], left[p] = send(r, right_line), send(l, left_line)
+        if k:
+            right = join(where, right, terms, n - k, k, True)
+            left = join(where, left, terms, k, n - k, False)
+        return send(right, right_line), send(left, left_line)
 
     def owned(terms, right, left):
-        moved = [r.astype(F32) + l.astype(F32) for r, l in zip(right, left)]
-        return terms[0].astype(F32) + (jnp.concatenate(moved, axis=1) if len(moved) > 1 else moved[0])
+        return terms[0].astype(F32) + right.astype(F32) + left.astype(F32)
 
     low = lambda v: v.astype(BF16)
     flat = lambda v: v.reshape(length, v.shape[-1])
@@ -570,16 +568,16 @@
     first_all, query, keys, vals = held
 
     grad_own = mixed_grad[0]
-    right = list(tie([grad_own], *block))
-    left = list(right)
-    grads_r, grads_l = [list(right)], [list(left)]
-    tick(0, right, left, None)
+    (right,) = tie([grad_own], block[0])
+    left = right
+    grads_r, grads_l = [right], [left]
+    right, left = tick(0, right, left, None)
     masked = attend(where, query, keys, vals, docs_col, docs_row, heads_col)
     terms = low(dot_t(flat(masked), output_weight)).reshape(n, rows, d)
     for k in range(1, n):
-        grads_r.append(list(right))
-        grads_l.append(list(left))
-        tick(k, right, left, terms)
+        grads_r.append(right)
+        grads_l.append(left)
+        right, left = tick(k, right, left, terms)
     attn = owned(terms, right, left)
     x_rows = own.astype(F32)
     state = x_rows + attn
@@ -595,7 +593,7 @@
                 term0, held = held[-1], held[:-1]
         after = hop(block) if s < n - 1 else None
         held = mlp_slot(
-            s, n, where, block, grads_l[s] + grads_r[n - s if s else 0], up_weight, down_weight, bucket_col, held
+            s, n, where, block, [grads_l[s], grads_r[n - s if s else 0]], up_weight, down_weight, bucket_col, held
         )
         if s >= 1:
             term = dot_t(held[1][s], up_weight)
@@ -607,32 +605,32 @@
             term0 = dot_t(held[1][0], up_weight)
         block = after
     active, grad_upper, second_all, grad_all = held
-    grad_all, active, second_all, grad_upper = tie([grad_all, active, second_all, grad_upper], sent)
+    grad_all, active = tie([grad_all, active], sent)
     pair = grad_part(0, flat(grad_all), flat(active), None)
-    pair = grad_part(1, flat(second_all), flat(grad_upper), pair)
-    (moved,) = tie([moved], pair)
+    (active,) = tie([active], pair)
+    ffn = low(dot_t(flat(active), down_weight)).reshape(n, rows, d)
+    (moved,) = tie([moved], ffn)
     grad_second = term0 + moved.astype(F32)
     back_two = norm_backward(grad_second, normed_two, inverse_two, gain2)
     second_gain_part = jnp.sum(grad_second * normed_two, axis=0)
     second_shift_part = jnp.sum(grad_second, axis=0)
     grad_state = grad_own.astype(F32) + back_two
 
+    start = low(grad_state)
+    second_all, grad_upper, start = tie([second_all, grad_upper, start])
+    right = left = start
+    rights, lefts = [start], [start]
+    right, left = tick(0, right, left, None)
+    pair = grad_part(1, flat(second_all), flat(grad_upper), pair)
     wide_grad = lax.psum_scatter(pair, "dp", scatter_dimension=1, tiled=True)
-
-    start = low(grad_state)
-    active, start = tie([active, start])
-    ffn = low(dot_t(flat(active), down_weight)).reshape(n, rows, d)
-    right = [start[:, :half], start[:, half:]]
-    left = list(right)
-    rights, lefts = [list(right)], [list(left)]
-    tick(0, right, left, None)
+    right, left = tie([right, left], pair)
     for k in range(1, n):
-        rights.append(list(right))
-        lefts.append(list(left))
-        tick(k, right, left, ffn)
+        rights.append(right)
+        lefts.append(left)
+        right, left = tick(k, right, left, ffn)
     late = sorted({1, n - 1})
     early = [s for s in range(n) if s not in late]
-    pick = lambda slots: sum((rights[0] if s == 0 else lefts[s] + rights[n - s] for s in slots), [])
+    pick = lambda slots: sum(([start] if s == 0 else [lefts[s], rights[n - s]] for s in slots), [])
     held = dom_part(n, early, where, pick(early), output_weight, None)
     grad_masked, state_all = dom_part(n, late, where, pick(late), output_weight, held)
     dqkv = attend_back(
@@ -640,19 +638,20 @@
     )
     mixed = low(state + owned(ffn, right, left))
 
-    (dqkv,) = tie([dqkv], *right, *left)
-    terms = low(dot_t(flat(dqkv), weights)).reshape(n, rows, d)
-    sent = terms[1]
+    (dqkv,) = tie([dqkv], right, left)
+    sent = low(dot_t(dqkv[1], weights))
     (dqkv,) = tie([dqkv], sent)
     moved = hop(sent)
-    attn_term, sum_d, sum_da = attn_grads(
-        flat(first_all), flat(state_all), flat(dqkv), flat(masked), query_weight, key_weight, value_weight
-    )
+    attn_term = attn_grads(flat(first_all), flat(state_all), flat(dqkv), flat(masked))
+    (dqkv,) = tie([dqkv], attn_term)
+    terms = low(dot_t(flat(dqkv), weights)).reshape(n, rows, d)
+    sum_d = jnp.sum(terms.astype(F32), axis=(0, 1))
+    sum_da = jnp.sum(terms.astype(F32) * first_all.astype(F32), axis=(0, 1))
     (late,) = tie([attn_term], wide_grad)
     attn_grad = lax.psum_scatter(late, "dp", scatter_dimension=0, tiled=True)
-    (moved,) = tie([moved], attn_term)
-    first_shift_part = sum_d[:, 0]
-    first_gain_part = (sum_da[:, 0] - first_shift * first_shift_part) / first_gain
+    (moved,) = tie([moved], terms)
+    first_shift_part = sum_d
+    first_gain_part = (sum_da - first_shift * sum_d) / first_gain
 
     lead = (rank == 0).astype(F32)
     bucket_part = lead * jnp.sum(
@@ -688,8 +687,8 @@
         lax.ppermute(small, "dp", [(i, (i + 2 * m) % n_dp) for i in range(n_dp)])
         for m in range(1, n_dp // 2)
     ]
-    small = small + sum(tie(others, moved))
     input_grad = last_step(own, gain1, terms[0], moved, grad_state)
+    small = small + sum(tie(others, input_grad))
     wide_grad, attn_grad = wide_grad.astype(F32), attn_grad.astype(F32)
     return (
         mixed[None],

time: 595 us -> 587 us (0.987)
  Pallas kernels: 163 us -> 212 us
  waiting for transfers between devices: 179 us -> 145 us
  starting transfers between devices: 116 us -> 86.9 us
  other arithmetic: 46.6 us -> 28.1 us
  local copies, waits for them, and re-layouts: 19.3 us -> 32.6 us
  matrix products: 46.6 us -> 57.4 us
    pallas_call x0 -> x12, Pallas kernels: none -> 51.4 us  [join(): pl.pallas_call(functools.partial(join_body, 0 if right else -1, first), g...]
    ppermute x42 -> x34, starting transfers between devices: 111 us -> 82.5 us  [per_device(): send = lambda v, pairs: lax.ppermute(v, 'mp', pairs)]
    ppermute x42 -> x34, waiting for transfers between devices: 162 us -> 140 us  [per_device(): send = lambda v, pairs: lax.ppermute(v, 'mp', pairs)]
    reduce_scatter x1, waiting for transfers between devices: 15.9 us -> 0.01 us  [per_device(): attn_grad = lax.psum_scatter(late, 'dp', scatter_dimension=0, tiled=True)]
    convert_element_type x9 -> x2, other arithmetic: 19.4 us -> 4 us  [per_device(): low = lambda v: v.astype(BF16)]
    unnamed x129 -> x103, local copies, waits for them, and re-layouts: 7.6 us -> 19.9 us
    dot_general x7 -> x8, matrix products: 46.6 us -> 57.4 us  [dot_t(): lax.dot_general(left, right, (((1,), (1,)), ((), ())), preferred_element_...]
  transfers between devices with their start and end apart: 48 -> 40, of which waited for: 26 -> 21; matrix products, arithmetic and copies ran while one was open for 15% -> 15% of each run, Pallas kernels for 28% -> 37%
where the time goes in v3:
time: 587 us; the launch traced here: 577 us
  Pallas kernels  212 us (36%)
  waiting for transfers between devices  145 us (25%)
  starting transfers between devices  86.9 us (15%)
  matrix products  57.4 us (10%)
  local copies, waits for them, and re-layouts  32.6 us (6%)
  other arithmetic  28.1 us (5%)
  between operations  15.2 us (3%)
    ppermute x34, waiting for transfers between devices, per_device(): send = lambda v, pairs: lax.ppermute(v, 'mp', pairs)  140 us
    ppermute x34, starting transfers between devices, per_device(): send = lambda v, pairs: lax.ppermute(v, 'mp', pairs)  82.5 us
    dot_general x8, matrix products, dot_t(): lax.dot_general(left, right, (((1,), (1,)), ((), ())), preferred_element_...  57.4 us
    pallas_call x12, Pallas kernels, join(): pl.pallas_call(functools.partial(join_body, 0 if right else -1, first), g...  51.4 us
    pallas_call x4, Pallas kernels, mlp_slot(): pl.pallas_call(functools.partial(mlp_body, slot, n), grid_spec=pltpu.Pref...  46.4 us
    pallas_call x4, Pallas kernels, qkv_slot(): pl.pallas_call(qkv_body, grid_spec=pltpu.PrefetchScalarGridSpec(num_scala...  28.6 us
    pallas_call x2, Pallas kernels, grad_part(): pl.pallas_call(grad_body, grid=(d // tile,), in_specs=[pl.BlockSpec((t, t...  26.9 us
    unnamed x103, local copies, waits for them, and re-layouts  19.9 us
  transfers between devices with their start and end apart: 40, of which 21 were waited for; matrix products, arithmetic and copies ran while one was open for 15% of the time, Pallas kernels for 37%

profile of v3, /device:TPU:0, one launch (start us, length us, event | category | flops | bytes accessed | tf_op | source)
XLA Modules:
  0.0 577.2 jit_solution(18138752686094552922)
XLA Ops:
  8.5 5.1 collective-permute-start
  17.9 7.2 %qkv_slot.4 = (bf16[4,256,2048]{2,1,0:T(8,128)(2,1)}, bf16[4,256,512]{2,1,0:T(8,128)(2,1)}, bf16[4,256,512]{2,1,0:T(8,128)(2,1)}, bf16[4,256,512]{2,1,0:T(8,128)(2,1)}) custom-call(s32[3]{0:T(128)} %pad_add_fusion.rank_ref, bf16[256,1024]{1,0:T(8,128)(2,1)} %copy-done.29, bf16[256,1024]{1,0:T(8,128)(2,1)} %copy-done.28, f32[1,2048]{1,0:T(1,128)} %bitcast.90, ...), custom_call_target="tpu_custom_call" | custom-call | flops 1610612736 | bytes 8388608 | tf_op jit(solution)/shard_map/qkv_slot/pallas_call | solution.py:107
  30.2 7.0 %collective-permute-done.2.xb_ref = bf16[256,1024]{1,0:T(8,128)(2,1)} collective-permute-done((bf16[256,1024]{1,0:T(8,128)(2,1)S(1)}, bf16[256,1024]{1,0:T(8,128)(2,1)}, u32[]{:S(2)}, u32[]{:S(2)}) %collective-permute-start.2) | collective-permute-done | bytes 524320 | tf_op jit(solution)/shard_map/ppermute | solution.py:527
  37.2 4.4 collective-permute-start.4
  41.6 7.1 %qkv_slot.5 = (bf16[4,256,2048]{2,1,0:T(8,128)(2,1)}, bf16[4,256,512]{2,1,0:T(8,128)(2,1)}, bf16[4,256,512]{2,1,0:T(8,128)(2,1)}, bf16[4,256,512]{2,1,0:T(8,128)(2,1)}) custom-call(s32[3]{0:T(128)} %pad_add_fusion.rank_ref, bf16[256,1024]{1,0:T(8,128)(2,1)} %copy-done.35, ...), custom_call_target="tpu_custom_call", output_to_operand_aliasing={{0}: (10, {}), {1}: (11, {}), {2}: (12, {}), {3}: (13, {})} | custom-call | flops 1610612736 | bytes 8388608 | tf_op jit(solution)/shard_map/qkv_slot/pallas_call | solution.py:107
  52.8 7.0 %collective-permute-done.4.xb_ref = bf16[256,1024]{1,0:T(8,128)(2,1)} collective-permute-done((bf16[256,1024]{1,0:T(8,128)(2,1)}, bf16[256,1024]{1,0:T(8,128)(2,1)}, u32[]{:S(2)}, u32[]{:S(2)}) %collective-permute-start.4) | collective-permute-done | bytes 524320 | tf_op jit(solution)/shard_map/ppermute | solution.py:527
  64.0 7.1 %qkv_slot.6 = (bf16[4,256,2048]{2,1,0:T(8,128)(2,1)}, bf16[4,256,512]{2,1,0:T(8,128)(2,1)}, bf16[4,256,512]{2,1,0:T(8,128)(2,1)}, bf16[4,256,512]{2,1,0:T(8,128)(2,1)}) custom-call(s32[3]{0:T(128)} %pad_add_fusion.rank_ref, bf16[256,1024]{1,0:T(8,128)(2,1)} %copy-done.37, ...), custom_call_target="tpu_custom_call", output_to_operand_aliasing={{0}: (10, {}), {1}: (11, {}), {2}: (12, {}), {3}: (13, {})} | custom-call | flops 1610612736 | bytes 8388608 | tf_op jit(solution)/shard_map/qkv_slot/pallas_call | solution.py:107
  82.3 7.2 %qkv_slot.7 = (bf16[4,256,2048]{2,1,0:T(8,128)(2,1)}, bf16[4,256,512]{2,1,0:T(8,128)(2,1)}, bf16[4,256,512]{2,1,0:T(8,128)(2,1)}, bf16[4,256,512]{2,1,0:T(8,128)(2,1)}) custom-call(s32[3]{0:T(128)} %pad_add_fusion.rank_ref, bf16[256,1024]{1,0:T(8,128)(2,1)} %copy-done.36, ...), custom_call_target="tpu_custom_call", output_to_operand_aliasing={{0}: (10, {}), {1}: (11, {}), {2}: (12, {}), {3}: (13, {})} | custom-call | flops 1610612736 | bytes 8388608 | tf_op jit(solution)/shard_map/qkv_slot/pallas_call | solution.py:107
  89.5 10.4 %attend.1 = bf16[4,256,512]{2,1,0:T(8,128)(2,1)} custom-call(s32[3]{0:T(128)} %pad_add_fusion.rank_ref, bf16[4,256,512]{2,1,0:T(8,128)(2,1)} %get-tuple-element.160.q_ref, bf16[4,256,512]{2,1,0:T(8,128)(2,1)} %get-tuple-element.161.k_ref, bf16[4,256,512]{2,1,0:T(8,128)(2,1)} %get-tuple-element.162.v_ref, s32[4,256,1]{2,1,0:T(8,128)} %reshape.185.dcol_ref, ...), custom_call_target="tpu_custom_call" | custom-call | flops 2147483648 | bytes 4194304 | tf_op jit(solution)/shard_map/attend/pallas_call | solution.py:170
  99.9 5.6 convolution_convert_fusion.2
  106.4 4.3 join.12
  119.6 15.3 %collective-permute-done.7.moved_ref.gr_ref = bf16[256,2048]{1,0:T(8,128)(2,1)S(1)} collective-permute-done((bf16[256,2048]{1,0:T(8,128)(2,1)}, bf16[256,2048]{1,0:T(8,128)(2,1)S(1)}, u32[]{:S(2)}, u32[]{:S(2)}) %collective-permute-start.7) | collective-permute-done | bytes 1048608 | tf_op jit(solution)/shard_map/ppermute | solution.py:527
  135.9 4.3 join.13
  140.2 4.4 collective-permute-start.8
  151.3 14.2 %collective-permute-done.8.moved_ref.gr_ref = bf16[256,2048]{1,0:T(8,128)(2,1)S(1)} collective-permute-done((bf16[256,2048]{1,0:T(8,128)(2,1)}, bf16[256,2048]{1,0:T(8,128)(2,1)S(1)}, u32[]{:S(2)}, u32[]{:S(2)}) %collective-permute-start.8) | collective-permute-done | bytes 1048608 | tf_op jit(solution)/shard_map/ppermute | solution.py:527
  166.5 4.3 join.14
  170.8 5.4 collective-permute-start.9
  187.9 7.4 %collective-permute-done.9 = bf16[256,2048]{1,0:T(8,128)(2,1)} collective-permute-done((bf16[256,2048]{1,0:T(8,128)(2,1)}, bf16[256,2048]{1,0:T(8,128)(2,1)}, u32[]{:S(2)}, u32[]{:S(2)}) %collective-permute-start.9) | collective-permute-done | bytes 1048608 | tf_op jit(solution)/shard_map/ppermute | solution.py:527
  195.2 10.2 %collective-permute-done.13 = bf16[256,2048]{1,0:T(8,128)(2,1)S(1)} collective-permute-done((bf16[256,2048]{1,0:T(8,128)(2,1)}, bf16[256,2048]{1,0:T(8,128)(2,1)S(1)}, u32[]{:S(2)}, u32[]{:S(2)}) %collective-permute-start.13) | collective-permute-done | bytes 1048608 | tf_op jit(solution)/shard_map/ppermute | solution.py:527
  209.4 12.4 %mlp_slot.4 = (bf16[4,256,2048]{2,1,0:T(8,128)(2,1)}, bf16[4,256,2048]{2,1,0:T(8,128)(2,1)}, bf16[4,256,2048]{2,1,0:T(8,128)(2,1)}, bf16[4,256,2048]{2,1,0:T(8,128)(2,1)}) custom-call(s32[3]{0:T(128)} %pad_add_fusion.rank_ref, bf16[256,2048]{1,0:T(8,128)(2,1)} %copy-done.25, bf16[256,2048]{1,0:T(8,128)(2,1)} %bitcast.79, bf16[256,2048]{1,0:T(8,128)(2,1)} %bitcast.80, ...), custom_call_target="tpu_custom_call" | custom-call | flops 4294967296 | bytes 20971520 | tf_op jit(solution)/shard_map/mlp_slot/pallas_call | solution.py:304
  221.8 7.4 %fusion.6 = f32[256,2048]{1,0:T(8,128)} fusion(bf16[2048,2048]{1,0:T(8,128)(2,1)} %up_ref.7, bf16[4,256,2048]{2,1,0:T(8,128)(2,1)} %get-tuple-element.171.rest_1_), kind=kOutput, calls=%fused_computation.29 | convolution fusion | flops 2147483648 | bytes 11534336 | tf_op jit(solution)/shard_map/dot_general | solution.py:54
  233.1 11.3 %mlp_slot.5 = (bf16[4,256,2048]{2,1,0:T(8,128)(2,1)}, bf16[4,256,2048]{2,1,0:T(8,128)(2,1)}, bf16[4,256,2048]{2,1,0:T(8,128)(2,1)}, bf16[4,256,2048]{2,1,0:T(8,128)(2,1)}) custom-call(s32[3]{0:T(128)} %pad_add_fusion.rank_ref, bf16[256,2048]{1,0:T(8,128)(2,1)} %copy-done.32, ...), custom_call_target="tpu_custom_call", output_to_operand_aliasing={{0}: (7, {}), {1}: (8, {}), {2}: (9, {}), {3}: (10, {})} | custom-call | flops 4294967296 | bytes 20971520 | tf_op jit(solution)/shard_map/mlp_slot/pallas_call | solution.py:304
  244.4 6.1 %convolution_convert_fusion.4 = bf16[256,2048]{1,0:T(8,128)(2,1)S(1)} fusion(bf16[2048,2048]{1,0:T(8,128)(2,1)} %up_ref.7, bf16[4,256,2048]{2,1,0:T(8,128)(2,1)} %get-tuple-element.180.rest_1_), kind=kOutput, calls=%fused_computation.6 | convolution fusion | flops 2148007936 | bytes 10485760 | tf_op jit(solution)/shard_map/dot_general | solution.py:54
  251.3 6.5 %collective-permute-done.15.a_ref = bf16[256,2048]{1,0:T(8,128)(2,1)S(1)} collective-permute-done((bf16[256,2048]{1,0:T(8,128)(2,1)S(1)}, bf16[256,2048]{1,0:T(8,128)(2,1)S(1)}, u32[]{:S(2)}, u32[]{:S(2)}) %collective-permute-start.15) | collective-permute-done | bytes 1048608 | tf_op jit(solution)/shard_map/ppermute | solution.py:527
  258.8 11.3 %mlp_slot.6 = (bf16[4,256,2048]{2,1,0:T(8,128)(2,1)}, bf16[4,256,2048]{2,1,0:T(8,128)(2,1)}, bf16[4,256,2048]{2,1,0:T(8,128)(2,1)}, bf16[4,256,2048]{2,1,0:T(8,128)(2,1)}) custom-call(s32[3]{0:T(128)} %pad_add_fusion.rank_ref, bf16[256,2048]{1,0:T(8,128)(2,1)} %copy-done.30, ...), custom_call_target="tpu_custom_call", output_to_operand_aliasing={{0}: (7, {}), {1}: (8, {}), {2}: (9, {}), {3}: (10, {})} | custom-call | flops 4294967296 | bytes 20971520 | tf_op jit(solution)/shard_map/mlp_slot/pallas_call | solution.py:304
  270.1 6.1 %fusion.2 = f32[256,2048]{1,0:T(8,128)S(1)} fusion(bf16[2048,2048]{1,0:T(8,128)(2,1)} %up_ref.7, bf16[4,256,2048]{2,1,0:T(8,128)(2,1)} %get-tuple-element.189.rest_1_), kind=kOutput, calls=%fused_computation.25 | convolution fusion | flops 2147483648 | bytes 11534336 | tf_op jit(solution)/shard_map/dot_general | solution.py:54
  281.6 21.1 %collective-permute-done.16.a_ref = bf16[256,2048]{1,0:T(8,128)(2,1)S(1)} collective-permute-done((bf16[256,2048]{1,0:T(8,128)(2,1)S(1)}, bf16[256,2048]{1,0:T(8,128)(2,1)S(1)}, u32[]{:S(2)}, u32[]{:S(2)}) %collective-permute-start.16) | collective-permute-done | bytes 1048608 | tf_op jit(solution)/shard_map/ppermute | solution.py:527
  303.7 11.3 %mlp_slot.7 = (bf16[4,256,2048]{2,1,0:T(8,128)(2,1)}, bf16[4,256,2048]{2,1,0:T(8,128)(2,1)}, bf16[4,256,2048]{2,1,0:T(8,128)(2,1)}, bf16[4,256,2048]{2,1,0:T(8,128)(2,1)}) custom-call(s32[3]{0:T(128)} %pad_add_fusion.rank_ref, bf16[256,2048]{1,0:T(8,128)(2,1)} %copy-done.31, ...), custom_call_target="tpu_custom_call", output_to_operand_aliasing={{0}: (7, {}), {1}: (8, {}), {2}: (9, {}), {3}: (10, {})} | custom-call | flops 4294967296 | bytes 20971520 | tf_op jit(solution)/shard_map/mlp_slot/pallas_call | solution.py:304
  315.1 6.1 %fusion.4 = f32[256,2048]{1,0:T(8,128)S(1)} fusion(bf16[2048,2048]{1,0:T(8,128)(2,1)} %up_ref.7, bf16[4,256,2048]{2,1,0:T(8,128)(2,1)} %get-tuple-element.203), kind=kOutput, calls=%fused_computation.27 | convolution fusion | flops 2147483648 | bytes 11534336 | tf_op jit(solution)/shard_map/dot_general | solution.py:54
  323.2 13.6 %grad_part.2.rest_0_ = bf16[2,2048,2048]{2,1,0:T(8,128)(2,1)} custom-call(bf16[1024,2048]{1,0:T(8,128)(2,1)} %bitcast.77, bf16[1024,2048]{1,0:T(8,128)(2,1)} %bitcast.75), custom_call_target="tpu_custom_call" | custom-call | flops 8589934592 | bytes 16777216 | tf_op jit(solution)/shard_map/grad_part/pallas_call | solution.py:392
  336.8 12.8 %convolution_convert_fusion.1 = bf16[1024,2048]{1,0:T(8,128)(2,1)} fusion(bf16[1024,2048]{1,0:T(8,128)(2,1)S(1)} %bitcast.76, bf16[2048,2048]{1,0:T(8,128)(2,1)} %down_ref.7), kind=kOutput, calls=%fused_computation.3 | convolution fusion | flops 8592031744 | bytes 16777216 | tf_op jit(solution)/shard_map/dot_general | solution.py:54
  359.4 13.3 %grad_part.3 = bf16[2,2048,2048]{2,1,0:T(8,128)(2,1)} custom-call(bf16[1024,2048]{1,0:T(8,128)(2,1)} %bitcast.74, bf16[1024,2048]{1,0:T(8,128)(2,1)} %bitcast.73, bf16[2,2048,2048]{2,1,0:T(8,128)(2,1)} %grad_part.2.rest_0_), custom_call_target="tpu_custom_call", output_to_operand_aliasing={{}: (2, {})} | custom-call | flops 8589934592 | bytes 16777216 | tf_op jit(solution)/shard_map/grad_part/pallas_call | solution.py:392
  378.7 4.5 join.18
  385.0 4.4 join.21
  390.7 9.6 %collective-permute-done.22.moved_ref.refs_2_ = bf16[256,2048]{1,0:T(8,128)(2,1)S(1)} collective-permute-done((bf16[256,2048]{1,0:T(8,128)(2,1)}, bf16[256,2048]{1,0:T(8,128)(2,1)S(1)}, u32[]{:S(2)}, u32[]{:S(2)}) %collective-permute-start.22) | collective-permute-done | bytes 1048608 | tf_op jit(solution)/shard_map/ppermute | solution.py:527
  401.3 4.3 join.19
  405.6 4.3 collective-permute-start.23
  417.6 5.9 %dom_part.2 = (bf16[4,256,512]{2,1,0:T(8,128)(2,1)}, bf16[4,256,2048]{2,1,0:T(8,128)(2,1)}) custom-call(s32[3]{0:T(128)} %pad_add_fusion.rank_ref, s32[2]{0:T(128)} %iota_multiply_fusion.slot_ref, bf16[256,2048]{1,0:T(8,128)(2,1)} %copy-done.21, bf16[256,2048]{1,0:T(8,128)(2,1)} %copy-done.23, bf16[256,2048]{1,0:T(8,128)(2,1)} %copy-done.22, ...), custom_call_target="tpu_custom_call" | custom-call | flops 1073741824 | bytes 8388608 | tf_op jit(solution)/shard_map/dom_part/pallas_call | solution.py:357
  425.4 4.3 join.20
  429.8 5.2 collective-permute-start.24
  441.5 5.9 %dom_part.3 = (bf16[4,256,512]{2,1,0:T(8,128)(2,1)}, bf16[4,256,2048]{2,1,0:T(8,128)(2,1)}) custom-call(s32[3]{0:T(128)} %pad_add_fusion.rank_ref, s32[2]{0:T(128)} %constant.41.clone.slot_ref, bf16[256,2048]{1,0:T(8,128)(2,1)} %copy-done.17, bf16[256,2048]{1,0:T(8,128)(2,1)} %copy-done.19, ...), custom_call_target="tpu_custom_call", output_to_operand_aliasing={{0}: (7, {}), {1}: (8, {})} | custom-call | flops 1073741824 | bytes 8388608 | tf_op jit(solution)/shard_map/dom_part/pallas_call | solution.py:357
  447.5 17.8 %attend_back.1 = bf16[4,256,1536]{2,1,0:T(8,128)(2,1)} custom-call(s32[3]{0:T(128)} %pad_add_fusion.rank_ref, bf16[4,256,512]{2,1,0:T(8,128)(2,1)} %get-tuple-element.160.q_ref, bf16[4,256,512]{2,1,0:T(8,128)(2,1)} %get-tuple-element.161.k_ref, bf16[4,256,512]{2,1,0:T(8,128)(2,1)} %get-tuple-element.162.v_ref, ...), custom_call_target="tpu_custom_call" | custom-call | flops 230000001024 | bytes 7340032 | tf_op jit(solution)/shard_map/attend_back/pallas_call | solution.py:252
  468.2 4.4 collective-permute-start.28
  472.6 14.0 %attn_grads.1 = bf16[2048,2048]{1,0:T(8,128)(2,1)} custom-call(bf16[1024,2048]{1,0:T(8,128)(2,1)} %bitcast.78, bf16[1024,2048]{1,0:T(8,128)(2,1)} %bitcast.83, bf16[1024,1536]{1,0:T(8,128)(2,1)} %bitcast.99, bf16[1024,512]{1,0:T(8,128)(2,1)} %bitcast.102), custom_call_target="tpu_custom_call" | custom-call | flops 8589934592 | bytes 20971520 | tf_op jit(solution)/shard_map/attn_grads/pallas_call | solution.py:420
  490.3 10.5 %multiply_reduce_fusion = (f32[2048]{0:T(1024)S(1)}, bf16[1024,2048]{1,0:T(8,128)(2,1)S(1)}) fusion(bf16[4,256,2048]{2,1,0:T(8,128)(2,1)} %get-tuple-element.211, bf16[1024,1536]{1,0:T(8,128)(2,1)} %bitcast.100, bf16[2048,1536]{1,0:T(8,128)(2,1)} %copy-done.33), kind=kOutput, calls=%fused_computation.1 | convolution fusion | flops 6452934656 | bytes 17833984 | tf_op jit(solution)/shard_map/dot_general | solution.py:54
  515.9 14.3 %collective-permute-done.29 = bf16[256,2048]{1,0:T(8,128)(2,1)} collective-permute-done((bf16[256,2048]{1,0:T(8,128)(2,1)S(1)}, bf16[256,2048]{1,0:T(8,128)(2,1)}, u32[]{:S(2)}, u32[]{:S(2)}) %collective-permute-start.29) | collective-permute-done | bytes 1048608 | tf_op jit(solution)/shard_map/ppermute | solution.py:527
  546.9 9.7 %collective-permute-done.30.moved_ref = bf16[256,2048]{1,0:T(8,128)(2,1)S(1)} collective-permute-done((bf16[256,2048]{1,0:T(8,128)(2,1)S(1)}, bf16[256,2048]{1,0:T(8,128)(2,1)S(1)}, u32[]{:S(2)}, u32[]{:S(2)}) %collective-permute-start.30) | collective-permute-done | bytes 1048608 | tf_op jit(solution)/shard_map/ppermute | solution.py:527
  557.6 5.1 last_step.1
  (220 shorter events, 160.7 us)
Async XLA Ops:
  7.2 483.1 %reduce-scatter.3.cloned.1.call-start = ((), (), s32[]{:S(2)}) async-start(), calls=%async_computation.2 | async-start | bytes 18874368 | tf_op jit(solution)/shard_map/reduce_scatter | solution.py:625
  8.5 17.4 %collective-permute-start = (bf16[256,1024]{1,0:T(8,128)(2,1)S(1)}, bf16[256,1024]{1,0:T(8,128)(2,1)S(1)}, u32[]{:S(2)}, u32[]{:S(2)}) collective-permute-start(bf16[256,1024]{1,0:T(8,128)(2,1)S(1)} %get-tuple-element.237.xa_ref), channel_id=1, source_target_pairs={{0,3},{1,0},{2,1},{3,2},{4,7},{5,4},{6,5},{7,6},{8,11},{9,8},{10,9... | collective-permute-start | bytes 1572872 | tf_op jit(solution)/shard_map/ppermute | solution.py:527
  13.6 23.6 %collective-permute-start.2 = (bf16[256,1024]{1,0:T(8,128)(2,1)S(1)}, bf16[256,1024]{1,0:T(8,128)(2,1)}, u32[]{:S(2)}, u32[]{:S(2)}) collective-permute-start(bf16[256,1024]{1,0:T(8,128)(2,1)S(1)} %get-tuple-element.236.xb_ref), channel_id=1, source_target_pairs={{0,3},{1,0},{2,1},{3,2},{4,7},{5,4},{6,5},{7,6},{8,11},{9,8},{10,9... | collective-permute-start | bytes 1572872 | tf_op jit(solution)/shard_map/ppermute | solution.py:527
  26.0 22.8 %collective-permute-start.1 = (bf16[256,1024]{1,0:T(8,128)(2,1)S(1)}, bf16[256,1024]{1,0:T(8,128)(2,1)S(1)}, u32[]{:S(2)}, u32[]{:S(2)}) collective-permute-start(bf16[256,1024]{1,0:T(8,128)(2,1)S(1)} %collective-permute-done.xa_ref), channel_id=1, source_target_pairs={{0,3},{1,0},{2,1},{3,2},{4,7},{5,4},{6,5},{7,6},{8,11},{9,8},{10,9... | collective-permute-start | bytes 1572872 | tf_op jit(solution)/shard_map/ppermute | solution.py:527
  37.2 22.6 %collective-permute-start.4 = (bf16[256,1024]{1,0:T(8,128)(2,1)}, bf16[256,1024]{1,0:T(8,128)(2,1)}, u32[]{:S(2)}, u32[]{:S(2)}) collective-permute-start(bf16[256,1024]{1,0:T(8,128)(2,1)} %collective-permute-done.2.xb_ref), channel_id=1, source_target_pairs={{0,3},{1,0},{2,1},{3,2},{4,7},{5,4},{6,5},{7,6},{8,11},{9,8},{10,9... | collective-permute-start | bytes 1572872 | tf_op jit(solution)/shard_map/ppermute | solution.py:527
  48.7 23.3 %copy-start.7 = (bf16[1,256,2048]{2,1,0:T(8,128)(2,1)S(1)}, bf16[1,256,2048]{2,1,0:T(8,128)(2,1)}, u32[]{:S(2)}) copy-start(bf16[1,256,2048]{2,1,0:T(8,128)(2,1)} %param.18) | copy-start | bytes 3145732
  48.7 27.4 %copy-start.47 = (s32[1,1024]{1,0:T(1,128)S(1)}, s32[1,1024]{1,0:T(1,128)}, u32[]{:S(2)}) copy-start(s32[1,1024]{1,0:T(1,128)} %param.19) | copy-start | bytes 12292
  48.7 29.2 %copy-start.43 = (s32[1,1024]{1,0:T(1,128)S(1)}, s32[1,1024]{1,0:T(1,128)}, u32[]{:S(2)}) copy-start(s32[1,1024]{1,0:T(1,128)} %param.20) | copy-start | bytes 12292
  48.8 22.4 %collective-permute-start.3 = (bf16[256,1024]{1,0:T(8,128)(2,1)S(1)}, bf16[256,1024]{1,0:T(8,128)(2,1)S(1)}, u32[]{:S(2)}, u32[]{:S(2)}) collective-permute-start(bf16[256,1024]{1,0:T(8,128)(2,1)S(1)} %collective-permute-done.1.xa_ref), channel_id=1, source_target_pairs={{0,3},{1,0},{2,1},{3,2},{4,7},{5,4},{6,5},{7,6},{8,11},{9,8},{10,9... | collective-permute-start | bytes 1572872 | tf_op jit(solution)/shard_map/ppermute | solution.py:527
  59.8 22.6 %collective-permute-start.5 = (bf16[256,1024]{1,0:T(8,128)(2,1)}, bf16[256,1024]{1,0:T(8,128)(2,1)}, u32[]{:S(2)}, u32[]{:S(2)}) collective-permute-start(bf16[256,1024]{1,0:T(8,128)(2,1)} %collective-permute-done.4.xb_ref), channel_id=1, source_target_pairs={{0,3},{1,0},{2,1},{3,2},{4,7},{5,4},{6,5},{7,6},{8,11},{9,8},{10,9... | collective-permute-start | bytes 1572872 | tf_op jit(solution)/shard_map/ppermute | solution.py:527
  72.0 33.5 %collective-permute-start.6 = (bf16[256,2048]{1,0:T(8,128)(2,1)S(1)}, bf16[256,2048]{1,0:T(8,128)(2,1)S(1)}, u32[]{:S(2)}, u32[]{:S(2)}) collective-permute-start(bf16[256,2048]{1,0:T(8,128)(2,1)S(1)} %bitcast.81), channel_id=1, source_target_pairs={{0,1},{1,2},{2,3},{4,5},{5,6},{6,7},{8,9},{9,10},{10,11},{12,13},{... | collective-permute-start | bytes 3145736 | tf_op jit(solution)/shard_map/ppermute | solution.py:527
  74.1 39.0 %collective-permute-start.10 = (bf16[256,2048]{1,0:T(8,128)(2,1)S(1)}, bf16[256,2048]{1,0:T(8,128)(2,1)S(1)}, u32[]{:S(2)}, u32[]{:S(2)}) collective-permute-start(bf16[256,2048]{1,0:T(8,128)(2,1)S(1)} %bitcast.82), channel_id=1, source_target_pairs={{1,0},{2,1},{3,2},{5,4},{6,5},{7,6},{9,8},{10,9},{11,10},{13,12},{... | collective-permute-start | bytes 3145736 | tf_op jit(solution)/shard_map/ppermute | solution.py:527
  110.7 24.2 %collective-permute-start.7 = (bf16[256,2048]{1,0:T(8,128)(2,1)}, bf16[256,2048]{1,0:T(8,128)(2,1)S(1)}, u32[]{:S(2)}, u32[]{:S(2)}) collective-permute-start(bf16[256,2048]{1,0:T(8,128)(2,1)} %join.12), channel_id=1, source_target_pairs={{0,1},{1,2},{2,3},{4,5},{5,6},{6,7},{8,9},{9,10},{10,11},{12,13},{... | collective-permute-start | bytes 3145736 | tf_op jit(solution)/shard_map/ppermute | solution.py:527
  118.3 26.5 %collective-permute-start.11 = (bf16[256,2048]{1,0:T(8,128)(2,1)}, bf16[256,2048]{1,0:T(8,128)(2,1)S(1)}, u32[]{:S(2)}, u32[]{:S(2)}) collective-permute-start(bf16[256,2048]{1,0:T(8,128)(2,1)} %join.15), channel_id=1, source_target_pairs={{1,0},{2,1},{3,2},{5,4},{6,5},{7,6},{9,8},{10,9},{11,10},{13,12},{... | collective-permute-start | bytes 3145736 | tf_op jit(solution)/shard_map/ppermute | solution.py:527
  140.2 25.3 %collective-permute-start.8 = (bf16[256,2048]{1,0:T(8,128)(2,1)}, bf16[256,2048]{1,0:T(8,128)(2,1)S(1)}, u32[]{:S(2)}, u32[]{:S(2)}) collective-permute-start(bf16[256,2048]{1,0:T(8,128)(2,1)} %join.13), channel_id=1, source_target_pairs={{0,1},{1,2},{2,3},{4,5},{5,6},{6,7},{8,9},{9,10},{10,11},{12,13},{... | collective-permute-start | bytes 3145736 | tf_op jit(solution)/shard_map/ppermute | solution.py:527
  150.0 26.2 %collective-permute-start.12 = (bf16[256,2048]{1,0:T(8,128)(2,1)}, bf16[256,2048]{1,0:T(8,128)(2,1)S(1)}, u32[]{:S(2)}, u32[]{:S(2)}) collective-permute-start(bf16[256,2048]{1,0:T(8,128)(2,1)} %join.16), channel_id=1, source_target_pairs={{1,0},{2,1},{3,2},{5,4},{6,5},{7,6},{9,8},{10,9},{11,10},{13,12},{... | collective-permute-start | bytes 3145736 | tf_op jit(solution)/shard_map/ppermute | solution.py:527
  170.8 24.4 %collective-permute-start.9 = (bf16[256,2048]{1,0:T(8,128)(2,1)}, bf16[256,2048]{1,0:T(8,128)(2,1)}, u32[]{:S(2)}, u32[]{:S(2)}) collective-permute-start(bf16[256,2048]{1,0:T(8,128)(2,1)} %join.14), channel_id=1, source_target_pairs={{0,1},{1,2},{2,3},{4,5},{5,6},{6,7},{8,9},{9,10},{10,11},{12,13},{... | collective-permute-start | bytes 3145736 | tf_op jit(solution)/shard_map/ppermute | solution.py:527
  181.4 24.0 %collective-permute-start.13 = (bf16[256,2048]{1,0:T(8,128)(2,1)}, bf16[256,2048]{1,0:T(8,128)(2,1)S(1)}, u32[]{:S(2)}, u32[]{:S(2)}) collective-permute-start(bf16[256,2048]{1,0:T(8,128)(2,1)} %join.17), channel_id=1, source_target_pairs={{1,0},{2,1},{3,2},{5,4},{6,5},{7,6},{9,8},{10,9},{11,10},{13,12},{... | collective-permute-start | bytes 3145736 | tf_op jit(solution)/shard_map/ppermute | solution.py:527
  187.8 19.8 %copy-start.33 = (bf16[2048,1536]{1,0:T(8,128)(2,1)}, bf16[2048,1536]{1,0:T(8,128)(2,1)S(1)}, u32[]{:S(2)}) copy-start(bf16[2048,1536]{1,0:T(8,128)(2,1)S(1)} %constant_dynamic-update-slice_fusion) | copy-start | bytes 18874372
  187.8 20.2 %copy-start.40 = (f32[2048]{0:T(1024)S(1)}, f32[2048]{0:T(1024)}, u32[]{:S(2)}) copy-start(f32[2048]{0:T(1024)} %param.28) | copy-start | bytes 24580
  187.8 20.2 %copy-start.46 = (f32[2048]{0:T(1024)S(1)}, f32[2048]{0:T(1024)}, u32[]{:S(2)}) copy-start(f32[2048]{0:T(1024)} %param.29) | copy-start | bytes 24580
  207.6 143.6 %copy-start = (f32[256,2048]{1,0:T(8,128)}, f32[256,2048]{1,0:T(8,128)S(1)}, u32[]{:S(2)}) copy-start(f32[256,2048]{1,0:T(8,128)S(1)} %get-tuple-element.229) | copy-start | bytes 6291460
  208.5 23.6 %collective-permute-start.14 = (bf16[256,2048]{1,0:T(8,128)(2,1)S(1)}, bf16[256,2048]{1,0:T(8,128)(2,1)S(1)}, u32[]{:S(2)}, u32[]{:S(2)}) collective-permute-start(bf16[256,2048]{1,0:T(8,128)(2,1)S(1)} %add_convert_fusion.5.a_ref), channel_id=1, source_target_pairs={{0,3},{1,0},{2,1},{3,2},{4,7},{5,4},{6,5},{7,6},{8,11},{9,8},{10,9... | collective-permute-start | bytes 3145736 | tf_op jit(solution)/shard_map/ppermute | solution.py:527
  232.0 25.8 %collective-permute-start.15 = (bf16[256,2048]{1,0:T(8,128)(2,1)S(1)}, bf16[256,2048]{1,0:T(8,128)(2,1)S(1)}, u32[]{:S(2)}, u32[]{:S(2)}) collective-permute-start(bf16[256,2048]{1,0:T(8,128)(2,1)S(1)} %collective-permute-done.14.a_ref), channel_id=1, source_target_pairs={{0,3},{1,0},{2,1},{3,2},{4,7},{5,4},{6,5},{7,6},{8,11},{9,8},{10,9... | collective-permute-start | bytes 3145736 | tf_op jit(solution)/shard_map/ppermute | solution.py:527
  250.5 29.8 %collective-permute-start.17 = (bf16[256,2048]{1,0:T(8,128)(2,1)S(1)}, bf16[256,2048]{1,0:T(8,128)(2,1)S(1)}, u32[]{:S(2)}, u32[]{:S(2)}) collective-permute-start(bf16[256,2048]{1,0:T(8,128)(2,1)S(1)} %convolution_convert_fusion.4), channel_id=1, source_target_pairs={{0,3},{1,0},{2,1},{3,2},{4,7},{5,4},{6,5},{7,6},{8,11},{9,8},{10,9... | collective-permute-start | bytes 3145736 | tf_op jit(solution)/shard_map/ppermute | solution.py:527
  257.8 44.9 %collective-permute-start.16 = (bf16[256,2048]{1,0:T(8,128)(2,1)S(1)}, bf16[256,2048]{1,0:T(8,128)(2,1)S(1)}, u32[]{:S(2)}, u32[]{:S(2)}) collective-permute-start(bf16[256,2048]{1,0:T(8,128)(2,1)S(1)} %collective-permute-done.15.a_ref), channel_id=1, source_target_pairs={{0,3},{1,0},{2,1},{3,2},{4,7},{5,4},{6,5},{7,6},{8,11},{9,8},{10,9... | collective-permute-start | bytes 3145736 | tf_op jit(solution)/shard_map/ppermute | solution.py:527
  280.6 40.6 %collective-permute-start.18 = (bf16[256,2048]{1,0:T(8,128)(2,1)S(1)}, bf16[256,2048]{1,0:T(8,128)(2,1)S(1)}, u32[]{:S(2)}, u32[]{:S(2)}) collective-permute-start(bf16[256,2048]{1,0:T(8,128)(2,1)S(1)} %add_convert_fusion.4), channel_id=1, source_target_pairs={{0,3},{1,0},{2,1},{3,2},{4,7},{5,4},{6,5},{7,6},{8,11},{9,8},{10,9... | collective-permute-start | bytes 3145736 | tf_op jit(solution)/shard_map/ppermute | solution.py:527
  322.4 27.2 %collective-permute-start.19 = (bf16[256,2048]{1,0:T(8,128)(2,1)}, bf16[256,2048]{1,0:T(8,128)(2,1)S(1)}, u32[]{:S(2)}, u32[]{:S(2)}) collective-permute-start(bf16[256,2048]{1,0:T(8,128)(2,1)} %add_convert_fusion.3), channel_id=1, source_target_pairs={{0,3},{1,0},{2,1},{3,2},{4,7},{5,4},{6,5},{7,6},{8,11},{9,8},{10,9... | collective-permute-start | bytes 3145736 | tf_op jit(solution)/shard_map/ppermute | solution.py:527
  354.8 19.7 %collective-permute-start.20 = (bf16[256,2048]{1,0:T(8,128)(2,1)S(1)}, bf16[256,2048]{1,0:T(8,128)(2,1)S(1)}, u32[]{:S(2)}, u32[]{:S(2)}) collective-permute-start(bf16[256,2048]{1,0:T(8,128)(2,1)S(1)} %get-tuple-element.201.refs_0_), channel_id=1, source_target_pairs={{0,1},{1,2},{2,3},{4,5},{5,6},{6,7},{8,9},{9,10},{10,11},{12,13},{... | collective-permute-start | bytes 3145736 | tf_op jit(solution)/shard_map/ppermute | solution.py:527
  357.9 20.8 %collective-permute-start.21 = (bf16[256,2048]{1,0:T(8,128)(2,1)S(1)}, bf16[256,2048]{1,0:T(8,128)(2,1)S(1)}, u32[]{:S(2)}, u32[]{:S(2)}) collective-permute-start(bf16[256,2048]{1,0:T(8,128)(2,1)S(1)} %get-tuple-element.201.refs_0_), channel_id=1, source_target_pairs={{1,0},{2,1},{3,2},{5,4},{6,5},{7,6},{9,8},{10,9},{11,10},{13,12},{... | collective-permute-start | bytes 3145736 | tf_op jit(solution)/shard_map/ppermute | solution.py:527
  372.8 194.5 %reduce-scatter.5.cloned.1.call-start = ((), (), s32[]{:S(2)}) async-start(), calls=%async_computation.3 | async-start | bytes 9437184 | tf_op jit(solution)/shard_map/reduce_scatter | solution.py:651
  383.2 17.1 %collective-permute-start.22 = (bf16[256,2048]{1,0:T(8,128)(2,1)}, bf16[256,2048]{1,0:T(8,128)(2,1)S(1)}, u32[]{:S(2)}, u32[]{:S(2)}) collective-permute-start(bf16[256,2048]{1,0:T(8,128)(2,1)} %join.18), channel_id=1, source_target_pairs={{0,1},{1,2},{2,3},{4,5},{5,6},{6,7},{8,9},{9,10},{10,11},{12,13},{... | collective-permute-start | bytes 3145736 | tf_op jit(solution)/shard_map/ppermute | solution.py:527
  389.4 20.5 %collective-permute-start.25 = (bf16[256,2048]{1,0:T(8,128)(2,1)}, bf16[256,2048]{1,0:T(8,128)(2,1)S(1)}, u32[]{:S(2)}, u32[]{:S(2)}) collective-permute-start(bf16[256,2048]{1,0:T(8,128)(2,1)} %join.21), channel_id=1, source_target_pairs={{1,0},{2,1},{3,2},{5,4},{6,5},{7,6},{9,8},{10,9},{11,10},{13,12},{... | collective-permute-start | bytes 3145736 | tf_op jit(solution)/shard_map/ppermute | solution.py:527
  405.6 18.9 %collective-permute-start.23 = (bf16[256,2048]{1,0:T(8,128)(2,1)}, bf16[256,2048]{1,0:T(8,128)(2,1)S(1)}, u32[]{:S(2)}, u32[]{:S(2)}) collective-permute-start(bf16[256,2048]{1,0:T(8,128)(2,1)} %join.19), channel_id=1, source_target_pairs={{0,1},{1,2},{2,3},{4,5},{5,6},{6,7},{8,9},{9,10},{10,11},{12,13},{... | collective-permute-start | bytes 3145736 | tf_op jit(solution)/shard_map/ppermute | solution.py:527
  415.1 19.9 %collective-permute-start.26 = (bf16[256,2048]{1,0:T(8,128)(2,1)}, bf16[256,2048]{1,0:T(8,128)(2,1)S(1)}, u32[]{:S(2)}, u32[]{:S(2)}) collective-permute-start(bf16[256,2048]{1,0:T(8,128)(2,1)} %join.22), channel_id=1, source_target_pairs={{1,0},{2,1},{3,2},{5,4},{6,5},{7,6},{9,8},{10,9},{11,10},{13,12},{... | collective-permute-start | bytes 3145736 | tf_op jit(solution)/shard_map/ppermute | solution.py:527
  429.8 35.5 %collective-permute-start.24 = (bf16[256,2048]{1,0:T(8,128)(2,1)}, bf16[256,2048]{1,0:T(8,128)(2,1)}, u32[]{:S(2)}, u32[]{:S(2)}) collective-permute-start(bf16[256,2048]{1,0:T(8,128)(2,1)} %join.20), channel_id=1, source_target_pairs={{0,1},{1,2},{2,3},{4,5},{5,6},{6,7},{8,9},{9,10},{10,11},{12,13},{... | collective-permute-start | bytes 3145736 | tf_op jit(solution)/shard_map/ppermute | solution.py:527
  440.2 25.0 %collective-permute-start.27 = (bf16[256,2048]{1,0:T(8,128)(2,1)}, bf16[256,2048]{1,0:T(8,128)(2,1)}, u32[]{:S(2)}, u32[]{:S(2)}) collective-permute-start(bf16[256,2048]{1,0:T(8,128)(2,1)} %join.23), channel_id=1, source_target_pairs={{1,0},{2,1},{3,2},{5,4},{6,5},{7,6},{9,8},{10,9},{11,10},{13,12},{... | collective-permute-start | bytes 3145736 | tf_op jit(solution)/shard_map/ppermute | solution.py:527
  468.2 32.6 %collective-permute-start.28 = (bf16[256,2048]{1,0:T(8,128)(2,1)S(1)}, bf16[256,2048]{1,0:T(8,128)(2,1)S(1)}, u32[]{:S(2)}, u32[]{:S(2)}) collective-permute-start(bf16[256,2048]{1,0:T(8,128)(2,1)S(1)} %convolution_convert_fusion.3), channel_id=1, source_target_pairs={{0,3},{1,0},{2,1},{3,2},{4,7},{5,4},{6,5},{7,6},{8,11},{9,8},{10,9... | collective-permute-start | bytes 3145736 | tf_op jit(solution)/shard_map/ppermute | solution.py:527
  503.7 26.6 %collective-permute-start.29 = (bf16[256,2048]{1,0:T(8,128)(2,1)S(1)}, bf16[256,2048]{1,0:T(8,128)(2,1)}, u32[]{:S(2)}, u32[]{:S(2)}) collective-permute-start(bf16[256,2048]{1,0:T(8,128)(2,1)S(1)} %add_convert_fusion.1), channel_id=1, source_target_pairs={{0,3},{1,0},{2,1},{3,2},{4,7},{5,4},{6,5},{7,6},{8,11},{9,8},{10,9... | collective-permute-start | bytes 3145736 | tf_op jit(solution)/shard_map/ppermute | solution.py:527
  507.2 29.6 %copy-start.1 = (f32[256,2048]{1,0:T(8,128)S(1)}, f32[256,2048]{1,0:T(8,128)}, u32[]{:S(2)}) copy-start(f32[256,2048]{1,0:T(8,128)} %copy-done) | copy-start | bytes 6291460
  510.9 1.2 collective-permute-start.31
  512.1 30.4 %collective-permute-start.32 = (f32[8320]{0:T(1024)S(1)}, f32[8320]{0:T(1024)S(1)}, u32[]{:S(2)}, u32[]{:S(2)}) collective-permute-start(f32[8320]{0:T(1024)S(1)} %add.111), channel_id=1, source_target_pairs={{0,1},{1,2},{2,3},{3,0},{4,5},{5,6},{6,7},{7,4},{8,9},{9,10},{10,1... | collective-permute-start | bytes 99848 | tf_op jit(solution)/shard_map/ppermute | solution.py:527
  512.1 30.4 %collective-permute-start.33 = (f32[8320]{0:T(1024)S(1)}, f32[8320]{0:T(1024)S(1)}, u32[]{:S(2)}, u32[]{:S(2)}) collective-permute-start(f32[8320]{0:T(1024)S(1)} %add.111), channel_id=1, source_target_pairs={{0,2},{1,3},{2,0},{3,1},{4,6},{5,7},{6,4},{7,5},{8,10},{9,11},{10,... | collective-permute-start | bytes 99848 | tf_op jit(solution)/shard_map/ppermute | solution.py:527
  513.4 29.1 %collective-permute-start.34 = (f32[8320]{0:T(1024)S(1)}, f32[8320]{0:T(1024)S(1)}, u32[]{:S(2)}, u32[]{:S(2)}) collective-permute-start(f32[8320]{0:T(1024)S(1)} %add.111), channel_id=1, source_target_pairs={{0,3},{1,0},{2,1},{3,2},{4,7},{5,4},{6,5},{7,6},{8,11},{9,8},{10,9... | collective-permute-start | bytes 99848 | tf_op jit(solution)/shard_map/ppermute | solution.py:527
  532.5 24.1 %collective-permute-start.30 = (bf16[256,2048]{1,0:T(8,128)(2,1)S(1)}, bf16[256,2048]{1,0:T(8,128)(2,1)S(1)}, u32[]{:S(2)}, u32[]{:S(2)}) collective-permute-start(bf16[256,2048]{1,0:T(8,128)(2,1)S(1)} %add_convert_fusion), channel_id=1, source_target_pairs={{0,3},{1,0},{2,1},{3,2},{4,7},{5,4},{6,5},{7,6},{8,11},{9,8},{10,9... | collective-permute-start | bytes 3145736 | tf_op jit(solution)/shard_map/ppermute | solution.py:527
  542.6 20.2 %collective-permute-start.35 = (f32[8320]{0:T(1024)S(1)}, f32[8320]{0:T(1024)S(1)}, u32[]{:S(2)}, u32[]{:S(2)}) collective-permute-start(f32[8320]{0:T(1024)S(1)} %add_add_fusion.2), channel_id=1, source_target_pairs={{0,8},{4,12},{8,16},{12,20},{16,24},{20,28},{24,0},{28,4},{1,9},{5... | collective-permute-start | bytes 99848 | tf_op jit(solution)/shard_map/ppermute | solution.py:687
  544.0 18.8 %collective-permute-start.36 = (f32[8320]{0:T(1024)S(1)}, f32[8320]{0:T(1024)S(1)}, u32[]{:S(2)}, u32[]{:S(2)}) collective-permute-start(f32[8320]{0:T(1024)S(1)} %add_add_fusion.2), channel_id=1, source_target_pairs={{0,16},{4,20},{8,24},{12,28},{16,0},{20,4},{24,8},{28,12},{1,17},{... | collective-permute-start | bytes 99848 | tf_op jit(solution)/shard_map/ppermute | solution.py:687
  544.6 18.2 %collective-permute-start.37 = (f32[8320]{0:T(1024)S(1)}, f32[8320]{0:T(1024)S(1)}, u32[]{:S(2)}, u32[]{:S(2)}) collective-permute-start(f32[8320]{0:T(1024)S(1)} %add_add_fusion.2), channel_id=1, source_target_pairs={{0,24},{4,28},{8,0},{12,4},{16,8},{20,12},{24,16},{28,20},{1,25},{... | collective-permute-start | bytes 99848 | tf_op jit(solution)/shard_map/ppermute | solution.py:687
  (42 other events, 248.3 us)
Sparse Core Ops, SparseCore 0:
  372.9 117.3 reduce-scatter.2
  493.8 72.3 reduce-scatter.4

commit v4 on v3

--- a/solution.py
+++ b/solution.py
@@ -14,11 +14,10 @@
 LOG2E = 1.4426950408889634
 F32 = jnp.float32
 BF16 = jnp.bfloat16
-VMEM_LIMIT = 56 * 1024 * 1024
-
-
-def params(**kw):
-    return pltpu.CompilerParams(vmem_limit_bytes=VMEM_LIMIT, **kw)
+
+
+def params(mib):
+    return pltpu.CompilerParams(vmem_limit_bytes=mib << 20)
 
 
 def cost(flops, nbytes, trans=0):
@@ -115,7 +114,7 @@
         out_shape=[jax.ShapeDtypeStruct((n, rows, d), BF16)]
         + [jax.ShapeDtypeStruct((n, rows, local), BF16)] * 3,
         input_output_aliases=aliases,
-        compiler_params=params(),
+        compiler_params=params(28),
         cost_estimate=cost(6 * rows * d * local, 6 * d * local + 4 * rows * d),
         name="qkv_slot",
     )(rank, xa, xb, gain, shift, wq, wk, wv, cos, sin, *extra)
@@ -176,7 +175,7 @@
             out_specs=spec,
         ),
         out_shape=jax.ShapeDtypeStruct((n, rows, local), BF16),
-        compiler_params=params(),
+        compiler_params=params(16),
         cost_estimate=cost(4 * t * t * local, 8 * t * local, t * t * local // E),
         name="attend",
     )(rank, q, k, v, docs_col, docs_row, heads_col)
@@ -259,8 +258,8 @@
             scratch_shapes=[pltpu.VMEM((n, rows, E), F32), pltpu.VMEM((n, rows, E), F32)],
         ),
         out_shape=jax.ShapeDtypeStruct((n, rows, 3 * local), BF16),
-        compiler_params=params(),
-        cost_estimate=cost(230e9, 14 * t * local),
+        compiler_params=params(24),
+        cost_estimate=cost(108e9, 14 * t * local),
         name="attend_back",
     )(rank, q, k, v, do, docs_col, docs_row, heads_col, cos, sin)
 
@@ -321,7 +320,7 @@
         out_shape=[jax.ShapeDtypeStruct((n, rows, hidden), BF16)] * 2
         + [jax.ShapeDtypeStruct((n, rows, d), BF16)] * 2,
         input_output_aliases=aliases,
-        compiler_params=params(),
+        compiler_params=params(28),
         cost_estimate=cost(4 * rows * d * hidden, 4 * d * hidden + 4 * rows * (d + hidden)),
         name="mlp_slot",
     )(rank, act, *grads, up, down, bucket_col, *extra)
@@ -372,7 +371,7 @@
             jax.ShapeDtypeStruct((n, rows, d), BF16),
         ],
         input_output_aliases={at + i: i for i in range(len(extra))},
-        compiler_params=params(),
+        compiler_params=params(24),
         cost_estimate=cost(
             2 * len(slots) * rows * d * local, 2 * d * local + 6 * len(slots) * rows * d
         ),
@@ -380,58 +379,100 @@
     )(rank, jnp.asarray(slots, jnp.int32), *flows, weight, *extra)
 
 
-def grad_body(lhs_ref, rhs_ref, *rest):
-    rest[-1][0] = outer(lhs_ref[...], rhs_ref[...]).astype(BF16)
-
-
-def grad_part(which, lhs, rhs, held):
+def grad_body(has_sum, rank_ref, lhs_ref, rhs_ref, *rest):
+    out = outer(lhs_ref[...], rhs_ref[...])
+    if has_sum:
+        rest[-1][0] = (out + rest[0][...].astype(F32)).astype(BF16)
+    else:
+        rest[-1][...] = out.astype(BF16)
+
+
+def grad_half(lhs, rhs, rank, partner, which=0, moved=None, held=None):
     t, d = lhs.shape
-    width = rhs.shape[1]
+    half = rhs.shape[1] // 2
     tile = min(512, d)
-    extra = [] if held is None else [held]
-    return pl.pallas_call(
-        grad_body,
-        grid=(d // tile,),
-        in_specs=[
-            pl.BlockSpec((t, tile), lambda j: (0, j)),
-            pl.BlockSpec((t, width), lambda j: (0, 0)),
-        ]
-        + [pl.BlockSpec(memory_space=pl.ANY)] * len(extra),
-        out_specs=pl.BlockSpec((1, tile, width), lambda j: (which, j, 0)),
-        out_shape=jax.ShapeDtypeStruct((2, d, width), BF16),
-        input_output_aliases={2: 0} if extra else {},
-        compiler_params=params(),
-        cost_estimate=cost(2 * t * d * width, 2 * t * (d + width) + 2 * d * width),
-        name="grad_part",
-    )(lhs, rhs, *extra)
-
-
-def attn_grad_body(a_ref, s_ref, dqkv_ref, om_ref, out_ref):
-    wide = dqkv_ref.shape[1]
-    out_ref[:, :wide] = outer(a_ref[...], dqkv_ref[...]).astype(BF16)
-    out_ref[:, wide:] = outer(s_ref[...], om_ref[...]).astype(BF16)
-
-
-def attn_grads(act, states, dqkv, om):
+    col = (lambda r: 1 - r[3]) if partner else (lambda r: r[3])
+    specs = [
+        pl.BlockSpec((t, tile), lambda j, r: (0, j)),
+        pl.BlockSpec((t, half), lambda j, r: (0, col(r))),
+    ]
+    args = [lhs, rhs]
+    aliases = {}
+    if partner:
+        ospec = pl.BlockSpec((tile, half), lambda j, r: (j, 0))
+        oshape = (d, half)
+    else:
+        specs.append(pl.BlockSpec((tile, half), lambda j, r: (j, 0)))
+        args.append(moved)
+        ospec = pl.BlockSpec((1, tile, half), lambda j, r: (which, j, 0))
+        oshape = (2, d, half)
+        if held is not None:
+            specs.append(pl.BlockSpec(memory_space=pl.ANY))
+            args.append(held)
+            aliases = {4: 0}
+    return pl.pallas_call(
+        functools.partial(grad_body, not partner),
+        grid_spec=pltpu.PrefetchScalarGridSpec(
+            num_scalar_prefetch=1, grid=(d // tile,), in_specs=specs, out_specs=ospec
+        ),
+        out_shape=jax.ShapeDtypeStruct(oshape, BF16),
+        input_output_aliases=aliases,
+        compiler_params=params(28),
+        cost_estimate=cost(1e6, 1e6),
+        name="grad_half",
+    )(rank, *args)
+
+
+def attn_grad_body(partner, rank_ref, a_ref, s_ref, one_ref, key_ref, om_ref, *rest):
+    out_ref = rest[-1]
+    local = om_ref.shape[1]
+    second = rank_ref[3] == (0 if partner else 1)
+    act = a_ref[...]
+
+    def put(cols, value):
+        if not partner:
+            value = value + rest[0][:, cols].astype(F32)
+        out_ref[:, cols] = value.astype(BF16)
+
+    put(slice(0, local), outer(act, one_ref[...]))
+
+    @pl.when(second)
+    def _():
+        put(slice(local, 2 * local), outer(s_ref[...], om_ref[...]))
+
+    @pl.when(jnp.logical_not(second))
+    def _():
+        put(slice(local, 2 * local), outer(act, key_ref[...]))
+
+
+def attn_grads(act, states, dqkv, om, rank, moved=None):
     t, d = act.shape
     local = om.shape[1]
     tile = min(512, d)
-    col = pl.BlockSpec((t, tile), lambda j: (0, j))
-    return pl.pallas_call(
-        attn_grad_body,
-        grid=(d // tile,),
-        in_specs=[
-            col,
-            col,
-            pl.BlockSpec((t, 3 * local), lambda j: (0, 0)),
-            pl.BlockSpec((t, local), lambda j: (0, 0)),
-        ],
-        out_specs=pl.BlockSpec((tile, 4 * local), lambda j: (j, 0)),
-        out_shape=jax.ShapeDtypeStruct((d, 4 * local), BF16),
-        compiler_params=params(),
-        cost_estimate=cost(8 * t * d * local, 2 * t * (2 * d + 4 * local) + 8 * d * local),
+    partner = moved is None
+    pos = (lambda r: 1 - r[3]) if partner else (lambda r: r[3])
+    col = pl.BlockSpec((t, tile), lambda j, r: (0, j))
+    out = pl.BlockSpec((tile, 2 * local), lambda j, r: (j, 0))
+    return pl.pallas_call(
+        functools.partial(attn_grad_body, partner),
+        grid_spec=pltpu.PrefetchScalarGridSpec(
+            num_scalar_prefetch=1,
+            grid=(d // tile,),
+            in_specs=[
+                col,
+                col,
+                pl.BlockSpec((t, local), lambda j, r: (0, 2 * pos(r))),
+                pl.BlockSpec((t, local), lambda j, r: (0, 1)),
+                pl.BlockSpec((t, local), lambda j, r: (0, 0)),
+            ]
+            + ([] if partner else [out]),
+            out_specs=out,
+        ),
+        out_shape=jax.ShapeDtypeStruct((d, 2 * local), BF16),
+        compiler_params=params(28),
+        cost_estimate=cost(4 * t * d * local, 2 * t * (2 * d + 3 * local) + 8 * d * local),
         name="attn_grads",
-    )(act, states, dqkv, om)
+    )(rank, act, states, dqkv, dqkv, om, *([] if partner else [moved]))
 
 
 def join_body(slot, first, rank_ref, moved_ref, term_ref, out_ref):
@@ -448,7 +489,7 @@
 
 def join(rank, moved, terms, slot, first, right):
     rows, d = moved.shape
-    tile = min(64, rows)
+    tile = min(128, rows)
     row = pl.BlockSpec((tile, d), lambda i, r: (i, 0))
     return pl.pallas_call(
         functools.partial(join_body, 0 if right else -1, first),
@@ -459,7 +500,7 @@
             out_specs=row,
         ),
         out_shape=jax.ShapeDtypeStruct((rows, d), BF16),
-        compiler_params=params(),
+        compiler_params=params(8),
         cost_estimate=cost(rows * d, 6 * rows * d),
         name="join",
     )(rank, moved, terms)
@@ -482,8 +523,8 @@
         in_specs=[row(d), pl.BlockSpec((1, d), lambda i: (0, 0)), row(d), row(d), row(d)],
         out_specs=row(d),
         out_shape=jax.ShapeDtypeStruct((rows, d), BF16),
-        compiler_params=params(),
-        cost_estimate=cost(73e9, 12 * rows * d),
+        compiler_params=params(12),
+        cost_estimate=cost(15e9, 12 * rows * d),
         name="last_step",
     )(x, gain, term, moved, state)
 
@@ -543,7 +584,10 @@
     flat = lambda v: v.reshape(length, v.shape[-1])
     add = lambda t, moved: (t.astype(F32) + moved.astype(F32)).astype(BF16)
 
-    where = jnp.stack([rank, rank * local_heads, rank * hidden]).astype(jnp.int32)
+    side = lax.rem(lax.axis_index("dp"), 2)
+    where = jnp.stack([rank, rank * local_heads, rank * hidden, side]).astype(jnp.int32)
+    swap = lambda v: lax.ppermute(v, "dp", [(i, i ^ 1) for i in range(n_dp)])
+    sides = [list(range(c, n_dp, 2)) for c in range(2)]
     docs_col = doc_ids.reshape(n, rows, 1)
     docs_row = doc_ids.reshape(n, 1, rows)
     heads_col = head_count.reshape(n, rows, 1)
@@ -605,11 +649,13 @@
             term0 = dot_t(held[1][0], up_weight)
         block = after
     active, grad_upper, second_all, grad_all = held
-    grad_all, active = tie([grad_all, active], sent)
-    pair = grad_part(0, flat(grad_all), flat(active), None)
-    (active,) = tie([active], pair)
-    ffn = low(dot_t(flat(active), down_weight)).reshape(n, rows, d)
-    (moved,) = tie([moved], ffn)
+    grad_all, active, second_all, grad_upper = tie([grad_all, active, second_all, grad_upper], sent)
+    gifts = [
+        grad_half(flat(grad_all), flat(active), where, True),
+        grad_half(flat(second_all), flat(grad_upper), where, True),
+    ]
+    (moved,) = tie([moved], *gifts)
+    down_gift, up_gift = (swap(v) for v in gifts)
     grad_second = term0 + moved.astype(F32)
     back_two = norm_backward(grad_second, normed_two, inverse_two, gain2)
     second_gain_part = jnp.sum(grad_second * normed_two, axis=0)
@@ -617,12 +663,14 @@
     grad_state = grad_own.astype(F32) + back_two
 
     start = low(grad_state)
-    second_all, grad_upper, start = tie([second_all, grad_upper, start])
+    grad_all, active, second_all, grad_upper, start = tie([grad_all, active, second_all, grad_upper, start])
     right = left = start
     rights, lefts = [start], [start]
     right, left = tick(0, right, left, None)
-    pair = grad_part(1, flat(second_all), flat(grad_upper), pair)
-    wide_grad = lax.psum_scatter(pair, "dp", scatter_dimension=1, tiled=True)
+    ffn = low(dot_t(flat(active), down_weight)).reshape(n, rows, d)
+    pair = grad_half(flat(grad_all), flat(active), where, False, 0, down_gift)
+    pair = grad_half(flat(second_all), flat(grad_upper), where, False, 1, up_gift, pair)
+    wide_grad = lax.psum_scatter(pair, "dp", scatter_dimension=1, axis_index_groups=sides, tiled=True)
     right, left = tie([right, left], pair)
     for k in range(1, n):
         rights.append(right)
@@ -639,17 +687,22 @@
     mixed = low(state + owned(ffn, right, left))
 
     (dqkv,) = tie([dqkv], right, left)
+    tokens_of = lambda v: (flat(first_all), flat(state_all), flat(v), flat(masked), where)
+    gift = attn_grads(*tokens_of(dqkv))
+    (dqkv,) = tie([dqkv], gift)
+    gift = swap(gift)
     sent = low(dot_t(dqkv[1], weights))
     (dqkv,) = tie([dqkv], sent)
     moved = hop(sent)
-    attn_term = attn_grads(flat(first_all), flat(state_all), flat(dqkv), flat(masked))
+    attn_term = attn_grads(*tokens_of(dqkv), gift)
+    (late,) = tie([attn_term], wide_grad)
+    attn_grad = lax.psum_scatter(late, "dp", scatter_dimension=0, axis_index_groups=sides, tiled=True)
     (dqkv,) = tie([dqkv], attn_term)
-    terms = low(dot_t(flat(dqkv), weights)).reshape(n, rows, d)
-    sum_d = jnp.sum(terms.astype(F32), axis=(0, 1))
-    sum_da = jnp.sum(terms.astype(F32) * first_all.astype(F32), axis=(0, 1))
-    (late,) = tie([attn_term], wide_grad)
-    attn_grad = lax.psum_scatter(late, "dp", scatter_dimension=0, tiled=True)
-    (moved,) = tie([moved], terms)
+    terms = {s: low(dot_t(dqkv[s], weights)) for s in range(1, n)}
+    (dqkv,) = tie([dqkv], terms[n - 1])
+    terms[0] = low(dot_t(dqkv[0], weights))
+    sum_d = sum(jnp.sum(terms[s].astype(F32), axis=0) for s in range(n))
+    sum_da = sum(jnp.sum(terms[s].astype(F32) * first_all[s].astype(F32), axis=0) for s in range(n))
     first_shift_part = sum_d
     first_gain_part = (sum_da - first_shift * sum_d) / first_gain
 
@@ -689,20 +742,28 @@
     ]
     input_grad = last_step(own, gain1, terms[0], moved, grad_state)
     small = small + sum(tie(others, input_grad))
-    wide_grad, attn_grad = wide_grad.astype(F32), attn_grad.astype(F32)
+
+    def whole(part):
+        span = part.shape[-2] // 2
+        mine = lax.dynamic_slice_in_dim(part, side * span, span, part.ndim - 2)
+        got = swap(lax.dynamic_slice_in_dim(part, (1 - side) * span, span, part.ndim - 2))
+        return jnp.where(side == 0, mine, got).astype(F32), jnp.where(side == 0, got, mine).astype(F32)
+
+    wide = jnp.concatenate(whole(wide_grad), axis=2)
+    query_key, value_out = whole(attn_grad)
     return (
         mixed[None],
         input_grad[None],
         small[:d],
         small[d : 2 * d],
-        attn_grad[:, :local],
-        attn_grad[:, local : 2 * local],
-        attn_grad[:, 2 * local : 3 * local],
-        attn_grad[:, 3 * local :],
+        query_key[:, :local],
+        query_key[:, local:],
+        value_out[:, :local],
+        value_out[:, local:],
         small[2 * d : 3 * d],
         small[3 * d : 4 * d],
-        wide_grad[1],
-        wide_grad[0],
+        wide[1],
+        wide[0],
         small[4 * d : 4 * d + 4].astype(jnp.int32),
         small[4 * d + 4 : 4 * d + 4 + HEADS].astype(jnp.int32),
     )

time: 587 us -> 580 us (0.988)
  Pallas kernels: 212 us -> 149 us
  waiting for transfers between devices: 145 us -> 167 us
  local copies, waits for them, and re-layouts: 32.6 us -> 49.3 us
  starting transfers between devices: 86.9 us -> 102 us
    pallas_call x12, Pallas kernels: 51.4 us -> 17.8 us  [join(): pl.pallas_call(functools.partial(join_body, 0 if right else -1, first), g...]
    ppermute x34, waiting for transfers between devices: 140 us -> 161 us  [per_device(): send = lambda v, pairs: lax.ppermute(v, 'mp', pairs)]
    unnamed x103 -> x177, local copies, waits for them, and re-layouts: 19.9 us -> 35.5 us
    ppermute x34, starting transfers between devices: 82.5 us -> 96.5 us  [per_device(): send = lambda v, pairs: lax.ppermute(v, 'mp', pairs)]
    pallas_call x4, Pallas kernels: 28.6 us -> 16.7 us  [qkv_slot(): pl.pallas_call(qkv_body, grid_spec=pltpu.PrefetchScalarGridSpec(num_scala...]
    pallas_call x4, Pallas kernels: 46.4 us -> 39.7 us  [mlp_slot(): pl.pallas_call(functools.partial(mlp_body, slot, n), grid_spec=pltpu.Pref...]
    dot_general x8 -> x11, matrix products: 57.4 us -> 62.9 us  [dot_t(): lax.dot_general(left, right, (((1,), (1,)), ((), ())), preferred_element_...]
    pallas_call x3 -> x6, Pallas kernels: 40.9 us -> 42.5 us  [the longest x4 27.9 us: grad_half(): pl.pallas_call(functools.partial(grad_body, not partner), grid_spec=pltpu...]
  transfers between devices with their start and end apart: 40 -> 45, of which waited for: 21 -> 26; matrix products, arithmetic and copies ran while one was open for 15% -> 16% of each run, Pallas kernels for 37% -> 26%
where the time goes in v4:
time: 580 us; the launch traced here: 572 us
  waiting for transfers between devices  167 us (29%)
  Pallas kernels  149 us (26%)
  starting transfers between devices  102 us (18%)
  matrix products  62.9 us (11%)
  local copies, waits for them, and re-layouts  49.3 us (8%)
  other arithmetic  25.9 us (4%)
  between operations  15.9 us (3%)
    ppermute x34, waiting for transfers between devices, per_device(): send = lambda v, pairs: lax.ppermute(v, 'mp', pairs)  161 us
    ppermute x34, starting transfers between devices, per_device(): send = lambda v, pairs: lax.ppermute(v, 'mp', pairs)  96.5 us
    dot_general x11, matrix products, dot_t(): lax.dot_general(left, right, (((1,), (1,)), ((), ())), preferred_element_...  62.9 us
    pallas_call x4, Pallas kernels, mlp_slot(): pl.pallas_call(functools.partial(mlp_body, slot, n), grid_spec=pltpu.Pref...  39.7 us
    unnamed x177, local copies, waits for them, and re-layouts  35.5 us
    pallas_call x4, Pallas kernels, grad_half(): pl.pallas_call(functools.partial(grad_body, not partner), grid_spec=pltpu...  27.9 us
    pallas_call x12, Pallas kernels, join(): pl.pallas_call(functools.partial(join_body, 0 if right else -1, first), g...  17.8 us
    pallas_call x4, Pallas kernels, qkv_slot(): pl.pallas_call(qkv_body, grid_spec=pltpu.PrefetchScalarGridSpec(num_scala...  16.7 us
  transfers between devices with their start and end apart: 45, of which 26 were waited for; matrix products, arithmetic and copies ran while one was open for 16% of the time, Pallas kernels for 26%

profile of v4, /device:TPU:0, one launch (start us, length us, event | category | flops | bytes accessed | tf_op | source)
XLA Modules:
  0.0 571.7 jit_solution(3295228716832754100)
XLA Ops:
  9.5 5.0 collective-permute-start
  22.2 4.2 qkv_slot.4
  27.2 4.3 collective-permute-start.1
  31.4 7.0 %collective-permute-done.2.xb_ref = bf16[256,1024]{1,0:T(8,128)(2,1)} collective-permute-done((bf16[256,1024]{1,0:T(8,128)(2,1)}, bf16[256,1024]{1,0:T(8,128)(2,1)}, u32[]{:S(2)}, u32[]{:S(2)}) %collective-permute-start.2) | collective-permute-done | bytes 524320 | tf_op jit(solution)/shard_map/ppermute | solution.py:568
  38.4 4.3 collective-permute-start.4
  42.7 4.3 qkv_slot.5
  49.6 4.2 collective-permute-start.3
  53.8 7.1 %collective-permute-done.4.xb_ref = bf16[256,1024]{1,0:T(8,128)(2,1)} collective-permute-done((bf16[256,1024]{1,0:T(8,128)(2,1)}, bf16[256,1024]{1,0:T(8,128)(2,1)}, u32[]{:S(2)}, u32[]{:S(2)}) %collective-permute-start.4) | collective-permute-done | bytes 524320 | tf_op jit(solution)/shard_map/ppermute | solution.py:568
  60.9 4.3 collective-permute-start.5
  65.1 4.1 qkv_slot.6
  93.5 4.1 qkv_slot.7
  97.7 8.5 %attend.1 = bf16[4,256,512]{2,1,0:T(8,128)(2,1)S(1)} custom-call(s32[4]{0:T(128)S(1)} %pad_add_fusion.rank_ref, bf16[4,256,512]{2,1,0:T(8,128)(2,1)S(1)} %get-tuple-element.164.q_ref, bf16[4,256,512]{2,1,0:T(8,128)(2,1)S(1)} %get-tuple-element.165.k_ref, bf16[4,256,512]{2,1,0:T(8,128)(2,1)S(1)} %get-tuple-element.166.v_ref, s32[4,256,1]{2,1,0:T(8,128)S(1)} %copy-done.55, ...), custom_call_target="tpu_custom_call" | custom-call | flops 2147483648 | bytes 4194304 | tf_op jit(solution)/shard_map/attend/pallas_call | solution.py:169
  118.5 16.6 %collective-permute-done.7.moved_ref.gr_ref = bf16[256,2048]{1,0:T(8,128)(2,1)S(1)} collective-permute-done((bf16[256,2048]{1,0:T(8,128)(2,1)S(1)}, bf16[256,2048]{1,0:T(8,128)(2,1)S(1)}, u32[]{:S(2)}, u32[]{:S(2)}) %collective-permute-start.7) | collective-permute-done | bytes 1048608 | tf_op jit(solution)/shard_map/ppermute | solution.py:568
  136.1 4.4 collective-permute-start.8
  143.5 15.9 %collective-permute-done.8.moved_ref.gr_ref = bf16[256,2048]{1,0:T(8,128)(2,1)S(1)} collective-permute-done((bf16[256,2048]{1,0:T(8,128)(2,1)S(1)}, bf16[256,2048]{1,0:T(8,128)(2,1)S(1)}, u32[]{:S(2)}, u32[]{:S(2)}) %collective-permute-start.8) | collective-permute-done | bytes 1048608 | tf_op jit(solution)/shard_map/ppermute | solution.py:568
  161.1 5.5 collective-permute-start.9
  173.8 10.0 %collective-permute-done.9 = bf16[256,2048]{1,0:T(8,128)(2,1)} collective-permute-done((bf16[256,2048]{1,0:T(8,128)(2,1)}, bf16[256,2048]{1,0:T(8,128)(2,1)}, u32[]{:S(2)}, u32[]{:S(2)}) %collective-permute-start.9) | collective-permute-done | bytes 1048608 | tf_op jit(solution)/shard_map/ppermute | solution.py:568
  183.9 6.7 %collective-permute-done.13 = bf16[256,2048]{1,0:T(8,128)(2,1)} collective-permute-done((bf16[256,2048]{1,0:T(8,128)(2,1)}, bf16[256,2048]{1,0:T(8,128)(2,1)}, u32[]{:S(2)}, u32[]{:S(2)}) %collective-permute-start.13) | collective-permute-done | bytes 1048608 | tf_op jit(solution)/shard_map/ppermute | solution.py:568
  196.2 11.2 %mlp_slot.4 = (bf16[4,256,2048]{2,1,0:T(8,128)(2,1)S(1)}, bf16[4,256,2048]{2,1,0:T(8,128)(2,1)S(1)}, bf16[4,256,2048]{2,1,0:T(8,128)(2,1)S(1)}, bf16[4,256,2048]{2,1,0:T(8,128)(2,1)S(1)}) custom-call(s32[4]{0:T(128)S(1)} %pad_add_fusion.rank_ref, bf16[256,2048]{1,0:T(8,128)(2,1)S(1)} %add_convert_fusion.3.a_ref, bf16[256,2048]{1,0:T(8,128)(2,1)} %bitcast.9.gl_ref.gr_ref, ...), custom_call_target="tpu_custom_call" | custom-call | flops 4294967296 | bytes 20971520 | tf_op jit(solution)/shard_map/mlp_slot/pallas_call | solution.py:303
  207.4 7.2 %fusion.12 = f32[256,2048]{1,0:T(8,128)} fusion(bf16[2048,2048]{1,0:T(8,128)(2,1)} %up_ref.7, bf16[4,256,2048]{2,1,0:T(8,128)(2,1)S(1)} %get-tuple-element.175.rest_1_), kind=kOutput, calls=%fused_computation.45 | convolution fusion | flops 2147483648 | bytes 11534336 | tf_op jit(solution)/shard_map/dot_general | solution.py:53
  219.2 9.6 %mlp_slot.5 = (bf16[4,256,2048]{2,1,0:T(8,128)(2,1)S(1)}, bf16[4,256,2048]{2,1,0:T(8,128)(2,1)S(1)}, bf16[4,256,2048]{2,1,0:T(8,128)(2,1)S(1)}, bf16[4,256,2048]{2,1,0:T(8,128)(2,1)S(1)}) custom-call(s32[4]{0:T(128)S(1)} %pad_add_fusion.rank_ref, ...), custom_call_target="tpu_custom_call", output_to_operand_aliasing={{0}: (7, {}), {1}: (8, {}), {2}: (9, {}), {3}: (10, {})} | custom-call | flops 4294967296 | bytes 20971520 | tf_op jit(solution)/shard_map/mlp_slot/pallas_call | solution.py:303
  230.9 6.9 %convolution_convert_fusion.7 = bf16[256,2048]{1,0:T(8,128)(2,1)} fusion(bf16[2048,2048]{1,0:T(8,128)(2,1)} %up_ref.7, bf16[4,256,2048]{2,1,0:T(8,128)(2,1)S(1)} %get-tuple-element.184.rest_1_), kind=kOutput, calls=%fused_computation.17 | convolution fusion | flops 2148007936 | bytes 10485760 | tf_op jit(solution)/shard_map/dot_general | solution.py:53
  245.1 9.3 %mlp_slot.6 = (bf16[4,256,2048]{2,1,0:T(8,128)(2,1)S(1)}, bf16[4,256,2048]{2,1,0:T(8,128)(2,1)S(1)}, bf16[4,256,2048]{2,1,0:T(8,128)(2,1)S(1)}, bf16[4,256,2048]{2,1,0:T(8,128)(2,1)S(1)}) custom-call(s32[4]{0:T(128)S(1)} %pad_add_fusion.rank_ref, ...), custom_call_target="tpu_custom_call", output_to_operand_aliasing={{0}: (7, {}), {1}: (8, {}), {2}: (9, {}), {3}: (10, {})} | custom-call | flops 4294967296 | bytes 20971520 | tf_op jit(solution)/shard_map/mlp_slot/pallas_call | solution.py:303
  254.4 5.7 %fusion.8 = f32[256,2048]{1,0:T(8,128)S(1)} fusion(bf16[2048,2048]{1,0:T(8,128)(2,1)} %up_ref.7, bf16[4,256,2048]{2,1,0:T(8,128)(2,1)S(1)} %get-tuple-element.193.rest_1_), kind=kOutput, calls=%fused_computation.41 | convolution fusion | flops 2147483648 | bytes 11534336 | tf_op jit(solution)/shard_map/dot_general | solution.py:53
  264.4 4.4 collective-permute-start.18
  268.8 17.7 %collective-permute-done.16.a_ref = bf16[256,2048]{1,0:T(8,128)(2,1)S(1)} collective-permute-done((bf16[256,2048]{1,0:T(8,128)(2,1)S(1)}, bf16[256,2048]{1,0:T(8,128)(2,1)S(1)}, u32[]{:S(2)}, u32[]{:S(2)}) %collective-permute-start.16) | collective-permute-done | bytes 1048608 | tf_op jit(solution)/shard_map/ppermute | solution.py:568
  286.5 9.6 %mlp_slot.7 = (bf16[4,256,2048]{2,1,0:T(8,128)(2,1)S(1)}, bf16[4,256,2048]{2,1,0:T(8,128)(2,1)S(1)}, bf16[4,256,2048]{2,1,0:T(8,128)(2,1)S(1)}, bf16[4,256,2048]{2,1,0:T(8,128)(2,1)S(1)}) custom-call(s32[4]{0:T(128)S(1)} %pad_add_fusion.rank_ref, ...), custom_call_target="tpu_custom_call", output_to_operand_aliasing={{0}: (7, {}), {1}: (8, {}), {2}: (9, {}), {3}: (10, {})} | custom-call | flops 4294967296 | bytes 20971520 | tf_op jit(solution)/shard_map/mlp_slot/pallas_call | solution.py:303
  296.1 7.3 %fusion.10 = f32[256,2048]{1,0:T(8,128)S(1)} fusion(bf16[2048,2048]{1,0:T(8,128)(2,1)} %up_ref.7, bf16[4,256,2048]{2,1,0:T(8,128)(2,1)S(1)} %get-tuple-element.209), kind=kOutput, calls=%fused_computation.43 | convolution fusion | flops 2147483648 | bytes 11534336 | tf_op jit(solution)/shard_map/dot_general | solution.py:53
  309.1 6.2 %grad_half.4 = bf16[2048,1024]{1,0:T(8,128)(2,1)S(1)} custom-call(s32[4]{0:T(128)S(1)} %pad_add_fusion.rank_ref, bf16[1024,2048]{1,0:T(8,128)(2,1)S(1)} %bitcast.110, bf16[1024,2048]{1,0:T(8,128)(2,1)S(1)} %bitcast.103), custom_call_target="tpu_custom_call" | custom-call | flops 1000000 | bytes 1000000 | tf_op jit(solution)/shard_map/grad_half/pallas_call | solution.py:413
  315.4 7.2 %grad_half.5 = bf16[2048,1024]{1,0:T(8,128)(2,1)} custom-call(s32[4]{0:T(128)S(1)} %pad_add_fusion.rank_ref, bf16[1024,2048]{1,0:T(8,128)(2,1)S(1)} %bitcast.108, bf16[1024,2048]{1,0:T(8,128)(2,1)S(1)} %bitcast.106), custom_call_target="tpu_custom_call" | custom-call | flops 1000000 | bytes 1000000 | tf_op jit(solution)/shard_map/grad_half/pallas_call | solution.py:413
  336.9 12.8 %convolution_convert_fusion = bf16[1024,2048]{1,0:T(8,128)(2,1)} fusion(bf16[1024,2048]{1,0:T(8,128)(2,1)S(1)} %bitcast.104, bf16[2048,2048]{1,0:T(8,128)(2,1)} %down_ref.7), kind=kOutput, calls=%fused_computation | convolution fusion | flops 8592031744 | bytes 16777216 | tf_op jit(solution)/shard_map/dot_general | solution.py:53
  349.6 7.2 %grad_half.6.rest_1_ = bf16[2,2048,1024]{2,1,0:T(8,128)(2,1)S(1)} custom-call(s32[4]{0:T(128)S(1)} %pad_add_fusion.rank_ref, bf16[1024,2048]{1,0:T(8,128)(2,1)S(1)} %bitcast.111, bf16[1024,2048]{1,0:T(8,128)(2,1)S(1)} %bitcast.105, bf16[2048,1024]{1,0:T(8,128)(2,1)} %collective-permute-done.23.rest_0_), custom_call_target="tpu_custom_call" | custom-call | flops 1000000 | bytes 1000000 | tf_op jit(solution)/shard_map/grad_half/pallas_call | solution.py:413
  356.9 7.2 %grad_half.7 = bf16[2,2048,1024]{2,1,0:T(8,128)(2,1)S(1)} custom-call(s32[4]{0:T(128)S(1)} %pad_add_fusion.rank_ref, bf16[1024,2048]{1,0:T(8,128)(2,1)S(1)} %bitcast.109, bf16[1024,2048]{1,0:T(8,128)(2,1)S(1)} %bitcast.107, bf16[2048,1024]{1,0:T(8,128)(2,1)} %collective-permute-done.22.rest_0_, ...), custom_call_target="tpu_custom_call", output_to_operand_aliasing={{}: (4, {})} | custom-call | flops 1000000 | bytes 1000000 | tf_op jit(solution)/shard_map/grad_half/pallas_call | solution.py:413
  371.3 5.5 collective-permute-start.24
  379.7 15.7 %collective-permute-done.24.moved_ref.refs_2_ = bf16[256,2048]{1,0:T(8,128)(2,1)} collective-permute-done((bf16[256,2048]{1,0:T(8,128)(2,1)}, bf16[256,2048]{1,0:T(8,128)(2,1)}, u32[]{:S(2)}, u32[]{:S(2)}) %collective-permute-start.24) | collective-permute-done | bytes 1048608 | tf_op jit(solution)/shard_map/ppermute | solution.py:568
  399.5 4.9 collective-permute-start.25
  407.7 4.2 dom_part.2
  412.0 10.6 %collective-permute-done.25.moved_ref.refs_1_ = bf16[256,2048]{1,0:T(8,128)(2,1)S(1)} collective-permute-done((bf16[256,2048]{1,0:T(8,128)(2,1)S(1)}, bf16[256,2048]{1,0:T(8,128)(2,1)S(1)}, u32[]{:S(2)}, u32[]{:S(2)}) %collective-permute-start.25) | collective-permute-done | bytes 1048608 | tf_op jit(solution)/shard_map/ppermute | solution.py:568
  423.4 4.5 collective-permute-start.26
  433.7 14.5 %attend_back.1 = bf16[4,256,1536]{2,1,0:T(8,128)(2,1)S(1)} custom-call(s32[4]{0:T(128)S(1)} %pad_add_fusion.rank_ref, bf16[4,256,512]{2,1,0:T(8,128)(2,1)S(1)} %copy-done.29, bf16[4,256,512]{2,1,0:T(8,128)(2,1)S(1)} %copy-done.33, bf16[4,256,512]{2,1,0:T(8,128)(2,1)S(1)} %copy-done.37, bf16[4,256,512]{2,1,0:T(8,128)(2,1)S(1)} %get-tuple-element.215.do_ref, ...), custom_call_target="tpu_custom_call" | custom-call | flops 108000002048 | bytes 7340032 | tf_op jit(solution)/shard_map/attend_back/pallas_call | solution.py:251
  452.0 7.4 %attn_grads.2 = bf16[2048,1024]{1,0:T(8,128)(2,1)S(1)} custom-call(s32[4]{0:T(128)S(1)} %pad_add_fusion.rank_ref, bf16[1024,2048]{1,0:T(8,128)(2,1)S(1)} %bitcast.112, bf16[1024,2048]{1,0:T(8,128)(2,1)S(1)} %bitcast.118, bf16[1024,1536]{1,0:T(8,128)(2,1)S(1)} %bitcast.114, bf16[1024,1536]{1,0:T(8,128)(2,1)S(1)} %bitcast.115, bf16[1024,512]{1,0:T(8,128)(2,1)S(1)} %bitcast.123), custom_call_target="tpu_custom_call" | custom-call | flops 4294967296 | bytes 19922944 | tf_op jit(solution)/shard_map/attn_grads/pallas_call | solution.py:456
  466.6 7.2 %attn_grads.3 = bf16[2048,1024]{1,0:T(8,128)(2,1)S(1)} custom-call(s32[4]{0:T(128)S(1)} %pad_add_fusion.rank_ref, bf16[1024,2048]{1,0:T(8,128)(2,1)S(1)} %bitcast.113, bf16[1024,2048]{1,0:T(8,128)(2,1)S(1)} %bitcast.119, bf16[1024,1536]{1,0:T(8,128)(2,1)S(1)} %bitcast.116, bf16[1024,1536]{1,0:T(8,128)(2,1)S(1)} %bitcast.117, ...), custom_call_target="tpu_custom_call" | custom-call | flops 4294967296 | bytes 19922944 | tf_op jit(solution)/shard_map/attn_grads/pallas_call | solution.py:456
  475.9 4.8 convolution_convert_fusion.5
  480.7 5.1 convolution_convert_fusion.3
  488.4 6.2 %fusion.1 = (f32[2048]{0:T(1024)S(1)}, f32[2048]{0:T(1024)S(1)}, f32[2048]{0:T(1024)S(1)}, f32[2048]{0:T(1024)S(1)}, f32[2048]{0:T(1024)S(1)}, /*index=5*/f32[20...) fusion(bf16[4,256,2048]{2,1,0:T(8,128)(2,1)} %copy-done.11, ...), kind=kOutput, calls=%fused_computation.19 | convolution fusion | flops 1623179264 | bytes 16580608 | tf_op jit(solution)/shard_map/dot_general | solution.py:53
  502.5 18.7 %collective-permute-done.32 = bf16[256,2048]{1,0:T(8,128)(2,1)S(1)} collective-permute-done((bf16[256,2048]{1,0:T(8,128)(2,1)}, bf16[256,2048]{1,0:T(8,128)(2,1)S(1)}, u32[]{:S(2)}, u32[]{:S(2)}) %collective-permute-start.32) | collective-permute-done | bytes 1048608 | tf_op jit(solution)/shard_map/ppermute | solution.py:568
  534.5 12.6 %collective-permute-done.33.moved_ref = bf16[256,2048]{1,0:T(8,128)(2,1)S(1)} collective-permute-done((bf16[256,2048]{1,0:T(8,128)(2,1)S(1)}, bf16[256,2048]{1,0:T(8,128)(2,1)S(1)}, u32[]{:S(2)}, u32[]{:S(2)}) %collective-permute-start.33) | collective-permute-done | bytes 1048608 | tf_op jit(solution)/shard_map/ppermute | solution.py:568
  557.2 4.8 slice_bitcast_fusion
  (314 shorter events, 179.2 us)
Async XLA Ops:
  7.2 468.7 %reduce-scatter.3.cloned.1.call-start = ((), (), s32[]{:S(2)}) async-start(), calls=%async_computation.2 | async-start | bytes 10485760 | tf_op jit(solution)/shard_map/reduce_scatter | solution.py:673
  9.5 17.7 %collective-permute-start = (bf16[256,1024]{1,0:T(8,128)(2,1)}, bf16[256,1024]{1,0:T(8,128)(2,1)}, u32[]{:S(2)}, u32[]{:S(2)}) collective-permute-start(bf16[256,1024]{1,0:T(8,128)(2,1)} %get-tuple-element.260.xa_ref), channel_id=1, source_target_pairs={{0,3},{1,0},{2,1},{3,2},{4,7},{5,4},{6,5},{7,6},{8,11},{9,8},{10,9... | collective-permute-start | bytes 1572872 | tf_op jit(solution)/shard_map/ppermute | solution.py:568
  14.5 23.9 %collective-permute-start.2 = (bf16[256,1024]{1,0:T(8,128)(2,1)}, bf16[256,1024]{1,0:T(8,128)(2,1)}, u32[]{:S(2)}, u32[]{:S(2)}) collective-permute-start(bf16[256,1024]{1,0:T(8,128)(2,1)} %get-tuple-element.259.xb_ref), channel_id=1, source_target_pairs={{0,3},{1,0},{2,1},{3,2},{4,7},{5,4},{6,5},{7,6},{8,11},{9,8},{10,9... | collective-permute-start | bytes 1572872 | tf_op jit(solution)/shard_map/ppermute | solution.py:568
  20.2 63.2 %copy-start.22 = (f32[4,256,128]{2,1,0:T(8,128)}, f32[4,256,128]{2,1,0:T(8,128)S(1)}, u32[]{:S(2)}) copy-start(f32[4,256,128]{2,1,0:T(8,128)S(1)} %get-tuple-element.268.cos_ref) | copy-start | bytes 1572868
  20.2 63.2 %copy-start.24 = (f32[4,256,128]{2,1,0:T(8,128)}, f32[4,256,128]{2,1,0:T(8,128)S(1)}, u32[]{:S(2)}) copy-start(f32[4,256,128]{2,1,0:T(8,128)S(1)} %get-tuple-element.269.sin_ref) | copy-start | bytes 1572868
  27.2 22.5 %collective-permute-start.1 = (bf16[256,1024]{1,0:T(8,128)(2,1)}, bf16[256,1024]{1,0:T(8,128)(2,1)S(1)}, u32[]{:S(2)}, u32[]{:S(2)}) collective-permute-start(bf16[256,1024]{1,0:T(8,128)(2,1)} %collective-permute-done.xa_ref), channel_id=1, source_target_pairs={{0,3},{1,0},{2,1},{3,2},{4,7},{5,4},{6,5},{7,6},{8,11},{9,8},{10,9... | collective-permute-start | bytes 1572872 | tf_op jit(solution)/shard_map/ppermute | solution.py:568
  38.4 22.5 %collective-permute-start.4 = (bf16[256,1024]{1,0:T(8,128)(2,1)}, bf16[256,1024]{1,0:T(8,128)(2,1)}, u32[]{:S(2)}, u32[]{:S(2)}) collective-permute-start(bf16[256,1024]{1,0:T(8,128)(2,1)} %collective-permute-done.2.xb_ref), channel_id=1, source_target_pairs={{0,3},{1,0},{2,1},{3,2},{4,7},{5,4},{6,5},{7,6},{8,11},{9,8},{10,9... | collective-permute-start | bytes 1572872 | tf_op jit(solution)/shard_map/ppermute | solution.py:568
  49.6 24.5 %collective-permute-start.3 = (bf16[256,1024]{1,0:T(8,128)(2,1)S(1)}, bf16[256,1024]{1,0:T(8,128)(2,1)S(1)}, u32[]{:S(2)}, u32[]{:S(2)}) collective-permute-start(bf16[256,1024]{1,0:T(8,128)(2,1)S(1)} %collective-permute-done.1.xa_ref), channel_id=1, source_target_pairs={{0,3},{1,0},{2,1},{3,2},{4,7},{5,4},{6,5},{7,6},{8,11},{9,8},{10,9... | collective-permute-start | bytes 1572872 | tf_op jit(solution)/shard_map/ppermute | solution.py:568
  60.9 22.6 %collective-permute-start.5 = (bf16[256,1024]{1,0:T(8,128)(2,1)}, bf16[256,1024]{1,0:T(8,128)(2,1)}, u32[]{:S(2)}, u32[]{:S(2)}) collective-permute-start(bf16[256,1024]{1,0:T(8,128)(2,1)} %collective-permute-done.4.xb_ref), channel_id=1, source_target_pairs={{0,3},{1,0},{2,1},{3,2},{4,7},{5,4},{6,5},{7,6},{8,11},{9,8},{10,9... | collective-permute-start | bytes 1572872 | tf_op jit(solution)/shard_map/ppermute | solution.py:568
  75.0 33.7 %collective-permute-start.6 = (bf16[256,2048]{1,0:T(8,128)(2,1)}, bf16[256,2048]{1,0:T(8,128)(2,1)}, u32[]{:S(2)}, u32[]{:S(2)}) collective-permute-start(bf16[256,2048]{1,0:T(8,128)(2,1)} %bitcast.9.gl_ref.gr_ref), channel_id=1, source_target_pairs={{0,1},{1,2},{2,3},{4,5},{5,6},{6,7},{8,9},{9,10},{10,11},{12,13},{... | collective-permute-start | bytes 3145736 | tf_op jit(solution)/shard_map/ppermute | solution.py:568
  77.2 38.1 %collective-permute-start.10 = (bf16[256,2048]{1,0:T(8,128)(2,1)}, bf16[256,2048]{1,0:T(8,128)(2,1)}, u32[]{:S(2)}, u32[]{:S(2)}) collective-permute-start(bf16[256,2048]{1,0:T(8,128)(2,1)} %bitcast.9.gl_ref.gr_ref), channel_id=1, source_target_pairs={{1,0},{2,1},{3,2},{5,4},{6,5},{7,6},{9,8},{10,9},{11,10},{13,12},{... | collective-permute-start | bytes 3145736 | tf_op jit(solution)/shard_map/ppermute | solution.py:568
  111.4 23.7 %collective-permute-start.7 = (bf16[256,2048]{1,0:T(8,128)(2,1)S(1)}, bf16[256,2048]{1,0:T(8,128)(2,1)S(1)}, u32[]{:S(2)}, u32[]{:S(2)}) collective-permute-start(bf16[256,2048]{1,0:T(8,128)(2,1)S(1)} %join.12), channel_id=1, source_target_pairs={{0,1},{1,2},{2,3},{4,5},{5,6},{6,7},{8,9},{9,10},{10,11},{12,13},{... | collective-permute-start | bytes 3145736 | tf_op jit(solution)/shard_map/ppermute | solution.py:568
  117.2 23.9 %collective-permute-start.11 = (bf16[256,2048]{1,0:T(8,128)(2,1)S(1)}, bf16[256,2048]{1,0:T(8,128)(2,1)S(1)}, u32[]{:S(2)}, u32[]{:S(2)}) collective-permute-start(bf16[256,2048]{1,0:T(8,128)(2,1)S(1)} %join.15), channel_id=1, source_target_pairs={{1,0},{2,1},{3,2},{5,4},{6,5},{7,6},{9,8},{10,9},{11,10},{13,12},{... | collective-permute-start | bytes 3145736 | tf_op jit(solution)/shard_map/ppermute | solution.py:568
  136.1 23.3 %collective-permute-start.8 = (bf16[256,2048]{1,0:T(8,128)(2,1)S(1)}, bf16[256,2048]{1,0:T(8,128)(2,1)S(1)}, u32[]{:S(2)}, u32[]{:S(2)}) collective-permute-start(bf16[256,2048]{1,0:T(8,128)(2,1)S(1)} %join.13), channel_id=1, source_target_pairs={{0,1},{1,2},{2,3},{4,5},{5,6},{6,7},{8,9},{9,10},{10,11},{12,13},{... | collective-permute-start | bytes 3145736 | tf_op jit(solution)/shard_map/ppermute | solution.py:568
  142.2 24.4 %collective-permute-start.12 = (bf16[256,2048]{1,0:T(8,128)(2,1)S(1)}, bf16[256,2048]{1,0:T(8,128)(2,1)S(1)}, u32[]{:S(2)}, u32[]{:S(2)}) collective-permute-start(bf16[256,2048]{1,0:T(8,128)(2,1)S(1)} %join.16), channel_id=1, source_target_pairs={{1,0},{2,1},{3,2},{5,4},{6,5},{7,6},{9,8},{10,9},{11,10},{13,12},{... | collective-permute-start | bytes 3145736 | tf_op jit(solution)/shard_map/ppermute | solution.py:568
  161.1 22.8 %collective-permute-start.9 = (bf16[256,2048]{1,0:T(8,128)(2,1)}, bf16[256,2048]{1,0:T(8,128)(2,1)}, u32[]{:S(2)}, u32[]{:S(2)}) collective-permute-start(bf16[256,2048]{1,0:T(8,128)(2,1)} %join.14), channel_id=1, source_target_pairs={{0,1},{1,2},{2,3},{4,5},{5,6},{6,7},{8,9},{9,10},{10,11},{12,13},{... | collective-permute-start | bytes 3145736 | tf_op jit(solution)/shard_map/ppermute | solution.py:568
  168.2 22.4 %collective-permute-start.13 = (bf16[256,2048]{1,0:T(8,128)(2,1)}, bf16[256,2048]{1,0:T(8,128)(2,1)}, u32[]{:S(2)}, u32[]{:S(2)}) collective-permute-start(bf16[256,2048]{1,0:T(8,128)(2,1)} %join.17), channel_id=1, source_target_pairs={{1,0},{2,1},{3,2},{5,4},{6,5},{7,6},{9,8},{10,9},{11,10},{13,12},{... | collective-permute-start | bytes 3145736 | tf_op jit(solution)/shard_map/ppermute | solution.py:568
  193.1 135.0 %copy-start.65 = (f32[256,2048]{1,0:T(8,128)}, f32[256,2048]{1,0:T(8,128)S(1)}, u32[]{:S(2)}) copy-start(f32[256,2048]{1,0:T(8,128)S(1)} %get-tuple-element.247) | copy-start | bytes 6291460
  194.3 22.7 %collective-permute-start.14 = (bf16[256,2048]{1,0:T(8,128)(2,1)S(1)}, bf16[256,2048]{1,0:T(8,128)(2,1)S(1)}, u32[]{:S(2)}, u32[]{:S(2)}) collective-permute-start(bf16[256,2048]{1,0:T(8,128)(2,1)S(1)} %add_convert_fusion.3.a_ref), channel_id=1, source_target_pairs={{0,3},{1,0},{2,1},{3,2},{4,7},{5,4},{6,5},{7,6},{8,11},{9,8},{10,9... | collective-permute-start | bytes 3145736 | tf_op jit(solution)/shard_map/ppermute | solution.py:568
  217.0 24.0 %collective-permute-start.15 = (bf16[256,2048]{1,0:T(8,128)(2,1)S(1)}, bf16[256,2048]{1,0:T(8,128)(2,1)S(1)}, u32[]{:S(2)}, u32[]{:S(2)}) collective-permute-start(bf16[256,2048]{1,0:T(8,128)(2,1)S(1)} %collective-permute-done.14.a_ref), channel_id=1, source_target_pairs={{0,3},{1,0},{2,1},{3,2},{4,7},{5,4},{6,5},{7,6},{8,11},{9,8},{10,9... | collective-permute-start | bytes 3145736 | tf_op jit(solution)/shard_map/ppermute | solution.py:568
  237.7 26.4 %collective-permute-start.17 = (bf16[256,2048]{1,0:T(8,128)(2,1)}, bf16[256,2048]{1,0:T(8,128)(2,1)S(1)}, u32[]{:S(2)}, u32[]{:S(2)}) collective-permute-start(bf16[256,2048]{1,0:T(8,128)(2,1)} %convolution_convert_fusion.7), channel_id=1, source_target_pairs={{0,3},{1,0},{2,1},{3,2},{4,7},{5,4},{6,5},{7,6},{8,11},{9,8},{10,9... | collective-permute-start | bytes 3145736 | tf_op jit(solution)/shard_map/ppermute | solution.py:568
  241.0 45.5 %collective-permute-start.16 = (bf16[256,2048]{1,0:T(8,128)(2,1)S(1)}, bf16[256,2048]{1,0:T(8,128)(2,1)S(1)}, u32[]{:S(2)}, u32[]{:S(2)}) collective-permute-start(bf16[256,2048]{1,0:T(8,128)(2,1)S(1)} %collective-permute-done.15.a_ref), channel_id=1, source_target_pairs={{0,3},{1,0},{2,1},{3,2},{4,7},{5,4},{6,5},{7,6},{8,11},{9,8},{10,9... | collective-permute-start | bytes 3145736 | tf_op jit(solution)/shard_map/ppermute | solution.py:568
  264.4 41.5 %collective-permute-start.18 = (bf16[256,2048]{1,0:T(8,128)(2,1)S(1)}, bf16[256,2048]{1,0:T(8,128)(2,1)S(1)}, u32[]{:S(2)}, u32[]{:S(2)}) collective-permute-start(bf16[256,2048]{1,0:T(8,128)(2,1)S(1)} %add_convert_fusion.2), channel_id=1, source_target_pairs={{0,3},{1,0},{2,1},{3,2},{4,7},{5,4},{6,5},{7,6},{8,11},{9,8},{10,9... | collective-permute-start | bytes 3145736 | tf_op jit(solution)/shard_map/ppermute | solution.py:568
  306.2 20.3 %collective-permute-start.19 = (bf16[256,2048]{1,0:T(8,128)(2,1)S(1)}, bf16[256,2048]{1,0:T(8,128)(2,1)S(1)}, u32[]{:S(2)}, u32[]{:S(2)}) collective-permute-start(bf16[256,2048]{1,0:T(8,128)(2,1)S(1)} %add_convert_fusion.1), channel_id=1, source_target_pairs={{0,3},{1,0},{2,1},{3,2},{4,7},{5,4},{6,5},{7,6},{8,11},{9,8},{10,9... | collective-permute-start | bytes 3145736 | tf_op jit(solution)/shard_map/ppermute | solution.py:568
  315.3 34.4 %collective-permute-start.23 = (bf16[2048,1024]{1,0:T(8,128)(2,1)S(1)}, bf16[2048,1024]{1,0:T(8,128)(2,1)}, u32[]{:S(2)}, u32[]{:S(2)}) collective-permute-start(bf16[2048,1024]{1,0:T(8,128)(2,1)S(1)} %grad_half.4), channel_id=1, source_target_pairs={{0,4},{4,0},{8,12},{12,8},{16,20},{20,16},{24,28},{28,24},{1,5},{5... | collective-permute-start | bytes 12582920 | tf_op jit(solution)/shard_map/ppermute | solution.py:589
  322.6 34.3 %collective-permute-start.22 = (bf16[2048,1024]{1,0:T(8,128)(2,1)}, bf16[2048,1024]{1,0:T(8,128)(2,1)}, u32[]{:S(2)}, u32[]{:S(2)}) collective-permute-start(bf16[2048,1024]{1,0:T(8,128)(2,1)} %grad_half.5), channel_id=1, source_target_pairs={{0,4},{4,0},{8,12},{12,8},{16,20},{20,16},{24,28},{28,24},{1,5},{5... | collective-permute-start | bytes 12582920 | tf_op jit(solution)/shard_map/ppermute | solution.py:589
  331.6 35.8 %collective-permute-start.20 = (bf16[256,2048]{1,0:T(8,128)(2,1)S(1)}, bf16[256,2048]{1,0:T(8,128)(2,1)S(1)}, u32[]{:S(2)}, u32[]{:S(2)}) collective-permute-start(bf16[256,2048]{1,0:T(8,128)(2,1)S(1)} %get-tuple-element.207.refs_0_), channel_id=1, source_target_pairs={{0,1},{1,2},{2,3},{4,5},{5,6},{6,7},{8,9},{9,10},{10,11},{12,13},{... | collective-permute-start | bytes 3145736 | tf_op jit(solution)/shard_map/ppermute | solution.py:568
  335.3 32.1 %collective-permute-start.21 = (bf16[256,2048]{1,0:T(8,128)(2,1)S(1)}, bf16[256,2048]{1,0:T(8,128)(2,1)S(1)}, u32[]{:S(2)}, u32[]{:S(2)}) collective-permute-start(bf16[256,2048]{1,0:T(8,128)(2,1)S(1)} %get-tuple-element.207.refs_0_), channel_id=1, source_target_pairs={{1,0},{2,1},{3,2},{5,4},{6,5},{7,6},{9,8},{10,9},{11,10},{13,12},{... | collective-permute-start | bytes 3145736 | tf_op jit(solution)/shard_map/ppermute | solution.py:568
  371.3 24.1 %collective-permute-start.24 = (bf16[256,2048]{1,0:T(8,128)(2,1)}, bf16[256,2048]{1,0:T(8,128)(2,1)}, u32[]{:S(2)}, u32[]{:S(2)}) collective-permute-start(bf16[256,2048]{1,0:T(8,128)(2,1)} %join.18), channel_id=1, source_target_pairs={{0,1},{1,2},{2,3},{4,5},{5,6},{6,7},{8,9},{9,10},{10,11},{12,13},{... | collective-permute-start | bytes 3145736 | tf_op jit(solution)/shard_map/ppermute | solution.py:568
  378.3 26.1 %collective-permute-start.27 = (bf16[256,2048]{1,0:T(8,128)(2,1)}, bf16[256,2048]{1,0:T(8,128)(2,1)}, u32[]{:S(2)}, u32[]{:S(2)}) collective-permute-start(bf16[256,2048]{1,0:T(8,128)(2,1)} %join.21), channel_id=1, source_target_pairs={{1,0},{2,1},{3,2},{5,4},{6,5},{7,6},{9,8},{10,9},{11,10},{13,12},{... | collective-permute-start | bytes 3145736 | tf_op jit(solution)/shard_map/ppermute | solution.py:568
  379.6 176.2 %reduce-scatter.5.cloned.1.call-start = ((), (), s32[]{:S(2)}) async-start(), calls=%async_computation.3 | async-start | bytes 5242880 | tf_op jit(solution)/shard_map/reduce_scatter | solution.py:699
  399.5 23.1 %collective-permute-start.25 = (bf16[256,2048]{1,0:T(8,128)(2,1)S(1)}, bf16[256,2048]{1,0:T(8,128)(2,1)S(1)}, u32[]{:S(2)}, u32[]{:S(2)}) collective-permute-start(bf16[256,2048]{1,0:T(8,128)(2,1)S(1)} %join.19), channel_id=1, source_target_pairs={{0,1},{1,2},{2,3},{4,5},{5,6},{6,7},{8,9},{9,10},{10,11},{12,13},{... | collective-permute-start | bytes 3145736 | tf_op jit(solution)/shard_map/ppermute | solution.py:568
  406.4 22.5 %collective-permute-start.28 = (bf16[256,2048]{1,0:T(8,128)(2,1)S(1)}, bf16[256,2048]{1,0:T(8,128)(2,1)S(1)}, u32[]{:S(2)}, u32[]{:S(2)}) collective-permute-start(bf16[256,2048]{1,0:T(8,128)(2,1)S(1)} %join.22), channel_id=1, source_target_pairs={{1,0},{2,1},{3,2},{5,4},{6,5},{7,6},{9,8},{10,9},{11,10},{13,12},{... | collective-permute-start | bytes 3145736 | tf_op jit(solution)/shard_map/ppermute | solution.py:568
  423.4 24.7 %collective-permute-start.26 = (bf16[256,2048]{1,0:T(8,128)(2,1)S(1)}, bf16[256,2048]{1,0:T(8,128)(2,1)S(1)}, u32[]{:S(2)}, u32[]{:S(2)}) collective-permute-start(bf16[256,2048]{1,0:T(8,128)(2,1)S(1)} %join.20), channel_id=1, source_target_pairs={{0,1},{1,2},{2,3},{4,5},{5,6},{6,7},{8,9},{9,10},{10,11},{12,13},{... | collective-permute-start | bytes 3145736 | tf_op jit(solution)/shard_map/ppermute | solution.py:568
  429.6 21.4 %collective-permute-start.29 = (bf16[256,2048]{1,0:T(8,128)(2,1)S(1)}, bf16[256,2048]{1,0:T(8,128)(2,1)S(1)}, u32[]{:S(2)}, u32[]{:S(2)}) collective-permute-start(bf16[256,2048]{1,0:T(8,128)(2,1)S(1)} %join.23), channel_id=1, source_target_pairs={{1,0},{2,1},{3,2},{5,4},{6,5},{7,6},{9,8},{10,9},{11,10},{13,12},{... | collective-permute-start | bytes 3145736 | tf_op jit(solution)/shard_map/ppermute | solution.py:568
  459.4 7.2 %collective-permute-start.30 = (bf16[2048,1024]{1,0:T(8,128)(2,1)S(1)}, bf16[2048,1024]{1,0:T(8,128)(2,1)S(1)}, u32[]{:S(2)}, u32[]{:S(2)}) collective-permute-start(bf16[2048,1024]{1,0:T(8,128)(2,1)S(1)} %attn_grads.2), channel_id=1, source_target_pairs={{0,4},{4,0},{8,12},{12,8},{16,20},{20,16},{24,28},{28,24},{1,5},{5... | collective-permute-start | bytes 12582920 | tf_op jit(solution)/shard_map/ppermute | solution.py:589
  462.3 26.1 %collective-permute-start.31 = (bf16[256,2048]{1,0:T(8,128)(2,1)}, bf16[256,2048]{1,0:T(8,128)(2,1)}, u32[]{:S(2)}, u32[]{:S(2)}) collective-permute-start(bf16[256,2048]{1,0:T(8,128)(2,1)} %convolution_convert_fusion.6), channel_id=1, source_target_pairs={{0,3},{1,0},{2,1},{3,2},{4,7},{5,4},{6,5},{7,6},{8,11},{9,8},{10,9... | collective-permute-start | bytes 3145736 | tf_op jit(solution)/shard_map/ppermute | solution.py:568
  494.7 26.5 %collective-permute-start.32 = (bf16[256,2048]{1,0:T(8,128)(2,1)}, bf16[256,2048]{1,0:T(8,128)(2,1)S(1)}, u32[]{:S(2)}, u32[]{:S(2)}) collective-permute-start(bf16[256,2048]{1,0:T(8,128)(2,1)} %get-tuple-element.258), channel_id=1, source_target_pairs={{0,3},{1,0},{2,1},{3,2},{4,7},{5,4},{6,5},{7,6},{8,11},{9,8},{10,9... | collective-permute-start | bytes 3145736 | tf_op jit(solution)/shard_map/ppermute | solution.py:568
  497.4 1.2 collective-permute-start.34
  498.6 31.4 %collective-permute-start.35 = (f32[8320]{0:T(1024)S(1)}, f32[8320]{0:T(1024)S(1)}, u32[]{:S(2)}, u32[]{:S(2)}) collective-permute-start(f32[8320]{0:T(1024)S(1)} %add.143), channel_id=1, source_target_pairs={{0,1},{1,2},{2,3},{3,0},{4,5},{5,6},{6,7},{7,4},{8,9},{9,10},{10,1... | collective-permute-start | bytes 99848 | tf_op jit(solution)/shard_map/ppermute | solution.py:568
  498.6 31.4 %collective-permute-start.36 = (f32[8320]{0:T(1024)S(1)}, f32[8320]{0:T(1024)S(1)}, u32[]{:S(2)}, u32[]{:S(2)}) collective-permute-start(f32[8320]{0:T(1024)S(1)} %add.143), channel_id=1, source_target_pairs={{0,2},{1,3},{2,0},{3,1},{4,6},{5,7},{6,4},{7,5},{8,10},{9,11},{10,... | collective-permute-start | bytes 99848 | tf_op jit(solution)/shard_map/ppermute | solution.py:568
  499.2 30.8 %collective-permute-start.37 = (f32[8320]{0:T(1024)S(1)}, f32[8320]{0:T(1024)S(1)}, u32[]{:S(2)}, u32[]{:S(2)}) collective-permute-start(f32[8320]{0:T(1024)S(1)} %add.143), channel_id=1, source_target_pairs={{0,3},{1,0},{2,1},{3,2},{4,7},{5,4},{6,5},{7,6},{8,11},{9,8},{10,9... | collective-permute-start | bytes 99848 | tf_op jit(solution)/shard_map/ppermute | solution.py:568
  522.8 24.3 %collective-permute-start.33 = (bf16[256,2048]{1,0:T(8,128)(2,1)S(1)}, bf16[256,2048]{1,0:T(8,128)(2,1)S(1)}, u32[]{:S(2)}, u32[]{:S(2)}) collective-permute-start(bf16[256,2048]{1,0:T(8,128)(2,1)S(1)} %fusion.2), channel_id=1, source_target_pairs={{0,3},{1,0},{2,1},{3,2},{4,7},{5,4},{6,5},{7,6},{8,11},{9,8},{10,9... | collective-permute-start | bytes 3145736 | tf_op jit(solution)/shard_map/ppermute | solution.py:568
  530.0 19.9 %collective-permute-start.38 = (f32[8320]{0:T(1024)S(1)}, f32[8320]{0:T(1024)S(1)}, u32[]{:S(2)}, u32[]{:S(2)}) collective-permute-start(f32[8320]{0:T(1024)S(1)} %add_add_fusion.2), channel_id=1, source_target_pairs={{0,8},{4,12},{8,16},{12,20},{16,24},{20,28},{24,0},{28,4},{1,9},{5... | collective-permute-start | bytes 99848 | tf_op jit(solution)/shard_map/ppermute | solution.py:740
  531.6 18.3 %collective-permute-start.39 = (f32[8320]{0:T(1024)S(1)}, f32[8320]{0:T(1024)S(1)}, u32[]{:S(2)}, u32[]{:S(2)}) collective-permute-start(f32[8320]{0:T(1024)S(1)} %add_add_fusion.2), channel_id=1, source_target_pairs={{0,16},{4,20},{8,24},{12,28},{16,0},{20,4},{24,8},{28,12},{1,17},{... | collective-permute-start | bytes 99848 | tf_op jit(solution)/shard_map/ppermute | solution.py:740
  533.2 16.7 %collective-permute-start.40 = (f32[8320]{0:T(1024)S(1)}, f32[8320]{0:T(1024)S(1)}, u32[]{:S(2)}, u32[]{:S(2)}) collective-permute-start(f32[8320]{0:T(1024)S(1)} %add_add_fusion.2), channel_id=1, source_target_pairs={{0,24},{4,28},{8,0},{12,4},{16,8},{20,12},{24,16},{28,20},{1,25},{... | collective-permute-start | bytes 99848 | tf_op jit(solution)/shard_map/ppermute | solution.py:740
  550.0 2.7 collective-permute-start.42
  557.0 5.0 collective-permute-start.41
  (84 other events, 749.3 us)
Sparse Core Ops, SparseCore 0:
  379.8 88.1 reduce-scatter.2
  476.0 51.2 reduce-scatter.4

commit v5 on v4

--- a/solution.py
+++ b/solution.py
@@ -114,7 +114,7 @@
         out_shape=[jax.ShapeDtypeStruct((n, rows, d), BF16)]
         + [jax.ShapeDtypeStruct((n, rows, local), BF16)] * 3,
         input_output_aliases=aliases,
-        compiler_params=params(28),
+        compiler_params=params(56),
         cost_estimate=cost(6 * rows * d * local, 6 * d * local + 4 * rows * d),
         name="qkv_slot",
     )(rank, xa, xb, gain, shift, wq, wk, wv, cos, sin, *extra)
@@ -470,7 +470,7 @@
         ),
         out_shape=jax.ShapeDtypeStruct((d, 2 * local), BF16),
         compiler_params=params(28),
-        cost_estimate=cost(4 * t * d * local, 2 * t * (2 * d + 3 * local) + 8 * d * local),
+        cost_estimate=cost(1e6, 1e6),
         name="attn_grads",
     )(rank, act, states, dqkv, dqkv, om, *([] if partner else [moved]))
 
@@ -524,7 +524,7 @@
         out_specs=row(d),
         out_shape=jax.ShapeDtypeStruct((rows, d), BF16),
         compiler_params=params(12),
-        cost_estimate=cost(15e9, 12 * rows * d),
+        cost_estimate=cost(22e9, 12 * rows * d),
         name="last_step",
     )(x, gain, term, moved, state)
 
@@ -575,7 +575,7 @@
         if k:
             right = join(where, right, terms, n - k, k, True)
             left = join(where, left, terms, k, n - k, False)
-        return send(right, right_line), send(left, left_line)
+        return send(right, right_line), send(left, left_line), right, left
 
     def owned(terms, right, left):
         return terms[0].astype(F32) + right.astype(F32) + left.astype(F32)
@@ -615,13 +615,13 @@
     (right,) = tie([grad_own], block[0])
     left = right
     grads_r, grads_l = [right], [left]
-    right, left = tick(0, right, left, None)
+    right, left, _, _ = tick(0, right, left, None)
     masked = attend(where, query, keys, vals, docs_col, docs_row, heads_col)
     terms = low(dot_t(flat(masked), output_weight)).reshape(n, rows, d)
     for k in range(1, n):
         grads_r.append(right)
         grads_l.append(left)
-        right, left = tick(k, right, left, terms)
+        right, left, _, _ = tick(k, right, left, terms)
     attn = owned(terms, right, left)
     x_rows = own.astype(F32)
     state = x_rows + attn
@@ -663,19 +663,24 @@
     grad_state = grad_own.astype(F32) + back_two
 
     start = low(grad_state)
-    grad_all, active, second_all, grad_upper, start = tie([grad_all, active, second_all, grad_upper, start])
+    grad_all, active, start = tie([grad_all, active, start])
     right = left = start
     rights, lefts = [start], [start]
-    right, left = tick(0, right, left, None)
+    right, left, _, _ = tick(0, right, left, None)
     ffn = low(dot_t(flat(active), down_weight)).reshape(n, rows, d)
     pair = grad_half(flat(grad_all), flat(active), where, False, 0, down_gift)
-    pair = grad_half(flat(second_all), flat(grad_upper), where, False, 1, up_gift, pair)
-    wide_grad = lax.psum_scatter(pair, "dp", scatter_dimension=1, axis_index_groups=sides, tiled=True)
-    right, left = tie([right, left], pair)
+    (right,) = tie([right], pair)
+    (left,) = tie([left], pair)
     for k in range(1, n):
         rights.append(right)
         lefts.append(left)
-        right, left = tick(k, right, left, ffn)
+        right, left, went_r, went_l = tick(k, right, left, ffn)
+        if k == 1:
+            second_all, grad_upper = tie([second_all, grad_upper], went_r, went_l)
+            pair = grad_half(flat(second_all), flat(grad_upper), where, False, 1, up_gift, pair)
+            wide_grad = lax.psum_scatter(pair, "dp", scatter_dimension=1, axis_index_groups=sides, tiled=True)
+            (right,) = tie([right], pair)
+            (left,) = tie([left], pair)
     late = sorted({1, n - 1})
     early = [s for s in range(n) if s not in late]
     pick = lambda slots: sum(([start] if s == 0 else [lefts[s], rights[n - s]] for s in slots), [])
@@ -687,22 +692,34 @@
     mixed = low(state + owned(ffn, right, left))
 
     (dqkv,) = tie([dqkv], right, left)
+    def whole(part):
+        span = part.shape[-2] // 2
+        mine = lax.dynamic_slice_in_dim(part, side * span, span, part.ndim - 2)
+        got = swap(lax.dynamic_slice_in_dim(part, (1 - side) * span, span, part.ndim - 2))
+        return jnp.where(side == 0, mine, got).astype(F32), jnp.where(side == 0, got, mine).astype(F32)
+
     tokens_of = lambda v: (flat(first_all), flat(state_all), flat(v), flat(masked), where)
-    gift = attn_grads(*tokens_of(dqkv))
-    (dqkv,) = tie([dqkv], gift)
-    gift = swap(gift)
     sent = low(dot_t(dqkv[1], weights))
     (dqkv,) = tie([dqkv], sent)
     moved = hop(sent)
-    attn_term = attn_grads(*tokens_of(dqkv), gift)
+    gift = attn_grads(*tokens_of(dqkv))
+    (dqkv,) = tie([dqkv], gift)
+    attn_term = attn_grads(*tokens_of(dqkv), swap(gift))
     (late,) = tie([attn_term], wide_grad)
     attn_grad = lax.psum_scatter(late, "dp", scatter_dimension=0, axis_index_groups=sides, tiled=True)
-    (dqkv,) = tie([dqkv], attn_term)
-    terms = {s: low(dot_t(dqkv[s], weights)) for s in range(1, n)}
-    (dqkv,) = tie([dqkv], terms[n - 1])
+    terms = {1: sent}
+    for s in range(2, n):
+        (dqkv,) = tie([dqkv], attn_term)
+        terms[s] = low(dot_t(dqkv[s], weights))
+        (dqkv,) = tie([dqkv], terms[s])
+        if s == 2:
+            sent2 = sent = add(terms[2], moved)
+            moved = hop(sent)
+            (dqkv,) = tie([dqkv], sent)
     terms[0] = low(dot_t(dqkv[0], weights))
-    sum_d = sum(jnp.sum(terms[s].astype(F32), axis=0) for s in range(n))
-    sum_da = sum(jnp.sum(terms[s].astype(F32) * first_all[s].astype(F32), axis=0) for s in range(n))
+    held = tie([terms[s] for s in range(n)], sent2)
+    sum_d = sum(jnp.sum(v.astype(F32), axis=0) for v in held)
+    sum_da = sum(jnp.sum(v.astype(F32) * first_all[s].astype(F32), axis=0) for s, v in enumerate(held))
     first_shift_part = sum_d
     first_gain_part = (sum_da - first_shift * sum_d) / first_gain
 
@@ -726,15 +743,14 @@
         ]
     )
     small = sum_over(small, "dp", [[(i, i ^ 1) for i in range(n_dp)]])
-    for s in range(2, n):
+    wide = jnp.concatenate(whole(wide_grad), axis=2)
+    for s in range(3, n):
+        if s == 3:
+            moved, wide = tie([moved, wide])
         sent = add(terms[s], moved)
-        if s == 2:
-            first_sent = sent
         moved = hop(sent)
-    if n == 2:
-        first_sent = sent
-
-    planes = tie([send(small, [(i, (i + m) % n) for i in range(n)]) for m in range(1, n)], first_sent)
+
+    planes = tie([send(small, [(i, (i + m) % n) for i in range(n)]) for m in range(1, n)], sent)
     small = small + sum(planes)
     others = [
         lax.ppermute(small, "dp", [(i, (i + 2 * m) % n_dp) for i in range(n_dp)])
@@ -743,13 +759,6 @@
     input_grad = last_step(own, gain1, terms[0], moved, grad_state)
     small = small + sum(tie(others, input_grad))
 
-    def whole(part):
-        span = part.shape[-2] // 2
-        mine = lax.dynamic_slice_in_dim(part, side * span, span, part.ndim - 2)
-        got = swap(lax.dynamic_slice_in_dim(part, (1 - side) * span, span, part.ndim - 2))
-        return jnp.where(side == 0, mine, got).astype(F32), jnp.where(side == 0, got, mine).astype(F32)
-
-    wide = jnp.concatenate(whole(wide_grad), axis=2)
     query_key, value_out = whole(attn_grad)
     return (
         mixed[None],

time: 580 us -> 564 us (0.972)
  Pallas kernels: 149 us -> 160 us
  local copies, waits for them, and re-layouts: 49.3 us -> 38.7 us
  waiting for transfers between devices: 167 us -> 158 us
  matrix products: 62.9 us -> 56 us
    pallas_call x4, Pallas kernels: 16.7 us -> 28.6 us  [qkv_slot(): pl.pallas_call(qkv_body, grid_spec=pltpu.PrefetchScalarGridSpec(num_scala...]
    dot_general x11 -> x10, matrix products: 62.9 us -> 56 us  [dot_t(): lax.dot_general(left, right, (((1,), (1,)), ((), ())), preferred_element_...]
    ppermute x34, waiting for transfers between devices: 161 us -> 154 us  [per_device(): send = lambda v, pairs: lax.ppermute(v, 'mp', pairs)]
    unnamed x177 -> x171, local copies, waits for them, and re-layouts: 35.5 us -> 29.1 us
  transfers between devices with their start and end apart: 45 -> 45, of which waited for: 26 -> 24; matrix products, arithmetic and copies ran while one was open for 16% -> 16% of each run, Pallas kernels for 26% -> 29%
where the time goes in v5:
time: 564 us; the launch traced here: 556 us
  Pallas kernels  160 us (28%)
  waiting for transfers between devices  158 us (28%)
  starting transfers between devices  97.8 us (17%)
  matrix products  56 us (10%)
  local copies, waits for them, and re-layouts  38.7 us (7%)
  other arithmetic  29.7 us (5%)
  between operations  15.9 us (3%)
    ppermute x34, waiting for transfers between devices, per_device(): send = lambda v, pairs: lax.ppermute(v, 'mp', pairs)  154 us
    ppermute x34, starting transfers between devices, per_device(): send = lambda v, pairs: lax.ppermute(v, 'mp', pairs)  92.6 us
    dot_general x10, matrix products, dot_t(): lax.dot_general(left, right, (((1,), (1,)), ((), ())), preferred_element_...  56 us
    pallas_call x4, Pallas kernels, mlp_slot(): pl.pallas_call(functools.partial(mlp_body, slot, n), grid_spec=pltpu.Pref...  37.5 us
    unnamed x171, local copies, waits for them, and re-layouts  29.1 us
    pallas_call x4, Pallas kernels, grad_half(): pl.pallas_call(functools.partial(grad_body, not partner), grid_spec=pltpu...  28.6 us
    pallas_call x4, Pallas kernels, qkv_slot(): pl.pallas_call(qkv_body, grid_spec=pltpu.PrefetchScalarGridSpec(num_scala...  28.6 us
    pallas_call x2, Pallas kernels, attn_grads(): pl.pallas_call(functools.partial(attn_grad_body, partner), grid_spec=pltp...  16.5 us
  transfers between devices with their start and end apart: 45, of which 24 were waited for; matrix products, arithmetic and copies ran while one was open for 16% of the time, Pallas kernels for 29%

profile of v5, /device:TPU:0, one launch (start us, length us, event | category | flops | bytes accessed | tf_op | source)
XLA Modules:
  0.0 555.9 jit_solution(2853994046834405332)
XLA Ops:
  8.5 5.1 collective-permute-start
  17.9 7.1 %qkv_slot.4 = (bf16[4,256,2048]{2,1,0:T(8,128)(2,1)}, bf16[4,256,512]{2,1,0:T(8,128)(2,1)}, bf16[4,256,512]{2,1,0:T(8,128)(2,1)}, bf16[4,256,512]{2,1,0:T(8,128)(2,1)}) custom-call(s32[4]{0:T(128)} %pad_add_fusion.rank_ref, bf16[256,1024]{1,0:T(8,128)(2,1)} %copy-done.64, bf16[256,1024]{1,0:T(8,128)(2,1)} %copy-done.63, f32[1,2048]{1,0:T(1,128)} %bitcast.123, ...), custom_call_target="tpu_custom_call" | custom-call | flops 1610612736 | bytes 8388608 | tf_op jit(solution)/shard_map/qkv_slot/pallas_call | solution.py:106
  26.0 4.4 collective-permute-start.1
  30.3 6.8 %collective-permute-done.2.xb_ref = bf16[256,1024]{1,0:T(8,128)(2,1)S(1)} collective-permute-done((bf16[256,1024]{1,0:T(8,128)(2,1)S(1)}, bf16[256,1024]{1,0:T(8,128)(2,1)S(1)}, u32[]{:S(2)}, u32[]{:S(2)}) %collective-permute-start.2) | collective-permute-done | bytes 524320 | tf_op jit(solution)/shard_map/ppermute | solution.py:568
  37.2 4.3 collective-permute-start.4
  41.5 7.1 %qkv_slot.5 = (bf16[4,256,2048]{2,1,0:T(8,128)(2,1)}, bf16[4,256,512]{2,1,0:T(8,128)(2,1)}, bf16[4,256,512]{2,1,0:T(8,128)(2,1)}, bf16[4,256,512]{2,1,0:T(8,128)(2,1)}) custom-call(s32[4]{0:T(128)} %pad_add_fusion.rank_ref, ...), custom_call_target="tpu_custom_call", output_to_operand_aliasing={{0}: (10, {}), {1}: (11, {}), {2}: (12, {}), {3}: (13, {})} | custom-call | flops 1610612736 | bytes 8388608 | tf_op jit(solution)/shard_map/qkv_slot/pallas_call | solution.py:106
  48.7 4.1 collective-permute-start.3
  52.8 6.9 %collective-permute-done.4.xb_ref = bf16[256,1024]{1,0:T(8,128)(2,1)} collective-permute-done((bf16[256,1024]{1,0:T(8,128)(2,1)S(1)}, bf16[256,1024]{1,0:T(8,128)(2,1)}, u32[]{:S(2)}, u32[]{:S(2)}) %collective-permute-start.4) | collective-permute-done | bytes 524320 | tf_op jit(solution)/shard_map/ppermute | solution.py:568
  59.7 4.4 collective-permute-start.5
  64.0 7.1 %qkv_slot.6 = (bf16[4,256,2048]{2,1,0:T(8,128)(2,1)}, bf16[4,256,512]{2,1,0:T(8,128)(2,1)}, bf16[4,256,512]{2,1,0:T(8,128)(2,1)}, bf16[4,256,512]{2,1,0:T(8,128)(2,1)}) custom-call(s32[4]{0:T(128)} %pad_add_fusion.rank_ref, bf16[256,1024]{1,0:T(8,128)(2,1)} %copy-done.70, ...), custom_call_target="tpu_custom_call", output_to_operand_aliasing={{0}: (10, {}), {1}: (11, {}), {2}: (12, {}), {3}: (13, {})} | custom-call | flops 1610612736 | bytes 8388608 | tf_op jit(solution)/shard_map/qkv_slot/pallas_call | solution.py:106
  78.2 4.1 collective-permute-done.5.xb_ref
  82.3 7.1 %qkv_slot.7 = (bf16[4,256,2048]{2,1,0:T(8,128)(2,1)}, bf16[4,256,512]{2,1,0:T(8,128)(2,1)}, bf16[4,256,512]{2,1,0:T(8,128)(2,1)}, bf16[4,256,512]{2,1,0:T(8,128)(2,1)}) custom-call(s32[4]{0:T(128)} %pad_add_fusion.rank_ref, bf16[256,1024]{1,0:T(8,128)(2,1)} %copy-done.69, ...), custom_call_target="tpu_custom_call", output_to_operand_aliasing={{0}: (10, {}), {1}: (11, {}), {2}: (12, {}), {3}: (13, {})} | custom-call | flops 1610612736 | bytes 8388608 | tf_op jit(solution)/shard_map/qkv_slot/pallas_call | solution.py:106
  93.2 8.6 %attend.1 = bf16[4,256,512]{2,1,0:T(8,128)(2,1)S(1)} custom-call(s32[4]{0:T(128)S(1)} %copy-done.49, bf16[4,256,512]{2,1,0:T(8,128)(2,1)S(1)} %copy-done.21, bf16[4,256,512]{2,1,0:T(8,128)(2,1)S(1)} %copy-done.23, bf16[4,256,512]{2,1,0:T(8,128)(2,1)S(1)} %copy-done.25, s32[4,256,1]{2,1,0:T(8,128)S(1)} %reshape.203.dcol_ref, s32[4,1,256]{2,1,0:T(1,128)S(1)} %bitcast.128, ...), custom_call_target="tpu_custom_call" | custom-call | flops 2147483648 | bytes 4194304 | tf_op jit(solution)/shard_map/attend/pallas_call | solution.py:169
  111.8 18.3 %collective-permute-done.7.moved_ref.gr_ref = bf16[256,2048]{1,0:T(8,128)(2,1)S(1)} collective-permute-done((bf16[256,2048]{1,0:T(8,128)(2,1)S(1)}, bf16[256,2048]{1,0:T(8,128)(2,1)S(1)}, u32[]{:S(2)}, u32[]{:S(2)}) %collective-permute-start.7) | collective-permute-done | bytes 1048608 | tf_op jit(solution)/shard_map/ppermute | solution.py:568
  131.2 4.4 collective-permute-start.8
  139.1 18.1 %collective-permute-done.8.moved_ref.gr_ref = bf16[256,2048]{1,0:T(8,128)(2,1)S(1)} collective-permute-done((bf16[256,2048]{1,0:T(8,128)(2,1)S(1)}, bf16[256,2048]{1,0:T(8,128)(2,1)S(1)}, u32[]{:S(2)}, u32[]{:S(2)}) %collective-permute-start.8) | collective-permute-done | bytes 1048608 | tf_op jit(solution)/shard_map/ppermute | solution.py:568
  158.9 5.5 collective-permute-start.9
  172.3 12.3 %collective-permute-done.9 = bf16[256,2048]{1,0:T(8,128)(2,1)} collective-permute-done((bf16[256,2048]{1,0:T(8,128)(2,1)}, bf16[256,2048]{1,0:T(8,128)(2,1)}, u32[]{:S(2)}, u32[]{:S(2)}) %collective-permute-start.9) | collective-permute-done | bytes 1048608 | tf_op jit(solution)/shard_map/ppermute | solution.py:568
  184.5 6.7 %collective-permute-done.13 = bf16[256,2048]{1,0:T(8,128)(2,1)} collective-permute-done((bf16[256,2048]{1,0:T(8,128)(2,1)}, bf16[256,2048]{1,0:T(8,128)(2,1)}, u32[]{:S(2)}, u32[]{:S(2)}) %collective-permute-start.13) | collective-permute-done | bytes 1048608 | tf_op jit(solution)/shard_map/ppermute | solution.py:568
  196.4 9.3 %mlp_slot.4 = (bf16[4,256,2048]{2,1,0:T(8,128)(2,1)S(1)}, bf16[4,256,2048]{2,1,0:T(8,128)(2,1)S(1)}, bf16[4,256,2048]{2,1,0:T(8,128)(2,1)S(1)}, bf16[4,256,2048]{2,1,0:T(8,128)(2,1)S(1)}) custom-call(s32[4]{0:T(128)S(1)} %copy-done.49, bf16[256,2048]{1,0:T(8,128)(2,1)S(1)} %add_convert_fusion.5.a_ref, bf16[256,2048]{1,0:T(8,128)(2,1)S(1)} %bitcast.116, ...), custom_call_target="tpu_custom_call" | custom-call | flops 4294967296 | bytes 20971520 | tf_op jit(solution)/shard_map/mlp_slot/pallas_call | solution.py:303
  205.7 7.2 %fusion.10 = f32[256,2048]{1,0:T(8,128)} fusion(bf16[2048,2048]{1,0:T(8,128)(2,1)} %up_ref.7, bf16[4,256,2048]{2,1,0:T(8,128)(2,1)S(1)} %get-tuple-element.186.rest_1_), kind=kOutput, calls=%fused_computation.42 | convolution fusion | flops 2147483648 | bytes 11534336 | tf_op jit(solution)/shard_map/dot_general | solution.py:53
  212.8 6.5 %collective-permute-done.14.a_ref = bf16[256,2048]{1,0:T(8,128)(2,1)S(1)} collective-permute-done((bf16[256,2048]{1,0:T(8,128)(2,1)S(1)}, bf16[256,2048]{1,0:T(8,128)(2,1)S(1)}, u32[]{:S(2)}, u32[]{:S(2)}) %collective-permute-start.14) | collective-permute-done | bytes 1048608 | tf_op jit(solution)/shard_map/ppermute | solution.py:568
  220.2 9.6 %mlp_slot.5 = (bf16[4,256,2048]{2,1,0:T(8,128)(2,1)S(1)}, bf16[4,256,2048]{2,1,0:T(8,128)(2,1)S(1)}, bf16[4,256,2048]{2,1,0:T(8,128)(2,1)S(1)}, bf16[4,256,2048]{2,1,0:T(8,128)(2,1)S(1)}) custom-call(s32[4]{0:T(128)S(1)} %copy-done.49, ...), custom_call_target="tpu_custom_call", output_to_operand_aliasing={{0}: (7, {}), {1}: (8, {}), {2}: (9, {}), {3}: (10, {})} | custom-call | flops 4294967296 | bytes 20971520 | tf_op jit(solution)/shard_map/mlp_slot/pallas_call | solution.py:303
  231.9 6.9 %convolution_convert_fusion.6 = bf16[256,2048]{1,0:T(8,128)(2,1)} fusion(bf16[2048,2048]{1,0:T(8,128)(2,1)} %up_ref.7, bf16[4,256,2048]{2,1,0:T(8,128)(2,1)S(1)} %get-tuple-element.195.rest_1_), kind=kOutput, calls=%fused_computation.14 | convolution fusion | flops 2148007936 | bytes 10485760 | tf_op jit(solution)/shard_map/dot_general | solution.py:53
  246.9 9.3 %mlp_slot.6 = (bf16[4,256,2048]{2,1,0:T(8,128)(2,1)S(1)}, bf16[4,256,2048]{2,1,0:T(8,128)(2,1)S(1)}, bf16[4,256,2048]{2,1,0:T(8,128)(2,1)S(1)}, bf16[4,256,2048]{2,1,0:T(8,128)(2,1)S(1)}) custom-call(s32[4]{0:T(128)S(1)} %copy-done.49, ...), custom_call_target="tpu_custom_call", output_to_operand_aliasing={{0}: (7, {}), {1}: (8, {}), {2}: (9, {}), {3}: (10, {})} | custom-call | flops 4294967296 | bytes 20971520 | tf_op jit(solution)/shard_map/mlp_slot/pallas_call | solution.py:303
  256.2 5.7 %fusion.6 = f32[256,2048]{1,0:T(8,128)S(1)} fusion(bf16[2048,2048]{1,0:T(8,128)(2,1)} %up_ref.7, bf16[4,256,2048]{2,1,0:T(8,128)(2,1)S(1)} %get-tuple-element.204.rest_1_), kind=kOutput, calls=%fused_computation.38 | convolution fusion | flops 2147483648 | bytes 11534336 | tf_op jit(solution)/shard_map/dot_general | solution.py:53
  261.9 4.3 collective-permute-done.17
  270.7 18.0 %collective-permute-done.16.a_ref = bf16[256,2048]{1,0:T(8,128)(2,1)S(1)} collective-permute-done((bf16[256,2048]{1,0:T(8,128)(2,1)S(1)}, bf16[256,2048]{1,0:T(8,128)(2,1)S(1)}, u32[]{:S(2)}, u32[]{:S(2)}) %collective-permute-start.16) | collective-permute-done | bytes 1048608 | tf_op jit(solution)/shard_map/ppermute | solution.py:568
  288.7 9.3 %mlp_slot.7 = (bf16[4,256,2048]{2,1,0:T(8,128)(2,1)S(1)}, bf16[4,256,2048]{2,1,0:T(8,128)(2,1)S(1)}, bf16[4,256,2048]{2,1,0:T(8,128)(2,1)S(1)}, bf16[4,256,2048]{2,1,0:T(8,128)(2,1)S(1)}) custom-call(s32[4]{0:T(128)S(1)} %copy-done.49, ...), custom_call_target="tpu_custom_call", output_to_operand_aliasing={{0}: (7, {}), {1}: (8, {}), {2}: (9, {}), {3}: (10, {})} | custom-call | flops 4294967296 | bytes 20971520 | tf_op jit(solution)/shard_map/mlp_slot/pallas_call | solution.py:303
  298.1 8.6 %fusion.8 = f32[256,2048]{1,0:T(8,128)S(1)} fusion(bf16[2048,2048]{1,0:T(8,128)(2,1)} %up_ref.7, bf16[4,256,2048]{2,1,0:T(8,128)(2,1)S(1)} %get-tuple-element.223), kind=kOutput, calls=%fused_computation.40 | convolution fusion | flops 2147483648 | bytes 11534336 | tf_op jit(solution)/shard_map/dot_general | solution.py:53
  311.0 6.2 %grad_half.4 = bf16[2048,1024]{1,0:T(8,128)(2,1)S(1)} custom-call(s32[4]{0:T(128)S(1)} %copy-done.49, bf16[1024,2048]{1,0:T(8,128)(2,1)S(1)} %bitcast.106, bf16[1024,2048]{1,0:T(8,128)(2,1)S(1)} %bitcast.99), custom_call_target="tpu_custom_call" | custom-call | flops 1000000 | bytes 1000000 | tf_op jit(solution)/shard_map/grad_half/pallas_call | solution.py:413
  317.3 7.2 %grad_half.5 = bf16[2048,1024]{1,0:T(8,128)(2,1)} custom-call(s32[4]{0:T(128)S(1)} %copy-done.49, bf16[1024,2048]{1,0:T(8,128)(2,1)S(1)} %bitcast.104, bf16[1024,2048]{1,0:T(8,128)(2,1)S(1)} %bitcast.102), custom_call_target="tpu_custom_call" | custom-call | flops 1000000 | bytes 1000000 | tf_op jit(solution)/shard_map/grad_half/pallas_call | solution.py:413
  325.0 5.5 collective-permute-done.19
  339.6 11.4 %convolution_convert_fusion = bf16[1024,2048]{1,0:T(8,128)(2,1)S(1)} fusion(bf16[1024,2048]{1,0:T(8,128)(2,1)S(1)} %bitcast.100, bf16[2048,2048]{1,0:T(8,128)(2,1)} %down_ref.7), kind=kOutput, calls=%fused_computation | convolution fusion | flops 8592031744 | bytes 16777216 | tf_op jit(solution)/shard_map/dot_general | solution.py:53
  351.1 8.0 %grad_half.6.rest_1_ = bf16[2,2048,1024]{2,1,0:T(8,128)(2,1)S(1)} custom-call(s32[4]{0:T(128)S(1)} %copy-done.49, bf16[1024,2048]{1,0:T(8,128)(2,1)S(1)} %bitcast.107, bf16[1024,2048]{1,0:T(8,128)(2,1)S(1)} %bitcast.101, bf16[2048,1024]{1,0:T(8,128)(2,1)} %collective-permute-done.21.rest_0_), custom_call_target="tpu_custom_call" | custom-call | flops 1000000 | bytes 1000000 | tf_op jit(solution)/shard_map/grad_half/pallas_call | solution.py:413
  362.0 4.8 collective-permute-start.22
  369.6 7.2 %grad_half.7 = bf16[2,2048,1024]{2,1,0:T(8,128)(2,1)S(1)} custom-call(s32[4]{0:T(128)S(1)} %copy-done.49, bf16[1024,2048]{1,0:T(8,128)(2,1)S(1)} %bitcast.105, bf16[1024,2048]{1,0:T(8,128)(2,1)S(1)} %bitcast.103, bf16[2048,1024]{1,0:T(8,128)(2,1)} %collective-permute-done.24.rest_0_, ...), custom_call_target="tpu_custom_call", output_to_operand_aliasing={{}: (4, {})} | custom-call | flops 1000000 | bytes 1000000 | tf_op jit(solution)/shard_map/grad_half/pallas_call | solution.py:413
  383.3 6.7 %collective-permute-done.27.moved_ref.refs_1_ = bf16[256,2048]{1,0:T(8,128)(2,1)} collective-permute-done((bf16[256,2048]{1,0:T(8,128)(2,1)}, bf16[256,2048]{1,0:T(8,128)(2,1)}, u32[]{:S(2)}, u32[]{:S(2)}) %collective-permute-start.27) | collective-permute-done | bytes 1048608 | tf_op jit(solution)/shard_map/ppermute | solution.py:568
  400.6 4.2 dom_part.2
  404.8 10.4 %collective-permute-done.25.moved_ref.refs_1_ = bf16[256,2048]{1,0:T(8,128)(2,1)S(1)} collective-permute-done((bf16[256,2048]{1,0:T(8,128)(2,1)S(1)}, bf16[256,2048]{1,0:T(8,128)(2,1)S(1)}, u32[]{:S(2)}, u32[]{:S(2)}) %collective-permute-start.25) | collective-permute-done | bytes 1048608 | tf_op jit(solution)/shard_map/ppermute | solution.py:568
  416.1 4.5 collective-permute-start.26
  426.1 14.5 %attend_back.1 = bf16[4,256,1536]{2,1,0:T(8,128)(2,1)S(1)} custom-call(s32[4]{0:T(128)S(1)} %copy-done.49, bf16[4,256,512]{2,1,0:T(8,128)(2,1)S(1)} %copy-done.22, bf16[4,256,512]{2,1,0:T(8,128)(2,1)S(1)} %copy-done.24, bf16[4,256,512]{2,1,0:T(8,128)(2,1)S(1)} %copy-done.26, bf16[4,256,512]{2,1,0:T(8,128)(2,1)S(1)} %get-tuple-element.228.do_ref, ...), custom_call_target="tpu_custom_call" | custom-call | flops 108000002048 | bytes 7340032 | tf_op jit(solution)/shard_map/attend_back/pallas_call | solution.py:251
  445.4 8.3 %attn_grads.2 = bf16[2048,1024]{1,0:T(8,128)(2,1)} custom-call(s32[4]{0:T(128)S(1)} %copy-done.49, bf16[1024,2048]{1,0:T(8,128)(2,1)S(1)} %bitcast.97, bf16[1024,2048]{1,0:T(8,128)(2,1)S(1)} %bitcast.112, bf16[1024,1536]{1,0:T(8,128)(2,1)S(1)} %bitcast.108, bf16[1024,1536]{1,0:T(8,128)(2,1)S(1)} %bitcast.109, bf16[1024,512]{1,0:T(8,128)(2,1)S(1)} %bitcast.121), custom_call_target="tpu_custom_call" | custom-call | flops 1000000 | bytes 1000000 | tf_op jit(solution)/shard_map/attn_grads/pallas_call | solution.py:456
  466.9 8.1 %attn_grads.3 = bf16[2048,1024]{1,0:T(8,128)(2,1)S(1)} custom-call(s32[4]{0:T(128)S(1)} %copy-done.49, bf16[1024,2048]{1,0:T(8,128)(2,1)S(1)} %bitcast.98, bf16[1024,2048]{1,0:T(8,128)(2,1)S(1)} %bitcast.113, bf16[1024,1536]{1,0:T(8,128)(2,1)S(1)} %bitcast.110, bf16[1024,1536]{1,0:T(8,128)(2,1)S(1)} %bitcast.111, bf16[1024,512]{1,0:T(8,128)(2,1)S(1)} %bitcast.122, ...), custom_call_target="tpu_custom_call" | custom-call | flops 1000000 | bytes 1000000 | tf_op jit(solution)/shard_map/attn_grads/pallas_call | solution.py:456
  477.0 4.6 convolution_convert_fusion.4
  488.0 4.6 convolution_convert_fusion.3
  513.5 4.4 collective-permute-start.34
  524.7 14.6 %collective-permute-done.34.moved_ref = bf16[256,2048]{1,0:T(8,128)(2,1)S(1)} collective-permute-done((bf16[256,2048]{1,0:T(8,128)(2,1)S(1)}, bf16[256,2048]{1,0:T(8,128)(2,1)S(1)}, u32[]{:S(2)}, u32[]{:S(2)}) %collective-permute-start.34) | collective-permute-done | bytes 1048608 | tf_op jit(solution)/shard_map/ppermute | solution.py:568
  (309 shorter events, 167.4 us)
Async XLA Ops:
  7.2 469.8 %reduce-scatter.3.cloned.1.call-start = ((), (), s32[]{:S(2)}) async-start(), calls=%async_computation.2 | async-start | bytes 10485760 | tf_op jit(solution)/shard_map/reduce_scatter | solution.py:681
  8.5 17.4 %collective-permute-start = (bf16[256,1024]{1,0:T(8,128)(2,1)S(1)}, bf16[256,1024]{1,0:T(8,128)(2,1)}, u32[]{:S(2)}, u32[]{:S(2)}) collective-permute-start(bf16[256,1024]{1,0:T(8,128)(2,1)S(1)} %get-tuple-element.281.xa_ref), channel_id=1, source_target_pairs={{0,3},{1,0},{2,1},{3,2},{4,7},{5,4},{6,5},{7,6},{8,11},{9,8},{10,9... | collective-permute-start | bytes 1572872 | tf_op jit(solution)/shard_map/ppermute | solution.py:568
  13.6 23.6 %collective-permute-start.2 = (bf16[256,1024]{1,0:T(8,128)(2,1)S(1)}, bf16[256,1024]{1,0:T(8,128)(2,1)S(1)}, u32[]{:S(2)}, u32[]{:S(2)}) collective-permute-start(bf16[256,1024]{1,0:T(8,128)(2,1)S(1)} %get-tuple-element.280.xb_ref), channel_id=1, source_target_pairs={{0,3},{1,0},{2,1},{3,2},{4,7},{5,4},{6,5},{7,6},{8,11},{9,8},{10,9... | collective-permute-start | bytes 1572872 | tf_op jit(solution)/shard_map/ppermute | solution.py:568
  26.0 22.7 %collective-permute-start.1 = (bf16[256,1024]{1,0:T(8,128)(2,1)}, bf16[256,1024]{1,0:T(8,128)(2,1)S(1)}, u32[]{:S(2)}, u32[]{:S(2)}) collective-permute-start(bf16[256,1024]{1,0:T(8,128)(2,1)} %collective-permute-done.xa_ref), channel_id=1, source_target_pairs={{0,3},{1,0},{2,1},{3,2},{4,7},{5,4},{6,5},{7,6},{8,11},{9,8},{10,9... | collective-permute-start | bytes 1572872 | tf_op jit(solution)/shard_map/ppermute | solution.py:568
  37.2 22.5 %collective-permute-start.4 = (bf16[256,1024]{1,0:T(8,128)(2,1)S(1)}, bf16[256,1024]{1,0:T(8,128)(2,1)}, u32[]{:S(2)}, u32[]{:S(2)}) collective-permute-start(bf16[256,1024]{1,0:T(8,128)(2,1)S(1)} %collective-permute-done.2.xb_ref), channel_id=1, source_target_pairs={{0,3},{1,0},{2,1},{3,2},{4,7},{5,4},{6,5},{7,6},{8,11},{9,8},{10,9... | collective-permute-start | bytes 1572872 | tf_op jit(solution)/shard_map/ppermute | solution.py:568
  48.6 27.5 %copy-start.51 = (s32[1,1024]{1,0:T(1,128)S(1)}, s32[1,1024]{1,0:T(1,128)}, u32[]{:S(2)}) copy-start(s32[1,1024]{1,0:T(1,128)} %param.19) | copy-start | bytes 12292
  48.6 28.5 %copy-start.75 = (s32[1,1024]{1,0:T(1,128)S(1)}, s32[1,1024]{1,0:T(1,128)}, u32[]{:S(2)}) copy-start(s32[1,1024]{1,0:T(1,128)} %param.20) | copy-start | bytes 12292
  48.7 22.5 %collective-permute-start.3 = (bf16[256,1024]{1,0:T(8,128)(2,1)S(1)}, bf16[256,1024]{1,0:T(8,128)(2,1)S(1)}, u32[]{:S(2)}, u32[]{:S(2)}) collective-permute-start(bf16[256,1024]{1,0:T(8,128)(2,1)S(1)} %collective-permute-done.1.xa_ref), channel_id=1, source_target_pairs={{0,3},{1,0},{2,1},{3,2},{4,7},{5,4},{6,5},{7,6},{8,11},{9,8},{10,9... | collective-permute-start | bytes 1572872 | tf_op jit(solution)/shard_map/ppermute | solution.py:568
  59.7 22.7 %collective-permute-start.5 = (bf16[256,1024]{1,0:T(8,128)(2,1)}, bf16[256,1024]{1,0:T(8,128)(2,1)}, u32[]{:S(2)}, u32[]{:S(2)}) collective-permute-start(bf16[256,1024]{1,0:T(8,128)(2,1)} %collective-permute-done.4.xb_ref), channel_id=1, source_target_pairs={{0,3},{1,0},{2,1},{3,2},{4,7},{5,4},{6,5},{7,6},{8,11},{9,8},{10,9... | collective-permute-start | bytes 1572872 | tf_op jit(solution)/shard_map/ppermute | solution.py:568
  72.0 32.2 %collective-permute-start.6 = (bf16[256,2048]{1,0:T(8,128)(2,1)S(1)}, bf16[256,2048]{1,0:T(8,128)(2,1)S(1)}, u32[]{:S(2)}, u32[]{:S(2)}) collective-permute-start(bf16[256,2048]{1,0:T(8,128)(2,1)S(1)} %bitcast.114), channel_id=1, source_target_pairs={{0,1},{1,2},{2,3},{4,5},{5,6},{6,7},{8,9},{9,10},{10,11},{12,13},{... | collective-permute-start | bytes 3145736 | tf_op jit(solution)/shard_map/ppermute | solution.py:568
  74.1 34.6 %collective-permute-start.10 = (bf16[256,2048]{1,0:T(8,128)(2,1)S(1)}, bf16[256,2048]{1,0:T(8,128)(2,1)}, u32[]{:S(2)}, u32[]{:S(2)}) collective-permute-start(bf16[256,2048]{1,0:T(8,128)(2,1)S(1)} %bitcast.115), channel_id=1, source_target_pairs={{1,0},{2,1},{3,2},{5,4},{6,5},{7,6},{9,8},{10,9},{11,10},{13,12},{... | collective-permute-start | bytes 3145736 | tf_op jit(solution)/shard_map/ppermute | solution.py:568
  104.2 60.2 %copy-start.3 = (bf16[1024,2048]{1,0:T(8,128)(2,1)}, bf16[1024,2048]{1,0:T(8,128)(2,1)S(1)}, u32[]{:S(2)}) copy-start(bf16[1024,2048]{1,0:T(8,128)(2,1)S(1)} %convolution_convert_fusion.1) | copy-start | bytes 12582916
  105.1 25.1 %collective-permute-start.7 = (bf16[256,2048]{1,0:T(8,128)(2,1)S(1)}, bf16[256,2048]{1,0:T(8,128)(2,1)S(1)}, u32[]{:S(2)}, u32[]{:S(2)}) collective-permute-start(bf16[256,2048]{1,0:T(8,128)(2,1)S(1)} %join.12), channel_id=1, source_target_pairs={{0,1},{1,2},{2,3},{4,5},{5,6},{6,7},{8,9},{9,10},{10,11},{12,13},{... | collective-permute-start | bytes 3145736 | tf_op jit(solution)/shard_map/ppermute | solution.py:568
  110.5 26.3 %collective-permute-start.11 = (bf16[256,2048]{1,0:T(8,128)(2,1)S(1)}, bf16[256,2048]{1,0:T(8,128)(2,1)S(1)}, u32[]{:S(2)}, u32[]{:S(2)}) collective-permute-start(bf16[256,2048]{1,0:T(8,128)(2,1)S(1)} %join.15), channel_id=1, source_target_pairs={{1,0},{2,1},{3,2},{5,4},{6,5},{7,6},{9,8},{10,9},{11,10},{13,12},{... | collective-permute-start | bytes 3145736 | tf_op jit(solution)/shard_map/ppermute | solution.py:568
  131.2 26.1 %collective-permute-start.8 = (bf16[256,2048]{1,0:T(8,128)(2,1)S(1)}, bf16[256,2048]{1,0:T(8,128)(2,1)S(1)}, u32[]{:S(2)}, u32[]{:S(2)}) collective-permute-start(bf16[256,2048]{1,0:T(8,128)(2,1)S(1)} %join.13), channel_id=1, source_target_pairs={{0,1},{1,2},{2,3},{4,5},{5,6},{6,7},{8,9},{9,10},{10,11},{12,13},{... | collective-permute-start | bytes 3145736 | tf_op jit(solution)/shard_map/ppermute | solution.py:568
  137.8 26.6 %collective-permute-start.12 = (bf16[256,2048]{1,0:T(8,128)(2,1)S(1)}, bf16[256,2048]{1,0:T(8,128)(2,1)S(1)}, u32[]{:S(2)}, u32[]{:S(2)}) collective-permute-start(bf16[256,2048]{1,0:T(8,128)(2,1)S(1)} %join.16), channel_id=1, source_target_pairs={{1,0},{2,1},{3,2},{5,4},{6,5},{7,6},{9,8},{10,9},{11,10},{13,12},{... | collective-permute-start | bytes 3145736 | tf_op jit(solution)/shard_map/ppermute | solution.py:568
  158.9 25.6 %collective-permute-start.9 = (bf16[256,2048]{1,0:T(8,128)(2,1)}, bf16[256,2048]{1,0:T(8,128)(2,1)}, u32[]{:S(2)}, u32[]{:S(2)}) collective-permute-start(bf16[256,2048]{1,0:T(8,128)(2,1)} %join.14), channel_id=1, source_target_pairs={{0,1},{1,2},{2,3},{4,5},{5,6},{6,7},{8,9},{9,10},{10,11},{12,13},{... | collective-permute-start | bytes 3145736 | tf_op jit(solution)/shard_map/ppermute | solution.py:568
  166.0 25.2 %collective-permute-start.13 = (bf16[256,2048]{1,0:T(8,128)(2,1)}, bf16[256,2048]{1,0:T(8,128)(2,1)}, u32[]{:S(2)}, u32[]{:S(2)}) collective-permute-start(bf16[256,2048]{1,0:T(8,128)(2,1)} %join.17), channel_id=1, source_target_pairs={{1,0},{2,1},{3,2},{5,4},{6,5},{7,6},{9,8},{10,9},{11,10},{13,12},{... | collective-permute-start | bytes 3145736 | tf_op jit(solution)/shard_map/ppermute | solution.py:568
  195.6 23.8 %collective-permute-start.14 = (bf16[256,2048]{1,0:T(8,128)(2,1)S(1)}, bf16[256,2048]{1,0:T(8,128)(2,1)S(1)}, u32[]{:S(2)}, u32[]{:S(2)}) collective-permute-start(bf16[256,2048]{1,0:T(8,128)(2,1)S(1)} %add_convert_fusion.5.a_ref), channel_id=1, source_target_pairs={{0,3},{1,0},{2,1},{3,2},{4,7},{5,4},{6,5},{7,6},{8,11},{9,8},{10,9... | collective-permute-start | bytes 3145736 | tf_op jit(solution)/shard_map/ppermute | solution.py:568
  219.4 24.4 %collective-permute-start.15 = (bf16[256,2048]{1,0:T(8,128)(2,1)S(1)}, bf16[256,2048]{1,0:T(8,128)(2,1)S(1)}, u32[]{:S(2)}, u32[]{:S(2)}) collective-permute-start(bf16[256,2048]{1,0:T(8,128)(2,1)S(1)} %collective-permute-done.14.a_ref), channel_id=1, source_target_pairs={{0,3},{1,0},{2,1},{3,2},{4,7},{5,4},{6,5},{7,6},{8,11},{9,8},{10,9... | collective-permute-start | bytes 3145736 | tf_op jit(solution)/shard_map/ppermute | solution.py:568
  238.8 27.5 %collective-permute-start.17 = (bf16[256,2048]{1,0:T(8,128)(2,1)}, bf16[256,2048]{1,0:T(8,128)(2,1)S(1)}, u32[]{:S(2)}, u32[]{:S(2)}) collective-permute-start(bf16[256,2048]{1,0:T(8,128)(2,1)} %convolution_convert_fusion.6), channel_id=1, source_target_pairs={{0,3},{1,0},{2,1},{3,2},{4,7},{5,4},{6,5},{7,6},{8,11},{9,8},{10,9... | collective-permute-start | bytes 3145736 | tf_op jit(solution)/shard_map/ppermute | solution.py:568
  243.8 44.9 %collective-permute-start.16 = (bf16[256,2048]{1,0:T(8,128)(2,1)S(1)}, bf16[256,2048]{1,0:T(8,128)(2,1)S(1)}, u32[]{:S(2)}, u32[]{:S(2)}) collective-permute-start(bf16[256,2048]{1,0:T(8,128)(2,1)S(1)} %collective-permute-done.15.a_ref), channel_id=1, source_target_pairs={{0,3},{1,0},{2,1},{3,2},{4,7},{5,4},{6,5},{7,6},{8,11},{9,8},{10,9... | collective-permute-start | bytes 3145736 | tf_op jit(solution)/shard_map/ppermute | solution.py:568
  267.5 40.5 %collective-permute-start.18 = (bf16[256,2048]{1,0:T(8,128)(2,1)}, bf16[256,2048]{1,0:T(8,128)(2,1)S(1)}, u32[]{:S(2)}, u32[]{:S(2)}) collective-permute-start(bf16[256,2048]{1,0:T(8,128)(2,1)} %add_convert_fusion.4), channel_id=1, source_target_pairs={{0,3},{1,0},{2,1},{3,2},{4,7},{5,4},{6,5},{7,6},{8,11},{9,8},{10,9... | collective-permute-start | bytes 3145736 | tf_op jit(solution)/shard_map/ppermute | solution.py:568
  308.4 22.1 %collective-permute-start.19 = (bf16[256,2048]{1,0:T(8,128)(2,1)S(1)}, bf16[256,2048]{1,0:T(8,128)(2,1)S(1)}, u32[]{:S(2)}, u32[]{:S(2)}) collective-permute-start(bf16[256,2048]{1,0:T(8,128)(2,1)S(1)} %add_convert_fusion.3), channel_id=1, source_target_pairs={{0,3},{1,0},{2,1},{3,2},{4,7},{5,4},{6,5},{7,6},{8,11},{9,8},{10,9... | collective-permute-start | bytes 3145736 | tf_op jit(solution)/shard_map/ppermute | solution.py:568
  317.2 33.9 %collective-permute-start.21 = (bf16[2048,1024]{1,0:T(8,128)(2,1)S(1)}, bf16[2048,1024]{1,0:T(8,128)(2,1)}, u32[]{:S(2)}, u32[]{:S(2)}) collective-permute-start(bf16[2048,1024]{1,0:T(8,128)(2,1)S(1)} %grad_half.4), channel_id=1, source_target_pairs={{0,4},{4,0},{8,12},{12,8},{16,20},{20,16},{24,28},{28,24},{1,5},{5... | collective-permute-start | bytes 12582920 | tf_op jit(solution)/shard_map/ppermute | solution.py:589
  324.5 45.1 %collective-permute-start.24 = (bf16[2048,1024]{1,0:T(8,128)(2,1)}, bf16[2048,1024]{1,0:T(8,128)(2,1)}, u32[]{:S(2)}, u32[]{:S(2)}) collective-permute-start(bf16[2048,1024]{1,0:T(8,128)(2,1)} %grad_half.5), channel_id=1, source_target_pairs={{0,4},{4,0},{8,12},{12,8},{16,20},{20,16},{24,28},{28,24},{1,5},{5... | collective-permute-start | bytes 12582920 | tf_op jit(solution)/shard_map/ppermute | solution.py:589
  334.6 24.6 %collective-permute-start.20 = (bf16[256,2048]{1,0:T(8,128)(2,1)S(1)}, bf16[256,2048]{1,0:T(8,128)(2,1)S(1)}, u32[]{:S(2)}, u32[]{:S(2)}) collective-permute-start(bf16[256,2048]{1,0:T(8,128)(2,1)S(1)} %get-tuple-element.218.refs_0_), channel_id=1, source_target_pairs={{0,1},{1,2},{2,3},{4,5},{5,6},{6,7},{8,9},{9,10},{10,11},{12,13},{... | collective-permute-start | bytes 3145736 | tf_op jit(solution)/shard_map/ppermute | solution.py:568
  338.1 22.1 %collective-permute-start.23 = (bf16[256,2048]{1,0:T(8,128)(2,1)S(1)}, bf16[256,2048]{1,0:T(8,128)(2,1)S(1)}, u32[]{:S(2)}, u32[]{:S(2)}) collective-permute-start(bf16[256,2048]{1,0:T(8,128)(2,1)S(1)} %get-tuple-element.218.refs_0_), channel_id=1, source_target_pairs={{1,0},{2,1},{3,2},{5,4},{6,5},{7,6},{9,8},{10,9},{11,10},{13,12},{... | collective-permute-start | bytes 3145736 | tf_op jit(solution)/shard_map/ppermute | solution.py:568
  362.0 21.4 %collective-permute-start.22 = (bf16[256,2048]{1,0:T(8,128)(2,1)}, bf16[256,2048]{1,0:T(8,128)(2,1)}, u32[]{:S(2)}, u32[]{:S(2)}) collective-permute-start(bf16[256,2048]{1,0:T(8,128)(2,1)} %join.18), channel_id=1, source_target_pairs={{0,1},{1,2},{2,3},{4,5},{5,6},{6,7},{8,9},{9,10},{10,11},{12,13},{... | collective-permute-start | bytes 3145736 | tf_op jit(solution)/shard_map/ppermute | solution.py:568
  368.3 21.7 %collective-permute-start.27 = (bf16[256,2048]{1,0:T(8,128)(2,1)}, bf16[256,2048]{1,0:T(8,128)(2,1)}, u32[]{:S(2)}, u32[]{:S(2)}) collective-permute-start(bf16[256,2048]{1,0:T(8,128)(2,1)} %join.19), channel_id=1, source_target_pairs={{1,0},{2,1},{3,2},{5,4},{6,5},{7,6},{9,8},{10,9},{11,10},{13,12},{... | collective-permute-start | bytes 3145736 | tf_op jit(solution)/shard_map/ppermute | solution.py:568
  380.2 161.9 %reduce-scatter.5.cloned.1.call-start = ((), (), s32[]{:S(2)}) async-start(), calls=%async_computation.3 | async-start | bytes 5242880 | tf_op jit(solution)/shard_map/reduce_scatter | solution.py:709
  394.1 21.1 %collective-permute-start.25 = (bf16[256,2048]{1,0:T(8,128)(2,1)S(1)}, bf16[256,2048]{1,0:T(8,128)(2,1)S(1)}, u32[]{:S(2)}, u32[]{:S(2)}) collective-permute-start(bf16[256,2048]{1,0:T(8,128)(2,1)S(1)} %join.20), channel_id=1, source_target_pairs={{0,1},{1,2},{2,3},{4,5},{5,6},{6,7},{8,9},{9,10},{10,11},{12,13},{... | collective-permute-start | bytes 3145736 | tf_op jit(solution)/shard_map/ppermute | solution.py:568
  399.3 22.0 %collective-permute-start.28 = (bf16[256,2048]{1,0:T(8,128)(2,1)S(1)}, bf16[256,2048]{1,0:T(8,128)(2,1)S(1)}, u32[]{:S(2)}, u32[]{:S(2)}) collective-permute-start(bf16[256,2048]{1,0:T(8,128)(2,1)S(1)} %join.22), channel_id=1, source_target_pairs={{1,0},{2,1},{3,2},{5,4},{6,5},{7,6},{9,8},{10,9},{11,10},{13,12},{... | collective-permute-start | bytes 3145736 | tf_op jit(solution)/shard_map/ppermute | solution.py:568
  416.1 24.6 %collective-permute-start.26 = (bf16[256,2048]{1,0:T(8,128)(2,1)S(1)}, bf16[256,2048]{1,0:T(8,128)(2,1)S(1)}, u32[]{:S(2)}, u32[]{:S(2)}) collective-permute-start(bf16[256,2048]{1,0:T(8,128)(2,1)S(1)} %join.21), channel_id=1, source_target_pairs={{0,1},{1,2},{2,3},{4,5},{5,6},{6,7},{8,9},{9,10},{10,11},{12,13},{... | collective-permute-start | bytes 3145736 | tf_op jit(solution)/shard_map/ppermute | solution.py:568
  421.9 19.7 %collective-permute-start.29 = (bf16[256,2048]{1,0:T(8,128)(2,1)S(1)}, bf16[256,2048]{1,0:T(8,128)(2,1)S(1)}, u32[]{:S(2)}, u32[]{:S(2)}) collective-permute-start(bf16[256,2048]{1,0:T(8,128)(2,1)S(1)} %join.23), channel_id=1, source_target_pairs={{1,0},{2,1},{3,2},{5,4},{6,5},{7,6},{9,8},{10,9},{11,10},{13,12},{... | collective-permute-start | bytes 3145736 | tf_op jit(solution)/shard_map/ppermute | solution.py:568
  453.7 7.5 %collective-permute-start.30 = (bf16[2048,1024]{1,0:T(8,128)(2,1)}, bf16[2048,1024]{1,0:T(8,128)(2,1)}, u32[]{:S(2)}, u32[]{:S(2)}) collective-permute-start(bf16[2048,1024]{1,0:T(8,128)(2,1)} %attn_grads.2), channel_id=1, source_target_pairs={{0,4},{4,0},{8,12},{12,8},{16,20},{20,16},{24,28},{28,24},{1,5},{5... | collective-permute-start | bytes 12582920 | tf_op jit(solution)/shard_map/ppermute | solution.py:589
  453.9 27.7 %collective-permute-start.31 = (bf16[256,2048]{1,0:T(8,128)(2,1)}, bf16[256,2048]{1,0:T(8,128)(2,1)}, u32[]{:S(2)}, u32[]{:S(2)}) collective-permute-start(bf16[256,2048]{1,0:T(8,128)(2,1)} %convolution_convert_fusion.5), channel_id=1, source_target_pairs={{0,3},{1,0},{2,1},{3,2},{4,7},{5,4},{6,5},{7,6},{8,11},{9,8},{10,9... | collective-permute-start | bytes 3145736 | tf_op jit(solution)/shard_map/ppermute | solution.py:568
  484.4 27.5 %collective-permute-start.32 = (bf16[256,2048]{1,0:T(8,128)(2,1)}, bf16[256,2048]{1,0:T(8,128)(2,1)}, u32[]{:S(2)}, u32[]{:S(2)}) collective-permute-start(bf16[256,2048]{1,0:T(8,128)(2,1)} %add_convert_fusion.1), channel_id=1, source_target_pairs={{0,3},{1,0},{2,1},{3,2},{4,7},{5,4},{6,5},{7,6},{8,11},{9,8},{10,9... | collective-permute-start | bytes 3145736 | tf_op jit(solution)/shard_map/ppermute | solution.py:568
  496.0 11.7 %collective-permute-start.33 = (bf16[2,256,1024]{2,1,0:T(8,128)(2,1)}, bf16[2,256,1024]{2,1,0:T(8,128)(2,1)S(1)}, u32[]{:S(2)}, u32[]{:S(2)}) collective-permute-start(bf16[2,256,1024]{2,1,0:T(8,128)(2,1)} %constant_dynamic-slice_fusion.1), channel_id=1, source_target_pairs={{0,4},{4,0},{8,12},{12,8},{16,20},{20,16},{24,28},{28,24},{1,5},{5... | collective-permute-start | bytes 3145736 | tf_op jit(solution)/shard_map/ppermute | solution.py:589
  500.1 3.7 collective-permute-start.35
  503.8 14.1 %collective-permute-start.36 = (f32[8320]{0:T(1024)S(1)}, f32[8320]{0:T(1024)S(1)}, u32[]{:S(2)}, u32[]{:S(2)}) collective-permute-start(f32[8320]{0:T(1024)S(1)} %add.145), channel_id=1, source_target_pairs={{0,1},{1,2},{2,3},{3,0},{4,5},{5,6},{6,7},{7,4},{8,9},{9,10},{10,1... | collective-permute-start | bytes 99848 | tf_op jit(solution)/shard_map/ppermute | solution.py:568
  503.9 14.1 %collective-permute-start.37 = (f32[8320]{0:T(1024)S(1)}, f32[8320]{0:T(1024)S(1)}, u32[]{:S(2)}, u32[]{:S(2)}) collective-permute-start(f32[8320]{0:T(1024)S(1)} %add.145), channel_id=1, source_target_pairs={{0,2},{1,3},{2,0},{3,1},{4,6},{5,7},{6,4},{7,5},{8,10},{9,11},{10,... | collective-permute-start | bytes 99848 | tf_op jit(solution)/shard_map/ppermute | solution.py:568
  505.7 12.3 %collective-permute-start.38 = (f32[8320]{0:T(1024)S(1)}, f32[8320]{0:T(1024)S(1)}, u32[]{:S(2)}, u32[]{:S(2)}) collective-permute-start(f32[8320]{0:T(1024)S(1)} %add.145), channel_id=1, source_target_pairs={{0,3},{1,0},{2,1},{3,2},{4,7},{5,4},{6,5},{7,6},{8,11},{9,8},{10,9... | collective-permute-start | bytes 99848 | tf_op jit(solution)/shard_map/ppermute | solution.py:568
  513.5 25.7 %collective-permute-start.34 = (bf16[256,2048]{1,0:T(8,128)(2,1)S(1)}, bf16[256,2048]{1,0:T(8,128)(2,1)S(1)}, u32[]{:S(2)}, u32[]{:S(2)}) collective-permute-start(bf16[256,2048]{1,0:T(8,128)(2,1)S(1)} %add_convert_fusion), channel_id=1, source_target_pairs={{0,3},{1,0},{2,1},{3,2},{4,7},{5,4},{6,5},{7,6},{8,11},{9,8},{10,9... | collective-permute-start | bytes 3145736 | tf_op jit(solution)/shard_map/ppermute | solution.py:568
  518.0 24.1 %collective-permute-start.39 = (f32[8320]{0:T(1024)S(1)}, f32[8320]{0:T(1024)S(1)}, u32[]{:S(2)}, u32[]{:S(2)}) collective-permute-start(f32[8320]{0:T(1024)S(1)} %add_add_fusion.2), channel_id=1, source_target_pairs={{0,8},{4,12},{8,16},{12,20},{16,24},{20,28},{24,0},{28,4},{1,9},{5... | collective-permute-start | bytes 99848 | tf_op jit(solution)/shard_map/ppermute | solution.py:756
  519.5 22.6 %collective-permute-start.40 = (f32[8320]{0:T(1024)S(1)}, f32[8320]{0:T(1024)S(1)}, u32[]{:S(2)}, u32[]{:S(2)}) collective-permute-start(f32[8320]{0:T(1024)S(1)} %add_add_fusion.2), channel_id=1, source_target_pairs={{0,16},{4,20},{8,24},{12,28},{16,0},{20,4},{24,8},{28,12},{1,17},{... | collective-permute-start | bytes 99848 | tf_op jit(solution)/shard_map/ppermute | solution.py:756
  521.1 21.0 %collective-permute-start.41 = (f32[8320]{0:T(1024)S(1)}, f32[8320]{0:T(1024)S(1)}, u32[]{:S(2)}, u32[]{:S(2)}) collective-permute-start(f32[8320]{0:T(1024)S(1)} %add_add_fusion.2), channel_id=1, source_target_pairs={{0,24},{4,28},{8,0},{12,4},{16,8},{20,12},{24,16},{28,20},{1,25},{... | collective-permute-start | bytes 99848 | tf_op jit(solution)/shard_map/ppermute | solution.py:756
  543.2 2.0 collective-permute-start.42
  (81 other events, 626.1 us)
Sparse Core Ops, SparseCore 0:
  380.3 88.8 reduce-scatter.2
  477.2 55.2 reduce-scatter.4

commit v6 on v5

--- a/solution.py
+++ b/solution.py
@@ -175,7 +175,7 @@
             out_specs=spec,
         ),
         out_shape=jax.ShapeDtypeStruct((n, rows, local), BF16),
-        compiler_params=params(16),
+        compiler_params=params(62),
         cost_estimate=cost(4 * t * t * local, 8 * t * local, t * t * local // E),
         name="attend",
     )(rank, q, k, v, docs_col, docs_row, heads_col)
@@ -259,7 +259,7 @@
         ),
         out_shape=jax.ShapeDtypeStruct((n, rows, 3 * local), BF16),
         compiler_params=params(24),
-        cost_estimate=cost(108e9, 14 * t * local),
+        cost_estimate=cost(116e9, 14 * t * local),
         name="attend_back",
     )(rank, q, k, v, do, docs_col, docs_row, heads_col, cos, sin)
 
@@ -417,7 +417,7 @@
         ),
         out_shape=jax.ShapeDtypeStruct(oshape, BF16),
         input_output_aliases=aliases,
-        compiler_params=params(28),
+        compiler_params=params(20),
         cost_estimate=cost(1e6, 1e6),
         name="grad_half",
     )(rank, *args)
@@ -469,10 +469,38 @@
             out_specs=out,
         ),
         out_shape=jax.ShapeDtypeStruct((d, 2 * local), BF16),
-        compiler_params=params(28),
-        cost_estimate=cost(1e6, 1e6),
+        compiler_params=params(62),
+        cost_estimate=cost(4e9 if partner else 1e6, 1e6),
         name="attn_grads",
     )(rank, act, states, dqkv, dqkv, om, *([] if partner else [moved]))
+
+
+def term_body(x_ref, w_ref, *rest):
+    out = dot_t(x_ref[0], w_ref[...])
+    if len(rest) > 1:
+        out = out + rest[0][...].astype(F32)
+    rest[-1][...] = out.astype(BF16)
+
+
+def block_term(acts, slot, weight, flops, moved=None):
+    _, rows, k = acts.shape
+    d = weight.shape[0]
+    tile = min(512, d)
+    out = pl.BlockSpec((rows, tile), lambda j: (0, j))
+    return pl.pallas_call(
+        term_body,
+        grid=(d // tile,),
+        in_specs=[
+            pl.BlockSpec((1, rows, k), lambda j: (slot, 0, 0)),
+            pl.BlockSpec((tile, k), lambda j: (j, 0)),
+        ]
+        + ([] if moved is None else [out]),
+        out_specs=out,
+        out_shape=jax.ShapeDtypeStruct((rows, d), BF16),
+        compiler_params=params(16),
+        cost_estimate=cost(flops, flops / 256),
+        name="block_term",
+    )(acts, weight, *([] if moved is None else [moved]))
 
 
 def join_body(slot, first, rank_ref, moved_ref, term_ref, out_ref):
@@ -501,7 +529,7 @@
         ),
         out_shape=jax.ShapeDtypeStruct((rows, d), BF16),
         compiler_params=params(8),
-        cost_estimate=cost(rows * d, 6 * rows * d),
+        cost_estimate=cost(1e6, 1e6),
         name="join",
     )(rank, moved, terms)
 
@@ -524,7 +552,7 @@
         out_specs=row(d),
         out_shape=jax.ShapeDtypeStruct((rows, d), BF16),
         compiler_params=params(12),
-        cost_estimate=cost(22e9, 12 * rows * d),
+        cost_estimate=cost(30e9, 12 * rows * d),
         name="last_step",
     )(x, gain, term, moved, state)
 
@@ -632,21 +660,19 @@
     (block,) = tie([low(second_out)], weights)
     for s in range(n):
         if s >= 1:
-            block, *held = tie([block] + list(held) + ([term0] if s == n - 1 else []))
-            if s == n - 1:
-                term0, held = held[-1], held[:-1]
+            block, *held = tie([block] + list(held), sent)
         after = hop(block) if s < n - 1 else None
         held = mlp_slot(
             s, n, where, block, [grads_l[s], grads_r[n - s if s else 0]], up_weight, down_weight, bucket_col, held
         )
         if s >= 1:
-            term = dot_t(held[1][s], up_weight)
-            if s > 1:
-                (term,) = tie([term])
-            sent = low(term) if moved is None else add(term, moved)
+            fused = moved if s == n - 1 and s > 1 else None
+            sent = block_term(held[1], s, up_weight, 2 * rows * d * hidden, fused)
+            if s > 1 and fused is None:
+                sent = add(sent, moved)
             moved = hop(sent)
         else:
-            term0 = dot_t(held[1][0], up_weight)
+            sent = term0 = block_term(held[1], 0, up_weight, 2 * rows * d * hidden)
         block = after
     active, grad_upper, second_all, grad_all = held
     grad_all, active, second_all, grad_upper = tie([grad_all, active, second_all, grad_upper], sent)
@@ -656,7 +682,7 @@
     ]
     (moved,) = tie([moved], *gifts)
     down_gift, up_gift = (swap(v) for v in gifts)
-    grad_second = term0 + moved.astype(F32)
+    grad_second = term0.astype(F32) + moved.astype(F32)
     back_two = norm_backward(grad_second, normed_two, inverse_two, gain2)
     second_gain_part = jnp.sum(grad_second * normed_two, axis=0)
     second_shift_part = jnp.sum(grad_second, axis=0)
@@ -699,24 +725,24 @@
         return jnp.where(side == 0, mine, got).astype(F32), jnp.where(side == 0, got, mine).astype(F32)
 
     tokens_of = lambda v: (flat(first_all), flat(state_all), flat(v), flat(masked), where)
-    sent = low(dot_t(dqkv[1], weights))
+    sent = block_term(dqkv, 1, weights, 1e6)
     (dqkv,) = tie([dqkv], sent)
     moved = hop(sent)
     gift = attn_grads(*tokens_of(dqkv))
     (dqkv,) = tie([dqkv], gift)
+    terms = {1: sent, 2: block_term(dqkv, 2, weights, 1e6)}
+    (dqkv,) = tie([dqkv], terms[2])
     attn_term = attn_grads(*tokens_of(dqkv), swap(gift))
     (late,) = tie([attn_term], wide_grad)
     attn_grad = lax.psum_scatter(late, "dp", scatter_dimension=0, axis_index_groups=sides, tiled=True)
-    terms = {1: sent}
-    for s in range(2, n):
-        (dqkv,) = tie([dqkv], attn_term)
-        terms[s] = low(dot_t(dqkv[s], weights))
-        (dqkv,) = tie([dqkv], terms[s])
-        if s == 2:
-            sent2 = sent = add(terms[2], moved)
-            moved = hop(sent)
-            (dqkv,) = tie([dqkv], sent)
-    terms[0] = low(dot_t(dqkv[0], weights))
+    (moved,) = tie([moved], attn_term)
+    sent2 = sent = add(terms[2], moved)
+    moved = hop(sent)
+    for s in range(3, n):
+        (dqkv,) = tie([dqkv], sent)
+        terms[s] = block_term(dqkv, s, weights, 1e6)
+    (dqkv,) = tie([dqkv], terms[n - 1])
+    terms[0] = block_term(dqkv, 0, weights, 1e6)
     held = tie([terms[s] for s in range(n)], sent2)
     sum_d = sum(jnp.sum(v.astype(F32), axis=0) for v in held)
     sum_da = sum(jnp.sum(v.astype(F32) * first_all[s].astype(F32), axis=0) for s, v in enumerate(held))

time: 564 us -> 559 us (level)
  matrix products: 56 us -> 15.6 us
  Pallas kernels: 160 us -> 192 us
    dot_general x10 -> x2, matrix products: 56 us -> 15.6 us  [dot_t(): lax.dot_general(left, right, (((1,), (1,)), ((), ())), preferred_element_...]
    pallas_call x0 -> x8, Pallas kernels: none -> 23.7 us  [block_term(): pl.pallas_call(term_body, grid=(d // tile,), in_specs=[pl.BlockSpec((1, r...]
    pallas_call x2, Pallas kernels: 16.5 us -> 22.5 us  [attn_grads(): pl.pallas_call(functools.partial(attn_grad_body, partner), grid_spec=pltp...]
    unnamed x171 -> x167, local copies, waits for them, and re-layouts: 29.1 us -> 29.6 us
  transfers between devices with their start and end apart: 45 -> 45, of which waited for: 24 -> 24; matrix products, arithmetic and copies ran while one was open for 16% -> 9% of each run, Pallas kernels for 29% -> 34%
where the time goes in v6:
time: 559 us; the launch traced here: 550 us
  Pallas kernels  192 us (34%)
  waiting for transfers between devices  158 us (28%)
  starting transfers between devices  100 us (18%)
  local copies, waits for them, and re-layouts  40.9 us (7%)
  other arithmetic  26.9 us (5%)
  between operations  15.8 us (3%)
  matrix products  15.6 us (3%)
    ppermute x34, waiting for transfers between devices, per_device(): send = lambda v, pairs: lax.ppermute(v, 'mp', pairs)  158 us
    ppermute x34, starting transfers between devices, per_device(): send = lambda v, pairs: lax.ppermute(v, 'mp', pairs)  95 us
    pallas_call x4, Pallas kernels, mlp_slot(): pl.pallas_call(functools.partial(mlp_body, slot, n), grid_spec=pltpu.Pref...  38.9 us
    pallas_call x4, Pallas kernels, grad_half(): pl.pallas_call(functools.partial(grad_body, not partner), grid_spec=pltpu...  29.6 us
    unnamed x167, local copies, waits for them, and re-layouts  29.6 us
    pallas_call x4, Pallas kernels, qkv_slot(): pl.pallas_call(qkv_body, grid_spec=pltpu.PrefetchScalarGridSpec(num_scala...  28.5 us
    pallas_call x8, Pallas kernels, block_term(): pl.pallas_call(term_body, grid=(d // tile,), in_specs=[pl.BlockSpec((1, r...  23.7 us
    pallas_call x2, Pallas kernels, attn_grads(): pl.pallas_call(functools.partial(attn_grad_body, partner), grid_spec=pltp...  22.5 us
  transfers between devices with their start and end apart: 45, of which 24 were waited for; matrix products, arithmetic and copies ran while one was open for 9% of the time, Pallas kernels for 34%

profile of v6, /device:TPU:0, one launch (start us, length us, event | category | flops | bytes accessed | tf_op | source)
XLA Modules:
  0.0 550.1 jit_solution(3532465792753760886)
XLA Ops:
  8.5 5.1 collective-permute-start
  17.9 7.1 %qkv_slot.4 = (bf16[4,256,2048]{2,1,0:T(8,128)(2,1)}, bf16[4,256,512]{2,1,0:T(8,128)(2,1)}, bf16[4,256,512]{2,1,0:T(8,128)(2,1)}, bf16[4,256,512]{2,1,0:T(8,128)(2,1)}) custom-call(s32[4]{0:T(128)} %pad_add_fusion.rank_ref, bf16[256,1024]{1,0:T(8,128)(2,1)} %copy-done.57, bf16[256,1024]{1,0:T(8,128)(2,1)} %copy-done.56, f32[1,2048]{1,0:T(1,128)} %bitcast.94, ...), custom_call_target="tpu_custom_call" | custom-call | flops 1610612736 | bytes 8388608 | tf_op jit(solution)/shard_map/qkv_slot/pallas_call | solution.py:106
  26.0 4.4 collective-permute-start.1
  30.3 6.8 %collective-permute-done.2.xb_ref = bf16[256,1024]{1,0:T(8,128)(2,1)S(1)} collective-permute-done((bf16[256,1024]{1,0:T(8,128)(2,1)S(1)}, bf16[256,1024]{1,0:T(8,128)(2,1)S(1)}, u32[]{:S(2)}, u32[]{:S(2)}) %collective-permute-start.2) | collective-permute-done | bytes 524320 | tf_op jit(solution)/shard_map/ppermute | solution.py:596
  37.2 4.3 collective-permute-start.4
  41.5 7.1 %qkv_slot.5 = (bf16[4,256,2048]{2,1,0:T(8,128)(2,1)}, bf16[4,256,512]{2,1,0:T(8,128)(2,1)}, bf16[4,256,512]{2,1,0:T(8,128)(2,1)}, bf16[4,256,512]{2,1,0:T(8,128)(2,1)}) custom-call(s32[4]{0:T(128)} %pad_add_fusion.rank_ref, ...), custom_call_target="tpu_custom_call", output_to_operand_aliasing={{0}: (10, {}), {1}: (11, {}), {2}: (12, {}), {3}: (13, {})} | custom-call | flops 1610612736 | bytes 8388608 | tf_op jit(solution)/shard_map/qkv_slot/pallas_call | solution.py:106
  48.7 4.1 collective-permute-start.3
  52.8 6.9 %collective-permute-done.4.xb_ref = bf16[256,1024]{1,0:T(8,128)(2,1)S(1)} collective-permute-done((bf16[256,1024]{1,0:T(8,128)(2,1)S(1)}, bf16[256,1024]{1,0:T(8,128)(2,1)S(1)}, u32[]{:S(2)}, u32[]{:S(2)}) %collective-permute-start.4) | collective-permute-done | bytes 524320 | tf_op jit(solution)/shard_map/ppermute | solution.py:596
  59.7 4.3 collective-permute-start.5
  63.9 7.1 %qkv_slot.6 = (bf16[4,256,2048]{2,1,0:T(8,128)(2,1)}, bf16[4,256,512]{2,1,0:T(8,128)(2,1)}, bf16[4,256,512]{2,1,0:T(8,128)(2,1)}, bf16[4,256,512]{2,1,0:T(8,128)(2,1)}) custom-call(s32[4]{0:T(128)} %pad_add_fusion.rank_ref, bf16[256,1024]{1,0:T(8,128)(2,1)} %copy-done.63, ...), custom_call_target="tpu_custom_call", output_to_operand_aliasing={{0}: (10, {}), {1}: (11, {}), {2}: (12, {}), {3}: (13, {})} | custom-call | flops 1610612736 | bytes 8388608 | tf_op jit(solution)/shard_map/qkv_slot/pallas_call | solution.py:106
  83.0 7.1 %qkv_slot.7 = (bf16[4,256,2048]{2,1,0:T(8,128)(2,1)}, bf16[4,256,512]{2,1,0:T(8,128)(2,1)}, bf16[4,256,512]{2,1,0:T(8,128)(2,1)}, bf16[4,256,512]{2,1,0:T(8,128)(2,1)}) custom-call(s32[4]{0:T(128)} %pad_add_fusion.rank_ref, bf16[256,1024]{1,0:T(8,128)(2,1)} %copy-done.62, ...), custom_call_target="tpu_custom_call", output_to_operand_aliasing={{0}: (10, {}), {1}: (11, {}), {2}: (12, {}), {3}: (13, {})} | custom-call | flops 1610612736 | bytes 8388608 | tf_op jit(solution)/shard_map/qkv_slot/pallas_call | solution.py:106
  90.2 10.3 %attend.1 = bf16[4,256,512]{2,1,0:T(8,128)(2,1)} custom-call(s32[4]{0:T(128)} %pad_add_fusion.rank_ref, bf16[4,256,512]{2,1,0:T(8,128)(2,1)} %get-tuple-element.173.q_ref, bf16[4,256,512]{2,1,0:T(8,128)(2,1)} %get-tuple-element.174.k_ref, bf16[4,256,512]{2,1,0:T(8,128)(2,1)} %get-tuple-element.175.v_ref, s32[4,256,1]{2,1,0:T(8,128)} %reshape.203.dcol_ref, ...), custom_call_target="tpu_custom_call" | custom-call | flops 2147483648 | bytes 4194304 | tf_op jit(solution)/shard_map/attend/pallas_call | solution.py:169
  100.4 4.3 convolution_convert_fusion.1
  113.0 18.3 %collective-permute-done.7.moved_ref.gr_ref = bf16[256,2048]{1,0:T(8,128)(2,1)S(1)} collective-permute-done((bf16[256,2048]{1,0:T(8,128)(2,1)S(1)}, bf16[256,2048]{1,0:T(8,128)(2,1)S(1)}, u32[]{:S(2)}, u32[]{:S(2)}) %collective-permute-start.7) | collective-permute-done | bytes 1048608 | tf_op jit(solution)/shard_map/ppermute | solution.py:596
  132.4 4.4 collective-permute-start.8
  140.3 18.2 %collective-permute-done.8.moved_ref.gr_ref = bf16[256,2048]{1,0:T(8,128)(2,1)S(1)} collective-permute-done((bf16[256,2048]{1,0:T(8,128)(2,1)S(1)}, bf16[256,2048]{1,0:T(8,128)(2,1)S(1)}, u32[]{:S(2)}, u32[]{:S(2)}) %collective-permute-start.8) | collective-permute-done | bytes 1048608 | tf_op jit(solution)/shard_map/ppermute | solution.py:596
  159.5 4.6 collective-permute-start.9
  171.3 13.5 %collective-permute-done.9 = bf16[256,2048]{1,0:T(8,128)(2,1)S(1)} collective-permute-done((bf16[256,2048]{1,0:T(8,128)(2,1)S(1)}, bf16[256,2048]{1,0:T(8,128)(2,1)S(1)}, u32[]{:S(2)}, u32[]{:S(2)}) %collective-permute-start.9) | collective-permute-done | bytes 1048608 | tf_op jit(solution)/shard_map/ppermute | solution.py:596
  184.8 6.0 %collective-permute-done.13 = bf16[256,2048]{1,0:T(8,128)(2,1)S(1)} collective-permute-done((bf16[256,2048]{1,0:T(8,128)(2,1)S(1)}, bf16[256,2048]{1,0:T(8,128)(2,1)S(1)}, u32[]{:S(2)}, u32[]{:S(2)}) %collective-permute-start.13) | collective-permute-done | bytes 1048608 | tf_op jit(solution)/shard_map/ppermute | solution.py:596
  194.7 9.3 %mlp_slot.4 = (bf16[4,256,2048]{2,1,0:T(8,128)(2,1)S(1)}, bf16[4,256,2048]{2,1,0:T(8,128)(2,1)S(1)}, bf16[4,256,2048]{2,1,0:T(8,128)(2,1)S(1)}, bf16[4,256,2048]{2,1,0:T(8,128)(2,1)S(1)}) custom-call(s32[4]{0:T(128)S(1)} %copy-done.41, bf16[256,2048]{1,0:T(8,128)(2,1)S(1)} %add_convert_fusion.4.a_ref, bf16[256,2048]{1,0:T(8,128)(2,1)S(1)} %bitcast.90, ...), custom_call_target="tpu_custom_call" | custom-call | flops 4294967296 | bytes 20971520 | tf_op jit(solution)/shard_map/mlp_slot/pallas_call | solution.py:303
  204.0 3.4 copy-done
  211.4 4.9 collective-permute-done.14.a_ref
  217.8 9.9 %mlp_slot.5 = (bf16[4,256,2048]{2,1,0:T(8,128)(2,1)S(1)}, bf16[4,256,2048]{2,1,0:T(8,128)(2,1)S(1)}, bf16[4,256,2048]{2,1,0:T(8,128)(2,1)S(1)}, bf16[4,256,2048]{2,1,0:T(8,128)(2,1)S(1)}) custom-call(s32[4]{0:T(128)S(1)} %copy-done.41, ...), custom_call_target="tpu_custom_call", output_to_operand_aliasing={{0}: (7, {}), {1}: (8, {}), {2}: (9, {}), {3}: (10, {})} | custom-call | flops 4294967296 | bytes 20971520 | tf_op jit(solution)/shard_map/mlp_slot/pallas_call | solution.py:303
  227.8 3.8 block_term.9
  232.8 9.8 %collective-permute-done.15.a_ref = bf16[256,2048]{1,0:T(8,128)(2,1)S(1)} collective-permute-done((bf16[256,2048]{1,0:T(8,128)(2,1)}, bf16[256,2048]{1,0:T(8,128)(2,1)S(1)}, u32[]{:S(2)}, u32[]{:S(2)}) %collective-permute-start.15) | collective-permute-done | bytes 1048608 | tf_op jit(solution)/shard_map/ppermute | solution.py:596
  245.9 9.3 %mlp_slot.6 = (bf16[4,256,2048]{2,1,0:T(8,128)(2,1)S(1)}, bf16[4,256,2048]{2,1,0:T(8,128)(2,1)S(1)}, bf16[4,256,2048]{2,1,0:T(8,128)(2,1)S(1)}, bf16[4,256,2048]{2,1,0:T(8,128)(2,1)S(1)}) custom-call(s32[4]{0:T(128)S(1)} %copy-done.41, ...), custom_call_target="tpu_custom_call", output_to_operand_aliasing={{0}: (7, {}), {1}: (8, {}), {2}: (9, {}), {3}: (10, {})} | custom-call | flops 4294967296 | bytes 20971520 | tf_op jit(solution)/shard_map/mlp_slot/pallas_call | solution.py:303
  258.3 6.8 %collective-permute-done.17 = bf16[256,2048]{1,0:T(8,128)(2,1)S(1)} collective-permute-done((bf16[256,2048]{1,0:T(8,128)(2,1)}, bf16[256,2048]{1,0:T(8,128)(2,1)S(1)}, u32[]{:S(2)}, u32[]{:S(2)}) %collective-permute-start.17) | collective-permute-done | bytes 1048608 | tf_op jit(solution)/shard_map/ppermute | solution.py:596
  268.8 18.8 %collective-permute-done.16.a_ref = bf16[256,2048]{1,0:T(8,128)(2,1)S(1)} collective-permute-done((bf16[256,2048]{1,0:T(8,128)(2,1)S(1)}, bf16[256,2048]{1,0:T(8,128)(2,1)S(1)}, u32[]{:S(2)}, u32[]{:S(2)}) %collective-permute-start.16) | collective-permute-done | bytes 1048608 | tf_op jit(solution)/shard_map/ppermute | solution.py:596
  287.6 10.3 %mlp_slot.7 = (bf16[4,256,2048]{2,1,0:T(8,128)(2,1)S(1)}, bf16[4,256,2048]{2,1,0:T(8,128)(2,1)S(1)}, bf16[4,256,2048]{2,1,0:T(8,128)(2,1)S(1)}, bf16[4,256,2048]{2,1,0:T(8,128)(2,1)S(1)}) custom-call(s32[4]{0:T(128)S(1)} %copy-done.41, ...), custom_call_target="tpu_custom_call", output_to_operand_aliasing={{0}: (7, {}), {1}: (8, {}), {2}: (9, {}), {3}: (10, {})} | custom-call | flops 4294967296 | bytes 20971520 | tf_op jit(solution)/shard_map/mlp_slot/pallas_call | solution.py:303
  297.9 7.6 %collective-permute-done.18.rest_0_ = bf16[256,2048]{1,0:T(8,128)(2,1)S(1)} collective-permute-done((bf16[256,2048]{1,0:T(8,128)(2,1)S(1)}, bf16[256,2048]{1,0:T(8,128)(2,1)S(1)}, u32[]{:S(2)}, u32[]{:S(2)}) %collective-permute-start.18) | collective-permute-done | bytes 1048608 | tf_op jit(solution)/shard_map/ppermute | solution.py:596
  311.9 7.2 %grad_half.4 = bf16[2048,1024]{1,0:T(8,128)(2,1)} custom-call(s32[4]{0:T(128)S(1)} %copy-done.41, bf16[1024,2048]{1,0:T(8,128)(2,1)S(1)} %bitcast.84, bf16[1024,2048]{1,0:T(8,128)(2,1)S(1)} %bitcast.79), custom_call_target="tpu_custom_call" | custom-call | flops 1000000 | bytes 1000000 | tf_op jit(solution)/shard_map/grad_half/pallas_call | solution.py:413
  319.1 7.2 %grad_half.5 = bf16[2048,1024]{1,0:T(8,128)(2,1)} custom-call(s32[4]{0:T(128)S(1)} %copy-done.41, bf16[1024,2048]{1,0:T(8,128)(2,1)S(1)} %bitcast.82, bf16[1024,2048]{1,0:T(8,128)(2,1)S(1)} %bitcast.59), custom_call_target="tpu_custom_call" | custom-call | flops 1000000 | bytes 1000000 | tf_op jit(solution)/shard_map/grad_half/pallas_call | solution.py:413
  338.0 11.3 %convolution_convert_fusion = bf16[1024,2048]{1,0:T(8,128)(2,1)S(1)} fusion(bf16[1024,2048]{1,0:T(8,128)(2,1)S(1)} %bitcast.80, bf16[2048,2048]{1,0:T(8,128)(2,1)} %down_ref.7), kind=kOutput, calls=%fused_computation | convolution fusion | flops 8592031744 | bytes 16777216 | tf_op jit(solution)/shard_map/dot_general | solution.py:53
  349.3 8.0 %grad_half.6.rest_1_ = bf16[2,2048,1024]{2,1,0:T(8,128)(2,1)S(1)} custom-call(s32[4]{0:T(128)S(1)} %copy-done.41, bf16[1024,2048]{1,0:T(8,128)(2,1)S(1)} %bitcast.85, bf16[1024,2048]{1,0:T(8,128)(2,1)S(1)} %bitcast.81, bf16[2048,1024]{1,0:T(8,128)(2,1)} %collective-permute-done.21.rest_0_), custom_call_target="tpu_custom_call" | custom-call | flops 1000000 | bytes 1000000 | tf_op jit(solution)/shard_map/grad_half/pallas_call | solution.py:413
  359.0 5.4 collective-permute-start.22
  367.3 7.2 %grad_half.7 = bf16[2,2048,1024]{2,1,0:T(8,128)(2,1)S(1)} custom-call(s32[4]{0:T(128)S(1)} %copy-done.41, bf16[1024,2048]{1,0:T(8,128)(2,1)S(1)} %bitcast.83, bf16[1024,2048]{1,0:T(8,128)(2,1)S(1)} %bitcast.60, bf16[2048,1024]{1,0:T(8,128)(2,1)} %collective-permute-done.24.rest_0_, ...), custom_call_target="tpu_custom_call", output_to_operand_aliasing={{}: (4, {})} | custom-call | flops 1000000 | bytes 1000000 | tf_op jit(solution)/shard_map/grad_half/pallas_call | solution.py:413
  378.0 3.7 collective-permute-done.22.moved_ref.refs_2_
  385.8 4.6 collective-permute-start.25
  393.8 4.2 dom_part.2
  398.0 10.3 %collective-permute-done.25.moved_ref.refs_1_ = bf16[256,2048]{1,0:T(8,128)(2,1)S(1)} collective-permute-done((bf16[256,2048]{1,0:T(8,128)(2,1)S(1)}, bf16[256,2048]{1,0:T(8,128)(2,1)S(1)}, u32[]{:S(2)}, u32[]{:S(2)}) %collective-permute-start.25) | collective-permute-done | bytes 1048608 | tf_op jit(solution)/shard_map/ppermute | solution.py:596
  409.1 4.5 collective-permute-start.26
  419.4 14.2 %attend_back.1.x_ref = bf16[4,256,1536]{2,1,0:T(8,128)(2,1)S(1)} custom-call(s32[4]{0:T(128)S(1)} %copy-done.41, bf16[4,256,512]{2,1,0:T(8,128)(2,1)S(1)} %copy-done.22, bf16[4,256,512]{2,1,0:T(8,128)(2,1)S(1)} %copy-done.23, bf16[4,256,512]{2,1,0:T(8,128)(2,1)S(1)} %copy-done.24, bf16[4,256,512]{2,1,0:T(8,128)(2,1)S(1)} %get-tuple-element.225.do_ref, ...), custom_call_target="tpu_custom_call" | custom-call | flops 115999997952 | bytes 7340032 | tf_op jit(solution)/shard_map/attend_back/pallas_call | solution.py:251
  439.0 10.8 %attn_grads.2 = bf16[2048,1024]{1,0:T(8,128)(2,1)} custom-call(s32[4]{0:T(128)} %pad_add_fusion.rank_ref, bf16[1024,2048]{1,0:T(8,128)(2,1)} %bitcast.101, bf16[1024,2048]{1,0:T(8,128)(2,1)} %bitcast.86, bf16[1024,1536]{1,0:T(8,128)(2,1)} %bitcast.61, bf16[1024,1536]{1,0:T(8,128)(2,1)} %bitcast.62, bf16[1024,512]{1,0:T(8,128)(2,1)} %bitcast.104), custom_call_target="tpu_custom_call" | custom-call | flops 4000000000 | bytes 1000000 | tf_op jit(solution)/shard_map/attn_grads/pallas_call | solution.py:456
  462.7 11.7 %attn_grads.3 = bf16[2048,1024]{1,0:T(8,128)(2,1)} custom-call(s32[4]{0:T(128)} %pad_add_fusion.rank_ref, bf16[1024,2048]{1,0:T(8,128)(2,1)} %bitcast.102, bf16[1024,2048]{1,0:T(8,128)(2,1)} %bitcast.87, bf16[1024,1536]{1,0:T(8,128)(2,1)} %bitcast.63, bf16[1024,1536]{1,0:T(8,128)(2,1)} %bitcast.64, bf16[1024,512]{1,0:T(8,128)(2,1)} %bitcast.105, ...), custom_call_target="tpu_custom_call" | custom-call | flops 1000000 | bytes 1000000 | tf_op jit(solution)/shard_map/attn_grads/pallas_call | solution.py:456
  478.9 4.5 collective-permute-start.32
  496.6 3.8 fusion.7
  508.9 4.4 collective-permute-start.34
  520.2 13.2 %collective-permute-done.34.moved_ref = bf16[256,2048]{1,0:T(8,128)(2,1)S(1)} collective-permute-done((bf16[256,2048]{1,0:T(8,128)(2,1)S(1)}, bf16[256,2048]{1,0:T(8,128)(2,1)S(1)}, u32[]{:S(2)}, u32[]{:S(2)}) %collective-permute-start.34) | collective-permute-done | bytes 1048608 | tf_op jit(solution)/shard_map/ppermute | solution.py:596
  (306 shorter events, 160.1 us)
Async XLA Ops:
  7.2 467.3 %reduce-scatter.3.cloned.1.call-start = ((), (), s32[]{:S(2)}) async-start(), calls=%async_computation.2 | async-start | bytes 10485760 | tf_op jit(solution)/shard_map/reduce_scatter | solution.py:707
  8.5 17.4 %collective-permute-start = (bf16[256,1024]{1,0:T(8,128)(2,1)S(1)}, bf16[256,1024]{1,0:T(8,128)(2,1)}, u32[]{:S(2)}, u32[]{:S(2)}) collective-permute-start(bf16[256,1024]{1,0:T(8,128)(2,1)S(1)} %get-tuple-element.277.xa_ref), channel_id=1, source_target_pairs={{0,3},{1,0},{2,1},{3,2},{4,7},{5,4},{6,5},{7,6},{8,11},{9,8},{10,9... | collective-permute-start | bytes 1572872 | tf_op jit(solution)/shard_map/ppermute | solution.py:596
  13.6 23.6 %collective-permute-start.2 = (bf16[256,1024]{1,0:T(8,128)(2,1)S(1)}, bf16[256,1024]{1,0:T(8,128)(2,1)S(1)}, u32[]{:S(2)}, u32[]{:S(2)}) collective-permute-start(bf16[256,1024]{1,0:T(8,128)(2,1)S(1)} %get-tuple-element.276.xb_ref), channel_id=1, source_target_pairs={{0,3},{1,0},{2,1},{3,2},{4,7},{5,4},{6,5},{7,6},{8,11},{9,8},{10,9... | collective-permute-start | bytes 1572872 | tf_op jit(solution)/shard_map/ppermute | solution.py:596
  26.0 22.7 %collective-permute-start.1 = (bf16[256,1024]{1,0:T(8,128)(2,1)}, bf16[256,1024]{1,0:T(8,128)(2,1)S(1)}, u32[]{:S(2)}, u32[]{:S(2)}) collective-permute-start(bf16[256,1024]{1,0:T(8,128)(2,1)} %collective-permute-done.xa_ref), channel_id=1, source_target_pairs={{0,3},{1,0},{2,1},{3,2},{4,7},{5,4},{6,5},{7,6},{8,11},{9,8},{10,9... | collective-permute-start | bytes 1572872 | tf_op jit(solution)/shard_map/ppermute | solution.py:596
  37.2 22.5 %collective-permute-start.4 = (bf16[256,1024]{1,0:T(8,128)(2,1)S(1)}, bf16[256,1024]{1,0:T(8,128)(2,1)S(1)}, u32[]{:S(2)}, u32[]{:S(2)}) collective-permute-start(bf16[256,1024]{1,0:T(8,128)(2,1)S(1)} %collective-permute-done.2.xb_ref), channel_id=1, source_target_pairs={{0,3},{1,0},{2,1},{3,2},{4,7},{5,4},{6,5},{7,6},{8,11},{9,8},{10,9... | collective-permute-start | bytes 1572872 | tf_op jit(solution)/shard_map/ppermute | solution.py:596
  48.6 27.6 %copy-start.43 = (s32[1,1024]{1,0:T(1,128)S(1)}, s32[1,1024]{1,0:T(1,128)}, u32[]{:S(2)}) copy-start(s32[1,1024]{1,0:T(1,128)} %param.19) | copy-start | bytes 12292
  48.6 29.4 %copy-start.69 = (s32[1,1024]{1,0:T(1,128)S(1)}, s32[1,1024]{1,0:T(1,128)}, u32[]{:S(2)}) copy-start(s32[1,1024]{1,0:T(1,128)} %param.20) | copy-start | bytes 12292
  48.7 22.4 %collective-permute-start.3 = (bf16[256,1024]{1,0:T(8,128)(2,1)S(1)}, bf16[256,1024]{1,0:T(8,128)(2,1)S(1)}, u32[]{:S(2)}, u32[]{:S(2)}) collective-permute-start(bf16[256,1024]{1,0:T(8,128)(2,1)S(1)} %collective-permute-done.1.xa_ref), channel_id=1, source_target_pairs={{0,3},{1,0},{2,1},{3,2},{4,7},{5,4},{6,5},{7,6},{8,11},{9,8},{10,9... | collective-permute-start | bytes 1572872 | tf_op jit(solution)/shard_map/ppermute | solution.py:596
  59.7 22.6 %collective-permute-start.5 = (bf16[256,1024]{1,0:T(8,128)(2,1)S(1)}, bf16[256,1024]{1,0:T(8,128)(2,1)S(1)}, u32[]{:S(2)}, u32[]{:S(2)}) collective-permute-start(bf16[256,1024]{1,0:T(8,128)(2,1)S(1)} %collective-permute-done.4.xb_ref), channel_id=1, source_target_pairs={{0,3},{1,0},{2,1},{3,2},{4,7},{5,4},{6,5},{7,6},{8,11},{9,8},{10,9... | collective-permute-start | bytes 1572872 | tf_op jit(solution)/shard_map/ppermute | solution.py:596
  71.1 33.6 %collective-permute-start.6 = (bf16[256,2048]{1,0:T(8,128)(2,1)S(1)}, bf16[256,2048]{1,0:T(8,128)(2,1)}, u32[]{:S(2)}, u32[]{:S(2)}) collective-permute-start(bf16[256,2048]{1,0:T(8,128)(2,1)S(1)} %bitcast.88), channel_id=1, source_target_pairs={{0,1},{1,2},{2,3},{4,5},{5,6},{6,7},{8,9},{9,10},{10,11},{12,13},{... | collective-permute-start | bytes 3145736 | tf_op jit(solution)/shard_map/ppermute | solution.py:596
  74.2 35.7 %collective-permute-start.10 = (bf16[256,2048]{1,0:T(8,128)(2,1)S(1)}, bf16[256,2048]{1,0:T(8,128)(2,1)}, u32[]{:S(2)}, u32[]{:S(2)}) collective-permute-start(bf16[256,2048]{1,0:T(8,128)(2,1)S(1)} %bitcast.89), channel_id=1, source_target_pairs={{1,0},{2,1},{3,2},{5,4},{6,5},{7,6},{9,8},{10,9},{11,10},{13,12},{... | collective-permute-start | bytes 3145736 | tf_op jit(solution)/shard_map/ppermute | solution.py:596
  106.7 24.7 %collective-permute-start.7 = (bf16[256,2048]{1,0:T(8,128)(2,1)S(1)}, bf16[256,2048]{1,0:T(8,128)(2,1)S(1)}, u32[]{:S(2)}, u32[]{:S(2)}) collective-permute-start(bf16[256,2048]{1,0:T(8,128)(2,1)S(1)} %join.12), channel_id=1, source_target_pairs={{0,1},{1,2},{2,3},{4,5},{5,6},{6,7},{8,9},{9,10},{10,11},{12,13},{... | collective-permute-start | bytes 3145736 | tf_op jit(solution)/shard_map/ppermute | solution.py:596
  111.7 26.3 %collective-permute-start.11 = (bf16[256,2048]{1,0:T(8,128)(2,1)S(1)}, bf16[256,2048]{1,0:T(8,128)(2,1)S(1)}, u32[]{:S(2)}, u32[]{:S(2)}) collective-permute-start(bf16[256,2048]{1,0:T(8,128)(2,1)S(1)} %join.15), channel_id=1, source_target_pairs={{1,0},{2,1},{3,2},{5,4},{6,5},{7,6},{9,8},{10,9},{11,10},{13,12},{... | collective-permute-start | bytes 3145736 | tf_op jit(solution)/shard_map/ppermute | solution.py:596
  132.4 26.1 %collective-permute-start.8 = (bf16[256,2048]{1,0:T(8,128)(2,1)S(1)}, bf16[256,2048]{1,0:T(8,128)(2,1)S(1)}, u32[]{:S(2)}, u32[]{:S(2)}) collective-permute-start(bf16[256,2048]{1,0:T(8,128)(2,1)S(1)} %join.13), channel_id=1, source_target_pairs={{0,1},{1,2},{2,3},{4,5},{5,6},{6,7},{8,9},{9,10},{10,11},{12,13},{... | collective-permute-start | bytes 3145736 | tf_op jit(solution)/shard_map/ppermute | solution.py:596
  139.0 25.3 %collective-permute-start.12 = (bf16[256,2048]{1,0:T(8,128)(2,1)S(1)}, bf16[256,2048]{1,0:T(8,128)(2,1)S(1)}, u32[]{:S(2)}, u32[]{:S(2)}) collective-permute-start(bf16[256,2048]{1,0:T(8,128)(2,1)S(1)} %join.16), channel_id=1, source_target_pairs={{1,0},{2,1},{3,2},{5,4},{6,5},{7,6},{9,8},{10,9},{11,10},{13,12},{... | collective-permute-start | bytes 3145736 | tf_op jit(solution)/shard_map/ppermute | solution.py:596
  159.5 25.3 %collective-permute-start.9 = (bf16[256,2048]{1,0:T(8,128)(2,1)S(1)}, bf16[256,2048]{1,0:T(8,128)(2,1)S(1)}, u32[]{:S(2)}, u32[]{:S(2)}) collective-permute-start(bf16[256,2048]{1,0:T(8,128)(2,1)S(1)} %join.14), channel_id=1, source_target_pairs={{0,1},{1,2},{2,3},{4,5},{5,6},{6,7},{8,9},{9,10},{10,11},{12,13},{... | collective-permute-start | bytes 3145736 | tf_op jit(solution)/shard_map/ppermute | solution.py:596
  165.3 25.5 %collective-permute-start.13 = (bf16[256,2048]{1,0:T(8,128)(2,1)S(1)}, bf16[256,2048]{1,0:T(8,128)(2,1)S(1)}, u32[]{:S(2)}, u32[]{:S(2)}) collective-permute-start(bf16[256,2048]{1,0:T(8,128)(2,1)S(1)} %join.17), channel_id=1, source_target_pairs={{1,0},{2,1},{3,2},{5,4},{6,5},{7,6},{9,8},{10,9},{11,10},{13,12},{... | collective-permute-start | bytes 3145736 | tf_op jit(solution)/shard_map/ppermute | solution.py:596
  192.8 23.5 %collective-permute-start.14 = (bf16[256,2048]{1,0:T(8,128)(2,1)S(1)}, bf16[256,2048]{1,0:T(8,128)(2,1)}, u32[]{:S(2)}, u32[]{:S(2)}) collective-permute-start(bf16[256,2048]{1,0:T(8,128)(2,1)S(1)} %add_convert_fusion.4.a_ref), channel_id=1, source_target_pairs={{0,3},{1,0},{2,1},{3,2},{4,7},{5,4},{6,5},{7,6},{8,11},{9,8},{10,9... | collective-permute-start | bytes 3145736 | tf_op jit(solution)/shard_map/ppermute | solution.py:596
  216.3 26.3 %collective-permute-start.15 = (bf16[256,2048]{1,0:T(8,128)(2,1)}, bf16[256,2048]{1,0:T(8,128)(2,1)S(1)}, u32[]{:S(2)}, u32[]{:S(2)}) collective-permute-start(bf16[256,2048]{1,0:T(8,128)(2,1)} %collective-permute-done.14.a_ref), channel_id=1, source_target_pairs={{0,3},{1,0},{2,1},{3,2},{4,7},{5,4},{6,5},{7,6},{8,11},{9,8},{10,9... | collective-permute-start | bytes 3145736 | tf_op jit(solution)/shard_map/ppermute | solution.py:596
  231.6 33.6 %collective-permute-start.17 = (bf16[256,2048]{1,0:T(8,128)(2,1)}, bf16[256,2048]{1,0:T(8,128)(2,1)S(1)}, u32[]{:S(2)}, u32[]{:S(2)}) collective-permute-start(bf16[256,2048]{1,0:T(8,128)(2,1)} %block_term.9), channel_id=1, source_target_pairs={{0,3},{1,0},{2,1},{3,2},{4,7},{5,4},{6,5},{7,6},{8,11},{9,8},{10,9... | collective-permute-start | bytes 3145736 | tf_op jit(solution)/shard_map/ppermute | solution.py:596
  242.6 44.9 %collective-permute-start.16 = (bf16[256,2048]{1,0:T(8,128)(2,1)S(1)}, bf16[256,2048]{1,0:T(8,128)(2,1)S(1)}, u32[]{:S(2)}, u32[]{:S(2)}) collective-permute-start(bf16[256,2048]{1,0:T(8,128)(2,1)S(1)} %collective-permute-done.15.a_ref), channel_id=1, source_target_pairs={{0,3},{1,0},{2,1},{3,2},{4,7},{5,4},{6,5},{7,6},{8,11},{9,8},{10,9... | collective-permute-start | bytes 3145736 | tf_op jit(solution)/shard_map/ppermute | solution.py:596
  258.3 29.3 %copy-start.27 = (bf16[256,2048]{1,0:T(8,128)(2,1)S(1)}, bf16[256,2048]{1,0:T(8,128)(2,1)}, u32[]{:S(2)}) copy-start(bf16[256,2048]{1,0:T(8,128)(2,1)} %copy-done.26) | copy-start | bytes 3145732
  265.5 40.0 %collective-permute-start.18 = (bf16[256,2048]{1,0:T(8,128)(2,1)S(1)}, bf16[256,2048]{1,0:T(8,128)(2,1)S(1)}, u32[]{:S(2)}, u32[]{:S(2)}) collective-permute-start(bf16[256,2048]{1,0:T(8,128)(2,1)S(1)} %add_convert_fusion.3), channel_id=1, source_target_pairs={{0,3},{1,0},{2,1},{3,2},{4,7},{5,4},{6,5},{7,6},{8,11},{9,8},{10,9... | collective-permute-start | bytes 3145736 | tf_op jit(solution)/shard_map/ppermute | solution.py:596
  308.7 21.2 %collective-permute-start.19 = (bf16[256,2048]{1,0:T(8,128)(2,1)S(1)}, bf16[256,2048]{1,0:T(8,128)(2,1)S(1)}, u32[]{:S(2)}, u32[]{:S(2)}) collective-permute-start(bf16[256,2048]{1,0:T(8,128)(2,1)S(1)} %block_term.11), channel_id=1, source_target_pairs={{0,3},{1,0},{2,1},{3,2},{4,7},{5,4},{6,5},{7,6},{8,11},{9,8},{10,9... | collective-permute-start | bytes 3145736 | tf_op jit(solution)/shard_map/ppermute | solution.py:596
  319.1 30.2 %collective-permute-start.21 = (bf16[2048,1024]{1,0:T(8,128)(2,1)}, bf16[2048,1024]{1,0:T(8,128)(2,1)}, u32[]{:S(2)}, u32[]{:S(2)}) collective-permute-start(bf16[2048,1024]{1,0:T(8,128)(2,1)} %grad_half.4), channel_id=1, source_target_pairs={{0,4},{4,0},{8,12},{12,8},{16,20},{20,16},{24,28},{28,24},{1,5},{5... | collective-permute-start | bytes 12582920 | tf_op jit(solution)/shard_map/ppermute | solution.py:617
  326.4 41.0 %collective-permute-start.24 = (bf16[2048,1024]{1,0:T(8,128)(2,1)}, bf16[2048,1024]{1,0:T(8,128)(2,1)}, u32[]{:S(2)}, u32[]{:S(2)}) collective-permute-start(bf16[2048,1024]{1,0:T(8,128)(2,1)} %grad_half.5), channel_id=1, source_target_pairs={{0,4},{4,0},{8,12},{12,8},{16,20},{20,16},{24,28},{28,24},{1,5},{5... | collective-permute-start | bytes 12582920 | tf_op jit(solution)/shard_map/ppermute | solution.py:617
  333.9 23.4 %collective-permute-start.20 = (bf16[256,2048]{1,0:T(8,128)(2,1)S(1)}, bf16[256,2048]{1,0:T(8,128)(2,1)S(1)}, u32[]{:S(2)}, u32[]{:S(2)}) collective-permute-start(bf16[256,2048]{1,0:T(8,128)(2,1)S(1)} %get-tuple-element.215.refs_0_), channel_id=1, source_target_pairs={{0,1},{1,2},{2,3},{4,5},{5,6},{6,7},{8,9},{9,10},{10,11},{12,13},{... | collective-permute-start | bytes 3145736 | tf_op jit(solution)/shard_map/ppermute | solution.py:596
  336.7 27.7 %collective-permute-start.23 = (bf16[256,2048]{1,0:T(8,128)(2,1)S(1)}, bf16[256,2048]{1,0:T(8,128)(2,1)S(1)}, u32[]{:S(2)}, u32[]{:S(2)}) collective-permute-start(bf16[256,2048]{1,0:T(8,128)(2,1)S(1)} %get-tuple-element.215.refs_0_), channel_id=1, source_target_pairs={{1,0},{2,1},{3,2},{5,4},{6,5},{7,6},{9,8},{10,9},{11,10},{13,12},{... | collective-permute-start | bytes 3145736 | tf_op jit(solution)/shard_map/ppermute | solution.py:596
  359.0 22.7 %collective-permute-start.22 = (bf16[256,2048]{1,0:T(8,128)(2,1)}, bf16[256,2048]{1,0:T(8,128)(2,1)}, u32[]{:S(2)}, u32[]{:S(2)}) collective-permute-start(bf16[256,2048]{1,0:T(8,128)(2,1)} %join.18), channel_id=1, source_target_pairs={{0,1},{1,2},{2,3},{4,5},{5,6},{6,7},{8,9},{9,10},{10,11},{12,13},{... | collective-permute-start | bytes 3145736 | tf_op jit(solution)/shard_map/ppermute | solution.py:596
  366.0 24.3 %collective-permute-start.27 = (bf16[256,2048]{1,0:T(8,128)(2,1)}, bf16[256,2048]{1,0:T(8,128)(2,1)}, u32[]{:S(2)}, u32[]{:S(2)}) collective-permute-start(bf16[256,2048]{1,0:T(8,128)(2,1)} %join.19), channel_id=1, source_target_pairs={{1,0},{2,1},{3,2},{5,4},{6,5},{7,6},{9,8},{10,9},{11,10},{13,12},{... | collective-permute-start | bytes 3145736 | tf_op jit(solution)/shard_map/ppermute | solution.py:596
  377.9 158.4 %reduce-scatter.5.cloned.1.call-start = ((), (), s32[]{:S(2)}) async-start(), calls=%async_computation.3 | async-start | bytes 5242880 | tf_op jit(solution)/shard_map/reduce_scatter | solution.py:737
  385.8 22.5 %collective-permute-start.25 = (bf16[256,2048]{1,0:T(8,128)(2,1)S(1)}, bf16[256,2048]{1,0:T(8,128)(2,1)S(1)}, u32[]{:S(2)}, u32[]{:S(2)}) collective-permute-start(bf16[256,2048]{1,0:T(8,128)(2,1)S(1)} %join.20), channel_id=1, source_target_pairs={{0,1},{1,2},{2,3},{4,5},{5,6},{6,7},{8,9},{9,10},{10,11},{12,13},{... | collective-permute-start | bytes 3145736 | tf_op jit(solution)/shard_map/ppermute | solution.py:596
  392.2 22.5 %collective-permute-start.28 = (bf16[256,2048]{1,0:T(8,128)(2,1)S(1)}, bf16[256,2048]{1,0:T(8,128)(2,1)S(1)}, u32[]{:S(2)}, u32[]{:S(2)}) collective-permute-start(bf16[256,2048]{1,0:T(8,128)(2,1)S(1)} %join.22), channel_id=1, source_target_pairs={{1,0},{2,1},{3,2},{5,4},{6,5},{7,6},{9,8},{10,9},{11,10},{13,12},{... | collective-permute-start | bytes 3145736 | tf_op jit(solution)/shard_map/ppermute | solution.py:596
  409.1 24.5 %collective-permute-start.26 = (bf16[256,2048]{1,0:T(8,128)(2,1)S(1)}, bf16[256,2048]{1,0:T(8,128)(2,1)S(1)}, u32[]{:S(2)}, u32[]{:S(2)}) collective-permute-start(bf16[256,2048]{1,0:T(8,128)(2,1)S(1)} %join.21), channel_id=1, source_target_pairs={{0,1},{1,2},{2,3},{4,5},{5,6},{6,7},{8,9},{9,10},{10,11},{12,13},{... | collective-permute-start | bytes 3145736 | tf_op jit(solution)/shard_map/ppermute | solution.py:596
  415.4 20.3 %collective-permute-start.29 = (bf16[256,2048]{1,0:T(8,128)(2,1)S(1)}, bf16[256,2048]{1,0:T(8,128)(2,1)S(1)}, u32[]{:S(2)}, u32[]{:S(2)}) collective-permute-start(bf16[256,2048]{1,0:T(8,128)(2,1)S(1)} %join.23), channel_id=1, source_target_pairs={{1,0},{2,1},{3,2},{5,4},{6,5},{7,6},{9,8},{10,9},{11,10},{13,12},{... | collective-permute-start | bytes 3145736 | tf_op jit(solution)/shard_map/ppermute | solution.py:596
  449.9 10.9 %collective-permute-start.31 = (bf16[2048,1024]{1,0:T(8,128)(2,1)}, bf16[2048,1024]{1,0:T(8,128)(2,1)S(1)}, u32[]{:S(2)}, u32[]{:S(2)}) collective-permute-start(bf16[2048,1024]{1,0:T(8,128)(2,1)} %attn_grads.2), channel_id=1, source_target_pairs={{0,4},{4,0},{8,12},{12,8},{16,20},{20,16},{24,28},{28,24},{1,5},{5... | collective-permute-start | bytes 12582920 | tf_op jit(solution)/shard_map/ppermute | solution.py:617
  449.9 26.1 %collective-permute-start.30 = (bf16[256,2048]{1,0:T(8,128)(2,1)}, bf16[256,2048]{1,0:T(8,128)(2,1)}, u32[]{:S(2)}, u32[]{:S(2)}) collective-permute-start(bf16[256,2048]{1,0:T(8,128)(2,1)} %block_term.12), channel_id=1, source_target_pairs={{0,3},{1,0},{2,1},{3,2},{4,7},{5,4},{6,5},{7,6},{8,11},{9,8},{10,9... | collective-permute-start | bytes 3145736 | tf_op jit(solution)/shard_map/ppermute | solution.py:596
  478.9 28.4 %collective-permute-start.32 = (bf16[256,2048]{1,0:T(8,128)(2,1)}, bf16[256,2048]{1,0:T(8,128)(2,1)}, u32[]{:S(2)}, u32[]{:S(2)}) collective-permute-start(bf16[256,2048]{1,0:T(8,128)(2,1)} %add_convert_fusion.1), channel_id=1, source_target_pairs={{0,3},{1,0},{2,1},{3,2},{4,7},{5,4},{6,5},{7,6},{8,11},{9,8},{10,9... | collective-permute-start | bytes 3145736 | tf_op jit(solution)/shard_map/ppermute | solution.py:596
  492.3 12.0 %collective-permute-start.33 = (bf16[2,256,1024]{2,1,0:T(8,128)(2,1)}, bf16[2,256,1024]{2,1,0:T(8,128)(2,1)S(1)}, u32[]{:S(2)}, u32[]{:S(2)}) collective-permute-start(bf16[2,256,1024]{2,1,0:T(8,128)(2,1)} %constant_dynamic-slice_fusion.1), channel_id=1, source_target_pairs={{0,4},{4,0},{8,12},{12,8},{16,20},{20,16},{24,28},{28,24},{1,5},{5... | collective-permute-start | bytes 3145736 | tf_op jit(solution)/shard_map/ppermute | solution.py:617
  496.6 3.8 collective-permute-start.35
  500.4 12.9 %collective-permute-start.36 = (f32[8320]{0:T(1024)S(1)}, f32[8320]{0:T(1024)S(1)}, u32[]{:S(2)}, u32[]{:S(2)}) collective-permute-start(f32[8320]{0:T(1024)S(1)} %add.141), channel_id=1, source_target_pairs={{0,1},{1,2},{2,3},{3,0},{4,5},{5,6},{6,7},{7,4},{8,9},{9,10},{10,1... | collective-permute-start | bytes 99848 | tf_op jit(solution)/shard_map/ppermute | solution.py:596
  500.4 12.8 %collective-permute-start.37 = (f32[8320]{0:T(1024)S(1)}, f32[8320]{0:T(1024)S(1)}, u32[]{:S(2)}, u32[]{:S(2)}) collective-permute-start(f32[8320]{0:T(1024)S(1)} %add.141), channel_id=1, source_target_pairs={{0,2},{1,3},{2,0},{3,1},{4,6},{5,7},{6,4},{7,5},{8,10},{9,11},{10,... | collective-permute-start | bytes 99848 | tf_op jit(solution)/shard_map/ppermute | solution.py:596
  501.4 11.9 %collective-permute-start.38 = (f32[8320]{0:T(1024)S(1)}, f32[8320]{0:T(1024)S(1)}, u32[]{:S(2)}, u32[]{:S(2)}) collective-permute-start(f32[8320]{0:T(1024)S(1)} %add.141), channel_id=1, source_target_pairs={{0,3},{1,0},{2,1},{3,2},{4,7},{5,4},{6,5},{7,6},{8,11},{9,8},{10,9... | collective-permute-start | bytes 99848 | tf_op jit(solution)/shard_map/ppermute | solution.py:596
  508.9 24.6 %collective-permute-start.34 = (bf16[256,2048]{1,0:T(8,128)(2,1)S(1)}, bf16[256,2048]{1,0:T(8,128)(2,1)S(1)}, u32[]{:S(2)}, u32[]{:S(2)}) collective-permute-start(bf16[256,2048]{1,0:T(8,128)(2,1)S(1)} %add_convert_fusion), channel_id=1, source_target_pairs={{0,3},{1,0},{2,1},{3,2},{4,7},{5,4},{6,5},{7,6},{8,11},{9,8},{10,9... | collective-permute-start | bytes 3145736 | tf_op jit(solution)/shard_map/ppermute | solution.py:596
  513.3 22.9 %collective-permute-start.39 = (f32[8320]{0:T(1024)S(1)}, f32[8320]{0:T(1024)S(1)}, u32[]{:S(2)}, u32[]{:S(2)}) collective-permute-start(f32[8320]{0:T(1024)S(1)} %add_add_fusion.2), channel_id=1, source_target_pairs={{0,8},{4,12},{8,16},{12,20},{16,24},{20,28},{24,0},{28,4},{1,9},{5... | collective-permute-start | bytes 99848 | tf_op jit(solution)/shard_map/ppermute | solution.py:782
  515.0 21.3 %collective-permute-start.40 = (f32[8320]{0:T(1024)S(1)}, f32[8320]{0:T(1024)S(1)}, u32[]{:S(2)}, u32[]{:S(2)}) collective-permute-start(f32[8320]{0:T(1024)S(1)} %add_add_fusion.2), channel_id=1, source_target_pairs={{0,16},{4,20},{8,24},{12,28},{16,0},{20,4},{24,8},{28,12},{1,17},{... | collective-permute-start | bytes 99848 | tf_op jit(solution)/shard_map/ppermute | solution.py:782
  516.6 19.7 %collective-permute-start.41 = (f32[8320]{0:T(1024)S(1)}, f32[8320]{0:T(1024)S(1)}, u32[]{:S(2)}, u32[]{:S(2)}) collective-permute-start(f32[8320]{0:T(1024)S(1)} %add_add_fusion.2), channel_id=1, source_target_pairs={{0,24},{4,28},{8,0},{12,4},{16,8},{20,12},{24,16},{28,20},{1,25},{... | collective-permute-start | bytes 99848 | tf_op jit(solution)/shard_map/ppermute | solution.py:782
  537.4 2.0 collective-permute-start.42
  (79 other events, 572.2 us)
Sparse Core Ops, SparseCore 0:
  378.1 90.1 reduce-scatter.2
  474.6 53.0 reduce-scatter.4

commit v7 on v6

--- a/solution.py
+++ b/solution.py
@@ -264,7 +264,7 @@
     )(rank, q, k, v, do, docs_col, docs_row, heads_col, cos, sin)
 
 
-def mlp_body(slot, n, rank_ref, a_ref, gl_ref, gr_ref, up_ref, down_ref, bucket_ref, *rest):
+def mlp_body(slot, n, rank_ref, a_ref, gla_ref, glb_ref, gra_ref, grb_ref, up_ref, down_ref, bucket_ref, *rest):
     r_ref, du_ref, aa_ref, ga_ref = rest[-4:]
     rows, cb = a_ref.shape[0], up_ref.shape[1]
 
@@ -273,14 +273,14 @@
         aa_ref[0] = a_ref[...]
         ahead = rank_ref[0] + slot < n
 
-
-        @pl.when(ahead)
-        def _():
-            ga_ref[0] = gl_ref[...]
-
-        @pl.when(jnp.logical_not(ahead))
-        def _():
-            ga_ref[0] = gr_ref[...]
+        half = gla_ref.shape[1]
+
+        def fill(first, second):
+            ga_ref[0, :, :half] = first[...]
+            ga_ref[0, :, half:] = second[...]
+
+        pl.when(ahead)(functools.partial(fill, gla_ref, glb_ref))
+        pl.when(jnp.logical_not(ahead))(functools.partial(fill, gra_ref, grb_ref))
 
     u = dot_n(a_ref[...], up_ref[...])
     dr = dot_n(ga_ref[0], down_ref[...]).astype(BF16).astype(F32)
@@ -297,7 +297,7 @@
     whole = lambda j, r: (0, 0)
     wspec = pl.BlockSpec((d, cb), lambda j, r: (0, j))
     extra = [] if held is None else list(held)
-    aliases = {} if held is None else {7 + i: i for i in range(4)}
+    aliases = {} if held is None else {9 + i: i for i in range(4)}
     ospec = pl.BlockSpec((1, rows, cb), lambda j, r: (slot, 0, j))
     aspec = pl.BlockSpec((1, rows, d), lambda j, r: (slot, 0, 0))
     return pl.pallas_call(
@@ -308,7 +308,7 @@
             in_specs=[
                 pl.BlockSpec((rows, d), whole),
             ]
-            + [pl.BlockSpec((rows, d), whole)] * 2
+            + [pl.BlockSpec((rows, d // 2), whole)] * 4
             + [
                 wspec,
                 wspec,
@@ -448,7 +448,7 @@
 def attn_grads(act, states, dqkv, om, rank, moved=None):
     t, d = act.shape
     local = om.shape[1]
-    tile = min(512, d)
+    tile = min(256, d)
     partner = moved is None
     pos = (lambda r: 1 - r[3]) if partner else (lambda r: r[3])
     col = pl.BlockSpec((t, tile), lambda j, r: (0, j))
@@ -460,7 +460,7 @@
             grid=(d // tile,),
             in_specs=[
                 col,
-                col,
+                pl.BlockSpec((t, tile), lambda j, r: (0, j * pos(r))),
                 pl.BlockSpec((t, local), lambda j, r: (0, 2 * pos(r))),
                 pl.BlockSpec((t, local), lambda j, r: (0, 1)),
                 pl.BlockSpec((t, local), lambda j, r: (0, 0)),
@@ -482,7 +482,7 @@
     rest[-1][...] = out.astype(BF16)
 
 
-def block_term(acts, slot, weight, flops, moved=None):
+def block_term(acts, slot, weight, flops, moved=None, mib=62):
     _, rows, k = acts.shape
     d = weight.shape[0]
     tile = min(512, d)
@@ -497,7 +497,7 @@
         + ([] if moved is None else [out]),
         out_specs=out,
         out_shape=jax.ShapeDtypeStruct((rows, d), BF16),
-        compiler_params=params(16),
+        compiler_params=params(mib),
         cost_estimate=cost(flops, flops / 256),
         name="block_term",
     )(acts, weight, *([] if moved is None else [moved]))
@@ -515,7 +515,7 @@
         out_ref[...] = moved_ref[...]
 
 
-def join(rank, moved, terms, slot, first, right):
+def join(rank, moved, terms, slot, first, right, part=0):
     rows, d = moved.shape
     tile = min(128, rows)
     row = pl.BlockSpec((tile, d), lambda i, r: (i, 0))
@@ -524,7 +524,7 @@
         grid_spec=pltpu.PrefetchScalarGridSpec(
             num_scalar_prefetch=1,
             grid=(rows // tile,),
-            in_specs=[row, pl.BlockSpec((1, tile, d), lambda i, r: (slot, i, 0))],
+            in_specs=[row, pl.BlockSpec((1, tile, d), lambda i, r: (slot, i, part))],
             out_specs=row,
         ),
         out_shape=jax.ShapeDtypeStruct((rows, d), BF16),
@@ -640,16 +640,26 @@
     first_all, query, keys, vals = held
 
     grad_own = mixed_grad[0]
-    (right,) = tie([grad_own], block[0])
-    left = right
-    grads_r, grads_l = [right], [left]
-    right, left, _, _ = tick(0, right, left, None)
+    (own_grad,) = tie([grad_own], block[0])
+    right = [own_grad[:, :half], own_grad[:, half:]]
+    left = list(right)
+    grads_r, grads_l = [list(right)], [list(left)]
+
+    def half_tick(k):
+        for p in range(2):
+            if k:
+                right[p] = join(where, right[p], terms, n - k, k, True, p)
+                left[p] = join(where, left[p], terms, k, n - k, False, p)
+            right[p], left[p] = send(right[p], right_line), send(left[p], left_line)
+
+    half_tick(0)
     masked = attend(where, query, keys, vals, docs_col, docs_row, heads_col)
     terms = low(dot_t(flat(masked), output_weight)).reshape(n, rows, d)
     for k in range(1, n):
-        grads_r.append(right)
-        grads_l.append(left)
-        right, left, _, _ = tick(k, right, left, terms)
+        grads_r.append(list(right))
+        grads_l.append(list(left))
+        half_tick(k)
+    right, left = (jnp.concatenate(v, axis=1) for v in (right, left))
     attn = owned(terms, right, left)
     x_rows = own.astype(F32)
     state = x_rows + attn
@@ -663,16 +673,16 @@
             block, *held = tie([block] + list(held), sent)
         after = hop(block) if s < n - 1 else None
         held = mlp_slot(
-            s, n, where, block, [grads_l[s], grads_r[n - s if s else 0]], up_weight, down_weight, bucket_col, held
+            s, n, where, block, grads_l[s] + grads_r[n - s if s else 0], up_weight, down_weight, bucket_col, held
         )
         if s >= 1:
             fused = moved if s == n - 1 and s > 1 else None
-            sent = block_term(held[1], s, up_weight, 2 * rows * d * hidden, fused)
+            sent = block_term(held[1], s, up_weight, 2 * rows * d * hidden, fused, 16)
             if s > 1 and fused is None:
                 sent = add(sent, moved)
             moved = hop(sent)
         else:
-            sent = term0 = block_term(held[1], 0, up_weight, 2 * rows * d * hidden)
+            sent = term0 = block_term(held[1], 0, up_weight, 2 * rows * d * hidden, None, 16)
         block = after
     active, grad_upper, second_all, grad_all = held
     grad_all, active, second_all, grad_upper = tie([grad_all, active, second_all, grad_upper], sent)

time: 559 us -> 566 us (1.013)
  Pallas kernels: 192 us -> 214 us
  waiting for transfers between devices: 158 us -> 138 us
  starting transfers between devices: 100 us -> 116 us
  local copies, waits for them, and re-layouts: 40.9 us -> 28.9 us
    ppermute x34 -> x42, waiting for transfers between devices: 158 us -> 137 us  [per_device(): send = lambda v, pairs: lax.ppermute(v, 'mp', pairs)]
    ppermute x34 -> x42, starting transfers between devices: 95 us -> 110 us  [per_device(): send = lambda v, pairs: lax.ppermute(v, 'mp', pairs)]
    unnamed x167 -> x163, local copies, waits for them, and re-layouts: 29.6 us -> 16.2 us
    pallas_call x8, Pallas kernels: 23.7 us -> 36.2 us  [block_term(): pl.pallas_call(term_body, grid=(d // tile,), in_specs=[pl.BlockSpec((1, r...]
    pallas_call x12 -> x18, Pallas kernels: 15.2 us -> 20.1 us  [join(): pl.pallas_call(functools.partial(join_body, 0 if right else -1, first), g...]
  transfers between devices with their start and end apart: 45 -> 53, of which waited for: 24 -> 24; matrix products, arithmetic and copies ran while one was open for 9% -> 9% of each run, Pallas kernels for 34% -> 38%
where the time goes in v7:
time: 566 us; the launch traced here: 556 us
  Pallas kernels  214 us (38%)
  waiting for transfers between devices  138 us (24%)
  starting transfers between devices  116 us (20%)
  other arithmetic  29.2 us (5%)
  local copies, waits for them, and re-layouts  28.9 us (5%)
  between operations  15.9 us (3%)
  matrix products  15.6 us (3%)
    ppermute x42, waiting for transfers between devices, per_device(): send = lambda v, pairs: lax.ppermute(v, 'mp', pairs)  137 us
    ppermute x42, starting transfers between devices, per_device(): send = lambda v, pairs: lax.ppermute(v, 'mp', pairs)  110 us
    pallas_call x4, Pallas kernels, mlp_slot(): pl.pallas_call(functools.partial(mlp_body, slot, n), grid_spec=pltpu.Pref...  39.3 us
    pallas_call x8, Pallas kernels, block_term(): pl.pallas_call(term_body, grid=(d // tile,), in_specs=[pl.BlockSpec((1, r...  36.2 us
    pallas_call x4, Pallas kernels, grad_half(): pl.pallas_call(functools.partial(grad_body, not partner), grid_spec=pltpu...  29.6 us
    pallas_call x4, Pallas kernels, qkv_slot(): pl.pallas_call(qkv_body, grid_spec=pltpu.PrefetchScalarGridSpec(num_scala...  28.7 us
    pallas_call x2, Pallas kernels, attn_grads(): pl.pallas_call(functools.partial(attn_grad_body, partner), grid_spec=pltp...  26.2 us
    pallas_call x18, Pallas kernels, join(): pl.pallas_call(functools.partial(join_body, 0 if right else -1, first), g...  20.1 us
  transfers between devices with their start and end apart: 53, of which 24 were waited for; matrix products, arithmetic and copies ran while one was open for 9% of the time, Pallas kernels for 38%

profile of v7, /device:TPU:0, one launch (start us, length us, event | category | flops | bytes accessed | tf_op | source)
XLA Modules:
  0.0 556.5 jit_solution(5230205756133265334)
XLA Ops:
  8.5 5.1 collective-permute-start
  17.9 7.1 %qkv_slot.4 = (bf16[4,256,2048]{2,1,0:T(8,128)(2,1)}, bf16[4,256,512]{2,1,0:T(8,128)(2,1)}, bf16[4,256,512]{2,1,0:T(8,128)(2,1)}, bf16[4,256,512]{2,1,0:T(8,128)(2,1)}) custom-call(s32[4]{0:T(128)} %pad_add_fusion.rank_ref, bf16[256,1024]{1,0:T(8,128)(2,1)} %copy-done.59, bf16[256,1024]{1,0:T(8,128)(2,1)} %copy-done.58, f32[1,2048]{1,0:T(1,128)} %bitcast.94, ...), custom_call_target="tpu_custom_call" | custom-call | flops 1610612736 | bytes 8388608 | tf_op jit(solution)/shard_map/qkv_slot/pallas_call | solution.py:106
  26.0 4.4 collective-permute-start.1
  30.3 6.8 %collective-permute-done.2.xb_ref = bf16[256,1024]{1,0:T(8,128)(2,1)S(1)} collective-permute-done((bf16[256,1024]{1,0:T(8,128)(2,1)S(1)}, bf16[256,1024]{1,0:T(8,128)(2,1)S(1)}, u32[]{:S(2)}, u32[]{:S(2)}) %collective-permute-start.2) | collective-permute-done | bytes 524320 | tf_op jit(solution)/shard_map/ppermute | solution.py:596
  41.5 7.1 %qkv_slot.5 = (bf16[4,256,2048]{2,1,0:T(8,128)(2,1)}, bf16[4,256,512]{2,1,0:T(8,128)(2,1)}, bf16[4,256,512]{2,1,0:T(8,128)(2,1)}, bf16[4,256,512]{2,1,0:T(8,128)(2,1)}) custom-call(s32[4]{0:T(128)} %pad_add_fusion.rank_ref, ...), custom_call_target="tpu_custom_call", output_to_operand_aliasing={{0}: (10, {}), {1}: (11, {}), {2}: (12, {}), {3}: (13, {})} | custom-call | flops 1610612736 | bytes 8388608 | tf_op jit(solution)/shard_map/qkv_slot/pallas_call | solution.py:106
  52.7 7.0 %collective-permute-done.4.xb_ref = bf16[256,1024]{1,0:T(8,128)(2,1)S(1)} collective-permute-done((bf16[256,1024]{1,0:T(8,128)(2,1)S(1)}, bf16[256,1024]{1,0:T(8,128)(2,1)S(1)}, u32[]{:S(2)}, u32[]{:S(2)}) %collective-permute-start.4) | collective-permute-done | bytes 524320 | tf_op jit(solution)/shard_map/ppermute | solution.py:596
  68.1 7.3 %qkv_slot.6 = (bf16[4,256,2048]{2,1,0:T(8,128)(2,1)}, bf16[4,256,512]{2,1,0:T(8,128)(2,1)}, bf16[4,256,512]{2,1,0:T(8,128)(2,1)}, bf16[4,256,512]{2,1,0:T(8,128)(2,1)}) custom-call(s32[4]{0:T(128)} %pad_add_fusion.rank_ref, bf16[256,1024]{1,0:T(8,128)(2,1)} %copy-done.64, ...), custom_call_target="tpu_custom_call", output_to_operand_aliasing={{0}: (10, {}), {1}: (11, {}), {2}: (12, {}), {3}: (13, {})} | custom-call | flops 1610612736 | bytes 8388608 | tf_op jit(solution)/shard_map/qkv_slot/pallas_call | solution.py:106
  78.1 5.4 collective-permute-start.10
  85.0 7.1 %qkv_slot.7 = (bf16[4,256,2048]{2,1,0:T(8,128)(2,1)}, bf16[4,256,512]{2,1,0:T(8,128)(2,1)}, bf16[4,256,512]{2,1,0:T(8,128)(2,1)}, bf16[4,256,512]{2,1,0:T(8,128)(2,1)}) custom-call(s32[4]{0:T(128)} %pad_add_fusion.rank_ref, bf16[256,1024]{1,0:T(8,128)(2,1)} %copy-done.63, ...), custom_call_target="tpu_custom_call", output_to_operand_aliasing={{0}: (10, {}), {1}: (11, {}), {2}: (12, {}), {3}: (13, {})} | custom-call | flops 1610612736 | bytes 8388608 | tf_op jit(solution)/shard_map/qkv_slot/pallas_call | solution.py:106
  92.1 10.3 %attend.1 = bf16[4,256,512]{2,1,0:T(8,128)(2,1)} custom-call(s32[4]{0:T(128)} %pad_add_fusion.rank_ref, bf16[4,256,512]{2,1,0:T(8,128)(2,1)} %get-tuple-element.173.q_ref, bf16[4,256,512]{2,1,0:T(8,128)(2,1)} %get-tuple-element.174.k_ref, bf16[4,256,512]{2,1,0:T(8,128)(2,1)} %get-tuple-element.175.v_ref, s32[4,256,1]{2,1,0:T(8,128)} %reshape.203.dcol_ref, ...), custom_call_target="tpu_custom_call" | custom-call | flops 2147483648 | bytes 4194304 | tf_op jit(solution)/shard_map/attend/pallas_call | solution.py:169
  102.4 4.3 convolution_convert_fusion.1
  107.5 4.6 collective-permute-start.7
  125.2 4.4 collective-permute-start.8
  129.7 6.0 %collective-permute-done.11.moved_ref.grb_ref = bf16[256,1024]{1,0:T(8,128)(2,1)S(1)} collective-permute-done((bf16[256,1024]{1,0:T(8,128)(2,1)S(1)}, bf16[256,1024]{1,0:T(8,128)(2,1)S(1)}, u32[]{:S(2)}, u32[]{:S(2)}) %collective-permute-start.11) | collective-permute-done | bytes 524320 | tf_op jit(solution)/shard_map/ppermute | solution.py:596
  136.5 4.4 collective-permute-start.12
  147.8 5.3 collective-permute-start.9
  153.1 5.1 collective-permute-done.12.moved_ref.grb_ref
  159.0 4.4 collective-permute-start.13
  169.7 6.6 %collective-permute-done.13 = bf16[256,1024]{1,0:T(8,128)(2,1)S(1)} collective-permute-done((bf16[256,1024]{1,0:T(8,128)(2,1)S(1)}, bf16[256,1024]{1,0:T(8,128)(2,1)S(1)}, u32[]{:S(2)}, u32[]{:S(2)}) %collective-permute-start.13) | collective-permute-done | bytes 524320 | tf_op jit(solution)/shard_map/ppermute | solution.py:596
  180.4 5.6 %collective-permute-done.21 = bf16[256,1024]{1,0:T(8,128)(2,1)S(1)} collective-permute-done((bf16[256,1024]{1,0:T(8,128)(2,1)S(1)}, bf16[256,1024]{1,0:T(8,128)(2,1)S(1)}, u32[]{:S(2)}, u32[]{:S(2)}) %collective-permute-start.21) | collective-permute-done | bytes 524320 | tf_op jit(solution)/shard_map/ppermute | solution.py:596
  190.5 9.3 %mlp_slot.4 = (bf16[4,256,2048]{2,1,0:T(8,128)(2,1)S(1)}, bf16[4,256,2048]{2,1,0:T(8,128)(2,1)S(1)}, bf16[4,256,2048]{2,1,0:T(8,128)(2,1)S(1)}, bf16[4,256,2048]{2,1,0:T(8,128)(2,1)S(1)}) custom-call(s32[4]{0:T(128)S(1)} %copy-done.37, bf16[256,2048]{1,0:T(8,128)(2,1)S(1)} %add_convert_fusion.4.a_ref, ...), custom_call_target="tpu_custom_call" | custom-call | flops 4294967296 | bytes 20971520 | tf_op jit(solution)/shard_map/mlp_slot/pallas_call | solution.py:303
  207.2 4.4 collective-permute-done.22.a_ref
  211.8 10.3 %mlp_slot.5 = (bf16[4,256,2048]{2,1,0:T(8,128)(2,1)S(1)}, bf16[4,256,2048]{2,1,0:T(8,128)(2,1)S(1)}, bf16[4,256,2048]{2,1,0:T(8,128)(2,1)S(1)}, bf16[4,256,2048]{2,1,0:T(8,128)(2,1)S(1)}) custom-call(s32[4]{0:T(128)S(1)} %copy-done.37, ...), custom_call_target="tpu_custom_call", output_to_operand_aliasing={{0}: (9, {}), {1}: (10, {}), {2}: (11, {}), {3}: (12, {})} | custom-call | flops 4294967296 | bytes 20971520 | tf_op jit(solution)/shard_map/mlp_slot/pallas_call | solution.py:303
  228.2 9.9 %collective-permute-done.23.a_ref = bf16[256,2048]{1,0:T(8,128)(2,1)} collective-permute-done((bf16[256,2048]{1,0:T(8,128)(2,1)}, bf16[256,2048]{1,0:T(8,128)(2,1)}, u32[]{:S(2)}, u32[]{:S(2)}) %collective-permute-start.23) | collective-permute-done | bytes 1048608 | tf_op jit(solution)/shard_map/ppermute | solution.py:596
  240.0 9.6 %mlp_slot.6 = (bf16[4,256,2048]{2,1,0:T(8,128)(2,1)S(1)}, bf16[4,256,2048]{2,1,0:T(8,128)(2,1)S(1)}, bf16[4,256,2048]{2,1,0:T(8,128)(2,1)S(1)}, bf16[4,256,2048]{2,1,0:T(8,128)(2,1)S(1)}) custom-call(s32[4]{0:T(128)S(1)} %copy-done.37, ...), custom_call_target="tpu_custom_call", output_to_operand_aliasing={{0}: (9, {}), {1}: (10, {}), {2}: (11, {}), {3}: (12, {})} | custom-call | flops 4294967296 | bytes 20971520 | tf_op jit(solution)/shard_map/mlp_slot/pallas_call | solution.py:303
  252.8 7.6 %collective-permute-done.25 = bf16[256,2048]{1,0:T(8,128)(2,1)S(1)} collective-permute-done((bf16[256,2048]{1,0:T(8,128)(2,1)}, bf16[256,2048]{1,0:T(8,128)(2,1)S(1)}, u32[]{:S(2)}, u32[]{:S(2)}) %collective-permute-start.25) | collective-permute-done | bytes 1048608 | tf_op jit(solution)/shard_map/ppermute | solution.py:596
  262.8 20.1 %collective-permute-done.24.a_ref = bf16[256,2048]{1,0:T(8,128)(2,1)S(1)} collective-permute-done((bf16[256,2048]{1,0:T(8,128)(2,1)}, bf16[256,2048]{1,0:T(8,128)(2,1)S(1)}, u32[]{:S(2)}, u32[]{:S(2)}) %collective-permute-start.24) | collective-permute-done | bytes 1048608 | tf_op jit(solution)/shard_map/ppermute | solution.py:596
  282.9 10.2 %mlp_slot.7 = (bf16[4,256,2048]{2,1,0:T(8,128)(2,1)S(1)}, bf16[4,256,2048]{2,1,0:T(8,128)(2,1)S(1)}, bf16[4,256,2048]{2,1,0:T(8,128)(2,1)S(1)}, bf16[4,256,2048]{2,1,0:T(8,128)(2,1)S(1)}) custom-call(s32[4]{0:T(128)S(1)} %copy-done.37, ...), custom_call_target="tpu_custom_call", output_to_operand_aliasing={{0}: (9, {}), {1}: (10, {}), {2}: (11, {}), {3}: (12, {})} | custom-call | flops 4294967296 | bytes 20971520 | tf_op jit(solution)/shard_map/mlp_slot/pallas_call | solution.py:303
  293.1 6.1 %collective-permute-done.26.rest_0_ = bf16[256,2048]{1,0:T(8,128)(2,1)S(1)} collective-permute-done((bf16[256,2048]{1,0:T(8,128)(2,1)S(1)}, bf16[256,2048]{1,0:T(8,128)(2,1)S(1)}, u32[]{:S(2)}, u32[]{:S(2)}) %collective-permute-start.26) | collective-permute-done | bytes 1048608 | tf_op jit(solution)/shard_map/ppermute | solution.py:596
  302.9 7.2 %grad_half.4 = bf16[2048,1024]{1,0:T(8,128)(2,1)} custom-call(s32[4]{0:T(128)S(1)} %copy-done.37, bf16[1024,2048]{1,0:T(8,128)(2,1)S(1)} %bitcast.88, bf16[1024,2048]{1,0:T(8,128)(2,1)S(1)} %bitcast.83), custom_call_target="tpu_custom_call" | custom-call | flops 1000000 | bytes 1000000 | tf_op jit(solution)/shard_map/grad_half/pallas_call | solution.py:413
  310.1 7.2 %grad_half.5 = bf16[2048,1024]{1,0:T(8,128)(2,1)} custom-call(s32[4]{0:T(128)S(1)} %copy-done.37, bf16[1024,2048]{1,0:T(8,128)(2,1)S(1)} %bitcast.86, bf16[1024,2048]{1,0:T(8,128)(2,1)S(1)} %bitcast.71), custom_call_target="tpu_custom_call" | custom-call | flops 1000000 | bytes 1000000 | tf_op jit(solution)/shard_map/grad_half/pallas_call | solution.py:413
  330.1 11.3 %convolution_convert_fusion = bf16[1024,2048]{1,0:T(8,128)(2,1)S(1)} fusion(bf16[1024,2048]{1,0:T(8,128)(2,1)S(1)} %bitcast.84, bf16[2048,2048]{1,0:T(8,128)(2,1)} %down_ref.7), kind=kOutput, calls=%fused_computation | convolution fusion | flops 8592031744 | bytes 16777216 | tf_op jit(solution)/shard_map/dot_general | solution.py:53
  341.4 8.0 %grad_half.6.rest_1_ = bf16[2,2048,1024]{2,1,0:T(8,128)(2,1)S(1)} custom-call(s32[4]{0:T(128)S(1)} %copy-done.37, bf16[1024,2048]{1,0:T(8,128)(2,1)S(1)} %bitcast.89, bf16[1024,2048]{1,0:T(8,128)(2,1)S(1)} %bitcast.85, bf16[2048,1024]{1,0:T(8,128)(2,1)} %collective-permute-done.29.rest_0_), custom_call_target="tpu_custom_call" | custom-call | flops 1000000 | bytes 1000000 | tf_op jit(solution)/shard_map/grad_half/pallas_call | solution.py:413
  351.2 5.5 collective-permute-start.30
  359.5 7.2 %grad_half.7 = bf16[2,2048,1024]{2,1,0:T(8,128)(2,1)S(1)} custom-call(s32[4]{0:T(128)S(1)} %copy-done.37, bf16[1024,2048]{1,0:T(8,128)(2,1)S(1)} %bitcast.87, bf16[1024,2048]{1,0:T(8,128)(2,1)S(1)} %bitcast.72, bf16[2048,1024]{1,0:T(8,128)(2,1)} %collective-permute-done.32.rest_0_, ...), custom_call_target="tpu_custom_call", output_to_operand_aliasing={{}: (4, {})} | custom-call | flops 1000000 | bytes 1000000 | tf_op jit(solution)/shard_map/grad_half/pallas_call | solution.py:413
  370.1 4.6 collective-permute-done.30.moved_ref.refs_2_
  378.8 5.0 collective-permute-start.33
  391.3 10.5 %collective-permute-done.33.moved_ref.refs_1_ = bf16[256,2048]{1,0:T(8,128)(2,1)S(1)} collective-permute-done((bf16[256,2048]{1,0:T(8,128)(2,1)S(1)}, bf16[256,2048]{1,0:T(8,128)(2,1)S(1)}, u32[]{:S(2)}, u32[]{:S(2)}) %collective-permute-start.33) | collective-permute-done | bytes 1048608 | tf_op jit(solution)/shard_map/ppermute | solution.py:596
  402.7 4.5 collective-permute-start.34
  413.3 14.4 %attend_back.1.x_ref = bf16[4,256,1536]{2,1,0:T(8,128)(2,1)S(1)} custom-call(s32[4]{0:T(128)S(1)} %copy-done.37, bf16[4,256,512]{2,1,0:T(8,128)(2,1)S(1)} %copy-done.11, bf16[4,256,512]{2,1,0:T(8,128)(2,1)S(1)} %copy-done.12, bf16[4,256,512]{2,1,0:T(8,128)(2,1)S(1)} %copy-done.13, bf16[4,256,512]{2,1,0:T(8,128)(2,1)S(1)} %get-tuple-element.225.do_ref, ...), custom_call_target="tpu_custom_call" | custom-call | flops 115999997952 | bytes 7340032 | tf_op jit(solution)/shard_map/attend_back/pallas_call | solution.py:251
  431.7 5.8 %block_term.12 = bf16[256,2048]{1,0:T(8,128)(2,1)} custom-call(bf16[4,256,1536]{2,1,0:T(8,128)(2,1)} %copy-done.1, bf16[2048,1536]{1,0:T(8,128)(2,1)} %copy-done.44), custom_call_target="tpu_custom_call" | custom-call | flops 1000000 | bytes 3906 | tf_op jit(solution)/shard_map/block_term/pallas_call | solution.py:490
  437.4 13.3 %attn_grads.2 = bf16[2048,1024]{1,0:T(8,128)(2,1)} custom-call(s32[4]{0:T(128)} %pad_add_fusion.rank_ref, bf16[1024,2048]{1,0:T(8,128)(2,1)} %bitcast.101, bf16[1024,2048]{1,0:T(8,128)(2,1)} %bitcast.90, bf16[1024,1536]{1,0:T(8,128)(2,1)} %bitcast.73, bf16[1024,1536]{1,0:T(8,128)(2,1)} %bitcast.74, bf16[1024,512]{1,0:T(8,128)(2,1)} %bitcast.105), custom_call_target="tpu_custom_call" | custom-call | flops 4000000000 | bytes 1000000 | tf_op jit(solution)/shard_map/attn_grads/pallas_call | solution.py:456
  454.1 5.8 %block_term.13 = bf16[256,2048]{1,0:T(8,128)(2,1)} custom-call(bf16[4,256,1536]{2,1,0:T(8,128)(2,1)} %copy-done.1, bf16[2048,1536]{1,0:T(8,128)(2,1)} %copy-done.44), custom_call_target="tpu_custom_call" | custom-call | flops 1000000 | bytes 3906 | tf_op jit(solution)/shard_map/block_term/pallas_call | solution.py:490
  459.9 12.9 %attn_grads.3 = bf16[2048,1024]{1,0:T(8,128)(2,1)} custom-call(s32[4]{0:T(128)} %pad_add_fusion.rank_ref, bf16[1024,2048]{1,0:T(8,128)(2,1)} %bitcast.102, bf16[1024,2048]{1,0:T(8,128)(2,1)} %bitcast.91, bf16[1024,1536]{1,0:T(8,128)(2,1)} %bitcast.75, bf16[1024,1536]{1,0:T(8,128)(2,1)} %bitcast.76, bf16[1024,512]{1,0:T(8,128)(2,1)} %bitcast.106, ...), custom_call_target="tpu_custom_call" | custom-call | flops 1000000 | bytes 1000000 | tf_op jit(solution)/shard_map/attn_grads/pallas_call | solution.py:456
  479.7 4.4 collective-permute-start.40
  484.1 5.8 %block_term.14 = bf16[256,2048]{1,0:T(8,128)(2,1)} custom-call(bf16[4,256,1536]{2,1,0:T(8,128)(2,1)} %copy-done.1, bf16[2048,1536]{1,0:T(8,128)(2,1)} %copy-done.44), custom_call_target="tpu_custom_call" | custom-call | flops 1000000 | bytes 3906 | tf_op jit(solution)/shard_map/block_term/pallas_call | solution.py:490
  489.9 5.8 %block_term.15.term_ref = bf16[256,2048]{1,0:T(8,128)(2,1)} custom-call(bf16[4,256,1536]{2,1,0:T(8,128)(2,1)} %copy-done.1, bf16[2048,1536]{1,0:T(8,128)(2,1)} %copy-done.44), custom_call_target="tpu_custom_call" | custom-call | flops 1000000 | bytes 3906 | tf_op jit(solution)/shard_map/block_term/pallas_call | solution.py:490
  523.2 16.7 %collective-permute-done.42.moved_ref = bf16[256,2048]{1,0:T(8,128)(2,1)S(1)} collective-permute-done((bf16[256,2048]{1,0:T(8,128)(2,1)S(1)}, bf16[256,2048]{1,0:T(8,128)(2,1)S(1)}, u32[]{:S(2)}, u32[]{:S(2)}) %collective-permute-start.42) | collective-permute-done | bytes 1048608 | tf_op jit(solution)/shard_map/ppermute | solution.py:596
  (324 shorter events, 178.9 us)
Async XLA Ops:
  7.2 465.6 %reduce-scatter.3.cloned.1.call-start = ((), (), s32[]{:S(2)}) async-start(), calls=%async_computation.2 | async-start | bytes 10485760 | tf_op jit(solution)/shard_map/reduce_scatter | solution.py:717
  8.5 17.4 %collective-permute-start = (bf16[256,1024]{1,0:T(8,128)(2,1)S(1)}, bf16[256,1024]{1,0:T(8,128)(2,1)}, u32[]{:S(2)}, u32[]{:S(2)}) collective-permute-start(bf16[256,1024]{1,0:T(8,128)(2,1)S(1)} %get-tuple-element.279.xa_ref), channel_id=1, source_target_pairs={{0,3},{1,0},{2,1},{3,2},{4,7},{5,4},{6,5},{7,6},{8,11},{9,8},{10,9... | collective-permute-start | bytes 1572872 | tf_op jit(solution)/shard_map/ppermute | solution.py:596
  13.6 23.6 %collective-permute-start.2 = (bf16[256,1024]{1,0:T(8,128)(2,1)S(1)}, bf16[256,1024]{1,0:T(8,128)(2,1)S(1)}, u32[]{:S(2)}, u32[]{:S(2)}) collective-permute-start(bf16[256,1024]{1,0:T(8,128)(2,1)S(1)} %get-tuple-element.278.xb_ref), channel_id=1, source_target_pairs={{0,3},{1,0},{2,1},{3,2},{4,7},{5,4},{6,5},{7,6},{8,11},{9,8},{10,9... | collective-permute-start | bytes 1572872 | tf_op jit(solution)/shard_map/ppermute | solution.py:596
  26.0 22.7 %collective-permute-start.1 = (bf16[256,1024]{1,0:T(8,128)(2,1)}, bf16[256,1024]{1,0:T(8,128)(2,1)S(1)}, u32[]{:S(2)}, u32[]{:S(2)}) collective-permute-start(bf16[256,1024]{1,0:T(8,128)(2,1)} %collective-permute-done.xa_ref), channel_id=1, source_target_pairs={{0,3},{1,0},{2,1},{3,2},{4,7},{5,4},{6,5},{7,6},{8,11},{9,8},{10,9... | collective-permute-start | bytes 1572872 | tf_op jit(solution)/shard_map/ppermute | solution.py:596
  37.2 22.5 %collective-permute-start.4 = (bf16[256,1024]{1,0:T(8,128)(2,1)S(1)}, bf16[256,1024]{1,0:T(8,128)(2,1)S(1)}, u32[]{:S(2)}, u32[]{:S(2)}) collective-permute-start(bf16[256,1024]{1,0:T(8,128)(2,1)S(1)} %collective-permute-done.2.xb_ref), channel_id=1, source_target_pairs={{0,3},{1,0},{2,1},{3,2},{4,7},{5,4},{6,5},{7,6},{8,11},{9,8},{10,9... | collective-permute-start | bytes 1572872 | tf_op jit(solution)/shard_map/ppermute | solution.py:596
  48.6 26.7 %collective-permute-start.3 = (bf16[256,1024]{1,0:T(8,128)(2,1)S(1)}, bf16[256,1024]{1,0:T(8,128)(2,1)S(1)}, u32[]{:S(2)}, u32[]{:S(2)}) collective-permute-start(bf16[256,1024]{1,0:T(8,128)(2,1)S(1)} %collective-permute-done.1.xa_ref), channel_id=1, source_target_pairs={{0,3},{1,0},{2,1},{3,2},{4,7},{5,4},{6,5},{7,6},{8,11},{9,8},{10,9... | collective-permute-start | bytes 1572872 | tf_op jit(solution)/shard_map/ppermute | solution.py:596
  59.7 25.3 %collective-permute-start.5 = (bf16[256,1024]{1,0:T(8,128)(2,1)S(1)}, bf16[256,1024]{1,0:T(8,128)(2,1)}, u32[]{:S(2)}, u32[]{:S(2)}) collective-permute-start(bf16[256,1024]{1,0:T(8,128)(2,1)S(1)} %collective-permute-done.4.xb_ref), channel_id=1, source_target_pairs={{0,3},{1,0},{2,1},{3,2},{4,7},{5,4},{6,5},{7,6},{8,11},{9,8},{10,9... | collective-permute-start | bytes 1572872 | tf_op jit(solution)/shard_map/ppermute | solution.py:596
  75.5 31.3 %collective-permute-start.6 = (bf16[256,1024]{1,0:T(8,128)(2,1)S(1)}, bf16[256,1024]{1,0:T(8,128)(2,1)S(1)}, u32[]{:S(2)}, u32[]{:S(2)}) collective-permute-start(bf16[256,1024]{1,0:T(8,128)(2,1)S(1)} %get-tuple-element.276.gla_ref.gra_ref), channel_id=1, source_target_pairs={{0,1},{1,2},{2,3},{4,5},{5,6},{6,7},{8,9},{9,10},{10,11},{12,13},{... | collective-permute-start | bytes 1572872 | tf_op jit(solution)/shard_map/ppermute | solution.py:596
  76.8 38.9 %collective-permute-start.14 = (bf16[256,1024]{1,0:T(8,128)(2,1)S(1)}, bf16[256,1024]{1,0:T(8,128)(2,1)}, u32[]{:S(2)}, u32[]{:S(2)}) collective-permute-start(bf16[256,1024]{1,0:T(8,128)(2,1)S(1)} %get-tuple-element.276.gla_ref.gra_ref), channel_id=1, source_target_pairs={{1,0},{2,1},{3,2},{5,4},{6,5},{7,6},{9,8},{10,9},{11,10},{13,12},{... | collective-permute-start | bytes 1572872 | tf_op jit(solution)/shard_map/ppermute | solution.py:596
  78.1 34.0 %collective-permute-start.10 = (bf16[256,1024]{1,0:T(8,128)(2,1)S(1)}, bf16[256,1024]{1,0:T(8,128)(2,1)}, u32[]{:S(2)}, u32[]{:S(2)}) collective-permute-start(bf16[256,1024]{1,0:T(8,128)(2,1)S(1)} %get-tuple-element.277.glb_ref.grb_ref), channel_id=1, source_target_pairs={{0,1},{1,2},{2,3},{4,5},{5,6},{6,7},{8,9},{9,10},{10,11},{12,13},{... | collective-permute-start | bytes 1572872 | tf_op jit(solution)/shard_map/ppermute | solution.py:596
  83.5 35.2 %collective-permute-start.18 = (bf16[256,1024]{1,0:T(8,128)(2,1)S(1)}, bf16[256,1024]{1,0:T(8,128)(2,1)}, u32[]{:S(2)}, u32[]{:S(2)}) collective-permute-start(bf16[256,1024]{1,0:T(8,128)(2,1)S(1)} %get-tuple-element.277.glb_ref.grb_ref), channel_id=1, source_target_pairs={{1,0},{2,1},{3,2},{5,4},{6,5},{7,6},{9,8},{10,9},{11,10},{13,12},{... | collective-permute-start | bytes 1572872 | tf_op jit(solution)/shard_map/ppermute | solution.py:596
  107.5 16.9 %collective-permute-start.7 = (bf16[256,1024]{1,0:T(8,128)(2,1)S(1)}, bf16[256,1024]{1,0:T(8,128)(2,1)S(1)}, u32[]{:S(2)}, u32[]{:S(2)}) collective-permute-start(bf16[256,1024]{1,0:T(8,128)(2,1)S(1)} %join.18), channel_id=1, source_target_pairs={{0,1},{1,2},{2,3},{4,5},{5,6},{6,7},{8,9},{9,10},{10,11},{12,13},{... | collective-permute-start | bytes 1572872 | tf_op jit(solution)/shard_map/ppermute | solution.py:596
  113.8 21.9 %collective-permute-start.11 = (bf16[256,1024]{1,0:T(8,128)(2,1)S(1)}, bf16[256,1024]{1,0:T(8,128)(2,1)S(1)}, u32[]{:S(2)}, u32[]{:S(2)}) collective-permute-start(bf16[256,1024]{1,0:T(8,128)(2,1)S(1)} %join.21), channel_id=1, source_target_pairs={{0,1},{1,2},{2,3},{4,5},{5,6},{6,7},{8,9},{9,10},{10,11},{12,13},{... | collective-permute-start | bytes 1572872 | tf_op jit(solution)/shard_map/ppermute | solution.py:596
  117.3 23.6 %collective-permute-start.15 = (bf16[256,1024]{1,0:T(8,128)(2,1)S(1)}, bf16[256,1024]{1,0:T(8,128)(2,1)S(1)}, u32[]{:S(2)}, u32[]{:S(2)}) collective-permute-start(bf16[256,1024]{1,0:T(8,128)(2,1)S(1)} %join.24), channel_id=1, source_target_pairs={{1,0},{2,1},{3,2},{5,4},{6,5},{7,6},{9,8},{10,9},{11,10},{13,12},{... | collective-permute-start | bytes 1572872 | tf_op jit(solution)/shard_map/ppermute | solution.py:596
  120.3 24.4 %collective-permute-start.19 = (bf16[256,1024]{1,0:T(8,128)(2,1)S(1)}, bf16[256,1024]{1,0:T(8,128)(2,1)S(1)}, u32[]{:S(2)}, u32[]{:S(2)}) collective-permute-start(bf16[256,1024]{1,0:T(8,128)(2,1)S(1)} %join.27), channel_id=1, source_target_pairs={{1,0},{2,1},{3,2},{5,4},{6,5},{7,6},{9,8},{10,9},{11,10},{13,12},{... | collective-permute-start | bytes 1572872 | tf_op jit(solution)/shard_map/ppermute | solution.py:596
  125.2 21.7 %collective-permute-start.8 = (bf16[256,1024]{1,0:T(8,128)(2,1)S(1)}, bf16[256,1024]{1,0:T(8,128)(2,1)S(1)}, u32[]{:S(2)}, u32[]{:S(2)}) collective-permute-start(bf16[256,1024]{1,0:T(8,128)(2,1)S(1)} %join.19), channel_id=1, source_target_pairs={{0,1},{1,2},{2,3},{4,5},{5,6},{6,7},{8,9},{9,10},{10,11},{12,13},{... | collective-permute-start | bytes 1572872 | tf_op jit(solution)/shard_map/ppermute | solution.py:596
  136.5 21.7 %collective-permute-start.12 = (bf16[256,1024]{1,0:T(8,128)(2,1)S(1)}, bf16[256,1024]{1,0:T(8,128)(2,1)S(1)}, u32[]{:S(2)}, u32[]{:S(2)}) collective-permute-start(bf16[256,1024]{1,0:T(8,128)(2,1)S(1)} %join.22), channel_id=1, source_target_pairs={{0,1},{1,2},{2,3},{4,5},{5,6},{6,7},{8,9},{9,10},{10,11},{12,13},{... | collective-permute-start | bytes 1572872 | tf_op jit(solution)/shard_map/ppermute | solution.py:596
  141.7 21.7 %collective-permute-start.16 = (bf16[256,1024]{1,0:T(8,128)(2,1)S(1)}, bf16[256,1024]{1,0:T(8,128)(2,1)S(1)}, u32[]{:S(2)}, u32[]{:S(2)}) collective-permute-start(bf16[256,1024]{1,0:T(8,128)(2,1)S(1)} %join.25), channel_id=1, source_target_pairs={{1,0},{2,1},{3,2},{5,4},{6,5},{7,6},{9,8},{10,9},{11,10},{13,12},{... | collective-permute-start | bytes 1572872 | tf_op jit(solution)/shard_map/ppermute | solution.py:596
  145.5 21.6 %collective-permute-start.20 = (bf16[256,1024]{1,0:T(8,128)(2,1)S(1)}, bf16[256,1024]{1,0:T(8,128)(2,1)S(1)}, u32[]{:S(2)}, u32[]{:S(2)}) collective-permute-start(bf16[256,1024]{1,0:T(8,128)(2,1)S(1)} %join.28), channel_id=1, source_target_pairs={{1,0},{2,1},{3,2},{5,4},{6,5},{7,6},{9,8},{10,9},{11,10},{13,12},{... | collective-permute-start | bytes 1572872 | tf_op jit(solution)/shard_map/ppermute | solution.py:596
  147.8 21.9 %collective-permute-start.9 = (bf16[256,1024]{1,0:T(8,128)(2,1)S(1)}, bf16[256,1024]{1,0:T(8,128)(2,1)S(1)}, u32[]{:S(2)}, u32[]{:S(2)}) collective-permute-start(bf16[256,1024]{1,0:T(8,128)(2,1)S(1)} %join.20), channel_id=1, source_target_pairs={{0,1},{1,2},{2,3},{4,5},{5,6},{6,7},{8,9},{9,10},{10,11},{12,13},{... | collective-permute-start | bytes 1572872 | tf_op jit(solution)/shard_map/ppermute | solution.py:596
  159.0 17.3 %collective-permute-start.13 = (bf16[256,1024]{1,0:T(8,128)(2,1)S(1)}, bf16[256,1024]{1,0:T(8,128)(2,1)S(1)}, u32[]{:S(2)}, u32[]{:S(2)}) collective-permute-start(bf16[256,1024]{1,0:T(8,128)(2,1)S(1)} %join.23), channel_id=1, source_target_pairs={{0,1},{1,2},{2,3},{4,5},{5,6},{6,7},{8,9},{9,10},{10,11},{12,13},{... | collective-permute-start | bytes 1572872 | tf_op jit(solution)/shard_map/ppermute | solution.py:596
  164.2 16.2 %collective-permute-start.17 = (bf16[256,1024]{1,0:T(8,128)(2,1)S(1)}, bf16[256,1024]{1,0:T(8,128)(2,1)S(1)}, u32[]{:S(2)}, u32[]{:S(2)}) collective-permute-start(bf16[256,1024]{1,0:T(8,128)(2,1)S(1)} %join.26), channel_id=1, source_target_pairs={{1,0},{2,1},{3,2},{5,4},{6,5},{7,6},{9,8},{10,9},{11,10},{13,12},{... | collective-permute-start | bytes 1572872 | tf_op jit(solution)/shard_map/ppermute | solution.py:596
  167.9 18.1 %collective-permute-start.21 = (bf16[256,1024]{1,0:T(8,128)(2,1)S(1)}, bf16[256,1024]{1,0:T(8,128)(2,1)S(1)}, u32[]{:S(2)}, u32[]{:S(2)}) collective-permute-start(bf16[256,1024]{1,0:T(8,128)(2,1)S(1)} %join.29), channel_id=1, source_target_pairs={{1,0},{2,1},{3,2},{5,4},{6,5},{7,6},{9,8},{10,9},{11,10},{13,12},{... | collective-permute-start | bytes 1572872 | tf_op jit(solution)/shard_map/ppermute | solution.py:596
  188.1 23.5 %collective-permute-start.22 = (bf16[256,2048]{1,0:T(8,128)(2,1)S(1)}, bf16[256,2048]{1,0:T(8,128)(2,1)}, u32[]{:S(2)}, u32[]{:S(2)}) collective-permute-start(bf16[256,2048]{1,0:T(8,128)(2,1)S(1)} %add_convert_fusion.4.a_ref), channel_id=1, source_target_pairs={{0,3},{1,0},{2,1},{3,2},{4,7},{5,4},{6,5},{7,6},{8,11},{9,8},{10,9... | collective-permute-start | bytes 3145736 | tf_op jit(solution)/shard_map/ppermute | solution.py:596
  211.6 26.4 %collective-permute-start.23 = (bf16[256,2048]{1,0:T(8,128)(2,1)}, bf16[256,2048]{1,0:T(8,128)(2,1)}, u32[]{:S(2)}, u32[]{:S(2)}) collective-permute-start(bf16[256,2048]{1,0:T(8,128)(2,1)} %collective-permute-done.22.a_ref), channel_id=1, source_target_pairs={{0,3},{1,0},{2,1},{3,2},{4,7},{5,4},{6,5},{7,6},{8,11},{9,8},{10,9... | collective-permute-start | bytes 3145736 | tf_op jit(solution)/shard_map/ppermute | solution.py:596
  225.9 34.5 %collective-permute-start.25 = (bf16[256,2048]{1,0:T(8,128)(2,1)}, bf16[256,2048]{1,0:T(8,128)(2,1)S(1)}, u32[]{:S(2)}, u32[]{:S(2)}) collective-permute-start(bf16[256,2048]{1,0:T(8,128)(2,1)} %block_term.9), channel_id=1, source_target_pairs={{0,3},{1,0},{2,1},{3,2},{4,7},{5,4},{6,5},{7,6},{8,11},{9,8},{10,9... | collective-permute-start | bytes 3145736 | tf_op jit(solution)/shard_map/ppermute | solution.py:596
  238.1 44.8 %collective-permute-start.24 = (bf16[256,2048]{1,0:T(8,128)(2,1)}, bf16[256,2048]{1,0:T(8,128)(2,1)S(1)}, u32[]{:S(2)}, u32[]{:S(2)}) collective-permute-start(bf16[256,2048]{1,0:T(8,128)(2,1)} %collective-permute-done.23.a_ref), channel_id=1, source_target_pairs={{0,3},{1,0},{2,1},{3,2},{4,7},{5,4},{6,5},{7,6},{8,11},{9,8},{10,9... | collective-permute-start | bytes 3145736 | tf_op jit(solution)/shard_map/ppermute | solution.py:596
  260.8 38.4 %collective-permute-start.26 = (bf16[256,2048]{1,0:T(8,128)(2,1)S(1)}, bf16[256,2048]{1,0:T(8,128)(2,1)S(1)}, u32[]{:S(2)}, u32[]{:S(2)}) collective-permute-start(bf16[256,2048]{1,0:T(8,128)(2,1)S(1)} %add_convert_fusion.3), channel_id=1, source_target_pairs={{0,3},{1,0},{2,1},{3,2},{4,7},{5,4},{6,5},{7,6},{8,11},{9,8},{10,9... | collective-permute-start | bytes 3145736 | tf_op jit(solution)/shard_map/ppermute | solution.py:596
  302.4 18.7 %collective-permute-start.27 = (bf16[256,2048]{1,0:T(8,128)(2,1)S(1)}, bf16[256,2048]{1,0:T(8,128)(2,1)S(1)}, u32[]{:S(2)}, u32[]{:S(2)}) collective-permute-start(bf16[256,2048]{1,0:T(8,128)(2,1)S(1)} %block_term.11), channel_id=1, source_target_pairs={{0,3},{1,0},{2,1},{3,2},{4,7},{5,4},{6,5},{7,6},{8,11},{9,8},{10,9... | collective-permute-start | bytes 3145736 | tf_op jit(solution)/shard_map/ppermute | solution.py:596
  310.0 31.4 %collective-permute-start.29 = (bf16[2048,1024]{1,0:T(8,128)(2,1)}, bf16[2048,1024]{1,0:T(8,128)(2,1)}, u32[]{:S(2)}, u32[]{:S(2)}) collective-permute-start(bf16[2048,1024]{1,0:T(8,128)(2,1)} %grad_half.4), channel_id=1, source_target_pairs={{0,4},{4,0},{8,12},{12,8},{16,20},{20,16},{24,28},{28,24},{1,5},{5... | collective-permute-start | bytes 12582920 | tf_op jit(solution)/shard_map/ppermute | solution.py:617
  317.3 42.2 %collective-permute-start.32 = (bf16[2048,1024]{1,0:T(8,128)(2,1)}, bf16[2048,1024]{1,0:T(8,128)(2,1)}, u32[]{:S(2)}, u32[]{:S(2)}) collective-permute-start(bf16[2048,1024]{1,0:T(8,128)(2,1)} %grad_half.5), channel_id=1, source_target_pairs={{0,4},{4,0},{8,12},{12,8},{16,20},{20,16},{24,28},{28,24},{1,5},{5... | collective-permute-start | bytes 12582920 | tf_op jit(solution)/shard_map/ppermute | solution.py:617
  325.1 24.3 %collective-permute-start.28 = (bf16[256,2048]{1,0:T(8,128)(2,1)S(1)}, bf16[256,2048]{1,0:T(8,128)(2,1)S(1)}, u32[]{:S(2)}, u32[]{:S(2)}) collective-permute-start(bf16[256,2048]{1,0:T(8,128)(2,1)S(1)} %get-tuple-element.215.refs_0_), channel_id=1, source_target_pairs={{0,1},{1,2},{2,3},{4,5},{5,6},{6,7},{8,9},{9,10},{10,11},{12,13},{... | collective-permute-start | bytes 3145736 | tf_op jit(solution)/shard_map/ppermute | solution.py:596
  328.8 27.8 %collective-permute-start.31 = (bf16[256,2048]{1,0:T(8,128)(2,1)S(1)}, bf16[256,2048]{1,0:T(8,128)(2,1)S(1)}, u32[]{:S(2)}, u32[]{:S(2)}) collective-permute-start(bf16[256,2048]{1,0:T(8,128)(2,1)S(1)} %get-tuple-element.215.refs_0_), channel_id=1, source_target_pairs={{1,0},{2,1},{3,2},{5,4},{6,5},{7,6},{9,8},{10,9},{11,10},{13,12},{... | collective-permute-start | bytes 3145736 | tf_op jit(solution)/shard_map/ppermute | solution.py:596
  351.2 23.6 %collective-permute-start.30 = (bf16[256,2048]{1,0:T(8,128)(2,1)}, bf16[256,2048]{1,0:T(8,128)(2,1)}, u32[]{:S(2)}, u32[]{:S(2)}) collective-permute-start(bf16[256,2048]{1,0:T(8,128)(2,1)} %join.30), channel_id=1, source_target_pairs={{0,1},{1,2},{2,3},{4,5},{5,6},{6,7},{8,9},{9,10},{10,11},{12,13},{... | collective-permute-start | bytes 3145736 | tf_op jit(solution)/shard_map/ppermute | solution.py:596
  358.2 25.6 %collective-permute-start.35 = (bf16[256,2048]{1,0:T(8,128)(2,1)}, bf16[256,2048]{1,0:T(8,128)(2,1)}, u32[]{:S(2)}, u32[]{:S(2)}) collective-permute-start(bf16[256,2048]{1,0:T(8,128)(2,1)} %join.31), channel_id=1, source_target_pairs={{1,0},{2,1},{3,2},{5,4},{6,5},{7,6},{9,8},{10,9},{11,10},{13,12},{... | collective-permute-start | bytes 3145736 | tf_op jit(solution)/shard_map/ppermute | solution.py:596
  370.1 172.6 %reduce-scatter.5.cloned.1.call-start = ((), (), s32[]{:S(2)}) async-start(), calls=%async_computation.3 | async-start | bytes 5242880 | tf_op jit(solution)/shard_map/reduce_scatter | solution.py:747
  378.8 23.0 %collective-permute-start.33 = (bf16[256,2048]{1,0:T(8,128)(2,1)S(1)}, bf16[256,2048]{1,0:T(8,128)(2,1)S(1)}, u32[]{:S(2)}, u32[]{:S(2)}) collective-permute-start(bf16[256,2048]{1,0:T(8,128)(2,1)S(1)} %join.32), channel_id=1, source_target_pairs={{0,1},{1,2},{2,3},{4,5},{5,6},{6,7},{8,9},{9,10},{10,11},{12,13},{... | collective-permute-start | bytes 3145736 | tf_op jit(solution)/shard_map/ppermute | solution.py:596
  385.7 22.9 %collective-permute-start.36 = (bf16[256,2048]{1,0:T(8,128)(2,1)S(1)}, bf16[256,2048]{1,0:T(8,128)(2,1)S(1)}, u32[]{:S(2)}, u32[]{:S(2)}) collective-permute-start(bf16[256,2048]{1,0:T(8,128)(2,1)S(1)} %join.34), channel_id=1, source_target_pairs={{1,0},{2,1},{3,2},{5,4},{6,5},{7,6},{9,8},{10,9},{11,10},{13,12},{... | collective-permute-start | bytes 3145736 | tf_op jit(solution)/shard_map/ppermute | solution.py:596
  402.7 26.7 %collective-permute-start.34 = (bf16[256,2048]{1,0:T(8,128)(2,1)S(1)}, bf16[256,2048]{1,0:T(8,128)(2,1)S(1)}, u32[]{:S(2)}, u32[]{:S(2)}) collective-permute-start(bf16[256,2048]{1,0:T(8,128)(2,1)S(1)} %join.33), channel_id=1, source_target_pairs={{0,1},{1,2},{2,3},{4,5},{5,6},{6,7},{8,9},{9,10},{10,11},{12,13},{... | collective-permute-start | bytes 3145736 | tf_op jit(solution)/shard_map/ppermute | solution.py:596
  409.3 22.4 %collective-permute-start.37 = (bf16[256,2048]{1,0:T(8,128)(2,1)S(1)}, bf16[256,2048]{1,0:T(8,128)(2,1)}, u32[]{:S(2)}, u32[]{:S(2)}) collective-permute-start(bf16[256,2048]{1,0:T(8,128)(2,1)S(1)} %join.35), channel_id=1, source_target_pairs={{1,0},{2,1},{3,2},{5,4},{6,5},{7,6},{9,8},{10,9},{11,10},{13,12},{... | collective-permute-start | bytes 3145736 | tf_op jit(solution)/shard_map/ppermute | solution.py:596
  450.7 26.4 %collective-permute-start.38 = (bf16[256,2048]{1,0:T(8,128)(2,1)S(1)}, bf16[256,2048]{1,0:T(8,128)(2,1)}, u32[]{:S(2)}, u32[]{:S(2)}) collective-permute-start(bf16[256,2048]{1,0:T(8,128)(2,1)S(1)} %copy-done.56), channel_id=1, source_target_pairs={{0,3},{1,0},{2,1},{3,2},{4,7},{5,4},{6,5},{7,6},{8,11},{9,8},{10,9... | collective-permute-start | bytes 3145736 | tf_op jit(solution)/shard_map/ppermute | solution.py:596
  479.7 33.6 %collective-permute-start.40 = (bf16[256,2048]{1,0:T(8,128)(2,1)}, bf16[256,2048]{1,0:T(8,128)(2,1)}, u32[]{:S(2)}, u32[]{:S(2)}) collective-permute-start(bf16[256,2048]{1,0:T(8,128)(2,1)} %add_convert_fusion.1), channel_id=1, source_target_pairs={{0,3},{1,0},{2,1},{3,2},{4,7},{5,4},{6,5},{7,6},{8,11},{9,8},{10,9... | collective-permute-start | bytes 3145736 | tf_op jit(solution)/shard_map/ppermute | solution.py:596
  498.1 12.5 %collective-permute-start.41 = (bf16[2,256,1024]{2,1,0:T(8,128)(2,1)}, bf16[2,256,1024]{2,1,0:T(8,128)(2,1)}, u32[]{:S(2)}, u32[]{:S(2)}) collective-permute-start(bf16[2,256,1024]{2,1,0:T(8,128)(2,1)} %constant_dynamic-slice_fusion.1), channel_id=1, source_target_pairs={{0,4},{4,0},{8,12},{12,8},{16,20},{20,16},{24,28},{28,24},{1,5},{5... | collective-permute-start | bytes 3145736 | tf_op jit(solution)/shard_map/ppermute | solution.py:617
  506.5 9.8 %collective-permute-start.44 = (f32[8320]{0:T(1024)S(1)}, f32[8320]{0:T(1024)S(1)}, u32[]{:S(2)}, u32[]{:S(2)}) collective-permute-start(f32[8320]{0:T(1024)S(1)} %add.141), channel_id=1, source_target_pairs={{0,1},{1,2},{2,3},{3,0},{4,5},{5,6},{6,7},{7,4},{8,9},{9,10},{10,1... | collective-permute-start | bytes 99848 | tf_op jit(solution)/shard_map/ppermute | solution.py:596
  515.6 24.3 %collective-permute-start.42 = (bf16[256,2048]{1,0:T(8,128)(2,1)S(1)}, bf16[256,2048]{1,0:T(8,128)(2,1)S(1)}, u32[]{:S(2)}, u32[]{:S(2)}) collective-permute-start(bf16[256,2048]{1,0:T(8,128)(2,1)S(1)} %add_convert_fusion), channel_id=1, source_target_pairs={{0,3},{1,0},{2,1},{3,2},{4,7},{5,4},{6,5},{7,6},{8,11},{9,8},{10,9... | collective-permute-start | bytes 3145736 | tf_op jit(solution)/shard_map/ppermute | solution.py:596
  516.3 26.3 %collective-permute-start.47 = (f32[8320]{0:T(1024)S(1)}, f32[8320]{0:T(1024)S(1)}, u32[]{:S(2)}, u32[]{:S(2)}) collective-permute-start(f32[8320]{0:T(1024)S(1)} %add_add_fusion.2), channel_id=1, source_target_pairs={{0,8},{4,12},{8,16},{12,20},{16,24},{20,28},{24,0},{28,4},{1,9},{5... | collective-permute-start | bytes 99848 | tf_op jit(solution)/shard_map/ppermute | solution.py:792
  517.9 24.7 %collective-permute-start.48 = (f32[8320]{0:T(1024)S(1)}, f32[8320]{0:T(1024)S(1)}, u32[]{:S(2)}, u32[]{:S(2)}) collective-permute-start(f32[8320]{0:T(1024)S(1)} %add_add_fusion.2), channel_id=1, source_target_pairs={{0,16},{4,20},{8,24},{12,28},{16,0},{20,4},{24,8},{28,12},{1,17},{... | collective-permute-start | bytes 99848 | tf_op jit(solution)/shard_map/ppermute | solution.py:792
  520.4 22.2 %collective-permute-start.49 = (f32[8320]{0:T(1024)S(1)}, f32[8320]{0:T(1024)S(1)}, u32[]{:S(2)}, u32[]{:S(2)}) collective-permute-start(f32[8320]{0:T(1024)S(1)} %add_add_fusion.2), channel_id=1, source_target_pairs={{0,24},{4,28},{8,0},{12,4},{16,8},{20,12},{24,16},{28,20},{1,25},{... | collective-permute-start | bytes 99848 | tf_op jit(solution)/shard_map/ppermute | solution.py:792
  (85 other events, 744.4 us)
Sparse Core Ops, SparseCore 0:
  370.2 86.7 reduce-scatter.2
  473.0 54.4 reduce-scatter.4

commit v8 on v7

--- a/solution.py
+++ b/solution.py
@@ -448,7 +448,7 @@
 def attn_grads(act, states, dqkv, om, rank, moved=None):
     t, d = act.shape
     local = om.shape[1]
-    tile = min(256, d)
+    tile = min(512, d)
     partner = moved is None
     pos = (lambda r: 1 - r[3]) if partner else (lambda r: r[3])
     col = pl.BlockSpec((t, tile), lambda j, r: (0, j))
@@ -469,7 +469,7 @@
             out_specs=out,
         ),
         out_shape=jax.ShapeDtypeStruct((d, 2 * local), BF16),
-        compiler_params=params(62),
+        compiler_params=params(28 if partner else 50),
         cost_estimate=cost(4e9 if partner else 1e6, 1e6),
         name="attn_grads",
     )(rank, act, states, dqkv, dqkv, om, *([] if partner else [moved]))
@@ -482,7 +482,7 @@
     rest[-1][...] = out.astype(BF16)
 
 
-def block_term(acts, slot, weight, flops, moved=None, mib=62):
+def block_term(acts, slot, weight, flops, moved=None, mib=16):
     _, rows, k = acts.shape
     d = weight.shape[0]
     tile = min(512, d)

time: 566 us -> 550 us (0.972)
  Pallas kernels: 214 us -> 193 us
    pallas_call x8, Pallas kernels: 36.2 us -> 23.7 us  [block_term(): pl.pallas_call(term_body, grid=(d // tile,), in_specs=[pl.BlockSpec((1, r...]
    pallas_call x2, Pallas kernels: 26.2 us -> 17.9 us  [attn_grads(): pl.pallas_call(functools.partial(attn_grad_body, partner), grid_spec=pltp...]
    unnamed x163 -> x185, local copies, waits for them, and re-layouts: 16.2 us -> 22.1 us
  transfers between devices with their start and end apart: 53 -> 53, of which waited for: 24 -> 26; matrix products, arithmetic and copies ran while one was open for 9% -> 9% of each run, Pallas kernels for 38% -> 35%
where the time goes in v8:
time: 550 us; the launch traced here: 541 us
  Pallas kernels  193 us (35%)
  waiting for transfers between devices  139 us (25%)
  starting transfers between devices  117 us (21%)
  local copies, waits for them, and re-layouts  33.5 us (6%)
  other arithmetic  27.3 us (5%)
  between operations  16.1 us (3%)
  matrix products  15.6 us (3%)
    ppermute x42, waiting for transfers between devices, per_device(): send = lambda v, pairs: lax.ppermute(v, 'mp', pairs)  137 us
    ppermute x42, starting transfers between devices, per_device(): send = lambda v, pairs: lax.ppermute(v, 'mp', pairs)  111 us
    pallas_call x4, Pallas kernels, mlp_slot(): pl.pallas_call(functools.partial(mlp_body, slot, n), grid_spec=pltpu.Pref...  39.3 us
    pallas_call x4, Pallas kernels, grad_half(): pl.pallas_call(functools.partial(grad_body, not partner), grid_spec=pltpu...  29.6 us
    pallas_call x4, Pallas kernels, qkv_slot(): pl.pallas_call(qkv_body, grid_spec=pltpu.PrefetchScalarGridSpec(num_scala...  28.7 us
    pallas_call x8, Pallas kernels, block_term(): pl.pallas_call(term_body, grid=(d // tile,), in_specs=[pl.BlockSpec((1, r...  23.7 us
    unnamed x185, local copies, waits for them, and re-layouts  22.1 us
    pallas_call x18, Pallas kernels, join(): pl.pallas_call(functools.partial(join_body, 0 if right else -1, first), g...  20 us
  transfers between devices with their start and end apart: 53, of which 26 were waited for; matrix products, arithmetic and copies ran while one was open for 9% of the time, Pallas kernels for 35%

profile of v8, /device:TPU:0, one launch (start us, length us, event | category | flops | bytes accessed | tf_op | source)
XLA Modules:
  0.0 541.0 jit_solution(15754869845574032474)
XLA Ops:
  8.5 5.1 collective-permute-start
  17.9 7.1 %qkv_slot.4 = (bf16[4,256,2048]{2,1,0:T(8,128)(2,1)}, bf16[4,256,512]{2,1,0:T(8,128)(2,1)}, bf16[4,256,512]{2,1,0:T(8,128)(2,1)}, bf16[4,256,512]{2,1,0:T(8,128)(2,1)}) custom-call(s32[4]{0:T(128)} %pad_add_fusion.rank_ref, bf16[256,1024]{1,0:T(8,128)(2,1)} %copy-done.67, bf16[256,1024]{1,0:T(8,128)(2,1)} %copy-done.66, f32[1,2048]{1,0:T(1,128)} %bitcast.101, ...), custom_call_target="tpu_custom_call" | custom-call | flops 1610612736 | bytes 8388608 | tf_op jit(solution)/shard_map/qkv_slot/pallas_call | solution.py:106
  26.0 4.4 collective-permute-start.1
  30.3 6.8 %collective-permute-done.2.xb_ref = bf16[256,1024]{1,0:T(8,128)(2,1)S(1)} collective-permute-done((bf16[256,1024]{1,0:T(8,128)(2,1)S(1)}, bf16[256,1024]{1,0:T(8,128)(2,1)S(1)}, u32[]{:S(2)}, u32[]{:S(2)}) %collective-permute-start.2) | collective-permute-done | bytes 524320 | tf_op jit(solution)/shard_map/ppermute | solution.py:596
  37.2 4.3 collective-permute-start.4
  41.5 7.1 %qkv_slot.5 = (bf16[4,256,2048]{2,1,0:T(8,128)(2,1)}, bf16[4,256,512]{2,1,0:T(8,128)(2,1)}, bf16[4,256,512]{2,1,0:T(8,128)(2,1)}, bf16[4,256,512]{2,1,0:T(8,128)(2,1)}) custom-call(s32[4]{0:T(128)} %pad_add_fusion.rank_ref, ...), custom_call_target="tpu_custom_call", output_to_operand_aliasing={{0}: (10, {}), {1}: (11, {}), {2}: (12, {}), {3}: (13, {})} | custom-call | flops 1610612736 | bytes 8388608 | tf_op jit(solution)/shard_map/qkv_slot/pallas_call | solution.py:106
  52.7 7.0 %collective-permute-done.4.xb_ref = bf16[256,1024]{1,0:T(8,128)(2,1)S(1)} collective-permute-done((bf16[256,1024]{1,0:T(8,128)(2,1)S(1)}, bf16[256,1024]{1,0:T(8,128)(2,1)S(1)}, u32[]{:S(2)}, u32[]{:S(2)}) %collective-permute-start.4) | collective-permute-done | bytes 524320 | tf_op jit(solution)/shard_map/ppermute | solution.py:596
  59.7 4.3 collective-permute-start.5
  68.1 7.3 %qkv_slot.6 = (bf16[4,256,2048]{2,1,0:T(8,128)(2,1)}, bf16[4,256,512]{2,1,0:T(8,128)(2,1)}, bf16[4,256,512]{2,1,0:T(8,128)(2,1)}, bf16[4,256,512]{2,1,0:T(8,128)(2,1)}) custom-call(s32[4]{0:T(128)} %pad_add_fusion.rank_ref, bf16[256,1024]{1,0:T(8,128)(2,1)} %copy-done.73, ...), custom_call_target="tpu_custom_call", output_to_operand_aliasing={{0}: (10, {}), {1}: (11, {}), {2}: (12, {}), {3}: (13, {})} | custom-call | flops 1610612736 | bytes 8388608 | tf_op jit(solution)/shard_map/qkv_slot/pallas_call | solution.py:106
  78.1 5.4 collective-permute-start.10
  85.0 7.1 %qkv_slot.7 = (bf16[4,256,2048]{2,1,0:T(8,128)(2,1)}, bf16[4,256,512]{2,1,0:T(8,128)(2,1)}, bf16[4,256,512]{2,1,0:T(8,128)(2,1)}, bf16[4,256,512]{2,1,0:T(8,128)(2,1)}) custom-call(s32[4]{0:T(128)} %pad_add_fusion.rank_ref, bf16[256,1024]{1,0:T(8,128)(2,1)} %copy-done.72, ...), custom_call_target="tpu_custom_call", output_to_operand_aliasing={{0}: (10, {}), {1}: (11, {}), {2}: (12, {}), {3}: (13, {})} | custom-call | flops 1610612736 | bytes 8388608 | tf_op jit(solution)/shard_map/qkv_slot/pallas_call | solution.py:106
  92.1 10.3 %attend.1 = bf16[4,256,512]{2,1,0:T(8,128)(2,1)} custom-call(s32[4]{0:T(128)} %pad_add_fusion.rank_ref, bf16[4,256,512]{2,1,0:T(8,128)(2,1)} %get-tuple-element.173.q_ref, bf16[4,256,512]{2,1,0:T(8,128)(2,1)} %get-tuple-element.174.k_ref, bf16[4,256,512]{2,1,0:T(8,128)(2,1)} %get-tuple-element.175.v_ref, s32[4,256,1]{2,1,0:T(8,128)} %reshape.203.dcol_ref, ...), custom_call_target="tpu_custom_call" | custom-call | flops 2147483648 | bytes 4194304 | tf_op jit(solution)/shard_map/attend/pallas_call | solution.py:169
  102.4 4.3 convolution_convert_fusion.1
  107.5 4.6 collective-permute-start.7
  125.2 4.4 collective-permute-start.8
  129.7 6.0 %collective-permute-done.11.moved_ref.grb_ref = bf16[256,1024]{1,0:T(8,128)(2,1)S(1)} collective-permute-done((bf16[256,1024]{1,0:T(8,128)(2,1)S(1)}, bf16[256,1024]{1,0:T(8,128)(2,1)S(1)}, u32[]{:S(2)}, u32[]{:S(2)}) %collective-permute-start.11) | collective-permute-done | bytes 524320 | tf_op jit(solution)/shard_map/ppermute | solution.py:596
  136.5 4.4 collective-permute-start.12
  147.8 5.3 collective-permute-start.9
  153.1 5.0 collective-permute-done.12.moved_ref.grb_ref
  158.9 4.4 collective-permute-start.13
  176.3 4.2 collective-permute-done.17
  180.5 5.6 %collective-permute-done.21 = bf16[256,1024]{1,0:T(8,128)(2,1)S(1)} collective-permute-done((bf16[256,1024]{1,0:T(8,128)(2,1)S(1)}, bf16[256,1024]{1,0:T(8,128)(2,1)S(1)}, u32[]{:S(2)}, u32[]{:S(2)}) %collective-permute-start.21) | collective-permute-done | bytes 524320 | tf_op jit(solution)/shard_map/ppermute | solution.py:596
  190.5 9.3 %mlp_slot.4 = (bf16[4,256,2048]{2,1,0:T(8,128)(2,1)S(1)}, bf16[4,256,2048]{2,1,0:T(8,128)(2,1)S(1)}, bf16[4,256,2048]{2,1,0:T(8,128)(2,1)S(1)}, bf16[4,256,2048]{2,1,0:T(8,128)(2,1)S(1)}) custom-call(s32[4]{0:T(128)S(1)} %copy-done.48, bf16[256,2048]{1,0:T(8,128)(2,1)S(1)} %add_convert_fusion.4.a_ref, ...), custom_call_target="tpu_custom_call" | custom-call | flops 4294967296 | bytes 20971520 | tf_op jit(solution)/shard_map/mlp_slot/pallas_call | solution.py:303
  207.2 4.4 collective-permute-done.22.a_ref
  211.8 10.3 %mlp_slot.5 = (bf16[4,256,2048]{2,1,0:T(8,128)(2,1)S(1)}, bf16[4,256,2048]{2,1,0:T(8,128)(2,1)S(1)}, bf16[4,256,2048]{2,1,0:T(8,128)(2,1)S(1)}, bf16[4,256,2048]{2,1,0:T(8,128)(2,1)S(1)}) custom-call(s32[4]{0:T(128)S(1)} %copy-done.48, ...), custom_call_target="tpu_custom_call", output_to_operand_aliasing={{0}: (9, {}), {1}: (10, {}), {2}: (11, {}), {3}: (12, {})} | custom-call | flops 4294967296 | bytes 20971520 | tf_op jit(solution)/shard_map/mlp_slot/pallas_call | solution.py:303
  228.2 9.9 %collective-permute-done.23.a_ref = bf16[256,2048]{1,0:T(8,128)(2,1)} collective-permute-done((bf16[256,2048]{1,0:T(8,128)(2,1)}, bf16[256,2048]{1,0:T(8,128)(2,1)}, u32[]{:S(2)}, u32[]{:S(2)}) %collective-permute-start.23) | collective-permute-done | bytes 1048608 | tf_op jit(solution)/shard_map/ppermute | solution.py:596
  240.1 9.6 %mlp_slot.6 = (bf16[4,256,2048]{2,1,0:T(8,128)(2,1)S(1)}, bf16[4,256,2048]{2,1,0:T(8,128)(2,1)S(1)}, bf16[4,256,2048]{2,1,0:T(8,128)(2,1)S(1)}, bf16[4,256,2048]{2,1,0:T(8,128)(2,1)S(1)}) custom-call(s32[4]{0:T(128)S(1)} %copy-done.48, ...), custom_call_target="tpu_custom_call", output_to_operand_aliasing={{0}: (9, {}), {1}: (10, {}), {2}: (11, {}), {3}: (12, {})} | custom-call | flops 4294967296 | bytes 20971520 | tf_op jit(solution)/shard_map/mlp_slot/pallas_call | solution.py:303
  252.8 7.6 %collective-permute-done.25 = bf16[256,2048]{1,0:T(8,128)(2,1)S(1)} collective-permute-done((bf16[256,2048]{1,0:T(8,128)(2,1)}, bf16[256,2048]{1,0:T(8,128)(2,1)S(1)}, u32[]{:S(2)}, u32[]{:S(2)}) %collective-permute-start.25) | collective-permute-done | bytes 1048608 | tf_op jit(solution)/shard_map/ppermute | solution.py:596
  262.9 20.1 %collective-permute-done.24.a_ref = bf16[256,2048]{1,0:T(8,128)(2,1)S(1)} collective-permute-done((bf16[256,2048]{1,0:T(8,128)(2,1)}, bf16[256,2048]{1,0:T(8,128)(2,1)S(1)}, u32[]{:S(2)}, u32[]{:S(2)}) %collective-permute-start.24) | collective-permute-done | bytes 1048608 | tf_op jit(solution)/shard_map/ppermute | solution.py:596
  282.9 10.2 %mlp_slot.7 = (bf16[4,256,2048]{2,1,0:T(8,128)(2,1)S(1)}, bf16[4,256,2048]{2,1,0:T(8,128)(2,1)S(1)}, bf16[4,256,2048]{2,1,0:T(8,128)(2,1)S(1)}, bf16[4,256,2048]{2,1,0:T(8,128)(2,1)S(1)}) custom-call(s32[4]{0:T(128)S(1)} %copy-done.48, ...), custom_call_target="tpu_custom_call", output_to_operand_aliasing={{0}: (9, {}), {1}: (10, {}), {2}: (11, {}), {3}: (12, {})} | custom-call | flops 4294967296 | bytes 20971520 | tf_op jit(solution)/shard_map/mlp_slot/pallas_call | solution.py:303
  293.1 6.1 %collective-permute-done.26.rest_0_ = bf16[256,2048]{1,0:T(8,128)(2,1)S(1)} collective-permute-done((bf16[256,2048]{1,0:T(8,128)(2,1)S(1)}, bf16[256,2048]{1,0:T(8,128)(2,1)S(1)}, u32[]{:S(2)}, u32[]{:S(2)}) %collective-permute-start.26) | collective-permute-done | bytes 1048608 | tf_op jit(solution)/shard_map/ppermute | solution.py:596
  302.9 7.2 %grad_half.4 = bf16[2048,1024]{1,0:T(8,128)(2,1)} custom-call(s32[4]{0:T(128)S(1)} %copy-done.48, bf16[1024,2048]{1,0:T(8,128)(2,1)S(1)} %bitcast.92, bf16[1024,2048]{1,0:T(8,128)(2,1)S(1)} %bitcast.87), custom_call_target="tpu_custom_call" | custom-call | flops 1000000 | bytes 1000000 | tf_op jit(solution)/shard_map/grad_half/pallas_call | solution.py:413
  310.1 7.2 %grad_half.5 = bf16[2048,1024]{1,0:T(8,128)(2,1)} custom-call(s32[4]{0:T(128)S(1)} %copy-done.48, bf16[1024,2048]{1,0:T(8,128)(2,1)S(1)} %bitcast.90, bf16[1024,2048]{1,0:T(8,128)(2,1)S(1)} %bitcast.71), custom_call_target="tpu_custom_call" | custom-call | flops 1000000 | bytes 1000000 | tf_op jit(solution)/shard_map/grad_half/pallas_call | solution.py:413
  330.2 11.3 %convolution_convert_fusion = bf16[1024,2048]{1,0:T(8,128)(2,1)S(1)} fusion(bf16[1024,2048]{1,0:T(8,128)(2,1)S(1)} %bitcast.88, bf16[2048,2048]{1,0:T(8,128)(2,1)} %down_ref.7), kind=kOutput, calls=%fused_computation | convolution fusion | flops 8592031744 | bytes 16777216 | tf_op jit(solution)/shard_map/dot_general | solution.py:53
  341.5 8.0 %grad_half.6.rest_1_ = bf16[2,2048,1024]{2,1,0:T(8,128)(2,1)S(1)} custom-call(s32[4]{0:T(128)S(1)} %copy-done.48, bf16[1024,2048]{1,0:T(8,128)(2,1)S(1)} %bitcast.93, bf16[1024,2048]{1,0:T(8,128)(2,1)S(1)} %bitcast.89, bf16[2048,1024]{1,0:T(8,128)(2,1)} %collective-permute-done.29.rest_0_), custom_call_target="tpu_custom_call" | custom-call | flops 1000000 | bytes 1000000 | tf_op jit(solution)/shard_map/grad_half/pallas_call | solution.py:413
  351.2 5.4 %collective-permute-start.30 = (bf16[256,2048]{1,0:T(8,128)(2,1)}, bf16[256,2048]{1,0:T(8,128)(2,1)}, u32[]{:S(2)}, u32[]{:S(2)}) collective-permute-start(bf16[256,2048]{1,0:T(8,128)(2,1)} %join.30), channel_id=1, source_target_pairs={{0,1},{1,2},{2,3},{4,5},{5,6},{6,7},{8,9},{9,10},{10,11},{12,13},{... | collective-permute-start | bytes 3145736 | tf_op jit(solution)/shard_map/ppermute | solution.py:596
  359.5 7.2 %grad_half.7 = bf16[2,2048,1024]{2,1,0:T(8,128)(2,1)S(1)} custom-call(s32[4]{0:T(128)S(1)} %copy-done.48, bf16[1024,2048]{1,0:T(8,128)(2,1)S(1)} %bitcast.91, bf16[1024,2048]{1,0:T(8,128)(2,1)S(1)} %bitcast.72, bf16[2048,1024]{1,0:T(8,128)(2,1)} %collective-permute-done.32.rest_0_, ...), custom_call_target="tpu_custom_call", output_to_operand_aliasing={{}: (4, {})} | custom-call | flops 1000000 | bytes 1000000 | tf_op jit(solution)/shard_map/grad_half/pallas_call | solution.py:413
  370.2 4.5 collective-permute-done.30.moved_ref.refs_2_
  378.8 5.0 collective-permute-start.33
  387.2 4.1 dom_part.2
  391.3 10.5 %collective-permute-done.33.moved_ref.refs_1_ = bf16[256,2048]{1,0:T(8,128)(2,1)S(1)} collective-permute-done((bf16[256,2048]{1,0:T(8,128)(2,1)S(1)}, bf16[256,2048]{1,0:T(8,128)(2,1)S(1)}, u32[]{:S(2)}, u32[]{:S(2)}) %collective-permute-start.33) | collective-permute-done | bytes 1048608 | tf_op jit(solution)/shard_map/ppermute | solution.py:596
  402.7 4.5 collective-permute-start.34
  413.3 14.2 %attend_back.1.x_ref = bf16[4,256,1536]{2,1,0:T(8,128)(2,1)S(1)} custom-call(s32[4]{0:T(128)S(1)} %copy-done.48, bf16[4,256,512]{2,1,0:T(8,128)(2,1)S(1)} %copy-done.20, bf16[4,256,512]{2,1,0:T(8,128)(2,1)S(1)} %copy-done.21, bf16[4,256,512]{2,1,0:T(8,128)(2,1)S(1)} %copy-done.22, bf16[4,256,512]{2,1,0:T(8,128)(2,1)S(1)} %get-tuple-element.225.do_ref, ...), custom_call_target="tpu_custom_call" | custom-call | flops 115999997952 | bytes 7340032 | tf_op jit(solution)/shard_map/attend_back/pallas_call | solution.py:251
  434.8 7.4 %attn_grads.2 = bf16[2048,1024]{1,0:T(8,128)(2,1)S(1)} custom-call(s32[4]{0:T(128)S(1)} %copy-done.48, bf16[1024,2048]{1,0:T(8,128)(2,1)S(1)} %bitcast.84, bf16[1024,2048]{1,0:T(8,128)(2,1)S(1)} %bitcast.94, bf16[1024,1536]{1,0:T(8,128)(2,1)S(1)} %bitcast.73, bf16[1024,1536]{1,0:T(8,128)(2,1)S(1)} %bitcast.74, bf16[1024,512]{1,0:T(8,128)(2,1)S(1)} %bitcast.99), custom_call_target="tpu_custom_call" | custom-call | flops 4000000000 | bytes 1000000 | tf_op jit(solution)/shard_map/attn_grads/pallas_call | solution.py:456
  451.4 10.5 %attn_grads.3 = bf16[2048,1024]{1,0:T(8,128)(2,1)} custom-call(s32[4]{0:T(128)S(1)} %copy-done.48, bf16[1024,2048]{1,0:T(8,128)(2,1)} %bitcast.83, bf16[1024,2048]{1,0:T(8,128)(2,1)} %bitcast.95, bf16[1024,1536]{1,0:T(8,128)(2,1)} %bitcast.75, bf16[1024,1536]{1,0:T(8,128)(2,1)} %bitcast.76, bf16[1024,512]{1,0:T(8,128)(2,1)S(1)} %bitcast.100, ...), custom_call_target="tpu_custom_call" | custom-call | flops 1000000 | bytes 1000000 | tf_op jit(solution)/shard_map/attn_grads/pallas_call | solution.py:456
  462.9 5.3 collective-permute-done.38
  500.2 4.7 collective-permute-start.42
  511.8 12.6 %collective-permute-done.42.moved_ref = bf16[256,2048]{1,0:T(8,128)(2,1)S(1)} collective-permute-done((bf16[256,2048]{1,0:T(8,128)(2,1)S(1)}, bf16[256,2048]{1,0:T(8,128)(2,1)S(1)}, u32[]{:S(2)}, u32[]{:S(2)}) %collective-permute-start.42) | collective-permute-done | bytes 1048608 | tf_op jit(solution)/shard_map/ppermute | solution.py:596
  (347 shorter events, 183.4 us)
Async XLA Ops:
  7.2 454.7 %reduce-scatter.3.cloned.1.call-start = ((), (), s32[]{:S(2)}) async-start(), calls=%async_computation.2 | async-start | bytes 10485760 | tf_op jit(solution)/shard_map/reduce_scatter | solution.py:717
  8.5 17.4 %collective-permute-start = (bf16[256,1024]{1,0:T(8,128)(2,1)S(1)}, bf16[256,1024]{1,0:T(8,128)(2,1)}, u32[]{:S(2)}, u32[]{:S(2)}) collective-permute-start(bf16[256,1024]{1,0:T(8,128)(2,1)S(1)} %get-tuple-element.279.xa_ref), channel_id=1, source_target_pairs={{0,3},{1,0},{2,1},{3,2},{4,7},{5,4},{6,5},{7,6},{8,11},{9,8},{10,9... | collective-permute-start | bytes 1572872 | tf_op jit(solution)/shard_map/ppermute | solution.py:596
  13.6 23.6 %collective-permute-start.2 = (bf16[256,1024]{1,0:T(8,128)(2,1)S(1)}, bf16[256,1024]{1,0:T(8,128)(2,1)S(1)}, u32[]{:S(2)}, u32[]{:S(2)}) collective-permute-start(bf16[256,1024]{1,0:T(8,128)(2,1)S(1)} %get-tuple-element.278.xb_ref), channel_id=1, source_target_pairs={{0,3},{1,0},{2,1},{3,2},{4,7},{5,4},{6,5},{7,6},{8,11},{9,8},{10,9... | collective-permute-start | bytes 1572872 | tf_op jit(solution)/shard_map/ppermute | solution.py:596
  26.0 22.7 %collective-permute-start.1 = (bf16[256,1024]{1,0:T(8,128)(2,1)}, bf16[256,1024]{1,0:T(8,128)(2,1)S(1)}, u32[]{:S(2)}, u32[]{:S(2)}) collective-permute-start(bf16[256,1024]{1,0:T(8,128)(2,1)} %collective-permute-done.xa_ref), channel_id=1, source_target_pairs={{0,3},{1,0},{2,1},{3,2},{4,7},{5,4},{6,5},{7,6},{8,11},{9,8},{10,9... | collective-permute-start | bytes 1572872 | tf_op jit(solution)/shard_map/ppermute | solution.py:596
  37.2 22.5 %collective-permute-start.4 = (bf16[256,1024]{1,0:T(8,128)(2,1)S(1)}, bf16[256,1024]{1,0:T(8,128)(2,1)S(1)}, u32[]{:S(2)}, u32[]{:S(2)}) collective-permute-start(bf16[256,1024]{1,0:T(8,128)(2,1)S(1)} %collective-permute-done.2.xb_ref), channel_id=1, source_target_pairs={{0,3},{1,0},{2,1},{3,2},{4,7},{5,4},{6,5},{7,6},{8,11},{9,8},{10,9... | collective-permute-start | bytes 1572872 | tf_op jit(solution)/shard_map/ppermute | solution.py:596
  48.6 26.7 %collective-permute-start.3 = (bf16[256,1024]{1,0:T(8,128)(2,1)S(1)}, bf16[256,1024]{1,0:T(8,128)(2,1)S(1)}, u32[]{:S(2)}, u32[]{:S(2)}) collective-permute-start(bf16[256,1024]{1,0:T(8,128)(2,1)S(1)} %collective-permute-done.1.xa_ref), channel_id=1, source_target_pairs={{0,3},{1,0},{2,1},{3,2},{4,7},{5,4},{6,5},{7,6},{8,11},{9,8},{10,9... | collective-permute-start | bytes 1572872 | tf_op jit(solution)/shard_map/ppermute | solution.py:596
  59.7 25.3 %collective-permute-start.5 = (bf16[256,1024]{1,0:T(8,128)(2,1)S(1)}, bf16[256,1024]{1,0:T(8,128)(2,1)}, u32[]{:S(2)}, u32[]{:S(2)}) collective-permute-start(bf16[256,1024]{1,0:T(8,128)(2,1)S(1)} %collective-permute-done.4.xb_ref), channel_id=1, source_target_pairs={{0,3},{1,0},{2,1},{3,2},{4,7},{5,4},{6,5},{7,6},{8,11},{9,8},{10,9... | collective-permute-start | bytes 1572872 | tf_op jit(solution)/shard_map/ppermute | solution.py:596
  75.5 31.3 %collective-permute-start.6 = (bf16[256,1024]{1,0:T(8,128)(2,1)S(1)}, bf16[256,1024]{1,0:T(8,128)(2,1)S(1)}, u32[]{:S(2)}, u32[]{:S(2)}) collective-permute-start(bf16[256,1024]{1,0:T(8,128)(2,1)S(1)} %get-tuple-element.276.gla_ref.gra_ref), channel_id=1, source_target_pairs={{0,1},{1,2},{2,3},{4,5},{5,6},{6,7},{8,9},{9,10},{10,11},{12,13},{... | collective-permute-start | bytes 1572872 | tf_op jit(solution)/shard_map/ppermute | solution.py:596
  76.8 38.9 %collective-permute-start.14 = (bf16[256,1024]{1,0:T(8,128)(2,1)S(1)}, bf16[256,1024]{1,0:T(8,128)(2,1)}, u32[]{:S(2)}, u32[]{:S(2)}) collective-permute-start(bf16[256,1024]{1,0:T(8,128)(2,1)S(1)} %get-tuple-element.276.gla_ref.gra_ref), channel_id=1, source_target_pairs={{1,0},{2,1},{3,2},{5,4},{6,5},{7,6},{9,8},{10,9},{11,10},{13,12},{... | collective-permute-start | bytes 1572872 | tf_op jit(solution)/shard_map/ppermute | solution.py:596
  78.1 34.0 %collective-permute-start.10 = (bf16[256,1024]{1,0:T(8,128)(2,1)S(1)}, bf16[256,1024]{1,0:T(8,128)(2,1)}, u32[]{:S(2)}, u32[]{:S(2)}) collective-permute-start(bf16[256,1024]{1,0:T(8,128)(2,1)S(1)} %get-tuple-element.277.glb_ref.grb_ref), channel_id=1, source_target_pairs={{0,1},{1,2},{2,3},{4,5},{5,6},{6,7},{8,9},{9,10},{10,11},{12,13},{... | collective-permute-start | bytes 1572872 | tf_op jit(solution)/shard_map/ppermute | solution.py:596
  83.4 35.2 %collective-permute-start.18 = (bf16[256,1024]{1,0:T(8,128)(2,1)S(1)}, bf16[256,1024]{1,0:T(8,128)(2,1)}, u32[]{:S(2)}, u32[]{:S(2)}) collective-permute-start(bf16[256,1024]{1,0:T(8,128)(2,1)S(1)} %get-tuple-element.277.glb_ref.grb_ref), channel_id=1, source_target_pairs={{1,0},{2,1},{3,2},{5,4},{6,5},{7,6},{9,8},{10,9},{11,10},{13,12},{... | collective-permute-start | bytes 1572872 | tf_op jit(solution)/shard_map/ppermute | solution.py:596
  107.5 16.9 %collective-permute-start.7 = (bf16[256,1024]{1,0:T(8,128)(2,1)S(1)}, bf16[256,1024]{1,0:T(8,128)(2,1)S(1)}, u32[]{:S(2)}, u32[]{:S(2)}) collective-permute-start(bf16[256,1024]{1,0:T(8,128)(2,1)S(1)} %join.18), channel_id=1, source_target_pairs={{0,1},{1,2},{2,3},{4,5},{5,6},{6,7},{8,9},{9,10},{10,11},{12,13},{... | collective-permute-start | bytes 1572872 | tf_op jit(solution)/shard_map/ppermute | solution.py:596
  113.8 21.9 %collective-permute-start.11 = (bf16[256,1024]{1,0:T(8,128)(2,1)S(1)}, bf16[256,1024]{1,0:T(8,128)(2,1)S(1)}, u32[]{:S(2)}, u32[]{:S(2)}) collective-permute-start(bf16[256,1024]{1,0:T(8,128)(2,1)S(1)} %join.21), channel_id=1, source_target_pairs={{0,1},{1,2},{2,3},{4,5},{5,6},{6,7},{8,9},{9,10},{10,11},{12,13},{... | collective-permute-start | bytes 1572872 | tf_op jit(solution)/shard_map/ppermute | solution.py:596
  117.3 23.6 %collective-permute-start.15 = (bf16[256,1024]{1,0:T(8,128)(2,1)S(1)}, bf16[256,1024]{1,0:T(8,128)(2,1)S(1)}, u32[]{:S(2)}, u32[]{:S(2)}) collective-permute-start(bf16[256,1024]{1,0:T(8,128)(2,1)S(1)} %join.24), channel_id=1, source_target_pairs={{1,0},{2,1},{3,2},{5,4},{6,5},{7,6},{9,8},{10,9},{11,10},{13,12},{... | collective-permute-start | bytes 1572872 | tf_op jit(solution)/shard_map/ppermute | solution.py:596
  120.3 24.5 %collective-permute-start.19 = (bf16[256,1024]{1,0:T(8,128)(2,1)S(1)}, bf16[256,1024]{1,0:T(8,128)(2,1)S(1)}, u32[]{:S(2)}, u32[]{:S(2)}) collective-permute-start(bf16[256,1024]{1,0:T(8,128)(2,1)S(1)} %join.27), channel_id=1, source_target_pairs={{1,0},{2,1},{3,2},{5,4},{6,5},{7,6},{9,8},{10,9},{11,10},{13,12},{... | collective-permute-start | bytes 1572872 | tf_op jit(solution)/shard_map/ppermute | solution.py:596
  125.2 21.8 %collective-permute-start.8 = (bf16[256,1024]{1,0:T(8,128)(2,1)S(1)}, bf16[256,1024]{1,0:T(8,128)(2,1)S(1)}, u32[]{:S(2)}, u32[]{:S(2)}) collective-permute-start(bf16[256,1024]{1,0:T(8,128)(2,1)S(1)} %join.19), channel_id=1, source_target_pairs={{0,1},{1,2},{2,3},{4,5},{5,6},{6,7},{8,9},{9,10},{10,11},{12,13},{... | collective-permute-start | bytes 1572872 | tf_op jit(solution)/shard_map/ppermute | solution.py:596
  136.5 21.7 %collective-permute-start.12 = (bf16[256,1024]{1,0:T(8,128)(2,1)S(1)}, bf16[256,1024]{1,0:T(8,128)(2,1)S(1)}, u32[]{:S(2)}, u32[]{:S(2)}) collective-permute-start(bf16[256,1024]{1,0:T(8,128)(2,1)S(1)} %join.22), channel_id=1, source_target_pairs={{0,1},{1,2},{2,3},{4,5},{5,6},{6,7},{8,9},{9,10},{10,11},{12,13},{... | collective-permute-start | bytes 1572872 | tf_op jit(solution)/shard_map/ppermute | solution.py:596
  141.7 21.7 %collective-permute-start.16 = (bf16[256,1024]{1,0:T(8,128)(2,1)S(1)}, bf16[256,1024]{1,0:T(8,128)(2,1)S(1)}, u32[]{:S(2)}, u32[]{:S(2)}) collective-permute-start(bf16[256,1024]{1,0:T(8,128)(2,1)S(1)} %join.25), channel_id=1, source_target_pairs={{1,0},{2,1},{3,2},{5,4},{6,5},{7,6},{9,8},{10,9},{11,10},{13,12},{... | collective-permute-start | bytes 1572872 | tf_op jit(solution)/shard_map/ppermute | solution.py:596
  145.6 21.7 %collective-permute-start.20 = (bf16[256,1024]{1,0:T(8,128)(2,1)S(1)}, bf16[256,1024]{1,0:T(8,128)(2,1)S(1)}, u32[]{:S(2)}, u32[]{:S(2)}) collective-permute-start(bf16[256,1024]{1,0:T(8,128)(2,1)S(1)} %join.28), channel_id=1, source_target_pairs={{1,0},{2,1},{3,2},{5,4},{6,5},{7,6},{9,8},{10,9},{11,10},{13,12},{... | collective-permute-start | bytes 1572872 | tf_op jit(solution)/shard_map/ppermute | solution.py:596
  147.8 24.6 %collective-permute-start.9 = (bf16[256,1024]{1,0:T(8,128)(2,1)S(1)}, bf16[256,1024]{1,0:T(8,128)(2,1)S(1)}, u32[]{:S(2)}, u32[]{:S(2)}) collective-permute-start(bf16[256,1024]{1,0:T(8,128)(2,1)S(1)} %join.20), channel_id=1, source_target_pairs={{0,1},{1,2},{2,3},{4,5},{5,6},{6,7},{8,9},{9,10},{10,11},{12,13},{... | collective-permute-start | bytes 1572872 | tf_op jit(solution)/shard_map/ppermute | solution.py:596
  158.9 17.3 %collective-permute-start.13 = (bf16[256,1024]{1,0:T(8,128)(2,1)S(1)}, bf16[256,1024]{1,0:T(8,128)(2,1)S(1)}, u32[]{:S(2)}, u32[]{:S(2)}) collective-permute-start(bf16[256,1024]{1,0:T(8,128)(2,1)S(1)} %join.23), channel_id=1, source_target_pairs={{0,1},{1,2},{2,3},{4,5},{5,6},{6,7},{8,9},{9,10},{10,11},{12,13},{... | collective-permute-start | bytes 1572872 | tf_op jit(solution)/shard_map/ppermute | solution.py:596
  164.2 16.3 %collective-permute-start.17 = (bf16[256,1024]{1,0:T(8,128)(2,1)S(1)}, bf16[256,1024]{1,0:T(8,128)(2,1)S(1)}, u32[]{:S(2)}, u32[]{:S(2)}) collective-permute-start(bf16[256,1024]{1,0:T(8,128)(2,1)S(1)} %join.26), channel_id=1, source_target_pairs={{1,0},{2,1},{3,2},{5,4},{6,5},{7,6},{9,8},{10,9},{11,10},{13,12},{... | collective-permute-start | bytes 1572872 | tf_op jit(solution)/shard_map/ppermute | solution.py:596
  168.0 18.1 %collective-permute-start.21 = (bf16[256,1024]{1,0:T(8,128)(2,1)S(1)}, bf16[256,1024]{1,0:T(8,128)(2,1)S(1)}, u32[]{:S(2)}, u32[]{:S(2)}) collective-permute-start(bf16[256,1024]{1,0:T(8,128)(2,1)S(1)} %join.29), channel_id=1, source_target_pairs={{1,0},{2,1},{3,2},{5,4},{6,5},{7,6},{9,8},{10,9},{11,10},{13,12},{... | collective-permute-start | bytes 1572872 | tf_op jit(solution)/shard_map/ppermute | solution.py:596
  188.2 23.5 %collective-permute-start.22 = (bf16[256,2048]{1,0:T(8,128)(2,1)S(1)}, bf16[256,2048]{1,0:T(8,128)(2,1)}, u32[]{:S(2)}, u32[]{:S(2)}) collective-permute-start(bf16[256,2048]{1,0:T(8,128)(2,1)S(1)} %add_convert_fusion.4.a_ref), channel_id=1, source_target_pairs={{0,3},{1,0},{2,1},{3,2},{4,7},{5,4},{6,5},{7,6},{8,11},{9,8},{10,9... | collective-permute-start | bytes 3145736 | tf_op jit(solution)/shard_map/ppermute | solution.py:596
  211.7 26.4 %collective-permute-start.23 = (bf16[256,2048]{1,0:T(8,128)(2,1)}, bf16[256,2048]{1,0:T(8,128)(2,1)}, u32[]{:S(2)}, u32[]{:S(2)}) collective-permute-start(bf16[256,2048]{1,0:T(8,128)(2,1)} %collective-permute-done.22.a_ref), channel_id=1, source_target_pairs={{0,3},{1,0},{2,1},{3,2},{4,7},{5,4},{6,5},{7,6},{8,11},{9,8},{10,9... | collective-permute-start | bytes 3145736 | tf_op jit(solution)/shard_map/ppermute | solution.py:596
  226.0 34.5 %collective-permute-start.25 = (bf16[256,2048]{1,0:T(8,128)(2,1)}, bf16[256,2048]{1,0:T(8,128)(2,1)S(1)}, u32[]{:S(2)}, u32[]{:S(2)}) collective-permute-start(bf16[256,2048]{1,0:T(8,128)(2,1)} %block_term.9), channel_id=1, source_target_pairs={{0,3},{1,0},{2,1},{3,2},{4,7},{5,4},{6,5},{7,6},{8,11},{9,8},{10,9... | collective-permute-start | bytes 3145736 | tf_op jit(solution)/shard_map/ppermute | solution.py:596
  238.1 44.8 %collective-permute-start.24 = (bf16[256,2048]{1,0:T(8,128)(2,1)}, bf16[256,2048]{1,0:T(8,128)(2,1)S(1)}, u32[]{:S(2)}, u32[]{:S(2)}) collective-permute-start(bf16[256,2048]{1,0:T(8,128)(2,1)} %collective-permute-done.23.a_ref), channel_id=1, source_target_pairs={{0,3},{1,0},{2,1},{3,2},{4,7},{5,4},{6,5},{7,6},{8,11},{9,8},{10,9... | collective-permute-start | bytes 3145736 | tf_op jit(solution)/shard_map/ppermute | solution.py:596
  260.8 38.4 %collective-permute-start.26 = (bf16[256,2048]{1,0:T(8,128)(2,1)S(1)}, bf16[256,2048]{1,0:T(8,128)(2,1)S(1)}, u32[]{:S(2)}, u32[]{:S(2)}) collective-permute-start(bf16[256,2048]{1,0:T(8,128)(2,1)S(1)} %add_convert_fusion.3), channel_id=1, source_target_pairs={{0,3},{1,0},{2,1},{3,2},{4,7},{5,4},{6,5},{7,6},{8,11},{9,8},{10,9... | collective-permute-start | bytes 3145736 | tf_op jit(solution)/shard_map/ppermute | solution.py:596
  302.4 18.7 %collective-permute-start.27 = (bf16[256,2048]{1,0:T(8,128)(2,1)S(1)}, bf16[256,2048]{1,0:T(8,128)(2,1)S(1)}, u32[]{:S(2)}, u32[]{:S(2)}) collective-permute-start(bf16[256,2048]{1,0:T(8,128)(2,1)S(1)} %block_term.11), channel_id=1, source_target_pairs={{0,3},{1,0},{2,1},{3,2},{4,7},{5,4},{6,5},{7,6},{8,11},{9,8},{10,9... | collective-permute-start | bytes 3145736 | tf_op jit(solution)/shard_map/ppermute | solution.py:596
  310.1 31.4 %collective-permute-start.29 = (bf16[2048,1024]{1,0:T(8,128)(2,1)}, bf16[2048,1024]{1,0:T(8,128)(2,1)}, u32[]{:S(2)}, u32[]{:S(2)}) collective-permute-start(bf16[2048,1024]{1,0:T(8,128)(2,1)} %grad_half.4), channel_id=1, source_target_pairs={{0,4},{4,0},{8,12},{12,8},{16,20},{20,16},{24,28},{28,24},{1,5},{5... | collective-permute-start | bytes 12582920 | tf_op jit(solution)/shard_map/ppermute | solution.py:617
  317.3 42.2 %collective-permute-start.32 = (bf16[2048,1024]{1,0:T(8,128)(2,1)}, bf16[2048,1024]{1,0:T(8,128)(2,1)}, u32[]{:S(2)}, u32[]{:S(2)}) collective-permute-start(bf16[2048,1024]{1,0:T(8,128)(2,1)} %grad_half.5), channel_id=1, source_target_pairs={{0,4},{4,0},{8,12},{12,8},{16,20},{20,16},{24,28},{28,24},{1,5},{5... | collective-permute-start | bytes 12582920 | tf_op jit(solution)/shard_map/ppermute | solution.py:617
  325.2 24.3 %collective-permute-start.28 = (bf16[256,2048]{1,0:T(8,128)(2,1)S(1)}, bf16[256,2048]{1,0:T(8,128)(2,1)S(1)}, u32[]{:S(2)}, u32[]{:S(2)}) collective-permute-start(bf16[256,2048]{1,0:T(8,128)(2,1)S(1)} %get-tuple-element.215.refs_0_), channel_id=1, source_target_pairs={{0,1},{1,2},{2,3},{4,5},{5,6},{6,7},{8,9},{9,10},{10,11},{12,13},{... | collective-permute-start | bytes 3145736 | tf_op jit(solution)/shard_map/ppermute | solution.py:596
  328.9 27.7 %collective-permute-start.31 = (bf16[256,2048]{1,0:T(8,128)(2,1)S(1)}, bf16[256,2048]{1,0:T(8,128)(2,1)S(1)}, u32[]{:S(2)}, u32[]{:S(2)}) collective-permute-start(bf16[256,2048]{1,0:T(8,128)(2,1)S(1)} %get-tuple-element.215.refs_0_), channel_id=1, source_target_pairs={{1,0},{2,1},{3,2},{5,4},{6,5},{7,6},{9,8},{10,9},{11,10},{13,12},{... | collective-permute-start | bytes 3145736 | tf_op jit(solution)/shard_map/ppermute | solution.py:596
  351.2 23.5 %collective-permute-start.30 = (bf16[256,2048]{1,0:T(8,128)(2,1)}, bf16[256,2048]{1,0:T(8,128)(2,1)}, u32[]{:S(2)}, u32[]{:S(2)}) collective-permute-start(bf16[256,2048]{1,0:T(8,128)(2,1)} %join.30), channel_id=1, source_target_pairs={{0,1},{1,2},{2,3},{4,5},{5,6},{6,7},{8,9},{9,10},{10,11},{12,13},{... | collective-permute-start | bytes 3145736 | tf_op jit(solution)/shard_map/ppermute | solution.py:596
  358.2 25.6 %collective-permute-start.35 = (bf16[256,2048]{1,0:T(8,128)(2,1)}, bf16[256,2048]{1,0:T(8,128)(2,1)}, u32[]{:S(2)}, u32[]{:S(2)}) collective-permute-start(bf16[256,2048]{1,0:T(8,128)(2,1)} %join.31), channel_id=1, source_target_pairs={{1,0},{2,1},{3,2},{5,4},{6,5},{7,6},{9,8},{10,9},{11,10},{13,12},{... | collective-permute-start | bytes 3145736 | tf_op jit(solution)/shard_map/ppermute | solution.py:596
  370.1 157.1 %reduce-scatter.5.cloned.1.call-start = ((), (), s32[]{:S(2)}) async-start(), calls=%async_computation.3 | async-start | bytes 5242880 | tf_op jit(solution)/shard_map/reduce_scatter | solution.py:747
  378.8 23.0 %collective-permute-start.33 = (bf16[256,2048]{1,0:T(8,128)(2,1)S(1)}, bf16[256,2048]{1,0:T(8,128)(2,1)S(1)}, u32[]{:S(2)}, u32[]{:S(2)}) collective-permute-start(bf16[256,2048]{1,0:T(8,128)(2,1)S(1)} %join.32), channel_id=1, source_target_pairs={{0,1},{1,2},{2,3},{4,5},{5,6},{6,7},{8,9},{9,10},{10,11},{12,13},{... | collective-permute-start | bytes 3145736 | tf_op jit(solution)/shard_map/ppermute | solution.py:596
  385.6 22.9 %collective-permute-start.36 = (bf16[256,2048]{1,0:T(8,128)(2,1)S(1)}, bf16[256,2048]{1,0:T(8,128)(2,1)S(1)}, u32[]{:S(2)}, u32[]{:S(2)}) collective-permute-start(bf16[256,2048]{1,0:T(8,128)(2,1)S(1)} %join.34), channel_id=1, source_target_pairs={{1,0},{2,1},{3,2},{5,4},{6,5},{7,6},{9,8},{10,9},{11,10},{13,12},{... | collective-permute-start | bytes 3145736 | tf_op jit(solution)/shard_map/ppermute | solution.py:596
  402.7 24.8 %collective-permute-start.34 = (bf16[256,2048]{1,0:T(8,128)(2,1)S(1)}, bf16[256,2048]{1,0:T(8,128)(2,1)S(1)}, u32[]{:S(2)}, u32[]{:S(2)}) collective-permute-start(bf16[256,2048]{1,0:T(8,128)(2,1)S(1)} %join.33), channel_id=1, source_target_pairs={{0,1},{1,2},{2,3},{4,5},{5,6},{6,7},{8,9},{9,10},{10,11},{12,13},{... | collective-permute-start | bytes 3145736 | tf_op jit(solution)/shard_map/ppermute | solution.py:596
  409.2 22.3 %collective-permute-start.37 = (bf16[256,2048]{1,0:T(8,128)(2,1)S(1)}, bf16[256,2048]{1,0:T(8,128)(2,1)S(1)}, u32[]{:S(2)}, u32[]{:S(2)}) collective-permute-start(bf16[256,2048]{1,0:T(8,128)(2,1)S(1)} %join.35), channel_id=1, source_target_pairs={{1,0},{2,1},{3,2},{5,4},{6,5},{7,6},{9,8},{10,9},{11,10},{13,12},{... | collective-permute-start | bytes 3145736 | tf_op jit(solution)/shard_map/ppermute | solution.py:596
  442.3 25.9 %collective-permute-start.38 = (bf16[256,2048]{1,0:T(8,128)(2,1)}, bf16[256,2048]{1,0:T(8,128)(2,1)}, u32[]{:S(2)}, u32[]{:S(2)}) collective-permute-start(bf16[256,2048]{1,0:T(8,128)(2,1)} %block_term.12), channel_id=1, source_target_pairs={{0,3},{1,0},{2,1},{3,2},{4,7},{5,4},{6,5},{7,6},{8,11},{9,8},{10,9... | collective-permute-start | bytes 3145736 | tf_op jit(solution)/shard_map/ppermute | solution.py:596
  471.5 27.1 %collective-permute-start.40 = (bf16[256,2048]{1,0:T(8,128)(2,1)}, bf16[256,2048]{1,0:T(8,128)(2,1)}, u32[]{:S(2)}, u32[]{:S(2)}) collective-permute-start(bf16[256,2048]{1,0:T(8,128)(2,1)} %add_convert_fusion.1), channel_id=1, source_target_pairs={{0,3},{1,0},{2,1},{3,2},{4,7},{5,4},{6,5},{7,6},{8,11},{9,8},{10,9... | collective-permute-start | bytes 3145736 | tf_op jit(solution)/shard_map/ppermute | solution.py:596
  492.2 12.7 %collective-permute-start.44 = (f32[8320]{0:T(1024)S(1)}, f32[8320]{0:T(1024)S(1)}, u32[]{:S(2)}, u32[]{:S(2)}) collective-permute-start(f32[8320]{0:T(1024)S(1)} %add.141), channel_id=1, source_target_pairs={{0,1},{1,2},{2,3},{3,0},{4,5},{5,6},{6,7},{7,4},{8,9},{9,10},{10,1... | collective-permute-start | bytes 99848 | tf_op jit(solution)/shard_map/ppermute | solution.py:596
  492.3 12.7 %collective-permute-start.45 = (f32[8320]{0:T(1024)S(1)}, f32[8320]{0:T(1024)S(1)}, u32[]{:S(2)}, u32[]{:S(2)}) collective-permute-start(f32[8320]{0:T(1024)S(1)} %add.141), channel_id=1, source_target_pairs={{0,2},{1,3},{2,0},{3,1},{4,6},{5,7},{6,4},{7,5},{8,10},{9,11},{10,... | collective-permute-start | bytes 99848 | tf_op jit(solution)/shard_map/ppermute | solution.py:596
  500.2 24.1 %collective-permute-start.42 = (bf16[256,2048]{1,0:T(8,128)(2,1)S(1)}, bf16[256,2048]{1,0:T(8,128)(2,1)S(1)}, u32[]{:S(2)}, u32[]{:S(2)}) collective-permute-start(bf16[256,2048]{1,0:T(8,128)(2,1)S(1)} %add_convert_fusion), channel_id=1, source_target_pairs={{0,3},{1,0},{2,1},{3,2},{4,7},{5,4},{6,5},{7,6},{8,11},{9,8},{10,9... | collective-permute-start | bytes 3145736 | tf_op jit(solution)/shard_map/ppermute | solution.py:596
  505.0 22.2 %collective-permute-start.47 = (f32[8320]{0:T(1024)S(1)}, f32[8320]{0:T(1024)S(1)}, u32[]{:S(2)}, u32[]{:S(2)}) collective-permute-start(f32[8320]{0:T(1024)S(1)} %add_add_fusion.2), channel_id=1, source_target_pairs={{0,8},{4,12},{8,16},{12,20},{16,24},{20,28},{24,0},{28,4},{1,9},{5... | collective-permute-start | bytes 99848 | tf_op jit(solution)/shard_map/ppermute | solution.py:792
  506.5 20.6 %collective-permute-start.48 = (f32[8320]{0:T(1024)S(1)}, f32[8320]{0:T(1024)S(1)}, u32[]{:S(2)}, u32[]{:S(2)}) collective-permute-start(f32[8320]{0:T(1024)S(1)} %add_add_fusion.2), channel_id=1, source_target_pairs={{0,16},{4,20},{8,24},{12,28},{16,0},{20,4},{24,8},{28,12},{1,17},{... | collective-permute-start | bytes 99848 | tf_op jit(solution)/shard_map/ppermute | solution.py:792
  508.0 19.1 %collective-permute-start.49 = (f32[8320]{0:T(1024)S(1)}, f32[8320]{0:T(1024)S(1)}, u32[]{:S(2)}, u32[]{:S(2)}) collective-permute-start(f32[8320]{0:T(1024)S(1)} %add_add_fusion.2), channel_id=1, source_target_pairs={{0,24},{4,28},{8,0},{12,4},{16,8},{20,12},{24,16},{28,20},{1,25},{... | collective-permute-start | bytes 99848 | tf_op jit(solution)/shard_map/ppermute | solution.py:792
  (96 other events, 836.5 us)
Sparse Core Ops, SparseCore 0:
  370.2 86.7 reduce-scatter.2
  462.0 54.4 reduce-scatter.4

commit v9 on v8

--- a/solution.py
+++ b/solution.py
@@ -470,7 +470,7 @@
         ),
         out_shape=jax.ShapeDtypeStruct((d, 2 * local), BF16),
         compiler_params=params(28 if partner else 50),
-        cost_estimate=cost(4e9 if partner else 1e6, 1e6),
+        cost_estimate=cost(1e6 if partner else 1e6, 1e6),
         name="attn_grads",
     )(rank, act, states, dqkv, dqkv, om, *([] if partner else [moved]))
 
@@ -515,7 +515,7 @@
         out_ref[...] = moved_ref[...]
 
 
-def join(rank, moved, terms, slot, first, right, part=0):
+def join(rank, moved, terms, slot, first, right, part=0, flops=1e6):
     rows, d = moved.shape
     tile = min(128, rows)
     row = pl.BlockSpec((tile, d), lambda i, r: (i, 0))
@@ -529,7 +529,7 @@
         ),
         out_shape=jax.ShapeDtypeStruct((rows, d), BF16),
         compiler_params=params(8),
-        cost_estimate=cost(1e6, 1e6),
+        cost_estimate=cost(flops, 1e6),
         name="join",
     )(rank, moved, terms)
 
@@ -552,7 +552,7 @@
         out_specs=row(d),
         out_shape=jax.ShapeDtypeStruct((rows, d), BF16),
         compiler_params=params(12),
-        cost_estimate=cost(30e9, 12 * rows * d),
+        cost_estimate=cost(1e6, 12 * rows * d),
         name="last_step",
     )(x, gain, term, moved, state)
 
@@ -727,7 +727,6 @@
     )
     mixed = low(state + owned(ffn, right, left))
 
-    (dqkv,) = tie([dqkv], right, left)
     def whole(part):
         span = part.shape[-2] // 2
         mine = lax.dynamic_slice_in_dim(part, side * span, span, part.ndim - 2)
@@ -736,7 +735,7 @@
 
     tokens_of = lambda v: (flat(first_all), flat(state_all), flat(v), flat(masked), where)
     sent = block_term(dqkv, 1, weights, 1e6)
-    (dqkv,) = tie([dqkv], sent)
+    (dqkv,) = tie([dqkv], sent, right, left)
     moved = hop(sent)
     gift = attn_grads(*tokens_of(dqkv))
     (dqkv,) = tie([dqkv], gift)
@@ -746,7 +745,7 @@
     (late,) = tie([attn_term], wide_grad)
     attn_grad = lax.psum_scatter(late, "dp", scatter_dimension=0, axis_index_groups=sides, tiled=True)
     (moved,) = tie([moved], attn_term)
-    sent2 = sent = add(terms[2], moved)
+    sent2 = sent = join(where, moved, terms[2][None], 0, n + 1, True)
     moved = hop(sent)
     for s in range(3, n):
         (dqkv,) = tie([dqkv], sent)
@@ -783,7 +782,7 @@
     for s in range(3, n):
         if s == 3:
             moved, wide = tie([moved, wide])
-        sent = add(terms[s], moved)
+        sent = join(where, moved, terms[s][None], 0, n + 1, True, 0, 60e9)
         moved = hop(sent)
 
     planes = tie([send(small, [(i, (i + m) % n) for i in range(n)]) for m in range(1, n)], sent)
@@ -792,10 +791,11 @@
         lax.ppermute(small, "dp", [(i, (i + 2 * m) % n_dp) for i in range(n_dp)])
         for m in range(1, n_dp // 2)
     ]
+    query_key, value_out = whole(attn_grad)
+    moved, query_key, value_out = tie([moved, query_key, value_out])
     input_grad = last_step(own, gain1, terms[0], moved, grad_state)
     small = small + sum(tie(others, input_grad))
 
-    query_key, value_out = whole(attn_grad)
     return (
         mixed[None],
         input_grad[None],

time: 550 us -> 555 us (level)
  starting transfers between devices: 117 us -> 109 us
  Pallas kernels: 193 us -> 200 us
    ppermute x42, starting transfers between devices: 111 us -> 104 us  [per_device(): send = lambda v, pairs: lax.ppermute(v, 'mp', pairs)]
    reduce_scatter x1, waiting for transfers between devices: 0.02 us -> 6.15 us  [per_device(): lax.psum_scatter(late, 'dp', scatter_dimension=0, axis_index_groups=sides...]
    pallas_call x18 -> x20, Pallas kernels: 20 us -> 25.6 us  [join(): pl.pallas_call(functools.partial(join_body, 0 if right else -1, first), g...]
    unnamed x185 -> x179, local copies, waits for them, and re-layouts: 22.1 us -> 22.8 us
  transfers between devices with their start and end apart: 53 -> 53, of which waited for: 26 -> 26; matrix products, arithmetic and copies ran while one was open for 9% -> 9% of each run, Pallas kernels for 35% -> 36%
where the time goes in v9:
time: 555 us; the launch traced here: 546 us
  Pallas kernels  200 us (36%)
  waiting for transfers between devices  144 us (26%)
  starting transfers between devices  109 us (20%)
  local copies, waits for them, and re-layouts  36.6 us (7%)
  other arithmetic  25.2 us (5%)
  between operations  16 us (3%)
  matrix products  15.6 us (3%)
    ppermute x42, waiting for transfers between devices, per_device(): send = lambda v, pairs: lax.ppermute(v, 'mp', pairs)  138 us
    ppermute x42, starting transfers between devices, per_device(): send = lambda v, pairs: lax.ppermute(v, 'mp', pairs)  104 us
    pallas_call x4, Pallas kernels, mlp_slot(): pl.pallas_call(functools.partial(mlp_body, slot, n), grid_spec=pltpu.Pref...  39.4 us
    pallas_call x4, Pallas kernels, grad_half(): pl.pallas_call(functools.partial(grad_body, not partner), grid_spec=pltpu...  29.6 us
    pallas_call x4, Pallas kernels, qkv_slot(): pl.pallas_call(qkv_body, grid_spec=pltpu.PrefetchScalarGridSpec(num_scala...  28.7 us
    pallas_call x20, Pallas kernels, join(): pl.pallas_call(functools.partial(join_body, 0 if right else -1, first), g...  25.6 us
    pallas_call x8, Pallas kernels, block_term(): pl.pallas_call(term_body, grid=(d // tile,), in_specs=[pl.BlockSpec((1, r...  23.9 us
    unnamed x179, local copies, waits for them, and re-layouts  22.8 us
  transfers between devices with their start and end apart: 53, of which 26 were waited for; matrix products, arithmetic and copies ran while one was open for 9% of the time, Pallas kernels for 36%

profile of v9, /device:TPU:0, one launch (start us, length us, event | category | flops | bytes accessed | tf_op | source)
XLA Modules:
  0.0 546.0 jit_solution(5650510594397814690)
XLA Ops:
  8.5 5.1 collective-permute-start
  17.9 7.1 %qkv_slot.4 = (bf16[4,256,2048]{2,1,0:T(8,128)(2,1)}, bf16[4,256,512]{2,1,0:T(8,128)(2,1)}, bf16[4,256,512]{2,1,0:T(8,128)(2,1)}, bf16[4,256,512]{2,1,0:T(8,128)(2,1)}) custom-call(s32[4]{0:T(128)} %pad_add_fusion.rank_ref, bf16[256,1024]{1,0:T(8,128)(2,1)} %copy-done.63, bf16[256,1024]{1,0:T(8,128)(2,1)} %copy-done.62, f32[1,2048]{1,0:T(1,128)} %bitcast.105, ...), custom_call_target="tpu_custom_call" | custom-call | flops 1610612736 | bytes 8388608 | tf_op jit(solution)/shard_map/qkv_slot/pallas_call | solution.py:106
  26.0 4.4 collective-permute-start.1
  30.3 6.8 %collective-permute-done.2.xb_ref = bf16[256,1024]{1,0:T(8,128)(2,1)S(1)} collective-permute-done((bf16[256,1024]{1,0:T(8,128)(2,1)S(1)}, bf16[256,1024]{1,0:T(8,128)(2,1)S(1)}, u32[]{:S(2)}, u32[]{:S(2)}) %collective-permute-start.2) | collective-permute-done | bytes 524320 | tf_op jit(solution)/shard_map/ppermute | solution.py:596
  37.2 4.3 collective-permute-start.4
  41.5 7.1 %qkv_slot.5 = (bf16[4,256,2048]{2,1,0:T(8,128)(2,1)}, bf16[4,256,512]{2,1,0:T(8,128)(2,1)}, bf16[4,256,512]{2,1,0:T(8,128)(2,1)}, bf16[4,256,512]{2,1,0:T(8,128)(2,1)}) custom-call(s32[4]{0:T(128)} %pad_add_fusion.rank_ref, ...), custom_call_target="tpu_custom_call", output_to_operand_aliasing={{0}: (10, {}), {1}: (11, {}), {2}: (12, {}), {3}: (13, {})} | custom-call | flops 1610612736 | bytes 8388608 | tf_op jit(solution)/shard_map/qkv_slot/pallas_call | solution.py:106
  52.7 7.0 %collective-permute-done.4.xb_ref = bf16[256,1024]{1,0:T(8,128)(2,1)S(1)} collective-permute-done((bf16[256,1024]{1,0:T(8,128)(2,1)S(1)}, bf16[256,1024]{1,0:T(8,128)(2,1)S(1)}, u32[]{:S(2)}, u32[]{:S(2)}) %collective-permute-start.4) | collective-permute-done | bytes 524320 | tf_op jit(solution)/shard_map/ppermute | solution.py:596
  59.7 4.3 collective-permute-start.5
  68.1 7.3 %qkv_slot.6 = (bf16[4,256,2048]{2,1,0:T(8,128)(2,1)}, bf16[4,256,512]{2,1,0:T(8,128)(2,1)}, bf16[4,256,512]{2,1,0:T(8,128)(2,1)}, bf16[4,256,512]{2,1,0:T(8,128)(2,1)}) custom-call(s32[4]{0:T(128)} %pad_add_fusion.rank_ref, bf16[256,1024]{1,0:T(8,128)(2,1)} %copy-done.70, ...), custom_call_target="tpu_custom_call", output_to_operand_aliasing={{0}: (10, {}), {1}: (11, {}), {2}: (12, {}), {3}: (13, {})} | custom-call | flops 1610612736 | bytes 8388608 | tf_op jit(solution)/shard_map/qkv_slot/pallas_call | solution.py:106
  78.1 5.4 collective-permute-start.10
  85.0 7.2 %qkv_slot.7 = (bf16[4,256,2048]{2,1,0:T(8,128)(2,1)}, bf16[4,256,512]{2,1,0:T(8,128)(2,1)}, bf16[4,256,512]{2,1,0:T(8,128)(2,1)}, bf16[4,256,512]{2,1,0:T(8,128)(2,1)}) custom-call(s32[4]{0:T(128)} %pad_add_fusion.rank_ref, bf16[256,1024]{1,0:T(8,128)(2,1)} %copy-done.69, ...), custom_call_target="tpu_custom_call", output_to_operand_aliasing={{0}: (10, {}), {1}: (11, {}), {2}: (12, {}), {3}: (13, {})} | custom-call | flops 1610612736 | bytes 8388608 | tf_op jit(solution)/shard_map/qkv_slot/pallas_call | solution.py:106
  92.2 10.3 %attend.1 = bf16[4,256,512]{2,1,0:T(8,128)(2,1)} custom-call(s32[4]{0:T(128)} %pad_add_fusion.rank_ref, bf16[4,256,512]{2,1,0:T(8,128)(2,1)} %get-tuple-element.175.q_ref, bf16[4,256,512]{2,1,0:T(8,128)(2,1)} %get-tuple-element.176.k_ref, bf16[4,256,512]{2,1,0:T(8,128)(2,1)} %get-tuple-element.177.v_ref, s32[4,256,1]{2,1,0:T(8,128)} %reshape.203.dcol_ref, ...), custom_call_target="tpu_custom_call" | custom-call | flops 2147483648 | bytes 4194304 | tf_op jit(solution)/shard_map/attend/pallas_call | solution.py:169
  102.4 4.3 convolution_convert_fusion.1
  107.6 4.6 collective-permute-start.7
  125.3 4.4 collective-permute-start.8
  129.7 6.0 %collective-permute-done.11.moved_ref.grb_ref = bf16[256,1024]{1,0:T(8,128)(2,1)S(1)} collective-permute-done((bf16[256,1024]{1,0:T(8,128)(2,1)S(1)}, bf16[256,1024]{1,0:T(8,128)(2,1)S(1)}, u32[]{:S(2)}, u32[]{:S(2)}) %collective-permute-start.11) | collective-permute-done | bytes 524320 | tf_op jit(solution)/shard_map/ppermute | solution.py:596
  136.5 4.4 collective-permute-start.12
  147.9 5.3 collective-permute-start.9
  153.2 5.0 collective-permute-done.12.moved_ref.grb_ref
  159.0 4.4 collective-permute-start.13
  180.5 5.6 %collective-permute-done.21 = bf16[256,1024]{1,0:T(8,128)(2,1)S(1)} collective-permute-done((bf16[256,1024]{1,0:T(8,128)(2,1)S(1)}, bf16[256,1024]{1,0:T(8,128)(2,1)S(1)}, u32[]{:S(2)}, u32[]{:S(2)}) %collective-permute-start.21) | collective-permute-done | bytes 524320 | tf_op jit(solution)/shard_map/ppermute | solution.py:596
  190.6 9.3 %mlp_slot.4 = (bf16[4,256,2048]{2,1,0:T(8,128)(2,1)S(1)}, bf16[4,256,2048]{2,1,0:T(8,128)(2,1)S(1)}, bf16[4,256,2048]{2,1,0:T(8,128)(2,1)S(1)}, bf16[4,256,2048]{2,1,0:T(8,128)(2,1)S(1)}) custom-call(s32[4]{0:T(128)S(1)} %copy-done.46, bf16[256,2048]{1,0:T(8,128)(2,1)S(1)} %add_convert_fusion.2.a_ref, ...), custom_call_target="tpu_custom_call" | custom-call | flops 4294967296 | bytes 20971520 | tf_op jit(solution)/shard_map/mlp_slot/pallas_call | solution.py:303
  207.3 4.4 collective-permute-done.22.a_ref
  211.9 10.3 %mlp_slot.5 = (bf16[4,256,2048]{2,1,0:T(8,128)(2,1)S(1)}, bf16[4,256,2048]{2,1,0:T(8,128)(2,1)S(1)}, bf16[4,256,2048]{2,1,0:T(8,128)(2,1)S(1)}, bf16[4,256,2048]{2,1,0:T(8,128)(2,1)S(1)}) custom-call(s32[4]{0:T(128)S(1)} %copy-done.46, ...), custom_call_target="tpu_custom_call", output_to_operand_aliasing={{0}: (9, {}), {1}: (10, {}), {2}: (11, {}), {3}: (12, {})} | custom-call | flops 4294967296 | bytes 20971520 | tf_op jit(solution)/shard_map/mlp_slot/pallas_call | solution.py:303
  228.3 9.8 %collective-permute-done.23.a_ref = bf16[256,2048]{1,0:T(8,128)(2,1)} collective-permute-done((bf16[256,2048]{1,0:T(8,128)(2,1)}, bf16[256,2048]{1,0:T(8,128)(2,1)}, u32[]{:S(2)}, u32[]{:S(2)}) %collective-permute-start.23) | collective-permute-done | bytes 1048608 | tf_op jit(solution)/shard_map/ppermute | solution.py:596
  240.1 9.6 %mlp_slot.6 = (bf16[4,256,2048]{2,1,0:T(8,128)(2,1)S(1)}, bf16[4,256,2048]{2,1,0:T(8,128)(2,1)S(1)}, bf16[4,256,2048]{2,1,0:T(8,128)(2,1)S(1)}, bf16[4,256,2048]{2,1,0:T(8,128)(2,1)S(1)}) custom-call(s32[4]{0:T(128)S(1)} %copy-done.46, ...), custom_call_target="tpu_custom_call", output_to_operand_aliasing={{0}: (9, {}), {1}: (10, {}), {2}: (11, {}), {3}: (12, {})} | custom-call | flops 4294967296 | bytes 20971520 | tf_op jit(solution)/shard_map/mlp_slot/pallas_call | solution.py:303
  252.9 7.6 %collective-permute-done.25 = bf16[256,2048]{1,0:T(8,128)(2,1)S(1)} collective-permute-done((bf16[256,2048]{1,0:T(8,128)(2,1)}, bf16[256,2048]{1,0:T(8,128)(2,1)S(1)}, u32[]{:S(2)}, u32[]{:S(2)}) %collective-permute-start.25) | collective-permute-done | bytes 1048608 | tf_op jit(solution)/shard_map/ppermute | solution.py:596
  262.9 20.0 %collective-permute-done.24.a_ref = bf16[256,2048]{1,0:T(8,128)(2,1)S(1)} collective-permute-done((bf16[256,2048]{1,0:T(8,128)(2,1)}, bf16[256,2048]{1,0:T(8,128)(2,1)S(1)}, u32[]{:S(2)}, u32[]{:S(2)}) %collective-permute-start.24) | collective-permute-done | bytes 1048608 | tf_op jit(solution)/shard_map/ppermute | solution.py:596
  283.0 10.2 %mlp_slot.7 = (bf16[4,256,2048]{2,1,0:T(8,128)(2,1)S(1)}, bf16[4,256,2048]{2,1,0:T(8,128)(2,1)S(1)}, bf16[4,256,2048]{2,1,0:T(8,128)(2,1)S(1)}, bf16[4,256,2048]{2,1,0:T(8,128)(2,1)S(1)}) custom-call(s32[4]{0:T(128)S(1)} %copy-done.46, ...), custom_call_target="tpu_custom_call", output_to_operand_aliasing={{0}: (9, {}), {1}: (10, {}), {2}: (11, {}), {3}: (12, {})} | custom-call | flops 4294967296 | bytes 20971520 | tf_op jit(solution)/shard_map/mlp_slot/pallas_call | solution.py:303
  293.1 6.1 %collective-permute-done.26.rest_0_ = bf16[256,2048]{1,0:T(8,128)(2,1)S(1)} collective-permute-done((bf16[256,2048]{1,0:T(8,128)(2,1)S(1)}, bf16[256,2048]{1,0:T(8,128)(2,1)S(1)}, u32[]{:S(2)}, u32[]{:S(2)}) %collective-permute-start.26) | collective-permute-done | bytes 1048608 | tf_op jit(solution)/shard_map/ppermute | solution.py:596
  302.9 7.2 %grad_half.4 = bf16[2048,1024]{1,0:T(8,128)(2,1)} custom-call(s32[4]{0:T(128)S(1)} %copy-done.46, bf16[1024,2048]{1,0:T(8,128)(2,1)S(1)} %bitcast.94, bf16[1024,2048]{1,0:T(8,128)(2,1)S(1)} %bitcast.89), custom_call_target="tpu_custom_call" | custom-call | flops 1000000 | bytes 1000000 | tf_op jit(solution)/shard_map/grad_half/pallas_call | solution.py:413
  310.1 7.2 %grad_half.5 = bf16[2048,1024]{1,0:T(8,128)(2,1)} custom-call(s32[4]{0:T(128)S(1)} %copy-done.46, bf16[1024,2048]{1,0:T(8,128)(2,1)S(1)} %bitcast.92, bf16[1024,2048]{1,0:T(8,128)(2,1)S(1)} %bitcast.73), custom_call_target="tpu_custom_call" | custom-call | flops 1000000 | bytes 1000000 | tf_op jit(solution)/shard_map/grad_half/pallas_call | solution.py:413
  330.2 11.3 %convolution_convert_fusion = bf16[1024,2048]{1,0:T(8,128)(2,1)S(1)} fusion(bf16[1024,2048]{1,0:T(8,128)(2,1)S(1)} %bitcast.90, bf16[2048,2048]{1,0:T(8,128)(2,1)} %down_ref.7), kind=kOutput, calls=%fused_computation | convolution fusion | flops 8592031744 | bytes 16777216 | tf_op jit(solution)/shard_map/dot_general | solution.py:53
  341.5 8.0 %grad_half.6.rest_1_ = bf16[2,2048,1024]{2,1,0:T(8,128)(2,1)S(1)} custom-call(s32[4]{0:T(128)S(1)} %copy-done.46, bf16[1024,2048]{1,0:T(8,128)(2,1)S(1)} %bitcast.95, bf16[1024,2048]{1,0:T(8,128)(2,1)S(1)} %bitcast.91, bf16[2048,1024]{1,0:T(8,128)(2,1)} %collective-permute-done.29.rest_0_), custom_call_target="tpu_custom_call" | custom-call | flops 1000000 | bytes 1000000 | tf_op jit(solution)/shard_map/grad_half/pallas_call | solution.py:413
  354.0 4.5 collective-permute-start.30
  361.4 7.2 %grad_half.7 = bf16[2,2048,1024]{2,1,0:T(8,128)(2,1)S(1)} custom-call(s32[4]{0:T(128)S(1)} %copy-done.46, bf16[1024,2048]{1,0:T(8,128)(2,1)S(1)} %bitcast.93, bf16[1024,2048]{1,0:T(8,128)(2,1)S(1)} %bitcast.74, bf16[2048,1024]{1,0:T(8,128)(2,1)} %collective-permute-done.32.rest_0_, ...), custom_call_target="tpu_custom_call", output_to_operand_aliasing={{}: (4, {})} | custom-call | flops 1000000 | bytes 1000000 | tf_op jit(solution)/shard_map/grad_half/pallas_call | solution.py:413
  372.0 5.5 %collective-permute-done.30.moved_ref.refs_2_ = bf16[256,2048]{1,0:T(8,128)(2,1)} collective-permute-done((bf16[256,2048]{1,0:T(8,128)(2,1)}, bf16[256,2048]{1,0:T(8,128)(2,1)}, u32[]{:S(2)}, u32[]{:S(2)}) %collective-permute-start.30) | collective-permute-done | bytes 1048608 | tf_op jit(solution)/shard_map/ppermute | solution.py:596
  377.6 6.7 %collective-permute-done.35.moved_ref.refs_1_ = bf16[256,2048]{1,0:T(8,128)(2,1)} collective-permute-done((bf16[256,2048]{1,0:T(8,128)(2,1)}, bf16[256,2048]{1,0:T(8,128)(2,1)}, u32[]{:S(2)}, u32[]{:S(2)}) %collective-permute-start.35) | collective-permute-done | bytes 1048608 | tf_op jit(solution)/shard_map/ppermute | solution.py:596
  397.8 11.4 %collective-permute-done.33.moved_ref.refs_1_ = bf16[256,2048]{1,0:T(8,128)(2,1)S(1)} collective-permute-done((bf16[256,2048]{1,0:T(8,128)(2,1)S(1)}, bf16[256,2048]{1,0:T(8,128)(2,1)S(1)}, u32[]{:S(2)}, u32[]{:S(2)}) %collective-permute-start.33) | collective-permute-done | bytes 1048608 | tf_op jit(solution)/shard_map/ppermute | solution.py:596
  410.0 4.5 collective-permute-start.34
  419.7 14.2 %attend_back.1.x_ref = bf16[4,256,1536]{2,1,0:T(8,128)(2,1)S(1)} custom-call(s32[4]{0:T(128)S(1)} %copy-done.46, bf16[4,256,512]{2,1,0:T(8,128)(2,1)S(1)} %copy-done.21, bf16[4,256,512]{2,1,0:T(8,128)(2,1)S(1)} %copy-done.22, bf16[4,256,512]{2,1,0:T(8,128)(2,1)S(1)} %copy-done.23, bf16[4,256,512]{2,1,0:T(8,128)(2,1)S(1)} %get-tuple-element.227.do_ref, ...), custom_call_target="tpu_custom_call" | custom-call | flops 115999997952 | bytes 7340032 | tf_op jit(solution)/shard_map/attend_back/pallas_call | solution.py:251
  439.2 8.4 %attn_grads.2 = bf16[2048,1024]{1,0:T(8,128)(2,1)} custom-call(s32[4]{0:T(128)S(1)} %copy-done.46, bf16[1024,2048]{1,0:T(8,128)(2,1)S(1)} %bitcast.86, bf16[1024,2048]{1,0:T(8,128)(2,1)S(1)} %bitcast.96, bf16[1024,1536]{1,0:T(8,128)(2,1)S(1)} %bitcast.75, bf16[1024,1536]{1,0:T(8,128)(2,1)S(1)} %bitcast.76, bf16[1024,512]{1,0:T(8,128)(2,1)S(1)} %bitcast.103), custom_call_target="tpu_custom_call" | custom-call | flops 1000000 | bytes 1000000 | tf_op jit(solution)/shard_map/attn_grads/pallas_call | solution.py:456
  455.2 10.5 %attn_grads.3 = bf16[2048,1024]{1,0:T(8,128)(2,1)} custom-call(s32[4]{0:T(128)S(1)} %copy-done.46, bf16[1024,2048]{1,0:T(8,128)(2,1)} %bitcast.85, bf16[1024,2048]{1,0:T(8,128)(2,1)} %bitcast.97, bf16[1024,1536]{1,0:T(8,128)(2,1)} %bitcast.77, bf16[1024,1536]{1,0:T(8,128)(2,1)} %bitcast.78, bf16[1024,512]{1,0:T(8,128)(2,1)S(1)} %bitcast.104, ...), custom_call_target="tpu_custom_call" | custom-call | flops 1000000 | bytes 1000000 | tf_op jit(solution)/shard_map/attn_grads/pallas_call | solution.py:456
  465.7 7.8 %collective-permute-done.38.moved_ref = bf16[256,2048]{1,0:T(8,128)(2,1)} collective-permute-done((bf16[256,2048]{1,0:T(8,128)(2,1)}, bf16[256,2048]{1,0:T(8,128)(2,1)}, u32[]{:S(2)}, u32[]{:S(2)}) %collective-permute-start.38) | collective-permute-done | bytes 1048608 | tf_op jit(solution)/shard_map/ppermute | solution.py:596
  491.9 4.3 fusion.7
  514.7 6.2 %reduce-scatter.5.cloned.1.call-done = bf16[512,1024]{1,0:T(8,128)(2,1)} async-done(((bf16[2048,1024]{1,0:T(8,128)(2,1)}), bf16[512,1024]{1,0:T(8,128)(2,1)}) %reduce-scatter.5.cloned.1.call-update) | async-done | bytes 1048592 | tf_op jit(solution)/shard_map/reduce_scatter | solution.py:746
  522.0 4.8 slice_bitcast_fusion
  527.1 5.0 collective-permute-done.42.moved_ref
  (341 shorter events, 188.0 us)
Async XLA Ops:
  7.2 458.5 %reduce-scatter.3.cloned.1.call-start = ((), (), s32[]{:S(2)}) async-start(), calls=%async_computation.2 | async-start | bytes 10485760 | tf_op jit(solution)/shard_map/reduce_scatter | solution.py:717
  8.5 17.4 %collective-permute-start = (bf16[256,1024]{1,0:T(8,128)(2,1)S(1)}, bf16[256,1024]{1,0:T(8,128)(2,1)}, u32[]{:S(2)}, u32[]{:S(2)}) collective-permute-start(bf16[256,1024]{1,0:T(8,128)(2,1)S(1)} %get-tuple-element.283.xa_ref), channel_id=1, source_target_pairs={{0,3},{1,0},{2,1},{3,2},{4,7},{5,4},{6,5},{7,6},{8,11},{9,8},{10,9... | collective-permute-start | bytes 1572872 | tf_op jit(solution)/shard_map/ppermute | solution.py:596
  13.6 23.6 %collective-permute-start.2 = (bf16[256,1024]{1,0:T(8,128)(2,1)S(1)}, bf16[256,1024]{1,0:T(8,128)(2,1)S(1)}, u32[]{:S(2)}, u32[]{:S(2)}) collective-permute-start(bf16[256,1024]{1,0:T(8,128)(2,1)S(1)} %get-tuple-element.282.xb_ref), channel_id=1, source_target_pairs={{0,3},{1,0},{2,1},{3,2},{4,7},{5,4},{6,5},{7,6},{8,11},{9,8},{10,9... | collective-permute-start | bytes 1572872 | tf_op jit(solution)/shard_map/ppermute | solution.py:596
  26.0 22.7 %collective-permute-start.1 = (bf16[256,1024]{1,0:T(8,128)(2,1)}, bf16[256,1024]{1,0:T(8,128)(2,1)S(1)}, u32[]{:S(2)}, u32[]{:S(2)}) collective-permute-start(bf16[256,1024]{1,0:T(8,128)(2,1)} %collective-permute-done.xa_ref), channel_id=1, source_target_pairs={{0,3},{1,0},{2,1},{3,2},{4,7},{5,4},{6,5},{7,6},{8,11},{9,8},{10,9... | collective-permute-start | bytes 1572872 | tf_op jit(solution)/shard_map/ppermute | solution.py:596
  37.2 22.5 %collective-permute-start.4 = (bf16[256,1024]{1,0:T(8,128)(2,1)S(1)}, bf16[256,1024]{1,0:T(8,128)(2,1)S(1)}, u32[]{:S(2)}, u32[]{:S(2)}) collective-permute-start(bf16[256,1024]{1,0:T(8,128)(2,1)S(1)} %collective-permute-done.2.xb_ref), channel_id=1, source_target_pairs={{0,3},{1,0},{2,1},{3,2},{4,7},{5,4},{6,5},{7,6},{8,11},{9,8},{10,9... | collective-permute-start | bytes 1572872 | tf_op jit(solution)/shard_map/ppermute | solution.py:596
  48.6 26.8 %collective-permute-start.3 = (bf16[256,1024]{1,0:T(8,128)(2,1)S(1)}, bf16[256,1024]{1,0:T(8,128)(2,1)S(1)}, u32[]{:S(2)}, u32[]{:S(2)}) collective-permute-start(bf16[256,1024]{1,0:T(8,128)(2,1)S(1)} %collective-permute-done.1.xa_ref), channel_id=1, source_target_pairs={{0,3},{1,0},{2,1},{3,2},{4,7},{5,4},{6,5},{7,6},{8,11},{9,8},{10,9... | collective-permute-start | bytes 1572872 | tf_op jit(solution)/shard_map/ppermute | solution.py:596
  59.7 25.3 %collective-permute-start.5 = (bf16[256,1024]{1,0:T(8,128)(2,1)S(1)}, bf16[256,1024]{1,0:T(8,128)(2,1)}, u32[]{:S(2)}, u32[]{:S(2)}) collective-permute-start(bf16[256,1024]{1,0:T(8,128)(2,1)S(1)} %collective-permute-done.4.xb_ref), channel_id=1, source_target_pairs={{0,3},{1,0},{2,1},{3,2},{4,7},{5,4},{6,5},{7,6},{8,11},{9,8},{10,9... | collective-permute-start | bytes 1572872 | tf_op jit(solution)/shard_map/ppermute | solution.py:596
  75.5 31.2 %collective-permute-start.6 = (bf16[256,1024]{1,0:T(8,128)(2,1)S(1)}, bf16[256,1024]{1,0:T(8,128)(2,1)S(1)}, u32[]{:S(2)}, u32[]{:S(2)}) collective-permute-start(bf16[256,1024]{1,0:T(8,128)(2,1)S(1)} %get-tuple-element.280.gla_ref.gra_ref), channel_id=1, source_target_pairs={{0,1},{1,2},{2,3},{4,5},{5,6},{6,7},{8,9},{9,10},{10,11},{12,13},{... | collective-permute-start | bytes 1572872 | tf_op jit(solution)/shard_map/ppermute | solution.py:596
  76.8 38.9 %collective-permute-start.14 = (bf16[256,1024]{1,0:T(8,128)(2,1)S(1)}, bf16[256,1024]{1,0:T(8,128)(2,1)}, u32[]{:S(2)}, u32[]{:S(2)}) collective-permute-start(bf16[256,1024]{1,0:T(8,128)(2,1)S(1)} %get-tuple-element.280.gla_ref.gra_ref), channel_id=1, source_target_pairs={{1,0},{2,1},{3,2},{5,4},{6,5},{7,6},{9,8},{10,9},{11,10},{13,12},{... | collective-permute-start | bytes 1572872 | tf_op jit(solution)/shard_map/ppermute | solution.py:596
  78.1 34.0 %collective-permute-start.10 = (bf16[256,1024]{1,0:T(8,128)(2,1)S(1)}, bf16[256,1024]{1,0:T(8,128)(2,1)}, u32[]{:S(2)}, u32[]{:S(2)}) collective-permute-start(bf16[256,1024]{1,0:T(8,128)(2,1)S(1)} %get-tuple-element.281.glb_ref.grb_ref), channel_id=1, source_target_pairs={{0,1},{1,2},{2,3},{4,5},{5,6},{6,7},{8,9},{9,10},{10,11},{12,13},{... | collective-permute-start | bytes 1572872 | tf_op jit(solution)/shard_map/ppermute | solution.py:596
  83.5 35.2 %collective-permute-start.18 = (bf16[256,1024]{1,0:T(8,128)(2,1)S(1)}, bf16[256,1024]{1,0:T(8,128)(2,1)}, u32[]{:S(2)}, u32[]{:S(2)}) collective-permute-start(bf16[256,1024]{1,0:T(8,128)(2,1)S(1)} %get-tuple-element.281.glb_ref.grb_ref), channel_id=1, source_target_pairs={{1,0},{2,1},{3,2},{5,4},{6,5},{7,6},{9,8},{10,9},{11,10},{13,12},{... | collective-permute-start | bytes 1572872 | tf_op jit(solution)/shard_map/ppermute | solution.py:596
  107.6 16.9 %collective-permute-start.7 = (bf16[256,1024]{1,0:T(8,128)(2,1)S(1)}, bf16[256,1024]{1,0:T(8,128)(2,1)S(1)}, u32[]{:S(2)}, u32[]{:S(2)}) collective-permute-start(bf16[256,1024]{1,0:T(8,128)(2,1)S(1)} %join.20), channel_id=1, source_target_pairs={{0,1},{1,2},{2,3},{4,5},{5,6},{6,7},{8,9},{9,10},{10,11},{12,13},{... | collective-permute-start | bytes 1572872 | tf_op jit(solution)/shard_map/ppermute | solution.py:596
  113.8 21.9 %collective-permute-start.11 = (bf16[256,1024]{1,0:T(8,128)(2,1)S(1)}, bf16[256,1024]{1,0:T(8,128)(2,1)S(1)}, u32[]{:S(2)}, u32[]{:S(2)}) collective-permute-start(bf16[256,1024]{1,0:T(8,128)(2,1)S(1)} %join.23), channel_id=1, source_target_pairs={{0,1},{1,2},{2,3},{4,5},{5,6},{6,7},{8,9},{9,10},{10,11},{12,13},{... | collective-permute-start | bytes 1572872 | tf_op jit(solution)/shard_map/ppermute | solution.py:596
  117.4 23.6 %collective-permute-start.15 = (bf16[256,1024]{1,0:T(8,128)(2,1)S(1)}, bf16[256,1024]{1,0:T(8,128)(2,1)S(1)}, u32[]{:S(2)}, u32[]{:S(2)}) collective-permute-start(bf16[256,1024]{1,0:T(8,128)(2,1)S(1)} %join.26), channel_id=1, source_target_pairs={{1,0},{2,1},{3,2},{5,4},{6,5},{7,6},{9,8},{10,9},{11,10},{13,12},{... | collective-permute-start | bytes 1572872 | tf_op jit(solution)/shard_map/ppermute | solution.py:596
  120.3 24.5 %collective-permute-start.19 = (bf16[256,1024]{1,0:T(8,128)(2,1)S(1)}, bf16[256,1024]{1,0:T(8,128)(2,1)S(1)}, u32[]{:S(2)}, u32[]{:S(2)}) collective-permute-start(bf16[256,1024]{1,0:T(8,128)(2,1)S(1)} %join.29), channel_id=1, source_target_pairs={{1,0},{2,1},{3,2},{5,4},{6,5},{7,6},{9,8},{10,9},{11,10},{13,12},{... | collective-permute-start | bytes 1572872 | tf_op jit(solution)/shard_map/ppermute | solution.py:596
  125.3 21.8 %collective-permute-start.8 = (bf16[256,1024]{1,0:T(8,128)(2,1)S(1)}, bf16[256,1024]{1,0:T(8,128)(2,1)S(1)}, u32[]{:S(2)}, u32[]{:S(2)}) collective-permute-start(bf16[256,1024]{1,0:T(8,128)(2,1)S(1)} %join.21), channel_id=1, source_target_pairs={{0,1},{1,2},{2,3},{4,5},{5,6},{6,7},{8,9},{9,10},{10,11},{12,13},{... | collective-permute-start | bytes 1572872 | tf_op jit(solution)/shard_map/ppermute | solution.py:596
  136.5 21.7 %collective-permute-start.12 = (bf16[256,1024]{1,0:T(8,128)(2,1)S(1)}, bf16[256,1024]{1,0:T(8,128)(2,1)S(1)}, u32[]{:S(2)}, u32[]{:S(2)}) collective-permute-start(bf16[256,1024]{1,0:T(8,128)(2,1)S(1)} %join.24), channel_id=1, source_target_pairs={{0,1},{1,2},{2,3},{4,5},{5,6},{6,7},{8,9},{9,10},{10,11},{12,13},{... | collective-permute-start | bytes 1572872 | tf_op jit(solution)/shard_map/ppermute | solution.py:596
  141.8 21.7 %collective-permute-start.16 = (bf16[256,1024]{1,0:T(8,128)(2,1)S(1)}, bf16[256,1024]{1,0:T(8,128)(2,1)S(1)}, u32[]{:S(2)}, u32[]{:S(2)}) collective-permute-start(bf16[256,1024]{1,0:T(8,128)(2,1)S(1)} %join.27), channel_id=1, source_target_pairs={{1,0},{2,1},{3,2},{5,4},{6,5},{7,6},{9,8},{10,9},{11,10},{13,12},{... | collective-permute-start | bytes 1572872 | tf_op jit(solution)/shard_map/ppermute | solution.py:596
  145.6 21.6 %collective-permute-start.20 = (bf16[256,1024]{1,0:T(8,128)(2,1)S(1)}, bf16[256,1024]{1,0:T(8,128)(2,1)S(1)}, u32[]{:S(2)}, u32[]{:S(2)}) collective-permute-start(bf16[256,1024]{1,0:T(8,128)(2,1)S(1)} %join.30), channel_id=1, source_target_pairs={{1,0},{2,1},{3,2},{5,4},{6,5},{7,6},{9,8},{10,9},{11,10},{13,12},{... | collective-permute-start | bytes 1572872 | tf_op jit(solution)/shard_map/ppermute | solution.py:596
  147.9 24.5 %collective-permute-start.9 = (bf16[256,1024]{1,0:T(8,128)(2,1)S(1)}, bf16[256,1024]{1,0:T(8,128)(2,1)S(1)}, u32[]{:S(2)}, u32[]{:S(2)}) collective-permute-start(bf16[256,1024]{1,0:T(8,128)(2,1)S(1)} %join.22), channel_id=1, source_target_pairs={{0,1},{1,2},{2,3},{4,5},{5,6},{6,7},{8,9},{9,10},{10,11},{12,13},{... | collective-permute-start | bytes 1572872 | tf_op jit(solution)/shard_map/ppermute | solution.py:596
  159.0 17.3 %collective-permute-start.13 = (bf16[256,1024]{1,0:T(8,128)(2,1)S(1)}, bf16[256,1024]{1,0:T(8,128)(2,1)S(1)}, u32[]{:S(2)}, u32[]{:S(2)}) collective-permute-start(bf16[256,1024]{1,0:T(8,128)(2,1)S(1)} %join.25), channel_id=1, source_target_pairs={{0,1},{1,2},{2,3},{4,5},{5,6},{6,7},{8,9},{9,10},{10,11},{12,13},{... | collective-permute-start | bytes 1572872 | tf_op jit(solution)/shard_map/ppermute | solution.py:596
  164.2 16.3 %collective-permute-start.17 = (bf16[256,1024]{1,0:T(8,128)(2,1)S(1)}, bf16[256,1024]{1,0:T(8,128)(2,1)S(1)}, u32[]{:S(2)}, u32[]{:S(2)}) collective-permute-start(bf16[256,1024]{1,0:T(8,128)(2,1)S(1)} %join.28), channel_id=1, source_target_pairs={{1,0},{2,1},{3,2},{5,4},{6,5},{7,6},{9,8},{10,9},{11,10},{13,12},{... | collective-permute-start | bytes 1572872 | tf_op jit(solution)/shard_map/ppermute | solution.py:596
  168.0 18.1 %collective-permute-start.21 = (bf16[256,1024]{1,0:T(8,128)(2,1)S(1)}, bf16[256,1024]{1,0:T(8,128)(2,1)S(1)}, u32[]{:S(2)}, u32[]{:S(2)}) collective-permute-start(bf16[256,1024]{1,0:T(8,128)(2,1)S(1)} %join.31), channel_id=1, source_target_pairs={{1,0},{2,1},{3,2},{5,4},{6,5},{7,6},{9,8},{10,9},{11,10},{13,12},{... | collective-permute-start | bytes 1572872 | tf_op jit(solution)/shard_map/ppermute | solution.py:596
  188.2 23.5 %collective-permute-start.22 = (bf16[256,2048]{1,0:T(8,128)(2,1)S(1)}, bf16[256,2048]{1,0:T(8,128)(2,1)}, u32[]{:S(2)}, u32[]{:S(2)}) collective-permute-start(bf16[256,2048]{1,0:T(8,128)(2,1)S(1)} %add_convert_fusion.2.a_ref), channel_id=1, source_target_pairs={{0,3},{1,0},{2,1},{3,2},{4,7},{5,4},{6,5},{7,6},{8,11},{9,8},{10,9... | collective-permute-start | bytes 3145736 | tf_op jit(solution)/shard_map/ppermute | solution.py:596
  211.7 26.4 %collective-permute-start.23 = (bf16[256,2048]{1,0:T(8,128)(2,1)}, bf16[256,2048]{1,0:T(8,128)(2,1)}, u32[]{:S(2)}, u32[]{:S(2)}) collective-permute-start(bf16[256,2048]{1,0:T(8,128)(2,1)} %collective-permute-done.22.a_ref), channel_id=1, source_target_pairs={{0,3},{1,0},{2,1},{3,2},{4,7},{5,4},{6,5},{7,6},{8,11},{9,8},{10,9... | collective-permute-start | bytes 3145736 | tf_op jit(solution)/shard_map/ppermute | solution.py:596
  226.1 34.4 %collective-permute-start.25 = (bf16[256,2048]{1,0:T(8,128)(2,1)}, bf16[256,2048]{1,0:T(8,128)(2,1)S(1)}, u32[]{:S(2)}, u32[]{:S(2)}) collective-permute-start(bf16[256,2048]{1,0:T(8,128)(2,1)} %block_term.9), channel_id=1, source_target_pairs={{0,3},{1,0},{2,1},{3,2},{4,7},{5,4},{6,5},{7,6},{8,11},{9,8},{10,9... | collective-permute-start | bytes 3145736 | tf_op jit(solution)/shard_map/ppermute | solution.py:596
  238.1 44.8 %collective-permute-start.24 = (bf16[256,2048]{1,0:T(8,128)(2,1)}, bf16[256,2048]{1,0:T(8,128)(2,1)S(1)}, u32[]{:S(2)}, u32[]{:S(2)}) collective-permute-start(bf16[256,2048]{1,0:T(8,128)(2,1)} %collective-permute-done.23.a_ref), channel_id=1, source_target_pairs={{0,3},{1,0},{2,1},{3,2},{4,7},{5,4},{6,5},{7,6},{8,11},{9,8},{10,9... | collective-permute-start | bytes 3145736 | tf_op jit(solution)/shard_map/ppermute | solution.py:596
  260.9 38.4 %collective-permute-start.26 = (bf16[256,2048]{1,0:T(8,128)(2,1)S(1)}, bf16[256,2048]{1,0:T(8,128)(2,1)S(1)}, u32[]{:S(2)}, u32[]{:S(2)}) collective-permute-start(bf16[256,2048]{1,0:T(8,128)(2,1)S(1)} %add_convert_fusion.1), channel_id=1, source_target_pairs={{0,3},{1,0},{2,1},{3,2},{4,7},{5,4},{6,5},{7,6},{8,11},{9,8},{10,9... | collective-permute-start | bytes 3145736 | tf_op jit(solution)/shard_map/ppermute | solution.py:596
  302.4 18.7 %collective-permute-start.27 = (bf16[256,2048]{1,0:T(8,128)(2,1)S(1)}, bf16[256,2048]{1,0:T(8,128)(2,1)S(1)}, u32[]{:S(2)}, u32[]{:S(2)}) collective-permute-start(bf16[256,2048]{1,0:T(8,128)(2,1)S(1)} %block_term.11), channel_id=1, source_target_pairs={{0,3},{1,0},{2,1},{3,2},{4,7},{5,4},{6,5},{7,6},{8,11},{9,8},{10,9... | collective-permute-start | bytes 3145736 | tf_op jit(solution)/shard_map/ppermute | solution.py:596
  310.1 31.3 %collective-permute-start.29 = (bf16[2048,1024]{1,0:T(8,128)(2,1)}, bf16[2048,1024]{1,0:T(8,128)(2,1)}, u32[]{:S(2)}, u32[]{:S(2)}) collective-permute-start(bf16[2048,1024]{1,0:T(8,128)(2,1)} %grad_half.4), channel_id=1, source_target_pairs={{0,4},{4,0},{8,12},{12,8},{16,20},{20,16},{24,28},{28,24},{1,5},{5... | collective-permute-start | bytes 12582920 | tf_op jit(solution)/shard_map/ppermute | solution.py:617
  317.4 44.0 %collective-permute-start.32 = (bf16[2048,1024]{1,0:T(8,128)(2,1)}, bf16[2048,1024]{1,0:T(8,128)(2,1)}, u32[]{:S(2)}, u32[]{:S(2)}) collective-permute-start(bf16[2048,1024]{1,0:T(8,128)(2,1)} %grad_half.5), channel_id=1, source_target_pairs={{0,4},{4,0},{8,12},{12,8},{16,20},{20,16},{24,28},{28,24},{1,5},{5... | collective-permute-start | bytes 12582920 | tf_op jit(solution)/shard_map/ppermute | solution.py:617
  325.2 24.3 %collective-permute-start.28 = (bf16[256,2048]{1,0:T(8,128)(2,1)S(1)}, bf16[256,2048]{1,0:T(8,128)(2,1)S(1)}, u32[]{:S(2)}, u32[]{:S(2)}) collective-permute-start(bf16[256,2048]{1,0:T(8,128)(2,1)S(1)} %get-tuple-element.217.refs_0_), channel_id=1, source_target_pairs={{0,1},{1,2},{2,3},{4,5},{5,6},{6,7},{8,9},{9,10},{10,11},{12,13},{... | collective-permute-start | bytes 3145736 | tf_op jit(solution)/shard_map/ppermute | solution.py:596
  328.9 23.4 %collective-permute-start.31 = (bf16[256,2048]{1,0:T(8,128)(2,1)S(1)}, bf16[256,2048]{1,0:T(8,128)(2,1)S(1)}, u32[]{:S(2)}, u32[]{:S(2)}) collective-permute-start(bf16[256,2048]{1,0:T(8,128)(2,1)S(1)} %get-tuple-element.217.refs_0_), channel_id=1, source_target_pairs={{1,0},{2,1},{3,2},{5,4},{6,5},{7,6},{9,8},{10,9},{11,10},{13,12},{... | collective-permute-start | bytes 3145736 | tf_op jit(solution)/shard_map/ppermute | solution.py:596
  354.0 23.5 %collective-permute-start.30 = (bf16[256,2048]{1,0:T(8,128)(2,1)}, bf16[256,2048]{1,0:T(8,128)(2,1)}, u32[]{:S(2)}, u32[]{:S(2)}) collective-permute-start(bf16[256,2048]{1,0:T(8,128)(2,1)} %join.32), channel_id=1, source_target_pairs={{0,1},{1,2},{2,3},{4,5},{5,6},{6,7},{8,9},{9,10},{10,11},{12,13},{... | collective-permute-start | bytes 3145736 | tf_op jit(solution)/shard_map/ppermute | solution.py:596
  360.1 24.1 %collective-permute-start.35 = (bf16[256,2048]{1,0:T(8,128)(2,1)}, bf16[256,2048]{1,0:T(8,128)(2,1)}, u32[]{:S(2)}, u32[]{:S(2)}) collective-permute-start(bf16[256,2048]{1,0:T(8,128)(2,1)} %join.33), channel_id=1, source_target_pairs={{1,0},{2,1},{3,2},{5,4},{6,5},{7,6},{9,8},{10,9},{11,10},{13,12},{... | collective-permute-start | bytes 3145736 | tf_op jit(solution)/shard_map/ppermute | solution.py:596
  372.0 148.9 %reduce-scatter.5.cloned.1.call-start = ((), (), s32[]{:S(2)}) async-start(), calls=%async_computation.3 | async-start | bytes 5242880 | tf_op jit(solution)/shard_map/reduce_scatter | solution.py:746
  388.6 20.5 %collective-permute-start.33 = (bf16[256,2048]{1,0:T(8,128)(2,1)S(1)}, bf16[256,2048]{1,0:T(8,128)(2,1)S(1)}, u32[]{:S(2)}, u32[]{:S(2)}) collective-permute-start(bf16[256,2048]{1,0:T(8,128)(2,1)S(1)} %join.34), channel_id=1, source_target_pairs={{0,1},{1,2},{2,3},{4,5},{5,6},{6,7},{8,9},{9,10},{10,11},{12,13},{... | collective-permute-start | bytes 3145736 | tf_op jit(solution)/shard_map/ppermute | solution.py:596
  392.1 23.1 %collective-permute-start.36 = (bf16[256,2048]{1,0:T(8,128)(2,1)S(1)}, bf16[256,2048]{1,0:T(8,128)(2,1)S(1)}, u32[]{:S(2)}, u32[]{:S(2)}) collective-permute-start(bf16[256,2048]{1,0:T(8,128)(2,1)S(1)} %join.36), channel_id=1, source_target_pairs={{1,0},{2,1},{3,2},{5,4},{6,5},{7,6},{9,8},{10,9},{11,10},{13,12},{... | collective-permute-start | bytes 3145736 | tf_op jit(solution)/shard_map/ppermute | solution.py:596
  410.0 27.3 %collective-permute-start.34 = (bf16[256,2048]{1,0:T(8,128)(2,1)S(1)}, bf16[256,2048]{1,0:T(8,128)(2,1)S(1)}, u32[]{:S(2)}, u32[]{:S(2)}) collective-permute-start(bf16[256,2048]{1,0:T(8,128)(2,1)S(1)} %join.35), channel_id=1, source_target_pairs={{0,1},{1,2},{2,3},{4,5},{5,6},{6,7},{8,9},{9,10},{10,11},{12,13},{... | collective-permute-start | bytes 3145736 | tf_op jit(solution)/shard_map/ppermute | solution.py:596
  415.9 22.3 %collective-permute-start.37 = (bf16[256,2048]{1,0:T(8,128)(2,1)S(1)}, bf16[256,2048]{1,0:T(8,128)(2,1)S(1)}, u32[]{:S(2)}, u32[]{:S(2)}) collective-permute-start(bf16[256,2048]{1,0:T(8,128)(2,1)S(1)} %join.37), channel_id=1, source_target_pairs={{1,0},{2,1},{3,2},{5,4},{6,5},{7,6},{9,8},{10,9},{11,10},{13,12},{... | collective-permute-start | bytes 3145736 | tf_op jit(solution)/shard_map/ppermute | solution.py:596
  447.5 26.0 %collective-permute-start.38 = (bf16[256,2048]{1,0:T(8,128)(2,1)}, bf16[256,2048]{1,0:T(8,128)(2,1)}, u32[]{:S(2)}, u32[]{:S(2)}) collective-permute-start(bf16[256,2048]{1,0:T(8,128)(2,1)} %block_term.12), channel_id=1, source_target_pairs={{0,3},{1,0},{2,1},{3,2},{4,7},{5,4},{6,5},{7,6},{8,11},{9,8},{10,9... | collective-permute-start | bytes 3145736 | tf_op jit(solution)/shard_map/ppermute | solution.py:596
  476.3 28.2 %collective-permute-start.40 = (bf16[256,2048]{1,0:T(8,128)(2,1)}, bf16[256,2048]{1,0:T(8,128)(2,1)}, u32[]{:S(2)}, u32[]{:S(2)}) collective-permute-start(bf16[256,2048]{1,0:T(8,128)(2,1)} %join.38), channel_id=1, source_target_pairs={{0,3},{1,0},{2,1},{3,2},{4,7},{5,4},{6,5},{7,6},{8,11},{9,8},{10,9... | collective-permute-start | bytes 3145736 | tf_op jit(solution)/shard_map/ppermute | solution.py:596
  496.2 14.0 %collective-permute-start.45 = (f32[8320]{0:T(1024)S(1)}, f32[8320]{0:T(1024)S(1)}, u32[]{:S(2)}, u32[]{:S(2)}) collective-permute-start(f32[8320]{0:T(1024)S(1)} %add.133), channel_id=1, source_target_pairs={{0,1},{1,2},{2,3},{3,0},{4,5},{5,6},{6,7},{7,4},{8,9},{9,10},{10,1... | collective-permute-start | bytes 99848 | tf_op jit(solution)/shard_map/ppermute | solution.py:596
  496.3 14.0 %collective-permute-start.46 = (f32[8320]{0:T(1024)S(1)}, f32[8320]{0:T(1024)S(1)}, u32[]{:S(2)}, u32[]{:S(2)}) collective-permute-start(f32[8320]{0:T(1024)S(1)} %add.133), channel_id=1, source_target_pairs={{0,2},{1,3},{2,0},{3,1},{4,6},{5,7},{6,4},{7,5},{8,10},{9,11},{10,... | collective-permute-start | bytes 99848 | tf_op jit(solution)/shard_map/ppermute | solution.py:596
  507.2 25.0 %collective-permute-start.42 = (bf16[256,2048]{1,0:T(8,128)(2,1)}, bf16[256,2048]{1,0:T(8,128)(2,1)S(1)}, u32[]{:S(2)}, u32[]{:S(2)}) collective-permute-start(bf16[256,2048]{1,0:T(8,128)(2,1)} %join.39), channel_id=1, source_target_pairs={{0,3},{1,0},{2,1},{3,2},{4,7},{5,4},{6,5},{7,6},{8,11},{9,8},{10,9... | collective-permute-start | bytes 3145736 | tf_op jit(solution)/shard_map/ppermute | solution.py:596
  510.3 24.6 %collective-permute-start.48 = (f32[8320]{0:T(1024)S(1)}, f32[8320]{0:T(1024)S(1)}, u32[]{:S(2)}, u32[]{:S(2)}) collective-permute-start(f32[8320]{0:T(1024)S(1)} %add_add_fusion.2), channel_id=1, source_target_pairs={{0,8},{4,12},{8,16},{12,20},{16,24},{20,28},{24,0},{28,4},{1,9},{5... | collective-permute-start | bytes 99848 | tf_op jit(solution)/shard_map/ppermute | solution.py:791
  511.8 23.1 %collective-permute-start.49 = (f32[8320]{0:T(1024)S(1)}, f32[8320]{0:T(1024)S(1)}, u32[]{:S(2)}, u32[]{:S(2)}) collective-permute-start(f32[8320]{0:T(1024)S(1)} %add_add_fusion.2), channel_id=1, source_target_pairs={{0,16},{4,20},{8,24},{12,28},{16,0},{20,4},{24,8},{28,12},{1,17},{... | collective-permute-start | bytes 99848 | tf_op jit(solution)/shard_map/ppermute | solution.py:791
  513.2 21.7 %collective-permute-start.50 = (f32[8320]{0:T(1024)S(1)}, f32[8320]{0:T(1024)S(1)}, u32[]{:S(2)}, u32[]{:S(2)}) collective-permute-start(f32[8320]{0:T(1024)S(1)} %add_add_fusion.2), channel_id=1, source_target_pairs={{0,24},{4,28},{8,0},{12,4},{16,8},{20,12},{24,16},{28,20},{1,25},{... | collective-permute-start | bytes 99848 | tf_op jit(solution)/shard_map/ppermute | solution.py:791
  (93 other events, 797.0 us)
Sparse Core Ops, SparseCore 0:
  372.1 86.6 reduce-scatter.2
  465.8 54.9 reduce-scatter.4

commit v10 on v9

--- a/solution.py
+++ b/solution.py
@@ -470,7 +470,7 @@
         ),
         out_shape=jax.ShapeDtypeStruct((d, 2 * local), BF16),
         compiler_params=params(28 if partner else 50),
-        cost_estimate=cost(1e6 if partner else 1e6, 1e6),
+        cost_estimate=cost(4e9 if partner else 1e6, 1e6),
         name="attn_grads",
     )(rank, act, states, dqkv, dqkv, om, *([] if partner else [moved]))
 
@@ -601,8 +601,8 @@
 
     def tick(k, right, left, terms):
         if k:
-            right = join(where, right, terms, n - k, k, True)
-            left = join(where, left, terms, k, n - k, False)
+            right = join(where, right, terms, n - k, k, True, 0, 1e9)
+            left = join(where, left, terms, k, n - k, False, 0, 1e6)
         return send(right, right_line), send(left, left_line), right, left
 
     def owned(terms, right, left):

time: 555 us -> 551 us (level)
  waiting for transfers between devices: 144 us -> 131 us
  starting transfers between devices: 109 us -> 118 us
    ppermute x42, waiting for transfers between devices: 138 us -> 125 us  [per_device(): send = lambda v, pairs: lax.ppermute(v, 'mp', pairs)]
    ppermute x42, starting transfers between devices: 104 us -> 112 us  [per_device(): send = lambda v, pairs: lax.ppermute(v, 'mp', pairs)]
  transfers between devices with their start and end apart: 53 -> 53, of which waited for: 26 -> 24; matrix products, arithmetic and copies ran while one was open for 9% -> 9% of each run, Pallas kernels for 36% -> 36%
where the time goes in v10:
time: 551 us; the launch traced here: 542 us
  Pallas kernels  199 us (36%)
  waiting for transfers between devices  131 us (24%)
  starting transfers between devices  118 us (21%)
  local copies, waits for them, and re-layouts  36.7 us (7%)
  other arithmetic  25.2 us (5%)
  between operations  16 us (3%)
  matrix products  15.6 us (3%)
    ppermute x42, waiting for transfers between devices, per_device(): send = lambda v, pairs: lax.ppermute(v, 'mp', pairs)  125 us
    ppermute x42, starting transfers between devices, per_device(): send = lambda v, pairs: lax.ppermute(v, 'mp', pairs)  112 us
    pallas_call x4, Pallas kernels, mlp_slot(): pl.pallas_call(functools.partial(mlp_body, slot, n), grid_spec=pltpu.Pref...  39.4 us
    pallas_call x4, Pallas kernels, grad_half(): pl.pallas_call(functools.partial(grad_body, not partner), grid_spec=pltpu...  29.6 us
    pallas_call x4, Pallas kernels, qkv_slot(): pl.pallas_call(qkv_body, grid_spec=pltpu.PrefetchScalarGridSpec(num_scala...  28.7 us
    pallas_call x20, Pallas kernels, join(): pl.pallas_call(functools.partial(join_body, 0 if right else -1, first), g...  25.5 us
    pallas_call x8, Pallas kernels, block_term(): pl.pallas_call(term_body, grid=(d // tile,), in_specs=[pl.BlockSpec((1, r...  23.9 us
    unnamed x179, local copies, waits for them, and re-layouts  22.8 us
  transfers between devices with their start and end apart: 53, of which 24 were waited for; matrix products, arithmetic and copies ran while one was open for 9% of the time, Pallas kernels for 36%

profile of v10, /device:TPU:0, one launch (start us, length us, event | category | flops | bytes accessed | tf_op | source)
XLA Modules:
  0.0 541.8 jit_solution(1584898128576668192)
XLA Ops:
  8.5 5.1 collective-permute-start
  17.9 7.1 %qkv_slot.4 = (bf16[4,256,2048]{2,1,0:T(8,128)(2,1)}, bf16[4,256,512]{2,1,0:T(8,128)(2,1)}, bf16[4,256,512]{2,1,0:T(8,128)(2,1)}, bf16[4,256,512]{2,1,0:T(8,128)(2,1)}) custom-call(s32[4]{0:T(128)} %pad_add_fusion.rank_ref, bf16[256,1024]{1,0:T(8,128)(2,1)} %copy-done.63, bf16[256,1024]{1,0:T(8,128)(2,1)} %copy-done.62, f32[1,2048]{1,0:T(1,128)} %bitcast.105, ...), custom_call_target="tpu_custom_call" | custom-call | flops 1610612736 | bytes 8388608 | tf_op jit(solution)/shard_map/qkv_slot/pallas_call | solution.py:106
  26.0 4.4 collective-permute-start.1
  30.3 6.8 %collective-permute-done.2.xb_ref = bf16[256,1024]{1,0:T(8,128)(2,1)S(1)} collective-permute-done((bf16[256,1024]{1,0:T(8,128)(2,1)S(1)}, bf16[256,1024]{1,0:T(8,128)(2,1)S(1)}, u32[]{:S(2)}, u32[]{:S(2)}) %collective-permute-start.2) | collective-permute-done | bytes 524320 | tf_op jit(solution)/shard_map/ppermute | solution.py:596
  41.5 7.1 %qkv_slot.5 = (bf16[4,256,2048]{2,1,0:T(8,128)(2,1)}, bf16[4,256,512]{2,1,0:T(8,128)(2,1)}, bf16[4,256,512]{2,1,0:T(8,128)(2,1)}, bf16[4,256,512]{2,1,0:T(8,128)(2,1)}) custom-call(s32[4]{0:T(128)} %pad_add_fusion.rank_ref, ...), custom_call_target="tpu_custom_call", output_to_operand_aliasing={{0}: (10, {}), {1}: (11, {}), {2}: (12, {}), {3}: (13, {})} | custom-call | flops 1610612736 | bytes 8388608 | tf_op jit(solution)/shard_map/qkv_slot/pallas_call | solution.py:106
  52.7 7.0 %collective-permute-done.4.xb_ref = bf16[256,1024]{1,0:T(8,128)(2,1)S(1)} collective-permute-done((bf16[256,1024]{1,0:T(8,128)(2,1)S(1)}, bf16[256,1024]{1,0:T(8,128)(2,1)S(1)}, u32[]{:S(2)}, u32[]{:S(2)}) %collective-permute-start.4) | collective-permute-done | bytes 524320 | tf_op jit(solution)/shard_map/ppermute | solution.py:596
  59.7 4.3 collective-permute-start.5
  68.1 7.3 %qkv_slot.6 = (bf16[4,256,2048]{2,1,0:T(8,128)(2,1)}, bf16[4,256,512]{2,1,0:T(8,128)(2,1)}, bf16[4,256,512]{2,1,0:T(8,128)(2,1)}, bf16[4,256,512]{2,1,0:T(8,128)(2,1)}) custom-call(s32[4]{0:T(128)} %pad_add_fusion.rank_ref, bf16[256,1024]{1,0:T(8,128)(2,1)} %copy-done.70, ...), custom_call_target="tpu_custom_call", output_to_operand_aliasing={{0}: (10, {}), {1}: (11, {}), {2}: (12, {}), {3}: (13, {})} | custom-call | flops 1610612736 | bytes 8388608 | tf_op jit(solution)/shard_map/qkv_slot/pallas_call | solution.py:106
  78.1 5.4 collective-permute-start.10
  85.0 7.2 %qkv_slot.7 = (bf16[4,256,2048]{2,1,0:T(8,128)(2,1)}, bf16[4,256,512]{2,1,0:T(8,128)(2,1)}, bf16[4,256,512]{2,1,0:T(8,128)(2,1)}, bf16[4,256,512]{2,1,0:T(8,128)(2,1)}) custom-call(s32[4]{0:T(128)} %pad_add_fusion.rank_ref, bf16[256,1024]{1,0:T(8,128)(2,1)} %copy-done.69, ...), custom_call_target="tpu_custom_call", output_to_operand_aliasing={{0}: (10, {}), {1}: (11, {}), {2}: (12, {}), {3}: (13, {})} | custom-call | flops 1610612736 | bytes 8388608 | tf_op jit(solution)/shard_map/qkv_slot/pallas_call | solution.py:106
  92.2 10.3 %attend.1 = bf16[4,256,512]{2,1,0:T(8,128)(2,1)} custom-call(s32[4]{0:T(128)} %pad_add_fusion.rank_ref, bf16[4,256,512]{2,1,0:T(8,128)(2,1)} %get-tuple-element.175.q_ref, bf16[4,256,512]{2,1,0:T(8,128)(2,1)} %get-tuple-element.176.k_ref, bf16[4,256,512]{2,1,0:T(8,128)(2,1)} %get-tuple-element.177.v_ref, s32[4,256,1]{2,1,0:T(8,128)} %reshape.203.dcol_ref, ...), custom_call_target="tpu_custom_call" | custom-call | flops 2147483648 | bytes 4194304 | tf_op jit(solution)/shard_map/attend/pallas_call | solution.py:169
  102.4 4.3 convolution_convert_fusion.1
  107.6 4.6 collective-permute-start.7
  125.3 4.4 collective-permute-start.8
  129.7 6.0 %collective-permute-done.11.moved_ref.grb_ref = bf16[256,1024]{1,0:T(8,128)(2,1)S(1)} collective-permute-done((bf16[256,1024]{1,0:T(8,128)(2,1)S(1)}, bf16[256,1024]{1,0:T(8,128)(2,1)S(1)}, u32[]{:S(2)}, u32[]{:S(2)}) %collective-permute-start.11) | collective-permute-done | bytes 524320 | tf_op jit(solution)/shard_map/ppermute | solution.py:596
  136.5 4.4 collective-permute-start.12
  147.9 5.3 collective-permute-start.9
  153.2 5.0 collective-permute-done.12.moved_ref.grb_ref
  159.0 4.4 collective-permute-start.13
  180.5 5.6 %collective-permute-done.21 = bf16[256,1024]{1,0:T(8,128)(2,1)S(1)} collective-permute-done((bf16[256,1024]{1,0:T(8,128)(2,1)S(1)}, bf16[256,1024]{1,0:T(8,128)(2,1)S(1)}, u32[]{:S(2)}, u32[]{:S(2)}) %collective-permute-start.21) | collective-permute-done | bytes 524320 | tf_op jit(solution)/shard_map/ppermute | solution.py:596
  190.6 9.3 %mlp_slot.4 = (bf16[4,256,2048]{2,1,0:T(8,128)(2,1)S(1)}, bf16[4,256,2048]{2,1,0:T(8,128)(2,1)S(1)}, bf16[4,256,2048]{2,1,0:T(8,128)(2,1)S(1)}, bf16[4,256,2048]{2,1,0:T(8,128)(2,1)S(1)}) custom-call(s32[4]{0:T(128)S(1)} %copy-done.46, bf16[256,2048]{1,0:T(8,128)(2,1)S(1)} %add_convert_fusion.2.a_ref, ...), custom_call_target="tpu_custom_call" | custom-call | flops 4294967296 | bytes 20971520 | tf_op jit(solution)/shard_map/mlp_slot/pallas_call | solution.py:303
  207.3 4.4 collective-permute-done.22.a_ref
  211.9 10.3 %mlp_slot.5 = (bf16[4,256,2048]{2,1,0:T(8,128)(2,1)S(1)}, bf16[4,256,2048]{2,1,0:T(8,128)(2,1)S(1)}, bf16[4,256,2048]{2,1,0:T(8,128)(2,1)S(1)}, bf16[4,256,2048]{2,1,0:T(8,128)(2,1)S(1)}) custom-call(s32[4]{0:T(128)S(1)} %copy-done.46, ...), custom_call_target="tpu_custom_call", output_to_operand_aliasing={{0}: (9, {}), {1}: (10, {}), {2}: (11, {}), {3}: (12, {})} | custom-call | flops 4294967296 | bytes 20971520 | tf_op jit(solution)/shard_map/mlp_slot/pallas_call | solution.py:303
  228.3 9.8 %collective-permute-done.23.a_ref = bf16[256,2048]{1,0:T(8,128)(2,1)} collective-permute-done((bf16[256,2048]{1,0:T(8,128)(2,1)}, bf16[256,2048]{1,0:T(8,128)(2,1)}, u32[]{:S(2)}, u32[]{:S(2)}) %collective-permute-start.23) | collective-permute-done | bytes 1048608 | tf_op jit(solution)/shard_map/ppermute | solution.py:596
  240.1 9.6 %mlp_slot.6 = (bf16[4,256,2048]{2,1,0:T(8,128)(2,1)S(1)}, bf16[4,256,2048]{2,1,0:T(8,128)(2,1)S(1)}, bf16[4,256,2048]{2,1,0:T(8,128)(2,1)S(1)}, bf16[4,256,2048]{2,1,0:T(8,128)(2,1)S(1)}) custom-call(s32[4]{0:T(128)S(1)} %copy-done.46, ...), custom_call_target="tpu_custom_call", output_to_operand_aliasing={{0}: (9, {}), {1}: (10, {}), {2}: (11, {}), {3}: (12, {})} | custom-call | flops 4294967296 | bytes 20971520 | tf_op jit(solution)/shard_map/mlp_slot/pallas_call | solution.py:303
  252.9 7.6 %collective-permute-done.25 = bf16[256,2048]{1,0:T(8,128)(2,1)S(1)} collective-permute-done((bf16[256,2048]{1,0:T(8,128)(2,1)}, bf16[256,2048]{1,0:T(8,128)(2,1)S(1)}, u32[]{:S(2)}, u32[]{:S(2)}) %collective-permute-start.25) | collective-permute-done | bytes 1048608 | tf_op jit(solution)/shard_map/ppermute | solution.py:596
  262.9 20.0 %collective-permute-done.24.a_ref = bf16[256,2048]{1,0:T(8,128)(2,1)S(1)} collective-permute-done((bf16[256,2048]{1,0:T(8,128)(2,1)}, bf16[256,2048]{1,0:T(8,128)(2,1)S(1)}, u32[]{:S(2)}, u32[]{:S(2)}) %collective-permute-start.24) | collective-permute-done | bytes 1048608 | tf_op jit(solution)/shard_map/ppermute | solution.py:596
  283.0 10.2 %mlp_slot.7 = (bf16[4,256,2048]{2,1,0:T(8,128)(2,1)S(1)}, bf16[4,256,2048]{2,1,0:T(8,128)(2,1)S(1)}, bf16[4,256,2048]{2,1,0:T(8,128)(2,1)S(1)}, bf16[4,256,2048]{2,1,0:T(8,128)(2,1)S(1)}) custom-call(s32[4]{0:T(128)S(1)} %copy-done.46, ...), custom_call_target="tpu_custom_call", output_to_operand_aliasing={{0}: (9, {}), {1}: (10, {}), {2}: (11, {}), {3}: (12, {})} | custom-call | flops 4294967296 | bytes 20971520 | tf_op jit(solution)/shard_map/mlp_slot/pallas_call | solution.py:303
  293.1 6.1 %collective-permute-done.26.rest_0_ = bf16[256,2048]{1,0:T(8,128)(2,1)S(1)} collective-permute-done((bf16[256,2048]{1,0:T(8,128)(2,1)S(1)}, bf16[256,2048]{1,0:T(8,128)(2,1)S(1)}, u32[]{:S(2)}, u32[]{:S(2)}) %collective-permute-start.26) | collective-permute-done | bytes 1048608 | tf_op jit(solution)/shard_map/ppermute | solution.py:596
  302.9 7.2 %grad_half.4 = bf16[2048,1024]{1,0:T(8,128)(2,1)} custom-call(s32[4]{0:T(128)S(1)} %copy-done.46, bf16[1024,2048]{1,0:T(8,128)(2,1)S(1)} %bitcast.94, bf16[1024,2048]{1,0:T(8,128)(2,1)S(1)} %bitcast.89), custom_call_target="tpu_custom_call" | custom-call | flops 1000000 | bytes 1000000 | tf_op jit(solution)/shard_map/grad_half/pallas_call | solution.py:413
  310.1 7.2 %grad_half.5 = bf16[2048,1024]{1,0:T(8,128)(2,1)} custom-call(s32[4]{0:T(128)S(1)} %copy-done.46, bf16[1024,2048]{1,0:T(8,128)(2,1)S(1)} %bitcast.92, bf16[1024,2048]{1,0:T(8,128)(2,1)S(1)} %bitcast.73), custom_call_target="tpu_custom_call" | custom-call | flops 1000000 | bytes 1000000 | tf_op jit(solution)/shard_map/grad_half/pallas_call | solution.py:413
  330.2 11.3 %convolution_convert_fusion = bf16[1024,2048]{1,0:T(8,128)(2,1)S(1)} fusion(bf16[1024,2048]{1,0:T(8,128)(2,1)S(1)} %bitcast.90, bf16[2048,2048]{1,0:T(8,128)(2,1)} %down_ref.7), kind=kOutput, calls=%fused_computation | convolution fusion | flops 8592031744 | bytes 16777216 | tf_op jit(solution)/shard_map/dot_general | solution.py:53
  341.5 8.0 %grad_half.6.rest_1_ = bf16[2,2048,1024]{2,1,0:T(8,128)(2,1)S(1)} custom-call(s32[4]{0:T(128)S(1)} %copy-done.46, bf16[1024,2048]{1,0:T(8,128)(2,1)S(1)} %bitcast.95, bf16[1024,2048]{1,0:T(8,128)(2,1)S(1)} %bitcast.91, bf16[2048,1024]{1,0:T(8,128)(2,1)} %collective-permute-done.29.rest_0_), custom_call_target="tpu_custom_call" | custom-call | flops 1000000 | bytes 1000000 | tf_op jit(solution)/shard_map/grad_half/pallas_call | solution.py:413
  351.2 5.4 %collective-permute-start.30 = (bf16[256,2048]{1,0:T(8,128)(2,1)}, bf16[256,2048]{1,0:T(8,128)(2,1)}, u32[]{:S(2)}, u32[]{:S(2)}) collective-permute-start(bf16[256,2048]{1,0:T(8,128)(2,1)} %join.32), channel_id=1, source_target_pairs={{0,1},{1,2},{2,3},{4,5},{5,6},{6,7},{8,9},{9,10},{10,11},{12,13},{... | collective-permute-start | bytes 3145736 | tf_op jit(solution)/shard_map/ppermute | solution.py:596
  359.5 7.2 %grad_half.7 = bf16[2,2048,1024]{2,1,0:T(8,128)(2,1)S(1)} custom-call(s32[4]{0:T(128)S(1)} %copy-done.46, bf16[1024,2048]{1,0:T(8,128)(2,1)S(1)} %bitcast.93, bf16[1024,2048]{1,0:T(8,128)(2,1)S(1)} %bitcast.74, bf16[2048,1024]{1,0:T(8,128)(2,1)} %collective-permute-done.32.rest_0_, ...), custom_call_target="tpu_custom_call", output_to_operand_aliasing={{}: (4, {})} | custom-call | flops 1000000 | bytes 1000000 | tf_op jit(solution)/shard_map/grad_half/pallas_call | solution.py:413
  370.2 4.6 collective-permute-done.30.moved_ref.refs_2_
  378.9 5.0 collective-permute-start.33
  391.4 10.5 %collective-permute-done.33.moved_ref.refs_1_ = bf16[256,2048]{1,0:T(8,128)(2,1)S(1)} collective-permute-done((bf16[256,2048]{1,0:T(8,128)(2,1)S(1)}, bf16[256,2048]{1,0:T(8,128)(2,1)S(1)}, u32[]{:S(2)}, u32[]{:S(2)}) %collective-permute-start.33) | collective-permute-done | bytes 1048608 | tf_op jit(solution)/shard_map/ppermute | solution.py:596
  402.8 4.5 collective-permute-start.34
  413.4 14.2 %attend_back.1.x_ref = bf16[4,256,1536]{2,1,0:T(8,128)(2,1)S(1)} custom-call(s32[4]{0:T(128)S(1)} %copy-done.46, bf16[4,256,512]{2,1,0:T(8,128)(2,1)S(1)} %copy-done.21, bf16[4,256,512]{2,1,0:T(8,128)(2,1)S(1)} %copy-done.22, bf16[4,256,512]{2,1,0:T(8,128)(2,1)S(1)} %copy-done.23, bf16[4,256,512]{2,1,0:T(8,128)(2,1)S(1)} %get-tuple-element.227.do_ref, ...), custom_call_target="tpu_custom_call" | custom-call | flops 115999997952 | bytes 7340032 | tf_op jit(solution)/shard_map/attend_back/pallas_call | solution.py:251
  432.5 8.4 %attn_grads.2 = bf16[2048,1024]{1,0:T(8,128)(2,1)} custom-call(s32[4]{0:T(128)S(1)} %copy-done.46, bf16[1024,2048]{1,0:T(8,128)(2,1)S(1)} %bitcast.86, bf16[1024,2048]{1,0:T(8,128)(2,1)S(1)} %bitcast.96, bf16[1024,1536]{1,0:T(8,128)(2,1)S(1)} %bitcast.75, bf16[1024,1536]{1,0:T(8,128)(2,1)S(1)} %bitcast.76, bf16[1024,512]{1,0:T(8,128)(2,1)S(1)} %bitcast.103), custom_call_target="tpu_custom_call" | custom-call | flops 4000000000 | bytes 1000000 | tf_op jit(solution)/shard_map/attn_grads/pallas_call | solution.py:456
  451.6 10.5 %attn_grads.3 = bf16[2048,1024]{1,0:T(8,128)(2,1)} custom-call(s32[4]{0:T(128)S(1)} %copy-done.46, bf16[1024,2048]{1,0:T(8,128)(2,1)} %bitcast.85, bf16[1024,2048]{1,0:T(8,128)(2,1)} %bitcast.97, bf16[1024,1536]{1,0:T(8,128)(2,1)} %bitcast.77, bf16[1024,1536]{1,0:T(8,128)(2,1)} %bitcast.78, bf16[1024,512]{1,0:T(8,128)(2,1)S(1)} %bitcast.104, ...), custom_call_target="tpu_custom_call" | custom-call | flops 1000000 | bytes 1000000 | tf_op jit(solution)/shard_map/attn_grads/pallas_call | solution.py:456
  462.1 5.9 %collective-permute-done.38.moved_ref = bf16[256,2048]{1,0:T(8,128)(2,1)} collective-permute-done((bf16[256,2048]{1,0:T(8,128)(2,1)}, bf16[256,2048]{1,0:T(8,128)(2,1)}, u32[]{:S(2)}, u32[]{:S(2)}) %collective-permute-start.38) | collective-permute-done | bytes 1048608 | tf_op jit(solution)/shard_map/ppermute | solution.py:596
  470.8 4.5 collective-permute-start.40
  488.0 4.3 fusion.7
  510.6 5.5 %reduce-scatter.5.cloned.1.call-done = bf16[512,1024]{1,0:T(8,128)(2,1)} async-done(((bf16[2048,1024]{1,0:T(8,128)(2,1)}), bf16[512,1024]{1,0:T(8,128)(2,1)}) %reduce-scatter.5.cloned.1.call-update) | async-done | bytes 1048592 | tf_op jit(solution)/shard_map/reduce_scatter | solution.py:746
  517.2 4.8 slice_bitcast_fusion
  522.3 5.6 %collective-permute-done.42.moved_ref = bf16[256,2048]{1,0:T(8,128)(2,1)S(1)} collective-permute-done((bf16[256,2048]{1,0:T(8,128)(2,1)}, bf16[256,2048]{1,0:T(8,128)(2,1)S(1)}, u32[]{:S(2)}, u32[]{:S(2)}) %collective-permute-start.42) | collective-permute-done | bytes 1048608 | tf_op jit(solution)/shard_map/ppermute | solution.py:596
  (341 shorter events, 188.1 us)
Async XLA Ops:
  7.2 454.9 %reduce-scatter.3.cloned.1.call-start = ((), (), s32[]{:S(2)}) async-start(), calls=%async_computation.2 | async-start | bytes 10485760 | tf_op jit(solution)/shard_map/reduce_scatter | solution.py:717
  8.5 17.4 %collective-permute-start = (bf16[256,1024]{1,0:T(8,128)(2,1)S(1)}, bf16[256,1024]{1,0:T(8,128)(2,1)}, u32[]{:S(2)}, u32[]{:S(2)}) collective-permute-start(bf16[256,1024]{1,0:T(8,128)(2,1)S(1)} %get-tuple-element.283.xa_ref), channel_id=1, source_target_pairs={{0,3},{1,0},{2,1},{3,2},{4,7},{5,4},{6,5},{7,6},{8,11},{9,8},{10,9... | collective-permute-start | bytes 1572872 | tf_op jit(solution)/shard_map/ppermute | solution.py:596
  13.6 23.6 %collective-permute-start.2 = (bf16[256,1024]{1,0:T(8,128)(2,1)S(1)}, bf16[256,1024]{1,0:T(8,128)(2,1)S(1)}, u32[]{:S(2)}, u32[]{:S(2)}) collective-permute-start(bf16[256,1024]{1,0:T(8,128)(2,1)S(1)} %get-tuple-element.282.xb_ref), channel_id=1, source_target_pairs={{0,3},{1,0},{2,1},{3,2},{4,7},{5,4},{6,5},{7,6},{8,11},{9,8},{10,9... | collective-permute-start | bytes 1572872 | tf_op jit(solution)/shard_map/ppermute | solution.py:596
  26.0 22.7 %collective-permute-start.1 = (bf16[256,1024]{1,0:T(8,128)(2,1)}, bf16[256,1024]{1,0:T(8,128)(2,1)S(1)}, u32[]{:S(2)}, u32[]{:S(2)}) collective-permute-start(bf16[256,1024]{1,0:T(8,128)(2,1)} %collective-permute-done.xa_ref), channel_id=1, source_target_pairs={{0,3},{1,0},{2,1},{3,2},{4,7},{5,4},{6,5},{7,6},{8,11},{9,8},{10,9... | collective-permute-start | bytes 1572872 | tf_op jit(solution)/shard_map/ppermute | solution.py:596
  37.2 22.5 %collective-permute-start.4 = (bf16[256,1024]{1,0:T(8,128)(2,1)S(1)}, bf16[256,1024]{1,0:T(8,128)(2,1)S(1)}, u32[]{:S(2)}, u32[]{:S(2)}) collective-permute-start(bf16[256,1024]{1,0:T(8,128)(2,1)S(1)} %collective-permute-done.2.xb_ref), channel_id=1, source_target_pairs={{0,3},{1,0},{2,1},{3,2},{4,7},{5,4},{6,5},{7,6},{8,11},{9,8},{10,9... | collective-permute-start | bytes 1572872 | tf_op jit(solution)/shard_map/ppermute | solution.py:596
  48.6 26.8 %collective-permute-start.3 = (bf16[256,1024]{1,0:T(8,128)(2,1)S(1)}, bf16[256,1024]{1,0:T(8,128)(2,1)S(1)}, u32[]{:S(2)}, u32[]{:S(2)}) collective-permute-start(bf16[256,1024]{1,0:T(8,128)(2,1)S(1)} %collective-permute-done.1.xa_ref), channel_id=1, source_target_pairs={{0,3},{1,0},{2,1},{3,2},{4,7},{5,4},{6,5},{7,6},{8,11},{9,8},{10,9... | collective-permute-start | bytes 1572872 | tf_op jit(solution)/shard_map/ppermute | solution.py:596
  59.7 25.3 %collective-permute-start.5 = (bf16[256,1024]{1,0:T(8,128)(2,1)S(1)}, bf16[256,1024]{1,0:T(8,128)(2,1)}, u32[]{:S(2)}, u32[]{:S(2)}) collective-permute-start(bf16[256,1024]{1,0:T(8,128)(2,1)S(1)} %collective-permute-done.4.xb_ref), channel_id=1, source_target_pairs={{0,3},{1,0},{2,1},{3,2},{4,7},{5,4},{6,5},{7,6},{8,11},{9,8},{10,9... | collective-permute-start | bytes 1572872 | tf_op jit(solution)/shard_map/ppermute | solution.py:596
  75.5 31.2 %collective-permute-start.6 = (bf16[256,1024]{1,0:T(8,128)(2,1)S(1)}, bf16[256,1024]{1,0:T(8,128)(2,1)S(1)}, u32[]{:S(2)}, u32[]{:S(2)}) collective-permute-start(bf16[256,1024]{1,0:T(8,128)(2,1)S(1)} %get-tuple-element.280.gla_ref.gra_ref), channel_id=1, source_target_pairs={{0,1},{1,2},{2,3},{4,5},{5,6},{6,7},{8,9},{9,10},{10,11},{12,13},{... | collective-permute-start | bytes 1572872 | tf_op jit(solution)/shard_map/ppermute | solution.py:596
  76.8 38.9 %collective-permute-start.14 = (bf16[256,1024]{1,0:T(8,128)(2,1)S(1)}, bf16[256,1024]{1,0:T(8,128)(2,1)}, u32[]{:S(2)}, u32[]{:S(2)}) collective-permute-start(bf16[256,1024]{1,0:T(8,128)(2,1)S(1)} %get-tuple-element.280.gla_ref.gra_ref), channel_id=1, source_target_pairs={{1,0},{2,1},{3,2},{5,4},{6,5},{7,6},{9,8},{10,9},{11,10},{13,12},{... | collective-permute-start | bytes 1572872 | tf_op jit(solution)/shard_map/ppermute | solution.py:596
  78.1 34.0 %collective-permute-start.10 = (bf16[256,1024]{1,0:T(8,128)(2,1)S(1)}, bf16[256,1024]{1,0:T(8,128)(2,1)}, u32[]{:S(2)}, u32[]{:S(2)}) collective-permute-start(bf16[256,1024]{1,0:T(8,128)(2,1)S(1)} %get-tuple-element.281.glb_ref.grb_ref), channel_id=1, source_target_pairs={{0,1},{1,2},{2,3},{4,5},{5,6},{6,7},{8,9},{9,10},{10,11},{12,13},{... | collective-permute-start | bytes 1572872 | tf_op jit(solution)/shard_map/ppermute | solution.py:596
  83.5 35.2 %collective-permute-start.18 = (bf16[256,1024]{1,0:T(8,128)(2,1)S(1)}, bf16[256,1024]{1,0:T(8,128)(2,1)}, u32[]{:S(2)}, u32[]{:S(2)}) collective-permute-start(bf16[256,1024]{1,0:T(8,128)(2,1)S(1)} %get-tuple-element.281.glb_ref.grb_ref), channel_id=1, source_target_pairs={{1,0},{2,1},{3,2},{5,4},{6,5},{7,6},{9,8},{10,9},{11,10},{13,12},{... | collective-permute-start | bytes 1572872 | tf_op jit(solution)/shard_map/ppermute | solution.py:596
  107.6 16.9 %collective-permute-start.7 = (bf16[256,1024]{1,0:T(8,128)(2,1)S(1)}, bf16[256,1024]{1,0:T(8,128)(2,1)S(1)}, u32[]{:S(2)}, u32[]{:S(2)}) collective-permute-start(bf16[256,1024]{1,0:T(8,128)(2,1)S(1)} %join.20), channel_id=1, source_target_pairs={{0,1},{1,2},{2,3},{4,5},{5,6},{6,7},{8,9},{9,10},{10,11},{12,13},{... | collective-permute-start | bytes 1572872 | tf_op jit(solution)/shard_map/ppermute | solution.py:596
  113.8 21.9 %collective-permute-start.11 = (bf16[256,1024]{1,0:T(8,128)(2,1)S(1)}, bf16[256,1024]{1,0:T(8,128)(2,1)S(1)}, u32[]{:S(2)}, u32[]{:S(2)}) collective-permute-start(bf16[256,1024]{1,0:T(8,128)(2,1)S(1)} %join.23), channel_id=1, source_target_pairs={{0,1},{1,2},{2,3},{4,5},{5,6},{6,7},{8,9},{9,10},{10,11},{12,13},{... | collective-permute-start | bytes 1572872 | tf_op jit(solution)/shard_map/ppermute | solution.py:596
  117.4 23.6 %collective-permute-start.15 = (bf16[256,1024]{1,0:T(8,128)(2,1)S(1)}, bf16[256,1024]{1,0:T(8,128)(2,1)S(1)}, u32[]{:S(2)}, u32[]{:S(2)}) collective-permute-start(bf16[256,1024]{1,0:T(8,128)(2,1)S(1)} %join.26), channel_id=1, source_target_pairs={{1,0},{2,1},{3,2},{5,4},{6,5},{7,6},{9,8},{10,9},{11,10},{13,12},{... | collective-permute-start | bytes 1572872 | tf_op jit(solution)/shard_map/ppermute | solution.py:596
  120.3 24.5 %collective-permute-start.19 = (bf16[256,1024]{1,0:T(8,128)(2,1)S(1)}, bf16[256,1024]{1,0:T(8,128)(2,1)S(1)}, u32[]{:S(2)}, u32[]{:S(2)}) collective-permute-start(bf16[256,1024]{1,0:T(8,128)(2,1)S(1)} %join.29), channel_id=1, source_target_pairs={{1,0},{2,1},{3,2},{5,4},{6,5},{7,6},{9,8},{10,9},{11,10},{13,12},{... | collective-permute-start | bytes 1572872 | tf_op jit(solution)/shard_map/ppermute | solution.py:596
  125.3 21.8 %collective-permute-start.8 = (bf16[256,1024]{1,0:T(8,128)(2,1)S(1)}, bf16[256,1024]{1,0:T(8,128)(2,1)S(1)}, u32[]{:S(2)}, u32[]{:S(2)}) collective-permute-start(bf16[256,1024]{1,0:T(8,128)(2,1)S(1)} %join.21), channel_id=1, source_target_pairs={{0,1},{1,2},{2,3},{4,5},{5,6},{6,7},{8,9},{9,10},{10,11},{12,13},{... | collective-permute-start | bytes 1572872 | tf_op jit(solution)/shard_map/ppermute | solution.py:596
  136.5 21.7 %collective-permute-start.12 = (bf16[256,1024]{1,0:T(8,128)(2,1)S(1)}, bf16[256,1024]{1,0:T(8,128)(2,1)S(1)}, u32[]{:S(2)}, u32[]{:S(2)}) collective-permute-start(bf16[256,1024]{1,0:T(8,128)(2,1)S(1)} %join.24), channel_id=1, source_target_pairs={{0,1},{1,2},{2,3},{4,5},{5,6},{6,7},{8,9},{9,10},{10,11},{12,13},{... | collective-permute-start | bytes 1572872 | tf_op jit(solution)/shard_map/ppermute | solution.py:596
  141.8 21.7 %collective-permute-start.16 = (bf16[256,1024]{1,0:T(8,128)(2,1)S(1)}, bf16[256,1024]{1,0:T(8,128)(2,1)S(1)}, u32[]{:S(2)}, u32[]{:S(2)}) collective-permute-start(bf16[256,1024]{1,0:T(8,128)(2,1)S(1)} %join.27), channel_id=1, source_target_pairs={{1,0},{2,1},{3,2},{5,4},{6,5},{7,6},{9,8},{10,9},{11,10},{13,12},{... | collective-permute-start | bytes 1572872 | tf_op jit(solution)/shard_map/ppermute | solution.py:596
  145.6 21.6 %collective-permute-start.20 = (bf16[256,1024]{1,0:T(8,128)(2,1)S(1)}, bf16[256,1024]{1,0:T(8,128)(2,1)S(1)}, u32[]{:S(2)}, u32[]{:S(2)}) collective-permute-start(bf16[256,1024]{1,0:T(8,128)(2,1)S(1)} %join.30), channel_id=1, source_target_pairs={{1,0},{2,1},{3,2},{5,4},{6,5},{7,6},{9,8},{10,9},{11,10},{13,12},{... | collective-permute-start | bytes 1572872 | tf_op jit(solution)/shard_map/ppermute | solution.py:596
  147.9 24.5 %collective-permute-start.9 = (bf16[256,1024]{1,0:T(8,128)(2,1)S(1)}, bf16[256,1024]{1,0:T(8,128)(2,1)S(1)}, u32[]{:S(2)}, u32[]{:S(2)}) collective-permute-start(bf16[256,1024]{1,0:T(8,128)(2,1)S(1)} %join.22), channel_id=1, source_target_pairs={{0,1},{1,2},{2,3},{4,5},{5,6},{6,7},{8,9},{9,10},{10,11},{12,13},{... | collective-permute-start | bytes 1572872 | tf_op jit(solution)/shard_map/ppermute | solution.py:596
  159.0 17.3 %collective-permute-start.13 = (bf16[256,1024]{1,0:T(8,128)(2,1)S(1)}, bf16[256,1024]{1,0:T(8,128)(2,1)S(1)}, u32[]{:S(2)}, u32[]{:S(2)}) collective-permute-start(bf16[256,1024]{1,0:T(8,128)(2,1)S(1)} %join.25), channel_id=1, source_target_pairs={{0,1},{1,2},{2,3},{4,5},{5,6},{6,7},{8,9},{9,10},{10,11},{12,13},{... | collective-permute-start | bytes 1572872 | tf_op jit(solution)/shard_map/ppermute | solution.py:596
  164.2 16.3 %collective-permute-start.17 = (bf16[256,1024]{1,0:T(8,128)(2,1)S(1)}, bf16[256,1024]{1,0:T(8,128)(2,1)S(1)}, u32[]{:S(2)}, u32[]{:S(2)}) collective-permute-start(bf16[256,1024]{1,0:T(8,128)(2,1)S(1)} %join.28), channel_id=1, source_target_pairs={{1,0},{2,1},{3,2},{5,4},{6,5},{7,6},{9,8},{10,9},{11,10},{13,12},{... | collective-permute-start | bytes 1572872 | tf_op jit(solution)/shard_map/ppermute | solution.py:596
  168.0 18.1 %collective-permute-start.21 = (bf16[256,1024]{1,0:T(8,128)(2,1)S(1)}, bf16[256,1024]{1,0:T(8,128)(2,1)S(1)}, u32[]{:S(2)}, u32[]{:S(2)}) collective-permute-start(bf16[256,1024]{1,0:T(8,128)(2,1)S(1)} %join.31), channel_id=1, source_target_pairs={{1,0},{2,1},{3,2},{5,4},{6,5},{7,6},{9,8},{10,9},{11,10},{13,12},{... | collective-permute-start | bytes 1572872 | tf_op jit(solution)/shard_map/ppermute | solution.py:596
  188.2 23.5 %collective-permute-start.22 = (bf16[256,2048]{1,0:T(8,128)(2,1)S(1)}, bf16[256,2048]{1,0:T(8,128)(2,1)}, u32[]{:S(2)}, u32[]{:S(2)}) collective-permute-start(bf16[256,2048]{1,0:T(8,128)(2,1)S(1)} %add_convert_fusion.2.a_ref), channel_id=1, source_target_pairs={{0,3},{1,0},{2,1},{3,2},{4,7},{5,4},{6,5},{7,6},{8,11},{9,8},{10,9... | collective-permute-start | bytes 3145736 | tf_op jit(solution)/shard_map/ppermute | solution.py:596
  211.7 26.4 %collective-permute-start.23 = (bf16[256,2048]{1,0:T(8,128)(2,1)}, bf16[256,2048]{1,0:T(8,128)(2,1)}, u32[]{:S(2)}, u32[]{:S(2)}) collective-permute-start(bf16[256,2048]{1,0:T(8,128)(2,1)} %collective-permute-done.22.a_ref), channel_id=1, source_target_pairs={{0,3},{1,0},{2,1},{3,2},{4,7},{5,4},{6,5},{7,6},{8,11},{9,8},{10,9... | collective-permute-start | bytes 3145736 | tf_op jit(solution)/shard_map/ppermute | solution.py:596
  226.1 34.4 %collective-permute-start.25 = (bf16[256,2048]{1,0:T(8,128)(2,1)}, bf16[256,2048]{1,0:T(8,128)(2,1)S(1)}, u32[]{:S(2)}, u32[]{:S(2)}) collective-permute-start(bf16[256,2048]{1,0:T(8,128)(2,1)} %block_term.9), channel_id=1, source_target_pairs={{0,3},{1,0},{2,1},{3,2},{4,7},{5,4},{6,5},{7,6},{8,11},{9,8},{10,9... | collective-permute-start | bytes 3145736 | tf_op jit(solution)/shard_map/ppermute | solution.py:596
  238.1 44.8 %collective-permute-start.24 = (bf16[256,2048]{1,0:T(8,128)(2,1)}, bf16[256,2048]{1,0:T(8,128)(2,1)S(1)}, u32[]{:S(2)}, u32[]{:S(2)}) collective-permute-start(bf16[256,2048]{1,0:T(8,128)(2,1)} %collective-permute-done.23.a_ref), channel_id=1, source_target_pairs={{0,3},{1,0},{2,1},{3,2},{4,7},{5,4},{6,5},{7,6},{8,11},{9,8},{10,9... | collective-permute-start | bytes 3145736 | tf_op jit(solution)/shard_map/ppermute | solution.py:596
  260.9 38.4 %collective-permute-start.26 = (bf16[256,2048]{1,0:T(8,128)(2,1)S(1)}, bf16[256,2048]{1,0:T(8,128)(2,1)S(1)}, u32[]{:S(2)}, u32[]{:S(2)}) collective-permute-start(bf16[256,2048]{1,0:T(8,128)(2,1)S(1)} %add_convert_fusion.1), channel_id=1, source_target_pairs={{0,3},{1,0},{2,1},{3,2},{4,7},{5,4},{6,5},{7,6},{8,11},{9,8},{10,9... | collective-permute-start | bytes 3145736 | tf_op jit(solution)/shard_map/ppermute | solution.py:596
  302.4 18.7 %collective-permute-start.27 = (bf16[256,2048]{1,0:T(8,128)(2,1)S(1)}, bf16[256,2048]{1,0:T(8,128)(2,1)S(1)}, u32[]{:S(2)}, u32[]{:S(2)}) collective-permute-start(bf16[256,2048]{1,0:T(8,128)(2,1)S(1)} %block_term.11), channel_id=1, source_target_pairs={{0,3},{1,0},{2,1},{3,2},{4,7},{5,4},{6,5},{7,6},{8,11},{9,8},{10,9... | collective-permute-start | bytes 3145736 | tf_op jit(solution)/shard_map/ppermute | solution.py:596
  310.1 31.3 %collective-permute-start.29 = (bf16[2048,1024]{1,0:T(8,128)(2,1)}, bf16[2048,1024]{1,0:T(8,128)(2,1)}, u32[]{:S(2)}, u32[]{:S(2)}) collective-permute-start(bf16[2048,1024]{1,0:T(8,128)(2,1)} %grad_half.4), channel_id=1, source_target_pairs={{0,4},{4,0},{8,12},{12,8},{16,20},{20,16},{24,28},{28,24},{1,5},{5... | collective-permute-start | bytes 12582920 | tf_op jit(solution)/shard_map/ppermute | solution.py:617
  317.4 42.2 %collective-permute-start.32 = (bf16[2048,1024]{1,0:T(8,128)(2,1)}, bf16[2048,1024]{1,0:T(8,128)(2,1)}, u32[]{:S(2)}, u32[]{:S(2)}) collective-permute-start(bf16[2048,1024]{1,0:T(8,128)(2,1)} %grad_half.5), channel_id=1, source_target_pairs={{0,4},{4,0},{8,12},{12,8},{16,20},{20,16},{24,28},{28,24},{1,5},{5... | collective-permute-start | bytes 12582920 | tf_op jit(solution)/shard_map/ppermute | solution.py:617
  325.2 24.3 %collective-permute-start.28 = (bf16[256,2048]{1,0:T(8,128)(2,1)S(1)}, bf16[256,2048]{1,0:T(8,128)(2,1)S(1)}, u32[]{:S(2)}, u32[]{:S(2)}) collective-permute-start(bf16[256,2048]{1,0:T(8,128)(2,1)S(1)} %get-tuple-element.217.refs_0_), channel_id=1, source_target_pairs={{0,1},{1,2},{2,3},{4,5},{5,6},{6,7},{8,9},{9,10},{10,11},{12,13},{... | collective-permute-start | bytes 3145736 | tf_op jit(solution)/shard_map/ppermute | solution.py:596
  328.9 27.8 %collective-permute-start.31 = (bf16[256,2048]{1,0:T(8,128)(2,1)S(1)}, bf16[256,2048]{1,0:T(8,128)(2,1)S(1)}, u32[]{:S(2)}, u32[]{:S(2)}) collective-permute-start(bf16[256,2048]{1,0:T(8,128)(2,1)S(1)} %get-tuple-element.217.refs_0_), channel_id=1, source_target_pairs={{1,0},{2,1},{3,2},{5,4},{6,5},{7,6},{9,8},{10,9},{11,10},{13,12},{... | collective-permute-start | bytes 3145736 | tf_op jit(solution)/shard_map/ppermute | solution.py:596
  351.2 23.5 %collective-permute-start.30 = (bf16[256,2048]{1,0:T(8,128)(2,1)}, bf16[256,2048]{1,0:T(8,128)(2,1)}, u32[]{:S(2)}, u32[]{:S(2)}) collective-permute-start(bf16[256,2048]{1,0:T(8,128)(2,1)} %join.32), channel_id=1, source_target_pairs={{0,1},{1,2},{2,3},{4,5},{5,6},{6,7},{8,9},{9,10},{10,11},{12,13},{... | collective-permute-start | bytes 3145736 | tf_op jit(solution)/shard_map/ppermute | solution.py:596
  358.2 25.7 %collective-permute-start.35 = (bf16[256,2048]{1,0:T(8,128)(2,1)}, bf16[256,2048]{1,0:T(8,128)(2,1)}, u32[]{:S(2)}, u32[]{:S(2)}) collective-permute-start(bf16[256,2048]{1,0:T(8,128)(2,1)} %join.33), channel_id=1, source_target_pairs={{1,0},{2,1},{3,2},{5,4},{6,5},{7,6},{9,8},{10,9},{11,10},{13,12},{... | collective-permute-start | bytes 3145736 | tf_op jit(solution)/shard_map/ppermute | solution.py:596
  370.1 145.9 %reduce-scatter.5.cloned.1.call-start = ((), (), s32[]{:S(2)}) async-start(), calls=%async_computation.3 | async-start | bytes 5242880 | tf_op jit(solution)/shard_map/reduce_scatter | solution.py:746
  378.9 23.0 %collective-permute-start.33 = (bf16[256,2048]{1,0:T(8,128)(2,1)S(1)}, bf16[256,2048]{1,0:T(8,128)(2,1)S(1)}, u32[]{:S(2)}, u32[]{:S(2)}) collective-permute-start(bf16[256,2048]{1,0:T(8,128)(2,1)S(1)} %join.34), channel_id=1, source_target_pairs={{0,1},{1,2},{2,3},{4,5},{5,6},{6,7},{8,9},{9,10},{10,11},{12,13},{... | collective-permute-start | bytes 3145736 | tf_op jit(solution)/shard_map/ppermute | solution.py:596
  385.7 22.9 %collective-permute-start.36 = (bf16[256,2048]{1,0:T(8,128)(2,1)S(1)}, bf16[256,2048]{1,0:T(8,128)(2,1)S(1)}, u32[]{:S(2)}, u32[]{:S(2)}) collective-permute-start(bf16[256,2048]{1,0:T(8,128)(2,1)S(1)} %join.36), channel_id=1, source_target_pairs={{1,0},{2,1},{3,2},{5,4},{6,5},{7,6},{9,8},{10,9},{11,10},{13,12},{... | collective-permute-start | bytes 3145736 | tf_op jit(solution)/shard_map/ppermute | solution.py:596
  402.8 28.2 %collective-permute-start.34 = (bf16[256,2048]{1,0:T(8,128)(2,1)S(1)}, bf16[256,2048]{1,0:T(8,128)(2,1)S(1)}, u32[]{:S(2)}, u32[]{:S(2)}) collective-permute-start(bf16[256,2048]{1,0:T(8,128)(2,1)S(1)} %join.35), channel_id=1, source_target_pairs={{0,1},{1,2},{2,3},{4,5},{5,6},{6,7},{8,9},{9,10},{10,11},{12,13},{... | collective-permute-start | bytes 3145736 | tf_op jit(solution)/shard_map/ppermute | solution.py:596
  409.3 22.2 %collective-permute-start.37 = (bf16[256,2048]{1,0:T(8,128)(2,1)S(1)}, bf16[256,2048]{1,0:T(8,128)(2,1)S(1)}, u32[]{:S(2)}, u32[]{:S(2)}) collective-permute-start(bf16[256,2048]{1,0:T(8,128)(2,1)S(1)} %join.37), channel_id=1, source_target_pairs={{1,0},{2,1},{3,2},{5,4},{6,5},{7,6},{9,8},{10,9},{11,10},{13,12},{... | collective-permute-start | bytes 3145736 | tf_op jit(solution)/shard_map/ppermute | solution.py:596
  440.9 27.1 %collective-permute-start.38 = (bf16[256,2048]{1,0:T(8,128)(2,1)}, bf16[256,2048]{1,0:T(8,128)(2,1)}, u32[]{:S(2)}, u32[]{:S(2)}) collective-permute-start(bf16[256,2048]{1,0:T(8,128)(2,1)} %block_term.12), channel_id=1, source_target_pairs={{0,3},{1,0},{2,1},{3,2},{4,7},{5,4},{6,5},{7,6},{8,11},{9,8},{10,9... | collective-permute-start | bytes 3145736 | tf_op jit(solution)/shard_map/ppermute | solution.py:596
  470.8 29.8 %collective-permute-start.40 = (bf16[256,2048]{1,0:T(8,128)(2,1)}, bf16[256,2048]{1,0:T(8,128)(2,1)}, u32[]{:S(2)}, u32[]{:S(2)}) collective-permute-start(bf16[256,2048]{1,0:T(8,128)(2,1)} %join.38), channel_id=1, source_target_pairs={{0,3},{1,0},{2,1},{3,2},{4,7},{5,4},{6,5},{7,6},{8,11},{9,8},{10,9... | collective-permute-start | bytes 3145736 | tf_op jit(solution)/shard_map/ppermute | solution.py:596
  492.3 13.9 %collective-permute-start.45 = (f32[8320]{0:T(1024)S(1)}, f32[8320]{0:T(1024)S(1)}, u32[]{:S(2)}, u32[]{:S(2)}) collective-permute-start(f32[8320]{0:T(1024)S(1)} %add.133), channel_id=1, source_target_pairs={{0,1},{1,2},{2,3},{3,0},{4,5},{5,6},{6,7},{7,4},{8,9},{9,10},{10,1... | collective-permute-start | bytes 99848 | tf_op jit(solution)/shard_map/ppermute | solution.py:596
  492.4 13.8 %collective-permute-start.46 = (f32[8320]{0:T(1024)S(1)}, f32[8320]{0:T(1024)S(1)}, u32[]{:S(2)}, u32[]{:S(2)}) collective-permute-start(f32[8320]{0:T(1024)S(1)} %add.133), channel_id=1, source_target_pairs={{0,2},{1,3},{2,0},{3,1},{4,6},{5,7},{6,4},{7,5},{8,10},{9,11},{10,... | collective-permute-start | bytes 99848 | tf_op jit(solution)/shard_map/ppermute | solution.py:596
  503.3 24.6 %collective-permute-start.42 = (bf16[256,2048]{1,0:T(8,128)(2,1)}, bf16[256,2048]{1,0:T(8,128)(2,1)S(1)}, u32[]{:S(2)}, u32[]{:S(2)}) collective-permute-start(bf16[256,2048]{1,0:T(8,128)(2,1)} %join.39), channel_id=1, source_target_pairs={{0,3},{1,0},{2,1},{3,2},{4,7},{5,4},{6,5},{7,6},{8,11},{9,8},{10,9... | collective-permute-start | bytes 3145736 | tf_op jit(solution)/shard_map/ppermute | solution.py:596
  506.2 24.5 %collective-permute-start.48 = (f32[8320]{0:T(1024)S(1)}, f32[8320]{0:T(1024)S(1)}, u32[]{:S(2)}, u32[]{:S(2)}) collective-permute-start(f32[8320]{0:T(1024)S(1)} %add_add_fusion.2), channel_id=1, source_target_pairs={{0,8},{4,12},{8,16},{12,20},{16,24},{20,28},{24,0},{28,4},{1,9},{5... | collective-permute-start | bytes 99848 | tf_op jit(solution)/shard_map/ppermute | solution.py:791
  507.6 23.1 %collective-permute-start.49 = (f32[8320]{0:T(1024)S(1)}, f32[8320]{0:T(1024)S(1)}, u32[]{:S(2)}, u32[]{:S(2)}) collective-permute-start(f32[8320]{0:T(1024)S(1)} %add_add_fusion.2), channel_id=1, source_target_pairs={{0,16},{4,20},{8,24},{12,28},{16,0},{20,4},{24,8},{28,12},{1,17},{... | collective-permute-start | bytes 99848 | tf_op jit(solution)/shard_map/ppermute | solution.py:791
  508.9 21.8 %collective-permute-start.50 = (f32[8320]{0:T(1024)S(1)}, f32[8320]{0:T(1024)S(1)}, u32[]{:S(2)}, u32[]{:S(2)}) collective-permute-start(f32[8320]{0:T(1024)S(1)} %add_add_fusion.2), channel_id=1, source_target_pairs={{0,24},{4,28},{8,0},{12,4},{16,8},{20,12},{24,16},{28,20},{1,25},{... | collective-permute-start | bytes 99848 | tf_op jit(solution)/shard_map/ppermute | solution.py:791
  (93 other events, 809.0 us)
Sparse Core Ops, SparseCore 0:
  370.3 86.7 reduce-scatter.2
  462.2 53.7 reduce-scatter.4

commit v11 on v10

--- a/solution.py
+++ b/solution.py
@@ -557,6 +557,46 @@
     )(x, gain, term, moved, state)
 
 
+def rows_body(rank_ref, mine_ref, got_ref, *outs):
+    parts, _, half = got_ref.shape
+    width = outs[0].shape[1]
+    first = rank_ref[3] == 0
+
+    def put(low_ref, high_ref):
+        if width > half:
+            for p in range(parts):
+                outs[p][:, :half] = low_ref[p].astype(F32)
+                outs[p][:, half:] = high_ref[p].astype(F32)
+        else:
+            for o, (ref, at) in zip(outs, ((low_ref, 0), (low_ref, width), (high_ref, 0), (high_ref, width))):
+                o[...] = ref[0, :, at : at + width].astype(F32)
+
+    pl.when(first)(functools.partial(put, mine_ref, got_ref))
+    pl.when(jnp.logical_not(first))(functools.partial(put, got_ref, mine_ref))
+
+
+def whole_rows(rank, part, got, widths):
+    parts, span, half = got.shape
+    tile = min(64, span)
+    steps = span // tile
+    return pl.pallas_call(
+        rows_body,
+        grid_spec=pltpu.PrefetchScalarGridSpec(
+            num_scalar_prefetch=1,
+            grid=(steps,),
+            in_specs=[
+                pl.BlockSpec((parts, tile, half), lambda i, r: (0, r[3] * steps + i, 0)),
+                pl.BlockSpec((parts, tile, half), lambda i, r: (0, i, 0)),
+            ],
+            out_specs=[pl.BlockSpec((tile, w), lambda i, r: (i, 0)) for w in widths],
+        ),
+        out_shape=[jax.ShapeDtypeStruct((span, w), F32) for w in widths],
+        compiler_params=params(16),
+        cost_estimate=cost(1e6, 1e6),
+        name="whole_rows",
+    )(rank, part, got)
+
+
 def tie(values, *others):
     values = tuple(values)
     return lax.optimization_barrier(values + others)[: len(values)]
@@ -727,11 +767,10 @@
     )
     mixed = low(state + owned(ffn, right, left))
 
-    def whole(part):
-        span = part.shape[-2] // 2
-        mine = lax.dynamic_slice_in_dim(part, side * span, span, part.ndim - 2)
-        got = swap(lax.dynamic_slice_in_dim(part, (1 - side) * span, span, part.ndim - 2))
-        return jnp.where(side == 0, mine, got).astype(F32), jnp.where(side == 0, got, mine).astype(F32)
+    def whole(part, widths):
+        span = part.shape[1] // 2
+        got = swap(lax.dynamic_slice_in_dim(part, (1 - side) * span, span, 1))
+        return whole_rows(where, part, got, widths)
 
     tokens_of = lambda v: (flat(first_all), flat(state_all), flat(v), flat(masked), where)
     sent = block_term(dqkv, 1, weights, 1e6)
@@ -778,11 +817,8 @@
         ]
     )
     small = sum_over(small, "dp", [[(i, i ^ 1) for i in range(n_dp)]])
-    wide = jnp.concatenate(whole(wide_grad), axis=2)
     for s in range(3, n):
-        if s == 3:
-            moved, wide = tie([moved, wide])
-        sent = join(where, moved, terms[s][None], 0, n + 1, True, 0, 60e9)
+        sent = join(where, moved, terms[s][None], 0, n + 1, True, 0, 64e9)
         moved = hop(sent)
 
     planes = tie([send(small, [(i, (i + m) % n) for i in range(n)]) for m in range(1, n)], sent)
@@ -791,8 +827,10 @@
         lax.ppermute(small, "dp", [(i, (i + 2 * m) % n_dp) for i in range(n_dp)])
         for m in range(1, n_dp // 2)
     ]
-    query_key, value_out = whole(attn_grad)
-    moved, query_key, value_out = tie([moved, query_key, value_out])
+    wide = whole(wide_grad, [hidden] * 2)
+    weight_grads = whole(attn_grad[None], [local] * 4)
+    moved, *outs = tie([moved, *wide, *weight_grads])
+    wide, weight_grads = outs[:2], outs[2:]
     input_grad = last_step(own, gain1, terms[0], moved, grad_state)
     small = small + sum(tie(others, input_grad))
 
@@ -801,10 +839,7 @@
         input_grad[None],
         small[:d],
         small[d : 2 * d],
-        query_key[:, :local],
-        query_key[:, local:],
-        value_out[:, :local],
-        value_out[:, local:],
+        *weight_grads,
         small[2 * d : 3 * d],
         small[3 * d : 4 * d],
         wide[1],

time: 551 us -> 550 us (level)
  Pallas kernels: 199 us -> 206 us
    pallas_call x0 -> x2, Pallas kernels: none -> 7.37 us  [whole_rows(): pl.pallas_call(rows_body, grid_spec=pltpu.PrefetchScalarGridSpec(num_scal...]
    unnamed x179 -> x185, local copies, waits for them, and re-layouts: 22.8 us -> 25 us
  transfers between devices with their start and end apart: 53 -> 53, of which waited for: 24 -> 25; matrix products, arithmetic and copies ran while one was open for 9% -> 7% of each run, Pallas kernels for 36% -> 38%
where the time goes in v11:
time: 550 us; the launch traced here: 541 us
  Pallas kernels  206 us (37%)
  waiting for transfers between devices  131 us (24%)
  starting transfers between devices  119 us (22%)
  local copies, waits for them, and re-layouts  31.9 us (6%)
  other arithmetic  20.8 us (4%)
  between operations  16 us (3%)
  matrix products  15.6 us (3%)
    ppermute x42, waiting for transfers between devices, per_device(): send = lambda v, pairs: lax.ppermute(v, 'mp', pairs)  125 us
    ppermute x42, starting transfers between devices, per_device(): send = lambda v, pairs: lax.ppermute(v, 'mp', pairs)  114 us
    pallas_call x4, Pallas kernels, mlp_slot(): pl.pallas_call(functools.partial(mlp_body, slot, n), grid_spec=pltpu.Pref...  39.4 us
    pallas_call x4, Pallas kernels, grad_half(): pl.pallas_call(functools.partial(grad_body, not partner), grid_spec=pltpu...  29.6 us
    pallas_call x4, Pallas kernels, qkv_slot(): pl.pallas_call(qkv_body, grid_spec=pltpu.PrefetchScalarGridSpec(num_scala...  28.7 us
    pallas_call x20, Pallas kernels, join(): pl.pallas_call(functools.partial(join_body, 0 if right else -1, first), g...  25.5 us
    unnamed x185, local copies, waits for them, and re-layouts  25 us
    pallas_call x8, Pallas kernels, block_term(): pl.pallas_call(term_body, grid=(d // tile,), in_specs=[pl.BlockSpec((1, r...  23.8 us
  transfers between devices with their start and end apart: 53, of which 25 were waited for; matrix products, arithmetic and copies ran while one was open for 7% of the time, Pallas kernels for 38%

profile of v11, /device:TPU:0, one launch (start us, length us, event | category | flops | bytes accessed | tf_op | source)
XLA Modules:
  0.0 540.9 jit_solution(17434033643702414697)
XLA Ops:
  8.5 5.1 collective-permute-start
  17.9 7.1 %qkv_slot.4 = (bf16[4,256,2048]{2,1,0:T(8,128)(2,1)}, bf16[4,256,512]{2,1,0:T(8,128)(2,1)}, bf16[4,256,512]{2,1,0:T(8,128)(2,1)}, bf16[4,256,512]{2,1,0:T(8,128)(2,1)}) custom-call(s32[4]{0:T(128)} %pad_add_fusion.rank_ref, bf16[256,1024]{1,0:T(8,128)(2,1)} %copy-done.67, bf16[256,1024]{1,0:T(8,128)(2,1)} %copy-done.66, f32[1,2048]{1,0:T(1,128)} %bitcast.105, ...), custom_call_target="tpu_custom_call" | custom-call | flops 1610612736 | bytes 8388608 | tf_op jit(solution)/shard_map/qkv_slot/pallas_call | solution.py:106
  26.0 4.4 collective-permute-start.1
  30.3 6.8 %collective-permute-done.2.xb_ref = bf16[256,1024]{1,0:T(8,128)(2,1)S(1)} collective-permute-done((bf16[256,1024]{1,0:T(8,128)(2,1)S(1)}, bf16[256,1024]{1,0:T(8,128)(2,1)S(1)}, u32[]{:S(2)}, u32[]{:S(2)}) %collective-permute-start.2) | collective-permute-done | bytes 524320 | tf_op jit(solution)/shard_map/ppermute | solution.py:636
  37.2 4.3 collective-permute-start.4
  41.5 7.1 %qkv_slot.5 = (bf16[4,256,2048]{2,1,0:T(8,128)(2,1)}, bf16[4,256,512]{2,1,0:T(8,128)(2,1)}, bf16[4,256,512]{2,1,0:T(8,128)(2,1)}, bf16[4,256,512]{2,1,0:T(8,128)(2,1)}) custom-call(s32[4]{0:T(128)} %pad_add_fusion.rank_ref, ...), custom_call_target="tpu_custom_call", output_to_operand_aliasing={{0}: (10, {}), {1}: (11, {}), {2}: (12, {}), {3}: (13, {})} | custom-call | flops 1610612736 | bytes 8388608 | tf_op jit(solution)/shard_map/qkv_slot/pallas_call | solution.py:106
  52.7 7.0 %collective-permute-done.4.xb_ref = bf16[256,1024]{1,0:T(8,128)(2,1)S(1)} collective-permute-done((bf16[256,1024]{1,0:T(8,128)(2,1)S(1)}, bf16[256,1024]{1,0:T(8,128)(2,1)S(1)}, u32[]{:S(2)}, u32[]{:S(2)}) %collective-permute-start.4) | collective-permute-done | bytes 524320 | tf_op jit(solution)/shard_map/ppermute | solution.py:636
  68.1 7.3 %qkv_slot.6 = (bf16[4,256,2048]{2,1,0:T(8,128)(2,1)}, bf16[4,256,512]{2,1,0:T(8,128)(2,1)}, bf16[4,256,512]{2,1,0:T(8,128)(2,1)}, bf16[4,256,512]{2,1,0:T(8,128)(2,1)}) custom-call(s32[4]{0:T(128)} %pad_add_fusion.rank_ref, bf16[256,1024]{1,0:T(8,128)(2,1)} %copy-done.73, ...), custom_call_target="tpu_custom_call", output_to_operand_aliasing={{0}: (10, {}), {1}: (11, {}), {2}: (12, {}), {3}: (13, {})} | custom-call | flops 1610612736 | bytes 8388608 | tf_op jit(solution)/shard_map/qkv_slot/pallas_call | solution.py:106
  78.1 5.4 collective-permute-start.10
  85.0 7.1 %qkv_slot.7 = (bf16[4,256,2048]{2,1,0:T(8,128)(2,1)}, bf16[4,256,512]{2,1,0:T(8,128)(2,1)}, bf16[4,256,512]{2,1,0:T(8,128)(2,1)}, bf16[4,256,512]{2,1,0:T(8,128)(2,1)}) custom-call(s32[4]{0:T(128)} %pad_add_fusion.rank_ref, bf16[256,1024]{1,0:T(8,128)(2,1)} %copy-done.72, ...), custom_call_target="tpu_custom_call", output_to_operand_aliasing={{0}: (10, {}), {1}: (11, {}), {2}: (12, {}), {3}: (13, {})} | custom-call | flops 1610612736 | bytes 8388608 | tf_op jit(solution)/shard_map/qkv_slot/pallas_call | solution.py:106
  92.1 10.3 %attend.1 = bf16[4,256,512]{2,1,0:T(8,128)(2,1)} custom-call(s32[4]{0:T(128)} %pad_add_fusion.rank_ref, bf16[4,256,512]{2,1,0:T(8,128)(2,1)} %get-tuple-element.183.q_ref, bf16[4,256,512]{2,1,0:T(8,128)(2,1)} %get-tuple-element.184.k_ref, bf16[4,256,512]{2,1,0:T(8,128)(2,1)} %get-tuple-element.185.v_ref, s32[4,256,1]{2,1,0:T(8,128)} %reshape.204.dcol_ref, ...), custom_call_target="tpu_custom_call" | custom-call | flops 2147483648 | bytes 4194304 | tf_op jit(solution)/shard_map/attend/pallas_call | solution.py:169
  102.4 4.3 convolution_convert_fusion.1
  107.6 4.5 collective-permute-start.7
  125.2 4.4 collective-permute-start.8
  129.7 6.0 %collective-permute-done.11.moved_ref.grb_ref = bf16[256,1024]{1,0:T(8,128)(2,1)S(1)} collective-permute-done((bf16[256,1024]{1,0:T(8,128)(2,1)S(1)}, bf16[256,1024]{1,0:T(8,128)(2,1)S(1)}, u32[]{:S(2)}, u32[]{:S(2)}) %collective-permute-start.11) | collective-permute-done | bytes 524320 | tf_op jit(solution)/shard_map/ppermute | solution.py:636
  136.5 4.4 collective-permute-start.12
  147.9 5.2 collective-permute-start.9
  153.1 5.0 collective-permute-done.12.moved_ref.grb_ref
  159.0 4.4 collective-permute-start.13
  180.5 5.6 %collective-permute-done.21 = bf16[256,1024]{1,0:T(8,128)(2,1)S(1)} collective-permute-done((bf16[256,1024]{1,0:T(8,128)(2,1)S(1)}, bf16[256,1024]{1,0:T(8,128)(2,1)S(1)}, u32[]{:S(2)}, u32[]{:S(2)}) %collective-permute-start.21) | collective-permute-done | bytes 524320 | tf_op jit(solution)/shard_map/ppermute | solution.py:636
  190.5 9.3 %mlp_slot.4 = (bf16[4,256,2048]{2,1,0:T(8,128)(2,1)S(1)}, bf16[4,256,2048]{2,1,0:T(8,128)(2,1)S(1)}, bf16[4,256,2048]{2,1,0:T(8,128)(2,1)S(1)}, bf16[4,256,2048]{2,1,0:T(8,128)(2,1)S(1)}) custom-call(s32[4]{0:T(128)S(1)} %copy-done.51, bf16[256,2048]{1,0:T(8,128)(2,1)S(1)} %add_convert_fusion.2.a_ref, ...), custom_call_target="tpu_custom_call" | custom-call | flops 4294967296 | bytes 20971520 | tf_op jit(solution)/shard_map/mlp_slot/pallas_call | solution.py:303
  207.3 4.4 collective-permute-done.22.a_ref
  211.9 10.3 %mlp_slot.5 = (bf16[4,256,2048]{2,1,0:T(8,128)(2,1)S(1)}, bf16[4,256,2048]{2,1,0:T(8,128)(2,1)S(1)}, bf16[4,256,2048]{2,1,0:T(8,128)(2,1)S(1)}, bf16[4,256,2048]{2,1,0:T(8,128)(2,1)S(1)}) custom-call(s32[4]{0:T(128)S(1)} %copy-done.51, ...), custom_call_target="tpu_custom_call", output_to_operand_aliasing={{0}: (9, {}), {1}: (10, {}), {2}: (11, {}), {3}: (12, {})} | custom-call | flops 4294967296 | bytes 20971520 | tf_op jit(solution)/shard_map/mlp_slot/pallas_call | solution.py:303
  228.2 9.9 %collective-permute-done.23.a_ref = bf16[256,2048]{1,0:T(8,128)(2,1)} collective-permute-done((bf16[256,2048]{1,0:T(8,128)(2,1)}, bf16[256,2048]{1,0:T(8,128)(2,1)}, u32[]{:S(2)}, u32[]{:S(2)}) %collective-permute-start.23) | collective-permute-done | bytes 1048608 | tf_op jit(solution)/shard_map/ppermute | solution.py:636
  240.1 9.6 %mlp_slot.6 = (bf16[4,256,2048]{2,1,0:T(8,128)(2,1)S(1)}, bf16[4,256,2048]{2,1,0:T(8,128)(2,1)S(1)}, bf16[4,256,2048]{2,1,0:T(8,128)(2,1)S(1)}, bf16[4,256,2048]{2,1,0:T(8,128)(2,1)S(1)}) custom-call(s32[4]{0:T(128)S(1)} %copy-done.51, ...), custom_call_target="tpu_custom_call", output_to_operand_aliasing={{0}: (9, {}), {1}: (10, {}), {2}: (11, {}), {3}: (12, {})} | custom-call | flops 4294967296 | bytes 20971520 | tf_op jit(solution)/shard_map/mlp_slot/pallas_call | solution.py:303
  252.8 7.6 %collective-permute-done.25 = bf16[256,2048]{1,0:T(8,128)(2,1)S(1)} collective-permute-done((bf16[256,2048]{1,0:T(8,128)(2,1)}, bf16[256,2048]{1,0:T(8,128)(2,1)S(1)}, u32[]{:S(2)}, u32[]{:S(2)}) %collective-permute-start.25) | collective-permute-done | bytes 1048608 | tf_op jit(solution)/shard_map/ppermute | solution.py:636
  262.9 20.0 %collective-permute-done.24.a_ref = bf16[256,2048]{1,0:T(8,128)(2,1)S(1)} collective-permute-done((bf16[256,2048]{1,0:T(8,128)(2,1)}, bf16[256,2048]{1,0:T(8,128)(2,1)S(1)}, u32[]{:S(2)}, u32[]{:S(2)}) %collective-permute-start.24) | collective-permute-done | bytes 1048608 | tf_op jit(solution)/shard_map/ppermute | solution.py:636
  282.9 10.2 %mlp_slot.7 = (bf16[4,256,2048]{2,1,0:T(8,128)(2,1)S(1)}, bf16[4,256,2048]{2,1,0:T(8,128)(2,1)S(1)}, bf16[4,256,2048]{2,1,0:T(8,128)(2,1)S(1)}, bf16[4,256,2048]{2,1,0:T(8,128)(2,1)S(1)}) custom-call(s32[4]{0:T(128)S(1)} %copy-done.51, ...), custom_call_target="tpu_custom_call", output_to_operand_aliasing={{0}: (9, {}), {1}: (10, {}), {2}: (11, {}), {3}: (12, {})} | custom-call | flops 4294967296 | bytes 20971520 | tf_op jit(solution)/shard_map/mlp_slot/pallas_call | solution.py:303
  293.1 6.1 %collective-permute-done.26.rest_0_ = bf16[256,2048]{1,0:T(8,128)(2,1)S(1)} collective-permute-done((bf16[256,2048]{1,0:T(8,128)(2,1)S(1)}, bf16[256,2048]{1,0:T(8,128)(2,1)S(1)}, u32[]{:S(2)}, u32[]{:S(2)}) %collective-permute-start.26) | collective-permute-done | bytes 1048608 | tf_op jit(solution)/shard_map/ppermute | solution.py:636
  302.9 7.2 %grad_half.4 = bf16[2048,1024]{1,0:T(8,128)(2,1)} custom-call(s32[4]{0:T(128)S(1)} %copy-done.51, bf16[1024,2048]{1,0:T(8,128)(2,1)S(1)} %bitcast.93, bf16[1024,2048]{1,0:T(8,128)(2,1)S(1)} %bitcast.88), custom_call_target="tpu_custom_call" | custom-call | flops 1000000 | bytes 1000000 | tf_op jit(solution)/shard_map/grad_half/pallas_call | solution.py:413
  310.1 7.2 %grad_half.5 = bf16[2048,1024]{1,0:T(8,128)(2,1)} custom-call(s32[4]{0:T(128)S(1)} %copy-done.51, bf16[1024,2048]{1,0:T(8,128)(2,1)S(1)} %bitcast.91, bf16[1024,2048]{1,0:T(8,128)(2,1)S(1)} %bitcast.72), custom_call_target="tpu_custom_call" | custom-call | flops 1000000 | bytes 1000000 | tf_op jit(solution)/shard_map/grad_half/pallas_call | solution.py:413
  330.1 11.3 %convolution_convert_fusion = bf16[1024,2048]{1,0:T(8,128)(2,1)S(1)} fusion(bf16[1024,2048]{1,0:T(8,128)(2,1)S(1)} %bitcast.89, bf16[2048,2048]{1,0:T(8,128)(2,1)} %down_ref.7), kind=kOutput, calls=%fused_computation | convolution fusion | flops 8592031744 | bytes 16777216 | tf_op jit(solution)/shard_map/dot_general | solution.py:53
  341.5 8.0 %grad_half.6.rest_1_ = bf16[2,2048,1024]{2,1,0:T(8,128)(2,1)S(1)} custom-call(s32[4]{0:T(128)S(1)} %copy-done.51, bf16[1024,2048]{1,0:T(8,128)(2,1)S(1)} %bitcast.94, bf16[1024,2048]{1,0:T(8,128)(2,1)S(1)} %bitcast.90, bf16[2048,1024]{1,0:T(8,128)(2,1)} %collective-permute-done.29.rest_0_), custom_call_target="tpu_custom_call" | custom-call | flops 1000000 | bytes 1000000 | tf_op jit(solution)/shard_map/grad_half/pallas_call | solution.py:413
  351.2 5.4 %collective-permute-start.30 = (bf16[256,2048]{1,0:T(8,128)(2,1)}, bf16[256,2048]{1,0:T(8,128)(2,1)}, u32[]{:S(2)}, u32[]{:S(2)}) collective-permute-start(bf16[256,2048]{1,0:T(8,128)(2,1)} %join.32), channel_id=1, source_target_pairs={{0,1},{1,2},{2,3},{4,5},{5,6},{6,7},{8,9},{9,10},{10,11},{12,13},{... | collective-permute-start | bytes 3145736 | tf_op jit(solution)/shard_map/ppermute | solution.py:636
  359.5 7.2 %grad_half.7 = bf16[2,2048,1024]{2,1,0:T(8,128)(2,1)S(1)} custom-call(s32[4]{0:T(128)S(1)} %copy-done.51, bf16[1024,2048]{1,0:T(8,128)(2,1)S(1)} %bitcast.92, bf16[1024,2048]{1,0:T(8,128)(2,1)S(1)} %bitcast.73, bf16[2048,1024]{1,0:T(8,128)(2,1)} %collective-permute-done.32.rest_0_, ...), custom_call_target="tpu_custom_call", output_to_operand_aliasing={{}: (4, {})} | custom-call | flops 1000000 | bytes 1000000 | tf_op jit(solution)/shard_map/grad_half/pallas_call | solution.py:413
  370.1 4.6 collective-permute-done.30.moved_ref.refs_2_
  378.8 5.1 collective-permute-start.33
  391.4 10.4 %collective-permute-done.33.moved_ref.refs_1_ = bf16[256,2048]{1,0:T(8,128)(2,1)S(1)} collective-permute-done((bf16[256,2048]{1,0:T(8,128)(2,1)S(1)}, bf16[256,2048]{1,0:T(8,128)(2,1)S(1)}, u32[]{:S(2)}, u32[]{:S(2)}) %collective-permute-start.33) | collective-permute-done | bytes 1048608 | tf_op jit(solution)/shard_map/ppermute | solution.py:636
  402.7 4.5 collective-permute-start.34
  413.3 14.4 %attend_back.1.x_ref = bf16[4,256,1536]{2,1,0:T(8,128)(2,1)S(1)} custom-call(s32[4]{0:T(128)S(1)} %copy-done.51, bf16[4,256,512]{2,1,0:T(8,128)(2,1)S(1)} %copy-done.23, bf16[4,256,512]{2,1,0:T(8,128)(2,1)S(1)} %copy-done.24, bf16[4,256,512]{2,1,0:T(8,128)(2,1)S(1)} %copy-done.25, bf16[4,256,512]{2,1,0:T(8,128)(2,1)S(1)} %get-tuple-element.235.do_ref, ...), custom_call_target="tpu_custom_call" | custom-call | flops 115999997952 | bytes 7340032 | tf_op jit(solution)/shard_map/attend_back/pallas_call | solution.py:251
  432.9 7.4 %attn_grads.2 = bf16[2048,1024]{1,0:T(8,128)(2,1)S(1)} custom-call(s32[4]{0:T(128)S(1)} %copy-done.51, bf16[1024,2048]{1,0:T(8,128)(2,1)S(1)} %bitcast.85, bf16[1024,2048]{1,0:T(8,128)(2,1)S(1)} %bitcast.95, bf16[1024,1536]{1,0:T(8,128)(2,1)S(1)} %bitcast.74, bf16[1024,1536]{1,0:T(8,128)(2,1)S(1)} %bitcast.75, bf16[1024,512]{1,0:T(8,128)(2,1)S(1)} %bitcast.102), custom_call_target="tpu_custom_call" | custom-call | flops 4000000000 | bytes 1000000 | tf_op jit(solution)/shard_map/attn_grads/pallas_call | solution.py:456
  449.8 10.6 %attn_grads.3 = bf16[2048,1024]{1,0:T(8,128)(2,1)} custom-call(s32[4]{0:T(128)S(1)} %copy-done.51, bf16[1024,2048]{1,0:T(8,128)(2,1)} %bitcast.84, bf16[1024,2048]{1,0:T(8,128)(2,1)} %bitcast.96, bf16[1024,1536]{1,0:T(8,128)(2,1)} %bitcast.76, bf16[1024,1536]{1,0:T(8,128)(2,1)} %bitcast.77, bf16[1024,512]{1,0:T(8,128)(2,1)S(1)} %bitcast.103, ...), custom_call_target="tpu_custom_call" | custom-call | flops 1000000 | bytes 1000000 | tf_op jit(solution)/shard_map/attn_grads/pallas_call | solution.py:456
  461.4 6.3 %collective-permute-done.38.moved_ref = bf16[256,2048]{1,0:T(8,128)(2,1)} collective-permute-done((bf16[256,2048]{1,0:T(8,128)(2,1)}, bf16[256,2048]{1,0:T(8,128)(2,1)}, u32[]{:S(2)}, u32[]{:S(2)}) %collective-permute-start.38) | collective-permute-done | bytes 1048608 | tf_op jit(solution)/shard_map/ppermute | solution.py:636
  471.9 4.4 collective-permute-start.40
  494.8 5.5 %collective-permute-done.40.moved_ref = bf16[256,2048]{1,0:T(8,128)(2,1)} collective-permute-done((bf16[256,2048]{1,0:T(8,128)(2,1)}, bf16[256,2048]{1,0:T(8,128)(2,1)}, u32[]{:S(2)}, u32[]{:S(2)}) %collective-permute-start.40) | collective-permute-done | bytes 1048608 | tf_op jit(solution)/shard_map/ppermute | solution.py:636
  503.0 4.3 collective-permute-start.41
  511.8 4.5 reduce-scatter.5.cloned.1.call-done
  521.7 5.0 whole_rows.2
  (343 shorter events, 188.3 us)
Async XLA Ops:
  7.2 453.2 %reduce-scatter.3.cloned.1.call-start = ((), (), s32[]{:S(2)}) async-start(), calls=%async_computation.2 | async-start | bytes 10485760 | tf_op jit(solution)/shard_map/reduce_scatter | solution.py:757
  8.5 17.4 %collective-permute-start = (bf16[256,1024]{1,0:T(8,128)(2,1)S(1)}, bf16[256,1024]{1,0:T(8,128)(2,1)}, u32[]{:S(2)}, u32[]{:S(2)}) collective-permute-start(bf16[256,1024]{1,0:T(8,128)(2,1)S(1)} %get-tuple-element.289.xa_ref), channel_id=1, source_target_pairs={{0,3},{1,0},{2,1},{3,2},{4,7},{5,4},{6,5},{7,6},{8,11},{9,8},{10,9... | collective-permute-start | bytes 1572872 | tf_op jit(solution)/shard_map/ppermute | solution.py:636
  13.6 23.6 %collective-permute-start.2 = (bf16[256,1024]{1,0:T(8,128)(2,1)S(1)}, bf16[256,1024]{1,0:T(8,128)(2,1)S(1)}, u32[]{:S(2)}, u32[]{:S(2)}) collective-permute-start(bf16[256,1024]{1,0:T(8,128)(2,1)S(1)} %get-tuple-element.288.xb_ref), channel_id=1, source_target_pairs={{0,3},{1,0},{2,1},{3,2},{4,7},{5,4},{6,5},{7,6},{8,11},{9,8},{10,9... | collective-permute-start | bytes 1572872 | tf_op jit(solution)/shard_map/ppermute | solution.py:636
  26.0 22.7 %collective-permute-start.1 = (bf16[256,1024]{1,0:T(8,128)(2,1)}, bf16[256,1024]{1,0:T(8,128)(2,1)S(1)}, u32[]{:S(2)}, u32[]{:S(2)}) collective-permute-start(bf16[256,1024]{1,0:T(8,128)(2,1)} %collective-permute-done.xa_ref), channel_id=1, source_target_pairs={{0,3},{1,0},{2,1},{3,2},{4,7},{5,4},{6,5},{7,6},{8,11},{9,8},{10,9... | collective-permute-start | bytes 1572872 | tf_op jit(solution)/shard_map/ppermute | solution.py:636
  37.2 22.5 %collective-permute-start.4 = (bf16[256,1024]{1,0:T(8,128)(2,1)S(1)}, bf16[256,1024]{1,0:T(8,128)(2,1)S(1)}, u32[]{:S(2)}, u32[]{:S(2)}) collective-permute-start(bf16[256,1024]{1,0:T(8,128)(2,1)S(1)} %collective-permute-done.2.xb_ref), channel_id=1, source_target_pairs={{0,3},{1,0},{2,1},{3,2},{4,7},{5,4},{6,5},{7,6},{8,11},{9,8},{10,9... | collective-permute-start | bytes 1572872 | tf_op jit(solution)/shard_map/ppermute | solution.py:636
  48.6 26.7 %collective-permute-start.3 = (bf16[256,1024]{1,0:T(8,128)(2,1)S(1)}, bf16[256,1024]{1,0:T(8,128)(2,1)S(1)}, u32[]{:S(2)}, u32[]{:S(2)}) collective-permute-start(bf16[256,1024]{1,0:T(8,128)(2,1)S(1)} %collective-permute-done.1.xa_ref), channel_id=1, source_target_pairs={{0,3},{1,0},{2,1},{3,2},{4,7},{5,4},{6,5},{7,6},{8,11},{9,8},{10,9... | collective-permute-start | bytes 1572872 | tf_op jit(solution)/shard_map/ppermute | solution.py:636
  59.7 25.3 %collective-permute-start.5 = (bf16[256,1024]{1,0:T(8,128)(2,1)S(1)}, bf16[256,1024]{1,0:T(8,128)(2,1)}, u32[]{:S(2)}, u32[]{:S(2)}) collective-permute-start(bf16[256,1024]{1,0:T(8,128)(2,1)S(1)} %collective-permute-done.4.xb_ref), channel_id=1, source_target_pairs={{0,3},{1,0},{2,1},{3,2},{4,7},{5,4},{6,5},{7,6},{8,11},{9,8},{10,9... | collective-permute-start | bytes 1572872 | tf_op jit(solution)/shard_map/ppermute | solution.py:636
  75.5 31.3 %collective-permute-start.6 = (bf16[256,1024]{1,0:T(8,128)(2,1)S(1)}, bf16[256,1024]{1,0:T(8,128)(2,1)S(1)}, u32[]{:S(2)}, u32[]{:S(2)}) collective-permute-start(bf16[256,1024]{1,0:T(8,128)(2,1)S(1)} %get-tuple-element.286.gla_ref.gra_ref), channel_id=1, source_target_pairs={{0,1},{1,2},{2,3},{4,5},{5,6},{6,7},{8,9},{9,10},{10,11},{12,13},{... | collective-permute-start | bytes 1572872 | tf_op jit(solution)/shard_map/ppermute | solution.py:636
  76.8 38.9 %collective-permute-start.14 = (bf16[256,1024]{1,0:T(8,128)(2,1)S(1)}, bf16[256,1024]{1,0:T(8,128)(2,1)}, u32[]{:S(2)}, u32[]{:S(2)}) collective-permute-start(bf16[256,1024]{1,0:T(8,128)(2,1)S(1)} %get-tuple-element.286.gla_ref.gra_ref), channel_id=1, source_target_pairs={{1,0},{2,1},{3,2},{5,4},{6,5},{7,6},{9,8},{10,9},{11,10},{13,12},{... | collective-permute-start | bytes 1572872 | tf_op jit(solution)/shard_map/ppermute | solution.py:636
  78.1 34.0 %collective-permute-start.10 = (bf16[256,1024]{1,0:T(8,128)(2,1)S(1)}, bf16[256,1024]{1,0:T(8,128)(2,1)}, u32[]{:S(2)}, u32[]{:S(2)}) collective-permute-start(bf16[256,1024]{1,0:T(8,128)(2,1)S(1)} %get-tuple-element.287.glb_ref.grb_ref), channel_id=1, source_target_pairs={{0,1},{1,2},{2,3},{4,5},{5,6},{6,7},{8,9},{9,10},{10,11},{12,13},{... | collective-permute-start | bytes 1572872 | tf_op jit(solution)/shard_map/ppermute | solution.py:636
  83.5 35.2 %collective-permute-start.18 = (bf16[256,1024]{1,0:T(8,128)(2,1)S(1)}, bf16[256,1024]{1,0:T(8,128)(2,1)}, u32[]{:S(2)}, u32[]{:S(2)}) collective-permute-start(bf16[256,1024]{1,0:T(8,128)(2,1)S(1)} %get-tuple-element.287.glb_ref.grb_ref), channel_id=1, source_target_pairs={{1,0},{2,1},{3,2},{5,4},{6,5},{7,6},{9,8},{10,9},{11,10},{13,12},{... | collective-permute-start | bytes 1572872 | tf_op jit(solution)/shard_map/ppermute | solution.py:636
  113.8 21.9 %collective-permute-start.11 = (bf16[256,1024]{1,0:T(8,128)(2,1)S(1)}, bf16[256,1024]{1,0:T(8,128)(2,1)S(1)}, u32[]{:S(2)}, u32[]{:S(2)}) collective-permute-start(bf16[256,1024]{1,0:T(8,128)(2,1)S(1)} %join.23), channel_id=1, source_target_pairs={{0,1},{1,2},{2,3},{4,5},{5,6},{6,7},{8,9},{9,10},{10,11},{12,13},{... | collective-permute-start | bytes 1572872 | tf_op jit(solution)/shard_map/ppermute | solution.py:636
  117.3 23.6 %collective-permute-start.15 = (bf16[256,1024]{1,0:T(8,128)(2,1)S(1)}, bf16[256,1024]{1,0:T(8,128)(2,1)S(1)}, u32[]{:S(2)}, u32[]{:S(2)}) collective-permute-start(bf16[256,1024]{1,0:T(8,128)(2,1)S(1)} %join.26), channel_id=1, source_target_pairs={{1,0},{2,1},{3,2},{5,4},{6,5},{7,6},{9,8},{10,9},{11,10},{13,12},{... | collective-permute-start | bytes 1572872 | tf_op jit(solution)/shard_map/ppermute | solution.py:636
  120.3 24.6 %collective-permute-start.19 = (bf16[256,1024]{1,0:T(8,128)(2,1)S(1)}, bf16[256,1024]{1,0:T(8,128)(2,1)S(1)}, u32[]{:S(2)}, u32[]{:S(2)}) collective-permute-start(bf16[256,1024]{1,0:T(8,128)(2,1)S(1)} %join.29), channel_id=1, source_target_pairs={{1,0},{2,1},{3,2},{5,4},{6,5},{7,6},{9,8},{10,9},{11,10},{13,12},{... | collective-permute-start | bytes 1572872 | tf_op jit(solution)/shard_map/ppermute | solution.py:636
  125.2 21.8 %collective-permute-start.8 = (bf16[256,1024]{1,0:T(8,128)(2,1)S(1)}, bf16[256,1024]{1,0:T(8,128)(2,1)S(1)}, u32[]{:S(2)}, u32[]{:S(2)}) collective-permute-start(bf16[256,1024]{1,0:T(8,128)(2,1)S(1)} %join.21), channel_id=1, source_target_pairs={{0,1},{1,2},{2,3},{4,5},{5,6},{6,7},{8,9},{9,10},{10,11},{12,13},{... | collective-permute-start | bytes 1572872 | tf_op jit(solution)/shard_map/ppermute | solution.py:636
  136.5 21.7 %collective-permute-start.12 = (bf16[256,1024]{1,0:T(8,128)(2,1)S(1)}, bf16[256,1024]{1,0:T(8,128)(2,1)S(1)}, u32[]{:S(2)}, u32[]{:S(2)}) collective-permute-start(bf16[256,1024]{1,0:T(8,128)(2,1)S(1)} %join.24), channel_id=1, source_target_pairs={{0,1},{1,2},{2,3},{4,5},{5,6},{6,7},{8,9},{9,10},{10,11},{12,13},{... | collective-permute-start | bytes 1572872 | tf_op jit(solution)/shard_map/ppermute | solution.py:636
  141.7 21.7 %collective-permute-start.16 = (bf16[256,1024]{1,0:T(8,128)(2,1)S(1)}, bf16[256,1024]{1,0:T(8,128)(2,1)S(1)}, u32[]{:S(2)}, u32[]{:S(2)}) collective-permute-start(bf16[256,1024]{1,0:T(8,128)(2,1)S(1)} %join.27), channel_id=1, source_target_pairs={{1,0},{2,1},{3,2},{5,4},{6,5},{7,6},{9,8},{10,9},{11,10},{13,12},{... | collective-permute-start | bytes 1572872 | tf_op jit(solution)/shard_map/ppermute | solution.py:636
  145.6 21.6 %collective-permute-start.20 = (bf16[256,1024]{1,0:T(8,128)(2,1)S(1)}, bf16[256,1024]{1,0:T(8,128)(2,1)S(1)}, u32[]{:S(2)}, u32[]{:S(2)}) collective-permute-start(bf16[256,1024]{1,0:T(8,128)(2,1)S(1)} %join.30), channel_id=1, source_target_pairs={{1,0},{2,1},{3,2},{5,4},{6,5},{7,6},{9,8},{10,9},{11,10},{13,12},{... | collective-permute-start | bytes 1572872 | tf_op jit(solution)/shard_map/ppermute | solution.py:636
  147.9 24.5 %collective-permute-start.9 = (bf16[256,1024]{1,0:T(8,128)(2,1)S(1)}, bf16[256,1024]{1,0:T(8,128)(2,1)S(1)}, u32[]{:S(2)}, u32[]{:S(2)}) collective-permute-start(bf16[256,1024]{1,0:T(8,128)(2,1)S(1)} %join.22), channel_id=1, source_target_pairs={{0,1},{1,2},{2,3},{4,5},{5,6},{6,7},{8,9},{9,10},{10,11},{12,13},{... | collective-permute-start | bytes 1572872 | tf_op jit(solution)/shard_map/ppermute | solution.py:636
  159.0 17.3 %collective-permute-start.13 = (bf16[256,1024]{1,0:T(8,128)(2,1)S(1)}, bf16[256,1024]{1,0:T(8,128)(2,1)S(1)}, u32[]{:S(2)}, u32[]{:S(2)}) collective-permute-start(bf16[256,1024]{1,0:T(8,128)(2,1)S(1)} %join.25), channel_id=1, source_target_pairs={{0,1},{1,2},{2,3},{4,5},{5,6},{6,7},{8,9},{9,10},{10,11},{12,13},{... | collective-permute-start | bytes 1572872 | tf_op jit(solution)/shard_map/ppermute | solution.py:636
  168.1 18.1 %collective-permute-start.21 = (bf16[256,1024]{1,0:T(8,128)(2,1)S(1)}, bf16[256,1024]{1,0:T(8,128)(2,1)S(1)}, u32[]{:S(2)}, u32[]{:S(2)}) collective-permute-start(bf16[256,1024]{1,0:T(8,128)(2,1)S(1)} %join.31), channel_id=1, source_target_pairs={{1,0},{2,1},{3,2},{5,4},{6,5},{7,6},{9,8},{10,9},{11,10},{13,12},{... | collective-permute-start | bytes 1572872 | tf_op jit(solution)/shard_map/ppermute | solution.py:636
  188.2 23.5 %collective-permute-start.22 = (bf16[256,2048]{1,0:T(8,128)(2,1)S(1)}, bf16[256,2048]{1,0:T(8,128)(2,1)}, u32[]{:S(2)}, u32[]{:S(2)}) collective-permute-start(bf16[256,2048]{1,0:T(8,128)(2,1)S(1)} %add_convert_fusion.2.a_ref), channel_id=1, source_target_pairs={{0,3},{1,0},{2,1},{3,2},{4,7},{5,4},{6,5},{7,6},{8,11},{9,8},{10,9... | collective-permute-start | bytes 3145736 | tf_op jit(solution)/shard_map/ppermute | solution.py:636
  211.7 26.4 %collective-permute-start.23 = (bf16[256,2048]{1,0:T(8,128)(2,1)}, bf16[256,2048]{1,0:T(8,128)(2,1)}, u32[]{:S(2)}, u32[]{:S(2)}) collective-permute-start(bf16[256,2048]{1,0:T(8,128)(2,1)} %collective-permute-done.22.a_ref), channel_id=1, source_target_pairs={{0,3},{1,0},{2,1},{3,2},{4,7},{5,4},{6,5},{7,6},{8,11},{9,8},{10,9... | collective-permute-start | bytes 3145736 | tf_op jit(solution)/shard_map/ppermute | solution.py:636
  226.0 34.5 %collective-permute-start.25 = (bf16[256,2048]{1,0:T(8,128)(2,1)}, bf16[256,2048]{1,0:T(8,128)(2,1)S(1)}, u32[]{:S(2)}, u32[]{:S(2)}) collective-permute-start(bf16[256,2048]{1,0:T(8,128)(2,1)} %block_term.9), channel_id=1, source_target_pairs={{0,3},{1,0},{2,1},{3,2},{4,7},{5,4},{6,5},{7,6},{8,11},{9,8},{10,9... | collective-permute-start | bytes 3145736 | tf_op jit(solution)/shard_map/ppermute | solution.py:636
  238.1 44.8 %collective-permute-start.24 = (bf16[256,2048]{1,0:T(8,128)(2,1)}, bf16[256,2048]{1,0:T(8,128)(2,1)S(1)}, u32[]{:S(2)}, u32[]{:S(2)}) collective-permute-start(bf16[256,2048]{1,0:T(8,128)(2,1)} %collective-permute-done.23.a_ref), channel_id=1, source_target_pairs={{0,3},{1,0},{2,1},{3,2},{4,7},{5,4},{6,5},{7,6},{8,11},{9,8},{10,9... | collective-permute-start | bytes 3145736 | tf_op jit(solution)/shard_map/ppermute | solution.py:636
  260.8 38.4 %collective-permute-start.26 = (bf16[256,2048]{1,0:T(8,128)(2,1)S(1)}, bf16[256,2048]{1,0:T(8,128)(2,1)S(1)}, u32[]{:S(2)}, u32[]{:S(2)}) collective-permute-start(bf16[256,2048]{1,0:T(8,128)(2,1)S(1)} %add_convert_fusion.1), channel_id=1, source_target_pairs={{0,3},{1,0},{2,1},{3,2},{4,7},{5,4},{6,5},{7,6},{8,11},{9,8},{10,9... | collective-permute-start | bytes 3145736 | tf_op jit(solution)/shard_map/ppermute | solution.py:636
  302.4 18.7 %collective-permute-start.27 = (bf16[256,2048]{1,0:T(8,128)(2,1)S(1)}, bf16[256,2048]{1,0:T(8,128)(2,1)S(1)}, u32[]{:S(2)}, u32[]{:S(2)}) collective-permute-start(bf16[256,2048]{1,0:T(8,128)(2,1)S(1)} %block_term.11), channel_id=1, source_target_pairs={{0,3},{1,0},{2,1},{3,2},{4,7},{5,4},{6,5},{7,6},{8,11},{9,8},{10,9... | collective-permute-start | bytes 3145736 | tf_op jit(solution)/shard_map/ppermute | solution.py:636
  310.1 31.3 %collective-permute-start.29 = (bf16[2048,1024]{1,0:T(8,128)(2,1)}, bf16[2048,1024]{1,0:T(8,128)(2,1)}, u32[]{:S(2)}, u32[]{:S(2)}) collective-permute-start(bf16[2048,1024]{1,0:T(8,128)(2,1)} %grad_half.4), channel_id=1, source_target_pairs={{0,4},{4,0},{8,12},{12,8},{16,20},{20,16},{24,28},{28,24},{1,5},{5... | collective-permute-start | bytes 12582920 | tf_op jit(solution)/shard_map/ppermute | solution.py:657
  317.3 42.1 %collective-permute-start.32 = (bf16[2048,1024]{1,0:T(8,128)(2,1)}, bf16[2048,1024]{1,0:T(8,128)(2,1)}, u32[]{:S(2)}, u32[]{:S(2)}) collective-permute-start(bf16[2048,1024]{1,0:T(8,128)(2,1)} %grad_half.5), channel_id=1, source_target_pairs={{0,4},{4,0},{8,12},{12,8},{16,20},{20,16},{24,28},{28,24},{1,5},{5... | collective-permute-start | bytes 12582920 | tf_op jit(solution)/shard_map/ppermute | solution.py:657
  325.1 24.3 %collective-permute-start.28 = (bf16[256,2048]{1,0:T(8,128)(2,1)S(1)}, bf16[256,2048]{1,0:T(8,128)(2,1)S(1)}, u32[]{:S(2)}, u32[]{:S(2)}) collective-permute-start(bf16[256,2048]{1,0:T(8,128)(2,1)S(1)} %get-tuple-element.225.refs_0_), channel_id=1, source_target_pairs={{0,1},{1,2},{2,3},{4,5},{5,6},{6,7},{8,9},{9,10},{10,11},{12,13},{... | collective-permute-start | bytes 3145736 | tf_op jit(solution)/shard_map/ppermute | solution.py:636
  328.8 27.7 %collective-permute-start.31 = (bf16[256,2048]{1,0:T(8,128)(2,1)S(1)}, bf16[256,2048]{1,0:T(8,128)(2,1)S(1)}, u32[]{:S(2)}, u32[]{:S(2)}) collective-permute-start(bf16[256,2048]{1,0:T(8,128)(2,1)S(1)} %get-tuple-element.225.refs_0_), channel_id=1, source_target_pairs={{1,0},{2,1},{3,2},{5,4},{6,5},{7,6},{9,8},{10,9},{11,10},{13,12},{... | collective-permute-start | bytes 3145736 | tf_op jit(solution)/shard_map/ppermute | solution.py:636
  351.2 23.6 %collective-permute-start.30 = (bf16[256,2048]{1,0:T(8,128)(2,1)}, bf16[256,2048]{1,0:T(8,128)(2,1)}, u32[]{:S(2)}, u32[]{:S(2)}) collective-permute-start(bf16[256,2048]{1,0:T(8,128)(2,1)} %join.32), channel_id=1, source_target_pairs={{0,1},{1,2},{2,3},{4,5},{5,6},{6,7},{8,9},{9,10},{10,11},{12,13},{... | collective-permute-start | bytes 3145736 | tf_op jit(solution)/shard_map/ppermute | solution.py:636
  358.2 25.7 %collective-permute-start.35 = (bf16[256,2048]{1,0:T(8,128)(2,1)}, bf16[256,2048]{1,0:T(8,128)(2,1)}, u32[]{:S(2)}, u32[]{:S(2)}) collective-permute-start(bf16[256,2048]{1,0:T(8,128)(2,1)} %join.33), channel_id=1, source_target_pairs={{1,0},{2,1},{3,2},{5,4},{6,5},{7,6},{9,8},{10,9},{11,10},{13,12},{... | collective-permute-start | bytes 3145736 | tf_op jit(solution)/shard_map/ppermute | solution.py:636
  370.1 146.2 %reduce-scatter.5.cloned.1.call-start = ((), (), s32[]{:S(2)}) async-start(), calls=%async_computation.3 | async-start | bytes 5242880 | tf_op jit(solution)/shard_map/reduce_scatter | solution.py:785
  378.8 23.0 %collective-permute-start.33 = (bf16[256,2048]{1,0:T(8,128)(2,1)S(1)}, bf16[256,2048]{1,0:T(8,128)(2,1)S(1)}, u32[]{:S(2)}, u32[]{:S(2)}) collective-permute-start(bf16[256,2048]{1,0:T(8,128)(2,1)S(1)} %join.34), channel_id=1, source_target_pairs={{0,1},{1,2},{2,3},{4,5},{5,6},{6,7},{8,9},{9,10},{10,11},{12,13},{... | collective-permute-start | bytes 3145736 | tf_op jit(solution)/shard_map/ppermute | solution.py:636
  385.7 22.8 %collective-permute-start.36 = (bf16[256,2048]{1,0:T(8,128)(2,1)S(1)}, bf16[256,2048]{1,0:T(8,128)(2,1)S(1)}, u32[]{:S(2)}, u32[]{:S(2)}) collective-permute-start(bf16[256,2048]{1,0:T(8,128)(2,1)S(1)} %join.36), channel_id=1, source_target_pairs={{1,0},{2,1},{3,2},{5,4},{6,5},{7,6},{9,8},{10,9},{11,10},{13,12},{... | collective-permute-start | bytes 3145736 | tf_op jit(solution)/shard_map/ppermute | solution.py:636
  402.7 28.5 %collective-permute-start.34 = (bf16[256,2048]{1,0:T(8,128)(2,1)S(1)}, bf16[256,2048]{1,0:T(8,128)(2,1)S(1)}, u32[]{:S(2)}, u32[]{:S(2)}) collective-permute-start(bf16[256,2048]{1,0:T(8,128)(2,1)S(1)} %join.35), channel_id=1, source_target_pairs={{0,1},{1,2},{2,3},{4,5},{5,6},{6,7},{8,9},{9,10},{10,11},{12,13},{... | collective-permute-start | bytes 3145736 | tf_op jit(solution)/shard_map/ppermute | solution.py:636
  409.2 22.3 %collective-permute-start.37 = (bf16[256,2048]{1,0:T(8,128)(2,1)S(1)}, bf16[256,2048]{1,0:T(8,128)(2,1)S(1)}, u32[]{:S(2)}, u32[]{:S(2)}) collective-permute-start(bf16[256,2048]{1,0:T(8,128)(2,1)S(1)} %join.37), channel_id=1, source_target_pairs={{1,0},{2,1},{3,2},{5,4},{6,5},{7,6},{9,8},{10,9},{11,10},{13,12},{... | collective-permute-start | bytes 3145736 | tf_op jit(solution)/shard_map/ppermute | solution.py:636
  440.4 27.3 %collective-permute-start.38 = (bf16[256,2048]{1,0:T(8,128)(2,1)}, bf16[256,2048]{1,0:T(8,128)(2,1)}, u32[]{:S(2)}, u32[]{:S(2)}) collective-permute-start(bf16[256,2048]{1,0:T(8,128)(2,1)} %block_term.12), channel_id=1, source_target_pairs={{0,3},{1,0},{2,1},{3,2},{4,7},{5,4},{6,5},{7,6},{8,11},{9,8},{10,9... | collective-permute-start | bytes 3145736 | tf_op jit(solution)/shard_map/ppermute | solution.py:636
  471.9 28.3 %collective-permute-start.40 = (bf16[256,2048]{1,0:T(8,128)(2,1)}, bf16[256,2048]{1,0:T(8,128)(2,1)}, u32[]{:S(2)}, u32[]{:S(2)}) collective-permute-start(bf16[256,2048]{1,0:T(8,128)(2,1)} %join.38), channel_id=1, source_target_pairs={{0,3},{1,0},{2,1},{3,2},{4,7},{5,4},{6,5},{7,6},{8,11},{9,8},{10,9... | collective-permute-start | bytes 3145736 | tf_op jit(solution)/shard_map/ppermute | solution.py:636
  489.9 17.5 %collective-permute-start.45 = (f32[8320]{0:T(1024)S(1)}, f32[8320]{0:T(1024)S(1)}, u32[]{:S(2)}, u32[]{:S(2)}) collective-permute-start(f32[8320]{0:T(1024)S(1)} %add.128), channel_id=1, source_target_pairs={{0,1},{1,2},{2,3},{3,0},{4,5},{5,6},{6,7},{7,4},{8,9},{9,10},{10,1... | collective-permute-start | bytes 99848 | tf_op jit(solution)/shard_map/ppermute | solution.py:636
  489.9 17.5 %collective-permute-start.46 = (f32[8320]{0:T(1024)S(1)}, f32[8320]{0:T(1024)S(1)}, u32[]{:S(2)}, u32[]{:S(2)}) collective-permute-start(f32[8320]{0:T(1024)S(1)} %add.128), channel_id=1, source_target_pairs={{0,2},{1,3},{2,0},{3,1},{4,6},{5,7},{6,4},{7,5},{8,10},{9,11},{10,... | collective-permute-start | bytes 99848 | tf_op jit(solution)/shard_map/ppermute | solution.py:636
  490.5 16.9 %collective-permute-start.47 = (f32[8320]{0:T(1024)S(1)}, f32[8320]{0:T(1024)S(1)}, u32[]{:S(2)}, u32[]{:S(2)}) collective-permute-start(f32[8320]{0:T(1024)S(1)} %add.128), channel_id=1, source_target_pairs={{0,3},{1,0},{2,1},{3,2},{4,7},{5,4},{6,5},{7,6},{8,11},{9,8},{10,9... | collective-permute-start | bytes 99848 | tf_op jit(solution)/shard_map/ppermute | solution.py:636
  494.8 22.6 %collective-permute-start.42 = (bf16[2,256,1024]{2,1,0:T(8,128)(2,1)}, bf16[2,256,1024]{2,1,0:T(8,128)(2,1)}, u32[]{:S(2)}, u32[]{:S(2)}) collective-permute-start(bf16[2,256,1024]{2,1,0:T(8,128)(2,1)} %constant_dynamic-slice_fusion), channel_id=1, source_target_pairs={{0,4},{4,0},{8,12},{12,8},{16,20},{20,16},{24,28},{28,24},{1,5},{5... | collective-permute-start | bytes 3145736 | tf_op jit(solution)/shard_map/ppermute | solution.py:657
  503.0 26.0 %collective-permute-start.41 = (bf16[256,2048]{1,0:T(8,128)(2,1)}, bf16[256,2048]{1,0:T(8,128)(2,1)S(1)}, u32[]{:S(2)}, u32[]{:S(2)}) collective-permute-start(bf16[256,2048]{1,0:T(8,128)(2,1)} %join.39), channel_id=1, source_target_pairs={{0,3},{1,0},{2,1},{3,2},{4,7},{5,4},{6,5},{7,6},{8,11},{9,8},{10,9... | collective-permute-start | bytes 3145736 | tf_op jit(solution)/shard_map/ppermute | solution.py:636
  507.4 24.5 %collective-permute-start.48 = (f32[8320]{0:T(1024)S(1)}, f32[8320]{0:T(1024)S(1)}, u32[]{:S(2)}, u32[]{:S(2)}) collective-permute-start(f32[8320]{0:T(1024)S(1)} %add_add_fusion.2), channel_id=1, source_target_pairs={{0,8},{4,12},{8,16},{12,20},{16,24},{20,28},{24,0},{28,4},{1,9},{5... | collective-permute-start | bytes 99848 | tf_op jit(solution)/shard_map/ppermute | solution.py:827
  508.9 23.1 %collective-permute-start.49 = (f32[8320]{0:T(1024)S(1)}, f32[8320]{0:T(1024)S(1)}, u32[]{:S(2)}, u32[]{:S(2)}) collective-permute-start(f32[8320]{0:T(1024)S(1)} %add_add_fusion.2), channel_id=1, source_target_pairs={{0,16},{4,20},{8,24},{12,28},{16,0},{20,4},{24,8},{28,12},{1,17},{... | collective-permute-start | bytes 99848 | tf_op jit(solution)/shard_map/ppermute | solution.py:827
  510.0 21.9 %collective-permute-start.50 = (f32[8320]{0:T(1024)S(1)}, f32[8320]{0:T(1024)S(1)}, u32[]{:S(2)}, u32[]{:S(2)}) collective-permute-start(f32[8320]{0:T(1024)S(1)} %add_add_fusion.2), channel_id=1, source_target_pairs={{0,24},{4,28},{8,0},{12,4},{16,8},{20,12},{24,16},{28,20},{1,25},{... | collective-permute-start | bytes 99848 | tf_op jit(solution)/shard_map/ppermute | solution.py:827
  (96 other events, 817.9 us)
Sparse Core Ops, SparseCore 0:
  370.2 86.7 reduce-scatter.2
  460.6 55.6 reduce-scatter.4

commit v12 on v11

--- a/solution.py
+++ b/solution.py
@@ -817,7 +817,10 @@
         ]
     )
     small = sum_over(small, "dp", [[(i, i ^ 1) for i in range(n_dp)]])
+    wide = whole(wide_grad, [hidden] * 2)
     for s in range(3, n):
+        if s == 3:
+            moved, *wide = tie([moved, *wide])
         sent = join(where, moved, terms[s][None], 0, n + 1, True, 0, 64e9)
         moved = hop(sent)
 
@@ -827,10 +830,8 @@
         lax.ppermute(small, "dp", [(i, (i + 2 * m) % n_dp) for i in range(n_dp)])
         for m in range(1, n_dp // 2)
     ]
-    wide = whole(wide_grad, [hidden] * 2)
     weight_grads = whole(attn_grad[None], [local] * 4)
-    moved, *outs = tie([moved, *wide, *weight_grads])
-    wide, weight_grads = outs[:2], outs[2:]
+    moved, *weight_grads = tie([moved, *weight_grads])
     input_grad = last_step(own, gain1, terms[0], moved, grad_state)
     small = small + sum(tie(others, input_grad))
 

time: 550 us -> 549 us (level)
    unnamed x185 -> x173, local copies, waits for them, and re-layouts: 25 us -> 23.6 us
  transfers between devices with their start and end apart: 53 -> 53, of which waited for: 25 -> 27; matrix products, arithmetic and copies ran while one was open for 7% -> 7% of each run, Pallas kernels for 38% -> 38%
where the time goes in v12:
time: 549 us; the launch traced here: 539 us
  Pallas kernels  207 us (38%)
  waiting for transfers between devices  131 us (24%)
  starting transfers between devices  119 us (22%)
  local copies, waits for them, and re-layouts  30.5 us (6%)
  other arithmetic  20.5 us (4%)
  between operations  15.9 us (3%)
  matrix products  15.6 us (3%)
    ppermute x42, waiting for transfers between devices, per_device(): send = lambda v, pairs: lax.ppermute(v, 'mp', pairs)  124 us
    ppermute x42, starting transfers between devices, per_device(): send = lambda v, pairs: lax.ppermute(v, 'mp', pairs)  113 us
    pallas_call x4, Pallas kernels, mlp_slot(): pl.pallas_call(functools.partial(mlp_body, slot, n), grid_spec=pltpu.Pref...  39.3 us
    pallas_call x4, Pallas kernels, grad_half(): pl.pallas_call(functools.partial(grad_body, not partner), grid_spec=pltpu...  29.6 us
    pallas_call x4, Pallas kernels, qkv_slot(): pl.pallas_call(qkv_body, grid_spec=pltpu.PrefetchScalarGridSpec(num_scala...  28.7 us
    pallas_call x20, Pallas kernels, join(): pl.pallas_call(functools.partial(join_body, 0 if right else -1, first), g...  26.4 us
    pallas_call x8, Pallas kernels, block_term(): pl.pallas_call(term_body, grid=(d // tile,), in_specs=[pl.BlockSpec((1, r...  23.8 us
    unnamed x173, local copies, waits for them, and re-layouts  23.6 us
  transfers between devices with their start and end apart: 53, of which 27 were waited for; matrix products, arithmetic and copies ran while one was open for 7% of the time, Pallas kernels for 38%

profile of v12, /device:TPU:0, one launch (start us, length us, event | category | flops | bytes accessed | tf_op | source)
XLA Modules:
  0.0 539.4 jit_solution(1945933033983695808)
XLA Ops:
  8.5 5.1 collective-permute-start
  17.9 7.1 %qkv_slot.4 = (bf16[4,256,2048]{2,1,0:T(8,128)(2,1)}, bf16[4,256,512]{2,1,0:T(8,128)(2,1)}, bf16[4,256,512]{2,1,0:T(8,128)(2,1)}, bf16[4,256,512]{2,1,0:T(8,128)(2,1)}) custom-call(s32[4]{0:T(128)} %pad_add_fusion.rank_ref, bf16[256,1024]{1,0:T(8,128)(2,1)} %copy-done.61, bf16[256,1024]{1,0:T(8,128)(2,1)} %copy-done.60, f32[1,2048]{1,0:T(1,128)} %bitcast.105, ...), custom_call_target="tpu_custom_call" | custom-call | flops 1610612736 | bytes 8388608 | tf_op jit(solution)/shard_map/qkv_slot/pallas_call | solution.py:106
  26.0 4.4 collective-permute-start.1
  30.3 6.8 %collective-permute-done.2.xb_ref = bf16[256,1024]{1,0:T(8,128)(2,1)S(1)} collective-permute-done((bf16[256,1024]{1,0:T(8,128)(2,1)S(1)}, bf16[256,1024]{1,0:T(8,128)(2,1)S(1)}, u32[]{:S(2)}, u32[]{:S(2)}) %collective-permute-start.2) | collective-permute-done | bytes 524320 | tf_op jit(solution)/shard_map/ppermute | solution.py:636
  37.2 4.3 collective-permute-start.4
  41.5 7.1 %qkv_slot.5 = (bf16[4,256,2048]{2,1,0:T(8,128)(2,1)}, bf16[4,256,512]{2,1,0:T(8,128)(2,1)}, bf16[4,256,512]{2,1,0:T(8,128)(2,1)}, bf16[4,256,512]{2,1,0:T(8,128)(2,1)}) custom-call(s32[4]{0:T(128)} %pad_add_fusion.rank_ref, ...), custom_call_target="tpu_custom_call", output_to_operand_aliasing={{0}: (10, {}), {1}: (11, {}), {2}: (12, {}), {3}: (13, {})} | custom-call | flops 1610612736 | bytes 8388608 | tf_op jit(solution)/shard_map/qkv_slot/pallas_call | solution.py:106
  52.7 7.0 %collective-permute-done.4.xb_ref = bf16[256,1024]{1,0:T(8,128)(2,1)S(1)} collective-permute-done((bf16[256,1024]{1,0:T(8,128)(2,1)S(1)}, bf16[256,1024]{1,0:T(8,128)(2,1)S(1)}, u32[]{:S(2)}, u32[]{:S(2)}) %collective-permute-start.4) | collective-permute-done | bytes 524320 | tf_op jit(solution)/shard_map/ppermute | solution.py:636
  59.7 4.3 collective-permute-start.5
  68.1 7.3 %qkv_slot.6 = (bf16[4,256,2048]{2,1,0:T(8,128)(2,1)}, bf16[4,256,512]{2,1,0:T(8,128)(2,1)}, bf16[4,256,512]{2,1,0:T(8,128)(2,1)}, bf16[4,256,512]{2,1,0:T(8,128)(2,1)}) custom-call(s32[4]{0:T(128)} %pad_add_fusion.rank_ref, bf16[256,1024]{1,0:T(8,128)(2,1)} %copy-done.67, ...), custom_call_target="tpu_custom_call", output_to_operand_aliasing={{0}: (10, {}), {1}: (11, {}), {2}: (12, {}), {3}: (13, {})} | custom-call | flops 1610612736 | bytes 8388608 | tf_op jit(solution)/shard_map/qkv_slot/pallas_call | solution.py:106
  78.1 5.4 collective-permute-start.10
  85.0 7.2 %qkv_slot.7 = (bf16[4,256,2048]{2,1,0:T(8,128)(2,1)}, bf16[4,256,512]{2,1,0:T(8,128)(2,1)}, bf16[4,256,512]{2,1,0:T(8,128)(2,1)}, bf16[4,256,512]{2,1,0:T(8,128)(2,1)}) custom-call(s32[4]{0:T(128)} %pad_add_fusion.rank_ref, bf16[256,1024]{1,0:T(8,128)(2,1)} %copy-done.66, ...), custom_call_target="tpu_custom_call", output_to_operand_aliasing={{0}: (10, {}), {1}: (11, {}), {2}: (12, {}), {3}: (13, {})} | custom-call | flops 1610612736 | bytes 8388608 | tf_op jit(solution)/shard_map/qkv_slot/pallas_call | solution.py:106
  92.2 10.2 %attend.1 = bf16[4,256,512]{2,1,0:T(8,128)(2,1)} custom-call(s32[4]{0:T(128)} %pad_add_fusion.rank_ref, bf16[4,256,512]{2,1,0:T(8,128)(2,1)} %get-tuple-element.184.q_ref, bf16[4,256,512]{2,1,0:T(8,128)(2,1)} %get-tuple-element.185.k_ref, bf16[4,256,512]{2,1,0:T(8,128)(2,1)} %get-tuple-element.186.v_ref, s32[4,256,1]{2,1,0:T(8,128)} %reshape.204.dcol_ref, ...), custom_call_target="tpu_custom_call" | custom-call | flops 2147483648 | bytes 4194304 | tf_op jit(solution)/shard_map/attend/pallas_call | solution.py:169
  102.4 4.3 convolution_convert_fusion.1
  107.5 4.6 collective-permute-start.7
  125.2 4.4 collective-permute-start.8
  129.7 6.0 %collective-permute-done.11.moved_ref.grb_ref = bf16[256,1024]{1,0:T(8,128)(2,1)S(1)} collective-permute-done((bf16[256,1024]{1,0:T(8,128)(2,1)S(1)}, bf16[256,1024]{1,0:T(8,128)(2,1)S(1)}, u32[]{:S(2)}, u32[]{:S(2)}) %collective-permute-start.11) | collective-permute-done | bytes 524320 | tf_op jit(solution)/shard_map/ppermute | solution.py:636
  136.5 4.4 collective-permute-start.12
  147.8 5.3 collective-permute-start.9
  153.1 5.1 collective-permute-done.12.moved_ref.grb_ref
  158.9 4.4 collective-permute-start.13
  180.5 5.6 %collective-permute-done.21 = bf16[256,1024]{1,0:T(8,128)(2,1)S(1)} collective-permute-done((bf16[256,1024]{1,0:T(8,128)(2,1)S(1)}, bf16[256,1024]{1,0:T(8,128)(2,1)S(1)}, u32[]{:S(2)}, u32[]{:S(2)}) %collective-permute-start.21) | collective-permute-done | bytes 524320 | tf_op jit(solution)/shard_map/ppermute | solution.py:636
  190.5 9.3 %mlp_slot.4 = (bf16[4,256,2048]{2,1,0:T(8,128)(2,1)S(1)}, bf16[4,256,2048]{2,1,0:T(8,128)(2,1)S(1)}, bf16[4,256,2048]{2,1,0:T(8,128)(2,1)S(1)}, bf16[4,256,2048]{2,1,0:T(8,128)(2,1)S(1)}) custom-call(s32[4]{0:T(128)S(1)} %copy-done.45, bf16[256,2048]{1,0:T(8,128)(2,1)S(1)} %add_convert_fusion.2.a_ref, ...), custom_call_target="tpu_custom_call" | custom-call | flops 4294967296 | bytes 20971520 | tf_op jit(solution)/shard_map/mlp_slot/pallas_call | solution.py:303
  207.2 4.5 collective-permute-done.22.a_ref
  211.7 10.2 %mlp_slot.5 = (bf16[4,256,2048]{2,1,0:T(8,128)(2,1)S(1)}, bf16[4,256,2048]{2,1,0:T(8,128)(2,1)S(1)}, bf16[4,256,2048]{2,1,0:T(8,128)(2,1)S(1)}, bf16[4,256,2048]{2,1,0:T(8,128)(2,1)S(1)}) custom-call(s32[4]{0:T(128)S(1)} %copy-done.45, ...), custom_call_target="tpu_custom_call", output_to_operand_aliasing={{0}: (9, {}), {1}: (10, {}), {2}: (11, {}), {3}: (12, {})} | custom-call | flops 4294967296 | bytes 20971520 | tf_op jit(solution)/shard_map/mlp_slot/pallas_call | solution.py:303
  228.1 10.0 %collective-permute-done.23.a_ref = bf16[256,2048]{1,0:T(8,128)(2,1)} collective-permute-done((bf16[256,2048]{1,0:T(8,128)(2,1)}, bf16[256,2048]{1,0:T(8,128)(2,1)}, u32[]{:S(2)}, u32[]{:S(2)}) %collective-permute-start.23) | collective-permute-done | bytes 1048608 | tf_op jit(solution)/shard_map/ppermute | solution.py:636
  240.0 9.6 %mlp_slot.6 = (bf16[4,256,2048]{2,1,0:T(8,128)(2,1)S(1)}, bf16[4,256,2048]{2,1,0:T(8,128)(2,1)S(1)}, bf16[4,256,2048]{2,1,0:T(8,128)(2,1)S(1)}, bf16[4,256,2048]{2,1,0:T(8,128)(2,1)S(1)}) custom-call(s32[4]{0:T(128)S(1)} %copy-done.45, ...), custom_call_target="tpu_custom_call", output_to_operand_aliasing={{0}: (9, {}), {1}: (10, {}), {2}: (11, {}), {3}: (12, {})} | custom-call | flops 4294967296 | bytes 20971520 | tf_op jit(solution)/shard_map/mlp_slot/pallas_call | solution.py:303
  252.7 7.8 %collective-permute-done.25 = bf16[256,2048]{1,0:T(8,128)(2,1)S(1)} collective-permute-done((bf16[256,2048]{1,0:T(8,128)(2,1)}, bf16[256,2048]{1,0:T(8,128)(2,1)S(1)}, u32[]{:S(2)}, u32[]{:S(2)}) %collective-permute-start.25) | collective-permute-done | bytes 1048608 | tf_op jit(solution)/shard_map/ppermute | solution.py:636
  262.8 20.2 %collective-permute-done.24.a_ref = bf16[256,2048]{1,0:T(8,128)(2,1)S(1)} collective-permute-done((bf16[256,2048]{1,0:T(8,128)(2,1)}, bf16[256,2048]{1,0:T(8,128)(2,1)S(1)}, u32[]{:S(2)}, u32[]{:S(2)}) %collective-permute-start.24) | collective-permute-done | bytes 1048608 | tf_op jit(solution)/shard_map/ppermute | solution.py:636
  282.9 10.2 %mlp_slot.7 = (bf16[4,256,2048]{2,1,0:T(8,128)(2,1)S(1)}, bf16[4,256,2048]{2,1,0:T(8,128)(2,1)S(1)}, bf16[4,256,2048]{2,1,0:T(8,128)(2,1)S(1)}, bf16[4,256,2048]{2,1,0:T(8,128)(2,1)S(1)}) custom-call(s32[4]{0:T(128)S(1)} %copy-done.45, ...), custom_call_target="tpu_custom_call", output_to_operand_aliasing={{0}: (9, {}), {1}: (10, {}), {2}: (11, {}), {3}: (12, {})} | custom-call | flops 4294967296 | bytes 20971520 | tf_op jit(solution)/shard_map/mlp_slot/pallas_call | solution.py:303
  293.1 6.1 %collective-permute-done.26.rest_0_ = bf16[256,2048]{1,0:T(8,128)(2,1)S(1)} collective-permute-done((bf16[256,2048]{1,0:T(8,128)(2,1)S(1)}, bf16[256,2048]{1,0:T(8,128)(2,1)S(1)}, u32[]{:S(2)}, u32[]{:S(2)}) %collective-permute-start.26) | collective-permute-done | bytes 1048608 | tf_op jit(solution)/shard_map/ppermute | solution.py:636
  302.9 7.2 %grad_half.4 = bf16[2048,1024]{1,0:T(8,128)(2,1)} custom-call(s32[4]{0:T(128)S(1)} %copy-done.45, bf16[1024,2048]{1,0:T(8,128)(2,1)S(1)} %bitcast.93, bf16[1024,2048]{1,0:T(8,128)(2,1)S(1)} %bitcast.88), custom_call_target="tpu_custom_call" | custom-call | flops 1000000 | bytes 1000000 | tf_op jit(solution)/shard_map/grad_half/pallas_call | solution.py:413
  310.1 7.2 %grad_half.5 = bf16[2048,1024]{1,0:T(8,128)(2,1)} custom-call(s32[4]{0:T(128)S(1)} %copy-done.45, bf16[1024,2048]{1,0:T(8,128)(2,1)S(1)} %bitcast.91, bf16[1024,2048]{1,0:T(8,128)(2,1)S(1)} %bitcast.72), custom_call_target="tpu_custom_call" | custom-call | flops 1000000 | bytes 1000000 | tf_op jit(solution)/shard_map/grad_half/pallas_call | solution.py:413
  330.2 11.3 %convolution_convert_fusion = bf16[1024,2048]{1,0:T(8,128)(2,1)S(1)} fusion(bf16[1024,2048]{1,0:T(8,128)(2,1)S(1)} %bitcast.89, bf16[2048,2048]{1,0:T(8,128)(2,1)} %down_ref.7), kind=kOutput, calls=%fused_computation | convolution fusion | flops 8592031744 | bytes 16777216 | tf_op jit(solution)/shard_map/dot_general | solution.py:53
  341.5 8.0 %grad_half.6.rest_1_ = bf16[2,2048,1024]{2,1,0:T(8,128)(2,1)S(1)} custom-call(s32[4]{0:T(128)S(1)} %copy-done.45, bf16[1024,2048]{1,0:T(8,128)(2,1)S(1)} %bitcast.94, bf16[1024,2048]{1,0:T(8,128)(2,1)S(1)} %bitcast.90, bf16[2048,1024]{1,0:T(8,128)(2,1)} %collective-permute-done.29.rest_0_), custom_call_target="tpu_custom_call" | custom-call | flops 1000000 | bytes 1000000 | tf_op jit(solution)/shard_map/grad_half/pallas_call | solution.py:413
  351.2 5.4 %collective-permute-start.30 = (bf16[256,2048]{1,0:T(8,128)(2,1)}, bf16[256,2048]{1,0:T(8,128)(2,1)}, u32[]{:S(2)}, u32[]{:S(2)}) collective-permute-start(bf16[256,2048]{1,0:T(8,128)(2,1)} %join.32), channel_id=1, source_target_pairs={{0,1},{1,2},{2,3},{4,5},{5,6},{6,7},{8,9},{9,10},{10,11},{12,13},{... | collective-permute-start | bytes 3145736 | tf_op jit(solution)/shard_map/ppermute | solution.py:636
  359.6 7.2 %grad_half.7 = bf16[2,2048,1024]{2,1,0:T(8,128)(2,1)S(1)} custom-call(s32[4]{0:T(128)S(1)} %copy-done.45, bf16[1024,2048]{1,0:T(8,128)(2,1)S(1)} %bitcast.92, bf16[1024,2048]{1,0:T(8,128)(2,1)S(1)} %bitcast.73, bf16[2048,1024]{1,0:T(8,128)(2,1)} %collective-permute-done.32.rest_0_, ...), custom_call_target="tpu_custom_call", output_to_operand_aliasing={{}: (4, {})} | custom-call | flops 1000000 | bytes 1000000 | tf_op jit(solution)/shard_map/grad_half/pallas_call | solution.py:413
  370.2 4.5 collective-permute-done.30.moved_ref.refs_2_
  378.8 5.0 collective-permute-start.33
  391.4 10.5 %collective-permute-done.33.moved_ref.refs_1_ = bf16[256,2048]{1,0:T(8,128)(2,1)S(1)} collective-permute-done((bf16[256,2048]{1,0:T(8,128)(2,1)S(1)}, bf16[256,2048]{1,0:T(8,128)(2,1)S(1)}, u32[]{:S(2)}, u32[]{:S(2)}) %collective-permute-start.33) | collective-permute-done | bytes 1048608 | tf_op jit(solution)/shard_map/ppermute | solution.py:636
  402.7 4.5 collective-permute-start.34
  413.3 14.4 %attend_back.1.x_ref = bf16[4,256,1536]{2,1,0:T(8,128)(2,1)S(1)} custom-call(s32[4]{0:T(128)S(1)} %copy-done.45, bf16[4,256,512]{2,1,0:T(8,128)(2,1)S(1)} %copy-done.18, bf16[4,256,512]{2,1,0:T(8,128)(2,1)S(1)} %copy-done.19, bf16[4,256,512]{2,1,0:T(8,128)(2,1)S(1)} %copy-done.20, bf16[4,256,512]{2,1,0:T(8,128)(2,1)S(1)} %get-tuple-element.236.do_ref, ...), custom_call_target="tpu_custom_call" | custom-call | flops 115999997952 | bytes 7340032 | tf_op jit(solution)/shard_map/attend_back/pallas_call | solution.py:251
  433.0 7.4 %attn_grads.2 = bf16[2048,1024]{1,0:T(8,128)(2,1)S(1)} custom-call(s32[4]{0:T(128)S(1)} %copy-done.45, bf16[1024,2048]{1,0:T(8,128)(2,1)S(1)} %bitcast.85, bf16[1024,2048]{1,0:T(8,128)(2,1)S(1)} %bitcast.95, bf16[1024,1536]{1,0:T(8,128)(2,1)S(1)} %bitcast.74, bf16[1024,1536]{1,0:T(8,128)(2,1)S(1)} %bitcast.75, bf16[1024,512]{1,0:T(8,128)(2,1)S(1)} %bitcast.102), custom_call_target="tpu_custom_call" | custom-call | flops 4000000000 | bytes 1000000 | tf_op jit(solution)/shard_map/attn_grads/pallas_call | solution.py:456
  449.5 10.7 %attn_grads.3 = bf16[2048,1024]{1,0:T(8,128)(2,1)} custom-call(s32[4]{0:T(128)S(1)} %copy-done.45, bf16[1024,2048]{1,0:T(8,128)(2,1)} %bitcast.84, bf16[1024,2048]{1,0:T(8,128)(2,1)} %bitcast.96, bf16[1024,1536]{1,0:T(8,128)(2,1)} %bitcast.76, bf16[1024,1536]{1,0:T(8,128)(2,1)} %bitcast.77, bf16[1024,512]{1,0:T(8,128)(2,1)S(1)} %bitcast.103, ...), custom_call_target="tpu_custom_call" | custom-call | flops 1000000 | bytes 1000000 | tf_op jit(solution)/shard_map/attn_grads/pallas_call | solution.py:456
  461.1 6.6 %collective-permute-done.38.moved_ref = bf16[256,2048]{1,0:T(8,128)(2,1)} collective-permute-done((bf16[256,2048]{1,0:T(8,128)(2,1)}, bf16[256,2048]{1,0:T(8,128)(2,1)}, u32[]{:S(2)}, u32[]{:S(2)}) %collective-permute-start.38) | collective-permute-done | bytes 1048608 | tf_op jit(solution)/shard_map/ppermute | solution.py:636
  494.6 4.6 whole_rows.2
  502.1 4.3 collective-permute-start.42
  510.9 5.5 %reduce-scatter.5.cloned.1.call-done = bf16[512,1024]{1,0:T(8,128)(2,1)} async-done(((bf16[2048,1024]{1,0:T(8,128)(2,1)}), bf16[512,1024]{1,0:T(8,128)(2,1)}) %reduce-scatter.5.cloned.1.call-update) | async-done | bytes 1048592 | tf_op jit(solution)/shard_map/reduce_scatter | solution.py:785
  517.6 4.3 fusion.7
  (331 shorter events, 186.8 us)
Async XLA Ops:
  7.2 453.0 %reduce-scatter.3.cloned.1.call-start = ((), (), s32[]{:S(2)}) async-start(), calls=%async_computation.2 | async-start | bytes 10485760 | tf_op jit(solution)/shard_map/reduce_scatter | solution.py:757
  8.5 17.4 %collective-permute-start = (bf16[256,1024]{1,0:T(8,128)(2,1)S(1)}, bf16[256,1024]{1,0:T(8,128)(2,1)}, u32[]{:S(2)}, u32[]{:S(2)}) collective-permute-start(bf16[256,1024]{1,0:T(8,128)(2,1)S(1)} %get-tuple-element.291.xa_ref), channel_id=1, source_target_pairs={{0,3},{1,0},{2,1},{3,2},{4,7},{5,4},{6,5},{7,6},{8,11},{9,8},{10,9... | collective-permute-start | bytes 1572872 | tf_op jit(solution)/shard_map/ppermute | solution.py:636
  13.6 23.6 %collective-permute-start.2 = (bf16[256,1024]{1,0:T(8,128)(2,1)S(1)}, bf16[256,1024]{1,0:T(8,128)(2,1)S(1)}, u32[]{:S(2)}, u32[]{:S(2)}) collective-permute-start(bf16[256,1024]{1,0:T(8,128)(2,1)S(1)} %get-tuple-element.290.xb_ref), channel_id=1, source_target_pairs={{0,3},{1,0},{2,1},{3,2},{4,7},{5,4},{6,5},{7,6},{8,11},{9,8},{10,9... | collective-permute-start | bytes 1572872 | tf_op jit(solution)/shard_map/ppermute | solution.py:636
  26.0 22.7 %collective-permute-start.1 = (bf16[256,1024]{1,0:T(8,128)(2,1)}, bf16[256,1024]{1,0:T(8,128)(2,1)S(1)}, u32[]{:S(2)}, u32[]{:S(2)}) collective-permute-start(bf16[256,1024]{1,0:T(8,128)(2,1)} %collective-permute-done.xa_ref), channel_id=1, source_target_pairs={{0,3},{1,0},{2,1},{3,2},{4,7},{5,4},{6,5},{7,6},{8,11},{9,8},{10,9... | collective-permute-start | bytes 1572872 | tf_op jit(solution)/shard_map/ppermute | solution.py:636
  37.2 22.5 %collective-permute-start.4 = (bf16[256,1024]{1,0:T(8,128)(2,1)S(1)}, bf16[256,1024]{1,0:T(8,128)(2,1)S(1)}, u32[]{:S(2)}, u32[]{:S(2)}) collective-permute-start(bf16[256,1024]{1,0:T(8,128)(2,1)S(1)} %collective-permute-done.2.xb_ref), channel_id=1, source_target_pairs={{0,3},{1,0},{2,1},{3,2},{4,7},{5,4},{6,5},{7,6},{8,11},{9,8},{10,9... | collective-permute-start | bytes 1572872 | tf_op jit(solution)/shard_map/ppermute | solution.py:636
  48.6 26.8 %collective-permute-start.3 = (bf16[256,1024]{1,0:T(8,128)(2,1)S(1)}, bf16[256,1024]{1,0:T(8,128)(2,1)S(1)}, u32[]{:S(2)}, u32[]{:S(2)}) collective-permute-start(bf16[256,1024]{1,0:T(8,128)(2,1)S(1)} %collective-permute-done.1.xa_ref), channel_id=1, source_target_pairs={{0,3},{1,0},{2,1},{3,2},{4,7},{5,4},{6,5},{7,6},{8,11},{9,8},{10,9... | collective-permute-start | bytes 1572872 | tf_op jit(solution)/shard_map/ppermute | solution.py:636
  59.7 25.3 %collective-permute-start.5 = (bf16[256,1024]{1,0:T(8,128)(2,1)S(1)}, bf16[256,1024]{1,0:T(8,128)(2,1)}, u32[]{:S(2)}, u32[]{:S(2)}) collective-permute-start(bf16[256,1024]{1,0:T(8,128)(2,1)S(1)} %collective-permute-done.4.xb_ref), channel_id=1, source_target_pairs={{0,3},{1,0},{2,1},{3,2},{4,7},{5,4},{6,5},{7,6},{8,11},{9,8},{10,9... | collective-permute-start | bytes 1572872 | tf_op jit(solution)/shard_map/ppermute | solution.py:636
  75.5 31.2 %collective-permute-start.6 = (bf16[256,1024]{1,0:T(8,128)(2,1)S(1)}, bf16[256,1024]{1,0:T(8,128)(2,1)S(1)}, u32[]{:S(2)}, u32[]{:S(2)}) collective-permute-start(bf16[256,1024]{1,0:T(8,128)(2,1)S(1)} %get-tuple-element.288.gla_ref.gra_ref), channel_id=1, source_target_pairs={{0,1},{1,2},{2,3},{4,5},{5,6},{6,7},{8,9},{9,10},{10,11},{12,13},{... | collective-permute-start | bytes 1572872 | tf_op jit(solution)/shard_map/ppermute | solution.py:636
  76.8 38.9 %collective-permute-start.14 = (bf16[256,1024]{1,0:T(8,128)(2,1)S(1)}, bf16[256,1024]{1,0:T(8,128)(2,1)}, u32[]{:S(2)}, u32[]{:S(2)}) collective-permute-start(bf16[256,1024]{1,0:T(8,128)(2,1)S(1)} %get-tuple-element.288.gla_ref.gra_ref), channel_id=1, source_target_pairs={{1,0},{2,1},{3,2},{5,4},{6,5},{7,6},{9,8},{10,9},{11,10},{13,12},{... | collective-permute-start | bytes 1572872 | tf_op jit(solution)/shard_map/ppermute | solution.py:636
  78.1 34.0 %collective-permute-start.10 = (bf16[256,1024]{1,0:T(8,128)(2,1)S(1)}, bf16[256,1024]{1,0:T(8,128)(2,1)}, u32[]{:S(2)}, u32[]{:S(2)}) collective-permute-start(bf16[256,1024]{1,0:T(8,128)(2,1)S(1)} %get-tuple-element.289.glb_ref.grb_ref), channel_id=1, source_target_pairs={{0,1},{1,2},{2,3},{4,5},{5,6},{6,7},{8,9},{9,10},{10,11},{12,13},{... | collective-permute-start | bytes 1572872 | tf_op jit(solution)/shard_map/ppermute | solution.py:636
  83.5 35.1 %collective-permute-start.18 = (bf16[256,1024]{1,0:T(8,128)(2,1)S(1)}, bf16[256,1024]{1,0:T(8,128)(2,1)}, u32[]{:S(2)}, u32[]{:S(2)}) collective-permute-start(bf16[256,1024]{1,0:T(8,128)(2,1)S(1)} %get-tuple-element.289.glb_ref.grb_ref), channel_id=1, source_target_pairs={{1,0},{2,1},{3,2},{5,4},{6,5},{7,6},{9,8},{10,9},{11,10},{13,12},{... | collective-permute-start | bytes 1572872 | tf_op jit(solution)/shard_map/ppermute | solution.py:636
  107.5 16.9 %collective-permute-start.7 = (bf16[256,1024]{1,0:T(8,128)(2,1)S(1)}, bf16[256,1024]{1,0:T(8,128)(2,1)S(1)}, u32[]{:S(2)}, u32[]{:S(2)}) collective-permute-start(bf16[256,1024]{1,0:T(8,128)(2,1)S(1)} %join.20), channel_id=1, source_target_pairs={{0,1},{1,2},{2,3},{4,5},{5,6},{6,7},{8,9},{9,10},{10,11},{12,13},{... | collective-permute-start | bytes 1572872 | tf_op jit(solution)/shard_map/ppermute | solution.py:636
  113.8 21.9 %collective-permute-start.11 = (bf16[256,1024]{1,0:T(8,128)(2,1)S(1)}, bf16[256,1024]{1,0:T(8,128)(2,1)S(1)}, u32[]{:S(2)}, u32[]{:S(2)}) collective-permute-start(bf16[256,1024]{1,0:T(8,128)(2,1)S(1)} %join.23), channel_id=1, source_target_pairs={{0,1},{1,2},{2,3},{4,5},{5,6},{6,7},{8,9},{9,10},{10,11},{12,13},{... | collective-permute-start | bytes 1572872 | tf_op jit(solution)/shard_map/ppermute | solution.py:636
  117.3 23.6 %collective-permute-start.15 = (bf16[256,1024]{1,0:T(8,128)(2,1)S(1)}, bf16[256,1024]{1,0:T(8,128)(2,1)S(1)}, u32[]{:S(2)}, u32[]{:S(2)}) collective-permute-start(bf16[256,1024]{1,0:T(8,128)(2,1)S(1)} %join.26), channel_id=1, source_target_pairs={{1,0},{2,1},{3,2},{5,4},{6,5},{7,6},{9,8},{10,9},{11,10},{13,12},{... | collective-permute-start | bytes 1572872 | tf_op jit(solution)/shard_map/ppermute | solution.py:636
  120.3 24.4 %collective-permute-start.19 = (bf16[256,1024]{1,0:T(8,128)(2,1)S(1)}, bf16[256,1024]{1,0:T(8,128)(2,1)S(1)}, u32[]{:S(2)}, u32[]{:S(2)}) collective-permute-start(bf16[256,1024]{1,0:T(8,128)(2,1)S(1)} %join.29), channel_id=1, source_target_pairs={{1,0},{2,1},{3,2},{5,4},{6,5},{7,6},{9,8},{10,9},{11,10},{13,12},{... | collective-permute-start | bytes 1572872 | tf_op jit(solution)/shard_map/ppermute | solution.py:636
  125.2 21.7 %collective-permute-start.8 = (bf16[256,1024]{1,0:T(8,128)(2,1)S(1)}, bf16[256,1024]{1,0:T(8,128)(2,1)S(1)}, u32[]{:S(2)}, u32[]{:S(2)}) collective-permute-start(bf16[256,1024]{1,0:T(8,128)(2,1)S(1)} %join.21), channel_id=1, source_target_pairs={{0,1},{1,2},{2,3},{4,5},{5,6},{6,7},{8,9},{9,10},{10,11},{12,13},{... | collective-permute-start | bytes 1572872 | tf_op jit(solution)/shard_map/ppermute | solution.py:636
  136.5 21.7 %collective-permute-start.12 = (bf16[256,1024]{1,0:T(8,128)(2,1)S(1)}, bf16[256,1024]{1,0:T(8,128)(2,1)S(1)}, u32[]{:S(2)}, u32[]{:S(2)}) collective-permute-start(bf16[256,1024]{1,0:T(8,128)(2,1)S(1)} %join.24), channel_id=1, source_target_pairs={{0,1},{1,2},{2,3},{4,5},{5,6},{6,7},{8,9},{9,10},{10,11},{12,13},{... | collective-permute-start | bytes 1572872 | tf_op jit(solution)/shard_map/ppermute | solution.py:636
  141.7 21.6 %collective-permute-start.16 = (bf16[256,1024]{1,0:T(8,128)(2,1)S(1)}, bf16[256,1024]{1,0:T(8,128)(2,1)S(1)}, u32[]{:S(2)}, u32[]{:S(2)}) collective-permute-start(bf16[256,1024]{1,0:T(8,128)(2,1)S(1)} %join.27), channel_id=1, source_target_pairs={{1,0},{2,1},{3,2},{5,4},{6,5},{7,6},{9,8},{10,9},{11,10},{13,12},{... | collective-permute-start | bytes 1572872 | tf_op jit(solution)/shard_map/ppermute | solution.py:636
  145.5 21.7 %collective-permute-start.20 = (bf16[256,1024]{1,0:T(8,128)(2,1)S(1)}, bf16[256,1024]{1,0:T(8,128)(2,1)S(1)}, u32[]{:S(2)}, u32[]{:S(2)}) collective-permute-start(bf16[256,1024]{1,0:T(8,128)(2,1)S(1)} %join.30), channel_id=1, source_target_pairs={{1,0},{2,1},{3,2},{5,4},{6,5},{7,6},{9,8},{10,9},{11,10},{13,12},{... | collective-permute-start | bytes 1572872 | tf_op jit(solution)/shard_map/ppermute | solution.py:636
  147.8 24.5 %collective-permute-start.9 = (bf16[256,1024]{1,0:T(8,128)(2,1)S(1)}, bf16[256,1024]{1,0:T(8,128)(2,1)S(1)}, u32[]{:S(2)}, u32[]{:S(2)}) collective-permute-start(bf16[256,1024]{1,0:T(8,128)(2,1)S(1)} %join.22), channel_id=1, source_target_pairs={{0,1},{1,2},{2,3},{4,5},{5,6},{6,7},{8,9},{9,10},{10,11},{12,13},{... | collective-permute-start | bytes 1572872 | tf_op jit(solution)/shard_map/ppermute | solution.py:636
  158.9 17.3 %collective-permute-start.13 = (bf16[256,1024]{1,0:T(8,128)(2,1)S(1)}, bf16[256,1024]{1,0:T(8,128)(2,1)S(1)}, u32[]{:S(2)}, u32[]{:S(2)}) collective-permute-start(bf16[256,1024]{1,0:T(8,128)(2,1)S(1)} %join.25), channel_id=1, source_target_pairs={{0,1},{1,2},{2,3},{4,5},{5,6},{6,7},{8,9},{9,10},{10,11},{12,13},{... | collective-permute-start | bytes 1572872 | tf_op jit(solution)/shard_map/ppermute | solution.py:636
  168.0 18.1 %collective-permute-start.21 = (bf16[256,1024]{1,0:T(8,128)(2,1)S(1)}, bf16[256,1024]{1,0:T(8,128)(2,1)S(1)}, u32[]{:S(2)}, u32[]{:S(2)}) collective-permute-start(bf16[256,1024]{1,0:T(8,128)(2,1)S(1)} %join.31), channel_id=1, source_target_pairs={{1,0},{2,1},{3,2},{5,4},{6,5},{7,6},{9,8},{10,9},{11,10},{13,12},{... | collective-permute-start | bytes 1572872 | tf_op jit(solution)/shard_map/ppermute | solution.py:636
  188.2 23.5 %collective-permute-start.22 = (bf16[256,2048]{1,0:T(8,128)(2,1)S(1)}, bf16[256,2048]{1,0:T(8,128)(2,1)}, u32[]{:S(2)}, u32[]{:S(2)}) collective-permute-start(bf16[256,2048]{1,0:T(8,128)(2,1)S(1)} %add_convert_fusion.2.a_ref), channel_id=1, source_target_pairs={{0,3},{1,0},{2,1},{3,2},{4,7},{5,4},{6,5},{7,6},{8,11},{9,8},{10,9... | collective-permute-start | bytes 3145736 | tf_op jit(solution)/shard_map/ppermute | solution.py:636
  211.7 26.4 %collective-permute-start.23 = (bf16[256,2048]{1,0:T(8,128)(2,1)}, bf16[256,2048]{1,0:T(8,128)(2,1)}, u32[]{:S(2)}, u32[]{:S(2)}) collective-permute-start(bf16[256,2048]{1,0:T(8,128)(2,1)} %collective-permute-done.22.a_ref), channel_id=1, source_target_pairs={{0,3},{1,0},{2,1},{3,2},{4,7},{5,4},{6,5},{7,6},{8,11},{9,8},{10,9... | collective-permute-start | bytes 3145736 | tf_op jit(solution)/shard_map/ppermute | solution.py:636
  225.8 34.7 %collective-permute-start.25 = (bf16[256,2048]{1,0:T(8,128)(2,1)}, bf16[256,2048]{1,0:T(8,128)(2,1)S(1)}, u32[]{:S(2)}, u32[]{:S(2)}) collective-permute-start(bf16[256,2048]{1,0:T(8,128)(2,1)} %block_term.9), channel_id=1, source_target_pairs={{0,3},{1,0},{2,1},{3,2},{4,7},{5,4},{6,5},{7,6},{8,11},{9,8},{10,9... | collective-permute-start | bytes 3145736 | tf_op jit(solution)/shard_map/ppermute | solution.py:636
  238.1 44.8 %collective-permute-start.24 = (bf16[256,2048]{1,0:T(8,128)(2,1)}, bf16[256,2048]{1,0:T(8,128)(2,1)S(1)}, u32[]{:S(2)}, u32[]{:S(2)}) collective-permute-start(bf16[256,2048]{1,0:T(8,128)(2,1)} %collective-permute-done.23.a_ref), channel_id=1, source_target_pairs={{0,3},{1,0},{2,1},{3,2},{4,7},{5,4},{6,5},{7,6},{8,11},{9,8},{10,9... | collective-permute-start | bytes 3145736 | tf_op jit(solution)/shard_map/ppermute | solution.py:636
  260.8 38.4 %collective-permute-start.26 = (bf16[256,2048]{1,0:T(8,128)(2,1)S(1)}, bf16[256,2048]{1,0:T(8,128)(2,1)S(1)}, u32[]{:S(2)}, u32[]{:S(2)}) collective-permute-start(bf16[256,2048]{1,0:T(8,128)(2,1)S(1)} %add_convert_fusion.1), channel_id=1, source_target_pairs={{0,3},{1,0},{2,1},{3,2},{4,7},{5,4},{6,5},{7,6},{8,11},{9,8},{10,9... | collective-permute-start | bytes 3145736 | tf_op jit(solution)/shard_map/ppermute | solution.py:636
  302.4 18.7 %collective-permute-start.27 = (bf16[256,2048]{1,0:T(8,128)(2,1)S(1)}, bf16[256,2048]{1,0:T(8,128)(2,1)S(1)}, u32[]{:S(2)}, u32[]{:S(2)}) collective-permute-start(bf16[256,2048]{1,0:T(8,128)(2,1)S(1)} %block_term.11), channel_id=1, source_target_pairs={{0,3},{1,0},{2,1},{3,2},{4,7},{5,4},{6,5},{7,6},{8,11},{9,8},{10,9... | collective-permute-start | bytes 3145736 | tf_op jit(solution)/shard_map/ppermute | solution.py:636
  310.1 31.4 %collective-permute-start.29 = (bf16[2048,1024]{1,0:T(8,128)(2,1)}, bf16[2048,1024]{1,0:T(8,128)(2,1)}, u32[]{:S(2)}, u32[]{:S(2)}) collective-permute-start(bf16[2048,1024]{1,0:T(8,128)(2,1)} %grad_half.4), channel_id=1, source_target_pairs={{0,4},{4,0},{8,12},{12,8},{16,20},{20,16},{24,28},{28,24},{1,5},{5... | collective-permute-start | bytes 12582920 | tf_op jit(solution)/shard_map/ppermute | solution.py:657
  317.3 42.3 %collective-permute-start.32 = (bf16[2048,1024]{1,0:T(8,128)(2,1)}, bf16[2048,1024]{1,0:T(8,128)(2,1)}, u32[]{:S(2)}, u32[]{:S(2)}) collective-permute-start(bf16[2048,1024]{1,0:T(8,128)(2,1)} %grad_half.5), channel_id=1, source_target_pairs={{0,4},{4,0},{8,12},{12,8},{16,20},{20,16},{24,28},{28,24},{1,5},{5... | collective-permute-start | bytes 12582920 | tf_op jit(solution)/shard_map/ppermute | solution.py:657
  325.2 24.3 %collective-permute-start.28 = (bf16[256,2048]{1,0:T(8,128)(2,1)S(1)}, bf16[256,2048]{1,0:T(8,128)(2,1)S(1)}, u32[]{:S(2)}, u32[]{:S(2)}) collective-permute-start(bf16[256,2048]{1,0:T(8,128)(2,1)S(1)} %get-tuple-element.226.refs_0_), channel_id=1, source_target_pairs={{0,1},{1,2},{2,3},{4,5},{5,6},{6,7},{8,9},{9,10},{10,11},{12,13},{... | collective-permute-start | bytes 3145736 | tf_op jit(solution)/shard_map/ppermute | solution.py:636
  328.9 27.8 %collective-permute-start.31 = (bf16[256,2048]{1,0:T(8,128)(2,1)S(1)}, bf16[256,2048]{1,0:T(8,128)(2,1)S(1)}, u32[]{:S(2)}, u32[]{:S(2)}) collective-permute-start(bf16[256,2048]{1,0:T(8,128)(2,1)S(1)} %get-tuple-element.226.refs_0_), channel_id=1, source_target_pairs={{1,0},{2,1},{3,2},{5,4},{6,5},{7,6},{9,8},{10,9},{11,10},{13,12},{... | collective-permute-start | bytes 3145736 | tf_op jit(solution)/shard_map/ppermute | solution.py:636
  351.2 23.5 %collective-permute-start.30 = (bf16[256,2048]{1,0:T(8,128)(2,1)}, bf16[256,2048]{1,0:T(8,128)(2,1)}, u32[]{:S(2)}, u32[]{:S(2)}) collective-permute-start(bf16[256,2048]{1,0:T(8,128)(2,1)} %join.32), channel_id=1, source_target_pairs={{0,1},{1,2},{2,3},{4,5},{5,6},{6,7},{8,9},{9,10},{10,11},{12,13},{... | collective-permute-start | bytes 3145736 | tf_op jit(solution)/shard_map/ppermute | solution.py:636
  358.3 25.6 %collective-permute-start.35 = (bf16[256,2048]{1,0:T(8,128)(2,1)}, bf16[256,2048]{1,0:T(8,128)(2,1)}, u32[]{:S(2)}, u32[]{:S(2)}) collective-permute-start(bf16[256,2048]{1,0:T(8,128)(2,1)} %join.33), channel_id=1, source_target_pairs={{1,0},{2,1},{3,2},{5,4},{6,5},{7,6},{9,8},{10,9},{11,10},{13,12},{... | collective-permute-start | bytes 3145736 | tf_op jit(solution)/shard_map/ppermute | solution.py:636
  370.1 146.2 %reduce-scatter.5.cloned.1.call-start = ((), (), s32[]{:S(2)}) async-start(), calls=%async_computation.3 | async-start | bytes 5242880 | tf_op jit(solution)/shard_map/reduce_scatter | solution.py:785
  378.8 23.0 %collective-permute-start.33 = (bf16[256,2048]{1,0:T(8,128)(2,1)S(1)}, bf16[256,2048]{1,0:T(8,128)(2,1)S(1)}, u32[]{:S(2)}, u32[]{:S(2)}) collective-permute-start(bf16[256,2048]{1,0:T(8,128)(2,1)S(1)} %join.34), channel_id=1, source_target_pairs={{0,1},{1,2},{2,3},{4,5},{5,6},{6,7},{8,9},{9,10},{10,11},{12,13},{... | collective-permute-start | bytes 3145736 | tf_op jit(solution)/shard_map/ppermute | solution.py:636
  385.7 22.9 %collective-permute-start.36 = (bf16[256,2048]{1,0:T(8,128)(2,1)S(1)}, bf16[256,2048]{1,0:T(8,128)(2,1)S(1)}, u32[]{:S(2)}, u32[]{:S(2)}) collective-permute-start(bf16[256,2048]{1,0:T(8,128)(2,1)S(1)} %join.36), channel_id=1, source_target_pairs={{1,0},{2,1},{3,2},{5,4},{6,5},{7,6},{9,8},{10,9},{11,10},{13,12},{... | collective-permute-start | bytes 3145736 | tf_op jit(solution)/shard_map/ppermute | solution.py:636
  402.7 28.5 %collective-permute-start.34 = (bf16[256,2048]{1,0:T(8,128)(2,1)S(1)}, bf16[256,2048]{1,0:T(8,128)(2,1)S(1)}, u32[]{:S(2)}, u32[]{:S(2)}) collective-permute-start(bf16[256,2048]{1,0:T(8,128)(2,1)S(1)} %join.35), channel_id=1, source_target_pairs={{0,1},{1,2},{2,3},{4,5},{5,6},{6,7},{8,9},{9,10},{10,11},{12,13},{... | collective-permute-start | bytes 3145736 | tf_op jit(solution)/shard_map/ppermute | solution.py:636
  409.3 22.3 %collective-permute-start.37 = (bf16[256,2048]{1,0:T(8,128)(2,1)S(1)}, bf16[256,2048]{1,0:T(8,128)(2,1)S(1)}, u32[]{:S(2)}, u32[]{:S(2)}) collective-permute-start(bf16[256,2048]{1,0:T(8,128)(2,1)S(1)} %join.37), channel_id=1, source_target_pairs={{1,0},{2,1},{3,2},{5,4},{6,5},{7,6},{9,8},{10,9},{11,10},{13,12},{... | collective-permute-start | bytes 3145736 | tf_op jit(solution)/shard_map/ppermute | solution.py:636
  440.4 27.3 %collective-permute-start.38 = (bf16[256,2048]{1,0:T(8,128)(2,1)}, bf16[256,2048]{1,0:T(8,128)(2,1)}, u32[]{:S(2)}, u32[]{:S(2)}) collective-permute-start(bf16[256,2048]{1,0:T(8,128)(2,1)} %block_term.12), channel_id=1, source_target_pairs={{0,3},{1,0},{2,1},{3,2},{4,7},{5,4},{6,5},{7,6},{8,11},{9,8},{10,9... | collective-permute-start | bytes 3145736 | tf_op jit(solution)/shard_map/ppermute | solution.py:636
  471.3 28.1 %collective-permute-start.40 = (bf16[256,2048]{1,0:T(8,128)(2,1)}, bf16[256,2048]{1,0:T(8,128)(2,1)}, u32[]{:S(2)}, u32[]{:S(2)}) collective-permute-start(bf16[256,2048]{1,0:T(8,128)(2,1)} %join.38), channel_id=1, source_target_pairs={{0,3},{1,0},{2,1},{3,2},{4,7},{5,4},{6,5},{7,6},{8,11},{9,8},{10,9... | collective-permute-start | bytes 3145736 | tf_op jit(solution)/shard_map/ppermute | solution.py:636
  489.2 17.3 %collective-permute-start.45 = (f32[8320]{0:T(1024)S(1)}, f32[8320]{0:T(1024)S(1)}, u32[]{:S(2)}, u32[]{:S(2)}) collective-permute-start(f32[8320]{0:T(1024)S(1)} %add.128), channel_id=1, source_target_pairs={{0,1},{1,2},{2,3},{3,0},{4,5},{5,6},{6,7},{7,4},{8,9},{9,10},{10,1... | collective-permute-start | bytes 99848 | tf_op jit(solution)/shard_map/ppermute | solution.py:636
  489.2 17.3 %collective-permute-start.46 = (f32[8320]{0:T(1024)S(1)}, f32[8320]{0:T(1024)S(1)}, u32[]{:S(2)}, u32[]{:S(2)}) collective-permute-start(f32[8320]{0:T(1024)S(1)} %add.128), channel_id=1, source_target_pairs={{0,2},{1,3},{2,0},{3,1},{4,6},{5,7},{6,4},{7,5},{8,10},{9,11},{10,... | collective-permute-start | bytes 99848 | tf_op jit(solution)/shard_map/ppermute | solution.py:636
  489.8 16.6 %collective-permute-start.47 = (f32[8320]{0:T(1024)S(1)}, f32[8320]{0:T(1024)S(1)}, u32[]{:S(2)}, u32[]{:S(2)}) collective-permute-start(f32[8320]{0:T(1024)S(1)} %add.128), channel_id=1, source_target_pairs={{0,3},{1,0},{2,1},{3,2},{4,7},{5,4},{6,5},{7,6},{8,11},{9,8},{10,9... | collective-permute-start | bytes 99848 | tf_op jit(solution)/shard_map/ppermute | solution.py:636
  502.1 25.4 %collective-permute-start.42 = (bf16[256,2048]{1,0:T(8,128)(2,1)}, bf16[256,2048]{1,0:T(8,128)(2,1)S(1)}, u32[]{:S(2)}, u32[]{:S(2)}) collective-permute-start(bf16[256,2048]{1,0:T(8,128)(2,1)} %join.39), channel_id=1, source_target_pairs={{0,3},{1,0},{2,1},{3,2},{4,7},{5,4},{6,5},{7,6},{8,11},{9,8},{10,9... | collective-permute-start | bytes 3145736 | tf_op jit(solution)/shard_map/ppermute | solution.py:636
  506.5 23.9 %collective-permute-start.48 = (f32[8320]{0:T(1024)S(1)}, f32[8320]{0:T(1024)S(1)}, u32[]{:S(2)}, u32[]{:S(2)}) collective-permute-start(f32[8320]{0:T(1024)S(1)} %add_add_fusion.2), channel_id=1, source_target_pairs={{0,8},{4,12},{8,16},{12,20},{16,24},{20,28},{24,0},{28,4},{1,9},{5... | collective-permute-start | bytes 99848 | tf_op jit(solution)/shard_map/ppermute | solution.py:830
  508.0 22.4 %collective-permute-start.49 = (f32[8320]{0:T(1024)S(1)}, f32[8320]{0:T(1024)S(1)}, u32[]{:S(2)}, u32[]{:S(2)}) collective-permute-start(f32[8320]{0:T(1024)S(1)} %add_add_fusion.2), channel_id=1, source_target_pairs={{0,16},{4,20},{8,24},{12,28},{16,0},{20,4},{24,8},{28,12},{1,17},{... | collective-permute-start | bytes 99848 | tf_op jit(solution)/shard_map/ppermute | solution.py:830
  509.4 20.9 %collective-permute-start.50 = (f32[8320]{0:T(1024)S(1)}, f32[8320]{0:T(1024)S(1)}, u32[]{:S(2)}, u32[]{:S(2)}) collective-permute-start(f32[8320]{0:T(1024)S(1)} %add_add_fusion.2), channel_id=1, source_target_pairs={{0,24},{4,28},{8,0},{12,4},{16,8},{20,12},{24,16},{28,20},{1,25},{... | collective-permute-start | bytes 99848 | tf_op jit(solution)/shard_map/ppermute | solution.py:830
  (90 other events, 785.1 us)
Sparse Core Ops, SparseCore 0:
  370.3 86.6 reduce-scatter.2
  460.3 55.9 reduce-scatter.4

commit v13 on v12

--- a/solution.py
+++ b/solution.py
@@ -120,11 +120,22 @@
     )(rank, xa, xb, gain, shift, wq, wk, wv, cos, sin, *extra)
 
 
+def by_reach(n, rows, edge_ref, block):
+    for b in range(n):
+        keys = list(range(first_key(b, rows), b + 1))
+        if len(keys) <= 2:
+            block(b, keys)
+        else:
+            far = edge_ref[n + b - 2] == edge_ref[b]
+            pl.when(far)(functools.partial(block, b, keys))
+            pl.when(jnp.logical_not(far))(functools.partial(block, b, keys[-2:]))
+
+
 def first_key(block, rows):
     return max(0, block - (DOC_MAX - 1 + rows - 1) // rows)
 
 
-def attend_body(rank_ref, q_ref, k_ref, v_ref, dcol_ref, drow_ref, hc_ref, o_ref):
+def attend_body(rank_ref, edge_ref, q_ref, k_ref, v_ref, dcol_ref, drow_ref, hc_ref, o_ref):
     n, rows, _ = q_ref.shape
     rank = rank_ref[0]
     head = rank_ref[1] + pl.program_id(0)
@@ -133,10 +144,10 @@
     low = lax.broadcasted_iota(jnp.int32, (rows, rows), 0) >= lax.broadcasted_iota(
         jnp.int32, (rows, rows), 1
     )
-    for b in range(n):
+
+    def block(b, keys):
         q = q_ref[slot(b)]
         doc = dcol_ref[b]
-        keys = range(first_key(b, rows), b + 1)
         scores = []
         for c in keys:
             s = dot_t(q, k_ref[slot(c)])
@@ -159,17 +170,19 @@
         gate = jnp.where(hc_ref[b] > head, 1.0, 0.0)
         o_ref[slot(b)] = (out * (gate / total)).astype(BF16)
 
-
-def attend(rank, q, k, v, docs_col, docs_row, heads_col):
+    by_reach(n, rows, edge_ref, block)
+
+
+def attend(rank, edges, q, k, v, docs_col, docs_row, heads_col):
     n, rows, local = q.shape
-    spec = pl.BlockSpec((n, rows, E), lambda h, r: (0, 0, h))
-    col = pl.BlockSpec((n, rows, 1), lambda h, r: (0, 0, 0))
-    row = pl.BlockSpec((n, 1, rows), lambda h, r: (0, 0, 0))
+    spec = pl.BlockSpec((n, rows, E), lambda h, r, e: (0, 0, h))
+    col = pl.BlockSpec((n, rows, 1), lambda h, r, e: (0, 0, 0))
+    row = pl.BlockSpec((n, 1, rows), lambda h, r, e: (0, 0, 0))
     t = n * rows
     return pl.pallas_call(
         attend_body,
         grid_spec=pltpu.PrefetchScalarGridSpec(
-            num_scalar_prefetch=1,
+            num_scalar_prefetch=2,
             grid=(local // E,),
             in_specs=[spec, spec, spec, col, row, col],
             out_specs=spec,
@@ -178,11 +191,11 @@
         compiler_params=params(62),
         cost_estimate=cost(4 * t * t * local, 8 * t * local, t * t * local // E),
         name="attend",
-    )(rank, q, k, v, docs_col, docs_row, heads_col)
+    )(rank, edges, q, k, v, docs_col, docs_row, heads_col)
 
 
 def attend_back_body(
-    rank_ref, q_ref, k_ref, v_ref, do_ref, dcol_ref, drow_ref, hc_ref, cos_ref, sin_ref, out_ref, dk_ref, dv_ref
+    rank_ref, edge_ref, q_ref, k_ref, v_ref, do_ref, dcol_ref, drow_ref, hc_ref, cos_ref, sin_ref, out_ref, dk_ref, dv_ref
 ):
     n, rows, _ = q_ref.shape
     rank = rank_ref[0]
@@ -202,10 +215,9 @@
         w = w * scale
         return (w * cos_ref[b] - pltpu.roll(w, E // 2, 1) * sin_ref[b]).astype(BF16)
 
-    for b in range(n):
+    def block(b, keys):
         q = q_ref[slot(b)]
         grad = jnp.where(hc_ref[b] > head, do_ref[slot(b)].astype(F32), 0.0).astype(BF16)
-        keys = range(first_key(b, rows), b + 1)
         scores = []
         for c in keys:
             s = dot_t(k_ref[slot(c)], q)
@@ -236,32 +248,34 @@
             part = outer(ds, k_ref[slot(c)])
             dq = part if dq is None else dq + part
         out_ref[slot(b), :, lanes(0)] = unrotate(dq, b)
+
+    by_reach(n, rows, edge_ref, block)
     for b in range(n):
         out_ref[slot(b), :, lanes(1)] = unrotate(dk_ref[b], b)
         out_ref[slot(b), :, lanes(2)] = dv_ref[b].astype(BF16)
 
 
-def attend_back(rank, q, k, v, do, docs_col, docs_row, heads_col, cos, sin):
+def attend_back(rank, edges, q, k, v, do, docs_col, docs_row, heads_col, cos, sin):
     n, rows, local = q.shape
-    spec = pl.BlockSpec((n, rows, E), lambda h, r: (0, 0, h))
-    col = pl.BlockSpec((n, rows, 1), lambda h, r: (0, 0, 0))
-    row = pl.BlockSpec((n, 1, rows), lambda h, r: (0, 0, 0))
-    table = pl.BlockSpec((n, rows, E), lambda h, r: (0, 0, 0))
+    spec = pl.BlockSpec((n, rows, E), lambda h, r, e: (0, 0, h))
+    col = pl.BlockSpec((n, rows, 1), lambda h, r, e: (0, 0, 0))
+    row = pl.BlockSpec((n, 1, rows), lambda h, r, e: (0, 0, 0))
+    table = pl.BlockSpec((n, rows, E), lambda h, r, e: (0, 0, 0))
     t = n * rows
     return pl.pallas_call(
         attend_back_body,
         grid_spec=pltpu.PrefetchScalarGridSpec(
-            num_scalar_prefetch=1,
+            num_scalar_prefetch=2,
             grid=(local // E,),
             in_specs=[spec, spec, spec, spec, col, row, col, table, table],
-            out_specs=pl.BlockSpec((n, rows, 3 * local), lambda h, r: (0, 0, 0)),
+            out_specs=pl.BlockSpec((n, rows, 3 * local), lambda h, r, e: (0, 0, 0)),
             scratch_shapes=[pltpu.VMEM((n, rows, E), F32), pltpu.VMEM((n, rows, E), F32)],
         ),
         out_shape=jax.ShapeDtypeStruct((n, rows, 3 * local), BF16),
         compiler_params=params(24),
         cost_estimate=cost(116e9, 14 * t * local),
         name="attend_back",
-    )(rank, q, k, v, do, docs_col, docs_row, heads_col, cos, sin)
+    )(rank, edges, q, k, v, do, docs_col, docs_row, heads_col, cos, sin)
 
 
 def mlp_body(slot, n, rank_ref, a_ref, gla_ref, glb_ref, gra_ref, grb_ref, up_ref, down_ref, bucket_ref, *rest):
@@ -657,6 +671,7 @@
     swap = lambda v: lax.ppermute(v, "dp", [(i, i ^ 1) for i in range(n_dp)])
     sides = [list(range(c, n_dp, 2)) for c in range(2)]
     docs_col = doc_ids.reshape(n, rows, 1)
+    edges = jnp.concatenate([doc_ids[0, ::rows], doc_ids[0, rows - 1 :: rows]])
     docs_row = doc_ids.reshape(n, 1, rows)
     heads_col = head_count.reshape(n, rows, 1)
     bucket_col = width_bucket.reshape(n, rows, 1)
@@ -693,7 +708,7 @@
             right[p], left[p] = send(right[p], right_line), send(left[p], left_line)
 
     half_tick(0)
-    masked = attend(where, query, keys, vals, docs_col, docs_row, heads_col)
+    masked = attend(where, edges, query, keys, vals, docs_col, docs_row, heads_col)
     terms = low(dot_t(flat(masked), output_weight)).reshape(n, rows, d)
     for k in range(1, n):
         grads_r.append(list(right))
@@ -763,7 +778,7 @@
     held = dom_part(n, early, where, pick(early), output_weight, None)
     grad_masked, state_all = dom_part(n, late, where, pick(late), output_weight, held)
     dqkv = attend_back(
-        where, query, keys, vals, grad_masked, docs_col, docs_row, heads_col, cos, sin
+        where, edges, query, keys, vals, grad_masked, docs_col, docs_row, heads_col, cos, sin
     )
     mixed = low(state + owned(ffn, right, left))
 

time: 549 us -> 549 us (level)
  waiting for transfers between devices: 131 us -> 123 us
  starting transfers between devices: 119 us -> 125 us
    ppermute x42, waiting for transfers between devices: 124 us -> 114 us  [per_device(): send = lambda v, pairs: lax.ppermute(v, 'mp', pairs)]
    unnamed x173 -> x177, local copies, waits for them, and re-layouts: 23.6 us -> 23.8 us
  transfers between devices with their start and end apart: 53 -> 53, of which waited for: 27 -> 25; matrix products, arithmetic and copies ran while one was open for 7% -> 7% of each run, Pallas kernels for 38% -> 38%
where the time goes in v13:
time: 549 us; the launch traced here: 539 us
  Pallas kernels  207 us (38%)
  starting transfers between devices  125 us (23%)
  waiting for transfers between devices  123 us (22%)
  local copies, waits for them, and re-layouts  31 us (6%)
  other arithmetic  21 us (4%)
  between operations  16 us (3%)
  matrix products  15.6 us (3%)
    ppermute x42, starting transfers between devices, per_device(): send = lambda v, pairs: lax.ppermute(v, 'mp', pairs)  117 us
    ppermute x42, waiting for transfers between devices, per_device(): send = lambda v, pairs: lax.ppermute(v, 'mp', pairs)  114 us
    pallas_call x4, Pallas kernels, mlp_slot(): pl.pallas_call(functools.partial(mlp_body, slot, n), grid_spec=pltpu.Pref...  39.2 us
    pallas_call x4, Pallas kernels, grad_half(): pl.pallas_call(functools.partial(grad_body, not partner), grid_spec=pltpu...  29.6 us
    pallas_call x4, Pallas kernels, qkv_slot(): pl.pallas_call(qkv_body, grid_spec=pltpu.PrefetchScalarGridSpec(num_scala...  28.7 us
    pallas_call x20, Pallas kernels, join(): pl.pallas_call(functools.partial(join_body, 0 if right else -1, first), g...  26 us
    unnamed x177, local copies, waits for them, and re-layouts  23.8 us
    pallas_call x8, Pallas kernels, block_term(): pl.pallas_call(term_body, grid=(d // tile,), in_specs=[pl.BlockSpec((1, r...  23.8 us
  transfers between devices with their start and end apart: 53, of which 25 were waited for; matrix products, arithmetic and copies ran while one was open for 7% of the time, Pallas kernels for 38%

profile of v13, /device:TPU:0, one launch (start us, length us, event | category | flops | bytes accessed | tf_op | source)
XLA Modules:
  0.0 538.8 jit_solution(16243568714519084533)
XLA Ops:
  8.5 5.1 collective-permute-start
  17.9 7.1 %qkv_slot.4 = (bf16[4,256,2048]{2,1,0:T(8,128)(2,1)}, bf16[4,256,512]{2,1,0:T(8,128)(2,1)}, bf16[4,256,512]{2,1,0:T(8,128)(2,1)}, bf16[4,256,512]{2,1,0:T(8,128)(2,1)}) custom-call(s32[4]{0:T(128)} %pad_add_fusion.rank_ref, bf16[256,1024]{1,0:T(8,128)(2,1)} %copy-done.62, bf16[256,1024]{1,0:T(8,128)(2,1)} %copy-done.61, f32[1,2048]{1,0:T(1,128)} %bitcast.107, ...), custom_call_target="tpu_custom_call" | custom-call | flops 1610612736 | bytes 8388608 | tf_op jit(solution)/shard_map/qkv_slot/pallas_call | solution.py:106
  26.0 4.4 collective-permute-start.1
  30.3 6.8 %collective-permute-done.2.xb_ref = bf16[256,1024]{1,0:T(8,128)(2,1)S(1)} collective-permute-done((bf16[256,1024]{1,0:T(8,128)(2,1)S(1)}, bf16[256,1024]{1,0:T(8,128)(2,1)S(1)}, u32[]{:S(2)}, u32[]{:S(2)}) %collective-permute-start.2) | collective-permute-done | bytes 524320 | tf_op jit(solution)/shard_map/ppermute | solution.py:650
  37.2 4.3 collective-permute-start.4
  41.5 7.1 %qkv_slot.5 = (bf16[4,256,2048]{2,1,0:T(8,128)(2,1)}, bf16[4,256,512]{2,1,0:T(8,128)(2,1)}, bf16[4,256,512]{2,1,0:T(8,128)(2,1)}, bf16[4,256,512]{2,1,0:T(8,128)(2,1)}) custom-call(s32[4]{0:T(128)} %pad_add_fusion.rank_ref, ...), custom_call_target="tpu_custom_call", output_to_operand_aliasing={{0}: (10, {}), {1}: (11, {}), {2}: (12, {}), {3}: (13, {})} | custom-call | flops 1610612736 | bytes 8388608 | tf_op jit(solution)/shard_map/qkv_slot/pallas_call | solution.py:106
  64.5 7.3 %qkv_slot.6 = (bf16[4,256,2048]{2,1,0:T(8,128)(2,1)}, bf16[4,256,512]{2,1,0:T(8,128)(2,1)}, bf16[4,256,512]{2,1,0:T(8,128)(2,1)}, bf16[4,256,512]{2,1,0:T(8,128)(2,1)}) custom-call(s32[4]{0:T(128)} %pad_add_fusion.rank_ref, bf16[256,1024]{1,0:T(8,128)(2,1)} %copy-done.68, ...), custom_call_target="tpu_custom_call", output_to_operand_aliasing={{0}: (10, {}), {1}: (11, {}), {2}: (12, {}), {3}: (13, {})} | custom-call | flops 1610612736 | bytes 8388608 | tf_op jit(solution)/shard_map/qkv_slot/pallas_call | solution.py:106
  74.7 5.4 collective-permute-start.10
  83.0 7.1 %qkv_slot.7 = (bf16[4,256,2048]{2,1,0:T(8,128)(2,1)}, bf16[4,256,512]{2,1,0:T(8,128)(2,1)}, bf16[4,256,512]{2,1,0:T(8,128)(2,1)}, bf16[4,256,512]{2,1,0:T(8,128)(2,1)}) custom-call(s32[4]{0:T(128)} %pad_add_fusion.rank_ref, bf16[256,1024]{1,0:T(8,128)(2,1)} %copy-done.67, ...), custom_call_target="tpu_custom_call", output_to_operand_aliasing={{0}: (10, {}), {1}: (11, {}), {2}: (12, {}), {3}: (13, {})} | custom-call | flops 1610612736 | bytes 8388608 | tf_op jit(solution)/shard_map/qkv_slot/pallas_call | solution.py:106
  90.2 11.0 %attend.1 = bf16[4,256,512]{2,1,0:T(8,128)(2,1)} custom-call(s32[4]{0:T(128)} %pad_add_fusion.rank_ref, s32[8]{0:T(128)} %pad_add_fusion.1.edge_ref, bf16[4,256,512]{2,1,0:T(8,128)(2,1)} %get-tuple-element.184.q_ref, bf16[4,256,512]{2,1,0:T(8,128)(2,1)} %get-tuple-element.185.k_ref, bf16[4,256,512]{2,1,0:T(8,128)(2,1)} %get-tuple-element.186.v_ref, ...), custom_call_target="tpu_custom_call" | custom-call | flops 2147483648 | bytes 4194304 | tf_op jit(solution)/shard_map/attend/pallas_call | solution.py:182
  101.2 4.3 convolution_convert_fusion.1
  112.0 4.6 collective-permute-start.11
  123.5 5.8 %collective-permute-start.8 = (bf16[256,1024]{1,0:T(8,128)(2,1)S(1)}, bf16[256,1024]{1,0:T(8,128)(2,1)S(1)}, u32[]{:S(2)}, u32[]{:S(2)}) collective-permute-start(bf16[256,1024]{1,0:T(8,128)(2,1)S(1)} %join.21), channel_id=1, source_target_pairs={{0,1},{1,2},{2,3},{4,5},{5,6},{6,7},{8,9},{9,10},{10,11},{12,13},{... | collective-permute-start | bytes 1572872 | tf_op jit(solution)/shard_map/ppermute | solution.py:650
  129.3 4.6 collective-permute-done.11.moved_ref.grb_ref
  134.7 4.7 collective-permute-start.12
  141.7 5.4 collective-permute-done.19.moved_ref.glb_ref
  150.1 4.6 collective-permute-start.9
  157.2 4.7 collective-permute-start.13
  164.1 5.4 %collective-permute-done.20.moved_ref.glb_ref = bf16[256,1024]{1,0:T(8,128)(2,1)S(1)} collective-permute-done((bf16[256,1024]{1,0:T(8,128)(2,1)S(1)}, bf16[256,1024]{1,0:T(8,128)(2,1)S(1)}, u32[]{:S(2)}, u32[]{:S(2)}) %collective-permute-start.20) | collective-permute-done | bytes 524320 | tf_op jit(solution)/shard_map/ppermute | solution.py:650
  175.5 5.3 collective-permute-done.17
  180.7 7.0 %collective-permute-done.21 = bf16[256,1024]{1,0:T(8,128)(2,1)S(1)} collective-permute-done((bf16[256,1024]{1,0:T(8,128)(2,1)S(1)}, bf16[256,1024]{1,0:T(8,128)(2,1)S(1)}, u32[]{:S(2)}, u32[]{:S(2)}) %collective-permute-start.21) | collective-permute-done | bytes 524320 | tf_op jit(solution)/shard_map/ppermute | solution.py:650
  191.7 9.3 %mlp_slot.4 = (bf16[4,256,2048]{2,1,0:T(8,128)(2,1)S(1)}, bf16[4,256,2048]{2,1,0:T(8,128)(2,1)S(1)}, bf16[4,256,2048]{2,1,0:T(8,128)(2,1)S(1)}, bf16[4,256,2048]{2,1,0:T(8,128)(2,1)S(1)}) custom-call(s32[4]{0:T(128)S(1)} %copy-done.45, bf16[256,2048]{1,0:T(8,128)(2,1)S(1)} %add_convert_fusion.2.a_ref, ...), custom_call_target="tpu_custom_call" | custom-call | flops 4294967296 | bytes 20971520 | tf_op jit(solution)/shard_map/mlp_slot/pallas_call | solution.py:317
  208.5 4.9 collective-permute-done.22.a_ref
  213.8 10.2 %mlp_slot.5 = (bf16[4,256,2048]{2,1,0:T(8,128)(2,1)S(1)}, bf16[4,256,2048]{2,1,0:T(8,128)(2,1)S(1)}, bf16[4,256,2048]{2,1,0:T(8,128)(2,1)S(1)}, bf16[4,256,2048]{2,1,0:T(8,128)(2,1)S(1)}) custom-call(s32[4]{0:T(128)S(1)} %copy-done.45, ...), custom_call_target="tpu_custom_call", output_to_operand_aliasing={{0}: (9, {}), {1}: (10, {}), {2}: (11, {}), {3}: (12, {})} | custom-call | flops 4294967296 | bytes 20971520 | tf_op jit(solution)/shard_map/mlp_slot/pallas_call | solution.py:317
  229.2 10.6 %collective-permute-done.23.a_ref = bf16[256,2048]{1,0:T(8,128)(2,1)} collective-permute-done((bf16[256,2048]{1,0:T(8,128)(2,1)}, bf16[256,2048]{1,0:T(8,128)(2,1)}, u32[]{:S(2)}, u32[]{:S(2)}) %collective-permute-start.23) | collective-permute-done | bytes 1048608 | tf_op jit(solution)/shard_map/ppermute | solution.py:650
  242.1 9.6 %mlp_slot.6 = (bf16[4,256,2048]{2,1,0:T(8,128)(2,1)S(1)}, bf16[4,256,2048]{2,1,0:T(8,128)(2,1)S(1)}, bf16[4,256,2048]{2,1,0:T(8,128)(2,1)S(1)}, bf16[4,256,2048]{2,1,0:T(8,128)(2,1)S(1)}) custom-call(s32[4]{0:T(128)S(1)} %copy-done.45, ...), custom_call_target="tpu_custom_call", output_to_operand_aliasing={{0}: (9, {}), {1}: (10, {}), {2}: (11, {}), {3}: (12, {})} | custom-call | flops 4294967296 | bytes 20971520 | tf_op jit(solution)/shard_map/mlp_slot/pallas_call | solution.py:317
  254.8 7.4 %collective-permute-done.25 = bf16[256,2048]{1,0:T(8,128)(2,1)S(1)} collective-permute-done((bf16[256,2048]{1,0:T(8,128)(2,1)}, bf16[256,2048]{1,0:T(8,128)(2,1)S(1)}, u32[]{:S(2)}, u32[]{:S(2)}) %collective-permute-start.25) | collective-permute-done | bytes 1048608 | tf_op jit(solution)/shard_map/ppermute | solution.py:650
  264.9 19.8 %collective-permute-done.24.a_ref = bf16[256,2048]{1,0:T(8,128)(2,1)S(1)} collective-permute-done((bf16[256,2048]{1,0:T(8,128)(2,1)}, bf16[256,2048]{1,0:T(8,128)(2,1)S(1)}, u32[]{:S(2)}, u32[]{:S(2)}) %collective-permute-start.24) | collective-permute-done | bytes 1048608 | tf_op jit(solution)/shard_map/ppermute | solution.py:650
  284.7 10.2 %mlp_slot.7 = (bf16[4,256,2048]{2,1,0:T(8,128)(2,1)S(1)}, bf16[4,256,2048]{2,1,0:T(8,128)(2,1)S(1)}, bf16[4,256,2048]{2,1,0:T(8,128)(2,1)S(1)}, bf16[4,256,2048]{2,1,0:T(8,128)(2,1)S(1)}) custom-call(s32[4]{0:T(128)S(1)} %copy-done.45, ...), custom_call_target="tpu_custom_call", output_to_operand_aliasing={{0}: (9, {}), {1}: (10, {}), {2}: (11, {}), {3}: (12, {})} | custom-call | flops 4294967296 | bytes 20971520 | tf_op jit(solution)/shard_map/mlp_slot/pallas_call | solution.py:317
  294.8 6.3 %collective-permute-done.26.rest_0_ = bf16[256,2048]{1,0:T(8,128)(2,1)S(1)} collective-permute-done((bf16[256,2048]{1,0:T(8,128)(2,1)S(1)}, bf16[256,2048]{1,0:T(8,128)(2,1)S(1)}, u32[]{:S(2)}, u32[]{:S(2)}) %collective-permute-start.26) | collective-permute-done | bytes 1048608 | tf_op jit(solution)/shard_map/ppermute | solution.py:650
  306.6 7.2 %grad_half.4 = bf16[2048,1024]{1,0:T(8,128)(2,1)} custom-call(s32[4]{0:T(128)S(1)} %copy-done.45, bf16[1024,2048]{1,0:T(8,128)(2,1)S(1)} %bitcast.95, bf16[1024,2048]{1,0:T(8,128)(2,1)S(1)} %bitcast.90), custom_call_target="tpu_custom_call" | custom-call | flops 1000000 | bytes 1000000 | tf_op jit(solution)/shard_map/grad_half/pallas_call | solution.py:427
  313.8 7.2 %grad_half.5 = bf16[2048,1024]{1,0:T(8,128)(2,1)} custom-call(s32[4]{0:T(128)S(1)} %copy-done.45, bf16[1024,2048]{1,0:T(8,128)(2,1)S(1)} %bitcast.93, bf16[1024,2048]{1,0:T(8,128)(2,1)S(1)} %bitcast.74), custom_call_target="tpu_custom_call" | custom-call | flops 1000000 | bytes 1000000 | tf_op jit(solution)/shard_map/grad_half/pallas_call | solution.py:427
  332.3 11.3 %convolution_convert_fusion = bf16[1024,2048]{1,0:T(8,128)(2,1)S(1)} fusion(bf16[1024,2048]{1,0:T(8,128)(2,1)S(1)} %bitcast.91, bf16[2048,2048]{1,0:T(8,128)(2,1)} %down_ref.7), kind=kOutput, calls=%fused_computation | convolution fusion | flops 8592031744 | bytes 16777216 | tf_op jit(solution)/shard_map/dot_general | solution.py:53
  343.6 8.0 %grad_half.6.rest_1_ = bf16[2,2048,1024]{2,1,0:T(8,128)(2,1)S(1)} custom-call(s32[4]{0:T(128)S(1)} %copy-done.45, bf16[1024,2048]{1,0:T(8,128)(2,1)S(1)} %bitcast.96, bf16[1024,2048]{1,0:T(8,128)(2,1)S(1)} %bitcast.92, bf16[2048,1024]{1,0:T(8,128)(2,1)} %collective-permute-done.29.rest_0_), custom_call_target="tpu_custom_call" | custom-call | flops 1000000 | bytes 1000000 | tf_op jit(solution)/shard_map/grad_half/pallas_call | solution.py:427
  353.3 5.4 %collective-permute-start.30 = (bf16[256,2048]{1,0:T(8,128)(2,1)}, bf16[256,2048]{1,0:T(8,128)(2,1)}, u32[]{:S(2)}, u32[]{:S(2)}) collective-permute-start(bf16[256,2048]{1,0:T(8,128)(2,1)} %join.32), channel_id=1, source_target_pairs={{0,1},{1,2},{2,3},{4,5},{5,6},{6,7},{8,9},{9,10},{10,11},{12,13},{... | collective-permute-start | bytes 3145736 | tf_op jit(solution)/shard_map/ppermute | solution.py:650
  361.7 7.2 %grad_half.7 = bf16[2,2048,1024]{2,1,0:T(8,128)(2,1)S(1)} custom-call(s32[4]{0:T(128)S(1)} %copy-done.45, bf16[1024,2048]{1,0:T(8,128)(2,1)S(1)} %bitcast.94, bf16[1024,2048]{1,0:T(8,128)(2,1)S(1)} %bitcast.75, bf16[2048,1024]{1,0:T(8,128)(2,1)} %collective-permute-done.32.rest_0_, ...), custom_call_target="tpu_custom_call", output_to_operand_aliasing={{}: (4, {})} | custom-call | flops 1000000 | bytes 1000000 | tf_op jit(solution)/shard_map/grad_half/pallas_call | solution.py:427
  372.3 4.3 collective-permute-done.30.moved_ref.refs_2_
  380.9 4.7 collective-permute-start.33
  393.3 10.2 %collective-permute-done.33.moved_ref.refs_1_ = bf16[256,2048]{1,0:T(8,128)(2,1)S(1)} collective-permute-done((bf16[256,2048]{1,0:T(8,128)(2,1)S(1)}, bf16[256,2048]{1,0:T(8,128)(2,1)S(1)}, u32[]{:S(2)}, u32[]{:S(2)}) %collective-permute-start.33) | collective-permute-done | bytes 1048608 | tf_op jit(solution)/shard_map/ppermute | solution.py:650
  404.4 4.5 collective-permute-start.34
  414.5 14.6 %attend_back.1.x_ref = bf16[4,256,1536]{2,1,0:T(8,128)(2,1)S(1)} custom-call(s32[4]{0:T(128)S(1)} %copy-done.45, s32[8]{0:T(128)S(1)} %copy-done.52, bf16[4,256,512]{2,1,0:T(8,128)(2,1)S(1)} %copy-done.18, bf16[4,256,512]{2,1,0:T(8,128)(2,1)S(1)} %copy-done.19, bf16[4,256,512]{2,1,0:T(8,128)(2,1)S(1)} %copy-done.20, ...), custom_call_target="tpu_custom_call" | custom-call | flops 115999997952 | bytes 7340032 | tf_op jit(solution)/shard_map/attend_back/pallas_call | solution.py:265
  433.5 7.4 %attn_grads.2 = bf16[2048,1024]{1,0:T(8,128)(2,1)S(1)} custom-call(s32[4]{0:T(128)S(1)} %copy-done.45, bf16[1024,2048]{1,0:T(8,128)(2,1)S(1)} %bitcast.87, bf16[1024,2048]{1,0:T(8,128)(2,1)S(1)} %bitcast.97, bf16[1024,1536]{1,0:T(8,128)(2,1)S(1)} %bitcast.76, bf16[1024,1536]{1,0:T(8,128)(2,1)S(1)} %bitcast.77, bf16[1024,512]{1,0:T(8,128)(2,1)S(1)} %bitcast.104), custom_call_target="tpu_custom_call" | custom-call | flops 4000000000 | bytes 1000000 | tf_op jit(solution)/shard_map/attn_grads/pallas_call | solution.py:470
  450.1 10.6 %attn_grads.3 = bf16[2048,1024]{1,0:T(8,128)(2,1)} custom-call(s32[4]{0:T(128)S(1)} %copy-done.45, bf16[1024,2048]{1,0:T(8,128)(2,1)} %bitcast.86, bf16[1024,2048]{1,0:T(8,128)(2,1)} %bitcast.98, bf16[1024,1536]{1,0:T(8,128)(2,1)} %bitcast.78, bf16[1024,1536]{1,0:T(8,128)(2,1)} %bitcast.79, bf16[1024,512]{1,0:T(8,128)(2,1)S(1)} %bitcast.105, ...), custom_call_target="tpu_custom_call" | custom-call | flops 1000000 | bytes 1000000 | tf_op jit(solution)/shard_map/attn_grads/pallas_call | solution.py:470
  461.6 6.3 %collective-permute-done.38.moved_ref = bf16[256,2048]{1,0:T(8,128)(2,1)} collective-permute-done((bf16[256,2048]{1,0:T(8,128)(2,1)}, bf16[256,2048]{1,0:T(8,128)(2,1)}, u32[]{:S(2)}, u32[]{:S(2)}) %collective-permute-start.38) | collective-permute-done | bytes 1048608 | tf_op jit(solution)/shard_map/ppermute | solution.py:650
  470.9 4.3 collective-permute-start.40
  494.3 4.6 whole_rows.2
  501.6 4.3 collective-permute-start.42
  512.7 6.3 %reduce-scatter.5.cloned.1.call-done = bf16[512,1024]{1,0:T(8,128)(2,1)} async-done(((bf16[2048,1024]{1,0:T(8,128)(2,1)}), bf16[512,1024]{1,0:T(8,128)(2,1)}) %reduce-scatter.5.cloned.1.call-update) | async-done | bytes 1048592 | tf_op jit(solution)/shard_map/reduce_scatter | solution.py:800
  (338 shorter events, 184.1 us)
Async XLA Ops:
  7.2 453.6 %reduce-scatter.3.cloned.1.call-start = ((), (), s32[]{:S(2)}) async-start(), calls=%async_computation.2 | async-start | bytes 10485760 | tf_op jit(solution)/shard_map/reduce_scatter | solution.py:772
  8.5 17.4 %collective-permute-start = (bf16[256,1024]{1,0:T(8,128)(2,1)S(1)}, bf16[256,1024]{1,0:T(8,128)(2,1)}, u32[]{:S(2)}, u32[]{:S(2)}) collective-permute-start(bf16[256,1024]{1,0:T(8,128)(2,1)S(1)} %get-tuple-element.291.xa_ref), channel_id=1, source_target_pairs={{0,3},{1,0},{2,1},{3,2},{4,7},{5,4},{6,5},{7,6},{8,11},{9,8},{10,9... | collective-permute-start | bytes 1572872 | tf_op jit(solution)/shard_map/ppermute | solution.py:650
  13.6 23.6 %collective-permute-start.2 = (bf16[256,1024]{1,0:T(8,128)(2,1)S(1)}, bf16[256,1024]{1,0:T(8,128)(2,1)S(1)}, u32[]{:S(2)}, u32[]{:S(2)}) collective-permute-start(bf16[256,1024]{1,0:T(8,128)(2,1)S(1)} %get-tuple-element.290.xb_ref), channel_id=1, source_target_pairs={{0,3},{1,0},{2,1},{3,2},{4,7},{5,4},{6,5},{7,6},{8,11},{9,8},{10,9... | collective-permute-start | bytes 1572872 | tf_op jit(solution)/shard_map/ppermute | solution.py:650
  26.0 22.7 %collective-permute-start.1 = (bf16[256,1024]{1,0:T(8,128)(2,1)}, bf16[256,1024]{1,0:T(8,128)(2,1)S(1)}, u32[]{:S(2)}, u32[]{:S(2)}) collective-permute-start(bf16[256,1024]{1,0:T(8,128)(2,1)} %collective-permute-done.xa_ref), channel_id=1, source_target_pairs={{0,3},{1,0},{2,1},{3,2},{4,7},{5,4},{6,5},{7,6},{8,11},{9,8},{10,9... | collective-permute-start | bytes 1572872 | tf_op jit(solution)/shard_map/ppermute | solution.py:650
  37.2 22.5 %collective-permute-start.4 = (bf16[256,1024]{1,0:T(8,128)(2,1)S(1)}, bf16[256,1024]{1,0:T(8,128)(2,1)S(1)}, u32[]{:S(2)}, u32[]{:S(2)}) collective-permute-start(bf16[256,1024]{1,0:T(8,128)(2,1)S(1)} %collective-permute-done.2.xb_ref), channel_id=1, source_target_pairs={{0,3},{1,0},{2,1},{3,2},{4,7},{5,4},{6,5},{7,6},{8,11},{9,8},{10,9... | collective-permute-start | bytes 1572872 | tf_op jit(solution)/shard_map/ppermute | solution.py:650
  48.6 23.2 %collective-permute-start.3 = (bf16[256,1024]{1,0:T(8,128)(2,1)S(1)}, bf16[256,1024]{1,0:T(8,128)(2,1)S(1)}, u32[]{:S(2)}, u32[]{:S(2)}) collective-permute-start(bf16[256,1024]{1,0:T(8,128)(2,1)S(1)} %collective-permute-done.1.xa_ref), channel_id=1, source_target_pairs={{0,3},{1,0},{2,1},{3,2},{4,7},{5,4},{6,5},{7,6},{8,11},{9,8},{10,9... | collective-permute-start | bytes 1572872 | tf_op jit(solution)/shard_map/ppermute | solution.py:650
  59.7 22.6 %collective-permute-start.5 = (bf16[256,1024]{1,0:T(8,128)(2,1)S(1)}, bf16[256,1024]{1,0:T(8,128)(2,1)S(1)}, u32[]{:S(2)}, u32[]{:S(2)}) collective-permute-start(bf16[256,1024]{1,0:T(8,128)(2,1)S(1)} %collective-permute-done.4.xb_ref), channel_id=1, source_target_pairs={{0,3},{1,0},{2,1},{3,2},{4,7},{5,4},{6,5},{7,6},{8,11},{9,8},{10,9... | collective-permute-start | bytes 1572872 | tf_op jit(solution)/shard_map/ppermute | solution.py:650
  71.9 33.6 %collective-permute-start.6 = (bf16[256,1024]{1,0:T(8,128)(2,1)S(1)}, bf16[256,1024]{1,0:T(8,128)(2,1)S(1)}, u32[]{:S(2)}, u32[]{:S(2)}) collective-permute-start(bf16[256,1024]{1,0:T(8,128)(2,1)S(1)} %get-tuple-element.288.gla_ref.gra_ref), channel_id=1, source_target_pairs={{0,1},{1,2},{2,3},{4,5},{5,6},{6,7},{8,9},{9,10},{10,11},{12,13},{... | collective-permute-start | bytes 1572872 | tf_op jit(solution)/shard_map/ppermute | solution.py:650
  73.4 43.3 %collective-permute-start.14 = (bf16[256,1024]{1,0:T(8,128)(2,1)S(1)}, bf16[256,1024]{1,0:T(8,128)(2,1)}, u32[]{:S(2)}, u32[]{:S(2)}) collective-permute-start(bf16[256,1024]{1,0:T(8,128)(2,1)S(1)} %get-tuple-element.288.gla_ref.gra_ref), channel_id=1, source_target_pairs={{1,0},{2,1},{3,2},{5,4},{6,5},{7,6},{9,8},{10,9},{11,10},{13,12},{... | collective-permute-start | bytes 1572872 | tf_op jit(solution)/shard_map/ppermute | solution.py:650
  74.7 35.6 %collective-permute-start.10 = (bf16[256,1024]{1,0:T(8,128)(2,1)S(1)}, bf16[256,1024]{1,0:T(8,128)(2,1)}, u32[]{:S(2)}, u32[]{:S(2)}) collective-permute-start(bf16[256,1024]{1,0:T(8,128)(2,1)S(1)} %get-tuple-element.289.glb_ref.grb_ref), channel_id=1, source_target_pairs={{0,1},{1,2},{2,3},{4,5},{5,6},{6,7},{8,9},{9,10},{10,11},{12,13},{... | collective-permute-start | bytes 1572872 | tf_op jit(solution)/shard_map/ppermute | solution.py:650
  80.0 39.6 %collective-permute-start.18 = (bf16[256,1024]{1,0:T(8,128)(2,1)S(1)}, bf16[256,1024]{1,0:T(8,128)(2,1)}, u32[]{:S(2)}, u32[]{:S(2)}) collective-permute-start(bf16[256,1024]{1,0:T(8,128)(2,1)S(1)} %get-tuple-element.289.glb_ref.grb_ref), channel_id=1, source_target_pairs={{1,0},{2,1},{3,2},{5,4},{6,5},{7,6},{9,8},{10,9},{11,10},{13,12},{... | collective-permute-start | bytes 1572872 | tf_op jit(solution)/shard_map/ppermute | solution.py:650
  112.0 21.9 %collective-permute-start.11 = (bf16[256,1024]{1,0:T(8,128)(2,1)S(1)}, bf16[256,1024]{1,0:T(8,128)(2,1)S(1)}, u32[]{:S(2)}, u32[]{:S(2)}) collective-permute-start(bf16[256,1024]{1,0:T(8,128)(2,1)S(1)} %join.23), channel_id=1, source_target_pairs={{0,1},{1,2},{2,3},{4,5},{5,6},{6,7},{8,9},{9,10},{10,11},{12,13},{... | collective-permute-start | bytes 1572872 | tf_op jit(solution)/shard_map/ppermute | solution.py:650
  118.3 21.1 %collective-permute-start.15 = (bf16[256,1024]{1,0:T(8,128)(2,1)S(1)}, bf16[256,1024]{1,0:T(8,128)(2,1)S(1)}, u32[]{:S(2)}, u32[]{:S(2)}) collective-permute-start(bf16[256,1024]{1,0:T(8,128)(2,1)S(1)} %join.26), channel_id=1, source_target_pairs={{1,0},{2,1},{3,2},{5,4},{6,5},{7,6},{9,8},{10,9},{11,10},{13,12},{... | collective-permute-start | bytes 1572872 | tf_op jit(solution)/shard_map/ppermute | solution.py:650
  121.2 25.8 %collective-permute-start.19 = (bf16[256,1024]{1,0:T(8,128)(2,1)S(1)}, bf16[256,1024]{1,0:T(8,128)(2,1)S(1)}, u32[]{:S(2)}, u32[]{:S(2)}) collective-permute-start(bf16[256,1024]{1,0:T(8,128)(2,1)S(1)} %join.29), channel_id=1, source_target_pairs={{1,0},{2,1},{3,2},{5,4},{6,5},{7,6},{9,8},{10,9},{11,10},{13,12},{... | collective-permute-start | bytes 1572872 | tf_op jit(solution)/shard_map/ppermute | solution.py:650
  123.5 25.8 %collective-permute-start.8 = (bf16[256,1024]{1,0:T(8,128)(2,1)S(1)}, bf16[256,1024]{1,0:T(8,128)(2,1)S(1)}, u32[]{:S(2)}, u32[]{:S(2)}) collective-permute-start(bf16[256,1024]{1,0:T(8,128)(2,1)S(1)} %join.21), channel_id=1, source_target_pairs={{0,1},{1,2},{2,3},{4,5},{5,6},{6,7},{8,9},{9,10},{10,11},{12,13},{... | collective-permute-start | bytes 1572872 | tf_op jit(solution)/shard_map/ppermute | solution.py:650
  134.7 21.7 %collective-permute-start.12 = (bf16[256,1024]{1,0:T(8,128)(2,1)S(1)}, bf16[256,1024]{1,0:T(8,128)(2,1)S(1)}, u32[]{:S(2)}, u32[]{:S(2)}) collective-permute-start(bf16[256,1024]{1,0:T(8,128)(2,1)S(1)} %join.24), channel_id=1, source_target_pairs={{0,1},{1,2},{2,3},{4,5},{5,6},{6,7},{8,9},{9,10},{10,11},{12,13},{... | collective-permute-start | bytes 1572872 | tf_op jit(solution)/shard_map/ppermute | solution.py:650
  140.2 21.6 %collective-permute-start.16 = (bf16[256,1024]{1,0:T(8,128)(2,1)S(1)}, bf16[256,1024]{1,0:T(8,128)(2,1)S(1)}, u32[]{:S(2)}, u32[]{:S(2)}) collective-permute-start(bf16[256,1024]{1,0:T(8,128)(2,1)S(1)} %join.27), channel_id=1, source_target_pairs={{1,0},{2,1},{3,2},{5,4},{6,5},{7,6},{9,8},{10,9},{11,10},{13,12},{... | collective-permute-start | bytes 1572872 | tf_op jit(solution)/shard_map/ppermute | solution.py:650
  147.9 21.6 %collective-permute-start.20 = (bf16[256,1024]{1,0:T(8,128)(2,1)S(1)}, bf16[256,1024]{1,0:T(8,128)(2,1)S(1)}, u32[]{:S(2)}, u32[]{:S(2)}) collective-permute-start(bf16[256,1024]{1,0:T(8,128)(2,1)S(1)} %join.30), channel_id=1, source_target_pairs={{1,0},{2,1},{3,2},{5,4},{6,5},{7,6},{9,8},{10,9},{11,10},{13,12},{... | collective-permute-start | bytes 1572872 | tf_op jit(solution)/shard_map/ppermute | solution.py:650
  150.1 24.5 %collective-permute-start.9 = (bf16[256,1024]{1,0:T(8,128)(2,1)S(1)}, bf16[256,1024]{1,0:T(8,128)(2,1)S(1)}, u32[]{:S(2)}, u32[]{:S(2)}) collective-permute-start(bf16[256,1024]{1,0:T(8,128)(2,1)S(1)} %join.22), channel_id=1, source_target_pairs={{0,1},{1,2},{2,3},{4,5},{5,6},{6,7},{8,9},{9,10},{10,11},{12,13},{... | collective-permute-start | bytes 1572872 | tf_op jit(solution)/shard_map/ppermute | solution.py:650
  157.2 18.3 %collective-permute-start.13 = (bf16[256,1024]{1,0:T(8,128)(2,1)S(1)}, bf16[256,1024]{1,0:T(8,128)(2,1)S(1)}, u32[]{:S(2)}, u32[]{:S(2)}) collective-permute-start(bf16[256,1024]{1,0:T(8,128)(2,1)S(1)} %join.25), channel_id=1, source_target_pairs={{0,1},{1,2},{2,3},{4,5},{5,6},{6,7},{8,9},{9,10},{10,11},{12,13},{... | collective-permute-start | bytes 1572872 | tf_op jit(solution)/shard_map/ppermute | solution.py:650
  162.7 18.1 %collective-permute-start.17 = (bf16[256,1024]{1,0:T(8,128)(2,1)S(1)}, bf16[256,1024]{1,0:T(8,128)(2,1)S(1)}, u32[]{:S(2)}, u32[]{:S(2)}) collective-permute-start(bf16[256,1024]{1,0:T(8,128)(2,1)S(1)} %join.28), channel_id=1, source_target_pairs={{1,0},{2,1},{3,2},{5,4},{6,5},{7,6},{9,8},{10,9},{11,10},{13,12},{... | collective-permute-start | bytes 1572872 | tf_op jit(solution)/shard_map/ppermute | solution.py:650
  170.3 17.5 %collective-permute-start.21 = (bf16[256,1024]{1,0:T(8,128)(2,1)S(1)}, bf16[256,1024]{1,0:T(8,128)(2,1)S(1)}, u32[]{:S(2)}, u32[]{:S(2)}) collective-permute-start(bf16[256,1024]{1,0:T(8,128)(2,1)S(1)} %join.31), channel_id=1, source_target_pairs={{1,0},{2,1},{3,2},{5,4},{6,5},{7,6},{9,8},{10,9},{11,10},{13,12},{... | collective-permute-start | bytes 1572872 | tf_op jit(solution)/shard_map/ppermute | solution.py:650
  189.9 23.5 %collective-permute-start.22 = (bf16[256,2048]{1,0:T(8,128)(2,1)S(1)}, bf16[256,2048]{1,0:T(8,128)(2,1)}, u32[]{:S(2)}, u32[]{:S(2)}) collective-permute-start(bf16[256,2048]{1,0:T(8,128)(2,1)S(1)} %add_convert_fusion.2.a_ref), channel_id=1, source_target_pairs={{0,3},{1,0},{2,1},{3,2},{4,7},{5,4},{6,5},{7,6},{8,11},{9,8},{10,9... | collective-permute-start | bytes 3145736 | tf_op jit(solution)/shard_map/ppermute | solution.py:650
  213.4 26.4 %collective-permute-start.23 = (bf16[256,2048]{1,0:T(8,128)(2,1)}, bf16[256,2048]{1,0:T(8,128)(2,1)}, u32[]{:S(2)}, u32[]{:S(2)}) collective-permute-start(bf16[256,2048]{1,0:T(8,128)(2,1)} %collective-permute-done.22.a_ref), channel_id=1, source_target_pairs={{0,3},{1,0},{2,1},{3,2},{4,7},{5,4},{6,5},{7,6},{8,11},{9,8},{10,9... | collective-permute-start | bytes 3145736 | tf_op jit(solution)/shard_map/ppermute | solution.py:650
  227.8 34.3 %collective-permute-start.25 = (bf16[256,2048]{1,0:T(8,128)(2,1)}, bf16[256,2048]{1,0:T(8,128)(2,1)S(1)}, u32[]{:S(2)}, u32[]{:S(2)}) collective-permute-start(bf16[256,2048]{1,0:T(8,128)(2,1)} %block_term.9), channel_id=1, source_target_pairs={{0,3},{1,0},{2,1},{3,2},{4,7},{5,4},{6,5},{7,6},{8,11},{9,8},{10,9... | collective-permute-start | bytes 3145736 | tf_op jit(solution)/shard_map/ppermute | solution.py:650
  239.8 44.8 %collective-permute-start.24 = (bf16[256,2048]{1,0:T(8,128)(2,1)}, bf16[256,2048]{1,0:T(8,128)(2,1)S(1)}, u32[]{:S(2)}, u32[]{:S(2)}) collective-permute-start(bf16[256,2048]{1,0:T(8,128)(2,1)} %collective-permute-done.23.a_ref), channel_id=1, source_target_pairs={{0,3},{1,0},{2,1},{3,2},{4,7},{5,4},{6,5},{7,6},{8,11},{9,8},{10,9... | collective-permute-start | bytes 3145736 | tf_op jit(solution)/shard_map/ppermute | solution.py:650
  262.6 38.6 %collective-permute-start.26 = (bf16[256,2048]{1,0:T(8,128)(2,1)S(1)}, bf16[256,2048]{1,0:T(8,128)(2,1)S(1)}, u32[]{:S(2)}, u32[]{:S(2)}) collective-permute-start(bf16[256,2048]{1,0:T(8,128)(2,1)S(1)} %add_convert_fusion.1), channel_id=1, source_target_pairs={{0,3},{1,0},{2,1},{3,2},{4,7},{5,4},{6,5},{7,6},{8,11},{9,8},{10,9... | collective-permute-start | bytes 3145736 | tf_op jit(solution)/shard_map/ppermute | solution.py:650
  304.3 19.4 %collective-permute-start.27 = (bf16[256,2048]{1,0:T(8,128)(2,1)S(1)}, bf16[256,2048]{1,0:T(8,128)(2,1)S(1)}, u32[]{:S(2)}, u32[]{:S(2)}) collective-permute-start(bf16[256,2048]{1,0:T(8,128)(2,1)S(1)} %block_term.11), channel_id=1, source_target_pairs={{0,3},{1,0},{2,1},{3,2},{4,7},{5,4},{6,5},{7,6},{8,11},{9,8},{10,9... | collective-permute-start | bytes 3145736 | tf_op jit(solution)/shard_map/ppermute | solution.py:650
  313.8 29.8 %collective-permute-start.29 = (bf16[2048,1024]{1,0:T(8,128)(2,1)}, bf16[2048,1024]{1,0:T(8,128)(2,1)}, u32[]{:S(2)}, u32[]{:S(2)}) collective-permute-start(bf16[2048,1024]{1,0:T(8,128)(2,1)} %grad_half.4), channel_id=1, source_target_pairs={{0,4},{4,0},{8,12},{12,8},{16,20},{20,16},{24,28},{28,24},{1,5},{5... | collective-permute-start | bytes 12582920 | tf_op jit(solution)/shard_map/ppermute | solution.py:671
  321.0 40.7 %collective-permute-start.32 = (bf16[2048,1024]{1,0:T(8,128)(2,1)}, bf16[2048,1024]{1,0:T(8,128)(2,1)}, u32[]{:S(2)}, u32[]{:S(2)}) collective-permute-start(bf16[2048,1024]{1,0:T(8,128)(2,1)} %grad_half.5), channel_id=1, source_target_pairs={{0,4},{4,0},{8,12},{12,8},{16,20},{20,16},{24,28},{28,24},{1,5},{5... | collective-permute-start | bytes 12582920 | tf_op jit(solution)/shard_map/ppermute | solution.py:671
  327.8 23.9 %collective-permute-start.28 = (bf16[256,2048]{1,0:T(8,128)(2,1)S(1)}, bf16[256,2048]{1,0:T(8,128)(2,1)S(1)}, u32[]{:S(2)}, u32[]{:S(2)}) collective-permute-start(bf16[256,2048]{1,0:T(8,128)(2,1)S(1)} %get-tuple-element.226.refs_0_), channel_id=1, source_target_pairs={{0,1},{1,2},{2,3},{4,5},{5,6},{6,7},{8,9},{9,10},{10,11},{12,13},{... | collective-permute-start | bytes 3145736 | tf_op jit(solution)/shard_map/ppermute | solution.py:650
  331.0 27.8 %collective-permute-start.31 = (bf16[256,2048]{1,0:T(8,128)(2,1)S(1)}, bf16[256,2048]{1,0:T(8,128)(2,1)S(1)}, u32[]{:S(2)}, u32[]{:S(2)}) collective-permute-start(bf16[256,2048]{1,0:T(8,128)(2,1)S(1)} %get-tuple-element.226.refs_0_), channel_id=1, source_target_pairs={{1,0},{2,1},{3,2},{5,4},{6,5},{7,6},{9,8},{10,9},{11,10},{13,12},{... | collective-permute-start | bytes 3145736 | tf_op jit(solution)/shard_map/ppermute | solution.py:650
  353.3 23.3 %collective-permute-start.30 = (bf16[256,2048]{1,0:T(8,128)(2,1)}, bf16[256,2048]{1,0:T(8,128)(2,1)}, u32[]{:S(2)}, u32[]{:S(2)}) collective-permute-start(bf16[256,2048]{1,0:T(8,128)(2,1)} %join.32), channel_id=1, source_target_pairs={{0,1},{1,2},{2,3},{4,5},{5,6},{6,7},{8,9},{9,10},{10,11},{12,13},{... | collective-permute-start | bytes 3145736 | tf_op jit(solution)/shard_map/ppermute | solution.py:650
  360.4 25.2 %collective-permute-start.35 = (bf16[256,2048]{1,0:T(8,128)(2,1)}, bf16[256,2048]{1,0:T(8,128)(2,1)}, u32[]{:S(2)}, u32[]{:S(2)}) collective-permute-start(bf16[256,2048]{1,0:T(8,128)(2,1)} %join.33), channel_id=1, source_target_pairs={{1,0},{2,1},{3,2},{5,4},{6,5},{7,6},{9,8},{10,9},{11,10},{13,12},{... | collective-permute-start | bytes 3145736 | tf_op jit(solution)/shard_map/ppermute | solution.py:650
  372.2 146.8 %reduce-scatter.5.cloned.1.call-start = ((), (), s32[]{:S(2)}) async-start(), calls=%async_computation.3 | async-start | bytes 5242880 | tf_op jit(solution)/shard_map/reduce_scatter | solution.py:800
  380.9 22.6 %collective-permute-start.33 = (bf16[256,2048]{1,0:T(8,128)(2,1)S(1)}, bf16[256,2048]{1,0:T(8,128)(2,1)S(1)}, u32[]{:S(2)}, u32[]{:S(2)}) collective-permute-start(bf16[256,2048]{1,0:T(8,128)(2,1)S(1)} %join.34), channel_id=1, source_target_pairs={{0,1},{1,2},{2,3},{4,5},{5,6},{6,7},{8,9},{9,10},{10,11},{12,13},{... | collective-permute-start | bytes 3145736 | tf_op jit(solution)/shard_map/ppermute | solution.py:650
  387.6 22.4 %collective-permute-start.36 = (bf16[256,2048]{1,0:T(8,128)(2,1)S(1)}, bf16[256,2048]{1,0:T(8,128)(2,1)S(1)}, u32[]{:S(2)}, u32[]{:S(2)}) collective-permute-start(bf16[256,2048]{1,0:T(8,128)(2,1)S(1)} %join.36), channel_id=1, source_target_pairs={{1,0},{2,1},{3,2},{5,4},{6,5},{7,6},{9,8},{10,9},{11,10},{13,12},{... | collective-permute-start | bytes 3145736 | tf_op jit(solution)/shard_map/ppermute | solution.py:650
  404.4 28.1 %collective-permute-start.34 = (bf16[256,2048]{1,0:T(8,128)(2,1)S(1)}, bf16[256,2048]{1,0:T(8,128)(2,1)S(1)}, u32[]{:S(2)}, u32[]{:S(2)}) collective-permute-start(bf16[256,2048]{1,0:T(8,128)(2,1)S(1)} %join.35), channel_id=1, source_target_pairs={{0,1},{1,2},{2,3},{4,5},{5,6},{6,7},{8,9},{9,10},{10,11},{12,13},{... | collective-permute-start | bytes 3145736 | tf_op jit(solution)/shard_map/ppermute | solution.py:650
  410.6 21.9 %collective-permute-start.37 = (bf16[256,2048]{1,0:T(8,128)(2,1)S(1)}, bf16[256,2048]{1,0:T(8,128)(2,1)S(1)}, u32[]{:S(2)}, u32[]{:S(2)}) collective-permute-start(bf16[256,2048]{1,0:T(8,128)(2,1)S(1)} %join.37), channel_id=1, source_target_pairs={{1,0},{2,1},{3,2},{5,4},{6,5},{7,6},{9,8},{10,9},{11,10},{13,12},{... | collective-permute-start | bytes 3145736 | tf_op jit(solution)/shard_map/ppermute | solution.py:650
  441.0 26.9 %collective-permute-start.38 = (bf16[256,2048]{1,0:T(8,128)(2,1)}, bf16[256,2048]{1,0:T(8,128)(2,1)}, u32[]{:S(2)}, u32[]{:S(2)}) collective-permute-start(bf16[256,2048]{1,0:T(8,128)(2,1)} %block_term.12), channel_id=1, source_target_pairs={{0,3},{1,0},{2,1},{3,2},{4,7},{5,4},{6,5},{7,6},{8,11},{9,8},{10,9... | collective-permute-start | bytes 3145736 | tf_op jit(solution)/shard_map/ppermute | solution.py:650
  470.9 28.1 %collective-permute-start.40 = (bf16[256,2048]{1,0:T(8,128)(2,1)}, bf16[256,2048]{1,0:T(8,128)(2,1)}, u32[]{:S(2)}, u32[]{:S(2)}) collective-permute-start(bf16[256,2048]{1,0:T(8,128)(2,1)} %join.38), channel_id=1, source_target_pairs={{0,3},{1,0},{2,1},{3,2},{4,7},{5,4},{6,5},{7,6},{8,11},{9,8},{10,9... | collective-permute-start | bytes 3145736 | tf_op jit(solution)/shard_map/ppermute | solution.py:650
  488.9 17.1 %collective-permute-start.45 = (f32[8320]{0:T(1024)S(1)}, f32[8320]{0:T(1024)S(1)}, u32[]{:S(2)}, u32[]{:S(2)}) collective-permute-start(f32[8320]{0:T(1024)S(1)} %add.128), channel_id=1, source_target_pairs={{0,1},{1,2},{2,3},{3,0},{4,5},{5,6},{6,7},{7,4},{8,9},{9,10},{10,1... | collective-permute-start | bytes 99848 | tf_op jit(solution)/shard_map/ppermute | solution.py:650
  488.9 17.1 %collective-permute-start.46 = (f32[8320]{0:T(1024)S(1)}, f32[8320]{0:T(1024)S(1)}, u32[]{:S(2)}, u32[]{:S(2)}) collective-permute-start(f32[8320]{0:T(1024)S(1)} %add.128), channel_id=1, source_target_pairs={{0,2},{1,3},{2,0},{3,1},{4,6},{5,7},{6,4},{7,5},{8,10},{9,11},{10,... | collective-permute-start | bytes 99848 | tf_op jit(solution)/shard_map/ppermute | solution.py:650
  489.3 16.7 %collective-permute-start.47 = (f32[8320]{0:T(1024)S(1)}, f32[8320]{0:T(1024)S(1)}, u32[]{:S(2)}, u32[]{:S(2)}) collective-permute-start(f32[8320]{0:T(1024)S(1)} %add.128), channel_id=1, source_target_pairs={{0,3},{1,0},{2,1},{3,2},{4,7},{5,4},{6,5},{7,6},{8,11},{9,8},{10,9... | collective-permute-start | bytes 99848 | tf_op jit(solution)/shard_map/ppermute | solution.py:650
  501.6 25.3 %collective-permute-start.42 = (bf16[256,2048]{1,0:T(8,128)(2,1)}, bf16[256,2048]{1,0:T(8,128)(2,1)S(1)}, u32[]{:S(2)}, u32[]{:S(2)}) collective-permute-start(bf16[256,2048]{1,0:T(8,128)(2,1)} %join.39), channel_id=1, source_target_pairs={{0,3},{1,0},{2,1},{3,2},{4,7},{5,4},{6,5},{7,6},{8,11},{9,8},{10,9... | collective-permute-start | bytes 3145736 | tf_op jit(solution)/shard_map/ppermute | solution.py:650
  506.0 23.8 %collective-permute-start.48 = (f32[8320]{0:T(1024)S(1)}, f32[8320]{0:T(1024)S(1)}, u32[]{:S(2)}, u32[]{:S(2)}) collective-permute-start(f32[8320]{0:T(1024)S(1)} %add_add_fusion.2), channel_id=1, source_target_pairs={{0,8},{4,12},{8,16},{12,20},{16,24},{20,28},{24,0},{28,4},{1,9},{5... | collective-permute-start | bytes 99848 | tf_op jit(solution)/shard_map/ppermute | solution.py:845
  509.6 20.1 %collective-permute-start.49 = (f32[8320]{0:T(1024)S(1)}, f32[8320]{0:T(1024)S(1)}, u32[]{:S(2)}, u32[]{:S(2)}) collective-permute-start(f32[8320]{0:T(1024)S(1)} %add_add_fusion.2), channel_id=1, source_target_pairs={{0,16},{4,20},{8,24},{12,28},{16,0},{20,4},{24,8},{28,12},{1,17},{... | collective-permute-start | bytes 99848 | tf_op jit(solution)/shard_map/ppermute | solution.py:845
  511.5 18.3 %collective-permute-start.50 = (f32[8320]{0:T(1024)S(1)}, f32[8320]{0:T(1024)S(1)}, u32[]{:S(2)}, u32[]{:S(2)}) collective-permute-start(f32[8320]{0:T(1024)S(1)} %add_add_fusion.2), channel_id=1, source_target_pairs={{0,24},{4,28},{8,0},{12,4},{16,8},{20,12},{24,16},{28,20},{1,25},{... | collective-permute-start | bytes 99848 | tf_op jit(solution)/shard_map/ppermute | solution.py:845
  (92 other events, 752.3 us)
Sparse Core Ops, SparseCore 0:
  372.4 87.8 reduce-scatter.2
  463.5 55.4 reduce-scatter.4

commit v14 on v12

--- a/solution.py
+++ b/solution.py
@@ -308,7 +308,10 @@
             in_specs=[
                 pl.BlockSpec((rows, d), whole),
             ]
-            + [pl.BlockSpec((rows, d // 2), whole)] * 4
+            + [
+                pl.BlockSpec((rows, d // 2), lambda j, r, c=p % 2 if g.shape[1] == d else 0: (0, c))
+                for p, g in enumerate(grads)
+            ]
             + [
                 wspec,
                 wspec,
@@ -515,16 +518,21 @@
         out_ref[...] = moved_ref[...]
 
 
-def join(rank, moved, terms, slot, first, right, part=0, flops=1e6):
-    rows, d = moved.shape
+def join(rank, moved, terms, slot, first, right, part=0, flops=1e6, width=None):
+    rows = moved.shape[0]
+    d = width or moved.shape[1]
     tile = min(128, rows)
+    at = part if moved.shape[1] > d else 0
     row = pl.BlockSpec((tile, d), lambda i, r: (i, 0))
     return pl.pallas_call(
         functools.partial(join_body, 0 if right else -1, first),
         grid_spec=pltpu.PrefetchScalarGridSpec(
             num_scalar_prefetch=1,
             grid=(rows // tile,),
-            in_specs=[row, pl.BlockSpec((1, tile, d), lambda i, r: (slot, i, part))],
+            in_specs=[
+                pl.BlockSpec((tile, d), lambda i, r: (i, at)),
+                pl.BlockSpec((1, tile, d), lambda i, r: (slot, i, part)),
+            ],
             out_specs=row,
         ),
         out_shape=jax.ShapeDtypeStruct((rows, d), BF16),
@@ -681,18 +689,16 @@
 
     grad_own = mixed_grad[0]
     (own_grad,) = tie([grad_own], block[0])
-    right = [own_grad[:, :half], own_grad[:, half:]]
-    left = list(right)
+    right, left = [own_grad] * 2, [own_grad] * 2
     grads_r, grads_l = [list(right)], [list(left)]
 
     def half_tick(k):
         for p in range(2):
-            if k:
-                right[p] = join(where, right[p], terms, n - k, k, True, p)
-                left[p] = join(where, left[p], terms, k, n - k, False, p)
+            right[p] = join(where, right[p], terms, n - k, k, True, p, width=half)
+            left[p] = join(where, left[p], terms, k, n - k, False, p, width=half)
             right[p], left[p] = send(right[p], right_line), send(left[p], left_line)
 
-    half_tick(0)
+    right, left = [send(own_grad, right_line)] * 2, [send(own_grad, left_line)] * 2
     masked = attend(where, query, keys, vals, docs_col, docs_row, heads_col)
     terms = low(dot_t(flat(masked), output_weight)).reshape(n, rows, d)
     for k in range(1, n):

time: 549 us -> 553 us (level)
    ppermute x42 -> x40, starting transfers between devices: 113 us -> 115 us  [per_device(): send = lambda v, pairs: lax.ppermute(v, 'mp', pairs)]
    ppermute x42 -> x40, waiting for transfers between devices: 124 us -> 125 us  [per_device(): send = lambda v, pairs: lax.ppermute(v, 'mp', pairs)]
    unnamed x173 -> x171, local copies, waits for them, and re-layouts: 23.6 us -> 23.3 us
  transfers between devices with their start and end apart: 53 -> 51, of which waited for: 27 -> 27; matrix products, arithmetic and copies ran while one was open for 7% -> 7% of each run, Pallas kernels for 38% -> 37%
where the time goes in v14:
time: 553 us; the launch traced here: 544 us
  Pallas kernels  207 us (37%)
  waiting for transfers between devices  135 us (24%)
  starting transfers between devices  120 us (22%)
  local copies, waits for them, and re-layouts  30.1 us (5%)
  other arithmetic  20.4 us (4%)
  between operations  15.9 us (3%)
  matrix products  15.6 us (3%)
    ppermute x40, waiting for transfers between devices, per_device(): send = lambda v, pairs: lax.ppermute(v, 'mp', pairs)  125 us
    ppermute x40, starting transfers between devices, per_device(): send = lambda v, pairs: lax.ppermute(v, 'mp', pairs)  115 us
    pallas_call x4, Pallas kernels, mlp_slot(): pl.pallas_call(functools.partial(mlp_body, slot, n), grid_spec=pltpu.Pref...  39.2 us
    pallas_call x4, Pallas kernels, grad_half(): pl.pallas_call(functools.partial(grad_body, not partner), grid_spec=pltpu...  29.6 us
    pallas_call x4, Pallas kernels, qkv_slot(): pl.pallas_call(qkv_body, grid_spec=pltpu.PrefetchScalarGridSpec(num_scala...  28.5 us
    pallas_call x20, Pallas kernels, join(): pl.pallas_call(functools.partial(join_body, 0 if right else -1, first), g...  26.6 us
    pallas_call x8, Pallas kernels, block_term(): pl.pallas_call(term_body, grid=(d // tile,), in_specs=[pl.BlockSpec((1, r...  23.8 us
    unnamed x171, local copies, waits for them, and re-layouts  23.3 us
  transfers between devices with their start and end apart: 51, of which 27 were waited for; matrix products, arithmetic and copies ran while one was open for 7% of the time, Pallas kernels for 37%

profile of v14, /device:TPU:0, one launch (start us, length us, event | category | flops | bytes accessed | tf_op | source)
XLA Modules:
  0.0 544.4 jit_solution(6765537531718644174)
XLA Ops:
  8.5 5.1 collective-permute-start
  17.9 7.1 %qkv_slot.4 = (bf16[4,256,2048]{2,1,0:T(8,128)(2,1)}, bf16[4,256,512]{2,1,0:T(8,128)(2,1)}, bf16[4,256,512]{2,1,0:T(8,128)(2,1)}, bf16[4,256,512]{2,1,0:T(8,128)(2,1)}) custom-call(s32[4]{0:T(128)} %pad_add_fusion.rank_ref, bf16[256,1024]{1,0:T(8,128)(2,1)} %copy-done.59, bf16[256,1024]{1,0:T(8,128)(2,1)} %copy-done.58, f32[1,2048]{1,0:T(1,128)} %bitcast.111, ...), custom_call_target="tpu_custom_call" | custom-call | flops 1610612736 | bytes 8388608 | tf_op jit(solution)/shard_map/qkv_slot/pallas_call | solution.py:106
  26.0 4.4 collective-permute-start.1
  30.3 6.8 %collective-permute-done.2.xb_ref = bf16[256,1024]{1,0:T(8,128)(2,1)S(1)} collective-permute-done((bf16[256,1024]{1,0:T(8,128)(2,1)S(1)}, bf16[256,1024]{1,0:T(8,128)(2,1)S(1)}, u32[]{:S(2)}, u32[]{:S(2)}) %collective-permute-start.2) | collective-permute-done | bytes 524320 | tf_op jit(solution)/shard_map/ppermute | solution.py:644
  37.2 4.3 collective-permute-start.4
  41.5 7.1 %qkv_slot.5 = (bf16[4,256,2048]{2,1,0:T(8,128)(2,1)}, bf16[4,256,512]{2,1,0:T(8,128)(2,1)}, bf16[4,256,512]{2,1,0:T(8,128)(2,1)}, bf16[4,256,512]{2,1,0:T(8,128)(2,1)}) custom-call(s32[4]{0:T(128)} %pad_add_fusion.rank_ref, ...), custom_call_target="tpu_custom_call", output_to_operand_aliasing={{0}: (10, {}), {1}: (11, {}), {2}: (12, {}), {3}: (13, {})} | custom-call | flops 1610612736 | bytes 8388608 | tf_op jit(solution)/shard_map/qkv_slot/pallas_call | solution.py:106
  52.8 6.9 %collective-permute-done.4.xb_ref = bf16[256,1024]{1,0:T(8,128)(2,1)S(1)} collective-permute-done((bf16[256,1024]{1,0:T(8,128)(2,1)S(1)}, bf16[256,1024]{1,0:T(8,128)(2,1)S(1)}, u32[]{:S(2)}, u32[]{:S(2)}) %collective-permute-start.4) | collective-permute-done | bytes 524320 | tf_op jit(solution)/shard_map/ppermute | solution.py:644
  59.7 4.3 collective-permute-start.5
  63.9 7.1 %qkv_slot.6 = (bf16[4,256,2048]{2,1,0:T(8,128)(2,1)}, bf16[4,256,512]{2,1,0:T(8,128)(2,1)}, bf16[4,256,512]{2,1,0:T(8,128)(2,1)}, bf16[4,256,512]{2,1,0:T(8,128)(2,1)}) custom-call(s32[4]{0:T(128)} %pad_add_fusion.rank_ref, bf16[256,1024]{1,0:T(8,128)(2,1)} %copy-done.65, ...), custom_call_target="tpu_custom_call", output_to_operand_aliasing={{0}: (10, {}), {1}: (11, {}), {2}: (12, {}), {3}: (13, {})} | custom-call | flops 1610612736 | bytes 8388608 | tf_op jit(solution)/shard_map/qkv_slot/pallas_call | solution.py:106
  83.0 7.1 %qkv_slot.7 = (bf16[4,256,2048]{2,1,0:T(8,128)(2,1)}, bf16[4,256,512]{2,1,0:T(8,128)(2,1)}, bf16[4,256,512]{2,1,0:T(8,128)(2,1)}, bf16[4,256,512]{2,1,0:T(8,128)(2,1)}) custom-call(s32[4]{0:T(128)} %pad_add_fusion.rank_ref, bf16[256,1024]{1,0:T(8,128)(2,1)} %copy-done.64, ...), custom_call_target="tpu_custom_call", output_to_operand_aliasing={{0}: (10, {}), {1}: (11, {}), {2}: (12, {}), {3}: (13, {})} | custom-call | flops 1610612736 | bytes 8388608 | tf_op jit(solution)/shard_map/qkv_slot/pallas_call | solution.py:106
  90.2 10.2 %attend.1 = bf16[4,256,512]{2,1,0:T(8,128)(2,1)} custom-call(s32[4]{0:T(128)} %pad_add_fusion.rank_ref, bf16[4,256,512]{2,1,0:T(8,128)(2,1)} %get-tuple-element.184.q_ref, bf16[4,256,512]{2,1,0:T(8,128)(2,1)} %get-tuple-element.185.k_ref, bf16[4,256,512]{2,1,0:T(8,128)(2,1)} %get-tuple-element.186.v_ref, s32[4,256,1]{2,1,0:T(8,128)} %reshape.204.dcol_ref, ...), custom_call_target="tpu_custom_call" | custom-call | flops 2147483648 | bytes 4194304 | tf_op jit(solution)/shard_map/attend/pallas_call | solution.py:169
  100.4 4.3 convolution_convert_fusion.1
  122.8 4.4 collective-permute-start.8
  127.3 6.0 %collective-permute-done.10.moved_ref.grb_ref = bf16[256,1024]{1,0:T(8,128)(2,1)S(1)} collective-permute-done((bf16[256,1024]{1,0:T(8,128)(2,1)S(1)}, bf16[256,1024]{1,0:T(8,128)(2,1)S(1)}, u32[]{:S(2)}, u32[]{:S(2)}) %collective-permute-start.10) | collective-permute-done | bytes 524320 | tf_op jit(solution)/shard_map/ppermute | solution.py:644
  134.1 4.4 collective-permute-start.11
  147.0 4.6 collective-permute-start.9
  156.5 4.4 collective-permute-start.12
  171.5 4.6 collective-permute-done.12
  178.7 9.0 %collective-permute-done.19 = bf16[256,1024]{1,0:T(8,128)(2,1)S(1)} collective-permute-done((bf16[256,1024]{1,0:T(8,128)(2,1)S(1)}, bf16[256,1024]{1,0:T(8,128)(2,1)S(1)}, u32[]{:S(2)}, u32[]{:S(2)}) %collective-permute-start.19) | collective-permute-done | bytes 524320 | tf_op jit(solution)/shard_map/ppermute | solution.py:644
  191.4 9.4 %mlp_slot.4 = (bf16[4,256,2048]{2,1,0:T(8,128)(2,1)S(1)}, bf16[4,256,2048]{2,1,0:T(8,128)(2,1)S(1)}, bf16[4,256,2048]{2,1,0:T(8,128)(2,1)S(1)}, bf16[4,256,2048]{2,1,0:T(8,128)(2,1)S(1)}) custom-call(s32[4]{0:T(128)S(1)} %copy-done.45, bf16[256,2048]{1,0:T(8,128)(2,1)S(1)} %add_convert_fusion.2.a_ref, bf16[256,2048]{1,0:T(8,128)(2,1)S(1)} %bitcast.99, ...), custom_call_target="tpu_custom_call" | custom-call | flops 4294967296 | bytes 20971520 | tf_op jit(solution)/shard_map/mlp_slot/pallas_call | solution.py:303
  208.2 5.1 collective-permute-done.20.a_ref
  215.3 9.9 %mlp_slot.5 = (bf16[4,256,2048]{2,1,0:T(8,128)(2,1)S(1)}, bf16[4,256,2048]{2,1,0:T(8,128)(2,1)S(1)}, bf16[4,256,2048]{2,1,0:T(8,128)(2,1)S(1)}, bf16[4,256,2048]{2,1,0:T(8,128)(2,1)S(1)}) custom-call(s32[4]{0:T(128)S(1)} %copy-done.45, ...), custom_call_target="tpu_custom_call", output_to_operand_aliasing={{0}: (9, {}), {1}: (10, {}), {2}: (11, {}), {3}: (12, {})} | custom-call | flops 4294967296 | bytes 20971520 | tf_op jit(solution)/shard_map/mlp_slot/pallas_call | solution.py:303
  229.3 10.4 %collective-permute-done.21.a_ref = bf16[256,2048]{1,0:T(8,128)(2,1)} collective-permute-done((bf16[256,2048]{1,0:T(8,128)(2,1)}, bf16[256,2048]{1,0:T(8,128)(2,1)}, u32[]{:S(2)}, u32[]{:S(2)}) %collective-permute-start.21) | collective-permute-done | bytes 1048608 | tf_op jit(solution)/shard_map/ppermute | solution.py:644
  243.5 9.6 %mlp_slot.6 = (bf16[4,256,2048]{2,1,0:T(8,128)(2,1)S(1)}, bf16[4,256,2048]{2,1,0:T(8,128)(2,1)S(1)}, bf16[4,256,2048]{2,1,0:T(8,128)(2,1)S(1)}, bf16[4,256,2048]{2,1,0:T(8,128)(2,1)S(1)}) custom-call(s32[4]{0:T(128)S(1)} %copy-done.45, ...), custom_call_target="tpu_custom_call", output_to_operand_aliasing={{0}: (9, {}), {1}: (10, {}), {2}: (11, {}), {3}: (12, {})} | custom-call | flops 4294967296 | bytes 20971520 | tf_op jit(solution)/shard_map/mlp_slot/pallas_call | solution.py:303
  256.2 5.8 %collective-permute-done.23 = bf16[256,2048]{1,0:T(8,128)(2,1)S(1)} collective-permute-done((bf16[256,2048]{1,0:T(8,128)(2,1)}, bf16[256,2048]{1,0:T(8,128)(2,1)S(1)}, u32[]{:S(2)}, u32[]{:S(2)}) %collective-permute-start.23) | collective-permute-done | bytes 1048608 | tf_op jit(solution)/shard_map/ppermute | solution.py:644
  266.3 18.2 %collective-permute-done.22.a_ref = bf16[256,2048]{1,0:T(8,128)(2,1)S(1)} collective-permute-done((bf16[256,2048]{1,0:T(8,128)(2,1)}, bf16[256,2048]{1,0:T(8,128)(2,1)S(1)}, u32[]{:S(2)}, u32[]{:S(2)}) %collective-permute-start.22) | collective-permute-done | bytes 1048608 | tf_op jit(solution)/shard_map/ppermute | solution.py:644
  284.5 10.3 %mlp_slot.7 = (bf16[4,256,2048]{2,1,0:T(8,128)(2,1)S(1)}, bf16[4,256,2048]{2,1,0:T(8,128)(2,1)S(1)}, bf16[4,256,2048]{2,1,0:T(8,128)(2,1)S(1)}, bf16[4,256,2048]{2,1,0:T(8,128)(2,1)S(1)}) custom-call(s32[4]{0:T(128)S(1)} %copy-done.45, ...), custom_call_target="tpu_custom_call", output_to_operand_aliasing={{0}: (9, {}), {1}: (10, {}), {2}: (11, {}), {3}: (12, {})} | custom-call | flops 4294967296 | bytes 20971520 | tf_op jit(solution)/shard_map/mlp_slot/pallas_call | solution.py:303
  294.8 8.1 %collective-permute-done.24.rest_0_ = bf16[256,2048]{1,0:T(8,128)(2,1)S(1)} collective-permute-done((bf16[256,2048]{1,0:T(8,128)(2,1)S(1)}, bf16[256,2048]{1,0:T(8,128)(2,1)S(1)}, u32[]{:S(2)}, u32[]{:S(2)}) %collective-permute-start.24) | collective-permute-done | bytes 1048608 | tf_op jit(solution)/shard_map/ppermute | solution.py:644
  310.1 7.2 %grad_half.4 = bf16[2048,1024]{1,0:T(8,128)(2,1)} custom-call(s32[4]{0:T(128)S(1)} %copy-done.45, bf16[1024,2048]{1,0:T(8,128)(2,1)S(1)} %bitcast.93, bf16[1024,2048]{1,0:T(8,128)(2,1)S(1)} %bitcast.88), custom_call_target="tpu_custom_call" | custom-call | flops 1000000 | bytes 1000000 | tf_op jit(solution)/shard_map/grad_half/pallas_call | solution.py:416
  317.3 7.2 %grad_half.5 = bf16[2048,1024]{1,0:T(8,128)(2,1)} custom-call(s32[4]{0:T(128)S(1)} %copy-done.45, bf16[1024,2048]{1,0:T(8,128)(2,1)S(1)} %bitcast.91, bf16[1024,2048]{1,0:T(8,128)(2,1)S(1)} %bitcast.72), custom_call_target="tpu_custom_call" | custom-call | flops 1000000 | bytes 1000000 | tf_op jit(solution)/shard_map/grad_half/pallas_call | solution.py:416
  335.5 11.3 %convolution_convert_fusion = bf16[1024,2048]{1,0:T(8,128)(2,1)S(1)} fusion(bf16[1024,2048]{1,0:T(8,128)(2,1)S(1)} %bitcast.89, bf16[2048,2048]{1,0:T(8,128)(2,1)} %down_ref.7), kind=kOutput, calls=%fused_computation | convolution fusion | flops 8592031744 | bytes 16777216 | tf_op jit(solution)/shard_map/dot_general | solution.py:53
  346.8 8.0 %grad_half.6.rest_1_ = bf16[2,2048,1024]{2,1,0:T(8,128)(2,1)S(1)} custom-call(s32[4]{0:T(128)S(1)} %copy-done.45, bf16[1024,2048]{1,0:T(8,128)(2,1)S(1)} %bitcast.94, bf16[1024,2048]{1,0:T(8,128)(2,1)S(1)} %bitcast.90, bf16[2048,1024]{1,0:T(8,128)(2,1)} %collective-permute-done.27.rest_0_), custom_call_target="tpu_custom_call" | custom-call | flops 1000000 | bytes 1000000 | tf_op jit(solution)/shard_map/grad_half/pallas_call | solution.py:416
  356.5 5.9 %collective-permute-start.28 = (bf16[256,2048]{1,0:T(8,128)(2,1)}, bf16[256,2048]{1,0:T(8,128)(2,1)}, u32[]{:S(2)}, u32[]{:S(2)}) collective-permute-start(bf16[256,2048]{1,0:T(8,128)(2,1)} %join.32), channel_id=1, source_target_pairs={{0,1},{1,2},{2,3},{4,5},{5,6},{6,7},{8,9},{9,10},{10,11},{12,13},{... | collective-permute-start | bytes 3145736 | tf_op jit(solution)/shard_map/ppermute | solution.py:644
  365.3 7.2 %grad_half.7 = bf16[2,2048,1024]{2,1,0:T(8,128)(2,1)S(1)} custom-call(s32[4]{0:T(128)S(1)} %copy-done.45, bf16[1024,2048]{1,0:T(8,128)(2,1)S(1)} %bitcast.92, bf16[1024,2048]{1,0:T(8,128)(2,1)S(1)} %bitcast.73, bf16[2048,1024]{1,0:T(8,128)(2,1)} %collective-permute-done.30.rest_0_, ...), custom_call_target="tpu_custom_call", output_to_operand_aliasing={{}: (4, {})} | custom-call | flops 1000000 | bytes 1000000 | tf_op jit(solution)/shard_map/grad_half/pallas_call | solution.py:416
  384.0 4.9 collective-permute-start.31
  392.2 4.3 dom_part.2
  396.5 10.2 %collective-permute-done.31.moved_ref.refs_1_ = bf16[256,2048]{1,0:T(8,128)(2,1)S(1)} collective-permute-done((bf16[256,2048]{1,0:T(8,128)(2,1)S(1)}, bf16[256,2048]{1,0:T(8,128)(2,1)S(1)}, u32[]{:S(2)}, u32[]{:S(2)}) %collective-permute-start.31) | collective-permute-done | bytes 1048608 | tf_op jit(solution)/shard_map/ppermute | solution.py:644
  407.6 4.5 collective-permute-start.32
  418.2 14.4 %attend_back.1.x_ref = bf16[4,256,1536]{2,1,0:T(8,128)(2,1)S(1)} custom-call(s32[4]{0:T(128)S(1)} %copy-done.45, bf16[4,256,512]{2,1,0:T(8,128)(2,1)S(1)} %copy-done.20, bf16[4,256,512]{2,1,0:T(8,128)(2,1)S(1)} %copy-done.21, bf16[4,256,512]{2,1,0:T(8,128)(2,1)S(1)} %copy-done.22, bf16[4,256,512]{2,1,0:T(8,128)(2,1)S(1)} %get-tuple-element.236.do_ref, ...), custom_call_target="tpu_custom_call" | custom-call | flops 115999997952 | bytes 7340032 | tf_op jit(solution)/shard_map/attend_back/pallas_call | solution.py:251
  437.1 7.4 %attn_grads.2 = bf16[2048,1024]{1,0:T(8,128)(2,1)S(1)} custom-call(s32[4]{0:T(128)S(1)} %copy-done.45, bf16[1024,2048]{1,0:T(8,128)(2,1)S(1)} %bitcast.85, bf16[1024,2048]{1,0:T(8,128)(2,1)S(1)} %bitcast.95, bf16[1024,1536]{1,0:T(8,128)(2,1)S(1)} %bitcast.74, bf16[1024,1536]{1,0:T(8,128)(2,1)S(1)} %bitcast.75, bf16[1024,512]{1,0:T(8,128)(2,1)S(1)} %bitcast.108), custom_call_target="tpu_custom_call" | custom-call | flops 4000000000 | bytes 1000000 | tf_op jit(solution)/shard_map/attn_grads/pallas_call | solution.py:459
  444.6 5.7 %collective-permute-start.36 = (bf16[256,2048]{1,0:T(8,128)(2,1)}, bf16[256,2048]{1,0:T(8,128)(2,1)}, u32[]{:S(2)}, u32[]{:S(2)}) collective-permute-start(bf16[256,2048]{1,0:T(8,128)(2,1)} %block_term.12), channel_id=1, source_target_pairs={{0,3},{1,0},{2,1},{3,2},{4,7},{5,4},{6,5},{7,6},{8,11},{9,8},{10,9... | collective-permute-start | bytes 3145736 | tf_op jit(solution)/shard_map/ppermute | solution.py:644
  454.8 10.7 %attn_grads.3 = bf16[2048,1024]{1,0:T(8,128)(2,1)} custom-call(s32[4]{0:T(128)S(1)} %copy-done.45, bf16[1024,2048]{1,0:T(8,128)(2,1)} %bitcast.84, bf16[1024,2048]{1,0:T(8,128)(2,1)} %bitcast.96, bf16[1024,1536]{1,0:T(8,128)(2,1)} %bitcast.76, bf16[1024,1536]{1,0:T(8,128)(2,1)} %bitcast.77, bf16[1024,512]{1,0:T(8,128)(2,1)S(1)} %bitcast.109, ...), custom_call_target="tpu_custom_call" | custom-call | flops 1000000 | bytes 1000000 | tf_op jit(solution)/shard_map/attn_grads/pallas_call | solution.py:459
  467.4 6.3 %collective-permute-done.36.moved_ref = bf16[256,2048]{1,0:T(8,128)(2,1)} collective-permute-done((bf16[256,2048]{1,0:T(8,128)(2,1)}, bf16[256,2048]{1,0:T(8,128)(2,1)}, u32[]{:S(2)}, u32[]{:S(2)}) %collective-permute-start.36) | collective-permute-done | bytes 1048608 | tf_op jit(solution)/shard_map/ppermute | solution.py:644
  476.6 4.5 collective-permute-start.38
  500.3 4.6 whole_rows.2
  507.7 4.3 collective-permute-start.40
  516.5 8.1 %reduce-scatter.5.cloned.1.call-done = bf16[512,1024]{1,0:T(8,128)(2,1)} async-done(((bf16[2048,1024]{1,0:T(8,128)(2,1)}), bf16[512,1024]{1,0:T(8,128)(2,1)}) %reduce-scatter.5.cloned.1.call-update) | async-done | bytes 1048592 | tf_op jit(solution)/shard_map/reduce_scatter | solution.py:791
  525.9 4.3 fusion.7
  (324 shorter events, 188.4 us)
Async XLA Ops:
  7.2 460.0 %reduce-scatter.3.cloned.1.call-start = ((), (), s32[]{:S(2)}) async-start(), calls=%async_computation.2 | async-start | bytes 10485760 | tf_op jit(solution)/shard_map/reduce_scatter | solution.py:763
  8.5 17.4 %collective-permute-start = (bf16[256,1024]{1,0:T(8,128)(2,1)S(1)}, bf16[256,1024]{1,0:T(8,128)(2,1)}, u32[]{:S(2)}, u32[]{:S(2)}) collective-permute-start(bf16[256,1024]{1,0:T(8,128)(2,1)S(1)} %get-tuple-element.289.xa_ref), channel_id=1, source_target_pairs={{0,3},{1,0},{2,1},{3,2},{4,7},{5,4},{6,5},{7,6},{8,11},{9,8},{10,9... | collective-permute-start | bytes 1572872 | tf_op jit(solution)/shard_map/ppermute | solution.py:644
  13.6 23.6 %collective-permute-start.2 = (bf16[256,1024]{1,0:T(8,128)(2,1)S(1)}, bf16[256,1024]{1,0:T(8,128)(2,1)S(1)}, u32[]{:S(2)}, u32[]{:S(2)}) collective-permute-start(bf16[256,1024]{1,0:T(8,128)(2,1)S(1)} %get-tuple-element.288.xb_ref), channel_id=1, source_target_pairs={{0,3},{1,0},{2,1},{3,2},{4,7},{5,4},{6,5},{7,6},{8,11},{9,8},{10,9... | collective-permute-start | bytes 1572872 | tf_op jit(solution)/shard_map/ppermute | solution.py:644
  26.0 22.7 %collective-permute-start.1 = (bf16[256,1024]{1,0:T(8,128)(2,1)}, bf16[256,1024]{1,0:T(8,128)(2,1)S(1)}, u32[]{:S(2)}, u32[]{:S(2)}) collective-permute-start(bf16[256,1024]{1,0:T(8,128)(2,1)} %collective-permute-done.xa_ref), channel_id=1, source_target_pairs={{0,3},{1,0},{2,1},{3,2},{4,7},{5,4},{6,5},{7,6},{8,11},{9,8},{10,9... | collective-permute-start | bytes 1572872 | tf_op jit(solution)/shard_map/ppermute | solution.py:644
  37.2 22.5 %collective-permute-start.4 = (bf16[256,1024]{1,0:T(8,128)(2,1)S(1)}, bf16[256,1024]{1,0:T(8,128)(2,1)S(1)}, u32[]{:S(2)}, u32[]{:S(2)}) collective-permute-start(bf16[256,1024]{1,0:T(8,128)(2,1)S(1)} %collective-permute-done.2.xb_ref), channel_id=1, source_target_pairs={{0,3},{1,0},{2,1},{3,2},{4,7},{5,4},{6,5},{7,6},{8,11},{9,8},{10,9... | collective-permute-start | bytes 1572872 | tf_op jit(solution)/shard_map/ppermute | solution.py:644
  48.7 22.4 %collective-permute-start.3 = (bf16[256,1024]{1,0:T(8,128)(2,1)S(1)}, bf16[256,1024]{1,0:T(8,128)(2,1)S(1)}, u32[]{:S(2)}, u32[]{:S(2)}) collective-permute-start(bf16[256,1024]{1,0:T(8,128)(2,1)S(1)} %collective-permute-done.1.xa_ref), channel_id=1, source_target_pairs={{0,3},{1,0},{2,1},{3,2},{4,7},{5,4},{6,5},{7,6},{8,11},{9,8},{10,9... | collective-permute-start | bytes 1572872 | tf_op jit(solution)/shard_map/ppermute | solution.py:644
  59.7 22.6 %collective-permute-start.5 = (bf16[256,1024]{1,0:T(8,128)(2,1)S(1)}, bf16[256,1024]{1,0:T(8,128)(2,1)S(1)}, u32[]{:S(2)}, u32[]{:S(2)}) collective-permute-start(bf16[256,1024]{1,0:T(8,128)(2,1)S(1)} %collective-permute-done.4.xb_ref), channel_id=1, source_target_pairs={{0,3},{1,0},{2,1},{3,2},{4,7},{5,4},{6,5},{7,6},{8,11},{9,8},{10,9... | collective-permute-start | bytes 1572872 | tf_op jit(solution)/shard_map/ppermute | solution.py:644
  71.1 33.6 %collective-permute-start.6 = (bf16[256,2048]{1,0:T(8,128)(2,1)S(1)}, bf16[256,2048]{1,0:T(8,128)(2,1)}, u32[]{:S(2)}, u32[]{:S(2)}) collective-permute-start(bf16[256,2048]{1,0:T(8,128)(2,1)S(1)} %bitcast.97), channel_id=1, source_target_pairs={{0,1},{1,2},{2,3},{4,5},{5,6},{6,7},{8,9},{9,10},{10,11},{12,13},{... | collective-permute-start | bytes 3145736 | tf_op jit(solution)/shard_map/ppermute | solution.py:644
  74.3 40.4 %collective-permute-start.13 = (bf16[256,2048]{1,0:T(8,128)(2,1)S(1)}, bf16[256,2048]{1,0:T(8,128)(2,1)}, u32[]{:S(2)}, u32[]{:S(2)}) collective-permute-start(bf16[256,2048]{1,0:T(8,128)(2,1)S(1)} %bitcast.98), channel_id=1, source_target_pairs={{1,0},{2,1},{3,2},{5,4},{6,5},{7,6},{9,8},{10,9},{11,10},{13,12},{... | collective-permute-start | bytes 3145736 | tf_op jit(solution)/shard_map/ppermute | solution.py:644
  106.4 15.6 %collective-permute-start.7 = (bf16[256,1024]{1,0:T(8,128)(2,1)S(1)}, bf16[256,1024]{1,0:T(8,128)(2,1)S(1)}, u32[]{:S(2)}, u32[]{:S(2)}) collective-permute-start(bf16[256,1024]{1,0:T(8,128)(2,1)S(1)} %join.20), channel_id=1, source_target_pairs={{0,1},{1,2},{2,3},{4,5},{5,6},{6,7},{8,9},{9,10},{10,11},{12,13},{... | collective-permute-start | bytes 1572872 | tf_op jit(solution)/shard_map/ppermute | solution.py:644
  111.4 21.9 %collective-permute-start.10 = (bf16[256,1024]{1,0:T(8,128)(2,1)S(1)}, bf16[256,1024]{1,0:T(8,128)(2,1)S(1)}, u32[]{:S(2)}, u32[]{:S(2)}) collective-permute-start(bf16[256,1024]{1,0:T(8,128)(2,1)S(1)} %join.23), channel_id=1, source_target_pairs={{0,1},{1,2},{2,3},{4,5},{5,6},{6,7},{8,9},{9,10},{10,11},{12,13},{... | collective-permute-start | bytes 1572872 | tf_op jit(solution)/shard_map/ppermute | solution.py:644
  116.3 22.2 %collective-permute-start.14 = (bf16[256,1024]{1,0:T(8,128)(2,1)S(1)}, bf16[256,1024]{1,0:T(8,128)(2,1)S(1)}, u32[]{:S(2)}, u32[]{:S(2)}) collective-permute-start(bf16[256,1024]{1,0:T(8,128)(2,1)S(1)} %join.26), channel_id=1, source_target_pairs={{1,0},{2,1},{3,2},{5,4},{6,5},{7,6},{9,8},{10,9},{11,10},{13,12},{... | collective-permute-start | bytes 1572872 | tf_op jit(solution)/shard_map/ppermute | solution.py:644
  119.2 24.7 %collective-permute-start.17 = (bf16[256,1024]{1,0:T(8,128)(2,1)S(1)}, bf16[256,1024]{1,0:T(8,128)(2,1)S(1)}, u32[]{:S(2)}, u32[]{:S(2)}) collective-permute-start(bf16[256,1024]{1,0:T(8,128)(2,1)S(1)} %join.29), channel_id=1, source_target_pairs={{1,0},{2,1},{3,2},{5,4},{6,5},{7,6},{9,8},{10,9},{11,10},{13,12},{... | collective-permute-start | bytes 1572872 | tf_op jit(solution)/shard_map/ppermute | solution.py:644
  122.8 23.3 %collective-permute-start.8 = (bf16[256,1024]{1,0:T(8,128)(2,1)S(1)}, bf16[256,1024]{1,0:T(8,128)(2,1)S(1)}, u32[]{:S(2)}, u32[]{:S(2)}) collective-permute-start(bf16[256,1024]{1,0:T(8,128)(2,1)S(1)} %join.21), channel_id=1, source_target_pairs={{0,1},{1,2},{2,3},{4,5},{5,6},{6,7},{8,9},{9,10},{10,11},{12,13},{... | collective-permute-start | bytes 1572872 | tf_op jit(solution)/shard_map/ppermute | solution.py:644
  134.1 21.7 %collective-permute-start.11 = (bf16[256,1024]{1,0:T(8,128)(2,1)S(1)}, bf16[256,1024]{1,0:T(8,128)(2,1)S(1)}, u32[]{:S(2)}, u32[]{:S(2)}) collective-permute-start(bf16[256,1024]{1,0:T(8,128)(2,1)S(1)} %join.24), channel_id=1, source_target_pairs={{0,1},{1,2},{2,3},{4,5},{5,6},{6,7},{8,9},{9,10},{10,11},{12,13},{... | collective-permute-start | bytes 1572872 | tf_op jit(solution)/shard_map/ppermute | solution.py:644
  139.3 21.7 %collective-permute-start.15 = (bf16[256,1024]{1,0:T(8,128)(2,1)S(1)}, bf16[256,1024]{1,0:T(8,128)(2,1)S(1)}, u32[]{:S(2)}, u32[]{:S(2)}) collective-permute-start(bf16[256,1024]{1,0:T(8,128)(2,1)S(1)} %join.27), channel_id=1, source_target_pairs={{1,0},{2,1},{3,2},{5,4},{6,5},{7,6},{9,8},{10,9},{11,10},{13,12},{... | collective-permute-start | bytes 1572872 | tf_op jit(solution)/shard_map/ppermute | solution.py:644
  144.7 21.6 %collective-permute-start.18 = (bf16[256,1024]{1,0:T(8,128)(2,1)S(1)}, bf16[256,1024]{1,0:T(8,128)(2,1)S(1)}, u32[]{:S(2)}, u32[]{:S(2)}) collective-permute-start(bf16[256,1024]{1,0:T(8,128)(2,1)S(1)} %join.30), channel_id=1, source_target_pairs={{1,0},{2,1},{3,2},{5,4},{6,5},{7,6},{9,8},{10,9},{11,10},{13,12},{... | collective-permute-start | bytes 1572872 | tf_op jit(solution)/shard_map/ppermute | solution.py:644
  147.0 24.5 %collective-permute-start.9 = (bf16[256,1024]{1,0:T(8,128)(2,1)S(1)}, bf16[256,1024]{1,0:T(8,128)(2,1)S(1)}, u32[]{:S(2)}, u32[]{:S(2)}) collective-permute-start(bf16[256,1024]{1,0:T(8,128)(2,1)S(1)} %join.22), channel_id=1, source_target_pairs={{0,1},{1,2},{2,3},{4,5},{5,6},{6,7},{8,9},{9,10},{10,11},{12,13},{... | collective-permute-start | bytes 1572872 | tf_op jit(solution)/shard_map/ppermute | solution.py:644
  156.5 19.6 %collective-permute-start.12 = (bf16[256,1024]{1,0:T(8,128)(2,1)S(1)}, bf16[256,1024]{1,0:T(8,128)(2,1)S(1)}, u32[]{:S(2)}, u32[]{:S(2)}) collective-permute-start(bf16[256,1024]{1,0:T(8,128)(2,1)S(1)} %join.25), channel_id=1, source_target_pairs={{0,1},{1,2},{2,3},{4,5},{5,6},{6,7},{8,9},{9,10},{10,11},{12,13},{... | collective-permute-start | bytes 1572872 | tf_op jit(solution)/shard_map/ppermute | solution.py:644
  161.8 16.9 %collective-permute-start.16 = (bf16[256,1024]{1,0:T(8,128)(2,1)S(1)}, bf16[256,1024]{1,0:T(8,128)(2,1)S(1)}, u32[]{:S(2)}, u32[]{:S(2)}) collective-permute-start(bf16[256,1024]{1,0:T(8,128)(2,1)S(1)} %join.28), channel_id=1, source_target_pairs={{1,0},{2,1},{3,2},{5,4},{6,5},{7,6},{9,8},{10,9},{11,10},{13,12},{... | collective-permute-start | bytes 1572872 | tf_op jit(solution)/shard_map/ppermute | solution.py:644
  167.1 20.5 %collective-permute-start.19 = (bf16[256,1024]{1,0:T(8,128)(2,1)S(1)}, bf16[256,1024]{1,0:T(8,128)(2,1)S(1)}, u32[]{:S(2)}, u32[]{:S(2)}) collective-permute-start(bf16[256,1024]{1,0:T(8,128)(2,1)S(1)} %join.31), channel_id=1, source_target_pairs={{1,0},{2,1},{3,2},{5,4},{6,5},{7,6},{9,8},{10,9},{11,10},{13,12},{... | collective-permute-start | bytes 1572872 | tf_op jit(solution)/shard_map/ppermute | solution.py:644
  189.8 23.5 %collective-permute-start.20 = (bf16[256,2048]{1,0:T(8,128)(2,1)S(1)}, bf16[256,2048]{1,0:T(8,128)(2,1)}, u32[]{:S(2)}, u32[]{:S(2)}) collective-permute-start(bf16[256,2048]{1,0:T(8,128)(2,1)S(1)} %add_convert_fusion.2.a_ref), channel_id=1, source_target_pairs={{0,3},{1,0},{2,1},{3,2},{4,7},{5,4},{6,5},{7,6},{8,11},{9,8},{10,9... | collective-permute-start | bytes 3145736 | tf_op jit(solution)/shard_map/ppermute | solution.py:644
  213.3 26.4 %collective-permute-start.21 = (bf16[256,2048]{1,0:T(8,128)(2,1)}, bf16[256,2048]{1,0:T(8,128)(2,1)}, u32[]{:S(2)}, u32[]{:S(2)}) collective-permute-start(bf16[256,2048]{1,0:T(8,128)(2,1)} %collective-permute-done.20.a_ref), channel_id=1, source_target_pairs={{0,3},{1,0},{2,1},{3,2},{4,7},{5,4},{6,5},{7,6},{8,11},{9,8},{10,9... | collective-permute-start | bytes 3145736 | tf_op jit(solution)/shard_map/ppermute | solution.py:644
  229.0 33.1 %collective-permute-start.23 = (bf16[256,2048]{1,0:T(8,128)(2,1)}, bf16[256,2048]{1,0:T(8,128)(2,1)S(1)}, u32[]{:S(2)}, u32[]{:S(2)}) collective-permute-start(bf16[256,2048]{1,0:T(8,128)(2,1)} %block_term.9), channel_id=1, source_target_pairs={{0,3},{1,0},{2,1},{3,2},{4,7},{5,4},{6,5},{7,6},{8,11},{9,8},{10,9... | collective-permute-start | bytes 3145736 | tf_op jit(solution)/shard_map/ppermute | solution.py:644
  239.7 44.8 %collective-permute-start.22 = (bf16[256,2048]{1,0:T(8,128)(2,1)}, bf16[256,2048]{1,0:T(8,128)(2,1)S(1)}, u32[]{:S(2)}, u32[]{:S(2)}) collective-permute-start(bf16[256,2048]{1,0:T(8,128)(2,1)} %collective-permute-done.21.a_ref), channel_id=1, source_target_pairs={{0,3},{1,0},{2,1},{3,2},{4,7},{5,4},{6,5},{7,6},{8,11},{9,8},{10,9... | collective-permute-start | bytes 3145736 | tf_op jit(solution)/shard_map/ppermute | solution.py:644
  262.4 40.5 %collective-permute-start.24 = (bf16[256,2048]{1,0:T(8,128)(2,1)S(1)}, bf16[256,2048]{1,0:T(8,128)(2,1)S(1)}, u32[]{:S(2)}, u32[]{:S(2)}) collective-permute-start(bf16[256,2048]{1,0:T(8,128)(2,1)S(1)} %add_convert_fusion.1), channel_id=1, source_target_pairs={{0,3},{1,0},{2,1},{3,2},{4,7},{5,4},{6,5},{7,6},{8,11},{9,8},{10,9... | collective-permute-start | bytes 3145736 | tf_op jit(solution)/shard_map/ppermute | solution.py:644
  306.1 22.6 %collective-permute-start.25 = (bf16[256,2048]{1,0:T(8,128)(2,1)S(1)}, bf16[256,2048]{1,0:T(8,128)(2,1)S(1)}, u32[]{:S(2)}, u32[]{:S(2)}) collective-permute-start(bf16[256,2048]{1,0:T(8,128)(2,1)S(1)} %block_term.11), channel_id=1, source_target_pairs={{0,3},{1,0},{2,1},{3,2},{4,7},{5,4},{6,5},{7,6},{8,11},{9,8},{10,9... | collective-permute-start | bytes 3145736 | tf_op jit(solution)/shard_map/ppermute | solution.py:644
  317.3 29.5 %collective-permute-start.27 = (bf16[2048,1024]{1,0:T(8,128)(2,1)}, bf16[2048,1024]{1,0:T(8,128)(2,1)}, u32[]{:S(2)}, u32[]{:S(2)}) collective-permute-start(bf16[2048,1024]{1,0:T(8,128)(2,1)} %grad_half.4), channel_id=1, source_target_pairs={{0,4},{4,0},{8,12},{12,8},{16,20},{20,16},{24,28},{28,24},{1,5},{5... | collective-permute-start | bytes 12582920 | tf_op jit(solution)/shard_map/ppermute | solution.py:665
  324.5 40.7 %collective-permute-start.30 = (bf16[2048,1024]{1,0:T(8,128)(2,1)}, bf16[2048,1024]{1,0:T(8,128)(2,1)}, u32[]{:S(2)}, u32[]{:S(2)}) collective-permute-start(bf16[2048,1024]{1,0:T(8,128)(2,1)} %grad_half.5), channel_id=1, source_target_pairs={{0,4},{4,0},{8,12},{12,8},{16,20},{20,16},{24,28},{28,24},{1,5},{5... | collective-permute-start | bytes 12582920 | tf_op jit(solution)/shard_map/ppermute | solution.py:665
  332.8 22.0 %collective-permute-start.26 = (bf16[256,2048]{1,0:T(8,128)(2,1)S(1)}, bf16[256,2048]{1,0:T(8,128)(2,1)S(1)}, u32[]{:S(2)}, u32[]{:S(2)}) collective-permute-start(bf16[256,2048]{1,0:T(8,128)(2,1)S(1)} %get-tuple-element.226.refs_0_), channel_id=1, source_target_pairs={{0,1},{1,2},{2,3},{4,5},{5,6},{6,7},{8,9},{9,10},{10,11},{12,13},{... | collective-permute-start | bytes 3145736 | tf_op jit(solution)/shard_map/ppermute | solution.py:644
  334.2 28.2 %collective-permute-start.29 = (bf16[256,2048]{1,0:T(8,128)(2,1)S(1)}, bf16[256,2048]{1,0:T(8,128)(2,1)S(1)}, u32[]{:S(2)}, u32[]{:S(2)}) collective-permute-start(bf16[256,2048]{1,0:T(8,128)(2,1)S(1)} %get-tuple-element.226.refs_0_), channel_id=1, source_target_pairs={{1,0},{2,1},{3,2},{5,4},{6,5},{7,6},{9,8},{10,9},{11,10},{13,12},{... | collective-permute-start | bytes 3145736 | tf_op jit(solution)/shard_map/ppermute | solution.py:644
  356.5 23.4 %collective-permute-start.28 = (bf16[256,2048]{1,0:T(8,128)(2,1)}, bf16[256,2048]{1,0:T(8,128)(2,1)}, u32[]{:S(2)}, u32[]{:S(2)}) collective-permute-start(bf16[256,2048]{1,0:T(8,128)(2,1)} %join.32), channel_id=1, source_target_pairs={{0,1},{1,2},{2,3},{4,5},{5,6},{6,7},{8,9},{9,10},{10,11},{12,13},{... | collective-permute-start | bytes 3145736 | tf_op jit(solution)/shard_map/ppermute | solution.py:644
  364.0 24.9 %collective-permute-start.33 = (bf16[256,2048]{1,0:T(8,128)(2,1)}, bf16[256,2048]{1,0:T(8,128)(2,1)}, u32[]{:S(2)}, u32[]{:S(2)}) collective-permute-start(bf16[256,2048]{1,0:T(8,128)(2,1)} %join.33), channel_id=1, source_target_pairs={{1,0},{2,1},{3,2},{5,4},{6,5},{7,6},{9,8},{10,9},{11,10},{13,12},{... | collective-permute-start | bytes 3145736 | tf_op jit(solution)/shard_map/ppermute | solution.py:644
  375.8 148.9 %reduce-scatter.5.cloned.1.call-start = ((), (), s32[]{:S(2)}) async-start(), calls=%async_computation.3 | async-start | bytes 5242880 | tf_op jit(solution)/shard_map/reduce_scatter | solution.py:791
  384.0 22.8 %collective-permute-start.31 = (bf16[256,2048]{1,0:T(8,128)(2,1)S(1)}, bf16[256,2048]{1,0:T(8,128)(2,1)S(1)}, u32[]{:S(2)}, u32[]{:S(2)}) collective-permute-start(bf16[256,2048]{1,0:T(8,128)(2,1)S(1)} %join.34), channel_id=1, source_target_pairs={{0,1},{1,2},{2,3},{4,5},{5,6},{6,7},{8,9},{9,10},{10,11},{12,13},{... | collective-permute-start | bytes 3145736 | tf_op jit(solution)/shard_map/ppermute | solution.py:644
  390.7 22.9 %collective-permute-start.34 = (bf16[256,2048]{1,0:T(8,128)(2,1)S(1)}, bf16[256,2048]{1,0:T(8,128)(2,1)S(1)}, u32[]{:S(2)}, u32[]{:S(2)}) collective-permute-start(bf16[256,2048]{1,0:T(8,128)(2,1)S(1)} %join.36), channel_id=1, source_target_pairs={{1,0},{2,1},{3,2},{5,4},{6,5},{7,6},{9,8},{10,9},{11,10},{13,12},{... | collective-permute-start | bytes 3145736 | tf_op jit(solution)/shard_map/ppermute | solution.py:644
  407.6 28.5 %collective-permute-start.32 = (bf16[256,2048]{1,0:T(8,128)(2,1)S(1)}, bf16[256,2048]{1,0:T(8,128)(2,1)S(1)}, u32[]{:S(2)}, u32[]{:S(2)}) collective-permute-start(bf16[256,2048]{1,0:T(8,128)(2,1)S(1)} %join.35), channel_id=1, source_target_pairs={{0,1},{1,2},{2,3},{4,5},{5,6},{6,7},{8,9},{9,10},{10,11},{12,13},{... | collective-permute-start | bytes 3145736 | tf_op jit(solution)/shard_map/ppermute | solution.py:644
  414.2 21.9 %collective-permute-start.35 = (bf16[256,2048]{1,0:T(8,128)(2,1)S(1)}, bf16[256,2048]{1,0:T(8,128)(2,1)S(1)}, u32[]{:S(2)}, u32[]{:S(2)}) collective-permute-start(bf16[256,2048]{1,0:T(8,128)(2,1)S(1)} %join.37), channel_id=1, source_target_pairs={{1,0},{2,1},{3,2},{5,4},{6,5},{7,6},{9,8},{10,9},{11,10},{13,12},{... | collective-permute-start | bytes 3145736 | tf_op jit(solution)/shard_map/ppermute | solution.py:644
  444.6 29.0 %collective-permute-start.36 = (bf16[256,2048]{1,0:T(8,128)(2,1)}, bf16[256,2048]{1,0:T(8,128)(2,1)}, u32[]{:S(2)}, u32[]{:S(2)}) collective-permute-start(bf16[256,2048]{1,0:T(8,128)(2,1)} %block_term.12), channel_id=1, source_target_pairs={{0,3},{1,0},{2,1},{3,2},{4,7},{5,4},{6,5},{7,6},{8,11},{9,8},{10,9... | collective-permute-start | bytes 3145736 | tf_op jit(solution)/shard_map/ppermute | solution.py:644
  476.6 28.3 %collective-permute-start.38 = (bf16[256,2048]{1,0:T(8,128)(2,1)}, bf16[256,2048]{1,0:T(8,128)(2,1)}, u32[]{:S(2)}, u32[]{:S(2)}) collective-permute-start(bf16[256,2048]{1,0:T(8,128)(2,1)} %join.38), channel_id=1, source_target_pairs={{0,3},{1,0},{2,1},{3,2},{4,7},{5,4},{6,5},{7,6},{8,11},{9,8},{10,9... | collective-permute-start | bytes 3145736 | tf_op jit(solution)/shard_map/ppermute | solution.py:644
  482.2 16.5 %collective-permute-start.39 = (bf16[2,256,1024]{2,1,0:T(8,128)(2,1)}, bf16[2,256,1024]{2,1,0:T(8,128)(2,1)}, u32[]{:S(2)}, u32[]{:S(2)}) collective-permute-start(bf16[2,256,1024]{2,1,0:T(8,128)(2,1)} %constant_dynamic-slice_fusion), channel_id=1, source_target_pairs={{0,4},{4,0},{8,12},{12,8},{16,20},{20,16},{24,28},{28,24},{1,5},{5... | collective-permute-start | bytes 3145736 | tf_op jit(solution)/shard_map/ppermute | solution.py:665
  494.8 17.2 %collective-permute-start.43 = (f32[8320]{0:T(1024)S(1)}, f32[8320]{0:T(1024)S(1)}, u32[]{:S(2)}, u32[]{:S(2)}) collective-permute-start(f32[8320]{0:T(1024)S(1)} %add.128), channel_id=1, source_target_pairs={{0,1},{1,2},{2,3},{3,0},{4,5},{5,6},{6,7},{7,4},{8,9},{9,10},{10,1... | collective-permute-start | bytes 99848 | tf_op jit(solution)/shard_map/ppermute | solution.py:644
  494.8 17.2 %collective-permute-start.44 = (f32[8320]{0:T(1024)S(1)}, f32[8320]{0:T(1024)S(1)}, u32[]{:S(2)}, u32[]{:S(2)}) collective-permute-start(f32[8320]{0:T(1024)S(1)} %add.128), channel_id=1, source_target_pairs={{0,2},{1,3},{2,0},{3,1},{4,6},{5,7},{6,4},{7,5},{8,10},{9,11},{10,... | collective-permute-start | bytes 99848 | tf_op jit(solution)/shard_map/ppermute | solution.py:644
  495.3 16.8 %collective-permute-start.45 = (f32[8320]{0:T(1024)S(1)}, f32[8320]{0:T(1024)S(1)}, u32[]{:S(2)}, u32[]{:S(2)}) collective-permute-start(f32[8320]{0:T(1024)S(1)} %add.128), channel_id=1, source_target_pairs={{0,3},{1,0},{2,1},{3,2},{4,7},{5,4},{6,5},{7,6},{8,11},{9,8},{10,9... | collective-permute-start | bytes 99848 | tf_op jit(solution)/shard_map/ppermute | solution.py:644
  507.7 24.9 %collective-permute-start.40 = (bf16[256,2048]{1,0:T(8,128)(2,1)}, bf16[256,2048]{1,0:T(8,128)(2,1)S(1)}, u32[]{:S(2)}, u32[]{:S(2)}) collective-permute-start(bf16[256,2048]{1,0:T(8,128)(2,1)} %join.39), channel_id=1, source_target_pairs={{0,3},{1,0},{2,1},{3,2},{4,7},{5,4},{6,5},{7,6},{8,11},{9,8},{10,9... | collective-permute-start | bytes 3145736 | tf_op jit(solution)/shard_map/ppermute | solution.py:644
  512.1 23.4 %collective-permute-start.46 = (f32[8320]{0:T(1024)S(1)}, f32[8320]{0:T(1024)S(1)}, u32[]{:S(2)}, u32[]{:S(2)}) collective-permute-start(f32[8320]{0:T(1024)S(1)} %add_add_fusion.2), channel_id=1, source_target_pairs={{0,8},{4,12},{8,16},{12,20},{16,24},{20,28},{24,0},{28,4},{1,9},{5... | collective-permute-start | bytes 99848 | tf_op jit(solution)/shard_map/ppermute | solution.py:836
  513.6 21.8 %collective-permute-start.47 = (f32[8320]{0:T(1024)S(1)}, f32[8320]{0:T(1024)S(1)}, u32[]{:S(2)}, u32[]{:S(2)}) collective-permute-start(f32[8320]{0:T(1024)S(1)} %add_add_fusion.2), channel_id=1, source_target_pairs={{0,16},{4,20},{8,24},{12,28},{16,0},{20,4},{24,8},{28,12},{1,17},{... | collective-permute-start | bytes 99848 | tf_op jit(solution)/shard_map/ppermute | solution.py:836
  514.9 20.5 %collective-permute-start.48 = (f32[8320]{0:T(1024)S(1)}, f32[8320]{0:T(1024)S(1)}, u32[]{:S(2)}, u32[]{:S(2)}) collective-permute-start(f32[8320]{0:T(1024)S(1)} %add_add_fusion.2), channel_id=1, source_target_pairs={{0,24},{4,28},{8,0},{12,4},{16,8},{20,12},{24,16},{28,20},{1,25},{... | collective-permute-start | bytes 99848 | tf_op jit(solution)/shard_map/ppermute | solution.py:836
  (87 other events, 721.8 us)
Sparse Core Ops, SparseCore 0:
  375.9 91.1 reduce-scatter.2
  470.4 54.2 reduce-scatter.4

commit v15 on v12

--- a/solution.py
+++ b/solution.py
@@ -517,7 +517,7 @@
 
 def join(rank, moved, terms, slot, first, right, part=0, flops=1e6):
     rows, d = moved.shape
-    tile = min(128, rows)
+    tile = min(256, rows)
     row = pl.BlockSpec((tile, d), lambda i, r: (i, 0))
     return pl.pallas_call(
         functools.partial(join_body, 0 if right else -1, first),
@@ -577,7 +577,7 @@
 
 def whole_rows(rank, part, got, widths):
     parts, span, half = got.shape
-    tile = min(64, span)
+    tile = min(128, span)
     steps = span // tile
     return pl.pallas_call(
         rows_body,

time: 549 us -> 549 us (level)
  transfers between devices with their start and end apart: 53 -> 53, of which waited for: 27 -> 27; matrix products, arithmetic and copies ran while one was open for 7% -> 7% of each run, Pallas kernels for 38% -> 37%
where the time goes in v15:
time: 549 us; the launch traced here: 540 us
  Pallas kernels  206 us (38%)
  waiting for transfers between devices  133 us (24%)
  starting transfers between devices  118 us (21%)
  local copies, waits for them, and re-layouts  31.2 us (6%)
  other arithmetic  20.5 us (4%)
  between operations  15.9 us (3%)
  matrix products  15.6 us (3%)
    ppermute x42, waiting for transfers between devices, per_device(): send = lambda v, pairs: lax.ppermute(v, 'mp', pairs)  126 us
    ppermute x42, starting transfers between devices, per_device(): send = lambda v, pairs: lax.ppermute(v, 'mp', pairs)  113 us
    pallas_call x4, Pallas kernels, mlp_slot(): pl.pallas_call(functools.partial(mlp_body, slot, n), grid_spec=pltpu.Pref...  39.3 us
    pallas_call x4, Pallas kernels, grad_half(): pl.pallas_call(functools.partial(grad_body, not partner), grid_spec=pltpu...  29.6 us
    pallas_call x4, Pallas kernels, qkv_slot(): pl.pallas_call(qkv_body, grid_spec=pltpu.PrefetchScalarGridSpec(num_scala...  28.7 us
    pallas_call x20, Pallas kernels, join(): pl.pallas_call(functools.partial(join_body, 0 if right else -1, first), g...  26.6 us
    unnamed x173, local copies, waits for them, and re-layouts  24.2 us
    pallas_call x8, Pallas kernels, block_term(): pl.pallas_call(term_body, grid=(d // tile,), in_specs=[pl.BlockSpec((1, r...  23.8 us
  transfers between devices with their start and end apart: 53, of which 27 were waited for; matrix products, arithmetic and copies ran while one was open for 7% of the time, Pallas kernels for 37%

profile of v15, /device:TPU:0, one launch (start us, length us, event | category | flops | bytes accessed | tf_op | source)
XLA Modules:
  0.0 539.9 jit_solution(14055605147052086288)
XLA Ops:
  8.5 5.1 collective-permute-start
  17.9 7.1 %qkv_slot.4 = (bf16[4,256,2048]{2,1,0:T(8,128)(2,1)}, bf16[4,256,512]{2,1,0:T(8,128)(2,1)}, bf16[4,256,512]{2,1,0:T(8,128)(2,1)}, bf16[4,256,512]{2,1,0:T(8,128)(2,1)}) custom-call(s32[4]{0:T(128)} %pad_add_fusion.rank_ref, bf16[256,1024]{1,0:T(8,128)(2,1)} %copy-done.61, bf16[256,1024]{1,0:T(8,128)(2,1)} %copy-done.60, f32[1,2048]{1,0:T(1,128)} %bitcast.105, ...), custom_call_target="tpu_custom_call" | custom-call | flops 1610612736 | bytes 8388608 | tf_op jit(solution)/shard_map/qkv_slot/pallas_call | solution.py:106
  26.0 4.4 collective-permute-start.1
  30.3 6.8 %collective-permute-done.2.xb_ref = bf16[256,1024]{1,0:T(8,128)(2,1)S(1)} collective-permute-done((bf16[256,1024]{1,0:T(8,128)(2,1)S(1)}, bf16[256,1024]{1,0:T(8,128)(2,1)S(1)}, u32[]{:S(2)}, u32[]{:S(2)}) %collective-permute-start.2) | collective-permute-done | bytes 524320 | tf_op jit(solution)/shard_map/ppermute | solution.py:636
  37.2 4.3 collective-permute-start.4
  41.5 7.1 %qkv_slot.5 = (bf16[4,256,2048]{2,1,0:T(8,128)(2,1)}, bf16[4,256,512]{2,1,0:T(8,128)(2,1)}, bf16[4,256,512]{2,1,0:T(8,128)(2,1)}, bf16[4,256,512]{2,1,0:T(8,128)(2,1)}) custom-call(s32[4]{0:T(128)} %pad_add_fusion.rank_ref, ...), custom_call_target="tpu_custom_call", output_to_operand_aliasing={{0}: (10, {}), {1}: (11, {}), {2}: (12, {}), {3}: (13, {})} | custom-call | flops 1610612736 | bytes 8388608 | tf_op jit(solution)/shard_map/qkv_slot/pallas_call | solution.py:106
  52.7 7.0 %collective-permute-done.4.xb_ref = bf16[256,1024]{1,0:T(8,128)(2,1)S(1)} collective-permute-done((bf16[256,1024]{1,0:T(8,128)(2,1)S(1)}, bf16[256,1024]{1,0:T(8,128)(2,1)S(1)}, u32[]{:S(2)}, u32[]{:S(2)}) %collective-permute-start.4) | collective-permute-done | bytes 524320 | tf_op jit(solution)/shard_map/ppermute | solution.py:636
  59.7 4.3 collective-permute-start.5
  68.1 7.3 %qkv_slot.6 = (bf16[4,256,2048]{2,1,0:T(8,128)(2,1)}, bf16[4,256,512]{2,1,0:T(8,128)(2,1)}, bf16[4,256,512]{2,1,0:T(8,128)(2,1)}, bf16[4,256,512]{2,1,0:T(8,128)(2,1)}) custom-call(s32[4]{0:T(128)} %pad_add_fusion.rank_ref, bf16[256,1024]{1,0:T(8,128)(2,1)} %copy-done.67, ...), custom_call_target="tpu_custom_call", output_to_operand_aliasing={{0}: (10, {}), {1}: (11, {}), {2}: (12, {}), {3}: (13, {})} | custom-call | flops 1610612736 | bytes 8388608 | tf_op jit(solution)/shard_map/qkv_slot/pallas_call | solution.py:106
  78.1 5.4 collective-permute-start.10
  85.0 7.2 %qkv_slot.7 = (bf16[4,256,2048]{2,1,0:T(8,128)(2,1)}, bf16[4,256,512]{2,1,0:T(8,128)(2,1)}, bf16[4,256,512]{2,1,0:T(8,128)(2,1)}, bf16[4,256,512]{2,1,0:T(8,128)(2,1)}) custom-call(s32[4]{0:T(128)} %pad_add_fusion.rank_ref, bf16[256,1024]{1,0:T(8,128)(2,1)} %copy-done.66, ...), custom_call_target="tpu_custom_call", output_to_operand_aliasing={{0}: (10, {}), {1}: (11, {}), {2}: (12, {}), {3}: (13, {})} | custom-call | flops 1610612736 | bytes 8388608 | tf_op jit(solution)/shard_map/qkv_slot/pallas_call | solution.py:106
  92.2 10.2 %attend.1 = bf16[4,256,512]{2,1,0:T(8,128)(2,1)} custom-call(s32[4]{0:T(128)} %pad_add_fusion.rank_ref, bf16[4,256,512]{2,1,0:T(8,128)(2,1)} %get-tuple-element.184.q_ref, bf16[4,256,512]{2,1,0:T(8,128)(2,1)} %get-tuple-element.185.k_ref, bf16[4,256,512]{2,1,0:T(8,128)(2,1)} %get-tuple-element.186.v_ref, s32[4,256,1]{2,1,0:T(8,128)} %reshape.204.dcol_ref, ...), custom_call_target="tpu_custom_call" | custom-call | flops 2147483648 | bytes 4194304 | tf_op jit(solution)/shard_map/attend/pallas_call | solution.py:169
  102.4 4.3 convolution_convert_fusion.1
  107.5 4.6 collective-permute-start.7
  125.2 4.4 collective-permute-start.8
  129.7 6.0 %collective-permute-done.11.moved_ref.grb_ref = bf16[256,1024]{1,0:T(8,128)(2,1)S(1)} collective-permute-done((bf16[256,1024]{1,0:T(8,128)(2,1)S(1)}, bf16[256,1024]{1,0:T(8,128)(2,1)S(1)}, u32[]{:S(2)}, u32[]{:S(2)}) %collective-permute-start.11) | collective-permute-done | bytes 524320 | tf_op jit(solution)/shard_map/ppermute | solution.py:636
  136.5 4.4 collective-permute-start.12
  147.8 5.3 collective-permute-start.9
  153.0 5.1 collective-permute-done.12.moved_ref.grb_ref
  158.9 4.4 collective-permute-start.13
  180.4 5.6 %collective-permute-done.21 = bf16[256,1024]{1,0:T(8,128)(2,1)S(1)} collective-permute-done((bf16[256,1024]{1,0:T(8,128)(2,1)S(1)}, bf16[256,1024]{1,0:T(8,128)(2,1)S(1)}, u32[]{:S(2)}, u32[]{:S(2)}) %collective-permute-start.21) | collective-permute-done | bytes 524320 | tf_op jit(solution)/shard_map/ppermute | solution.py:636
  190.4 9.3 %mlp_slot.4 = (bf16[4,256,2048]{2,1,0:T(8,128)(2,1)S(1)}, bf16[4,256,2048]{2,1,0:T(8,128)(2,1)S(1)}, bf16[4,256,2048]{2,1,0:T(8,128)(2,1)S(1)}, bf16[4,256,2048]{2,1,0:T(8,128)(2,1)S(1)}) custom-call(s32[4]{0:T(128)S(1)} %copy-done.45, bf16[256,2048]{1,0:T(8,128)(2,1)S(1)} %add_convert_fusion.2.a_ref, ...), custom_call_target="tpu_custom_call" | custom-call | flops 4294967296 | bytes 20971520 | tf_op jit(solution)/shard_map/mlp_slot/pallas_call | solution.py:303
  207.1 4.5 collective-permute-done.22.a_ref
  211.7 10.2 %mlp_slot.5 = (bf16[4,256,2048]{2,1,0:T(8,128)(2,1)S(1)}, bf16[4,256,2048]{2,1,0:T(8,128)(2,1)S(1)}, bf16[4,256,2048]{2,1,0:T(8,128)(2,1)S(1)}, bf16[4,256,2048]{2,1,0:T(8,128)(2,1)S(1)}) custom-call(s32[4]{0:T(128)S(1)} %copy-done.45, ...), custom_call_target="tpu_custom_call", output_to_operand_aliasing={{0}: (9, {}), {1}: (10, {}), {2}: (11, {}), {3}: (12, {})} | custom-call | flops 4294967296 | bytes 20971520 | tf_op jit(solution)/shard_map/mlp_slot/pallas_call | solution.py:303
  228.0 10.0 %collective-permute-done.23.a_ref = bf16[256,2048]{1,0:T(8,128)(2,1)} collective-permute-done((bf16[256,2048]{1,0:T(8,128)(2,1)}, bf16[256,2048]{1,0:T(8,128)(2,1)}, u32[]{:S(2)}, u32[]{:S(2)}) %collective-permute-start.23) | collective-permute-done | bytes 1048608 | tf_op jit(solution)/shard_map/ppermute | solution.py:636
  239.9 9.6 %mlp_slot.6 = (bf16[4,256,2048]{2,1,0:T(8,128)(2,1)S(1)}, bf16[4,256,2048]{2,1,0:T(8,128)(2,1)S(1)}, bf16[4,256,2048]{2,1,0:T(8,128)(2,1)S(1)}, bf16[4,256,2048]{2,1,0:T(8,128)(2,1)S(1)}) custom-call(s32[4]{0:T(128)S(1)} %copy-done.45, ...), custom_call_target="tpu_custom_call", output_to_operand_aliasing={{0}: (9, {}), {1}: (10, {}), {2}: (11, {}), {3}: (12, {})} | custom-call | flops 4294967296 | bytes 20971520 | tf_op jit(solution)/shard_map/mlp_slot/pallas_call | solution.py:303
  252.7 7.8 %collective-permute-done.25 = bf16[256,2048]{1,0:T(8,128)(2,1)S(1)} collective-permute-done((bf16[256,2048]{1,0:T(8,128)(2,1)}, bf16[256,2048]{1,0:T(8,128)(2,1)S(1)}, u32[]{:S(2)}, u32[]{:S(2)}) %collective-permute-start.25) | collective-permute-done | bytes 1048608 | tf_op jit(solution)/shard_map/ppermute | solution.py:636
  262.7 20.2 %collective-permute-done.24.a_ref = bf16[256,2048]{1,0:T(8,128)(2,1)S(1)} collective-permute-done((bf16[256,2048]{1,0:T(8,128)(2,1)}, bf16[256,2048]{1,0:T(8,128)(2,1)S(1)}, u32[]{:S(2)}, u32[]{:S(2)}) %collective-permute-start.24) | collective-permute-done | bytes 1048608 | tf_op jit(solution)/shard_map/ppermute | solution.py:636
  282.9 10.2 %mlp_slot.7 = (bf16[4,256,2048]{2,1,0:T(8,128)(2,1)S(1)}, bf16[4,256,2048]{2,1,0:T(8,128)(2,1)S(1)}, bf16[4,256,2048]{2,1,0:T(8,128)(2,1)S(1)}, bf16[4,256,2048]{2,1,0:T(8,128)(2,1)S(1)}) custom-call(s32[4]{0:T(128)S(1)} %copy-done.45, ...), custom_call_target="tpu_custom_call", output_to_operand_aliasing={{0}: (9, {}), {1}: (10, {}), {2}: (11, {}), {3}: (12, {})} | custom-call | flops 4294967296 | bytes 20971520 | tf_op jit(solution)/shard_map/mlp_slot/pallas_call | solution.py:303
  293.1 6.1 %collective-permute-done.26.rest_0_ = bf16[256,2048]{1,0:T(8,128)(2,1)S(1)} collective-permute-done((bf16[256,2048]{1,0:T(8,128)(2,1)S(1)}, bf16[256,2048]{1,0:T(8,128)(2,1)S(1)}, u32[]{:S(2)}, u32[]{:S(2)}) %collective-permute-start.26) | collective-permute-done | bytes 1048608 | tf_op jit(solution)/shard_map/ppermute | solution.py:636
  302.8 7.2 %grad_half.4 = bf16[2048,1024]{1,0:T(8,128)(2,1)} custom-call(s32[4]{0:T(128)S(1)} %copy-done.45, bf16[1024,2048]{1,0:T(8,128)(2,1)S(1)} %bitcast.93, bf16[1024,2048]{1,0:T(8,128)(2,1)S(1)} %bitcast.88), custom_call_target="tpu_custom_call" | custom-call | flops 1000000 | bytes 1000000 | tf_op jit(solution)/shard_map/grad_half/pallas_call | solution.py:413
  310.0 7.2 %grad_half.5 = bf16[2048,1024]{1,0:T(8,128)(2,1)} custom-call(s32[4]{0:T(128)S(1)} %copy-done.45, bf16[1024,2048]{1,0:T(8,128)(2,1)S(1)} %bitcast.91, bf16[1024,2048]{1,0:T(8,128)(2,1)S(1)} %bitcast.72), custom_call_target="tpu_custom_call" | custom-call | flops 1000000 | bytes 1000000 | tf_op jit(solution)/shard_map/grad_half/pallas_call | solution.py:413
  330.2 11.3 %convolution_convert_fusion = bf16[1024,2048]{1,0:T(8,128)(2,1)S(1)} fusion(bf16[1024,2048]{1,0:T(8,128)(2,1)S(1)} %bitcast.89, bf16[2048,2048]{1,0:T(8,128)(2,1)} %down_ref.7), kind=kOutput, calls=%fused_computation | convolution fusion | flops 8592031744 | bytes 16777216 | tf_op jit(solution)/shard_map/dot_general | solution.py:53
  341.5 8.0 %grad_half.6.rest_1_ = bf16[2,2048,1024]{2,1,0:T(8,128)(2,1)S(1)} custom-call(s32[4]{0:T(128)S(1)} %copy-done.45, bf16[1024,2048]{1,0:T(8,128)(2,1)S(1)} %bitcast.94, bf16[1024,2048]{1,0:T(8,128)(2,1)S(1)} %bitcast.90, bf16[2048,1024]{1,0:T(8,128)(2,1)} %collective-permute-done.29.rest_0_), custom_call_target="tpu_custom_call" | custom-call | flops 1000000 | bytes 1000000 | tf_op jit(solution)/shard_map/grad_half/pallas_call | solution.py:413
  351.3 5.4 collective-permute-start.30
  359.6 7.2 %grad_half.7 = bf16[2,2048,1024]{2,1,0:T(8,128)(2,1)S(1)} custom-call(s32[4]{0:T(128)S(1)} %copy-done.45, bf16[1024,2048]{1,0:T(8,128)(2,1)S(1)} %bitcast.92, bf16[1024,2048]{1,0:T(8,128)(2,1)S(1)} %bitcast.73, bf16[2048,1024]{1,0:T(8,128)(2,1)} %collective-permute-done.32.rest_0_, ...), custom_call_target="tpu_custom_call", output_to_operand_aliasing={{}: (4, {})} | custom-call | flops 1000000 | bytes 1000000 | tf_op jit(solution)/shard_map/grad_half/pallas_call | solution.py:413
  370.2 4.5 collective-permute-done.30.moved_ref.refs_2_
  378.9 5.2 collective-permute-start.33
  391.6 10.6 %collective-permute-done.33.moved_ref.refs_1_ = bf16[256,2048]{1,0:T(8,128)(2,1)S(1)} collective-permute-done((bf16[256,2048]{1,0:T(8,128)(2,1)S(1)}, bf16[256,2048]{1,0:T(8,128)(2,1)S(1)}, u32[]{:S(2)}, u32[]{:S(2)}) %collective-permute-start.33) | collective-permute-done | bytes 1048608 | tf_op jit(solution)/shard_map/ppermute | solution.py:636
  403.0 4.5 collective-permute-start.34
  413.5 14.5 %attend_back.1.x_ref = bf16[4,256,1536]{2,1,0:T(8,128)(2,1)S(1)} custom-call(s32[4]{0:T(128)S(1)} %copy-done.45, bf16[4,256,512]{2,1,0:T(8,128)(2,1)S(1)} %copy-done.18, bf16[4,256,512]{2,1,0:T(8,128)(2,1)S(1)} %copy-done.19, bf16[4,256,512]{2,1,0:T(8,128)(2,1)S(1)} %copy-done.20, bf16[4,256,512]{2,1,0:T(8,128)(2,1)S(1)} %get-tuple-element.236.do_ref, ...), custom_call_target="tpu_custom_call" | custom-call | flops 115999997952 | bytes 7340032 | tf_op jit(solution)/shard_map/attend_back/pallas_call | solution.py:251
  433.2 7.4 %attn_grads.2 = bf16[2048,1024]{1,0:T(8,128)(2,1)S(1)} custom-call(s32[4]{0:T(128)S(1)} %copy-done.45, bf16[1024,2048]{1,0:T(8,128)(2,1)S(1)} %bitcast.85, bf16[1024,2048]{1,0:T(8,128)(2,1)S(1)} %bitcast.95, bf16[1024,1536]{1,0:T(8,128)(2,1)S(1)} %bitcast.74, bf16[1024,1536]{1,0:T(8,128)(2,1)S(1)} %bitcast.75, bf16[1024,512]{1,0:T(8,128)(2,1)S(1)} %bitcast.102), custom_call_target="tpu_custom_call" | custom-call | flops 4000000000 | bytes 1000000 | tf_op jit(solution)/shard_map/attn_grads/pallas_call | solution.py:456
  449.8 10.6 %attn_grads.3 = bf16[2048,1024]{1,0:T(8,128)(2,1)} custom-call(s32[4]{0:T(128)S(1)} %copy-done.45, bf16[1024,2048]{1,0:T(8,128)(2,1)} %bitcast.84, bf16[1024,2048]{1,0:T(8,128)(2,1)} %bitcast.96, bf16[1024,1536]{1,0:T(8,128)(2,1)} %bitcast.76, bf16[1024,1536]{1,0:T(8,128)(2,1)} %bitcast.77, bf16[1024,512]{1,0:T(8,128)(2,1)S(1)} %bitcast.103, ...), custom_call_target="tpu_custom_call" | custom-call | flops 1000000 | bytes 1000000 | tf_op jit(solution)/shard_map/attn_grads/pallas_call | solution.py:456
  461.3 6.5 %collective-permute-done.38.moved_ref = bf16[256,2048]{1,0:T(8,128)(2,1)} collective-permute-done((bf16[256,2048]{1,0:T(8,128)(2,1)}, bf16[256,2048]{1,0:T(8,128)(2,1)}, u32[]{:S(2)}, u32[]{:S(2)}) %collective-permute-start.38) | collective-permute-done | bytes 1048608 | tf_op jit(solution)/shard_map/ppermute | solution.py:636
  471.8 4.3 collective-permute-start.40
  503.0 4.3 collective-permute-start.42
  511.8 4.9 reduce-scatter.5.cloned.1.call-done
  517.9 4.3 fusion.7
  (331 shorter events, 188.0 us)
Async XLA Ops:
  7.2 453.2 %reduce-scatter.3.cloned.1.call-start = ((), (), s32[]{:S(2)}) async-start(), calls=%async_computation.2 | async-start | bytes 10485760 | tf_op jit(solution)/shard_map/reduce_scatter | solution.py:757
  8.5 17.4 %collective-permute-start = (bf16[256,1024]{1,0:T(8,128)(2,1)S(1)}, bf16[256,1024]{1,0:T(8,128)(2,1)}, u32[]{:S(2)}, u32[]{:S(2)}) collective-permute-start(bf16[256,1024]{1,0:T(8,128)(2,1)S(1)} %get-tuple-element.291.xa_ref), channel_id=1, source_target_pairs={{0,3},{1,0},{2,1},{3,2},{4,7},{5,4},{6,5},{7,6},{8,11},{9,8},{10,9... | collective-permute-start | bytes 1572872 | tf_op jit(solution)/shard_map/ppermute | solution.py:636
  13.6 23.6 %collective-permute-start.2 = (bf16[256,1024]{1,0:T(8,128)(2,1)S(1)}, bf16[256,1024]{1,0:T(8,128)(2,1)S(1)}, u32[]{:S(2)}, u32[]{:S(2)}) collective-permute-start(bf16[256,1024]{1,0:T(8,128)(2,1)S(1)} %get-tuple-element.290.xb_ref), channel_id=1, source_target_pairs={{0,3},{1,0},{2,1},{3,2},{4,7},{5,4},{6,5},{7,6},{8,11},{9,8},{10,9... | collective-permute-start | bytes 1572872 | tf_op jit(solution)/shard_map/ppermute | solution.py:636
  26.0 22.7 %collective-permute-start.1 = (bf16[256,1024]{1,0:T(8,128)(2,1)}, bf16[256,1024]{1,0:T(8,128)(2,1)S(1)}, u32[]{:S(2)}, u32[]{:S(2)}) collective-permute-start(bf16[256,1024]{1,0:T(8,128)(2,1)} %collective-permute-done.xa_ref), channel_id=1, source_target_pairs={{0,3},{1,0},{2,1},{3,2},{4,7},{5,4},{6,5},{7,6},{8,11},{9,8},{10,9... | collective-permute-start | bytes 1572872 | tf_op jit(solution)/shard_map/ppermute | solution.py:636
  37.2 22.5 %collective-permute-start.4 = (bf16[256,1024]{1,0:T(8,128)(2,1)S(1)}, bf16[256,1024]{1,0:T(8,128)(2,1)S(1)}, u32[]{:S(2)}, u32[]{:S(2)}) collective-permute-start(bf16[256,1024]{1,0:T(8,128)(2,1)S(1)} %collective-permute-done.2.xb_ref), channel_id=1, source_target_pairs={{0,3},{1,0},{2,1},{3,2},{4,7},{5,4},{6,5},{7,6},{8,11},{9,8},{10,9... | collective-permute-start | bytes 1572872 | tf_op jit(solution)/shard_map/ppermute | solution.py:636
  48.6 26.8 %collective-permute-start.3 = (bf16[256,1024]{1,0:T(8,128)(2,1)S(1)}, bf16[256,1024]{1,0:T(8,128)(2,1)S(1)}, u32[]{:S(2)}, u32[]{:S(2)}) collective-permute-start(bf16[256,1024]{1,0:T(8,128)(2,1)S(1)} %collective-permute-done.1.xa_ref), channel_id=1, source_target_pairs={{0,3},{1,0},{2,1},{3,2},{4,7},{5,4},{6,5},{7,6},{8,11},{9,8},{10,9... | collective-permute-start | bytes 1572872 | tf_op jit(solution)/shard_map/ppermute | solution.py:636
  59.7 25.3 %collective-permute-start.5 = (bf16[256,1024]{1,0:T(8,128)(2,1)S(1)}, bf16[256,1024]{1,0:T(8,128)(2,1)}, u32[]{:S(2)}, u32[]{:S(2)}) collective-permute-start(bf16[256,1024]{1,0:T(8,128)(2,1)S(1)} %collective-permute-done.4.xb_ref), channel_id=1, source_target_pairs={{0,3},{1,0},{2,1},{3,2},{4,7},{5,4},{6,5},{7,6},{8,11},{9,8},{10,9... | collective-permute-start | bytes 1572872 | tf_op jit(solution)/shard_map/ppermute | solution.py:636
  75.5 31.2 %collective-permute-start.6 = (bf16[256,1024]{1,0:T(8,128)(2,1)S(1)}, bf16[256,1024]{1,0:T(8,128)(2,1)S(1)}, u32[]{:S(2)}, u32[]{:S(2)}) collective-permute-start(bf16[256,1024]{1,0:T(8,128)(2,1)S(1)} %get-tuple-element.288.gla_ref.gra_ref), channel_id=1, source_target_pairs={{0,1},{1,2},{2,3},{4,5},{5,6},{6,7},{8,9},{9,10},{10,11},{12,13},{... | collective-permute-start | bytes 1572872 | tf_op jit(solution)/shard_map/ppermute | solution.py:636
  76.8 38.9 %collective-permute-start.14 = (bf16[256,1024]{1,0:T(8,128)(2,1)S(1)}, bf16[256,1024]{1,0:T(8,128)(2,1)}, u32[]{:S(2)}, u32[]{:S(2)}) collective-permute-start(bf16[256,1024]{1,0:T(8,128)(2,1)S(1)} %get-tuple-element.288.gla_ref.gra_ref), channel_id=1, source_target_pairs={{1,0},{2,1},{3,2},{5,4},{6,5},{7,6},{9,8},{10,9},{11,10},{13,12},{... | collective-permute-start | bytes 1572872 | tf_op jit(solution)/shard_map/ppermute | solution.py:636
  78.1 34.0 %collective-permute-start.10 = (bf16[256,1024]{1,0:T(8,128)(2,1)S(1)}, bf16[256,1024]{1,0:T(8,128)(2,1)}, u32[]{:S(2)}, u32[]{:S(2)}) collective-permute-start(bf16[256,1024]{1,0:T(8,128)(2,1)S(1)} %get-tuple-element.289.glb_ref.grb_ref), channel_id=1, source_target_pairs={{0,1},{1,2},{2,3},{4,5},{5,6},{6,7},{8,9},{9,10},{10,11},{12,13},{... | collective-permute-start | bytes 1572872 | tf_op jit(solution)/shard_map/ppermute | solution.py:636
  83.5 35.1 %collective-permute-start.18 = (bf16[256,1024]{1,0:T(8,128)(2,1)S(1)}, bf16[256,1024]{1,0:T(8,128)(2,1)}, u32[]{:S(2)}, u32[]{:S(2)}) collective-permute-start(bf16[256,1024]{1,0:T(8,128)(2,1)S(1)} %get-tuple-element.289.glb_ref.grb_ref), channel_id=1, source_target_pairs={{1,0},{2,1},{3,2},{5,4},{6,5},{7,6},{9,8},{10,9},{11,10},{13,12},{... | collective-permute-start | bytes 1572872 | tf_op jit(solution)/shard_map/ppermute | solution.py:636
  107.5 16.9 %collective-permute-start.7 = (bf16[256,1024]{1,0:T(8,128)(2,1)S(1)}, bf16[256,1024]{1,0:T(8,128)(2,1)S(1)}, u32[]{:S(2)}, u32[]{:S(2)}) collective-permute-start(bf16[256,1024]{1,0:T(8,128)(2,1)S(1)} %join.20), channel_id=1, source_target_pairs={{0,1},{1,2},{2,3},{4,5},{5,6},{6,7},{8,9},{9,10},{10,11},{12,13},{... | collective-permute-start | bytes 1572872 | tf_op jit(solution)/shard_map/ppermute | solution.py:636
  113.8 21.8 %collective-permute-start.11 = (bf16[256,1024]{1,0:T(8,128)(2,1)S(1)}, bf16[256,1024]{1,0:T(8,128)(2,1)S(1)}, u32[]{:S(2)}, u32[]{:S(2)}) collective-permute-start(bf16[256,1024]{1,0:T(8,128)(2,1)S(1)} %join.23), channel_id=1, source_target_pairs={{0,1},{1,2},{2,3},{4,5},{5,6},{6,7},{8,9},{9,10},{10,11},{12,13},{... | collective-permute-start | bytes 1572872 | tf_op jit(solution)/shard_map/ppermute | solution.py:636
  117.3 23.6 %collective-permute-start.15 = (bf16[256,1024]{1,0:T(8,128)(2,1)S(1)}, bf16[256,1024]{1,0:T(8,128)(2,1)S(1)}, u32[]{:S(2)}, u32[]{:S(2)}) collective-permute-start(bf16[256,1024]{1,0:T(8,128)(2,1)S(1)} %join.26), channel_id=1, source_target_pairs={{1,0},{2,1},{3,2},{5,4},{6,5},{7,6},{9,8},{10,9},{11,10},{13,12},{... | collective-permute-start | bytes 1572872 | tf_op jit(solution)/shard_map/ppermute | solution.py:636
  120.2 24.4 %collective-permute-start.19 = (bf16[256,1024]{1,0:T(8,128)(2,1)S(1)}, bf16[256,1024]{1,0:T(8,128)(2,1)S(1)}, u32[]{:S(2)}, u32[]{:S(2)}) collective-permute-start(bf16[256,1024]{1,0:T(8,128)(2,1)S(1)} %join.29), channel_id=1, source_target_pairs={{1,0},{2,1},{3,2},{5,4},{6,5},{7,6},{9,8},{10,9},{11,10},{13,12},{... | collective-permute-start | bytes 1572872 | tf_op jit(solution)/shard_map/ppermute | solution.py:636
  125.2 21.7 %collective-permute-start.8 = (bf16[256,1024]{1,0:T(8,128)(2,1)S(1)}, bf16[256,1024]{1,0:T(8,128)(2,1)S(1)}, u32[]{:S(2)}, u32[]{:S(2)}) collective-permute-start(bf16[256,1024]{1,0:T(8,128)(2,1)S(1)} %join.21), channel_id=1, source_target_pairs={{0,1},{1,2},{2,3},{4,5},{5,6},{6,7},{8,9},{9,10},{10,11},{12,13},{... | collective-permute-start | bytes 1572872 | tf_op jit(solution)/shard_map/ppermute | solution.py:636
  136.5 21.7 %collective-permute-start.12 = (bf16[256,1024]{1,0:T(8,128)(2,1)S(1)}, bf16[256,1024]{1,0:T(8,128)(2,1)S(1)}, u32[]{:S(2)}, u32[]{:S(2)}) collective-permute-start(bf16[256,1024]{1,0:T(8,128)(2,1)S(1)} %join.24), channel_id=1, source_target_pairs={{0,1},{1,2},{2,3},{4,5},{5,6},{6,7},{8,9},{9,10},{10,11},{12,13},{... | collective-permute-start | bytes 1572872 | tf_op jit(solution)/shard_map/ppermute | solution.py:636
  141.7 21.6 %collective-permute-start.16 = (bf16[256,1024]{1,0:T(8,128)(2,1)S(1)}, bf16[256,1024]{1,0:T(8,128)(2,1)S(1)}, u32[]{:S(2)}, u32[]{:S(2)}) collective-permute-start(bf16[256,1024]{1,0:T(8,128)(2,1)S(1)} %join.27), channel_id=1, source_target_pairs={{1,0},{2,1},{3,2},{5,4},{6,5},{7,6},{9,8},{10,9},{11,10},{13,12},{... | collective-permute-start | bytes 1572872 | tf_op jit(solution)/shard_map/ppermute | solution.py:636
  145.5 21.7 %collective-permute-start.20 = (bf16[256,1024]{1,0:T(8,128)(2,1)S(1)}, bf16[256,1024]{1,0:T(8,128)(2,1)S(1)}, u32[]{:S(2)}, u32[]{:S(2)}) collective-permute-start(bf16[256,1024]{1,0:T(8,128)(2,1)S(1)} %join.30), channel_id=1, source_target_pairs={{1,0},{2,1},{3,2},{5,4},{6,5},{7,6},{9,8},{10,9},{11,10},{13,12},{... | collective-permute-start | bytes 1572872 | tf_op jit(solution)/shard_map/ppermute | solution.py:636
  147.8 24.5 %collective-permute-start.9 = (bf16[256,1024]{1,0:T(8,128)(2,1)S(1)}, bf16[256,1024]{1,0:T(8,128)(2,1)S(1)}, u32[]{:S(2)}, u32[]{:S(2)}) collective-permute-start(bf16[256,1024]{1,0:T(8,128)(2,1)S(1)} %join.22), channel_id=1, source_target_pairs={{0,1},{1,2},{2,3},{4,5},{5,6},{6,7},{8,9},{9,10},{10,11},{12,13},{... | collective-permute-start | bytes 1572872 | tf_op jit(solution)/shard_map/ppermute | solution.py:636
  158.9 17.3 %collective-permute-start.13 = (bf16[256,1024]{1,0:T(8,128)(2,1)S(1)}, bf16[256,1024]{1,0:T(8,128)(2,1)S(1)}, u32[]{:S(2)}, u32[]{:S(2)}) collective-permute-start(bf16[256,1024]{1,0:T(8,128)(2,1)S(1)} %join.25), channel_id=1, source_target_pairs={{0,1},{1,2},{2,3},{4,5},{5,6},{6,7},{8,9},{9,10},{10,11},{12,13},{... | collective-permute-start | bytes 1572872 | tf_op jit(solution)/shard_map/ppermute | solution.py:636
  168.0 18.1 %collective-permute-start.21 = (bf16[256,1024]{1,0:T(8,128)(2,1)S(1)}, bf16[256,1024]{1,0:T(8,128)(2,1)S(1)}, u32[]{:S(2)}, u32[]{:S(2)}) collective-permute-start(bf16[256,1024]{1,0:T(8,128)(2,1)S(1)} %join.31), channel_id=1, source_target_pairs={{1,0},{2,1},{3,2},{5,4},{6,5},{7,6},{9,8},{10,9},{11,10},{13,12},{... | collective-permute-start | bytes 1572872 | tf_op jit(solution)/shard_map/ppermute | solution.py:636
  188.2 23.5 %collective-permute-start.22 = (bf16[256,2048]{1,0:T(8,128)(2,1)S(1)}, bf16[256,2048]{1,0:T(8,128)(2,1)}, u32[]{:S(2)}, u32[]{:S(2)}) collective-permute-start(bf16[256,2048]{1,0:T(8,128)(2,1)S(1)} %add_convert_fusion.2.a_ref), channel_id=1, source_target_pairs={{0,3},{1,0},{2,1},{3,2},{4,7},{5,4},{6,5},{7,6},{8,11},{9,8},{10,9... | collective-permute-start | bytes 3145736 | tf_op jit(solution)/shard_map/ppermute | solution.py:636
  211.7 26.4 %collective-permute-start.23 = (bf16[256,2048]{1,0:T(8,128)(2,1)}, bf16[256,2048]{1,0:T(8,128)(2,1)}, u32[]{:S(2)}, u32[]{:S(2)}) collective-permute-start(bf16[256,2048]{1,0:T(8,128)(2,1)} %collective-permute-done.22.a_ref), channel_id=1, source_target_pairs={{0,3},{1,0},{2,1},{3,2},{4,7},{5,4},{6,5},{7,6},{8,11},{9,8},{10,9... | collective-permute-start | bytes 3145736 | tf_op jit(solution)/shard_map/ppermute | solution.py:636
  225.7 34.7 %collective-permute-start.25 = (bf16[256,2048]{1,0:T(8,128)(2,1)}, bf16[256,2048]{1,0:T(8,128)(2,1)S(1)}, u32[]{:S(2)}, u32[]{:S(2)}) collective-permute-start(bf16[256,2048]{1,0:T(8,128)(2,1)} %block_term.9), channel_id=1, source_target_pairs={{0,3},{1,0},{2,1},{3,2},{4,7},{5,4},{6,5},{7,6},{8,11},{9,8},{10,9... | collective-permute-start | bytes 3145736 | tf_op jit(solution)/shard_map/ppermute | solution.py:636
  238.1 44.8 %collective-permute-start.24 = (bf16[256,2048]{1,0:T(8,128)(2,1)}, bf16[256,2048]{1,0:T(8,128)(2,1)S(1)}, u32[]{:S(2)}, u32[]{:S(2)}) collective-permute-start(bf16[256,2048]{1,0:T(8,128)(2,1)} %collective-permute-done.23.a_ref), channel_id=1, source_target_pairs={{0,3},{1,0},{2,1},{3,2},{4,7},{5,4},{6,5},{7,6},{8,11},{9,8},{10,9... | collective-permute-start | bytes 3145736 | tf_op jit(solution)/shard_map/ppermute | solution.py:636
  260.8 38.4 %collective-permute-start.26 = (bf16[256,2048]{1,0:T(8,128)(2,1)S(1)}, bf16[256,2048]{1,0:T(8,128)(2,1)S(1)}, u32[]{:S(2)}, u32[]{:S(2)}) collective-permute-start(bf16[256,2048]{1,0:T(8,128)(2,1)S(1)} %add_convert_fusion.1), channel_id=1, source_target_pairs={{0,3},{1,0},{2,1},{3,2},{4,7},{5,4},{6,5},{7,6},{8,11},{9,8},{10,9... | collective-permute-start | bytes 3145736 | tf_op jit(solution)/shard_map/ppermute | solution.py:636
  302.4 18.8 %collective-permute-start.27 = (bf16[256,2048]{1,0:T(8,128)(2,1)S(1)}, bf16[256,2048]{1,0:T(8,128)(2,1)S(1)}, u32[]{:S(2)}, u32[]{:S(2)}) collective-permute-start(bf16[256,2048]{1,0:T(8,128)(2,1)S(1)} %block_term.11), channel_id=1, source_target_pairs={{0,3},{1,0},{2,1},{3,2},{4,7},{5,4},{6,5},{7,6},{8,11},{9,8},{10,9... | collective-permute-start | bytes 3145736 | tf_op jit(solution)/shard_map/ppermute | solution.py:636
  310.0 31.5 %collective-permute-start.29 = (bf16[2048,1024]{1,0:T(8,128)(2,1)}, bf16[2048,1024]{1,0:T(8,128)(2,1)}, u32[]{:S(2)}, u32[]{:S(2)}) collective-permute-start(bf16[2048,1024]{1,0:T(8,128)(2,1)} %grad_half.4), channel_id=1, source_target_pairs={{0,4},{4,0},{8,12},{12,8},{16,20},{20,16},{24,28},{28,24},{1,5},{5... | collective-permute-start | bytes 12582920 | tf_op jit(solution)/shard_map/ppermute | solution.py:657
  317.3 42.3 %collective-permute-start.32 = (bf16[2048,1024]{1,0:T(8,128)(2,1)}, bf16[2048,1024]{1,0:T(8,128)(2,1)}, u32[]{:S(2)}, u32[]{:S(2)}) collective-permute-start(bf16[2048,1024]{1,0:T(8,128)(2,1)} %grad_half.5), channel_id=1, source_target_pairs={{0,4},{4,0},{8,12},{12,8},{16,20},{20,16},{24,28},{28,24},{1,5},{5... | collective-permute-start | bytes 12582920 | tf_op jit(solution)/shard_map/ppermute | solution.py:657
  325.2 24.3 %collective-permute-start.28 = (bf16[256,2048]{1,0:T(8,128)(2,1)S(1)}, bf16[256,2048]{1,0:T(8,128)(2,1)S(1)}, u32[]{:S(2)}, u32[]{:S(2)}) collective-permute-start(bf16[256,2048]{1,0:T(8,128)(2,1)S(1)} %get-tuple-element.226.refs_0_), channel_id=1, source_target_pairs={{0,1},{1,2},{2,3},{4,5},{5,6},{6,7},{8,9},{9,10},{10,11},{12,13},{... | collective-permute-start | bytes 3145736 | tf_op jit(solution)/shard_map/ppermute | solution.py:636
  328.9 27.8 %collective-permute-start.31 = (bf16[256,2048]{1,0:T(8,128)(2,1)S(1)}, bf16[256,2048]{1,0:T(8,128)(2,1)S(1)}, u32[]{:S(2)}, u32[]{:S(2)}) collective-permute-start(bf16[256,2048]{1,0:T(8,128)(2,1)S(1)} %get-tuple-element.226.refs_0_), channel_id=1, source_target_pairs={{1,0},{2,1},{3,2},{5,4},{6,5},{7,6},{9,8},{10,9},{11,10},{13,12},{... | collective-permute-start | bytes 3145736 | tf_op jit(solution)/shard_map/ppermute | solution.py:636
  351.3 23.4 %collective-permute-start.30 = (bf16[256,2048]{1,0:T(8,128)(2,1)}, bf16[256,2048]{1,0:T(8,128)(2,1)}, u32[]{:S(2)}, u32[]{:S(2)}) collective-permute-start(bf16[256,2048]{1,0:T(8,128)(2,1)} %join.32), channel_id=1, source_target_pairs={{0,1},{1,2},{2,3},{4,5},{5,6},{6,7},{8,9},{9,10},{10,11},{12,13},{... | collective-permute-start | bytes 3145736 | tf_op jit(solution)/shard_map/ppermute | solution.py:636
  358.3 25.9 %collective-permute-start.35 = (bf16[256,2048]{1,0:T(8,128)(2,1)}, bf16[256,2048]{1,0:T(8,128)(2,1)}, u32[]{:S(2)}, u32[]{:S(2)}) collective-permute-start(bf16[256,2048]{1,0:T(8,128)(2,1)} %join.33), channel_id=1, source_target_pairs={{1,0},{2,1},{3,2},{5,4},{6,5},{7,6},{9,8},{10,9},{11,10},{13,12},{... | collective-permute-start | bytes 3145736 | tf_op jit(solution)/shard_map/ppermute | solution.py:636
  370.1 146.6 %reduce-scatter.5.cloned.1.call-start = ((), (), s32[]{:S(2)}) async-start(), calls=%async_computation.3 | async-start | bytes 5242880 | tf_op jit(solution)/shard_map/reduce_scatter | solution.py:785
  378.9 23.2 %collective-permute-start.33 = (bf16[256,2048]{1,0:T(8,128)(2,1)S(1)}, bf16[256,2048]{1,0:T(8,128)(2,1)S(1)}, u32[]{:S(2)}, u32[]{:S(2)}) collective-permute-start(bf16[256,2048]{1,0:T(8,128)(2,1)S(1)} %join.34), channel_id=1, source_target_pairs={{0,1},{1,2},{2,3},{4,5},{5,6},{6,7},{8,9},{9,10},{10,11},{12,13},{... | collective-permute-start | bytes 3145736 | tf_op jit(solution)/shard_map/ppermute | solution.py:636
  386.0 22.8 %collective-permute-start.36 = (bf16[256,2048]{1,0:T(8,128)(2,1)S(1)}, bf16[256,2048]{1,0:T(8,128)(2,1)S(1)}, u32[]{:S(2)}, u32[]{:S(2)}) collective-permute-start(bf16[256,2048]{1,0:T(8,128)(2,1)S(1)} %join.36), channel_id=1, source_target_pairs={{1,0},{2,1},{3,2},{5,4},{6,5},{7,6},{9,8},{10,9},{11,10},{13,12},{... | collective-permute-start | bytes 3145736 | tf_op jit(solution)/shard_map/ppermute | solution.py:636
  403.0 28.4 %collective-permute-start.34 = (bf16[256,2048]{1,0:T(8,128)(2,1)S(1)}, bf16[256,2048]{1,0:T(8,128)(2,1)S(1)}, u32[]{:S(2)}, u32[]{:S(2)}) collective-permute-start(bf16[256,2048]{1,0:T(8,128)(2,1)S(1)} %join.35), channel_id=1, source_target_pairs={{0,1},{1,2},{2,3},{4,5},{5,6},{6,7},{8,9},{9,10},{10,11},{12,13},{... | collective-permute-start | bytes 3145736 | tf_op jit(solution)/shard_map/ppermute | solution.py:636
  409.5 22.3 %collective-permute-start.37 = (bf16[256,2048]{1,0:T(8,128)(2,1)S(1)}, bf16[256,2048]{1,0:T(8,128)(2,1)S(1)}, u32[]{:S(2)}, u32[]{:S(2)}) collective-permute-start(bf16[256,2048]{1,0:T(8,128)(2,1)S(1)} %join.37), channel_id=1, source_target_pairs={{1,0},{2,1},{3,2},{5,4},{6,5},{7,6},{9,8},{10,9},{11,10},{13,12},{... | collective-permute-start | bytes 3145736 | tf_op jit(solution)/shard_map/ppermute | solution.py:636
  440.7 27.1 %collective-permute-start.38 = (bf16[256,2048]{1,0:T(8,128)(2,1)}, bf16[256,2048]{1,0:T(8,128)(2,1)}, u32[]{:S(2)}, u32[]{:S(2)}) collective-permute-start(bf16[256,2048]{1,0:T(8,128)(2,1)} %block_term.12), channel_id=1, source_target_pairs={{0,3},{1,0},{2,1},{3,2},{4,7},{5,4},{6,5},{7,6},{8,11},{9,8},{10,9... | collective-permute-start | bytes 3145736 | tf_op jit(solution)/shard_map/ppermute | solution.py:636
  471.8 28.3 %collective-permute-start.40 = (bf16[256,2048]{1,0:T(8,128)(2,1)}, bf16[256,2048]{1,0:T(8,128)(2,1)}, u32[]{:S(2)}, u32[]{:S(2)}) collective-permute-start(bf16[256,2048]{1,0:T(8,128)(2,1)} %join.38), channel_id=1, source_target_pairs={{0,3},{1,0},{2,1},{3,2},{4,7},{5,4},{6,5},{7,6},{8,11},{9,8},{10,9... | collective-permute-start | bytes 3145736 | tf_op jit(solution)/shard_map/ppermute | solution.py:636
  489.7 17.6 %collective-permute-start.45 = (f32[8320]{0:T(1024)S(1)}, f32[8320]{0:T(1024)S(1)}, u32[]{:S(2)}, u32[]{:S(2)}) collective-permute-start(f32[8320]{0:T(1024)S(1)} %add.128), channel_id=1, source_target_pairs={{0,1},{1,2},{2,3},{3,0},{4,5},{5,6},{6,7},{7,4},{8,9},{9,10},{10,1... | collective-permute-start | bytes 99848 | tf_op jit(solution)/shard_map/ppermute | solution.py:636
  489.7 17.6 %collective-permute-start.46 = (f32[8320]{0:T(1024)S(1)}, f32[8320]{0:T(1024)S(1)}, u32[]{:S(2)}, u32[]{:S(2)}) collective-permute-start(f32[8320]{0:T(1024)S(1)} %add.128), channel_id=1, source_target_pairs={{0,2},{1,3},{2,0},{3,1},{4,6},{5,7},{6,4},{7,5},{8,10},{9,11},{10,... | collective-permute-start | bytes 99848 | tf_op jit(solution)/shard_map/ppermute | solution.py:636
  490.4 16.9 %collective-permute-start.47 = (f32[8320]{0:T(1024)S(1)}, f32[8320]{0:T(1024)S(1)}, u32[]{:S(2)}, u32[]{:S(2)}) collective-permute-start(f32[8320]{0:T(1024)S(1)} %add.128), channel_id=1, source_target_pairs={{0,3},{1,0},{2,1},{3,2},{4,7},{5,4},{6,5},{7,6},{8,11},{9,8},{10,9... | collective-permute-start | bytes 99848 | tf_op jit(solution)/shard_map/ppermute | solution.py:636
  503.0 25.0 %collective-permute-start.42 = (bf16[256,2048]{1,0:T(8,128)(2,1)}, bf16[256,2048]{1,0:T(8,128)(2,1)S(1)}, u32[]{:S(2)}, u32[]{:S(2)}) collective-permute-start(bf16[256,2048]{1,0:T(8,128)(2,1)} %join.39), channel_id=1, source_target_pairs={{0,3},{1,0},{2,1},{3,2},{4,7},{5,4},{6,5},{7,6},{8,11},{9,8},{10,9... | collective-permute-start | bytes 3145736 | tf_op jit(solution)/shard_map/ppermute | solution.py:636
  507.4 23.5 %collective-permute-start.48 = (f32[8320]{0:T(1024)S(1)}, f32[8320]{0:T(1024)S(1)}, u32[]{:S(2)}, u32[]{:S(2)}) collective-permute-start(f32[8320]{0:T(1024)S(1)} %add_add_fusion.2), channel_id=1, source_target_pairs={{0,8},{4,12},{8,16},{12,20},{16,24},{20,28},{24,0},{28,4},{1,9},{5... | collective-permute-start | bytes 99848 | tf_op jit(solution)/shard_map/ppermute | solution.py:830
  508.9 22.0 %collective-permute-start.49 = (f32[8320]{0:T(1024)S(1)}, f32[8320]{0:T(1024)S(1)}, u32[]{:S(2)}, u32[]{:S(2)}) collective-permute-start(f32[8320]{0:T(1024)S(1)} %add_add_fusion.2), channel_id=1, source_target_pairs={{0,16},{4,20},{8,24},{12,28},{16,0},{20,4},{24,8},{28,12},{1,17},{... | collective-permute-start | bytes 99848 | tf_op jit(solution)/shard_map/ppermute | solution.py:830
  510.4 20.5 %collective-permute-start.50 = (f32[8320]{0:T(1024)S(1)}, f32[8320]{0:T(1024)S(1)}, u32[]{:S(2)}, u32[]{:S(2)}) collective-permute-start(f32[8320]{0:T(1024)S(1)} %add_add_fusion.2), channel_id=1, source_target_pairs={{0,24},{4,28},{8,0},{12,4},{16,8},{20,12},{24,16},{28,20},{1,25},{... | collective-permute-start | bytes 99848 | tf_op jit(solution)/shard_map/ppermute | solution.py:830
  (90 other events, 787.0 us)
Sparse Core Ops, SparseCore 0:
  370.3 86.6 reduce-scatter.2
  460.5 56.1 reduce-scatter.4

commit v16 on v12

--- a/solution.py
+++ b/solution.py
@@ -824,8 +824,11 @@
         sent = join(where, moved, terms[s][None], 0, n + 1, True, 0, 64e9)
         moved = hop(sent)
 
-    planes = tie([send(small, [(i, (i + m) % n) for i in range(n)]) for m in range(1, n)], sent)
-    small = small + sum(planes)
+    step = 1
+    while step < n:
+        (got,) = tie([send(small, [(i, i ^ step) for i in range(n)])], sent2 if step * 2 < n else sent)
+        small = small + got
+        step *= 2
     others = [
         lax.ppermute(small, "dp", [(i, (i + 2 * m) % n_dp) for i in range(n_dp)])
         for m in range(1, n_dp // 2)

time: 549 us -> 564 us (1.027)
  waiting for transfers between devices: 131 us -> 155 us
    ppermute x42 -> x41, waiting for transfers between devices: 124 us -> 153 us  [per_device(): send = lambda v, pairs: lax.ppermute(v, 'mp', pairs)]
    ppermute x42 -> x41, starting transfers between devices: 113 us -> 112 us  [per_device(): send = lambda v, pairs: lax.ppermute(v, 'mp', pairs)]
  transfers between devices with their start and end apart: 53 -> 52, of which waited for: 27 -> 27; matrix products, arithmetic and copies ran while one was open for 7% -> 7% of each run, Pallas kernels for 38% -> 36%
where the time goes in v16:
time: 564 us; the launch traced here: 555 us
  Pallas kernels  203 us (36%)
  waiting for transfers between devices  155 us (27%)
  starting transfers between devices  117 us (21%)
  local copies, waits for them, and re-layouts  27.7 us (5%)
  other arithmetic  20.7 us (4%)
  between operations  16 us (3%)
  matrix products  15.6 us (3%)
    ppermute x41, waiting for transfers between devices, per_device(): send = lambda v, pairs: lax.ppermute(v, 'mp', pairs)  153 us
    ppermute x41, starting transfers between devices, per_device(): send = lambda v, pairs: lax.ppermute(v, 'mp', pairs)  112 us
    pallas_call x4, Pallas kernels, mlp_slot(): pl.pallas_call(functools.partial(mlp_body, slot, n), grid_spec=pltpu.Pref...  39.3 us
    pallas_call x4, Pallas kernels, grad_half(): pl.pallas_call(functools.partial(grad_body, not partner), grid_spec=pltpu...  29.6 us
    pallas_call x4, Pallas kernels, qkv_slot(): pl.pallas_call(qkv_body, grid_spec=pltpu.PrefetchScalarGridSpec(num_scala...  28.7 us
    pallas_call x20, Pallas kernels, join(): pl.pallas_call(functools.partial(join_body, 0 if right else -1, first), g...  24.5 us
    pallas_call x8, Pallas kernels, block_term(): pl.pallas_call(term_body, grid=(d // tile,), in_specs=[pl.BlockSpec((1, r...  23.8 us
    unnamed x173, local copies, waits for them, and re-layouts  21.7 us
  transfers between devices with their start and end apart: 52, of which 27 were waited for; matrix products, arithmetic and copies ran while one was open for 7% of the time, Pallas kernels for 36%

profile of v16, /device:TPU:0, one launch (start us, length us, event | category | flops | bytes accessed | tf_op | source)
XLA Modules:
  0.0 555.1 jit_solution(6851614456464654342)
XLA Ops:
  8.5 5.1 collective-permute-start
  17.9 7.1 %qkv_slot.4 = (bf16[4,256,2048]{2,1,0:T(8,128)(2,1)}, bf16[4,256,512]{2,1,0:T(8,128)(2,1)}, bf16[4,256,512]{2,1,0:T(8,128)(2,1)}, bf16[4,256,512]{2,1,0:T(8,128)(2,1)}) custom-call(s32[4]{0:T(128)} %pad_add_fusion.rank_ref, bf16[256,1024]{1,0:T(8,128)(2,1)} %copy-done.61, bf16[256,1024]{1,0:T(8,128)(2,1)} %copy-done.60, f32[1,2048]{1,0:T(1,128)} %bitcast.105, ...), custom_call_target="tpu_custom_call" | custom-call | flops 1610612736 | bytes 8388608 | tf_op jit(solution)/shard_map/qkv_slot/pallas_call | solution.py:106
  26.0 4.4 collective-permute-start.1
  30.3 6.8 %collective-permute-done.2.xb_ref = bf16[256,1024]{1,0:T(8,128)(2,1)S(1)} collective-permute-done((bf16[256,1024]{1,0:T(8,128)(2,1)S(1)}, bf16[256,1024]{1,0:T(8,128)(2,1)S(1)}, u32[]{:S(2)}, u32[]{:S(2)}) %collective-permute-start.2) | collective-permute-done | bytes 524320 | tf_op jit(solution)/shard_map/ppermute | solution.py:636
  37.2 4.3 collective-permute-start.4
  41.5 7.1 %qkv_slot.5 = (bf16[4,256,2048]{2,1,0:T(8,128)(2,1)}, bf16[4,256,512]{2,1,0:T(8,128)(2,1)}, bf16[4,256,512]{2,1,0:T(8,128)(2,1)}, bf16[4,256,512]{2,1,0:T(8,128)(2,1)}) custom-call(s32[4]{0:T(128)} %pad_add_fusion.rank_ref, ...), custom_call_target="tpu_custom_call", output_to_operand_aliasing={{0}: (10, {}), {1}: (11, {}), {2}: (12, {}), {3}: (13, {})} | custom-call | flops 1610612736 | bytes 8388608 | tf_op jit(solution)/shard_map/qkv_slot/pallas_call | solution.py:106
  52.7 7.0 %collective-permute-done.4.xb_ref = bf16[256,1024]{1,0:T(8,128)(2,1)S(1)} collective-permute-done((bf16[256,1024]{1,0:T(8,128)(2,1)S(1)}, bf16[256,1024]{1,0:T(8,128)(2,1)S(1)}, u32[]{:S(2)}, u32[]{:S(2)}) %collective-permute-start.4) | collective-permute-done | bytes 524320 | tf_op jit(solution)/shard_map/ppermute | solution.py:636
  59.7 4.3 collective-permute-start.5
  68.1 7.3 %qkv_slot.6 = (bf16[4,256,2048]{2,1,0:T(8,128)(2,1)}, bf16[4,256,512]{2,1,0:T(8,128)(2,1)}, bf16[4,256,512]{2,1,0:T(8,128)(2,1)}, bf16[4,256,512]{2,1,0:T(8,128)(2,1)}) custom-call(s32[4]{0:T(128)} %pad_add_fusion.rank_ref, bf16[256,1024]{1,0:T(8,128)(2,1)} %copy-done.67, ...), custom_call_target="tpu_custom_call", output_to_operand_aliasing={{0}: (10, {}), {1}: (11, {}), {2}: (12, {}), {3}: (13, {})} | custom-call | flops 1610612736 | bytes 8388608 | tf_op jit(solution)/shard_map/qkv_slot/pallas_call | solution.py:106
  78.1 5.4 collective-permute-start.10
  85.0 7.1 %qkv_slot.7 = (bf16[4,256,2048]{2,1,0:T(8,128)(2,1)}, bf16[4,256,512]{2,1,0:T(8,128)(2,1)}, bf16[4,256,512]{2,1,0:T(8,128)(2,1)}, bf16[4,256,512]{2,1,0:T(8,128)(2,1)}) custom-call(s32[4]{0:T(128)} %pad_add_fusion.rank_ref, bf16[256,1024]{1,0:T(8,128)(2,1)} %copy-done.66, ...), custom_call_target="tpu_custom_call", output_to_operand_aliasing={{0}: (10, {}), {1}: (11, {}), {2}: (12, {}), {3}: (13, {})} | custom-call | flops 1610612736 | bytes 8388608 | tf_op jit(solution)/shard_map/qkv_slot/pallas_call | solution.py:106
  92.2 10.2 %attend.1 = bf16[4,256,512]{2,1,0:T(8,128)(2,1)} custom-call(s32[4]{0:T(128)} %pad_add_fusion.rank_ref, bf16[4,256,512]{2,1,0:T(8,128)(2,1)} %get-tuple-element.183.q_ref, bf16[4,256,512]{2,1,0:T(8,128)(2,1)} %get-tuple-element.184.k_ref, bf16[4,256,512]{2,1,0:T(8,128)(2,1)} %get-tuple-element.185.v_ref, s32[4,256,1]{2,1,0:T(8,128)} %reshape.204.dcol_ref, ...), custom_call_target="tpu_custom_call" | custom-call | flops 2147483648 | bytes 4194304 | tf_op jit(solution)/shard_map/attend/pallas_call | solution.py:169
  102.4 4.3 convolution_convert_fusion.1
  107.6 4.6 collective-permute-start.7
  125.3 4.4 collective-permute-start.8
  129.7 6.0 %collective-permute-done.11.moved_ref.grb_ref = bf16[256,1024]{1,0:T(8,128)(2,1)S(1)} collective-permute-done((bf16[256,1024]{1,0:T(8,128)(2,1)S(1)}, bf16[256,1024]{1,0:T(8,128)(2,1)S(1)}, u32[]{:S(2)}, u32[]{:S(2)}) %collective-permute-start.11) | collective-permute-done | bytes 524320 | tf_op jit(solution)/shard_map/ppermute | solution.py:636
  136.5 4.4 collective-permute-start.12
  147.8 5.3 collective-permute-start.9
  153.1 5.1 collective-permute-done.12.moved_ref.grb_ref
  159.0 4.4 collective-permute-start.13
  180.5 5.6 %collective-permute-done.21 = bf16[256,1024]{1,0:T(8,128)(2,1)S(1)} collective-permute-done((bf16[256,1024]{1,0:T(8,128)(2,1)S(1)}, bf16[256,1024]{1,0:T(8,128)(2,1)S(1)}, u32[]{:S(2)}, u32[]{:S(2)}) %collective-permute-start.21) | collective-permute-done | bytes 524320 | tf_op jit(solution)/shard_map/ppermute | solution.py:636
  190.5 9.3 %mlp_slot.4 = (bf16[4,256,2048]{2,1,0:T(8,128)(2,1)S(1)}, bf16[4,256,2048]{2,1,0:T(8,128)(2,1)S(1)}, bf16[4,256,2048]{2,1,0:T(8,128)(2,1)S(1)}, bf16[4,256,2048]{2,1,0:T(8,128)(2,1)S(1)}) custom-call(s32[4]{0:T(128)S(1)} %copy-done.45, bf16[256,2048]{1,0:T(8,128)(2,1)S(1)} %add_convert_fusion.2.a_ref, ...), custom_call_target="tpu_custom_call" | custom-call | flops 4294967296 | bytes 20971520 | tf_op jit(solution)/shard_map/mlp_slot/pallas_call | solution.py:303
  207.2 4.5 collective-permute-done.22.a_ref
  211.7 10.2 %mlp_slot.5 = (bf16[4,256,2048]{2,1,0:T(8,128)(2,1)S(1)}, bf16[4,256,2048]{2,1,0:T(8,128)(2,1)S(1)}, bf16[4,256,2048]{2,1,0:T(8,128)(2,1)S(1)}, bf16[4,256,2048]{2,1,0:T(8,128)(2,1)S(1)}) custom-call(s32[4]{0:T(128)S(1)} %copy-done.45, ...), custom_call_target="tpu_custom_call", output_to_operand_aliasing={{0}: (9, {}), {1}: (10, {}), {2}: (11, {}), {3}: (12, {})} | custom-call | flops 4294967296 | bytes 20971520 | tf_op jit(solution)/shard_map/mlp_slot/pallas_call | solution.py:303
  228.1 10.0 %collective-permute-done.23.a_ref = bf16[256,2048]{1,0:T(8,128)(2,1)} collective-permute-done((bf16[256,2048]{1,0:T(8,128)(2,1)}, bf16[256,2048]{1,0:T(8,128)(2,1)}, u32[]{:S(2)}, u32[]{:S(2)}) %collective-permute-start.23) | collective-permute-done | bytes 1048608 | tf_op jit(solution)/shard_map/ppermute | solution.py:636
  240.0 9.6 %mlp_slot.6 = (bf16[4,256,2048]{2,1,0:T(8,128)(2,1)S(1)}, bf16[4,256,2048]{2,1,0:T(8,128)(2,1)S(1)}, bf16[4,256,2048]{2,1,0:T(8,128)(2,1)S(1)}, bf16[4,256,2048]{2,1,0:T(8,128)(2,1)S(1)}) custom-call(s32[4]{0:T(128)S(1)} %copy-done.45, ...), custom_call_target="tpu_custom_call", output_to_operand_aliasing={{0}: (9, {}), {1}: (10, {}), {2}: (11, {}), {3}: (12, {})} | custom-call | flops 4294967296 | bytes 20971520 | tf_op jit(solution)/shard_map/mlp_slot/pallas_call | solution.py:303
  252.7 7.8 %collective-permute-done.25 = bf16[256,2048]{1,0:T(8,128)(2,1)S(1)} collective-permute-done((bf16[256,2048]{1,0:T(8,128)(2,1)}, bf16[256,2048]{1,0:T(8,128)(2,1)S(1)}, u32[]{:S(2)}, u32[]{:S(2)}) %collective-permute-start.25) | collective-permute-done | bytes 1048608 | tf_op jit(solution)/shard_map/ppermute | solution.py:636
  262.8 20.2 %collective-permute-done.24.a_ref = bf16[256,2048]{1,0:T(8,128)(2,1)S(1)} collective-permute-done((bf16[256,2048]{1,0:T(8,128)(2,1)}, bf16[256,2048]{1,0:T(8,128)(2,1)S(1)}, u32[]{:S(2)}, u32[]{:S(2)}) %collective-permute-start.24) | collective-permute-done | bytes 1048608 | tf_op jit(solution)/shard_map/ppermute | solution.py:636
  283.0 10.2 %mlp_slot.7 = (bf16[4,256,2048]{2,1,0:T(8,128)(2,1)S(1)}, bf16[4,256,2048]{2,1,0:T(8,128)(2,1)S(1)}, bf16[4,256,2048]{2,1,0:T(8,128)(2,1)S(1)}, bf16[4,256,2048]{2,1,0:T(8,128)(2,1)S(1)}) custom-call(s32[4]{0:T(128)S(1)} %copy-done.45, ...), custom_call_target="tpu_custom_call", output_to_operand_aliasing={{0}: (9, {}), {1}: (10, {}), {2}: (11, {}), {3}: (12, {})} | custom-call | flops 4294967296 | bytes 20971520 | tf_op jit(solution)/shard_map/mlp_slot/pallas_call | solution.py:303
  293.1 6.1 %collective-permute-done.26.rest_0_ = bf16[256,2048]{1,0:T(8,128)(2,1)S(1)} collective-permute-done((bf16[256,2048]{1,0:T(8,128)(2,1)S(1)}, bf16[256,2048]{1,0:T(8,128)(2,1)S(1)}, u32[]{:S(2)}, u32[]{:S(2)}) %collective-permute-start.26) | collective-permute-done | bytes 1048608 | tf_op jit(solution)/shard_map/ppermute | solution.py:636
  302.9 7.2 %grad_half.4 = bf16[2048,1024]{1,0:T(8,128)(2,1)} custom-call(s32[4]{0:T(128)S(1)} %copy-done.45, bf16[1024,2048]{1,0:T(8,128)(2,1)S(1)} %bitcast.93, bf16[1024,2048]{1,0:T(8,128)(2,1)S(1)} %bitcast.88), custom_call_target="tpu_custom_call" | custom-call | flops 1000000 | bytes 1000000 | tf_op jit(solution)/shard_map/grad_half/pallas_call | solution.py:413
  310.1 7.2 %grad_half.5 = bf16[2048,1024]{1,0:T(8,128)(2,1)} custom-call(s32[4]{0:T(128)S(1)} %copy-done.45, bf16[1024,2048]{1,0:T(8,128)(2,1)S(1)} %bitcast.91, bf16[1024,2048]{1,0:T(8,128)(2,1)S(1)} %bitcast.72), custom_call_target="tpu_custom_call" | custom-call | flops 1000000 | bytes 1000000 | tf_op jit(solution)/shard_map/grad_half/pallas_call | solution.py:413
  330.2 11.3 %convolution_convert_fusion = bf16[1024,2048]{1,0:T(8,128)(2,1)S(1)} fusion(bf16[1024,2048]{1,0:T(8,128)(2,1)S(1)} %bitcast.89, bf16[2048,2048]{1,0:T(8,128)(2,1)} %down_ref.7), kind=kOutput, calls=%fused_computation | convolution fusion | flops 8592031744 | bytes 16777216 | tf_op jit(solution)/shard_map/dot_general | solution.py:53
  341.5 8.0 %grad_half.6.rest_1_ = bf16[2,2048,1024]{2,1,0:T(8,128)(2,1)S(1)} custom-call(s32[4]{0:T(128)S(1)} %copy-done.45, bf16[1024,2048]{1,0:T(8,128)(2,1)S(1)} %bitcast.94, bf16[1024,2048]{1,0:T(8,128)(2,1)S(1)} %bitcast.90, bf16[2048,1024]{1,0:T(8,128)(2,1)} %collective-permute-done.29.rest_0_), custom_call_target="tpu_custom_call" | custom-call | flops 1000000 | bytes 1000000 | tf_op jit(solution)/shard_map/grad_half/pallas_call | solution.py:413
  351.2 5.4 collective-permute-start.30
  359.6 7.2 %grad_half.7 = bf16[2,2048,1024]{2,1,0:T(8,128)(2,1)S(1)} custom-call(s32[4]{0:T(128)S(1)} %copy-done.45, bf16[1024,2048]{1,0:T(8,128)(2,1)S(1)} %bitcast.92, bf16[1024,2048]{1,0:T(8,128)(2,1)S(1)} %bitcast.73, bf16[2048,1024]{1,0:T(8,128)(2,1)} %collective-permute-done.32.rest_0_, ...), custom_call_target="tpu_custom_call", output_to_operand_aliasing={{}: (4, {})} | custom-call | flops 1000000 | bytes 1000000 | tf_op jit(solution)/shard_map/grad_half/pallas_call | solution.py:413
  370.2 4.5 collective-permute-done.30.moved_ref.refs_2_
  378.9 5.0 collective-permute-start.33
  391.4 10.4 %collective-permute-done.33.moved_ref.refs_1_ = bf16[256,2048]{1,0:T(8,128)(2,1)S(1)} collective-permute-done((bf16[256,2048]{1,0:T(8,128)(2,1)S(1)}, bf16[256,2048]{1,0:T(8,128)(2,1)S(1)}, u32[]{:S(2)}, u32[]{:S(2)}) %collective-permute-start.33) | collective-permute-done | bytes 1048608 | tf_op jit(solution)/shard_map/ppermute | solution.py:636
  402.7 4.5 collective-permute-start.34
  413.3 14.4 %attend_back.1.x_ref = bf16[4,256,1536]{2,1,0:T(8,128)(2,1)S(1)} custom-call(s32[4]{0:T(128)S(1)} %copy-done.45, bf16[4,256,512]{2,1,0:T(8,128)(2,1)S(1)} %copy-done.18, bf16[4,256,512]{2,1,0:T(8,128)(2,1)S(1)} %copy-done.19, bf16[4,256,512]{2,1,0:T(8,128)(2,1)S(1)} %copy-done.20, bf16[4,256,512]{2,1,0:T(8,128)(2,1)S(1)} %get-tuple-element.235.do_ref, ...), custom_call_target="tpu_custom_call" | custom-call | flops 115999997952 | bytes 7340032 | tf_op jit(solution)/shard_map/attend_back/pallas_call | solution.py:251
  432.9 7.4 %attn_grads.2 = bf16[2048,1024]{1,0:T(8,128)(2,1)S(1)} custom-call(s32[4]{0:T(128)S(1)} %copy-done.45, bf16[1024,2048]{1,0:T(8,128)(2,1)S(1)} %bitcast.85, bf16[1024,2048]{1,0:T(8,128)(2,1)S(1)} %bitcast.95, bf16[1024,1536]{1,0:T(8,128)(2,1)S(1)} %bitcast.74, bf16[1024,1536]{1,0:T(8,128)(2,1)S(1)} %bitcast.75, bf16[1024,512]{1,0:T(8,128)(2,1)S(1)} %bitcast.102), custom_call_target="tpu_custom_call" | custom-call | flops 4000000000 | bytes 1000000 | tf_op jit(solution)/shard_map/attn_grads/pallas_call | solution.py:456
  449.5 10.7 %attn_grads.3 = bf16[2048,1024]{1,0:T(8,128)(2,1)} custom-call(s32[4]{0:T(128)S(1)} %copy-done.45, bf16[1024,2048]{1,0:T(8,128)(2,1)} %bitcast.84, bf16[1024,2048]{1,0:T(8,128)(2,1)} %bitcast.96, bf16[1024,1536]{1,0:T(8,128)(2,1)} %bitcast.76, bf16[1024,1536]{1,0:T(8,128)(2,1)} %bitcast.77, bf16[1024,512]{1,0:T(8,128)(2,1)S(1)} %bitcast.103, ...), custom_call_target="tpu_custom_call" | custom-call | flops 1000000 | bytes 1000000 | tf_op jit(solution)/shard_map/attn_grads/pallas_call | solution.py:456
  461.0 6.7 %collective-permute-done.38.moved_ref = bf16[256,2048]{1,0:T(8,128)(2,1)} collective-permute-done((bf16[256,2048]{1,0:T(8,128)(2,1)}, bf16[256,2048]{1,0:T(8,128)(2,1)}, u32[]{:S(2)}, u32[]{:S(2)}) %collective-permute-start.38) | collective-permute-done | bytes 1048608 | tf_op jit(solution)/shard_map/ppermute | solution.py:636
  489.2 8.2 %collective-permute-done.40.moved_ref = bf16[256,2048]{1,0:T(8,128)(2,1)S(1)} collective-permute-done((bf16[256,2048]{1,0:T(8,128)(2,1)S(1)}, bf16[256,2048]{1,0:T(8,128)(2,1)S(1)}, u32[]{:S(2)}, u32[]{:S(2)}) %collective-permute-start.40) | collective-permute-done | bytes 1048608 | tf_op jit(solution)/shard_map/ppermute | solution.py:636
  499.0 4.3 collective-permute-start.42
  504.7 21.4 %collective-permute-done.45 = f32[8320]{0:T(1024)S(1)} collective-permute-done((f32[8320]{0:T(1024)S(1)}, f32[8320]{0:T(1024)S(1)}, u32[]{:S(2)}, u32[]{:S(2)}) %collective-permute-start.45) | collective-permute-done | bytes 33312 | tf_op jit(solution)/shard_map/ppermute | solution.py:636
  536.5 4.3 fusion.7
  (330 shorter events, 182.9 us)
Async XLA Ops:
  7.2 453.0 %reduce-scatter.3.cloned.1.call-start = ((), (), s32[]{:S(2)}) async-start(), calls=%async_computation.2 | async-start | bytes 10485760 | tf_op jit(solution)/shard_map/reduce_scatter | solution.py:757
  8.5 17.4 %collective-permute-start = (bf16[256,1024]{1,0:T(8,128)(2,1)S(1)}, bf16[256,1024]{1,0:T(8,128)(2,1)}, u32[]{:S(2)}, u32[]{:S(2)}) collective-permute-start(bf16[256,1024]{1,0:T(8,128)(2,1)S(1)} %get-tuple-element.289.xa_ref), channel_id=1, source_target_pairs={{0,3},{1,0},{2,1},{3,2},{4,7},{5,4},{6,5},{7,6},{8,11},{9,8},{10,9... | collective-permute-start | bytes 1572872 | tf_op jit(solution)/shard_map/ppermute | solution.py:636
  13.6 23.6 %collective-permute-start.2 = (bf16[256,1024]{1,0:T(8,128)(2,1)S(1)}, bf16[256,1024]{1,0:T(8,128)(2,1)S(1)}, u32[]{:S(2)}, u32[]{:S(2)}) collective-permute-start(bf16[256,1024]{1,0:T(8,128)(2,1)S(1)} %get-tuple-element.288.xb_ref), channel_id=1, source_target_pairs={{0,3},{1,0},{2,1},{3,2},{4,7},{5,4},{6,5},{7,6},{8,11},{9,8},{10,9... | collective-permute-start | bytes 1572872 | tf_op jit(solution)/shard_map/ppermute | solution.py:636
  26.0 22.7 %collective-permute-start.1 = (bf16[256,1024]{1,0:T(8,128)(2,1)}, bf16[256,1024]{1,0:T(8,128)(2,1)S(1)}, u32[]{:S(2)}, u32[]{:S(2)}) collective-permute-start(bf16[256,1024]{1,0:T(8,128)(2,1)} %collective-permute-done.xa_ref), channel_id=1, source_target_pairs={{0,3},{1,0},{2,1},{3,2},{4,7},{5,4},{6,5},{7,6},{8,11},{9,8},{10,9... | collective-permute-start | bytes 1572872 | tf_op jit(solution)/shard_map/ppermute | solution.py:636
  37.2 22.5 %collective-permute-start.4 = (bf16[256,1024]{1,0:T(8,128)(2,1)S(1)}, bf16[256,1024]{1,0:T(8,128)(2,1)S(1)}, u32[]{:S(2)}, u32[]{:S(2)}) collective-permute-start(bf16[256,1024]{1,0:T(8,128)(2,1)S(1)} %collective-permute-done.2.xb_ref), channel_id=1, source_target_pairs={{0,3},{1,0},{2,1},{3,2},{4,7},{5,4},{6,5},{7,6},{8,11},{9,8},{10,9... | collective-permute-start | bytes 1572872 | tf_op jit(solution)/shard_map/ppermute | solution.py:636
  48.6 26.8 %collective-permute-start.3 = (bf16[256,1024]{1,0:T(8,128)(2,1)S(1)}, bf16[256,1024]{1,0:T(8,128)(2,1)S(1)}, u32[]{:S(2)}, u32[]{:S(2)}) collective-permute-start(bf16[256,1024]{1,0:T(8,128)(2,1)S(1)} %collective-permute-done.1.xa_ref), channel_id=1, source_target_pairs={{0,3},{1,0},{2,1},{3,2},{4,7},{5,4},{6,5},{7,6},{8,11},{9,8},{10,9... | collective-permute-start | bytes 1572872 | tf_op jit(solution)/shard_map/ppermute | solution.py:636
  59.7 25.4 %collective-permute-start.5 = (bf16[256,1024]{1,0:T(8,128)(2,1)S(1)}, bf16[256,1024]{1,0:T(8,128)(2,1)}, u32[]{:S(2)}, u32[]{:S(2)}) collective-permute-start(bf16[256,1024]{1,0:T(8,128)(2,1)S(1)} %collective-permute-done.4.xb_ref), channel_id=1, source_target_pairs={{0,3},{1,0},{2,1},{3,2},{4,7},{5,4},{6,5},{7,6},{8,11},{9,8},{10,9... | collective-permute-start | bytes 1572872 | tf_op jit(solution)/shard_map/ppermute | solution.py:636
  75.5 31.2 %collective-permute-start.6 = (bf16[256,1024]{1,0:T(8,128)(2,1)S(1)}, bf16[256,1024]{1,0:T(8,128)(2,1)S(1)}, u32[]{:S(2)}, u32[]{:S(2)}) collective-permute-start(bf16[256,1024]{1,0:T(8,128)(2,1)S(1)} %get-tuple-element.286.gla_ref.gra_ref), channel_id=1, source_target_pairs={{0,1},{1,2},{2,3},{4,5},{5,6},{6,7},{8,9},{9,10},{10,11},{12,13},{... | collective-permute-start | bytes 1572872 | tf_op jit(solution)/shard_map/ppermute | solution.py:636
  76.8 38.9 %collective-permute-start.14 = (bf16[256,1024]{1,0:T(8,128)(2,1)S(1)}, bf16[256,1024]{1,0:T(8,128)(2,1)}, u32[]{:S(2)}, u32[]{:S(2)}) collective-permute-start(bf16[256,1024]{1,0:T(8,128)(2,1)S(1)} %get-tuple-element.286.gla_ref.gra_ref), channel_id=1, source_target_pairs={{1,0},{2,1},{3,2},{5,4},{6,5},{7,6},{9,8},{10,9},{11,10},{13,12},{... | collective-permute-start | bytes 1572872 | tf_op jit(solution)/shard_map/ppermute | solution.py:636
  78.1 34.0 %collective-permute-start.10 = (bf16[256,1024]{1,0:T(8,128)(2,1)S(1)}, bf16[256,1024]{1,0:T(8,128)(2,1)}, u32[]{:S(2)}, u32[]{:S(2)}) collective-permute-start(bf16[256,1024]{1,0:T(8,128)(2,1)S(1)} %get-tuple-element.287.glb_ref.grb_ref), channel_id=1, source_target_pairs={{0,1},{1,2},{2,3},{4,5},{5,6},{6,7},{8,9},{9,10},{10,11},{12,13},{... | collective-permute-start | bytes 1572872 | tf_op jit(solution)/shard_map/ppermute | solution.py:636
  83.5 35.1 %collective-permute-start.18 = (bf16[256,1024]{1,0:T(8,128)(2,1)S(1)}, bf16[256,1024]{1,0:T(8,128)(2,1)}, u32[]{:S(2)}, u32[]{:S(2)}) collective-permute-start(bf16[256,1024]{1,0:T(8,128)(2,1)S(1)} %get-tuple-element.287.glb_ref.grb_ref), channel_id=1, source_target_pairs={{1,0},{2,1},{3,2},{5,4},{6,5},{7,6},{9,8},{10,9},{11,10},{13,12},{... | collective-permute-start | bytes 1572872 | tf_op jit(solution)/shard_map/ppermute | solution.py:636
  107.6 16.9 %collective-permute-start.7 = (bf16[256,1024]{1,0:T(8,128)(2,1)S(1)}, bf16[256,1024]{1,0:T(8,128)(2,1)S(1)}, u32[]{:S(2)}, u32[]{:S(2)}) collective-permute-start(bf16[256,1024]{1,0:T(8,128)(2,1)S(1)} %join.20), channel_id=1, source_target_pairs={{0,1},{1,2},{2,3},{4,5},{5,6},{6,7},{8,9},{9,10},{10,11},{12,13},{... | collective-permute-start | bytes 1572872 | tf_op jit(solution)/shard_map/ppermute | solution.py:636
  113.8 21.9 %collective-permute-start.11 = (bf16[256,1024]{1,0:T(8,128)(2,1)S(1)}, bf16[256,1024]{1,0:T(8,128)(2,1)S(1)}, u32[]{:S(2)}, u32[]{:S(2)}) collective-permute-start(bf16[256,1024]{1,0:T(8,128)(2,1)S(1)} %join.23), channel_id=1, source_target_pairs={{0,1},{1,2},{2,3},{4,5},{5,6},{6,7},{8,9},{9,10},{10,11},{12,13},{... | collective-permute-start | bytes 1572872 | tf_op jit(solution)/shard_map/ppermute | solution.py:636
  117.3 23.6 %collective-permute-start.15 = (bf16[256,1024]{1,0:T(8,128)(2,1)S(1)}, bf16[256,1024]{1,0:T(8,128)(2,1)S(1)}, u32[]{:S(2)}, u32[]{:S(2)}) collective-permute-start(bf16[256,1024]{1,0:T(8,128)(2,1)S(1)} %join.26), channel_id=1, source_target_pairs={{1,0},{2,1},{3,2},{5,4},{6,5},{7,6},{9,8},{10,9},{11,10},{13,12},{... | collective-permute-start | bytes 1572872 | tf_op jit(solution)/shard_map/ppermute | solution.py:636
  120.3 24.4 %collective-permute-start.19 = (bf16[256,1024]{1,0:T(8,128)(2,1)S(1)}, bf16[256,1024]{1,0:T(8,128)(2,1)S(1)}, u32[]{:S(2)}, u32[]{:S(2)}) collective-permute-start(bf16[256,1024]{1,0:T(8,128)(2,1)S(1)} %join.29), channel_id=1, source_target_pairs={{1,0},{2,1},{3,2},{5,4},{6,5},{7,6},{9,8},{10,9},{11,10},{13,12},{... | collective-permute-start | bytes 1572872 | tf_op jit(solution)/shard_map/ppermute | solution.py:636
  125.3 21.7 %collective-permute-start.8 = (bf16[256,1024]{1,0:T(8,128)(2,1)S(1)}, bf16[256,1024]{1,0:T(8,128)(2,1)S(1)}, u32[]{:S(2)}, u32[]{:S(2)}) collective-permute-start(bf16[256,1024]{1,0:T(8,128)(2,1)S(1)} %join.21), channel_id=1, source_target_pairs={{0,1},{1,2},{2,3},{4,5},{5,6},{6,7},{8,9},{9,10},{10,11},{12,13},{... | collective-permute-start | bytes 1572872 | tf_op jit(solution)/shard_map/ppermute | solution.py:636
  136.5 21.7 %collective-permute-start.12 = (bf16[256,1024]{1,0:T(8,128)(2,1)S(1)}, bf16[256,1024]{1,0:T(8,128)(2,1)S(1)}, u32[]{:S(2)}, u32[]{:S(2)}) collective-permute-start(bf16[256,1024]{1,0:T(8,128)(2,1)S(1)} %join.24), channel_id=1, source_target_pairs={{0,1},{1,2},{2,3},{4,5},{5,6},{6,7},{8,9},{9,10},{10,11},{12,13},{... | collective-permute-start | bytes 1572872 | tf_op jit(solution)/shard_map/ppermute | solution.py:636
  141.7 21.6 %collective-permute-start.16 = (bf16[256,1024]{1,0:T(8,128)(2,1)S(1)}, bf16[256,1024]{1,0:T(8,128)(2,1)S(1)}, u32[]{:S(2)}, u32[]{:S(2)}) collective-permute-start(bf16[256,1024]{1,0:T(8,128)(2,1)S(1)} %join.27), channel_id=1, source_target_pairs={{1,0},{2,1},{3,2},{5,4},{6,5},{7,6},{9,8},{10,9},{11,10},{13,12},{... | collective-permute-start | bytes 1572872 | tf_op jit(solution)/shard_map/ppermute | solution.py:636
  145.5 21.7 %collective-permute-start.20 = (bf16[256,1024]{1,0:T(8,128)(2,1)S(1)}, bf16[256,1024]{1,0:T(8,128)(2,1)S(1)}, u32[]{:S(2)}, u32[]{:S(2)}) collective-permute-start(bf16[256,1024]{1,0:T(8,128)(2,1)S(1)} %join.30), channel_id=1, source_target_pairs={{1,0},{2,1},{3,2},{5,4},{6,5},{7,6},{9,8},{10,9},{11,10},{13,12},{... | collective-permute-start | bytes 1572872 | tf_op jit(solution)/shard_map/ppermute | solution.py:636
  147.8 24.5 %collective-permute-start.9 = (bf16[256,1024]{1,0:T(8,128)(2,1)S(1)}, bf16[256,1024]{1,0:T(8,128)(2,1)S(1)}, u32[]{:S(2)}, u32[]{:S(2)}) collective-permute-start(bf16[256,1024]{1,0:T(8,128)(2,1)S(1)} %join.22), channel_id=1, source_target_pairs={{0,1},{1,2},{2,3},{4,5},{5,6},{6,7},{8,9},{9,10},{10,11},{12,13},{... | collective-permute-start | bytes 1572872 | tf_op jit(solution)/shard_map/ppermute | solution.py:636
  159.0 17.3 %collective-permute-start.13 = (bf16[256,1024]{1,0:T(8,128)(2,1)S(1)}, bf16[256,1024]{1,0:T(8,128)(2,1)S(1)}, u32[]{:S(2)}, u32[]{:S(2)}) collective-permute-start(bf16[256,1024]{1,0:T(8,128)(2,1)S(1)} %join.25), channel_id=1, source_target_pairs={{0,1},{1,2},{2,3},{4,5},{5,6},{6,7},{8,9},{9,10},{10,11},{12,13},{... | collective-permute-start | bytes 1572872 | tf_op jit(solution)/shard_map/ppermute | solution.py:636
  164.2 16.3 %collective-permute-start.17 = (bf16[256,1024]{1,0:T(8,128)(2,1)S(1)}, bf16[256,1024]{1,0:T(8,128)(2,1)S(1)}, u32[]{:S(2)}, u32[]{:S(2)}) collective-permute-start(bf16[256,1024]{1,0:T(8,128)(2,1)S(1)} %join.28), channel_id=1, source_target_pairs={{1,0},{2,1},{3,2},{5,4},{6,5},{7,6},{9,8},{10,9},{11,10},{13,12},{... | collective-permute-start | bytes 1572872 | tf_op jit(solution)/shard_map/ppermute | solution.py:636
  168.0 18.1 %collective-permute-start.21 = (bf16[256,1024]{1,0:T(8,128)(2,1)S(1)}, bf16[256,1024]{1,0:T(8,128)(2,1)S(1)}, u32[]{:S(2)}, u32[]{:S(2)}) collective-permute-start(bf16[256,1024]{1,0:T(8,128)(2,1)S(1)} %join.31), channel_id=1, source_target_pairs={{1,0},{2,1},{3,2},{5,4},{6,5},{7,6},{9,8},{10,9},{11,10},{13,12},{... | collective-permute-start | bytes 1572872 | tf_op jit(solution)/shard_map/ppermute | solution.py:636
  188.2 23.5 %collective-permute-start.22 = (bf16[256,2048]{1,0:T(8,128)(2,1)S(1)}, bf16[256,2048]{1,0:T(8,128)(2,1)}, u32[]{:S(2)}, u32[]{:S(2)}) collective-permute-start(bf16[256,2048]{1,0:T(8,128)(2,1)S(1)} %add_convert_fusion.2.a_ref), channel_id=1, source_target_pairs={{0,3},{1,0},{2,1},{3,2},{4,7},{5,4},{6,5},{7,6},{8,11},{9,8},{10,9... | collective-permute-start | bytes 3145736 | tf_op jit(solution)/shard_map/ppermute | solution.py:636
  211.7 26.4 %collective-permute-start.23 = (bf16[256,2048]{1,0:T(8,128)(2,1)}, bf16[256,2048]{1,0:T(8,128)(2,1)}, u32[]{:S(2)}, u32[]{:S(2)}) collective-permute-start(bf16[256,2048]{1,0:T(8,128)(2,1)} %collective-permute-done.22.a_ref), channel_id=1, source_target_pairs={{0,3},{1,0},{2,1},{3,2},{4,7},{5,4},{6,5},{7,6},{8,11},{9,8},{10,9... | collective-permute-start | bytes 3145736 | tf_op jit(solution)/shard_map/ppermute | solution.py:636
  225.8 34.7 %collective-permute-start.25 = (bf16[256,2048]{1,0:T(8,128)(2,1)}, bf16[256,2048]{1,0:T(8,128)(2,1)S(1)}, u32[]{:S(2)}, u32[]{:S(2)}) collective-permute-start(bf16[256,2048]{1,0:T(8,128)(2,1)} %block_term.9), channel_id=1, source_target_pairs={{0,3},{1,0},{2,1},{3,2},{4,7},{5,4},{6,5},{7,6},{8,11},{9,8},{10,9... | collective-permute-start | bytes 3145736 | tf_op jit(solution)/shard_map/ppermute | solution.py:636
  238.1 44.8 %collective-permute-start.24 = (bf16[256,2048]{1,0:T(8,128)(2,1)}, bf16[256,2048]{1,0:T(8,128)(2,1)S(1)}, u32[]{:S(2)}, u32[]{:S(2)}) collective-permute-start(bf16[256,2048]{1,0:T(8,128)(2,1)} %collective-permute-done.23.a_ref), channel_id=1, source_target_pairs={{0,3},{1,0},{2,1},{3,2},{4,7},{5,4},{6,5},{7,6},{8,11},{9,8},{10,9... | collective-permute-start | bytes 3145736 | tf_op jit(solution)/shard_map/ppermute | solution.py:636
  260.9 38.4 %collective-permute-start.26 = (bf16[256,2048]{1,0:T(8,128)(2,1)S(1)}, bf16[256,2048]{1,0:T(8,128)(2,1)S(1)}, u32[]{:S(2)}, u32[]{:S(2)}) collective-permute-start(bf16[256,2048]{1,0:T(8,128)(2,1)S(1)} %add_convert_fusion.1), channel_id=1, source_target_pairs={{0,3},{1,0},{2,1},{3,2},{4,7},{5,4},{6,5},{7,6},{8,11},{9,8},{10,9... | collective-permute-start | bytes 3145736 | tf_op jit(solution)/shard_map/ppermute | solution.py:636
  302.4 18.7 %collective-permute-start.27 = (bf16[256,2048]{1,0:T(8,128)(2,1)S(1)}, bf16[256,2048]{1,0:T(8,128)(2,1)S(1)}, u32[]{:S(2)}, u32[]{:S(2)}) collective-permute-start(bf16[256,2048]{1,0:T(8,128)(2,1)S(1)} %block_term.11), channel_id=1, source_target_pairs={{0,3},{1,0},{2,1},{3,2},{4,7},{5,4},{6,5},{7,6},{8,11},{9,8},{10,9... | collective-permute-start | bytes 3145736 | tf_op jit(solution)/shard_map/ppermute | solution.py:636
  310.1 31.4 %collective-permute-start.29 = (bf16[2048,1024]{1,0:T(8,128)(2,1)}, bf16[2048,1024]{1,0:T(8,128)(2,1)}, u32[]{:S(2)}, u32[]{:S(2)}) collective-permute-start(bf16[2048,1024]{1,0:T(8,128)(2,1)} %grad_half.4), channel_id=1, source_target_pairs={{0,4},{4,0},{8,12},{12,8},{16,20},{20,16},{24,28},{28,24},{1,5},{5... | collective-permute-start | bytes 12582920 | tf_op jit(solution)/shard_map/ppermute | solution.py:657
  317.3 42.3 %collective-permute-start.32 = (bf16[2048,1024]{1,0:T(8,128)(2,1)}, bf16[2048,1024]{1,0:T(8,128)(2,1)}, u32[]{:S(2)}, u32[]{:S(2)}) collective-permute-start(bf16[2048,1024]{1,0:T(8,128)(2,1)} %grad_half.5), channel_id=1, source_target_pairs={{0,4},{4,0},{8,12},{12,8},{16,20},{20,16},{24,28},{28,24},{1,5},{5... | collective-permute-start | bytes 12582920 | tf_op jit(solution)/shard_map/ppermute | solution.py:657
  325.2 24.3 %collective-permute-start.28 = (bf16[256,2048]{1,0:T(8,128)(2,1)S(1)}, bf16[256,2048]{1,0:T(8,128)(2,1)S(1)}, u32[]{:S(2)}, u32[]{:S(2)}) collective-permute-start(bf16[256,2048]{1,0:T(8,128)(2,1)S(1)} %get-tuple-element.225.refs_0_), channel_id=1, source_target_pairs={{0,1},{1,2},{2,3},{4,5},{5,6},{6,7},{8,9},{9,10},{10,11},{12,13},{... | collective-permute-start | bytes 3145736 | tf_op jit(solution)/shard_map/ppermute | solution.py:636
  328.9 27.8 %collective-permute-start.31 = (bf16[256,2048]{1,0:T(8,128)(2,1)S(1)}, bf16[256,2048]{1,0:T(8,128)(2,1)S(1)}, u32[]{:S(2)}, u32[]{:S(2)}) collective-permute-start(bf16[256,2048]{1,0:T(8,128)(2,1)S(1)} %get-tuple-element.225.refs_0_), channel_id=1, source_target_pairs={{1,0},{2,1},{3,2},{5,4},{6,5},{7,6},{9,8},{10,9},{11,10},{13,12},{... | collective-permute-start | bytes 3145736 | tf_op jit(solution)/shard_map/ppermute | solution.py:636
  351.2 23.5 %collective-permute-start.30 = (bf16[256,2048]{1,0:T(8,128)(2,1)}, bf16[256,2048]{1,0:T(8,128)(2,1)}, u32[]{:S(2)}, u32[]{:S(2)}) collective-permute-start(bf16[256,2048]{1,0:T(8,128)(2,1)} %join.32), channel_id=1, source_target_pairs={{0,1},{1,2},{2,3},{4,5},{5,6},{6,7},{8,9},{9,10},{10,11},{12,13},{... | collective-permute-start | bytes 3145736 | tf_op jit(solution)/shard_map/ppermute | solution.py:636
  358.3 25.6 %collective-permute-start.35 = (bf16[256,2048]{1,0:T(8,128)(2,1)}, bf16[256,2048]{1,0:T(8,128)(2,1)}, u32[]{:S(2)}, u32[]{:S(2)}) collective-permute-start(bf16[256,2048]{1,0:T(8,128)(2,1)} %join.33), channel_id=1, source_target_pairs={{1,0},{2,1},{3,2},{5,4},{6,5},{7,6},{9,8},{10,9},{11,10},{13,12},{... | collective-permute-start | bytes 3145736 | tf_op jit(solution)/shard_map/ppermute | solution.py:636
  370.2 165.2 %reduce-scatter.5.cloned.1.call-start = ((), (), s32[]{:S(2)}) async-start(), calls=%async_computation.3 | async-start | bytes 5242880 | tf_op jit(solution)/shard_map/reduce_scatter | solution.py:785
  378.9 23.0 %collective-permute-start.33 = (bf16[256,2048]{1,0:T(8,128)(2,1)S(1)}, bf16[256,2048]{1,0:T(8,128)(2,1)S(1)}, u32[]{:S(2)}, u32[]{:S(2)}) collective-permute-start(bf16[256,2048]{1,0:T(8,128)(2,1)S(1)} %join.34), channel_id=1, source_target_pairs={{0,1},{1,2},{2,3},{4,5},{5,6},{6,7},{8,9},{9,10},{10,11},{12,13},{... | collective-permute-start | bytes 3145736 | tf_op jit(solution)/shard_map/ppermute | solution.py:636
  385.7 22.9 %collective-permute-start.36 = (bf16[256,2048]{1,0:T(8,128)(2,1)S(1)}, bf16[256,2048]{1,0:T(8,128)(2,1)S(1)}, u32[]{:S(2)}, u32[]{:S(2)}) collective-permute-start(bf16[256,2048]{1,0:T(8,128)(2,1)S(1)} %join.36), channel_id=1, source_target_pairs={{1,0},{2,1},{3,2},{5,4},{6,5},{7,6},{9,8},{10,9},{11,10},{13,12},{... | collective-permute-start | bytes 3145736 | tf_op jit(solution)/shard_map/ppermute | solution.py:636
  402.7 28.5 %collective-permute-start.34 = (bf16[256,2048]{1,0:T(8,128)(2,1)S(1)}, bf16[256,2048]{1,0:T(8,128)(2,1)S(1)}, u32[]{:S(2)}, u32[]{:S(2)}) collective-permute-start(bf16[256,2048]{1,0:T(8,128)(2,1)S(1)} %join.35), channel_id=1, source_target_pairs={{0,1},{1,2},{2,3},{4,5},{5,6},{6,7},{8,9},{9,10},{10,11},{12,13},{... | collective-permute-start | bytes 3145736 | tf_op jit(solution)/shard_map/ppermute | solution.py:636
  409.3 22.3 %collective-permute-start.37 = (bf16[256,2048]{1,0:T(8,128)(2,1)S(1)}, bf16[256,2048]{1,0:T(8,128)(2,1)S(1)}, u32[]{:S(2)}, u32[]{:S(2)}) collective-permute-start(bf16[256,2048]{1,0:T(8,128)(2,1)S(1)} %join.37), channel_id=1, source_target_pairs={{1,0},{2,1},{3,2},{5,4},{6,5},{7,6},{9,8},{10,9},{11,10},{13,12},{... | collective-permute-start | bytes 3145736 | tf_op jit(solution)/shard_map/ppermute | solution.py:636
  440.4 27.3 %collective-permute-start.38 = (bf16[256,2048]{1,0:T(8,128)(2,1)}, bf16[256,2048]{1,0:T(8,128)(2,1)}, u32[]{:S(2)}, u32[]{:S(2)}) collective-permute-start(bf16[256,2048]{1,0:T(8,128)(2,1)} %block_term.12), channel_id=1, source_target_pairs={{0,3},{1,0},{2,1},{3,2},{4,7},{5,4},{6,5},{7,6},{8,11},{9,8},{10,9... | collective-permute-start | bytes 3145736 | tf_op jit(solution)/shard_map/ppermute | solution.py:636
  470.5 26.8 %collective-permute-start.40 = (bf16[256,2048]{1,0:T(8,128)(2,1)S(1)}, bf16[256,2048]{1,0:T(8,128)(2,1)S(1)}, u32[]{:S(2)}, u32[]{:S(2)}) collective-permute-start(bf16[256,2048]{1,0:T(8,128)(2,1)S(1)} %join.38), channel_id=1, source_target_pairs={{0,3},{1,0},{2,1},{3,2},{4,7},{5,4},{6,5},{7,6},{8,11},{9,8},{10,9... | collective-permute-start | bytes 3145736 | tf_op jit(solution)/shard_map/ppermute | solution.py:636
  474.8 11.3 %collective-permute-start.41 = (bf16[2,256,1024]{2,1,0:T(8,128)(2,1)S(1)}, bf16[2,256,1024]{2,1,0:T(8,128)(2,1)S(1)}, u32[]{:S(2)}, u32[]{:S(2)}) collective-permute-start(bf16[2,256,1024]{2,1,0:T(8,128)(2,1)S(1)} %constant_dynamic-slice_fusion), channel_id=1, source_target_pairs={{0,4},{4,0},{8,12},{12,8},{16,20},{20,16},{24,28},{28,24},{1,5},{5... | collective-permute-start | bytes 3145736 | tf_op jit(solution)/shard_map/ppermute | solution.py:657
  499.0 44.2 %collective-permute-start.42 = (bf16[256,2048]{1,0:T(8,128)(2,1)}, bf16[256,2048]{1,0:T(8,128)(2,1)S(1)}, u32[]{:S(2)}, u32[]{:S(2)}) collective-permute-start(bf16[256,2048]{1,0:T(8,128)(2,1)} %join.39), channel_id=1, source_target_pairs={{0,3},{1,0},{2,1},{3,2},{4,7},{5,4},{6,5},{7,6},{8,11},{9,8},{10,9... | collective-permute-start | bytes 3145736 | tf_op jit(solution)/shard_map/ppermute | solution.py:636
  504.6 21.4 %collective-permute-start.45 = (f32[8320]{0:T(1024)S(1)}, f32[8320]{0:T(1024)S(1)}, u32[]{:S(2)}, u32[]{:S(2)}) collective-permute-start(f32[8320]{0:T(1024)S(1)} %add.125), channel_id=1, source_target_pairs={{0,1},{1,0},{2,3},{3,2},{4,5},{5,4},{6,7},{7,6},{8,9},{9,8},{10,11... | collective-permute-start | bytes 99848 | tf_op jit(solution)/shard_map/ppermute | solution.py:636
  531.0 15.1 %collective-permute-start.47 = (f32[8320]{0:T(1024)S(1)}, f32[8320]{0:T(1024)S(1)}, u32[]{:S(2)}, u32[]{:S(2)}) collective-permute-start(f32[8320]{0:T(1024)S(1)} %add.127), channel_id=1, source_target_pairs={{0,8},{4,12},{8,16},{12,20},{16,24},{20,28},{24,0},{28,4},{1,9},{5... | collective-permute-start | bytes 99848 | tf_op jit(solution)/shard_map/ppermute | solution.py:833
  532.4 13.7 %collective-permute-start.48 = (f32[8320]{0:T(1024)S(1)}, f32[8320]{0:T(1024)S(1)}, u32[]{:S(2)}, u32[]{:S(2)}) collective-permute-start(f32[8320]{0:T(1024)S(1)} %add.127), channel_id=1, source_target_pairs={{0,16},{4,20},{8,24},{12,28},{16,0},{20,4},{24,8},{28,12},{1,17},{... | collective-permute-start | bytes 99848 | tf_op jit(solution)/shard_map/ppermute | solution.py:833
  533.5 12.5 %collective-permute-start.49 = (f32[8320]{0:T(1024)S(1)}, f32[8320]{0:T(1024)S(1)}, u32[]{:S(2)}, u32[]{:S(2)}) collective-permute-start(f32[8320]{0:T(1024)S(1)} %add.127), channel_id=1, source_target_pairs={{0,24},{4,28},{8,0},{12,4},{16,8},{20,12},{24,16},{28,20},{1,25},{... | collective-permute-start | bytes 99848 | tf_op jit(solution)/shard_map/ppermute | solution.py:833
  (89 other events, 759.7 us)
Sparse Core Ops, SparseCore 0:
  370.3 86.6 reduce-scatter.2
  460.3 54.3 reduce-scatter.4
